TPU v7x, 32 devices: a whole 2x2x4 slice. The times are simulated.
32 devices in a mesh: groups: 2 (over x), tile: 8 (over z, y), dp: 2 (over core).
Axes of the slice: x: 2, y: 2, z: 4, core: 2. Of those that a mesh axis runs over, the one named last changes fastest.
Arguments:
- initial_state: bfloat16 [4, 6, 24, 24, 256], P(('groups', 'dp'), None, 'tile'), parts along dimension 0, may hold values from -6 to 6
- state_cotangents: bfloat16 [1, 4, 6, 24, 24, 256], P(None, ('groups', 'dp'), None, 'tile'), parts along dimension 1, may hold values from -6 to 6
- w_first: bfloat16 [3, 3, 256, 256], replicated, may hold values from -0.125 to 0.125
- bias: float32 [256], replicated, may hold values from -3 to 3
- w_second: bfloat16 [3, 3, 256, 256], replicated, may hold values from -0.125 to 0.125
- edge_partner: int32 [6, 4], replicated, may hold values from 0 to 23, as said below
Outputs:
- final_state: bfloat16 [4, 6, 24, 24, 256], P(('groups', 'dp'), None, 'tile'), parts along dimension 0
- state_grad: float32 [4, 6, 24, 24, 256], P(('groups', 'dp'), None, 'tile'), parts along dimension 0
- w_first_step: float32 [6, 3, 256, 256], P('groups'), parts along dimension 0
- bias_step: float32 [512], P('groups'), parts along dimension 0
- w_second_step: float32 [6, 3, 256, 256], P('groups'), parts along dimension 0
There are 2 independent parts, one for each index of `groups`. A program takes and returns all parts, laid end to end along the dimension named above; an argument that names none is the same for every part. Nothing has to cross between parts.
Inputs may be any that keep to these rules, and one draw needn't show every extreme that they name: `edge_partner`: entry [f, e] names edge e2 of face f2 as 4 * f2 + e2. The pairing is its own inverse, joins no edge to itself or to an edge of its own face, and glues the six faces into the surface of a cube with every face seen from outside.
All inputs are finite; a program needn't handle non-finite values.
Results may differ from a plain program's by a relative error of at most 0.005.
Values may be sent and summed in bfloat16 or wider, within the bound.
No kernel may reach another device: no remote copies, remote signals or barrier semaphores. Data moves between devices by JAX's collectives and lax.ppermute only.
A program may use at most 128 MiB of HBM per device.

v0:
```python
import jax
import jax.numpy as jnp
from jax import lax
from jax.sharding import PartitionSpec as P


def extended(cells, sides, width):
    for axis, dim in sides:
        count = lax.axis_size(axis)
        ends = count - 1
        head = lax.slice_in_dim(cells, 0, width, axis=dim)
        tail = lax.slice_in_dim(cells, cells.shape[dim] - width, cells.shape[dim], axis=dim)
        cells = jnp.concatenate(
            [
                lax.ppermute(tail, axis, [(i, (i + 1) % count) for i in range(ends)]),
                cells,
                lax.ppermute(head, axis, [((i + 1) % count, i) for i in range(ends)]),
            ],
            axis=dim,
        )
    return cells


def edge_match(strip_table, edge_partner):
    samples_here = strip_table.shape[0]
    flat_rows = strip_table.reshape((samples_here, 24) + strip_table.shape[3:])
    partner_flat = edge_partner.reshape(24)
    moved_rows = jnp.take(flat_rows, partner_flat, axis=1)
    own_side = jnp.arange(24, dtype=jnp.int32) % 4 < 2
    far_side = partner_flat % 4 < 2
    flipped = own_side == far_side
    moved_rows = jnp.where(flipped[None, :, None, None], moved_rows[:, :, ::-1], moved_rows)
    return moved_rows.reshape(strip_table.shape)


def tile_strips(grid_field, tile_index, tile_count):
    row_count = grid_field.shape[2]
    col_count = grid_field.shape[3]
    blank = jnp.zeros_like(grid_field[:, :, 0])
    upper_row = jnp.where(tile_index == 0, grid_field[:, :, 0], blank)
    lower_row = jnp.where(tile_index == tile_count - 1, grid_field[:, :, row_count - 1], blank)
    zero_rows = jnp.zeros(grid_field.shape[:2] + (col_count, grid_field.shape[4]), grid_field.dtype)
    eastern = lax.dynamic_update_slice_in_dim(
        zero_rows, grid_field[:, :, :, col_count - 1], tile_index * row_count, 2
    )
    western = lax.dynamic_update_slice_in_dim(
        zero_rows, grid_field[:, :, :, 0], tile_index * row_count, 2
    )
    return jnp.stack([upper_row, eastern, lower_row, western], axis=2)


def pad_local(grid_field, edge_partner, tile_index, tile_count):
    row_count = grid_field.shape[2]
    strip_sums = lax.psum(tile_strips(grid_field, tile_index, tile_count), "tile").astype(
        jnp.float32
    )
    ghost_rows = edge_match(strip_sums.astype(jnp.bfloat16), edge_partner)
    western = lax.dynamic_slice_in_dim(ghost_rows[:, :, 3], tile_index * row_count, row_count, 2)
    eastern = lax.dynamic_slice_in_dim(ghost_rows[:, :, 1], tile_index * row_count, row_count, 2)
    middle = jnp.concatenate([western[:, :, :, None], grid_field, eastern[:, :, :, None]], axis=3)
    framed = extended(middle, (("tile", 2),), 1)
    corner = jnp.zeros_like(ghost_rows[:, :, 0][:, :, :1])
    upper_row = jnp.concatenate([corner, ghost_rows[:, :, 0], corner], axis=2)
    lower_row = jnp.concatenate([corner, ghost_rows[:, :, 2], corner], axis=2)
    head_row = jnp.where(tile_index == 0, upper_row, framed[:, :, 0])
    tail_row = jnp.where(tile_index == tile_count - 1, lower_row, framed[:, :, row_count + 1])
    return jnp.concatenate(
        [head_row[:, :, None], framed[:, :, 1 : row_count + 1], tail_row[:, :, None]], axis=2
    )


def pad_back(framed_grad, edge_partner, tile_index, tile_count):
    row_count = framed_grad.shape[2] - 2
    col_count = framed_grad.shape[3] - 2
    outgoing = jnp.concatenate([framed_grad[:, :, :1], framed_grad[:, :, row_count + 1 :]], axis=2)
    incoming = extended(outgoing.astype(jnp.bfloat16), (("tile", 2),), 1).astype(outgoing.dtype)
    inner_rows = framed_grad[:, :, 1 : row_count + 1]
    inner_rows = inner_rows.at[:, :, 0].add(incoming[:, :, 0])
    inner_rows = inner_rows.at[:, :, row_count - 1].add(incoming[:, :, 3])
    upper_row = jnp.where(tile_index == 0, framed_grad[:, :, 0, 1 : col_count + 1], 0.0)
    lower_row = jnp.where(
        tile_index == tile_count - 1, framed_grad[:, :, row_count + 1, 1 : col_count + 1], 0.0
    )
    zero_rows = jnp.zeros(framed_grad.shape[:2] + (col_count, framed_grad.shape[4]), jnp.float32)
    eastern = lax.dynamic_update_slice_in_dim(
        zero_rows, inner_rows[:, :, :, col_count + 1], tile_index * row_count, 2
    )
    western = lax.dynamic_update_slice_in_dim(
        zero_rows, inner_rows[:, :, :, 0], tile_index * row_count, 2
    )
    strip_table = jnp.stack([upper_row, eastern, lower_row, western], axis=2)
    moved_rows = edge_match(
        lax.psum(strip_table.astype(jnp.bfloat16), "tile").astype(jnp.float32), edge_partner
    )
    first_back = moved_rows[:, :, 0]
    last_back = moved_rows[:, :, 2]
    east_back = lax.dynamic_slice_in_dim(moved_rows[:, :, 1], tile_index * row_count, row_count, 2)
    west_back = lax.dynamic_slice_in_dim(moved_rows[:, :, 3], tile_index * row_count, row_count, 2)
    cell_grad = inner_rows[:, :, :, 1 : col_count + 1]
    cell_grad = cell_grad.at[:, :, 0].add(jnp.where(tile_index == 0, first_back, 0.0))
    cell_grad = cell_grad.at[:, :, row_count - 1].add(
        jnp.where(tile_index == tile_count - 1, last_back, 0.0)
    )
    cell_grad = cell_grad.at[:, :, :, col_count - 1].add(east_back)
    cell_grad = cell_grad.at[:, :, :, 0].add(west_back)
    return cell_grad


def convolve(framed, weights):
    row_count = framed.shape[2] - 2
    col_count = framed.shape[3] - 2
    channels = framed.shape[4]
    summed_taps = None
    for tap_row in range(3):
        for tap_col in range(3):
            window = framed[
                :, :, tap_row : tap_row + row_count, tap_col : tap_col + col_count
            ].reshape(-1, channels)
            tap_term = jnp.dot(
                window, weights[tap_row, tap_col], preferred_element_type=jnp.float32
            )
            summed_taps = tap_term if summed_taps is None else summed_taps + tap_term
    return summed_taps.reshape(framed.shape[:2] + (row_count, col_count, weights.shape[3]))


def convolve_back(upstream, weights):
    row_count = upstream.shape[2]
    col_count = upstream.shape[3]
    flat_rows = upstream.reshape(-1, upstream.shape[4])
    framed = jnp.zeros(
        upstream.shape[:2] + (row_count + 2, col_count + 2, weights.shape[2]), jnp.float32
    )
    for tap_row in range(3):
        for tap_col in range(3):
            tap_term = lax.dot_general(
                flat_rows,
                weights[tap_row, tap_col],
                (((1,), (1,)), ((), ())),
                preferred_element_type=jnp.float32,
            )
            framed = framed.at[
                :, :, tap_row : tap_row + row_count, tap_col : tap_col + col_count
            ].add(tap_term.reshape(upstream.shape[:4] + (weights.shape[2],)))
    return framed


def weight_grad(framed, upstream):
    row_count = upstream.shape[2]
    col_count = upstream.shape[3]
    channels = framed.shape[4]
    flat_up = upstream.reshape(-1, upstream.shape[4])
    tap_grads = []
    for tap_row in range(3):
        for tap_col in range(3):
            window = framed[
                :, :, tap_row : tap_row + row_count, tap_col : tap_col + col_count
            ].reshape(-1, channels)
            tap_grads.append(
                lax.dot_general(
                    window, flat_up, (((0,), (0,)), ((), ())), preferred_element_type=jnp.float32
                )
            )
    return jnp.stack(tap_grads).reshape(3, 3, channels, flat_up.shape[1])


def silu_slope(before):
    sigmoid_value = jax.nn.sigmoid(before)
    return sigmoid_value * (1.0 + before * (1.0 - sigmoid_value))


def normalized(gradient):
    return gradient / jnp.sqrt(jnp.mean(gradient * gradient) + 1e-06)


def summed(vector):
    return lax.psum(vector, ("tile", "dp"))


def on_device(initial_state, state_cotangents, w_first, bias, w_second, edge_partner):
    tile_index = lax.axis_index("tile")
    tile_count = lax.axis_size("tile")
    steps_total = state_cotangents.shape[0]
    tap_block = w_first.size
    current = initial_state
    rollout_step = 0
    framed_state = pad_local(current, edge_partner, tile_index, tile_count)
    before = convolve(framed_state, w_first) + bias
    hidden = jax.nn.silu(before).astype(jnp.bfloat16)
    framed_hidden = pad_local(hidden, edge_partner, tile_index, tile_count)
    update = convolve(framed_hidden, w_second)
    history = [(current, before, hidden)]
    current = (current.astype(jnp.float32) + update).astype(jnp.bfloat16)
    state_grad = state_cotangents[steps_total - 1].astype(jnp.float32)
    grad_first = jnp.zeros(w_first.shape, jnp.float32)
    grad_bias = jnp.zeros(bias.shape, jnp.float32)
    grad_second = jnp.zeros(w_second.shape, jnp.float32)
    early_total = None
    for rollout_step in reversed(range(steps_total)):
        first_input, before, second_input = history[rollout_step]
        first_input = pad_local(first_input, edge_partner, tile_index, tile_count)
        second_input = pad_local(second_input, edge_partner, tile_index, tile_count)
        upstream = state_grad.astype(jnp.bfloat16)
        grad_second = weight_grad(second_input, upstream)
        early_total = summed(grad_second.reshape(-1))
        hidden_grad = pad_back(
            convolve_back(upstream, w_second), edge_partner, tile_index, tile_count
        )
        before_grad = hidden_grad * silu_slope(before)
        grad_bias = jnp.sum(before_grad, axis=(0, 1, 2, 3))
        inner_up = before_grad.astype(jnp.bfloat16)
        grad_first = weight_grad(first_input, inner_up)
        state_grad = state_grad + pad_back(
            convolve_back(inner_up, w_first), edge_partner, tile_index, tile_count
        )
    late_total = summed(jnp.concatenate([grad_first.reshape(-1), grad_bias]))
    total_first = late_total[:tap_block].reshape(w_first.shape)
    total_bias = late_total[tap_block:]
    total_second = early_total.reshape(w_second.shape)
    return (
        current,
        state_grad,
        normalized(total_first),
        normalized(total_bias),
        normalized(total_second),
    )


def solution(mesh):
    return jax.shard_map(
        on_device,
        mesh=mesh,
        in_specs=(
            P(("groups", "dp"), None, "tile", None, None),
            P(None, ("groups", "dp"), None, "tile", None, None),
            P(),
            P(),
            P(),
            P(),
        ),
        out_specs=(
            P(("groups", "dp"), None, "tile", None, None),
            P(("groups", "dp"), None, "tile", None, None),
            P("groups", None, None, None),
            P("groups"),
            P("groups", None, None, None),
        ),
        check_vma=False,
    )
```

profile of v0, /device:TPU:0, one launch (start us, length us, event | category | flops | bytes accessed | tf_op | source)
XLA Modules:
  0.0 483.6 jit_solution(12643501133654342980)
XLA Ops:
  7.2 1.3 convolution_bitcast_fusion.7
  8.5 1.4 fusion.36
  12.0 2.3 fusion
  14.3 4.3 scatter-add.101
  21.0 3.2 scatter-add.104
  24.7 2.0 scatter-add.106
  27.0 2.0 scatter-add.109
  29.5 2.0 scatter-add.111
  31.8 2.0 scatter-add.114
  33.9 1.3 collective-permute-start.5
  35.4 5.5 %collective-permute-start.4 = (bf16[1,6,1,26,256]{4,2,1,3,0:T(2,128)(2,1)S(1)}, bf16[1,6,1,26,256]{4,2,1,3,0:T(2,128)(2,1)S(1)}, u32[]{:S(2)}, u32[]{:S(2)}) collective-permute-start(bf16[1,6,1,26,256]{4,2,1,3,0:T(2,128)(2,1)S(1)} %copy.519), channel_id=1, source_target_pairs={{0,2},{2,4},{4,6},{6,8},{8,10},{10,12},{12,14},{1,3},{3,5},{5,7},{... | collective-permute-start | bytes 239624 | tf_op jit(solution)/shard_map/ppermute | solution.py:15
  44.5 2.0 collective-permute-done.4
  47.1 4.4 scatter-add.115
  52.1 4.4 scatter-add.116
  58.0 73.8 %all-reduce.13.cloned.1.call-done = (bf16[1,24,24,256]{3,2,1,0:T(8,128)(2,1)}, bf16[1,24,24,256]{3,2,1,0:T(8,128)(2,1)}) async-done(((bf16[1,24,24,256]{3,2,1,0:T(8,128)(2,1)}, bf16[1,24,24,256]{3,2,1,0:T(8,128)(2,1)}), (bf16[1,24,24,256]{3,2,1,0:T(8,128)(2,1)}, bf16[1,24,24,256]{3,2,1,0:T(8,128)(2,1)})) %all-reduce.13.cloned.1.call-update) | async-done | bytes 589840 | tf_op jit(solution)/shard_map/psum | solution.py:54
  131.9 1.5 gather_fusion
  136.7 1.3 collective-permute-start.1
  138.0 5.4 %collective-permute-start = (bf16[1,6,1,26,256]{4,2,1,3,0:T(2,128)(2,1)}, bf16[1,6,1,26,256]{4,2,1,3,0:T(2,128)(2,1)}, u32[]{:S(2)}, u32[]{:S(2)}) collective-permute-start(bf16[1,6,1,26,256]{4,2,1,3,0:T(2,128)(2,1)} %get-tuple-element.441), channel_id=1, source_target_pairs={{0,2},{2,4},{4,6},{6,8},{8,10},{10,12},{12,14},{1,3},{3,5},{5,7},{... | collective-permute-start | bytes 239624 | tf_op jit(solution)/shard_map/ppermute | solution.py:15
  146.5 1.9 scatter-add.119
  148.7 1.9 scatter-add.120
  151.0 1.6 broadcast_select_fusion.1
  153.2 1.4 slice_bitcast_fusion.5
  154.7 1.3 slice_bitcast_fusion.8
  167.8 1.6 bitcast_add_fusion
  169.5 4.7 scatter-add.126
  174.2 3.2 add_select_fusion
  177.5 4.6 scatter-add.129
  182.1 1.4 slice_add_fusion.5
  183.5 3.4 scatter-add.130
  186.9 1.4 slice_add_fusion.4
  188.3 3.4 scatter-add.131
  191.7 1.4 slice_add_fusion.3
  193.1 3.4 scatter-add.134
  196.6 1.4 slice_add_fusion.2
  197.9 3.6 scatter-add.135
  201.6 1.4 slice_add_fusion.1
  203.0 3.4 scatter-add.136
  206.8 3.4 scatter-add.139
  210.4 3.0 collective-permute-start.6
  213.5 1.3 collective-permute-start.7
  214.8 1.4 broadcast_select_fusion.17
  221.3 2.6 copy.460
  226.3 4.4 scatter-add.140
  230.7 1.6 fusion.47
  232.4 4.4 scatter-add.141
  240.6 1.6 pad_maximum_fusion
  242.3 72.6 %all-reduce.11.cloned.1.call-done = (bf16[1,24,24,256]{3,2,1,0:T(8,128)(2,1)}, bf16[1,24,24,256]{3,2,1,0:T(8,128)(2,1)}) async-done(((bf16[1,24,24,256]{3,2,1,0:T(8,128)(2,1)}, bf16[1,24,24,256]{3,2,1,0:T(8,128)(2,1)}), (bf16[1,24,24,256]{3,2,1,0:T(8,128)(2,1)}, bf16[1,24,24,256]{3,2,1,0:T(8,128)(2,1)})) %all-reduce.11.cloned.1.call-update) | async-done | bytes 589840 | tf_op jit(solution)/shard_map/psum | solution.py:54
  314.9 1.5 gather_fusion.1
  318.7 1.3 collective-permute-start.3
  320.0 5.2 %collective-permute-start.2 = (bf16[1,6,1,26,256]{4,2,1,3,0:T(2,128)(2,1)}, bf16[1,6,1,26,256]{4,2,1,3,0:T(2,128)(2,1)}, u32[]{:S(2)}, u32[]{:S(2)}) collective-permute-start(bf16[1,6,1,26,256]{4,2,1,3,0:T(2,128)(2,1)} %get-tuple-element.434), channel_id=1, source_target_pairs={{0,2},{2,4},{4,6},{6,8},{8,10},{10,12},{12,14},{1,3},{3,5},{5,7},{... | collective-permute-start | bytes 239624 | tf_op jit(solution)/shard_map/ppermute | solution.py:15
  326.3 1.3 fusion.53
  327.6 1.9 scatter-add.144
  329.8 1.9 scatter-add.145
  333.2 1.6 broadcast_select_fusion
  338.9 2.6 copy.461
  341.6 1.2 copy-done.6
  346.2 113.0 %all-reduce.9.cloned.1.call-done = (f32[590080]{0:T(1024)}, f32[589824]{0:T(1024)}) async-done(((f32[590080]{0:T(1024)}, f32[589824]{0:T(1024)}), (f32[590080]{0:T(1024)}, f32[589824]{0:T(1024)})) %all-reduce.9.cloned.1.call-update) | async-done | bytes 4719632 | tf_op jit(solution)/shard_map/psum | solution.py:176
  459.2 1.4 multiply_reduce_fusion.2
  460.6 2.9 multiply_reduce_fusion.1
  466.8 1.6 broadcast_divide_fusion
  468.4 3.5 div.65
  471.8 1.2 slice_divide_fusion.1
  473.1 1.8 slice_divide_fusion
  474.9 1.8 div.58
  (274 shorter events, 57.1 us)
Async XLA Ops:
  7.2 3.9 copy-start.34
  7.2 124.7 %all-reduce.13.cloned.1.call-start = ((), (), s32[]{:S(2)}) async-start(), calls=%async_computation.2 | async-start | bytes 1179648 | tf_op jit(solution)/shard_map/psum | solution.py:54
  8.5 3.5 copy-start
  8.5 3.5 copy-start.5
  31.5 9.4 %copy-start.3 = (bf16[1,6,3,24,256]{4,3,2,1,0:T(8,128)(2,1)S(1)}, bf16[1,6,3,24,256]{4,3,2,1,0:T(8,128)(2,1)}, u32[]{:S(2)}) copy-start(bf16[1,6,3,24,256]{4,3,2,1,0:T(8,128)(2,1)} %param.70) | copy-start | bytes 663556
  33.9 10.5 %collective-permute-start.5 = (bf16[1,6,1,26,256]{4,2,1,3,0:T(2,128)(2,1)S(1)}, bf16[1,6,1,26,256]{4,2,1,3,0:T(2,128)(2,1)S(1)}, u32[]{:S(2)}, u32[]{:S(2)}) collective-permute-start(bf16[1,6,1,26,256]{4,2,1,3,0:T(2,128)(2,1)S(1)} %copy.518), channel_id=1, source_target_pairs={{2,0},{4,2},{6,4},{8,6},{10,8},{12,10},{14,12},{3,1},{5,3},{7,5},{... | collective-permute-start | bytes 239624 | tf_op jit(solution)/shard_map/ppermute | solution.py:17
  35.4 11.1 %collective-permute-start.4 = (bf16[1,6,1,26,256]{4,2,1,3,0:T(2,128)(2,1)S(1)}, bf16[1,6,1,26,256]{4,2,1,3,0:T(2,128)(2,1)S(1)}, u32[]{:S(2)}, u32[]{:S(2)}) collective-permute-start(bf16[1,6,1,26,256]{4,2,1,3,0:T(2,128)(2,1)S(1)} %copy.519), channel_id=1, source_target_pairs={{0,2},{2,4},{4,6},{6,8},{8,10},{10,12},{12,14},{1,3},{3,5},{5,7},{... | collective-permute-start | bytes 239624 | tf_op jit(solution)/shard_map/ppermute | solution.py:15
  51.5 6.2 %copy-start.32 = (s32[6,4]{0,1:T(4,128)S(1)}, s32[6,4]{0,1:T(4,128)}, u32[]{:S(2)}) copy-start(s32[6,4]{0,1:T(4,128)} %param.75) | copy-start | bytes 292
  57.6 257.3 %all-reduce.11.cloned.1.call-start = ((), (), s32[]{:S(2)}) async-start(), calls=%async_computation.1 | async-start | bytes 1179648 | tf_op jit(solution)/shard_map/psum | solution.py:54
  133.9 9.5 %copy-start.24 = (bf16[1,24,24,256]{3,2,1,0:T(8,128)(2,1)S(1)}, bf16[1,24,24,256]{3,2,1,0:T(8,128)(2,1)}, u32[]{:S(2)}) copy-start(bf16[1,24,24,256]{3,2,1,0:T(8,128)(2,1)} %get-tuple-element.392) | copy-start | bytes 884740
  136.7 14.2 %collective-permute-start.1 = (bf16[1,6,1,26,256]{4,2,1,3,0:T(2,128)(2,1)}, bf16[1,6,1,26,256]{4,2,1,3,0:T(2,128)(2,1)}, u32[]{:S(2)}, u32[]{:S(2)}) collective-permute-start(bf16[1,6,1,26,256]{4,2,1,3,0:T(2,128)(2,1)} %get-tuple-element.440), channel_id=1, source_target_pairs={{2,0},{4,2},{6,4},{8,6},{10,8},{12,10},{14,12},{3,1},{5,3},{7,5},{... | collective-permute-start | bytes 239624 | tf_op jit(solution)/shard_map/ppermute | solution.py:17
  138.0 12.9 %collective-permute-start = (bf16[1,6,1,26,256]{4,2,1,3,0:T(2,128)(2,1)}, bf16[1,6,1,26,256]{4,2,1,3,0:T(2,128)(2,1)}, u32[]{:S(2)}, u32[]{:S(2)}) collective-permute-start(bf16[1,6,1,26,256]{4,2,1,3,0:T(2,128)(2,1)} %get-tuple-element.441), channel_id=1, source_target_pairs={{0,2},{2,4},{4,6},{6,8},{8,10},{10,12},{12,14},{1,3},{3,5},{5,7},{... | collective-permute-start | bytes 239624 | tf_op jit(solution)/shard_map/ppermute | solution.py:15
  146.3 4.7 copy-start.22
  146.3 4.7 copy-start.23
  150.7 2.5 copy-start.9
  150.9 7.1 %copy-start.14 = (bf16[1,6,3,24,256]{4,3,2,1,0:T(8,128)(2,1)}, bf16[1,6,3,24,256]{4,3,2,1,0:T(8,128)(2,1)S(1)}, u32[]{:S(2)}) copy-start(bf16[1,6,3,24,256]{4,3,2,1,0:T(8,128)(2,1)S(1)} %get-tuple-element.459) | copy-start | bytes 663556
  156.0 1.3 copy-start.4
  158.9 1.1 copy-start.10
  158.9 1.1 copy-start.33
  159.4 1.5 copy-start.11
  210.4 13.9 %collective-permute-start.6 = (bf16[1,6,1,26,256]{4,2,1,3,0:T(2,128)(2,1)S(1)}, bf16[1,6,1,26,256]{4,2,1,3,0:T(2,128)(2,1)S(1)}, u32[]{:S(2)}, u32[]{:S(2)}) collective-permute-start(bf16[1,6,1,26,256]{4,2,1,3,0:T(2,128)(2,1)S(1)} %get-tuple-element.397), channel_id=1, source_target_pairs={{0,2},{2,4},{4,6},{6,8},{8,10},{10,12},{12,14},{1,3},{3,5},{5,7},{... | collective-permute-start | bytes 239624 | tf_op jit(solution)/shard_map/ppermute | solution.py:15
  213.5 10.9 %collective-permute-start.7 = (bf16[1,6,1,26,256]{4,2,1,3,0:T(2,128)(2,1)S(1)}, bf16[1,6,1,26,256]{4,2,1,3,0:T(2,128)(2,1)S(1)}, u32[]{:S(2)}, u32[]{:S(2)}) collective-permute-start(bf16[1,6,1,26,256]{4,2,1,3,0:T(2,128)(2,1)S(1)} %get-tuple-element.398), channel_id=1, source_target_pairs={{2,0},{4,2},{6,4},{8,6},{10,8},{12,10},{14,12},{3,1},{5,3},{7,5},{... | collective-permute-start | bytes 239624 | tf_op jit(solution)/shard_map/ppermute | solution.py:17
  214.8 1.8 copy-start.31
  216.3 1.0 copy-start.30
  216.9 1.0 copy-start.29
  217.6 1.0 copy-start.15
  218.8 1.0 copy-start.28
  219.4 1.0 copy-start.27
  220.1 1.0 copy-start.26
  224.3 0.7 copy-start.16
  225.0 0.7 copy-start.17
  226.3 11.3 %copy-start.20 = (bf16[1,6,1,24,256]{4,2,1,3,0:T(2,128)(2,1)S(1)}, bf16[1,6,1,24,256]{4,2,1,3,0:T(2,128)(2,1)}, u32[]{:S(2)}) copy-start(bf16[1,6,1,24,256]{4,2,1,3,0:T(2,128)(2,1)} %get-tuple-element.448) | copy-start | bytes 221188
  226.3 11.3 %copy-start.21 = (bf16[1,6,1,24,256]{4,2,1,3,0:T(2,128)(2,1)S(1)}, bf16[1,6,1,24,256]{4,2,1,3,0:T(2,128)(2,1)}, u32[]{:S(2)}) copy-start(bf16[1,6,1,24,256]{4,2,1,3,0:T(2,128)(2,1)} %get-tuple-element.449) | copy-start | bytes 221188
  232.3 6.7 %copy-start.18 = (bf16[1,6,1,24,256]{4,2,1,3,0:T(2,128)(2,1)S(1)}, bf16[1,6,1,24,256]{4,2,1,3,0:T(2,128)(2,1)}, u32[]{:S(2)}) copy-start(bf16[1,6,1,24,256]{4,2,1,3,0:T(2,128)(2,1)} %get-tuple-element.476) | copy-start | bytes 221188
  232.3 6.7 %copy-start.19 = (bf16[1,6,1,24,256]{4,2,1,3,0:T(2,128)(2,1)S(1)}, bf16[1,6,1,24,256]{4,2,1,3,0:T(2,128)(2,1)}, u32[]{:S(2)}) copy-start(bf16[1,6,1,24,256]{4,2,1,3,0:T(2,128)(2,1)} %get-tuple-element.477) | copy-start | bytes 221188
  236.7 0.8 copy-start.7
  238.3 2.3 copy-start.1
  240.5 218.7 %all-reduce.9.cloned.1.call-start = ((), (), s32[]{:S(2)}) async-start(), calls=%async_computation | async-start | bytes 9445376 | tf_op jit(solution)/shard_map/psum | solution.py:176
  240.6 1.6 copy-start.8
  317.2 8.0 %copy-start.25 = (bf16[1,24,24,256]{3,2,1,0:T(8,128)(2,1)S(1)}, bf16[1,24,24,256]{3,2,1,0:T(8,128)(2,1)}, u32[]{:S(2)}) copy-start(bf16[1,24,24,256]{3,2,1,0:T(8,128)(2,1)} %get-tuple-element.390) | copy-start | bytes 884740
  318.7 14.5 %collective-permute-start.3 = (bf16[1,6,1,26,256]{4,2,1,3,0:T(2,128)(2,1)}, bf16[1,6,1,26,256]{4,2,1,3,0:T(2,128)(2,1)}, u32[]{:S(2)}, u32[]{:S(2)}) collective-permute-start(bf16[1,6,1,26,256]{4,2,1,3,0:T(2,128)(2,1)} %get-tuple-element.433), channel_id=1, source_target_pairs={{2,0},{4,2},{6,4},{8,6},{10,8},{12,10},{14,12},{3,1},{5,3},{7,5},{... | collective-permute-start | bytes 239624 | tf_op jit(solution)/shard_map/ppermute | solution.py:17
  320.0 13.2 %collective-permute-start.2 = (bf16[1,6,1,26,256]{4,2,1,3,0:T(2,128)(2,1)}, bf16[1,6,1,26,256]{4,2,1,3,0:T(2,128)(2,1)}, u32[]{:S(2)}, u32[]{:S(2)}) collective-permute-start(bf16[1,6,1,26,256]{4,2,1,3,0:T(2,128)(2,1)} %get-tuple-element.434), channel_id=1, source_target_pairs={{0,2},{2,4},{4,6},{6,8},{8,10},{10,12},{12,14},{1,3},{3,5},{5,7},{... | collective-permute-start | bytes 239624 | tf_op jit(solution)/shard_map/ppermute | solution.py:15
  336.3 1.2 copy-start.12
  341.5 1.3 copy-start.6
  343.2 1.0 copy-start.13
  459.2 5.7 %copy-start.2 = (f32[589824]{0:T(1024)S(1)}, f32[589824]{0:T(1024)}, u32[]{:S(2)}) copy-start(f32[589824]{0:T(1024)} %get-tuple-element.388) | copy-start | bytes 7077892
Sparse Core Ops, SparseCore 0:
  57.7 74.0 all-reduce.12
  240.7 74.1 all-reduce.10
  341.7 117.4 all-reduce.8
where the time goes:
time: 493 us; the launch traced here: 484 us
  waiting for transfers between devices  262 us (53%)
  local copies, waits for them, and re-layouts  112 us (23%)
  other arithmetic  45.4 us (9%)
  starting transfers between devices  24.3 us (5%)
  matrix products  22.4 us (5%)
  between operations  18.2 us (4%)
    psum x2, waiting for transfers between devices, pad_local(): lax.psum(tile_strips(grid_field, tile_index, tile_count), 'tile')  146 us
    psum x1, waiting for transfers between devices, summed(): return lax.psum(vector, ('tile', 'dp'))  113 us
    scatter-add x16, local copies, waits for them, and re-layouts, convolve_back(): framed = framed.at[:, :, tap_row:tap_row + row_count, tap_col:tap_col + c...  45.7 us
    ppermute x4, starting transfers between devices, extended(): lax.ppermute(tail, axis, [(i, (i + 1) % count) for i in range(ends)])  19.1 us
    unnamed x84, local copies, waits for them, and re-layouts  16.1 us
    dot_general x18, matrix products, convolve_back(): lax.dot_general(flat_rows, weights[tap_row, tap_col], (((1,), (1,)), ((),...  13.4 us
  transfers between devices with their start and end apart: 11, of which 4 were waited for; matrix products, arithmetic and copies ran while one was open for 6% of the time, Pallas kernels for 0%

commit v1 on v0

v1 whole, which is shorter than its diff:
```python
import functools

import jax
import jax.numpy as jnp
from jax import lax
from jax.experimental import pallas as pl
from jax.experimental.pallas import tpu as pltpu
from jax.sharding import PartitionSpec as P

BF = jnp.bfloat16
F32 = jnp.float32
EXTRA = 16


class Dims:
    def __init__(self, rows, face, tiles, channels):
        self.R, self.F, self.T, self.C = rows, face, tiles, channels
        self.N = 6 * rows * face
        self.ROW = 6 * face
        self.SLOT = -(-(2 * rows + 2) // 8) * 8
        self.RC = 6 * self.SLOT
        self.BASE = self.RC + 16
        self.MIR = 16 * rows
        self.row_ks = []
        k = 1
        while k < tiles:
            self.row_ks.append(k)
            k = 2 * k + 1
        self.o_msg = self.N
        self.o_mir = self.o_msg + tiles * self.BASE
        self.o_row = self.o_mir + self.MIR
        self.NT = self.o_row + len(self.row_ks) * self.ROW
        self.WE = 12 * 8
        self.S = self.WE + self.ROW

    def msg_rows(self, k):
        rows = self.BASE
        if k == self.T - 1:
            rows += self.MIR
        if k in self.row_ks:
            rows += self.ROW
        return rows


def col_iota(n):
    return lax.broadcasted_iota(jnp.int32, (n, 1), 0)


def one_hot(target, width):
    lanes = lax.broadcasted_iota(jnp.int32, (target.shape[0], width), 1)
    return jnp.where(lanes == target, 1.0, 0.0).astype(BF)


def edge_of(ep, strip):
    value = ep[strip]
    face = value // 4
    edge = value % 4
    own_low = (strip % 4) < 2
    far_low = edge < 2
    reverse = (far_low == own_low) if not isinstance(own_low, bool) else (far_low if own_low else edge >= 2)
    return face, edge, reverse


def message_targets(dm, ep, t, k):
    R, F, T = dm.R, dm.F, dm.T
    d = t ^ k
    parts = []
    i = col_iota(dm.SLOT)
    at_first = t == 0
    q = R * d - 1 + i
    inside = (q >= 0) & (q < F) & (i < R + 2)
    i2 = i - (R + 2)
    to_first = d == 0
    for f in range(6):
        strip = jnp.where(at_first, 4 * f, 4 * f + 2)
        value = ep[strip]
        far_low = (value % 4) < 2
        own_low = at_first
        reverse = far_low == own_low
        p0 = jnp.where(reverse, F - 1, 0)
        sgn = jnp.where(reverse, -1, 1)
        row = jnp.where(at_first, 0, R - 1)
        tgt_r = jnp.where(inside, (f * R + row) * F + p0 + sgn * q, -1)
        gvalue = ep[jnp.where(to_first, 4 * f, 4 * f + 2)]
        f2 = gvalue // 4
        column = jnp.where(gvalue % 4 == 1, F - 1, 0)
        tgt_c = f2 * (R * F) + column + F * i2
        parts.append(jnp.where(i2 < 0, tgt_r, jnp.where(i2 < R, tgt_c, -1)))
    s = col_iota(16)
    column_cells = (s // 2) * (R * F) + (s % 2) * (F - 1)
    row = jnp.where(d == T - 2 - t, R - 1, 0)
    parts.append(jnp.where(s < 12, column_cells + row * F, -1))
    if k == T - 1:
        for r in range(R):
            parts.append(jnp.where(s < 12, column_cells + r * F, -1))
    if k in dm.row_ks:
        row = jnp.where(d == (t + 1) % T, R - 1, 0)
        j = col_iota(F)
        for f in range(6):
            parts.append((f * R + row) * F + j)
    return jnp.concatenate(parts, axis=0)


def write_messages(dm, ep, t, sources, refs):
    for k in range(dm.T):
        hot = one_hot(message_targets(dm, ep, t, k), dm.N)
        for which, source in enumerate(sources):
            refs[k][which] = jnp.dot(hot, source, preferred_element_type=F32).astype(BF)


def pack_kernel(dm, sc, x_ref, up_ref, *refs):
    write_messages(dm, sc, sc[24], (x_ref[...], up_ref[...]), refs)


def ghost_targets(dm, ep, t):
    R, F, T = dm.R, dm.F, dm.T

    def o_row(k):
        out = dm.o_row
        for j, kk in enumerate(dm.row_ks):
            out = jnp.where(k == kk, dm.o_row + j * dm.ROW, out)
        return out

    parts = []
    m = col_iota(8)
    q = R * t - 1 + m
    inside = (q >= 0) & (q < F) & (m < R + 2)
    row_prev = o_row(t ^ (t - 1))
    row_next = o_row(t ^ (t + 1))
    ab_first = dm.o_msg + (t ^ (T - t)) * dm.BASE + dm.RC
    ab_last = dm.o_msg + (t ^ (T - 2 - t)) * dm.BASE + dm.RC
    for f in range(6):
        for edge in (3, 1):
            strip = 4 * f + edge
            value = ep[strip]
            f2, e2 = value // 4, value % 4
            far_low = e2 < 2
            reverse = far_low if edge < 2 else e2 >= 2
            is_col = (e2 % 2) == 1
            column = jnp.where(e2 == 1, F - 1, 0)
            s = 2 * f2 + jnp.where(e2 == 1, 1, 0)
            src_k = jnp.where(e2 == 0, t, t ^ (T - 1))
            slot = dm.o_msg + src_k * dm.BASE + f2 * dm.SLOT
            i0 = jnp.where(is_col, jnp.where(reverse, ab_first + s, row_prev + f2 * F + column), slot)
            i4 = jnp.where(is_col, jnp.where(reverse, ab_last + s, row_next + f2 * F + column), slot + R + 1)
            base = jnp.where(
                is_col, jnp.where(reverse, dm.o_mir + 16 * R + s, (f2 * R - 1) * F + column), slot
            )
            step = jnp.where(is_col, jnp.where(reverse, -16, F), 1)
            target = jnp.where(m == 0, i0, jnp.where(m == R + 1, i4, base + step * m))
            parts.append(jnp.where(inside, target, -1))
    j = col_iota(F)
    jt = jnp.zeros_like(j)
    for b in range(1, T):
        jt = jt + jnp.where(j >= b * R, 1, 0)
    jr = j - R * jt
    wrap = o_row(jnp.int32(T - 1))
    for edge in (0, 2):
        at_edge = (t == 0) if edge == 0 else (t == T - 1)
        inner_base = row_prev if edge == 0 else row_next
        own_row = 0 if edge == 0 else R - 1
        for f in range(6):
            value = ep[4 * f + edge]
            f2, e2 = value // 4, value % 4
            far_low = e2 < 2
            reverse = far_low if edge < 2 else e2 >= 2
            is_col = (e2 % 2) == 1
            same = e2 == edge
            row_base = jnp.where(same, (f2 * R + own_row) * F, wrap + f2 * F)
            lin_base = row_base + jnp.where(reverse, F - 1, 0)
            lin_step = jnp.where(reverse, -1, 1)
            k0 = jnp.where(reverse, T - 1, 0)
            ks = jnp.where(reverse, -1, 1)
            if edge == 2:
                k0 = T - 1 - k0
                ks = -ks
            col_base = dm.o_msg + k0 * dm.BASE + f * dm.SLOT + R + 2 + jnp.where(reverse, R - 1, 0)
            base = jnp.where(is_col, col_base, lin_base)
            sj = jnp.where(is_col, 0, lin_step)
            st = jnp.where(is_col, ks * dm.BASE, 0)
            sr = jnp.where(is_col, jnp.where(reverse, -1, 1), 0)
            base = jnp.where(at_edge, base, inner_base + f * F)
            sj = jnp.where(at_edge, sj, 1)
            st = jnp.where(at_edge, st, 0)
            sr = jnp.where(at_edge, sr, 0)
            parts.append(base + sj * j + st * jt + sr * jr)
    return jnp.concatenate(parts, axis=0)


def gather_ghosts(dm, ep, t, own, messages, table_ref):
    hot = one_hot(ghost_targets(dm, ep, t), dm.NT)
    out = []
    for which in range(2):
        table_ref[0 : dm.N] = own[which]
        for k in range(dm.T):
            ref = messages[k]
            at = dm.o_msg + k * dm.BASE
            table_ref[at : at + dm.BASE] = ref[which, 0 : dm.BASE]
            row = dm.BASE
            if k == dm.T - 1:
                table_ref[dm.o_mir : dm.o_mir + dm.MIR] = ref[which, row : row + dm.MIR]
                row += dm.MIR
            if k in dm.row_ks:
                at = dm.o_row + dm.row_ks.index(k) * dm.ROW
                table_ref[at : at + dm.ROW] = ref[which, row : row + dm.ROW]
        out.append(jnp.dot(hot, table_ref[...], preferred_element_type=F32))
    return out


def build_shifts(dm, field_ref, ghosts, top, bottom, frame_ref, shift_ref):
    R, F, C = dm.R, dm.F, dm.C
    for f in range(6):
        for r in range(R):
            frame_ref[r + 1, f, 8 : 8 + F] = field_ref[f * R + r].astype(F32)
    frame_ref[0, :, 8 : 8 + F] = top.reshape(6, F, C)
    frame_ref[R + 1, :, 8 : 8 + F] = bottom.reshape(6, F, C)
    for m in range(R + 2):
        for f in range(6):
            if ghosts is None:
                west = jnp.zeros((1, C), F32)
                east = west
            else:
                west = ghosts[16 * f + m : 16 * f + m + 1]
                east = ghosts[16 * f + 8 + m : 16 * f + 8 + m + 1]
            frame_ref[m, f, 7:8] = west
            frame_ref[m, f, 8 + F : 9 + F] = east
    for m in range(R + 2):
        for b in range(3):
            plane = frame_ref[m, :, 7 + b : 7 + b + F].reshape(dm.ROW, C)
            shift_ref[b, m * dm.ROW : (m + 1) * dm.ROW] = plane.astype(BF)


def build_strip_terms(dm, ep, t, ghosts, top, bottom, z_ref):
    R, F = dm.R, dm.F
    z_ref[...] = jnp.zeros(z_ref.shape, F32)

    def tap_of(strip, shift):
        value = ep[strip]
        e2 = value % 4
        far_low = e2 < 2
        own_low = (strip % 4) < 2
        reverse = far_low if own_low else jnp.logical_not(far_low)
        along = 1 - jnp.where(reverse, -shift, shift)
        return jnp.where(
            e2 == 0, along, jnp.where(e2 == 2, 6 + along, jnp.where(e2 == 1, 3 * along + 2, 3 * along))
        )

    live = lax.rem(lax.broadcasted_iota(jnp.int32, (dm.WE, 1), 0), 8) < R
    for shift in (-1, 0, 1):
        moved = pltpu.roll(ghosts, (dm.WE - 1 - shift) % dm.WE, 0) if shift > -1 else ghosts
        moved = jnp.where(live, moved, 0.0)
        for f in range(6):
            for side, edge in ((0, 3), (1, 1)):
                at = 16 * f + 8 * side
                z_ref[tap_of(4 * f + edge, shift), at : at + 8] = moved[at : at + 8]

    def add_rows(edge, rows):
        j = lax.rem(lax.broadcasted_iota(jnp.int32, (dm.ROW, 1), 0), F)
        for shift in (-1, 0, 1):
            if shift == 0:
                moved = rows
            else:
                moved = pltpu.roll(rows, (-shift) % dm.ROW, 0)
                moved = jnp.where((j + shift >= 0) & (j + shift < F), moved, 0.0)
            for f in range(6):
                at = dm.WE + F * f
                z_ref[tap_of(4 * f + edge, shift), at : at + F] = moved[F * f : F * (f + 1)]

    @pl.when(t == 0)
    def _():
        add_rows(0, top)

    @pl.when(t == dm.T - 1)
    def _():
        add_rows(2, bottom)


def adjoint(dm, t, u_ref, z_ref, w_ref, acc_ref):
    R, F = dm.R, dm.F
    total = None
    strips = None
    for a in range(3):
        for b in range(3):
            main = u_ref[2 - b, (2 - a) * dm.ROW : (2 - a + R) * dm.ROW]
            w = w_ref[3 * a + b]
            dims = (((1,), (1,)), ((), ()))
            term = lax.dot_general(main, w, dims, preferred_element_type=F32)
            strip = lax.dot_general(z_ref[3 * a + b].astype(BF), w, dims, preferred_element_type=F32)
            total = term if total is None else total + term
            strips = strip if strips is None else strips + strip
    acc_ref[...] = total
    for f in range(6):
        for side in range(2):
            for r in range(R):
                at = (r * 6 + f) * F + side * (F - 1)
                row = 16 * f + 8 * side + r
                acc_ref[at : at + 1] += strips[row : row + 1]

    @pl.when(t == 0)
    def _():
        acc_ref[0 : dm.ROW] += strips[dm.WE :]

    @pl.when(t == dm.T - 1)
    def _():
        acc_ref[(R - 1) * dm.ROW : R * dm.ROW] += strips[dm.WE :]


def put_tap(send_ref, keep_ref, p, tap, value):
    half = send_ref.shape[0] - EXTRA
    unit = value.shape[0] // 2
    for part in range(2):
        row = tap * 2 * unit + part * unit
        owner = row // half
        at = row - owner * half
        piece = value[part * unit : (part + 1) * unit]

        @pl.when(p == owner)
        def _():
            keep_ref[at : at + unit] = piece

        @pl.when(p != owner)
        def _():
            send_ref[at : at + unit] = piece.astype(BF)


def put_extra(send_ref, keep_ref, row):
    c = row.shape[1]
    n = send_ref.shape[0] - EXTRA
    i = lax.broadcasted_iota(jnp.int32, (EXTRA, c), 0)
    high = row.astype(BF)
    low = (row - high.astype(F32)).astype(BF).astype(F32)
    keep_ref[n:] = jnp.where(i == 0, row, 0.0)
    send_ref[n:] = jnp.where(i == 0, high.astype(F32), jnp.where(i == 1, low, 0.0)).astype(BF)


def first_kernel(dm, sc, x_ref, up_ref, w1_ref, bias_ref, w2_ref, *refs):
    T, R, F, N, C = dm.T, dm.R, dm.F, dm.N, dm.C
    messages = refs[:T]
    s1_ref, k1_ref, s2_ref, k2_ref, hid_ref, inner_ref = refs[T : T + 6]
    out_messages = refs[T + 6 : 2 * T + 6]
    table_ref, frame_ref, xs_ref, us_ref, z_ref, before_ref, acc_ref, hcat_ref = refs[2 * T + 6 :]
    t, p = sc[24], sc[25]
    own = (x_ref[...].reshape(N, C), up_ref[...].reshape(N, C))
    gx, gu = gather_ghosts(dm, sc, t, own, messages, table_ref)
    top, bottom = dm.WE, dm.WE + dm.ROW
    build_shifts(dm, x_ref, gx[:top], gx[top:bottom], gx[bottom:], frame_ref, xs_ref)
    total = None
    for a in range(3):
        for b in range(3):
            term = jnp.dot(
                xs_ref[b, a * dm.ROW : (a + R) * dm.ROW], w1_ref[3 * a + b], preferred_element_type=F32
            )
            total = term if total is None else total + term
    before = total + bias_ref[...]
    before_ref[...] = before
    sig = 1.0 / (1.0 + jnp.exp(-before))
    hidden = before * sig
    acc_ref[...] = hidden
    hidden_bf = hidden.astype(BF)
    up_top = jnp.where(t == 0, 0.0, gu[top:bottom])
    up_bottom = jnp.where(t == T - 1, 0.0, gu[bottom:])
    build_shifts(dm, up_ref, None, up_top, up_bottom, frame_ref, us_ref)
    build_strip_terms(dm, sc, t, gu[:top], gu[top:bottom], gu[bottom:], z_ref)
    hcat_ref[...] = jnp.zeros(hcat_ref.shape, F32)
    for f in range(6):
        for side in range(2):
            for r in range(R):
                at = (r * 6 + f) * F + side * (F - 1)
                row = 16 * f + 8 * side + r
                hcat_ref[row : row + 1] = acc_ref[at : at + 1]
    first_row = acc_ref[0 : dm.ROW]
    last_row = acc_ref[(R - 1) * dm.ROW : R * dm.ROW]
    hcat_ref[dm.WE :] = jnp.where(t == 0, first_row, last_row)
    hidden_t = hidden_bf.T
    edge_t = hcat_ref[...].astype(BF).T
    for a in range(3):
        for b in range(3):
            main = us_ref[2 - b, (2 - a) * dm.ROW : (2 - a + R) * dm.ROW]
            grad = jnp.dot(hidden_t, main, preferred_element_type=F32)
            grad = grad + jnp.dot(edge_t, z_ref[3 * a + b].astype(BF), preferred_element_type=F32)
            put_tap(s2_ref, k2_ref, p, 3 * a + b, grad)
    put_extra(s2_ref, k2_ref, jnp.zeros((1, C), F32))
    for r in range(R):
        for f in range(6):
            at = (r * 6 + f) * F
            hid_ref[f * R + r] = acc_ref[at : at + F].astype(BF)
    adjoint(dm, t, us_ref, z_ref, w2_ref, acc_ref)
    before = before_ref[...]
    sig = 1.0 / (1.0 + jnp.exp(-before))
    before_grad = acc_ref[...] * (sig * (1.0 + before * (1.0 - sig)))
    acc_ref[...] = before_grad
    inner = before_grad.astype(BF)
    for a in range(3):
        for b in range(3):
            grad = lax.dot_general(
                xs_ref[b, a * dm.ROW : (a + R) * dm.ROW],
                inner,
                (((0,), (0,)), ((), ())),
                preferred_element_type=F32,
            )
            put_tap(s1_ref, k1_ref, p, 3 * a + b, grad)
    put_extra(s1_ref, k1_ref, jnp.sum(before_grad, axis=0, keepdims=True))
    for r in range(R):
        for f in range(6):
            at = (r * 6 + f) * F
            inner_ref[f * R + r] = acc_ref[at : at + F].astype(BF)
    write_messages(
        dm, sc, t, (hid_ref[...].reshape(N, C), inner_ref[...].reshape(N, C)), out_messages
    )


def second_kernel(dm, sc, x_ref, d_ref, hid_ref, inner_ref, w1_ref, w2_ref, *refs):
    T, R, F, N, C = dm.T, dm.R, dm.F, dm.N, dm.C
    messages = refs[:T]
    state_ref, grad_ref = refs[T : T + 2]
    table_ref, frame_ref, shift_ref, z_ref, acc_ref = refs[T + 2 :]
    t = sc[24]
    own = (hid_ref[...].reshape(N, C), inner_ref[...].reshape(N, C))
    gh, gi = gather_ghosts(dm, sc, t, own, messages, table_ref)
    top, bottom = dm.WE, dm.WE + dm.ROW
    build_shifts(dm, hid_ref, gh[:top], gh[top:bottom], gh[bottom:], frame_ref, shift_ref)
    total = None
    for a in range(3):
        for b in range(3):
            term = jnp.dot(
                shift_ref[b, a * dm.ROW : (a + R) * dm.ROW],
                w2_ref[3 * a + b],
                preferred_element_type=F32,
            )
            total = term if total is None else total + term
    acc_ref[...] = total
    for r in range(R):
        for f in range(6):
            at = (r * 6 + f) * F
            value = x_ref[f * R + r].astype(F32) + acc_ref[at : at + F]
            state_ref[f * R + r] = value.astype(BF)
    in_top = jnp.where(t == 0, 0.0, gi[top:bottom])
    in_bottom = jnp.where(t == T - 1, 0.0, gi[bottom:])
    build_shifts(dm, inner_ref, None, in_top, in_bottom, frame_ref, shift_ref)
    build_strip_terms(dm, sc, t, gi[:top], gi[top:bottom], gi[bottom:], z_ref)
    adjoint(dm, t, shift_ref, z_ref, w1_ref, acc_ref)
    for r in range(R):
        for f in range(6):
            at = (r * 6 + f) * F
            grad_ref[f * R + r] = d_ref[f * R + r].astype(F32) + acc_ref[at : at + F]


def extra_sum(keep, recv, n):
    return keep[n : n + 1] + recv[n : n + 1].astype(F32) + recv[n + 1 : n + 2].astype(F32)


def halve_kernel(pieces, shift, sc, keep_ref, recv_ref, *refs):
    out_keep, out_sends, sum_ref = refs[0], refs[1:pieces], refs[pieces]
    n = keep_ref.shape[0] - EXTRA
    size = n // pieces
    own = sc[24] % 2 if shift == 0 else sc[24] // 2
    sum_ref[...] = keep_ref[0:n] + recv_ref[0:n].astype(F32)
    extra = extra_sum(keep_ref, recv_ref, n)
    out_keep[0:size] = sum_ref[pl.ds(pl.multiple_of(own * size, 8), size)]
    i = lax.broadcasted_iota(jnp.int32, (EXTRA, extra.shape[1]), 0)
    high = extra.astype(BF).astype(F32)
    out_keep[size:] = jnp.where(i == 0, extra, 0.0)
    tail = jnp.where(i == 0, high, jnp.where(i == 1, extra - high, 0.0)).astype(BF)
    for j in range(1, pieces):
        at = pl.multiple_of((own ^ j) * size, 8)
        out_sends[j - 1][0:size] = sum_ref[pl.ds(at, size)].astype(BF)
        out_sends[j - 1][size:] = tail


def last_kernel(keep_ref, *refs):
    recvs, (block_ref, extra_ref) = refs[:-2], refs[-2:]
    n = keep_ref.shape[0] - EXTRA
    total = keep_ref[0:n]
    extra = keep_ref[n : n + 1]
    for ref in recvs:
        total = total + ref[0:n].astype(F32)
        extra = extra + ref[n : n + 1].astype(F32) + ref[n + 1 : n + 2].astype(F32)
    block_ref[...] = total.astype(BF)
    extra_ref[...] = jnp.broadcast_to(extra, extra_ref.shape)


def normal_kernel(zcount, sc, a_ref, b_ref, c_ref, d_ref, extra_ref, out_ref, bias_ref):
    t, p = sc[24], sc[25]
    refs = (a_ref, b_ref, c_ref, d_ref)
    square = None
    for ref in refs:
        v = ref[...].astype(F32)
        s = jnp.sum(v * v, axis=0, keepdims=True)
        square = s if square is None else square + s
    mean = jnp.sum(square, keepdims=True) / (out_ref.shape[0] * out_ref.shape[1])
    scale = lax.rsqrt(mean + 1e-06)
    size = a_ref.shape[0] // zcount
    for index, ref in enumerate(refs):
        block = (p ^ (index // 2)) * 2 + ((t % 2) ^ (index % 2))
        for j in range(zcount):
            at = (block * zcount + ((t // 2) ^ j)) * size
            value = ref[j * size : (j + 1) * size].astype(F32) * scale
            out_ref[pl.ds(pl.multiple_of(at, 8), size)] = value
    extra = extra_ref[0:1]
    bias_mean = jnp.mean(extra * extra, keepdims=True)
    bias_ref[...] = jnp.broadcast_to(extra * lax.rsqrt(bias_mean + 1e-06), bias_ref.shape)


def call(kernel, out_shapes, scratch=(), smem_first=True):
    def run(*args):
        vmem = pl.BlockSpec(memory_space=pltpu.VMEM)
        smem = pl.BlockSpec(memory_space=pltpu.SMEM)
        specs = [smem if smem_first and i == 0 else vmem for i in range(len(args))]
        return pl.pallas_call(
            kernel,
            out_shape=[jax.ShapeDtypeStruct(s, dt) for s, dt in out_shapes],
            in_specs=specs,
            out_specs=[vmem] * len(out_shapes),
            scratch_shapes=[pltpu.VMEM(s, dt) for s, dt in scratch],
            compiler_params=pltpu.CompilerParams(vmem_limit_bytes=56 << 20),
        )(*args)

    return run


def exchange(tiles, messages):
    return [messages[0]] + [
        lax.ppermute(messages[k], "tile", [(i, i ^ k) for i in range(tiles)]) for k in range(1, tiles)
    ]


def swap_dp(v):
    count = lax.axis_size("dp")
    return lax.ppermute(v, "dp", [(i, count - 1 - i) for i in range(count)])


def on_device(initial_state, state_cotangents, w_first, bias, w_second, edge_partner):
    tiles = lax.axis_size("tile")
    _, _, rows, face, channels = initial_state.shape
    dm = Dims(rows, face, tiles, channels)
    planes = (6 * rows, face, channels)
    sc = jnp.concatenate(
        [
            edge_partner.reshape(24).astype(jnp.int32),
            lax.axis_index("tile")[None].astype(jnp.int32),
            lax.axis_index("dp")[None].astype(jnp.int32),
        ]
    )
    x = initial_state.reshape(planes)
    d = state_cotangents[state_cotangents.shape[0] - 1].reshape(planes)
    w1 = w_first.reshape(9, channels, channels)
    w2 = w_second.reshape(9, channels, channels)
    msg_shapes = [((2, dm.msg_rows(k), channels), BF) for k in range(tiles)]
    flat = (dm.N, channels)
    messages = call(functools.partial(pack_kernel, dm), msg_shapes)(sc, x.reshape(flat), d.reshape(flat))
    messages = exchange(tiles, messages)
    half = 9 * channels // 2 + EXTRA
    shift_rows = (3, (rows + 2) * dm.ROW, channels)
    frame = (rows + 2, 6, face + 16, channels)
    outs = call(
        functools.partial(first_kernel, dm),
        [((half, channels), BF), ((half, channels), F32)] * 2 + [(planes, BF)] * 2 + msg_shapes,
        [
            ((dm.NT, channels), BF),
            (frame, F32),
            (shift_rows, BF),
            (shift_rows, BF),
            ((9, dm.S, channels), F32),
            (flat, F32),
            (flat, F32),
            ((dm.S, channels), F32),
        ],
    )(sc, x, d, w1, bias.reshape(1, channels), w2, *messages)
    send_first, keep_first, send_second, keep_second, hidden, inner = outs[:6]

    zcount = tiles // 2

    def reduced(send, keep):
        recv = swap_dp(send)
        n = (half - EXTRA) // 2
        keep, send = call(
            functools.partial(halve_kernel, 2, 0),
            [((n + EXTRA, channels), F32), ((n + EXTRA, channels), BF)],
            [((2 * n, channels), F32)],
        )(sc, keep, recv)
        recv = lax.ppermute(send, "tile", [(i, i ^ 1) for i in range(tiles)])
        m = n // zcount
        keep, *sends = call(
            functools.partial(halve_kernel, zcount, 1),
            [((m + EXTRA, channels), F32)] + [((m + EXTRA, channels), BF)] * (zcount - 1),
            [((n, channels), F32)],
        )(sc, keep, recv)
        recvs = [
            lax.ppermute(v, "tile", [(i, i ^ (2 * (j + 1))) for i in range(tiles)])
            for j, v in enumerate(sends)
        ]
        block, extra = call(last_kernel, [((m, channels), BF), ((8, channels), F32)], smem_first=False)(
            keep, *recvs
        )
        blocks = [block] + [
            lax.ppermute(block, "tile", [(i, i ^ (2 * j)) for i in range(tiles)])
            for j in range(1, zcount)
        ]
        own = jnp.concatenate(blocks, axis=0)
        other = lax.ppermute(own, "tile", [(i, i ^ 1) for i in range(tiles)])
        far_own = swap_dp(own)
        far_other = swap_dp(other)
        return call(
            functools.partial(normal_kernel, zcount),
            [((9 * channels, channels), F32), ((8, channels), F32)],
        )(sc, own, other, far_own, far_other, extra)

    second_step, _ = reduced(send_second, keep_second)
    first_step, bias_step = reduced(send_first, keep_first)

    messages = exchange(tiles, outs[6:])
    state, grad = call(
        functools.partial(second_kernel, dm),
        [(planes, BF), (planes, F32)],
        [
            ((dm.NT, channels), BF),
            (frame, F32),
            (shift_rows, BF),
            ((9, dm.S, channels), F32),
            (flat, F32),
        ],
    )(sc, x, d, hidden, inner, w1, w2, *messages)
    return (
        state.reshape(initial_state.shape),
        grad.reshape(initial_state.shape),
        first_step.reshape(w_first.shape),
        bias_step[0],
        second_step.reshape(w_second.shape),
    )


def solution(mesh):
    return jax.shard_map(
        on_device,
        mesh=mesh,
        in_specs=(
            P(("groups", "dp"), None, "tile", None, None),
            P(None, ("groups", "dp"), None, "tile", None, None),
            P(),
            P(),
            P(),
            P(),
        ),
        out_specs=(
            P(("groups", "dp"), None, "tile", None, None),
            P(("groups", "dp"), None, "tile", None, None),
            P("groups", None, None, None),
            P("groups"),
            P("groups", None, None, None),
        ),
        check_vma=False,
    )
```

time: 493 us -> 153 us (0.31); the launches traced: 484 us -> 152 us
  waiting for transfers between devices: 262 us -> 46.2 us
  local copies, waits for them, and re-layouts: 112 us -> 11.5 us
  other arithmetic: 45.4 us -> 0.58 us
  Pallas kernels: 0 us -> 44.7 us
  starting transfers between devices: 24.3 us -> 47.9 us
  matrix products: 22.4 us -> 0 us
  between operations: 18.2 us -> 1.01 us
    psum x3 -> x0, waiting for transfers between devices: 259 us -> none  [the longest x2 146 us: pad_local(): lax.psum(tile_strips(grid_field, tile_index, tile_count), 'tile')]
    scatter-add x24 -> x0, local copies, waits for them, and re-layouts: 70.8 us -> none  [the longest x16 45.7 us: convolve_back(): framed = framed.at[:, :, tap_row:tap_row + row_count, tap_col:tap_col + c...]
    pallas_call x0 -> x11, Pallas kernels: none -> 44.7 us  [run(): pl.pallas_call(kernel, out_shape=[jax.ShapeDtypeStruct(s, dt) for s, dt i...]
    ppermute x8 -> x36, waiting for transfers between devices: 2.04 us -> 46.2 us  [the longest x14 37.4 us: exchange(): lax.ppermute(messages[k], 'tile', [(i, i ^ k) for i in range(tiles)])]
    ppermute x8 -> x36, starting transfers between devices: 24.2 us -> 47.9 us  [the longest x14 22.4 us: exchange(): lax.ppermute(messages[k], 'tile', [(i, i ^ k) for i in range(tiles)])]
    dot_general x54 -> x0, matrix products: 22.4 us -> none  [the longest x18 13.4 us: convolve_back(): lax.dot_general(flat_rows, weights[tap_row, tap_col], (((1,), (1,)), ((),...]
    add x16 -> x0, other arithmetic: 14.5 us -> none  [the longest x7 8.84 us: convolve_back(): framed = framed.at[:, :, tap_row:tap_row + row_count, tap_col:tap_col + c...]
    another operation x11 -> x0, other arithmetic: 8.13 us -> none
  transfers between devices with their start and end apart: 11 -> 36, of which waited for: 4 -> 12; matrix products, arithmetic and copies ran while one was open for 6% -> 2% of each run, Pallas kernels for 0% -> 15%
where the time goes in v1:
time: 153 us; the launch traced here: 152 us
  starting transfers between devices  47.9 us (31%)
  waiting for transfers between devices  46.2 us (30%)
  Pallas kernels  44.7 us (29%)
  local copies, waits for them, and re-layouts  11.5 us (8%)
    pallas_call x11, Pallas kernels, run(): pl.pallas_call(kernel, out_shape=[jax.ShapeDtypeStruct(s, dt) for s, dt i...  44.7 us
    ppermute x14, waiting for transfers between devices, exchange(): lax.ppermute(messages[k], 'tile', [(i, i ^ k) for i in range(tiles)])  37.4 us
    ppermute x14, starting transfers between devices, exchange(): lax.ppermute(messages[k], 'tile', [(i, i ^ k) for i in range(tiles)])  22.4 us
    unnamed x85, local copies, waits for them, and re-layouts  10.2 us
    ppermute x6, starting transfers between devices, reduced(): lax.ppermute(block, 'tile', [(i, i ^ 2 * j) for i in range(tiles)])  9 us
    ppermute x6, starting transfers between devices, reduced(): lax.ppermute(v, 'tile', [(i, i ^ 2 * (j + 1)) for i in range(tiles)])  8.84 us
    ppermute x2, waiting for transfers between devices, reduced(): recv = lax.ppermute(send, 'tile', [(i, i ^ 1) for i in range(tiles)])  4.78 us
    ppermute x2, starting transfers between devices, reduced(): other = lax.ppermute(own, 'tile', [(i, i ^ 1) for i in range(tiles)])  4.1 us
  transfers between devices with their start and end apart: 36, of which 12 were waited for; matrix products, arithmetic and copies ran while one was open for 2% of the time, Pallas kernels for 15%

profile of v1, /device:TPU:0, one launch (start us, length us, event | category | flops | bytes accessed | tf_op | source)
XLA Modules:
  0.0 152.0 jit_solution(8525816828180263307)
XLA Ops:
  0.6 0.8 copy.12
  1.5 0.6 pad_add_fusion.sc
  2.1 3.2 %shard_map.101 = (bf16[2,64,256]{2,1,0:T(8,128)(2,1)}, bf16[2,208,256]{2,1,0:T(8,128)(2,1)}, bf16[2,64,256]{2,1,0:T(8,128)(2,1)}, bf16[2,208,256]{2,1,0:T(8,128)...) custom-call(s32[26]{0:T(128)} %pad_add_fusion.sc, ...), custom_call_target="tpu_custom_call" | custom-call | tf_op jit(solution)/shard_map/pallas_call | solution.py:509
  5.2 6.0 %collective-permute-start.6 = (bf16[2,256,256]{2,1,0:T(8,128)(2,1)}, bf16[2,256,256]{2,1,0:T(8,128)(2,1)S(1)}, u32[]{:S(2)}, u32[]{:S(2)}) collective-permute-start(bf16[2,256,256]{2,1,0:T(8,128)(2,1)} %get-tuple-element.55), channel_id=1, source_target_pairs={{0,14},{2,12},{4,10},{6,8},{8,6},{10,4},{12,2},{14,0},{1,15},{3,13... | collective-permute-start | bytes 786440 | tf_op jit(solution)/shard_map/ppermute | solution.py:523
  11.3 0.5 collective-permute-start
  11.8 0.5 collective-permute-start.2
  12.3 2.5 %collective-permute-start.1 = (bf16[2,64,256]{2,1,0:T(8,128)(2,1)}, bf16[2,64,256]{2,1,0:T(8,128)(2,1)S(1)}, u32[]{:S(2)}, u32[]{:S(2)}) collective-permute-start(bf16[2,64,256]{2,1,0:T(8,128)(2,1)} %get-tuple-element.50), channel_id=1, source_target_pairs={{0,4},{2,6},{4,0},{6,2},{8,12},{10,14},{12,8},{14,10},{1,5},{3,7},... | collective-permute-start | bytes 196616 | tf_op jit(solution)/shard_map/ppermute | solution.py:523
  14.7 11.2 %collective-permute-done.1.refs_2_ = bf16[2,64,256]{2,1,0:T(8,128)(2,1)S(1)} collective-permute-done((bf16[2,64,256]{2,1,0:T(8,128)(2,1)}, bf16[2,64,256]{2,1,0:T(8,128)(2,1)S(1)}, u32[]{:S(2)}, u32[]{:S(2)}) %collective-permute-start.1) | collective-permute-done | bytes 65568 | tf_op jit(solution)/shard_map/ppermute | solution.py:523
  25.9 0.5 collective-permute-start.4
  26.4 0.7 collective-permute-done.3.refs_4_
  27.1 3.3 %collective-permute-start.5 = (bf16[2,64,256]{2,1,0:T(8,128)(2,1)}, bf16[2,64,256]{2,1,0:T(8,128)(2,1)S(1)}, u32[]{:S(2)}, u32[]{:S(2)}) collective-permute-start(bf16[2,64,256]{2,1,0:T(8,128)(2,1)} %get-tuple-element.54), channel_id=1, source_target_pairs={{0,12},{2,14},{4,8},{6,10},{8,4},{10,6},{12,0},{14,2},{1,13},{3,15... | collective-permute-start | bytes 196616 | tf_op jit(solution)/shard_map/ppermute | solution.py:523
  30.4 2.4 %collective-permute-done.4.refs_5_ = bf16[2,64,256]{2,1,0:T(8,128)(2,1)S(1)} collective-permute-done((bf16[2,64,256]{2,1,0:T(8,128)(2,1)}, bf16[2,64,256]{2,1,0:T(8,128)(2,1)S(1)}, u32[]{:S(2)}, u32[]{:S(2)}) %collective-permute-start.4) | collective-permute-done | bytes 65568 | tf_op jit(solution)/shard_map/ppermute | solution.py:523
  32.8 0.8 collective-permute-done.5.refs_6_
  33.7 0.6 copy-done.31
  34.5 15.6 %shard_map.102 = (bf16[1168,256]{1,0:T(8,128)(2,1)}, f32[1168,256]{1,0:T(8,128)}, bf16[1168,256]{1,0:T(8,128)(2,1)}, f32[1168,256]{1,0:T(8,128)}, bf16[18,24,256...) custom-call(s32[26]{0:T(128)} %pad_add_fusion.sc, ...), custom_call_target="tpu_custom_call" | custom-call | tf_op jit(solution)/shard_map/pallas_call | solution.py:509
  50.2 0.5 collective-permute-start.25
  50.7 1.7 %collective-permute-done.14.recv_ref = bf16[1168,256]{1,0:T(8,128)(2,1)S(1)} collective-permute-done((bf16[1168,256]{1,0:T(8,128)(2,1)}, bf16[1168,256]{1,0:T(8,128)(2,1)S(1)}, u32[]{:S(2)}, u32[]{:S(2)}) %collective-permute-start.14) | collective-permute-done | bytes 598048 | tf_op jit(solution)/shard_map/ppermute | solution.py:529
  52.4 0.8 copy-done.1
  53.3 2.6 %shard_map.104 = (f32[592,256]{1,0:T(8,128)}, bf16[592,256]{1,0:T(8,128)(2,1)}) custom-call(s32[26]{0:T(128)} %pad_add_fusion.sc, f32[1168,256]{1,0:T(8,128)} %get-tuple-element.68.keep_ref, bf16[1168,256]{1,0:T(8,128)(2,1)} %copy-done.1), custom_call_target="tpu_custom_call" | custom-call | tf_op jit(solution)/shard_map/pallas_call | solution.py:509
  55.9 1.7 %collective-permute-start.15 = (bf16[592,256]{1,0:T(8,128)(2,1)}, bf16[592,256]{1,0:T(8,128)(2,1)S(1)}, u32[]{:S(2)}, u32[]{:S(2)}) collective-permute-start(bf16[592,256]{1,0:T(8,128)(2,1)} %get-tuple-element.71), channel_id=1, source_target_pairs={{0,2},{2,0},{4,6},{6,4},{8,10},{10,8},{12,14},{14,12},{1,3},{3,1},... | collective-permute-start | bytes 909320 | tf_op jit(solution)/shard_map/ppermute | solution.py:581
  57.5 0.8 copy-done
  58.3 2.6 %shard_map.108 = (f32[592,256]{1,0:T(8,128)}, bf16[592,256]{1,0:T(8,128)(2,1)}) custom-call(s32[26]{0:T(128)} %pad_add_fusion.sc, f32[1168,256]{1,0:T(8,128)} %get-tuple-element.80.keep_ref, bf16[1168,256]{1,0:T(8,128)(2,1)} %copy-done), custom_call_target="tpu_custom_call" | custom-call | tf_op jit(solution)/shard_map/pallas_call | solution.py:509
  61.3 4.8 %collective-permute-done.15.recv_ref = bf16[592,256]{1,0:T(8,128)(2,1)S(1)} collective-permute-done((bf16[592,256]{1,0:T(8,128)(2,1)}, bf16[592,256]{1,0:T(8,128)(2,1)S(1)}, u32[]{:S(2)}, u32[]{:S(2)}) %collective-permute-start.15) | collective-permute-done | bytes 303136 | tf_op jit(solution)/shard_map/ppermute | solution.py:581
  66.1 0.7 copy-done.5
  66.8 2.0 %shard_map.105 = (f32[160,256]{1,0:T(8,128)}, bf16[160,256]{1,0:T(8,128)(2,1)}, bf16[160,256]{1,0:T(8,128)(2,1)}, bf16[160,256]{1,0:T(8,128)(2,1)}) custom-call(s32[26]{0:T(128)} %pad_add_fusion.sc, f32[592,256]{1,0:T(8,128)} %get-tuple-element.70.keep_ref, bf16[592,256]{1,0:T(8,128)(2,1)} %copy-done.5), custom_call_target="tpu_custom_call" | custom-call | tf_op jit(solution)/shard_map/pallas_call | solution.py:509
  68.8 1.2 collective-permute-start.16
  70.0 2.3 %collective-permute-start.17 = (bf16[160,256]{1,0:T(8,128)(2,1)}, bf16[160,256]{1,0:T(8,128)(2,1)S(1)}, u32[]{:S(2)}, u32[]{:S(2)}) collective-permute-start(bf16[160,256]{1,0:T(8,128)(2,1)} %get-tuple-element.74), channel_id=1, source_target_pairs={{0,8},{2,10},{4,12},{6,14},{8,0},{10,2},{12,4},{14,6},{1,9},{3,11}... | collective-permute-start | bytes 245768 | tf_op jit(solution)/shard_map/ppermute | solution.py:589
  72.3 0.9 collective-permute-start.18
  73.2 0.7 copy-done.4
  73.9 2.0 %shard_map.109 = (f32[160,256]{1,0:T(8,128)}, bf16[160,256]{1,0:T(8,128)(2,1)}, bf16[160,256]{1,0:T(8,128)(2,1)}, bf16[160,256]{1,0:T(8,128)(2,1)}) custom-call(s32[26]{0:T(128)} %pad_add_fusion.sc, f32[592,256]{1,0:T(8,128)} %get-tuple-element.82.keep_ref, bf16[592,256]{1,0:T(8,128)(2,1)} %copy-done.4), custom_call_target="tpu_custom_call" | custom-call | tf_op jit(solution)/shard_map/pallas_call | solution.py:509
  76.3 3.2 %collective-permute-start.28 = (bf16[160,256]{1,0:T(8,128)(2,1)}, bf16[160,256]{1,0:T(8,128)(2,1)S(1)}, u32[]{:S(2)}, u32[]{:S(2)}) collective-permute-start(bf16[160,256]{1,0:T(8,128)(2,1)} %get-tuple-element.86), channel_id=1, source_target_pairs={{0,8},{2,10},{4,12},{6,14},{8,0},{10,2},{12,4},{14,6},{1,9},{3,11}... | collective-permute-start | bytes 245768 | tf_op jit(solution)/shard_map/ppermute | solution.py:589
  79.5 0.9 collective-permute-start.29
  80.4 0.6 copy-done.22
  81.1 1.7 %shard_map.106 = (bf16[144,256]{1,0:T(8,128)(2,1)}, f32[8,256]{1,0:T(8,128)}) custom-call(f32[160,256]{1,0:T(8,128)} %get-tuple-element.72.keep_ref, bf16[160,256]{1,0:T(8,128)(2,1)} %copy-done.20, bf16[160,256]{1,0:T(8,128)(2,1)} %copy-done.22, bf16[160,256]{1,0:T(8,128)(2,1)} %copy-done.23), custom_call_target="tpu_custom_call" | custom-call | tf_op jit(solution)/shard_map/pallas_call | solution.py:509
  82.8 2.9 %collective-permute-start.21 = (bf16[144,256]{1,0:T(8,128)(2,1)}, bf16[144,256]{1,0:T(8,128)(2,1)S(1)}, u32[]{:S(2)}, u32[]{:S(2)}) collective-permute-start(bf16[144,256]{1,0:T(8,128)(2,1)} %get-tuple-element.76), channel_id=1, source_target_pairs={{0,12},{2,14},{4,8},{6,10},{8,4},{10,6},{12,0},{14,2},{1,13},{3,15... | collective-permute-start | bytes 221192 | tf_op jit(solution)/shard_map/ppermute | solution.py:596
  85.7 1.0 constant_dynamic-update-slice_fusion.3
  86.7 1.5 collective-permute-start.19
  88.2 0.6 copy-done.19
  88.8 1.7 %shard_map.110 = (bf16[144,256]{1,0:T(8,128)(2,1)}, f32[8,256]{1,0:T(8,128)}) custom-call(f32[160,256]{1,0:T(8,128)} %get-tuple-element.84.keep_ref, bf16[160,256]{1,0:T(8,128)(2,1)} %copy-done.18, bf16[160,256]{1,0:T(8,128)(2,1)} %copy-done.19, bf16[160,256]{1,0:T(8,128)(2,1)} %copy-done.21), custom_call_target="tpu_custom_call" | custom-call | tf_op jit(solution)/shard_map/pallas_call | solution.py:509
  90.6 2.9 %collective-permute-start.32 = (bf16[144,256]{1,0:T(8,128)(2,1)}, bf16[144,256]{1,0:T(8,128)(2,1)S(1)}, u32[]{:S(2)}, u32[]{:S(2)}) collective-permute-start(bf16[144,256]{1,0:T(8,128)(2,1)} %get-tuple-element.88), channel_id=1, source_target_pairs={{0,12},{2,14},{4,8},{6,10},{8,4},{10,6},{12,0},{14,2},{1,13},{3,15... | collective-permute-start | bytes 221192 | tf_op jit(solution)/shard_map/ppermute | solution.py:596
  93.5 1.0 collective-permute-start.31
  94.5 0.9 constant_dynamic-update-slice_fusion.7
  95.4 0.7 collective-permute-start.30
  96.1 1.9 %collective-permute-start.22 = (bf16[576,256]{1,0:T(8,128)(2,1)S(1)}, bf16[576,256]{1,0:T(8,128)(2,1)S(1)}, u32[]{:S(2)}, u32[]{:S(2)}) collective-permute-start(bf16[576,256]{1,0:T(8,128)(2,1)S(1)} %constant_dynamic-update-slice_fusion.a_ref), channel_id=1, source_target_pairs={{0,2},{2,0},{4,6},{6,4},{8,10},{10,8},{12,14},{14,12},{1,3},{3,1},... | collective-permute-start | bytes 884744 | tf_op jit(solution)/shard_map/ppermute | solution.py:600
  98.0 2.3 %collective-permute-done.30 = bf16[144,256]{1,0:T(8,128)(2,1)S(1)} collective-permute-done((bf16[144,256]{1,0:T(8,128)(2,1)}, bf16[144,256]{1,0:T(8,128)(2,1)S(1)}, u32[]{:S(2)}, u32[]{:S(2)}) %collective-permute-start.30) | collective-permute-done | bytes 73760 | tf_op jit(solution)/shard_map/ppermute | solution.py:596
  100.4 2.2 %collective-permute-start.33 = (bf16[576,256]{1,0:T(8,128)(2,1)S(1)}, bf16[576,256]{1,0:T(8,128)(2,1)S(1)}, u32[]{:S(2)}, u32[]{:S(2)}) collective-permute-start(bf16[576,256]{1,0:T(8,128)(2,1)S(1)} %constant_dynamic-update-slice_fusion.4.a_ref), channel_id=1, source_target_pairs={{0,2},{2,0},{4,6},{6,4},{8,10},{10,8},{12,14},{14,12},{1,3},{3,1},... | collective-permute-start | bytes 884744 | tf_op jit(solution)/shard_map/ppermute | solution.py:600
  102.9 0.4 collective-permute-start.7
  103.3 3.8 %collective-permute-start.10 = (bf16[2,64,256]{2,1,0:T(8,128)(2,1)S(1)}, bf16[2,64,256]{2,1,0:T(8,128)(2,1)S(1)}, u32[]{:S(2)}, u32[]{:S(2)}) collective-permute-start(bf16[2,64,256]{2,1,0:T(8,128)(2,1)S(1)} %copy-done.37), channel_id=1, source_target_pairs={{0,8},{2,10},{4,12},{6,14},{8,0},{10,2},{12,4},{14,6},{1,9},{3,11}... | collective-permute-start | bytes 196616 | tf_op jit(solution)/shard_map/ppermute | solution.py:523
  107.8 2.6 %collective-permute-done.10.refs_4_ = bf16[2,64,256]{2,1,0:T(8,128)(2,1)S(1)} collective-permute-done((bf16[2,64,256]{2,1,0:T(8,128)(2,1)S(1)}, bf16[2,64,256]{2,1,0:T(8,128)(2,1)S(1)}, u32[]{:S(2)}, u32[]{:S(2)}) %collective-permute-start.10) | collective-permute-done | bytes 65568 | tf_op jit(solution)/shard_map/ppermute | solution.py:523
  110.4 1.4 collective-permute-start.11
  111.9 4.9 %collective-permute-done.11.refs_5_ = bf16[2,64,256]{2,1,0:T(8,128)(2,1)S(1)} collective-permute-done((bf16[2,64,256]{2,1,0:T(8,128)(2,1)S(1)}, bf16[2,64,256]{2,1,0:T(8,128)(2,1)S(1)}, u32[]{:S(2)}, u32[]{:S(2)}) %collective-permute-start.11) | collective-permute-done | bytes 65568 | tf_op jit(solution)/shard_map/ppermute | solution.py:523
  116.7 1.2 collective-permute-start.12
  117.9 4.9 %collective-permute-done.12.refs_6_ = bf16[2,64,256]{2,1,0:T(8,128)(2,1)S(1)} collective-permute-done((bf16[2,64,256]{2,1,0:T(8,128)(2,1)S(1)}, bf16[2,64,256]{2,1,0:T(8,128)(2,1)S(1)}, u32[]{:S(2)}, u32[]{:S(2)}) %collective-permute-start.12) | collective-permute-done | bytes 65568 | tf_op jit(solution)/shard_map/ppermute | solution.py:523
  122.8 0.5 collective-permute-start.24
  123.4 0.4 collective-permute-start.35
  123.8 1.7 %collective-permute-start.13 = (bf16[2,256,256]{2,1,0:T(8,128)(2,1)S(1)}, bf16[2,256,256]{2,1,0:T(8,128)(2,1)S(1)}, u32[]{:S(2)}, u32[]{:S(2)}) collective-permute-start(bf16[2,256,256]{2,1,0:T(8,128)(2,1)S(1)} %copy-done.32), channel_id=1, source_target_pairs={{0,14},{2,12},{4,10},{6,8},{8,6},{10,4},{12,2},{14,0},{1,15},{3,13... | collective-permute-start | bytes 786440 | tf_op jit(solution)/shard_map/ppermute | solution.py:523
  125.6 9.4 %collective-permute-done.13.refs_7_ = bf16[2,256,256]{2,1,0:T(8,128)(2,1)S(1)} collective-permute-done((bf16[2,256,256]{2,1,0:T(8,128)(2,1)S(1)}, bf16[2,256,256]{2,1,0:T(8,128)(2,1)S(1)}, u32[]{:S(2)}, u32[]{:S(2)}) %collective-permute-start.13) | collective-permute-done | bytes 262176 | tf_op jit(solution)/shard_map/ppermute | solution.py:523
  135.0 0.7 copy-done.13
  135.7 7.3 %shard_map.103 = (bf16[18,24,256]{2,1,0:T(8,128)(2,1)}, f32[18,24,256]{2,1,0:T(8,128)}) custom-call(s32[26]{0:T(128)} %pad_add_fusion.sc, bf16[18,24,256]{2,1,0:T(8,128)(2,1)} %bitcast.20, bf16[18,24,256]{2,1,0:T(8,128)(2,1)} %bitcast.23, bf16[18,24,256]{2,1,0:T(8,128)(2,1)} %get-tuple-element.56.hid_ref, bf16[18,24,256]{2,1,0:T(8,128)(2,1)} %get-tuple-element.57.inner_ref, ...), custom_call_target="tpu_custom_call" | custom-call | tf_op jit(solution)/shard_map/pallas_call | solution.py:509
  143.1 0.7 copy-done.9
  143.9 3.0 %shard_map.107 = (f32[2304,256]{1,0:T(8,128)}, f32[8,256]{1,0:T(8,128)}) custom-call(s32[26]{0:T(128)} %pad_add_fusion.sc, bf16[576,256]{1,0:T(8,128)(2,1)} %copy-done.2, bf16[576,256]{1,0:T(8,128)(2,1)} %copy-done.6, bf16[576,256]{1,0:T(8,128)(2,1)} %copy-done.9, bf16[576,256]{1,0:T(8,128)(2,1)} %copy-done.11, f32[8,256]{1,0:T(8,128)} %get-tuple-element.77.extra_ref), custom_call_target="tpu_custom_call" | custom-call | tf_op jit(solution)/shard_map/pallas_call | solution.py:509
  146.9 1.3 slice.3
  148.2 0.7 copy-done.8
  149.0 3.0 %shard_map.111 = (f32[2304,256]{1,0:T(8,128)}, f32[8,256]{1,0:T(8,128)}) custom-call(s32[26]{0:T(128)} %pad_add_fusion.sc, bf16[576,256]{1,0:T(8,128)(2,1)} %copy-done.3, bf16[576,256]{1,0:T(8,128)(2,1)} %copy-done.7, bf16[576,256]{1,0:T(8,128)(2,1)} %copy-done.8, bf16[576,256]{1,0:T(8,128)(2,1)} %copy-done.10, f32[8,256]{1,0:T(8,128)} %get-tuple-element.89.extra_ref), custom_call_target="tpu_custom_call" | custom-call | tf_op jit(solution)/shard_map/pallas_call | solution.py:509
  (109 shorter events, 2.6 us)
Async XLA Ops:
  5.2 28.4 %collective-permute-start.6 = (bf16[2,256,256]{2,1,0:T(8,128)(2,1)}, bf16[2,256,256]{2,1,0:T(8,128)(2,1)S(1)}, u32[]{:S(2)}, u32[]{:S(2)}) collective-permute-start(bf16[2,256,256]{2,1,0:T(8,128)(2,1)} %get-tuple-element.55), channel_id=1, source_target_pairs={{0,14},{2,12},{4,10},{6,8},{8,6},{10,4},{12,2},{14,0},{1,15},{3,13... | collective-permute-start | bytes 786440 | tf_op jit(solution)/shard_map/ppermute | solution.py:523
  11.3 22.4 %collective-permute-start = (bf16[2,208,256]{2,1,0:T(8,128)(2,1)}, bf16[2,208,256]{2,1,0:T(8,128)(2,1)S(1)}, u32[]{:S(2)}, u32[]{:S(2)}) collective-permute-start(bf16[2,208,256]{2,1,0:T(8,128)(2,1)} %get-tuple-element.49), channel_id=1, source_target_pairs={{0,2},{2,0},{4,6},{6,4},{8,10},{10,8},{12,14},{14,12},{1,3},{3,1},... | collective-permute-start | bytes 638984 | tf_op jit(solution)/shard_map/ppermute | solution.py:523
  11.8 21.9 %collective-permute-start.2 = (bf16[2,208,256]{2,1,0:T(8,128)(2,1)}, bf16[2,208,256]{2,1,0:T(8,128)(2,1)S(1)}, u32[]{:S(2)}, u32[]{:S(2)}) collective-permute-start(bf16[2,208,256]{2,1,0:T(8,128)(2,1)} %get-tuple-element.51), channel_id=1, source_target_pairs={{0,6},{2,4},{4,2},{6,0},{8,14},{10,12},{12,10},{14,8},{1,7},{3,5},... | collective-permute-start | bytes 638984 | tf_op jit(solution)/shard_map/ppermute | solution.py:523
  12.3 13.7 %collective-permute-start.1 = (bf16[2,64,256]{2,1,0:T(8,128)(2,1)}, bf16[2,64,256]{2,1,0:T(8,128)(2,1)S(1)}, u32[]{:S(2)}, u32[]{:S(2)}) collective-permute-start(bf16[2,64,256]{2,1,0:T(8,128)(2,1)} %get-tuple-element.50), channel_id=1, source_target_pairs={{0,4},{2,6},{4,0},{6,2},{8,12},{10,14},{12,8},{14,10},{1,5},{3,7},... | collective-permute-start | bytes 196616 | tf_op jit(solution)/shard_map/ppermute | solution.py:523
  14.7 12.4 %collective-permute-start.3 = (bf16[2,64,256]{2,1,0:T(8,128)(2,1)}, bf16[2,64,256]{2,1,0:T(8,128)(2,1)S(1)}, u32[]{:S(2)}, u32[]{:S(2)}) collective-permute-start(bf16[2,64,256]{2,1,0:T(8,128)(2,1)} %get-tuple-element.52), channel_id=1, source_target_pairs={{0,8},{2,10},{4,12},{6,14},{8,0},{10,2},{12,4},{14,6},{1,9},{3,11}... | collective-permute-start | bytes 196616 | tf_op jit(solution)/shard_map/ppermute | solution.py:523
  25.9 7.8 %copy-start.27 = (bf16[2,64,256]{2,1,0:T(8,128)(2,1)}, bf16[2,64,256]{2,1,0:T(8,128)(2,1)S(1)}, u32[]{:S(2)}) copy-start(bf16[2,64,256]{2,1,0:T(8,128)(2,1)S(1)} %collective-permute-done.1.refs_2_) | copy-start | bytes 196612
  25.9 6.9 %collective-permute-start.4 = (bf16[2,64,256]{2,1,0:T(8,128)(2,1)}, bf16[2,64,256]{2,1,0:T(8,128)(2,1)S(1)}, u32[]{:S(2)}, u32[]{:S(2)}) collective-permute-start(bf16[2,64,256]{2,1,0:T(8,128)(2,1)} %get-tuple-element.53), channel_id=1, source_target_pairs={{0,10},{2,8},{4,14},{6,12},{8,2},{10,0},{12,6},{14,4},{1,11},{3,9}... | collective-permute-start | bytes 196616 | tf_op jit(solution)/shard_map/ppermute | solution.py:523
  27.1 6.6 %copy-start.28 = (bf16[2,64,256]{2,1,0:T(8,128)(2,1)}, bf16[2,64,256]{2,1,0:T(8,128)(2,1)S(1)}, u32[]{:S(2)}) copy-start(bf16[2,64,256]{2,1,0:T(8,128)(2,1)S(1)} %collective-permute-done.3.refs_4_) | copy-start | bytes 196612
  27.1 6.5 %collective-permute-start.5 = (bf16[2,64,256]{2,1,0:T(8,128)(2,1)}, bf16[2,64,256]{2,1,0:T(8,128)(2,1)S(1)}, u32[]{:S(2)}, u32[]{:S(2)}) collective-permute-start(bf16[2,64,256]{2,1,0:T(8,128)(2,1)} %get-tuple-element.54), channel_id=1, source_target_pairs={{0,12},{2,14},{4,8},{6,10},{8,4},{10,6},{12,0},{14,2},{1,13},{3,15... | collective-permute-start | bytes 196616 | tf_op jit(solution)/shard_map/ppermute | solution.py:523
  32.8 0.9 copy-start.30
  33.6 0.8 copy-start.17
  33.7 0.8 copy-start.12
  50.1 2.3 %collective-permute-start.14 = (bf16[1168,256]{1,0:T(8,128)(2,1)}, bf16[1168,256]{1,0:T(8,128)(2,1)S(1)}, u32[]{:S(2)}, u32[]{:S(2)}) collective-permute-start(bf16[1168,256]{1,0:T(8,128)(2,1)} %get-tuple-element.69), channel_id=1, source_target_pairs={{0,1},{1,0},{2,3},{3,2},{4,5},{5,4},{6,7},{7,6},{8,9},{9,8},{10,11... | collective-permute-start | bytes 1794056 | tf_op jit(solution)/shard_map/ppermute | solution.py:529
  50.2 7.3 %collective-permute-start.25 = (bf16[1168,256]{1,0:T(8,128)(2,1)}, bf16[1168,256]{1,0:T(8,128)(2,1)S(1)}, u32[]{:S(2)}, u32[]{:S(2)}) collective-permute-start(bf16[1168,256]{1,0:T(8,128)(2,1)} %get-tuple-element.81), channel_id=1, source_target_pairs={{0,1},{1,0},{2,3},{3,2},{4,5},{5,4},{6,7},{7,6},{8,9},{9,8},{10,11... | collective-permute-start | bytes 1794056 | tf_op jit(solution)/shard_map/ppermute | solution.py:529
  52.4 0.8 copy-start.1
  55.9 10.2 %collective-permute-start.15 = (bf16[592,256]{1,0:T(8,128)(2,1)}, bf16[592,256]{1,0:T(8,128)(2,1)S(1)}, u32[]{:S(2)}, u32[]{:S(2)}) collective-permute-start(bf16[592,256]{1,0:T(8,128)(2,1)} %get-tuple-element.71), channel_id=1, source_target_pairs={{0,2},{2,0},{4,6},{6,4},{8,10},{10,8},{12,14},{14,12},{1,3},{3,1},... | collective-permute-start | bytes 909320 | tf_op jit(solution)/shard_map/ppermute | solution.py:581
  57.5 0.8 copy-start
  61.0 12.2 %collective-permute-start.26 = (bf16[592,256]{1,0:T(8,128)(2,1)}, bf16[592,256]{1,0:T(8,128)(2,1)S(1)}, u32[]{:S(2)}, u32[]{:S(2)}) collective-permute-start(bf16[592,256]{1,0:T(8,128)(2,1)} %get-tuple-element.83), channel_id=1, source_target_pairs={{0,2},{2,0},{4,6},{6,4},{8,10},{10,8},{12,14},{14,12},{1,3},{3,1},... | collective-permute-start | bytes 909320 | tf_op jit(solution)/shard_map/ppermute | solution.py:581
  68.8 10.7 %collective-permute-start.16 = (bf16[160,256]{1,0:T(8,128)(2,1)}, bf16[160,256]{1,0:T(8,128)(2,1)S(1)}, u32[]{:S(2)}, u32[]{:S(2)}) collective-permute-start(bf16[160,256]{1,0:T(8,128)(2,1)} %get-tuple-element.73), channel_id=1, source_target_pairs={{0,4},{2,6},{4,0},{6,2},{8,12},{10,14},{12,8},{14,10},{1,5},{3,7},... | collective-permute-start | bytes 245768 | tf_op jit(solution)/shard_map/ppermute | solution.py:589
  70.0 10.4 %collective-permute-start.17 = (bf16[160,256]{1,0:T(8,128)(2,1)}, bf16[160,256]{1,0:T(8,128)(2,1)S(1)}, u32[]{:S(2)}, u32[]{:S(2)}) collective-permute-start(bf16[160,256]{1,0:T(8,128)(2,1)} %get-tuple-element.74), channel_id=1, source_target_pairs={{0,8},{2,10},{4,12},{6,14},{8,0},{10,2},{12,4},{14,6},{1,9},{3,11}... | collective-permute-start | bytes 245768 | tf_op jit(solution)/shard_map/ppermute | solution.py:589
  72.3 8.1 %collective-permute-start.18 = (bf16[160,256]{1,0:T(8,128)(2,1)}, bf16[160,256]{1,0:T(8,128)(2,1)S(1)}, u32[]{:S(2)}, u32[]{:S(2)}) collective-permute-start(bf16[160,256]{1,0:T(8,128)(2,1)} %get-tuple-element.75), channel_id=1, source_target_pairs={{0,12},{2,14},{4,8},{6,10},{8,4},{10,6},{12,0},{14,2},{1,13},{3,15... | collective-permute-start | bytes 245768 | tf_op jit(solution)/shard_map/ppermute | solution.py:589
  75.9 26.7 %copy-start.38 = (bf16[2,64,256]{2,1,0:T(8,128)(2,1)S(1)}, bf16[2,64,256]{2,1,0:T(8,128)(2,1)}, u32[]{:S(2)}) copy-start(bf16[2,64,256]{2,1,0:T(8,128)(2,1)} %get-tuple-element.60) | copy-start | bytes 196612
  75.9 27.0 %copy-start.34 = (bf16[2,208,256]{2,1,0:T(8,128)(2,1)S(1)}, bf16[2,208,256]{2,1,0:T(8,128)(2,1)}, u32[]{:S(2)}) copy-start(bf16[2,208,256]{2,1,0:T(8,128)(2,1)} %get-tuple-element.59) | copy-start | bytes 638980
  75.9 27.4 %copy-start.37 = (bf16[2,64,256]{2,1,0:T(8,128)(2,1)S(1)}, bf16[2,64,256]{2,1,0:T(8,128)(2,1)}, u32[]{:S(2)}) copy-start(bf16[2,64,256]{2,1,0:T(8,128)(2,1)} %get-tuple-element.62) | copy-start | bytes 196612
  75.9 31.6 %copy-start.33 = (bf16[2,208,256]{2,1,0:T(8,128)(2,1)S(1)}, bf16[2,208,256]{2,1,0:T(8,128)(2,1)}, u32[]{:S(2)}) copy-start(bf16[2,208,256]{2,1,0:T(8,128)(2,1)} %get-tuple-element.61) | copy-start | bytes 638980
  75.9 34.5 %copy-start.36 = (bf16[2,64,256]{2,1,0:T(8,128)(2,1)S(1)}, bf16[2,64,256]{2,1,0:T(8,128)(2,1)}, u32[]{:S(2)}) copy-start(bf16[2,64,256]{2,1,0:T(8,128)(2,1)} %get-tuple-element.63) | copy-start | bytes 196612
  75.9 40.8 %copy-start.35 = (bf16[2,64,256]{2,1,0:T(8,128)(2,1)S(1)}, bf16[2,64,256]{2,1,0:T(8,128)(2,1)}, u32[]{:S(2)}) copy-start(bf16[2,64,256]{2,1,0:T(8,128)(2,1)} %get-tuple-element.64) | copy-start | bytes 196612
  75.9 47.9 %copy-start.32 = (bf16[2,256,256]{2,1,0:T(8,128)(2,1)S(1)}, bf16[2,256,256]{2,1,0:T(8,128)(2,1)}, u32[]{:S(2)}) copy-start(bf16[2,256,256]{2,1,0:T(8,128)(2,1)} %get-tuple-element.65) | copy-start | bytes 786436
  75.9 10.7 %collective-permute-start.27 = (bf16[160,256]{1,0:T(8,128)(2,1)}, bf16[160,256]{1,0:T(8,128)(2,1)S(1)}, u32[]{:S(2)}, u32[]{:S(2)}) collective-permute-start(bf16[160,256]{1,0:T(8,128)(2,1)} %get-tuple-element.85), channel_id=1, source_target_pairs={{0,4},{2,6},{4,0},{6,2},{8,12},{10,14},{12,8},{14,10},{1,5},{3,7},... | collective-permute-start | bytes 245768 | tf_op jit(solution)/shard_map/ppermute | solution.py:589
  76.3 11.9 %collective-permute-start.28 = (bf16[160,256]{1,0:T(8,128)(2,1)}, bf16[160,256]{1,0:T(8,128)(2,1)S(1)}, u32[]{:S(2)}, u32[]{:S(2)}) collective-permute-start(bf16[160,256]{1,0:T(8,128)(2,1)} %get-tuple-element.86), channel_id=1, source_target_pairs={{0,8},{2,10},{4,12},{6,14},{8,0},{10,2},{12,4},{14,6},{1,9},{3,11}... | collective-permute-start | bytes 245768 | tf_op jit(solution)/shard_map/ppermute | solution.py:589
  79.5 0.9 copy-start.20
  79.5 8.7 %collective-permute-start.29 = (bf16[160,256]{1,0:T(8,128)(2,1)}, bf16[160,256]{1,0:T(8,128)(2,1)S(1)}, u32[]{:S(2)}, u32[]{:S(2)}) collective-permute-start(bf16[160,256]{1,0:T(8,128)(2,1)} %get-tuple-element.87), channel_id=1, source_target_pairs={{0,12},{2,14},{4,8},{6,10},{8,4},{10,6},{12,0},{14,2},{1,13},{3,15... | collective-permute-start | bytes 245768 | tf_op jit(solution)/shard_map/ppermute | solution.py:589
  82.8 13.3 %collective-permute-start.21 = (bf16[144,256]{1,0:T(8,128)(2,1)}, bf16[144,256]{1,0:T(8,128)(2,1)S(1)}, u32[]{:S(2)}, u32[]{:S(2)}) collective-permute-start(bf16[144,256]{1,0:T(8,128)(2,1)} %get-tuple-element.76), channel_id=1, source_target_pairs={{0,12},{2,14},{4,8},{6,10},{8,4},{10,6},{12,0},{14,2},{1,13},{3,15... | collective-permute-start | bytes 221192 | tf_op jit(solution)/shard_map/ppermute | solution.py:596
  85.7 10.4 %collective-permute-start.20 = (bf16[144,256]{1,0:T(8,128)(2,1)}, bf16[144,256]{1,0:T(8,128)(2,1)S(1)}, u32[]{:S(2)}, u32[]{:S(2)}) collective-permute-start(bf16[144,256]{1,0:T(8,128)(2,1)} %get-tuple-element.76), channel_id=1, source_target_pairs={{0,8},{2,10},{4,12},{6,14},{8,0},{10,2},{12,4},{14,6},{1,9},{3,11}... | collective-permute-start | bytes 221192 | tf_op jit(solution)/shard_map/ppermute | solution.py:596
  86.7 1.5 %copy-start.18 = (bf16[160,256]{1,0:T(8,128)(2,1)}, bf16[160,256]{1,0:T(8,128)(2,1)S(1)}, u32[]{:S(2)}) copy-start(bf16[160,256]{1,0:T(8,128)(2,1)S(1)} %collective-permute-done.27.refs_0_) | copy-start | bytes 245764
  86.7 8.7 %collective-permute-start.19 = (bf16[144,256]{1,0:T(8,128)(2,1)}, bf16[144,256]{1,0:T(8,128)(2,1)S(1)}, u32[]{:S(2)}, u32[]{:S(2)}) collective-permute-start(bf16[144,256]{1,0:T(8,128)(2,1)} %get-tuple-element.76), channel_id=1, source_target_pairs={{0,4},{2,6},{4,0},{6,2},{8,12},{10,14},{12,8},{14,10},{1,5},{3,7},... | collective-permute-start | bytes 221192 | tf_op jit(solution)/shard_map/ppermute | solution.py:596
  90.6 9.8 %collective-permute-start.32 = (bf16[144,256]{1,0:T(8,128)(2,1)}, bf16[144,256]{1,0:T(8,128)(2,1)S(1)}, u32[]{:S(2)}, u32[]{:S(2)}) collective-permute-start(bf16[144,256]{1,0:T(8,128)(2,1)} %get-tuple-element.88), channel_id=1, source_target_pairs={{0,12},{2,14},{4,8},{6,10},{8,4},{10,6},{12,0},{14,2},{1,13},{3,15... | collective-permute-start | bytes 221192 | tf_op jit(solution)/shard_map/ppermute | solution.py:596
  93.5 6.8 %collective-permute-start.31 = (bf16[144,256]{1,0:T(8,128)(2,1)}, bf16[144,256]{1,0:T(8,128)(2,1)S(1)}, u32[]{:S(2)}, u32[]{:S(2)}) collective-permute-start(bf16[144,256]{1,0:T(8,128)(2,1)} %get-tuple-element.88), channel_id=1, source_target_pairs={{0,8},{2,10},{4,12},{6,14},{8,0},{10,2},{12,4},{14,6},{1,9},{3,11}... | collective-permute-start | bytes 221192 | tf_op jit(solution)/shard_map/ppermute | solution.py:596
  95.4 4.9 %collective-permute-start.30 = (bf16[144,256]{1,0:T(8,128)(2,1)}, bf16[144,256]{1,0:T(8,128)(2,1)S(1)}, u32[]{:S(2)}, u32[]{:S(2)}) collective-permute-start(bf16[144,256]{1,0:T(8,128)(2,1)} %get-tuple-element.88), channel_id=1, source_target_pairs={{0,4},{2,6},{4,0},{6,2},{8,12},{10,14},{12,8},{14,10},{1,5},{3,7},... | collective-permute-start | bytes 221192 | tf_op jit(solution)/shard_map/ppermute | solution.py:596
  96.1 46.9 %copy-start.2 = (bf16[576,256]{1,0:T(8,128)(2,1)}, bf16[576,256]{1,0:T(8,128)(2,1)S(1)}, u32[]{:S(2)}) copy-start(bf16[576,256]{1,0:T(8,128)(2,1)S(1)} %constant_dynamic-update-slice_fusion.a_ref) | copy-start | bytes 884740
  96.1 26.7 %collective-permute-start.22 = (bf16[576,256]{1,0:T(8,128)(2,1)S(1)}, bf16[576,256]{1,0:T(8,128)(2,1)S(1)}, u32[]{:S(2)}, u32[]{:S(2)}) collective-permute-start(bf16[576,256]{1,0:T(8,128)(2,1)S(1)} %constant_dynamic-update-slice_fusion.a_ref), channel_id=1, source_target_pairs={{0,2},{2,0},{4,6},{6,4},{8,10},{10,8},{12,14},{14,12},{1,3},{3,1},... | collective-permute-start | bytes 884744 | tf_op jit(solution)/shard_map/ppermute | solution.py:600
  100.4 42.7 %copy-start.3 = (bf16[576,256]{1,0:T(8,128)(2,1)}, bf16[576,256]{1,0:T(8,128)(2,1)S(1)}, u32[]{:S(2)}) copy-start(bf16[576,256]{1,0:T(8,128)(2,1)S(1)} %constant_dynamic-update-slice_fusion.4.a_ref) | copy-start | bytes 884740
  100.4 23.0 %collective-permute-start.33 = (bf16[576,256]{1,0:T(8,128)(2,1)S(1)}, bf16[576,256]{1,0:T(8,128)(2,1)S(1)}, u32[]{:S(2)}, u32[]{:S(2)}) collective-permute-start(bf16[576,256]{1,0:T(8,128)(2,1)S(1)} %constant_dynamic-update-slice_fusion.4.a_ref), channel_id=1, source_target_pairs={{0,2},{2,0},{4,6},{6,4},{8,10},{10,8},{12,14},{14,12},{1,3},{3,1},... | collective-permute-start | bytes 884744 | tf_op jit(solution)/shard_map/ppermute | solution.py:600
  102.6 5.0 %collective-permute-start.8 = (bf16[2,64,256]{2,1,0:T(8,128)(2,1)S(1)}, bf16[2,64,256]{2,1,0:T(8,128)(2,1)S(1)}, u32[]{:S(2)}, u32[]{:S(2)}) collective-permute-start(bf16[2,64,256]{2,1,0:T(8,128)(2,1)S(1)} %copy-done.38), channel_id=1, source_target_pairs={{0,4},{2,6},{4,0},{6,2},{8,12},{10,14},{12,8},{14,10},{1,5},{3,7},... | collective-permute-start | bytes 196616 | tf_op jit(solution)/shard_map/ppermute | solution.py:523
  102.9 20.4 %collective-permute-start.7 = (bf16[2,208,256]{2,1,0:T(8,128)(2,1)S(1)}, bf16[2,208,256]{2,1,0:T(8,128)(2,1)S(1)}, u32[]{:S(2)}, u32[]{:S(2)}) collective-permute-start(bf16[2,208,256]{2,1,0:T(8,128)(2,1)S(1)} %copy-done.34), channel_id=1, source_target_pairs={{0,2},{2,0},{4,6},{6,4},{8,10},{10,8},{12,14},{14,12},{1,3},{3,1},... | collective-permute-start | bytes 638984 | tf_op jit(solution)/shard_map/ppermute | solution.py:523
  103.3 7.1 %collective-permute-start.10 = (bf16[2,64,256]{2,1,0:T(8,128)(2,1)S(1)}, bf16[2,64,256]{2,1,0:T(8,128)(2,1)S(1)}, u32[]{:S(2)}, u32[]{:S(2)}) collective-permute-start(bf16[2,64,256]{2,1,0:T(8,128)(2,1)S(1)} %copy-done.37), channel_id=1, source_target_pairs={{0,8},{2,10},{4,12},{6,14},{8,0},{10,2},{12,4},{14,6},{1,9},{3,11}... | collective-permute-start | bytes 196616 | tf_op jit(solution)/shard_map/ppermute | solution.py:523
  107.5 27.5 %copy-start.24 = (bf16[2,64,256]{2,1,0:T(8,128)(2,1)}, bf16[2,64,256]{2,1,0:T(8,128)(2,1)S(1)}, u32[]{:S(2)}) copy-start(bf16[2,64,256]{2,1,0:T(8,128)(2,1)S(1)} %collective-permute-done.8.refs_2_) | copy-start | bytes 196612
  107.5 16.3 %collective-permute-start.9 = (bf16[2,208,256]{2,1,0:T(8,128)(2,1)S(1)}, bf16[2,208,256]{2,1,0:T(8,128)(2,1)S(1)}, u32[]{:S(2)}, u32[]{:S(2)}) collective-permute-start(bf16[2,208,256]{2,1,0:T(8,128)(2,1)S(1)} %copy-done.33), channel_id=1, source_target_pairs={{0,6},{2,4},{4,2},{6,0},{8,14},{10,12},{12,10},{14,8},{1,7},{3,5},... | collective-permute-start | bytes 638984 | tf_op jit(solution)/shard_map/ppermute | solution.py:523
  110.4 24.6 %copy-start.25 = (bf16[2,64,256]{2,1,0:T(8,128)(2,1)}, bf16[2,64,256]{2,1,0:T(8,128)(2,1)S(1)}, u32[]{:S(2)}) copy-start(bf16[2,64,256]{2,1,0:T(8,128)(2,1)S(1)} %collective-permute-done.10.refs_4_) | copy-start | bytes 196612
  110.4 6.3 %collective-permute-start.11 = (bf16[2,64,256]{2,1,0:T(8,128)(2,1)S(1)}, bf16[2,64,256]{2,1,0:T(8,128)(2,1)S(1)}, u32[]{:S(2)}, u32[]{:S(2)}) collective-permute-start(bf16[2,64,256]{2,1,0:T(8,128)(2,1)S(1)} %copy-done.36), channel_id=1, source_target_pairs={{0,10},{2,8},{4,14},{6,12},{8,2},{10,0},{12,6},{14,4},{1,11},{3,9}... | collective-permute-start | bytes 196616 | tf_op jit(solution)/shard_map/ppermute | solution.py:523
  116.7 18.3 %copy-start.26 = (bf16[2,64,256]{2,1,0:T(8,128)(2,1)}, bf16[2,64,256]{2,1,0:T(8,128)(2,1)S(1)}, u32[]{:S(2)}) copy-start(bf16[2,64,256]{2,1,0:T(8,128)(2,1)S(1)} %collective-permute-done.11.refs_5_) | copy-start | bytes 196612
  116.7 6.1 %collective-permute-start.12 = (bf16[2,64,256]{2,1,0:T(8,128)(2,1)S(1)}, bf16[2,64,256]{2,1,0:T(8,128)(2,1)S(1)}, u32[]{:S(2)}, u32[]{:S(2)}) collective-permute-start(bf16[2,64,256]{2,1,0:T(8,128)(2,1)S(1)} %copy-done.35), channel_id=1, source_target_pairs={{0,12},{2,14},{4,8},{6,10},{8,4},{10,6},{12,0},{14,2},{1,13},{3,15... | collective-permute-start | bytes 196616 | tf_op jit(solution)/shard_map/ppermute | solution.py:523
  122.8 12.2 %copy-start.29 = (bf16[2,64,256]{2,1,0:T(8,128)(2,1)}, bf16[2,64,256]{2,1,0:T(8,128)(2,1)S(1)}, u32[]{:S(2)}) copy-start(bf16[2,64,256]{2,1,0:T(8,128)(2,1)S(1)} %collective-permute-done.12.refs_6_) | copy-start | bytes 196612
  122.8 20.3 %collective-permute-start.23 = (bf16[576,256]{1,0:T(8,128)(2,1)S(1)}, bf16[576,256]{1,0:T(8,128)(2,1)S(1)}, u32[]{:S(2)}, u32[]{:S(2)}) collective-permute-start(bf16[576,256]{1,0:T(8,128)(2,1)S(1)} %constant_dynamic-update-slice_fusion.a_ref), channel_id=1, source_target_pairs={{0,1},{1,0},{2,3},{3,2},{4,5},{5,4},{6,7},{7,6},{8,9},{9,8},{10,11... | collective-permute-start | bytes 884744 | tf_op jit(solution)/shard_map/ppermute | solution.py:529
  122.8 20.2 %copy-start.6 = (bf16[576,256]{1,0:T(8,128)(2,1)}, bf16[576,256]{1,0:T(8,128)(2,1)S(1)}, u32[]{:S(2)}) copy-start(bf16[576,256]{1,0:T(8,128)(2,1)S(1)} %collective-permute-done.22.b_ref) | copy-start | bytes 884740
  122.8 20.3 %collective-permute-start.24 = (bf16[576,256]{1,0:T(8,128)(2,1)S(1)}, bf16[576,256]{1,0:T(8,128)(2,1)S(1)}, u32[]{:S(2)}, u32[]{:S(2)}) collective-permute-start(bf16[576,256]{1,0:T(8,128)(2,1)S(1)} %collective-permute-done.22.b_ref), channel_id=1, source_target_pairs={{0,1},{1,0},{2,3},{3,2},{4,5},{5,4},{6,7},{7,6},{8,9},{9,8},{10,11... | collective-permute-start | bytes 884744 | tf_op jit(solution)/shard_map/ppermute | solution.py:529
  123.3 11.7 %copy-start.14 = (bf16[2,208,256]{2,1,0:T(8,128)(2,1)}, bf16[2,208,256]{2,1,0:T(8,128)(2,1)S(1)}, u32[]{:S(2)}) copy-start(bf16[2,208,256]{2,1,0:T(8,128)(2,1)S(1)} %collective-permute-done.7.refs_1_) | copy-start | bytes 638980
  123.3 24.8 %collective-permute-start.34 = (bf16[576,256]{1,0:T(8,128)(2,1)S(1)}, bf16[576,256]{1,0:T(8,128)(2,1)S(1)}, u32[]{:S(2)}, u32[]{:S(2)}) collective-permute-start(bf16[576,256]{1,0:T(8,128)(2,1)S(1)} %constant_dynamic-update-slice_fusion.4.a_ref), channel_id=1, source_target_pairs={{0,1},{1,0},{2,3},{3,2},{4,5},{5,4},{6,7},{7,6},{8,9},{9,8},{10,11... | collective-permute-start | bytes 884744 | tf_op jit(solution)/shard_map/ppermute | solution.py:529
  123.4 19.6 %copy-start.7 = (bf16[576,256]{1,0:T(8,128)(2,1)}, bf16[576,256]{1,0:T(8,128)(2,1)S(1)}, u32[]{:S(2)}) copy-start(bf16[576,256]{1,0:T(8,128)(2,1)S(1)} %collective-permute-done.33.b_ref) | copy-start | bytes 884740
  123.4 24.7 %collective-permute-start.35 = (bf16[576,256]{1,0:T(8,128)(2,1)S(1)}, bf16[576,256]{1,0:T(8,128)(2,1)S(1)}, u32[]{:S(2)}, u32[]{:S(2)}) collective-permute-start(bf16[576,256]{1,0:T(8,128)(2,1)S(1)} %collective-permute-done.33.b_ref), channel_id=1, source_target_pairs={{0,1},{1,0},{2,3},{3,2},{4,5},{5,4},{6,7},{7,6},{8,9},{9,8},{10,11... | collective-permute-start | bytes 884744 | tf_op jit(solution)/shard_map/ppermute | solution.py:529
  123.8 11.2 %copy-start.15 = (bf16[2,208,256]{2,1,0:T(8,128)(2,1)}, bf16[2,208,256]{2,1,0:T(8,128)(2,1)S(1)}, u32[]{:S(2)}) copy-start(bf16[2,208,256]{2,1,0:T(8,128)(2,1)S(1)} %collective-permute-done.9.refs_3_) | copy-start | bytes 638980
  123.8 11.2 %collective-permute-start.13 = (bf16[2,256,256]{2,1,0:T(8,128)(2,1)S(1)}, bf16[2,256,256]{2,1,0:T(8,128)(2,1)S(1)}, u32[]{:S(2)}, u32[]{:S(2)}) collective-permute-start(bf16[2,256,256]{2,1,0:T(8,128)(2,1)S(1)} %copy-done.32), channel_id=1, source_target_pairs={{0,14},{2,12},{4,10},{6,8},{8,6},{10,4},{12,2},{14,0},{1,15},{3,13... | collective-permute-start | bytes 786440 | tf_op jit(solution)/shard_map/ppermute | solution.py:523
  143.1 0.8 copy-start.11
  148.2 0.8 copy-start.10
  (11 other events, 7.5 us)

commit v2 on v1

--- a/solution.py
+++ b/solution.py
@@ -18,28 +18,39 @@
         self.N = 6 * rows * face
         self.ROW = 6 * face
         self.SLOT = -(-(2 * rows + 2) // 8) * 8
-        self.RC = 6 * self.SLOT
-        self.BASE = self.RC + 16
+        self.BASE = 6 * self.SLOT
         self.MIR = 16 * rows
-        self.row_ks = []
-        k = 1
-        while k < tiles:
-            self.row_ks.append(k)
-            k = 2 * k + 1
         self.o_msg = self.N
         self.o_mir = self.o_msg + tiles * self.BASE
         self.o_row = self.o_mir + self.MIR
-        self.NT = self.o_row + len(self.row_ks) * self.ROW
+        self.NT = self.o_row + 2 * self.ROW
         self.WE = 12 * 8
         self.S = self.WE + self.ROW
 
-    def msg_rows(self, k):
-        rows = self.BASE
-        if k == self.T - 1:
-            rows += self.MIR
-        if k in self.row_ks:
-            rows += self.ROW
+    def messages(self):
+        rows = [self.BASE] * (self.T - 1) + [self.MIR, self.BASE + self.ROW]
+        rows[1] += self.ROW
         return rows
+
+    def table_parts(self):
+        parts = [(k, 0, self.BASE, self.o_msg + k * self.BASE) for k in range(self.T - 1)]
+        parts.append((self.T, 0, self.BASE, self.o_msg + (self.T - 1) * self.BASE))
+        parts.append((self.T - 1, 0, self.MIR, self.o_mir))
+        parts.append((1, self.BASE, self.ROW, self.o_row))
+        parts.append((self.T, self.BASE, self.ROW, self.o_row + self.ROW))
+        return parts
+
+    def pairs(self):
+        T = self.T
+        edges = (0, T - 1)
+
+        def needed(i, d):
+            return i in edges or d in edges or d in (T - 2 - i, T - i)
+
+        out = [[(i, i ^ k) for i in range(T) if k == 1 or needed(i, i ^ k)] for k in range(T - 1)]
+        out.append([(i, T - 1 - i) for i in range(T)])
+        out.append([(i, (i + 1) % T if i % 2 else (i - 1) % T) for i in range(T)])
+        return out
 
 
 def col_iota(n):
@@ -51,100 +62,97 @@
     return jnp.where(lanes == target, 1.0, 0.0).astype(BF)
 
 
-def edge_of(ep, strip):
-    value = ep[strip]
-    face = value // 4
-    edge = value % 4
-    own_low = (strip % 4) < 2
-    far_low = edge < 2
-    reverse = (far_low == own_low) if not isinstance(own_low, bool) else (far_low if own_low else edge >= 2)
-    return face, edge, reverse
-
-
-def message_targets(dm, ep, t, k):
+def strip_targets(dm, ep, t, d):
     R, F, T = dm.R, dm.F, dm.T
-    d = t ^ k
-    parts = []
+    at_edge = (t == 0) | (t == T - 1)
+    to_edge = (d == 0) | (d == T - 1)
+    own_edge = jnp.where(t == 0, 0, 2)
+    far_edge = jnp.where(d == 0, 0, 2)
+    side_row = jnp.where(d == T - 2 - t, R - 1, 0)
     i = col_iota(dm.SLOT)
-    at_first = t == 0
     q = R * d - 1 + i
     inside = (q >= 0) & (q < F) & (i < R + 2)
     i2 = i - (R + 2)
-    to_first = d == 0
+    parts = []
     for f in range(6):
-        strip = jnp.where(at_first, 4 * f, 4 * f + 2)
-        value = ep[strip]
-        far_low = (value % 4) < 2
-        own_low = at_first
-        reverse = far_low == own_low
+        far_low = (ep[f, own_edge] % 4) < 2
+        reverse = far_low == (t == 0)
         p0 = jnp.where(reverse, F - 1, 0)
         sgn = jnp.where(reverse, -1, 1)
-        row = jnp.where(at_first, 0, R - 1)
-        tgt_r = jnp.where(inside, (f * R + row) * F + p0 + sgn * q, -1)
-        gvalue = ep[jnp.where(to_first, 4 * f, 4 * f + 2)]
-        f2 = gvalue // 4
-        column = jnp.where(gvalue % 4 == 1, F - 1, 0)
-        tgt_c = f2 * (R * F) + column + F * i2
-        parts.append(jnp.where(i2 < 0, tgt_r, jnp.where(i2 < R, tgt_c, -1)))
-    s = col_iota(16)
-    column_cells = (s // 2) * (R * F) + (s % 2) * (F - 1)
-    row = jnp.where(d == T - 2 - t, R - 1, 0)
-    parts.append(jnp.where(s < 12, column_cells + row * F, -1))
+        row = jnp.where(t == 0, 0, R - 1)
+        strip = jnp.where(inside, (f * R + row) * F + p0 + sgn * q, -1)
+        sides = (f * R + side_row) * F
+        low = jnp.where(at_edge, strip, sides + i * (F - 1))
+        low = jnp.where(at_edge | (i < 2), low, -1)
+        gvalue = ep[f, far_edge]
+        column = jnp.where(gvalue % 4 == 1, F - 1, 0) + (gvalue // 4) * (R * F)
+        high = jnp.where(to_edge, column + F * i2, jnp.where(i2 < 2, sides + i2 * (F - 1), -1))
+        parts.append(jnp.where(i2 < 0, low, jnp.where(i2 < R, high, -1)))
+    return parts
+
+
+def row_targets(dm, row):
+    j = col_iota(dm.F)
+    return [(f * dm.R + row) * dm.F + j for f in range(6)]
+
+
+def message_targets(dm, ep, t, k):
+    R, F, T = dm.R, dm.F, dm.T
     if k == T - 1:
-        for r in range(R):
-            parts.append(jnp.where(s < 12, column_cells + r * F, -1))
-    if k in dm.row_ks:
-        row = jnp.where(d == (t + 1) % T, R - 1, 0)
-        j = col_iota(F)
-        for f in range(6):
-            parts.append((f * R + row) * F + j)
+        s = col_iota(16)
+        cells = (s // 2) * (R * F) + (s % 2) * (F - 1)
+        parts = [jnp.where(s < 12, cells + r * F, -1) for r in range(R)]
+    elif k == T:
+        parts = strip_targets(dm, ep, t, T - 1 - t)
+        parts += row_targets(dm, jnp.where(t % 2 == 1, R - 1, 0))
+    else:
+        parts = strip_targets(dm, ep, t, t ^ k)
+        if k == 1:
+            parts += row_targets(dm, jnp.where(t % 2 == 0, R - 1, 0))
     return jnp.concatenate(parts, axis=0)
 
 
 def write_messages(dm, ep, t, sources, refs):
-    for k in range(dm.T):
+    for k in range(dm.T + 1):
         hot = one_hot(message_targets(dm, ep, t, k), dm.N)
         for which, source in enumerate(sources):
             refs[k][which] = jnp.dot(hot, source, preferred_element_type=F32).astype(BF)
 
 
-def pack_kernel(dm, sc, x_ref, up_ref, *refs):
-    write_messages(dm, sc, sc[24], (x_ref[...], up_ref[...]), refs)
+def pack_kernel(dm, ep, x_ref, up_ref, *refs):
+    write_messages(dm, ep, lax.axis_index("tile"), (x_ref[...], up_ref[...]), refs)
 
 
 def ghost_targets(dm, ep, t):
     R, F, T = dm.R, dm.F, dm.T
-
-    def o_row(k):
-        out = dm.o_row
-        for j, kk in enumerate(dm.row_ks):
-            out = jnp.where(k == kk, dm.o_row + j * dm.ROW, out)
-        return out
-
+    odd = t % 2
     parts = []
     m = col_iota(8)
     q = R * t - 1 + m
     inside = (q >= 0) & (q < F) & (m < R + 2)
-    row_prev = o_row(t ^ (t - 1))
-    row_next = o_row(t ^ (t + 1))
-    ab_first = dm.o_msg + (t ^ (T - t)) * dm.BASE + dm.RC
-    ab_last = dm.o_msg + (t ^ (T - 2 - t)) * dm.BASE + dm.RC
+    row_prev = dm.o_row + (1 - odd) * dm.ROW
+    row_next = dm.o_row + odd * dm.ROW
+    side_first = dm.o_msg + (t ^ (T - t)) * dm.BASE + jnp.where(t == 1, R + 2, 0)
+    side_last = dm.o_msg + (t ^ (T - 2 - t)) * dm.BASE + jnp.where(t == T - 2, R + 2, 0)
     for f in range(6):
         for edge in (3, 1):
-            strip = 4 * f + edge
-            value = ep[strip]
+            value = ep[f, edge]
             f2, e2 = value // 4, value % 4
             far_low = e2 < 2
             reverse = far_low if edge < 2 else e2 >= 2
             is_col = (e2 % 2) == 1
-            column = jnp.where(e2 == 1, F - 1, 0)
-            s = 2 * f2 + jnp.where(e2 == 1, 1, 0)
+            side = jnp.where(e2 == 1, 1, 0)
+            column = side * (F - 1)
+            s = 2 * f2 + side
+            slot = f2 * dm.SLOT + side
             src_k = jnp.where(e2 == 0, t, t ^ (T - 1))
-            slot = dm.o_msg + src_k * dm.BASE + f2 * dm.SLOT
-            i0 = jnp.where(is_col, jnp.where(reverse, ab_first + s, row_prev + f2 * F + column), slot)
-            i4 = jnp.where(is_col, jnp.where(reverse, ab_last + s, row_next + f2 * F + column), slot + R + 1)
+            row = dm.o_msg + src_k * dm.BASE + f2 * dm.SLOT
+            i0 = jnp.where(is_col, jnp.where(reverse, side_first + slot, row_prev + f2 * F + column), row)
+            i4 = jnp.where(
+                is_col, jnp.where(reverse, side_last + slot, row_next + f2 * F + column), row + R + 1
+            )
             base = jnp.where(
-                is_col, jnp.where(reverse, dm.o_mir + 16 * R + s, (f2 * R - 1) * F + column), slot
+                is_col, jnp.where(reverse, dm.o_mir + 16 * R + s, (f2 * R - 1) * F + column), row
             )
             step = jnp.where(is_col, jnp.where(reverse, -16, F), 1)
             target = jnp.where(m == 0, i0, jnp.where(m == R + 1, i4, base + step * m))
@@ -154,13 +162,13 @@
     for b in range(1, T):
         jt = jt + jnp.where(j >= b * R, 1, 0)
     jr = j - R * jt
-    wrap = o_row(jnp.int32(T - 1))
+    wrap = dm.o_row + dm.ROW
     for edge in (0, 2):
         at_edge = (t == 0) if edge == 0 else (t == T - 1)
         inner_base = row_prev if edge == 0 else row_next
         own_row = 0 if edge == 0 else R - 1
         for f in range(6):
-            value = ep[4 * f + edge]
+            value = ep[f, edge]
             f2, e2 = value // 4, value % 4
             far_low = e2 < 2
             reverse = far_low if edge < 2 else e2 >= 2
@@ -192,17 +200,8 @@
     out = []
     for which in range(2):
         table_ref[0 : dm.N] = own[which]
-        for k in range(dm.T):
-            ref = messages[k]
-            at = dm.o_msg + k * dm.BASE
-            table_ref[at : at + dm.BASE] = ref[which, 0 : dm.BASE]
-            row = dm.BASE
-            if k == dm.T - 1:
-                table_ref[dm.o_mir : dm.o_mir + dm.MIR] = ref[which, row : row + dm.MIR]
-                row += dm.MIR
-            if k in dm.row_ks:
-                at = dm.o_row + dm.row_ks.index(k) * dm.ROW
-                table_ref[at : at + dm.ROW] = ref[which, row : row + dm.ROW]
+        for k, row, count, at in dm.table_parts():
+            table_ref[at : at + count] = messages[k][which, row : row + count]
         out.append(jnp.dot(hot, table_ref[...], preferred_element_type=F32))
     return out
 
@@ -234,12 +233,9 @@
     R, F = dm.R, dm.F
     z_ref[...] = jnp.zeros(z_ref.shape, F32)
 
-    def tap_of(strip, shift):
-        value = ep[strip]
-        e2 = value % 4
-        far_low = e2 < 2
-        own_low = (strip % 4) < 2
-        reverse = far_low if own_low else jnp.logical_not(far_low)
+    def tap_of(f, edge, shift):
+        e2 = ep[f, edge] % 4
+        reverse = e2 < 2 if edge < 2 else e2 >= 2
         along = 1 - jnp.where(reverse, -shift, shift)
         return jnp.where(
             e2 == 0, along, jnp.where(e2 == 2, 6 + along, jnp.where(e2 == 1, 3 * along + 2, 3 * along))
@@ -252,7 +248,7 @@
         for f in range(6):
             for side, edge in ((0, 3), (1, 1)):
                 at = 16 * f + 8 * side
-                z_ref[tap_of(4 * f + edge, shift), at : at + 8] = moved[at : at + 8]
+                z_ref[tap_of(f, edge, shift), at : at + 8] = moved[at : at + 8]
 
     def add_rows(edge, rows):
         j = lax.rem(lax.broadcasted_iota(jnp.int32, (dm.ROW, 1), 0), F)
@@ -264,7 +260,7 @@
                 moved = jnp.where((j + shift >= 0) & (j + shift < F), moved, 0.0)
             for f in range(6):
                 at = dm.WE + F * f
-                z_ref[tap_of(4 * f + edge, shift), at : at + F] = moved[F * f : F * (f + 1)]
+                z_ref[tap_of(f, edge, shift), at : at + F] = moved[F * f : F * (f + 1)]
 
     @pl.when(t == 0)
     def _():
@@ -333,15 +329,16 @@
     send_ref[n:] = jnp.where(i == 0, high.astype(F32), jnp.where(i == 1, low, 0.0)).astype(BF)
 
 
-def first_kernel(dm, sc, x_ref, up_ref, w1_ref, bias_ref, w2_ref, *refs):
+def first_kernel(dm, ep, x_ref, up_ref, w1_ref, bias_ref, w2_ref, *refs):
     T, R, F, N, C = dm.T, dm.R, dm.F, dm.N, dm.C
-    messages = refs[:T]
-    s1_ref, k1_ref, s2_ref, k2_ref, hid_ref, inner_ref = refs[T : T + 6]
-    out_messages = refs[T + 6 : 2 * T + 6]
-    table_ref, frame_ref, xs_ref, us_ref, z_ref, before_ref, acc_ref, hcat_ref = refs[2 * T + 6 :]
-    t, p = sc[24], sc[25]
+    M = T + 1
+    messages = refs[:M]
+    s1_ref, k1_ref, s2_ref, k2_ref, hid_ref, inner_ref = refs[M : M + 6]
+    out_messages = refs[M + 6 : 2 * M + 6]
+    table_ref, frame_ref, xs_ref, us_ref, z_ref, before_ref, acc_ref, hcat_ref = refs[2 * M + 6 :]
+    t, p = lax.axis_index("tile"), lax.axis_index("dp")
     own = (x_ref[...].reshape(N, C), up_ref[...].reshape(N, C))
-    gx, gu = gather_ghosts(dm, sc, t, own, messages, table_ref)
+    gx, gu = gather_ghosts(dm, ep, t, own, messages, table_ref)
     top, bottom = dm.WE, dm.WE + dm.ROW
     build_shifts(dm, x_ref, gx[:top], gx[top:bottom], gx[bottom:], frame_ref, xs_ref)
     total = None
@@ -360,7 +357,7 @@
     up_top = jnp.where(t == 0, 0.0, gu[top:bottom])
     up_bottom = jnp.where(t == T - 1, 0.0, gu[bottom:])
     build_shifts(dm, up_ref, None, up_top, up_bottom, frame_ref, us_ref)
-    build_strip_terms(dm, sc, t, gu[:top], gu[top:bottom], gu[bottom:], z_ref)
+    build_strip_terms(dm, ep, t, gu[:top], gu[top:bottom], gu[bottom:], z_ref)
     hcat_ref[...] = jnp.zeros(hcat_ref.shape, F32)
     for f in range(6):
         for side in range(2):
@@ -405,18 +402,18 @@
             at = (r * 6 + f) * F
             inner_ref[f * R + r] = acc_ref[at : at + F].astype(BF)
     write_messages(
-        dm, sc, t, (hid_ref[...].reshape(N, C), inner_ref[...].reshape(N, C)), out_messages
+        dm, ep, t, (hid_ref[...].reshape(N, C), inner_ref[...].reshape(N, C)), out_messages
     )
 
 
-def second_kernel(dm, sc, x_ref, d_ref, hid_ref, inner_ref, w1_ref, w2_ref, *refs):
+def second_kernel(dm, ep, x_ref, d_ref, hid_ref, inner_ref, w1_ref, w2_ref, *refs):
     T, R, F, N, C = dm.T, dm.R, dm.F, dm.N, dm.C
-    messages = refs[:T]
-    state_ref, grad_ref = refs[T : T + 2]
-    table_ref, frame_ref, shift_ref, z_ref, acc_ref = refs[T + 2 :]
-    t = sc[24]
+    messages = refs[: T + 1]
+    state_ref, grad_ref = refs[T + 1 : T + 3]
+    table_ref, frame_ref, shift_ref, z_ref, acc_ref = refs[T + 3 :]
+    t = lax.axis_index("tile")
     own = (hid_ref[...].reshape(N, C), inner_ref[...].reshape(N, C))
-    gh, gi = gather_ghosts(dm, sc, t, own, messages, table_ref)
+    gh, gi = gather_ghosts(dm, ep, t, own, messages, table_ref)
     top, bottom = dm.WE, dm.WE + dm.ROW
     build_shifts(dm, hid_ref, gh[:top], gh[top:bottom], gh[bottom:], frame_ref, shift_ref)
     total = None
@@ -437,7 +434,7 @@
     in_top = jnp.where(t == 0, 0.0, gi[top:bottom])
     in_bottom = jnp.where(t == T - 1, 0.0, gi[bottom:])
     build_shifts(dm, inner_ref, None, in_top, in_bottom, frame_ref, shift_ref)
-    build_strip_terms(dm, sc, t, gi[:top], gi[top:bottom], gi[bottom:], z_ref)
+    build_strip_terms(dm, ep, t, gi[:top], gi[top:bottom], gi[bottom:], z_ref)
     adjoint(dm, t, shift_ref, z_ref, w1_ref, acc_ref)
     for r in range(R):
         for f in range(6):
@@ -449,11 +446,12 @@
     return keep[n : n + 1] + recv[n : n + 1].astype(F32) + recv[n + 1 : n + 2].astype(F32)
 
 
-def halve_kernel(pieces, shift, sc, keep_ref, recv_ref, *refs):
+def halve_kernel(pieces, shift, keep_ref, recv_ref, *refs):
     out_keep, out_sends, sum_ref = refs[0], refs[1:pieces], refs[pieces]
     n = keep_ref.shape[0] - EXTRA
     size = n // pieces
-    own = sc[24] % 2 if shift == 0 else sc[24] // 2
+    t = lax.axis_index("tile")
+    own = t % 2 if shift == 0 else t // 2
     sum_ref[...] = keep_ref[0:n] + recv_ref[0:n].astype(F32)
     extra = extra_sum(keep_ref, recv_ref, n)
     out_keep[0:size] = sum_ref[pl.ds(pl.multiple_of(own * size, 8), size)]
@@ -479,8 +477,8 @@
     extra_ref[...] = jnp.broadcast_to(extra, extra_ref.shape)
 
 
-def normal_kernel(zcount, sc, a_ref, b_ref, c_ref, d_ref, extra_ref, out_ref, bias_ref):
-    t, p = sc[24], sc[25]
+def normal_kernel(zcount, a_ref, b_ref, c_ref, d_ref, extra_ref, out_ref, bias_ref):
+    t, p = lax.axis_index("tile"), lax.axis_index("dp")
     refs = (a_ref, b_ref, c_ref, d_ref)
     square = None
     for ref in refs:
@@ -498,10 +496,10 @@
             out_ref[pl.ds(pl.multiple_of(at, 8), size)] = value
     extra = extra_ref[0:1]
     bias_mean = jnp.mean(extra * extra, keepdims=True)
-    bias_ref[...] = jnp.broadcast_to(extra * lax.rsqrt(bias_mean + 1e-06), bias_ref.shape)
-
-
-def call(kernel, out_shapes, scratch=(), smem_first=True):
+    bias_ref[...] = extra * lax.rsqrt(bias_mean + 1e-06)
+
+
+def call(kernel, out_shapes, scratch=(), smem_first=False):
     def run(*args):
         vmem = pl.BlockSpec(memory_space=pltpu.VMEM)
         smem = pl.BlockSpec(memory_space=pltpu.SMEM)
@@ -518,10 +516,9 @@
     return run
 
 
-def exchange(tiles, messages):
-    return [messages[0]] + [
-        lax.ppermute(messages[k], "tile", [(i, i ^ k) for i in range(tiles)]) for k in range(1, tiles)
-    ]
+def exchange(dm, messages):
+    pairs = dm.pairs()
+    return [messages[0]] + [lax.ppermute(messages[k], "tile", pairs[k]) for k in range(1, dm.T + 1)]
 
 
 def swap_dp(v):
@@ -534,27 +531,22 @@
     _, _, rows, face, channels = initial_state.shape
     dm = Dims(rows, face, tiles, channels)
     planes = (6 * rows, face, channels)
-    sc = jnp.concatenate(
-        [
-            edge_partner.reshape(24).astype(jnp.int32),
-            lax.axis_index("tile")[None].astype(jnp.int32),
-            lax.axis_index("dp")[None].astype(jnp.int32),
-        ]
-    )
     x = initial_state.reshape(planes)
     d = state_cotangents[state_cotangents.shape[0] - 1].reshape(planes)
     w1 = w_first.reshape(9, channels, channels)
     w2 = w_second.reshape(9, channels, channels)
-    msg_shapes = [((2, dm.msg_rows(k), channels), BF) for k in range(tiles)]
+    msg_shapes = [((2, n, channels), BF) for n in dm.messages()]
     flat = (dm.N, channels)
-    messages = call(functools.partial(pack_kernel, dm), msg_shapes)(sc, x.reshape(flat), d.reshape(flat))
-    messages = exchange(tiles, messages)
-    half = 9 * channels // 2 + EXTRA
+    messages = call(functools.partial(pack_kernel, dm), msg_shapes, smem_first=True)(
+        edge_partner, x.reshape(flat), d.reshape(flat)
+    )
+    messages = exchange(dm, messages)
+    half = 9 * channels // 2
     shift_rows = (3, (rows + 2) * dm.ROW, channels)
     frame = (rows + 2, 6, face + 16, channels)
     outs = call(
         functools.partial(first_kernel, dm),
-        [((half, channels), BF), ((half, channels), F32)] * 2 + [(planes, BF)] * 2 + msg_shapes,
+        [((half + EXTRA, channels), BF), ((half + EXTRA, channels), F32)] * 2 + [(planes, BF)] * 2 + msg_shapes,
         [
             ((dm.NT, channels), BF),
             (frame, F32),
@@ -565,50 +557,59 @@
             (flat, F32),
             ((dm.S, channels), F32),
         ],
-    )(sc, x, d, w1, bias.reshape(1, channels), w2, *messages)
+        smem_first=True,
+    )(edge_partner, x, d, w1, bias.reshape(1, channels), w2, *messages)
     send_first, keep_first, send_second, keep_second, hidden, inner = outs[:6]
 
     zcount = tiles // 2
-
-    def reduced(send, keep):
-        recv = swap_dp(send)
-        n = (half - EXTRA) // 2
+    n = half // 2
+    m = n // zcount
+
+    def along_z(v, j):
+        return lax.ppermute(v, "tile", [(i, i ^ (2 * j)) for i in range(tiles)])
+
+    def along_y(v):
+        return lax.ppermute(v, "tile", [(i, i ^ 1) for i in range(tiles)])
+
+    def reduce_y(keep, recv):
         keep, send = call(
             functools.partial(halve_kernel, 2, 0),
             [((n + EXTRA, channels), F32), ((n + EXTRA, channels), BF)],
             [((2 * n, channels), F32)],
-        )(sc, keep, recv)
-        recv = lax.ppermute(send, "tile", [(i, i ^ 1) for i in range(tiles)])
-        m = n // zcount
+        )(keep, recv)
+        return keep, along_y(send)
+
+    def reduce_z(keep, recv):
         keep, *sends = call(
             functools.partial(halve_kernel, zcount, 1),
             [((m + EXTRA, channels), F32)] + [((m + EXTRA, channels), BF)] * (zcount - 1),
             [((n, channels), F32)],
-        )(sc, keep, recv)
-        recvs = [
-            lax.ppermute(v, "tile", [(i, i ^ (2 * (j + 1))) for i in range(tiles)])
-            for j, v in enumerate(sends)
-        ]
-        block, extra = call(last_kernel, [((m, channels), BF), ((8, channels), F32)], smem_first=False)(
-            keep, *recvs
-        )
-        blocks = [block] + [
-            lax.ppermute(block, "tile", [(i, i ^ (2 * j)) for i in range(tiles)])
-            for j in range(1, zcount)
-        ]
-        own = jnp.concatenate(blocks, axis=0)
-        other = lax.ppermute(own, "tile", [(i, i ^ 1) for i in range(tiles)])
-        far_own = swap_dp(own)
-        far_other = swap_dp(other)
+        )(keep, recv)
+        return keep, [along_z(v, j + 1) for j, v in enumerate(sends)]
+
+    def gather_z(keep, recvs):
+        block, extra = call(last_kernel, [((m, channels), BF), ((8, channels), F32)])(keep, *recvs)
+        return [block] + [along_z(block, j) for j in range(1, zcount)], extra
+
+    def finish(own, other, extra):
         return call(
             functools.partial(normal_kernel, zcount),
-            [((9 * channels, channels), F32), ((8, channels), F32)],
-        )(sc, own, other, far_own, far_other, extra)
-
-    second_step, _ = reduced(send_second, keep_second)
-    first_step, bias_step = reduced(send_first, keep_first)
-
-    messages = exchange(tiles, outs[6:])
+            [((9 * channels, channels), F32), ((1, channels), F32)],
+        )(own, other, swap_dp(own), swap_dp(other), extra)
+
+    keep2, recv2 = reduce_y(keep_second, swap_dp(send_second))
+    messages = exchange(dm, outs[6:])
+    keep1, recv1 = reduce_y(keep_first, swap_dp(send_first))
+    (keep2, recv2), messages = lax.optimization_barrier(((keep2, recv2), messages))
+    keep2, recvs2 = reduce_z(keep2, recv2)
+    keep1, recvs1 = reduce_z(keep1, recv1)
+    blocks2, extra2 = gather_z(keep2, recvs2)
+    blocks1, extra1 = gather_z(keep1, recvs1)
+    own2 = jnp.concatenate(blocks2, axis=0)
+    other2 = along_y(own2)
+    own1 = jnp.concatenate(blocks1, axis=0)
+    other1 = along_y(own1)
+    messages, _ = lax.optimization_barrier((messages, own1))
     state, grad = call(
         functools.partial(second_kernel, dm),
         [(planes, BF), (planes, F32)],
@@ -619,12 +620,15 @@
             ((9, dm.S, channels), F32),
             (flat, F32),
         ],
-    )(sc, x, d, hidden, inner, w1, w2, *messages)
+        smem_first=True,
+    )(edge_partner, x, d, hidden, inner, w1, w2, *messages)
+    second_step, _ = finish(own2, other2, extra2)
+    first_step, bias_step = finish(own1, other1, extra1)
     return (
         state.reshape(initial_state.shape),
         grad.reshape(initial_state.shape),
         first_step.reshape(w_first.shape),
-        bias_step[0],
+        bias_step.reshape(channels),
         second_step.reshape(w_second.shape),
     )
 

time: 153 us -> 152 us (level)
  starting transfers between devices: 47.9 us -> 62.4 us
  waiting for transfers between devices: 46.2 us -> 33.6 us
    ppermute x30 -> x32, starting transfers between devices: 46.3 us -> 61.2 us  [the longest x16 36.9 us: exchange(): lax.ppermute(messages[k], 'tile', pairs[k])]
    ppermute x30 -> x32, waiting for transfers between devices: 44.5 us -> 31.9 us  [the longest x16 19.2 us: exchange(): lax.ppermute(messages[k], 'tile', pairs[k])]
    unnamed x85 -> x91, local copies, waits for them, and re-layouts: 10.2 us -> 9.98 us
  transfers between devices with their start and end apart: 36 -> 38, of which waited for: 12 -> 9; matrix products, arithmetic and copies ran while one was open for 2% -> 1% of each run, Pallas kernels for 15% -> 15%
where the time goes in v2:
time: 152 us; the launch traced here: 151 us
  starting transfers between devices  62.4 us (41%)
  Pallas kernels  44.2 us (29%)
  waiting for transfers between devices  33.6 us (22%)
  local copies, waits for them, and re-layouts  10 us (7%)
    pallas_call x11, Pallas kernels, run(): pl.pallas_call(kernel, out_shape=[jax.ShapeDtypeStruct(s, dt) for s, dt i...  44.2 us
    ppermute x16, starting transfers between devices, exchange(): lax.ppermute(messages[k], 'tile', pairs[k])  36.9 us
    ppermute x16, waiting for transfers between devices, exchange(): lax.ppermute(messages[k], 'tile', pairs[k])  19.2 us
    ppermute x12, starting transfers between devices, along_z(): return lax.ppermute(v, 'tile', [(i, i ^ 2 * j) for i in range(tiles)])  17.9 us
    unnamed x91, local copies, waits for them, and re-layouts  9.98 us
    ppermute x4, waiting for transfers between devices, along_y(): return lax.ppermute(v, 'tile', [(i, i ^ 1) for i in range(tiles)])  7.12 us
    ppermute x4, starting transfers between devices, along_y(): return lax.ppermute(v, 'tile', [(i, i ^ 1) for i in range(tiles)])  6.49 us
    ppermute x12, waiting for transfers between devices, along_z(): return lax.ppermute(v, 'tile', [(i, i ^ 2 * j) for i in range(tiles)])  5.5 us
  transfers between devices with their start and end apart: 38, of which 9 were waited for; matrix products, arithmetic and copies ran while one was open for 1% of the time, Pallas kernels for 15%

profile of v2, /device:TPU:0, one launch (start us, length us, event | category | flops | bytes accessed | tf_op | source)
XLA Modules:
  0.0 151.3 jit_solution(4630839617908908371)
XLA Ops:
  0.6 1.3 copy.13.ep
  2.0 3.2 %shard_map.101 = (bf16[2,48,256]{2,1,0:T(8,128)(2,1)}, bf16[2,192,256]{2,1,0:T(8,128)(2,1)}, bf16[2,48,256]{2,1,0:T(8,128)(2,1)}, bf16[2,48,256]{2,1,0:T(8,128)(...) custom-call(s32[6,4]{1,0:T(8,128)} %copy.13.ep, ...), custom_call_target="tpu_custom_call" | custom-call | tf_op jit(solution)/shard_map/pallas_call | solution.py:507
  5.2 3.0 %collective-permute-start = (bf16[2,192,256]{2,1,0:T(8,128)(2,1)}, bf16[2,192,256]{2,1,0:T(8,128)(2,1)S(1)}, u32[]{:S(2)}, u32[]{:S(2)}) collective-permute-start(bf16[2,192,256]{2,1,0:T(8,128)(2,1)} %get-tuple-element.71), channel_id=1, source_target_pairs={{0,2},{2,0},{4,6},{6,4},{8,10},{10,8},{12,14},{14,12},{1,3},{3,1},... | collective-permute-start | bytes 589832 | tf_op jit(solution)/shard_map/ppermute | solution.py:521
  8.2 3.5 %collective-permute-start.7 = (bf16[2,192,256]{2,1,0:T(8,128)(2,1)}, bf16[2,192,256]{2,1,0:T(8,128)(2,1)S(1)}, u32[]{:S(2)}, u32[]{:S(2)}) collective-permute-start(bf16[2,192,256]{2,1,0:T(8,128)(2,1)} %get-tuple-element.78), channel_id=1, source_target_pairs={{0,14},{2,4},{4,2},{6,8},{8,6},{10,12},{12,10},{14,0},{1,15},{3,5}... | collective-permute-start | bytes 589832 | tf_op jit(solution)/shard_map/ppermute | solution.py:521
  11.7 1.9 %collective-permute-start.1 = (bf16[2,48,256]{2,1,0:T(8,128)(2,1)}, bf16[2,48,256]{2,1,0:T(8,128)(2,1)S(1)}, u32[]{:S(2)}, u32[]{:S(2)}) collective-permute-start(bf16[2,48,256]{2,1,0:T(8,128)(2,1)} %get-tuple-element.72), channel_id=1, source_target_pairs={{0,4},{4,0},{10,14},{14,10},{1,5},{5,1},{11,15},{15,11},{16,20},{2... | collective-permute-start | bytes 147464 | tf_op jit(solution)/shard_map/ppermute | solution.py:521
  13.6 1.9 %collective-permute-start.2 = (bf16[2,48,256]{2,1,0:T(8,128)(2,1)}, bf16[2,48,256]{2,1,0:T(8,128)(2,1)S(1)}, u32[]{:S(2)}, u32[]{:S(2)}) collective-permute-start(bf16[2,48,256]{2,1,0:T(8,128)(2,1)} %get-tuple-element.73), channel_id=1, source_target_pairs={{0,6},{6,0},{8,14},{14,8},{1,7},{7,1},{9,15},{15,9},{16,22},{22,16... | collective-permute-start | bytes 147464 | tf_op jit(solution)/shard_map/ppermute | solution.py:521
  15.6 3.6 %collective-permute-start.3 = (bf16[2,48,256]{2,1,0:T(8,128)(2,1)}, bf16[2,48,256]{2,1,0:T(8,128)(2,1)S(1)}, u32[]{:S(2)}, u32[]{:S(2)}) collective-permute-start(bf16[2,48,256]{2,1,0:T(8,128)(2,1)} %get-tuple-element.74), channel_id=1, source_target_pairs={{0,8},{2,10},{4,12},{6,14},{8,0},{10,2},{12,4},{14,6},{1,9},{3,11}... | collective-permute-start | bytes 147464 | tf_op jit(solution)/shard_map/ppermute | solution.py:521
  19.2 2.5 %collective-permute-start.4 = (bf16[2,48,256]{2,1,0:T(8,128)(2,1)}, bf16[2,48,256]{2,1,0:T(8,128)(2,1)S(1)}, u32[]{:S(2)}, u32[]{:S(2)}) collective-permute-start(bf16[2,48,256]{2,1,0:T(8,128)(2,1)} %get-tuple-element.75), channel_id=1, source_target_pairs={{0,10},{4,14},{10,0},{14,4},{1,11},{5,15},{11,1},{15,5},{16,26},{2... | collective-permute-start | bytes 147464 | tf_op jit(solution)/shard_map/ppermute | solution.py:521
  21.6 0.1 collective-permute-start.5
  21.7 3.5 %collective-permute-start.6 = (bf16[2,48,256]{2,1,0:T(8,128)(2,1)}, bf16[2,48,256]{2,1,0:T(8,128)(2,1)S(1)}, u32[]{:S(2)}, u32[]{:S(2)}) collective-permute-start(bf16[2,48,256]{2,1,0:T(8,128)(2,1)} %get-tuple-element.77), channel_id=1, source_target_pairs={{0,14},{2,12},{4,10},{6,8},{8,6},{10,4},{12,2},{14,0},{1,15},{3,13... | collective-permute-start | bytes 147464 | tf_op jit(solution)/shard_map/ppermute | solution.py:521
  25.2 4.0 %collective-permute-done.4.refs_5_ = bf16[2,48,256]{2,1,0:T(8,128)(2,1)S(1)} collective-permute-done((bf16[2,48,256]{2,1,0:T(8,128)(2,1)}, bf16[2,48,256]{2,1,0:T(8,128)(2,1)S(1)}, u32[]{:S(2)}, u32[]{:S(2)}) %collective-permute-start.4) | collective-permute-done | bytes 49184 | tf_op jit(solution)/shard_map/ppermute | solution.py:521
  29.3 0.5 copy-done.31
  30.0 15.2 %shard_map.102 = (bf16[1168,256]{1,0:T(8,128)(2,1)}, f32[1168,256]{1,0:T(8,128)}, bf16[1168,256]{1,0:T(8,128)(2,1)}, f32[1168,256]{1,0:T(8,128)}, bf16[18,24,256...) custom-call(s32[6,4]{1,0:T(8,128)} %copy.13.ep, ...), custom_call_target="tpu_custom_call" | custom-call | tf_op jit(solution)/shard_map/pallas_call | solution.py:507
  45.2 0.1 collective-permute-start.8
  45.3 0.5 collective-permute-start.18
  45.8 1.7 %collective-permute-done.8.recv_ref = bf16[1168,256]{1,0:T(8,128)(2,1)S(1)} collective-permute-done((bf16[1168,256]{1,0:T(8,128)(2,1)}, bf16[1168,256]{1,0:T(8,128)(2,1)S(1)}, u32[]{:S(2)}, u32[]{:S(2)}) %collective-permute-start.8) | collective-permute-done | bytes 598048 | tf_op jit(solution)/shard_map/ppermute | solution.py:526
  47.5 0.8 copy-done.1
  48.4 2.6 %shard_map.103 = (f32[592,256]{1,0:T(8,128)}, bf16[592,256]{1,0:T(8,128)(2,1)}) custom-call(f32[1168,256]{1,0:T(8,128)} %get-tuple-element.81.keep_ref, bf16[1168,256]{1,0:T(8,128)(2,1)} %copy-done.1), custom_call_target="tpu_custom_call" | custom-call | tf_op jit(solution)/shard_map/pallas_call | solution.py:507
  51.0 3.4 %collective-permute-start.9 = (bf16[592,256]{1,0:T(8,128)(2,1)}, bf16[592,256]{1,0:T(8,128)(2,1)S(1)}, u32[]{:S(2)}, u32[]{:S(2)}) collective-permute-start(bf16[592,256]{1,0:T(8,128)(2,1)} %get-tuple-element.84), channel_id=1, source_target_pairs={{0,2},{2,0},{4,6},{6,4},{8,10},{10,8},{12,14},{14,12},{1,3},{3,1},... | collective-permute-start | bytes 909320 | tf_op jit(solution)/shard_map/ppermute | solution.py:572
  54.4 1.9 %collective-permute-start.11 = (bf16[2,48,256]{2,1,0:T(8,128)(2,1)S(1)}, bf16[2,48,256]{2,1,0:T(8,128)(2,1)S(1)}, u32[]{:S(2)}, u32[]{:S(2)}) collective-permute-start(bf16[2,48,256]{2,1,0:T(8,128)(2,1)S(1)} %copy-done.41), channel_id=1, source_target_pairs={{0,4},{4,0},{10,14},{14,10},{1,5},{5,1},{11,15},{15,11},{16,20},{2... | collective-permute-start | bytes 147464 | tf_op jit(solution)/shard_map/ppermute | solution.py:521
  56.4 1.9 %collective-permute-start.12 = (bf16[2,48,256]{2,1,0:T(8,128)(2,1)S(1)}, bf16[2,48,256]{2,1,0:T(8,128)(2,1)S(1)}, u32[]{:S(2)}, u32[]{:S(2)}) collective-permute-start(bf16[2,48,256]{2,1,0:T(8,128)(2,1)S(1)} %copy-done.40), channel_id=1, source_target_pairs={{0,6},{6,0},{8,14},{14,8},{1,7},{7,1},{9,15},{15,9},{16,22},{22,16... | collective-permute-start | bytes 147464 | tf_op jit(solution)/shard_map/ppermute | solution.py:521
  58.3 0.8 copy-done
  59.1 2.6 %shard_map.104 = (f32[592,256]{1,0:T(8,128)}, bf16[592,256]{1,0:T(8,128)(2,1)}) custom-call(f32[1168,256]{1,0:T(8,128)} %get-tuple-element.103.keep_ref, bf16[1168,256]{1,0:T(8,128)(2,1)} %copy-done), custom_call_target="tpu_custom_call" | custom-call | tf_op jit(solution)/shard_map/pallas_call | solution.py:507
  61.7 1.9 %collective-permute-start.13 = (bf16[2,48,256]{2,1,0:T(8,128)(2,1)S(1)}, bf16[2,48,256]{2,1,0:T(8,128)(2,1)S(1)}, u32[]{:S(2)}, u32[]{:S(2)}) collective-permute-start(bf16[2,48,256]{2,1,0:T(8,128)(2,1)S(1)} %copy-done.39), channel_id=1, source_target_pairs={{0,8},{2,10},{4,12},{6,14},{8,0},{10,2},{12,4},{14,6},{1,9},{3,11}... | collective-permute-start | bytes 147464 | tf_op jit(solution)/shard_map/ppermute | solution.py:521
  63.6 2.0 %collective-permute-start.10 = (bf16[2,192,256]{2,1,0:T(8,128)(2,1)S(1)}, bf16[2,192,256]{2,1,0:T(8,128)(2,1)S(1)}, u32[]{:S(2)}, u32[]{:S(2)}) collective-permute-start(bf16[2,192,256]{2,1,0:T(8,128)(2,1)S(1)} %copy-done.35), channel_id=1, source_target_pairs={{0,2},{2,0},{4,6},{6,4},{8,10},{10,8},{12,14},{14,12},{1,3},{3,1},... | collective-permute-start | bytes 589832 | tf_op jit(solution)/shard_map/ppermute | solution.py:521
  65.7 3.5 %collective-permute-start.17 = (bf16[2,192,256]{2,1,0:T(8,128)(2,1)S(1)}, bf16[2,192,256]{2,1,0:T(8,128)(2,1)S(1)}, u32[]{:S(2)}, u32[]{:S(2)}) collective-permute-start(bf16[2,192,256]{2,1,0:T(8,128)(2,1)S(1)} %copy-done.34), channel_id=1, source_target_pairs={{0,14},{2,4},{4,2},{6,8},{8,6},{10,12},{12,10},{14,0},{1,15},{3,5}... | collective-permute-start | bytes 589832 | tf_op jit(solution)/shard_map/ppermute | solution.py:521
  69.2 3.4 %collective-permute-start.14 = (bf16[2,48,256]{2,1,0:T(8,128)(2,1)S(1)}, bf16[2,48,256]{2,1,0:T(8,128)(2,1)S(1)}, u32[]{:S(2)}, u32[]{:S(2)}) collective-permute-start(bf16[2,48,256]{2,1,0:T(8,128)(2,1)S(1)} %copy-done.38), channel_id=1, source_target_pairs={{0,10},{4,14},{10,0},{14,4},{1,11},{5,15},{11,1},{15,5},{16,26},{2... | collective-permute-start | bytes 147464 | tf_op jit(solution)/shard_map/ppermute | solution.py:521
  72.6 4.9 %collective-permute-done.14.refs_5_ = bf16[2,48,256]{2,1,0:T(8,128)(2,1)S(1)} collective-permute-done((bf16[2,48,256]{2,1,0:T(8,128)(2,1)S(1)}, bf16[2,48,256]{2,1,0:T(8,128)(2,1)S(1)}, u32[]{:S(2)}, u32[]{:S(2)}) %collective-permute-start.14) | collective-permute-done | bytes 49184 | tf_op jit(solution)/shard_map/ppermute | solution.py:521
  77.5 5.9 %collective-permute-done.15.refs_6_ = bf16[2,48,256]{2,1,0:T(8,128)(2,1)S(1)} collective-permute-done((bf16[2,48,256]{2,1,0:T(8,128)(2,1)S(1)}, bf16[2,48,256]{2,1,0:T(8,128)(2,1)S(1)}, u32[]{:S(2)}, u32[]{:S(2)}) %collective-permute-start.15) | collective-permute-done | bytes 49184 | tf_op jit(solution)/shard_map/ppermute | solution.py:521
  83.4 2.3 %collective-permute-start.16 = (bf16[2,48,256]{2,1,0:T(8,128)(2,1)S(1)}, bf16[2,48,256]{2,1,0:T(8,128)(2,1)S(1)}, u32[]{:S(2)}, u32[]{:S(2)}) collective-permute-start(bf16[2,48,256]{2,1,0:T(8,128)(2,1)S(1)} %copy-done.36), channel_id=1, source_target_pairs={{0,14},{2,12},{4,10},{6,8},{8,6},{10,4},{12,2},{14,0},{1,15},{3,13... | collective-permute-start | bytes 147464 | tf_op jit(solution)/shard_map/ppermute | solution.py:521
  85.7 4.5 %collective-permute-done.16.refs_7_ = bf16[2,48,256]{2,1,0:T(8,128)(2,1)S(1)} collective-permute-done((bf16[2,48,256]{2,1,0:T(8,128)(2,1)S(1)}, bf16[2,48,256]{2,1,0:T(8,128)(2,1)S(1)}, u32[]{:S(2)}, u32[]{:S(2)}) %collective-permute-start.16) | collective-permute-done | bytes 49184 | tf_op jit(solution)/shard_map/ppermute | solution.py:521
  90.2 0.8 copy-done.5
  91.0 2.0 %shard_map.109 = (f32[160,256]{1,0:T(8,128)}, bf16[160,256]{1,0:T(8,128)(2,1)}, bf16[160,256]{1,0:T(8,128)(2,1)}, bf16[160,256]{1,0:T(8,128)(2,1)}) custom-call(f32[592,256]{1,0:T(8,128)} %get-tuple-element.126.keep_ref, bf16[592,256]{1,0:T(8,128)(2,1)} %copy-done.5), custom_call_target="tpu_custom_call" | custom-call | tf_op jit(solution)/shard_map/pallas_call | solution.py:507
  93.0 0.7 collective-permute-start.30
  93.6 3.7 %collective-permute-start.31 = (bf16[160,256]{1,0:T(8,128)(2,1)}, bf16[160,256]{1,0:T(8,128)(2,1)S(1)}, u32[]{:S(2)}, u32[]{:S(2)}) collective-permute-start(bf16[160,256]{1,0:T(8,128)(2,1)} %get-tuple-element.131), channel_id=1, source_target_pairs={{0,12},{2,14},{4,8},{6,10},{8,4},{10,6},{12,0},{14,2},{1,13},{3,15... | collective-permute-start | bytes 245768 | tf_op jit(solution)/shard_map/ppermute | solution.py:569
  97.3 0.7 copy-done.4
  98.1 2.0 %shard_map.105 = (f32[160,256]{1,0:T(8,128)}, bf16[160,256]{1,0:T(8,128)(2,1)}, bf16[160,256]{1,0:T(8,128)(2,1)}, bf16[160,256]{1,0:T(8,128)(2,1)}) custom-call(f32[592,256]{1,0:T(8,128)} %get-tuple-element.105.keep_ref, bf16[592,256]{1,0:T(8,128)(2,1)} %copy-done.4), custom_call_target="tpu_custom_call" | custom-call | tf_op jit(solution)/shard_map/pallas_call | solution.py:507
  100.0 0.7 collective-permute-start.21
  100.7 3.7 %collective-permute-start.22 = (bf16[160,256]{1,0:T(8,128)(2,1)}, bf16[160,256]{1,0:T(8,128)(2,1)S(1)}, u32[]{:S(2)}, u32[]{:S(2)}) collective-permute-start(bf16[160,256]{1,0:T(8,128)(2,1)} %get-tuple-element.110), channel_id=1, source_target_pairs={{0,12},{2,14},{4,8},{6,10},{8,4},{10,6},{12,0},{14,2},{1,13},{3,15... | collective-permute-start | bytes 245768 | tf_op jit(solution)/shard_map/ppermute | solution.py:569
  104.5 0.6 copy-done.20
  105.1 1.7 %shard_map.110 = (bf16[144,256]{1,0:T(8,128)(2,1)}, f32[8,256]{1,0:T(8,128)}) custom-call(f32[160,256]{1,0:T(8,128)} %get-tuple-element.128.keep_ref, bf16[160,256]{1,0:T(8,128)(2,1)} %copy-done.18, bf16[160,256]{1,0:T(8,128)(2,1)} %copy-done.20, bf16[160,256]{1,0:T(8,128)(2,1)} %copy-done.21), custom_call_target="tpu_custom_call" | custom-call | tf_op jit(solution)/shard_map/pallas_call | solution.py:507
  106.8 0.4 collective-permute-start.34
  107.2 1.4 collective-permute-start.33
  108.5 0.9 constant_dynamic-update-slice_fusion.7
  109.5 2.7 %collective-permute-start.32 = (bf16[144,256]{1,0:T(8,128)(2,1)}, bf16[144,256]{1,0:T(8,128)(2,1)S(1)}, u32[]{:S(2)}, u32[]{:S(2)}) collective-permute-start(bf16[144,256]{1,0:T(8,128)(2,1)} %get-tuple-element.132), channel_id=1, source_target_pairs={{0,4},{2,6},{4,0},{6,2},{8,12},{10,14},{12,8},{14,10},{1,5},{3,7},... | collective-permute-start | bytes 221192 | tf_op jit(solution)/shard_map/ppermute | solution.py:569
  112.2 0.6 copy-done.17
  112.9 1.7 %shard_map.106 = (bf16[144,256]{1,0:T(8,128)(2,1)}, f32[8,256]{1,0:T(8,128)}) custom-call(f32[160,256]{1,0:T(8,128)} %get-tuple-element.107.keep_ref, bf16[160,256]{1,0:T(8,128)(2,1)} %copy-done.16, bf16[160,256]{1,0:T(8,128)(2,1)} %copy-done.17, bf16[160,256]{1,0:T(8,128)(2,1)} %copy-done.19), custom_call_target="tpu_custom_call" | custom-call | tf_op jit(solution)/shard_map/pallas_call | solution.py:507
  114.6 0.4 collective-permute-start.25
  114.9 2.1 %collective-permute-start.23 = (bf16[144,256]{1,0:T(8,128)(2,1)}, bf16[144,256]{1,0:T(8,128)(2,1)S(1)}, u32[]{:S(2)}, u32[]{:S(2)}) collective-permute-start(bf16[144,256]{1,0:T(8,128)(2,1)} %get-tuple-element.111), channel_id=1, source_target_pairs={{0,4},{2,6},{4,0},{6,2},{8,12},{10,14},{12,8},{14,10},{1,5},{3,7},... | collective-permute-start | bytes 221192 | tf_op jit(solution)/shard_map/ppermute | solution.py:569
  117.0 0.9 constant_dynamic-update-slice_fusion.3
  118.0 2.2 %collective-permute-done.23 = bf16[144,256]{1,0:T(8,128)(2,1)S(1)} collective-permute-done((bf16[144,256]{1,0:T(8,128)(2,1)}, bf16[144,256]{1,0:T(8,128)(2,1)S(1)}, u32[]{:S(2)}, u32[]{:S(2)}) %collective-permute-start.23) | collective-permute-done | bytes 73760 | tf_op jit(solution)/shard_map/ppermute | solution.py:569
  120.1 2.2 %collective-permute-start.24 = (bf16[144,256]{1,0:T(8,128)(2,1)}, bf16[144,256]{1,0:T(8,128)(2,1)S(1)}, u32[]{:S(2)}, u32[]{:S(2)}) collective-permute-start(bf16[144,256]{1,0:T(8,128)(2,1)} %get-tuple-element.111), channel_id=1, source_target_pairs={{0,8},{2,10},{4,12},{6,14},{8,0},{10,2},{12,4},{14,6},{1,9},{3,11}... | collective-permute-start | bytes 221192 | tf_op jit(solution)/shard_map/ppermute | solution.py:569
  122.3 3.3 %collective-permute-done.24 = bf16[144,256]{1,0:T(8,128)(2,1)S(1)} collective-permute-done((bf16[144,256]{1,0:T(8,128)(2,1)}, bf16[144,256]{1,0:T(8,128)(2,1)S(1)}, u32[]{:S(2)}, u32[]{:S(2)}) %collective-permute-start.24) | collective-permute-done | bytes 73760 | tf_op jit(solution)/shard_map/ppermute | solution.py:569
  125.6 3.0 %collective-permute-start.26 = (bf16[576,256]{1,0:T(8,128)(2,1)S(1)}, bf16[576,256]{1,0:T(8,128)(2,1)S(1)}, u32[]{:S(2)}, u32[]{:S(2)}) collective-permute-start(bf16[576,256]{1,0:T(8,128)(2,1)S(1)} %constant_dynamic-update-slice_fusion.a_ref), channel_id=1, source_target_pairs={{0,2},{2,0},{4,6},{6,4},{8,10},{10,8},{12,14},{14,12},{1,3},{3,1},... | collective-permute-start | bytes 884744 | tf_op jit(solution)/shard_map/ppermute | solution.py:572
  128.7 0.1 collective-permute-start.35
  128.8 4.5 %collective-permute-done.26.b_ref = bf16[576,256]{1,0:T(8,128)(2,1)S(1)} collective-permute-done((bf16[576,256]{1,0:T(8,128)(2,1)S(1)}, bf16[576,256]{1,0:T(8,128)(2,1)S(1)}, u32[]{:S(2)}, u32[]{:S(2)}) %collective-permute-start.26) | collective-permute-done | bytes 294944 | tf_op jit(solution)/shard_map/ppermute | solution.py:572
  133.3 0.5 collective-permute-start.36
  133.8 2.6 %collective-permute-done.35.b_ref = bf16[576,256]{1,0:T(8,128)(2,1)S(1)} collective-permute-done((bf16[576,256]{1,0:T(8,128)(2,1)S(1)}, bf16[576,256]{1,0:T(8,128)(2,1)S(1)}, u32[]{:S(2)}, u32[]{:S(2)}) %collective-permute-start.35) | collective-permute-done | bytes 294944 | tf_op jit(solution)/shard_map/ppermute | solution.py:572
  136.5 7.2 %shard_map.107 = (bf16[18,24,256]{2,1,0:T(8,128)(2,1)}, f32[18,24,256]{2,1,0:T(8,128)}) custom-call(s32[6,4]{1,0:T(8,128)} %copy.13.ep, bf16[18,24,256]{2,1,0:T(8,128)(2,1)} %bitcast.18, bf16[18,24,256]{2,1,0:T(8,128)(2,1)} %bitcast.21, bf16[18,24,256]{2,1,0:T(8,128)(2,1)} %get-tuple-element.79.hid_ref, bf16[18,24,256]{2,1,0:T(8,128)(2,1)} %get-tuple-element.80.inner_ref, ...), custom_call_target="tpu_custom_call" | custom-call | tf_op jit(solution)/shard_map/pallas_call | solution.py:507
  143.8 0.7 copy-done.9
  144.5 0.1 copy-done.11
  144.6 3.0 %shard_map.108 = (f32[2304,256]{1,0:T(8,128)}, f32[1,256]{1,0:T(1,128)}) custom-call(bf16[576,256]{1,0:T(8,128)(2,1)} %copy-done.3, bf16[576,256]{1,0:T(8,128)(2,1)} %copy-done.6, bf16[576,256]{1,0:T(8,128)(2,1)} %copy-done.9, bf16[576,256]{1,0:T(8,128)(2,1)} %copy-done.11, f32[8,256]{1,0:T(8,128)} %get-tuple-element.123.extra_ref), custom_call_target="tpu_custom_call" | custom-call | tf_op jit(solution)/shard_map/pallas_call | solution.py:507
  147.6 0.7 copy-done.8
  148.4 3.0 %shard_map.111 = (f32[2304,256]{1,0:T(8,128)}, f32[1,256]{1,0:T(1,128)}) custom-call(bf16[576,256]{1,0:T(8,128)(2,1)} %copy-done.2, bf16[576,256]{1,0:T(8,128)(2,1)} %copy-done.7, bf16[576,256]{1,0:T(8,128)(2,1)} %copy-done.8, bf16[576,256]{1,0:T(8,128)(2,1)} %copy-done.10, f32[8,256]{1,0:T(8,128)} %get-tuple-element.133.extra_ref), custom_call_target="tpu_custom_call" | custom-call | tf_op jit(solution)/shard_map/pallas_call | solution.py:507
  (116 shorter events, 0.6 us)
Async XLA Ops:
  5.2 24.0 %collective-permute-start = (bf16[2,192,256]{2,1,0:T(8,128)(2,1)}, bf16[2,192,256]{2,1,0:T(8,128)(2,1)S(1)}, u32[]{:S(2)}, u32[]{:S(2)}) collective-permute-start(bf16[2,192,256]{2,1,0:T(8,128)(2,1)} %get-tuple-element.71), channel_id=1, source_target_pairs={{0,2},{2,0},{4,6},{6,4},{8,10},{10,8},{12,14},{14,12},{1,3},{3,1},... | collective-permute-start | bytes 589832 | tf_op jit(solution)/shard_map/ppermute | solution.py:521
  8.2 21.1 %collective-permute-start.7 = (bf16[2,192,256]{2,1,0:T(8,128)(2,1)}, bf16[2,192,256]{2,1,0:T(8,128)(2,1)S(1)}, u32[]{:S(2)}, u32[]{:S(2)}) collective-permute-start(bf16[2,192,256]{2,1,0:T(8,128)(2,1)} %get-tuple-element.78), channel_id=1, source_target_pairs={{0,14},{2,4},{4,2},{6,8},{8,6},{10,12},{12,10},{14,0},{1,15},{3,5}... | collective-permute-start | bytes 589832 | tf_op jit(solution)/shard_map/ppermute | solution.py:521
  11.7 7.4 %collective-permute-start.1 = (bf16[2,48,256]{2,1,0:T(8,128)(2,1)}, bf16[2,48,256]{2,1,0:T(8,128)(2,1)S(1)}, u32[]{:S(2)}, u32[]{:S(2)}) collective-permute-start(bf16[2,48,256]{2,1,0:T(8,128)(2,1)} %get-tuple-element.72), channel_id=1, source_target_pairs={{0,4},{4,0},{10,14},{14,10},{1,5},{5,1},{11,15},{15,11},{16,20},{2... | collective-permute-start | bytes 147464 | tf_op jit(solution)/shard_map/ppermute | solution.py:521
  13.6 8.0 %collective-permute-start.2 = (bf16[2,48,256]{2,1,0:T(8,128)(2,1)}, bf16[2,48,256]{2,1,0:T(8,128)(2,1)S(1)}, u32[]{:S(2)}, u32[]{:S(2)}) collective-permute-start(bf16[2,48,256]{2,1,0:T(8,128)(2,1)} %get-tuple-element.73), channel_id=1, source_target_pairs={{0,6},{6,0},{8,14},{14,8},{1,7},{7,1},{9,15},{15,9},{16,22},{22,16... | collective-permute-start | bytes 147464 | tf_op jit(solution)/shard_map/ppermute | solution.py:521
  15.6 6.2 %collective-permute-start.3 = (bf16[2,48,256]{2,1,0:T(8,128)(2,1)}, bf16[2,48,256]{2,1,0:T(8,128)(2,1)S(1)}, u32[]{:S(2)}, u32[]{:S(2)}) collective-permute-start(bf16[2,48,256]{2,1,0:T(8,128)(2,1)} %get-tuple-element.74), channel_id=1, source_target_pairs={{0,8},{2,10},{4,12},{6,14},{8,0},{10,2},{12,4},{14,6},{1,9},{3,11}... | collective-permute-start | bytes 147464 | tf_op jit(solution)/shard_map/ppermute | solution.py:521
  19.2 10.1 %copy-start.28 = (bf16[2,48,256]{2,1,0:T(8,128)(2,1)}, bf16[2,48,256]{2,1,0:T(8,128)(2,1)S(1)}, u32[]{:S(2)}) copy-start(bf16[2,48,256]{2,1,0:T(8,128)(2,1)S(1)} %collective-permute-done.1.refs_2_) | copy-start | bytes 147460
  19.2 10.0 %collective-permute-start.4 = (bf16[2,48,256]{2,1,0:T(8,128)(2,1)}, bf16[2,48,256]{2,1,0:T(8,128)(2,1)S(1)}, u32[]{:S(2)}, u32[]{:S(2)}) collective-permute-start(bf16[2,48,256]{2,1,0:T(8,128)(2,1)} %get-tuple-element.75), channel_id=1, source_target_pairs={{0,10},{4,14},{10,0},{14,4},{1,11},{5,15},{11,1},{15,5},{16,26},{2... | collective-permute-start | bytes 147464 | tf_op jit(solution)/shard_map/ppermute | solution.py:521
  21.6 7.6 %copy-start.29 = (bf16[2,48,256]{2,1,0:T(8,128)(2,1)}, bf16[2,48,256]{2,1,0:T(8,128)(2,1)S(1)}, u32[]{:S(2)}) copy-start(bf16[2,48,256]{2,1,0:T(8,128)(2,1)S(1)} %collective-permute-done.2.refs_3_) | copy-start | bytes 147460
  21.6 7.5 %collective-permute-start.5 = (bf16[2,48,256]{2,1,0:T(8,128)(2,1)}, bf16[2,48,256]{2,1,0:T(8,128)(2,1)S(1)}, u32[]{:S(2)}, u32[]{:S(2)}) collective-permute-start(bf16[2,48,256]{2,1,0:T(8,128)(2,1)} %get-tuple-element.76), channel_id=1, source_target_pairs={{0,12},{2,14},{4,8},{6,10},{8,4},{10,6},{12,0},{14,2},{1,13},{3,15... | collective-permute-start | bytes 147464 | tf_op jit(solution)/shard_map/ppermute | solution.py:521
  21.7 7.5 %copy-start.30 = (bf16[2,48,256]{2,1,0:T(8,128)(2,1)}, bf16[2,48,256]{2,1,0:T(8,128)(2,1)S(1)}, u32[]{:S(2)}) copy-start(bf16[2,48,256]{2,1,0:T(8,128)(2,1)S(1)} %collective-permute-done.3.refs_4_) | copy-start | bytes 147460
  21.7 7.5 %collective-permute-start.6 = (bf16[2,48,256]{2,1,0:T(8,128)(2,1)}, bf16[2,48,256]{2,1,0:T(8,128)(2,1)S(1)}, u32[]{:S(2)}, u32[]{:S(2)}) collective-permute-start(bf16[2,48,256]{2,1,0:T(8,128)(2,1)} %get-tuple-element.77), channel_id=1, source_target_pairs={{0,14},{2,12},{4,10},{6,8},{8,6},{10,4},{12,2},{14,0},{1,15},{3,13... | collective-permute-start | bytes 147464 | tf_op jit(solution)/shard_map/ppermute | solution.py:521
  45.2 9.2 %copy-start.41 = (bf16[2,48,256]{2,1,0:T(8,128)(2,1)S(1)}, bf16[2,48,256]{2,1,0:T(8,128)(2,1)}, u32[]{:S(2)}) copy-start(bf16[2,48,256]{2,1,0:T(8,128)(2,1)} %get-tuple-element.87) | copy-start | bytes 147460
  45.2 11.1 %copy-start.40 = (bf16[2,48,256]{2,1,0:T(8,128)(2,1)S(1)}, bf16[2,48,256]{2,1,0:T(8,128)(2,1)}, u32[]{:S(2)}) copy-start(bf16[2,48,256]{2,1,0:T(8,128)(2,1)} %get-tuple-element.88) | copy-start | bytes 147460
  45.2 2.3 %collective-permute-start.8 = (bf16[1168,256]{1,0:T(8,128)(2,1)}, bf16[1168,256]{1,0:T(8,128)(2,1)S(1)}, u32[]{:S(2)}, u32[]{:S(2)}) collective-permute-start(bf16[1168,256]{1,0:T(8,128)(2,1)} %get-tuple-element.82), channel_id=1, source_target_pairs={{0,1},{1,0},{2,3},{3,2},{4,5},{5,4},{6,7},{7,6},{8,9},{9,8},{10,11... | collective-permute-start | bytes 1794056 | tf_op jit(solution)/shard_map/ppermute | solution.py:526
  45.3 13.0 %collective-permute-start.18 = (bf16[1168,256]{1,0:T(8,128)(2,1)}, bf16[1168,256]{1,0:T(8,128)(2,1)S(1)}, u32[]{:S(2)}, u32[]{:S(2)}) collective-permute-start(bf16[1168,256]{1,0:T(8,128)(2,1)} %get-tuple-element.104), channel_id=1, source_target_pairs={{0,1},{1,0},{2,3},{3,2},{4,5},{5,4},{6,7},{7,6},{8,9},{9,8},{10,11... | collective-permute-start | bytes 1794056 | tf_op jit(solution)/shard_map/ppermute | solution.py:526
  47.5 0.8 copy-start.1
  51.0 10.8 %copy-start.39 = (bf16[2,48,256]{2,1,0:T(8,128)(2,1)S(1)}, bf16[2,48,256]{2,1,0:T(8,128)(2,1)}, u32[]{:S(2)}) copy-start(bf16[2,48,256]{2,1,0:T(8,128)(2,1)} %get-tuple-element.89) | copy-start | bytes 147460
  51.0 12.7 %copy-start.35 = (bf16[2,192,256]{2,1,0:T(8,128)(2,1)S(1)}, bf16[2,192,256]{2,1,0:T(8,128)(2,1)}, u32[]{:S(2)}) copy-start(bf16[2,192,256]{2,1,0:T(8,128)(2,1)} %get-tuple-element.86) | copy-start | bytes 589828
  51.0 14.7 %copy-start.34 = (bf16[2,192,256]{2,1,0:T(8,128)(2,1)S(1)}, bf16[2,192,256]{2,1,0:T(8,128)(2,1)}, u32[]{:S(2)}) copy-start(bf16[2,192,256]{2,1,0:T(8,128)(2,1)} %get-tuple-element.93) | copy-start | bytes 589828
  51.0 18.2 %copy-start.38 = (bf16[2,48,256]{2,1,0:T(8,128)(2,1)S(1)}, bf16[2,48,256]{2,1,0:T(8,128)(2,1)}, u32[]{:S(2)}) copy-start(bf16[2,48,256]{2,1,0:T(8,128)(2,1)} %get-tuple-element.90) | copy-start | bytes 147460
  51.0 26.5 %copy-start.37 = (bf16[2,48,256]{2,1,0:T(8,128)(2,1)S(1)}, bf16[2,48,256]{2,1,0:T(8,128)(2,1)}, u32[]{:S(2)}) copy-start(bf16[2,48,256]{2,1,0:T(8,128)(2,1)} %get-tuple-element.91) | copy-start | bytes 147460
  51.0 32.4 %copy-start.36 = (bf16[2,48,256]{2,1,0:T(8,128)(2,1)S(1)}, bf16[2,48,256]{2,1,0:T(8,128)(2,1)}, u32[]{:S(2)}) copy-start(bf16[2,48,256]{2,1,0:T(8,128)(2,1)} %get-tuple-element.92) | copy-start | bytes 147460
  51.0 39.2 %collective-permute-start.9 = (bf16[592,256]{1,0:T(8,128)(2,1)}, bf16[592,256]{1,0:T(8,128)(2,1)S(1)}, u32[]{:S(2)}, u32[]{:S(2)}) collective-permute-start(bf16[592,256]{1,0:T(8,128)(2,1)} %get-tuple-element.84), channel_id=1, source_target_pairs={{0,2},{2,0},{4,6},{6,4},{8,10},{10,8},{12,14},{14,12},{1,3},{3,1},... | collective-permute-start | bytes 909320 | tf_op jit(solution)/shard_map/ppermute | solution.py:572
  54.4 9.2 %collective-permute-start.11 = (bf16[2,48,256]{2,1,0:T(8,128)(2,1)S(1)}, bf16[2,48,256]{2,1,0:T(8,128)(2,1)S(1)}, u32[]{:S(2)}, u32[]{:S(2)}) collective-permute-start(bf16[2,48,256]{2,1,0:T(8,128)(2,1)S(1)} %copy-done.41), channel_id=1, source_target_pairs={{0,4},{4,0},{10,14},{14,10},{1,5},{5,1},{11,15},{15,11},{16,20},{2... | collective-permute-start | bytes 147464 | tf_op jit(solution)/shard_map/ppermute | solution.py:521
  56.4 9.3 %collective-permute-start.12 = (bf16[2,48,256]{2,1,0:T(8,128)(2,1)S(1)}, bf16[2,48,256]{2,1,0:T(8,128)(2,1)S(1)}, u32[]{:S(2)}, u32[]{:S(2)}) collective-permute-start(bf16[2,48,256]{2,1,0:T(8,128)(2,1)S(1)} %copy-done.40), channel_id=1, source_target_pairs={{0,6},{6,0},{8,14},{14,8},{1,7},{7,1},{9,15},{15,9},{16,22},{22,16... | collective-permute-start | bytes 147464 | tf_op jit(solution)/shard_map/ppermute | solution.py:521
  61.7 35.6 %collective-permute-start.19 = (bf16[592,256]{1,0:T(8,128)(2,1)}, bf16[592,256]{1,0:T(8,128)(2,1)S(1)}, u32[]{:S(2)}, u32[]{:S(2)}) collective-permute-start(bf16[592,256]{1,0:T(8,128)(2,1)} %get-tuple-element.106), channel_id=1, source_target_pairs={{0,2},{2,0},{4,6},{6,4},{8,10},{10,8},{12,14},{14,12},{1,3},{3,1},... | collective-permute-start | bytes 909320 | tf_op jit(solution)/shard_map/ppermute | solution.py:572
  61.7 7.4 %collective-permute-start.13 = (bf16[2,48,256]{2,1,0:T(8,128)(2,1)S(1)}, bf16[2,48,256]{2,1,0:T(8,128)(2,1)S(1)}, u32[]{:S(2)}, u32[]{:S(2)}) collective-permute-start(bf16[2,48,256]{2,1,0:T(8,128)(2,1)S(1)} %copy-done.39), channel_id=1, source_target_pairs={{0,8},{2,10},{4,12},{6,14},{8,0},{10,2},{12,4},{14,6},{1,9},{3,11}... | collective-permute-start | bytes 147464 | tf_op jit(solution)/shard_map/ppermute | solution.py:521
  63.6 72.8 %copy-start.22 = (bf16[2,48,256]{2,1,0:T(8,128)(2,1)}, bf16[2,48,256]{2,1,0:T(8,128)(2,1)S(1)}, u32[]{:S(2)}) copy-start(bf16[2,48,256]{2,1,0:T(8,128)(2,1)S(1)} %collective-permute-done.11.refs_2_) | copy-start | bytes 147460
  63.6 26.5 %collective-permute-start.10 = (bf16[2,192,256]{2,1,0:T(8,128)(2,1)S(1)}, bf16[2,192,256]{2,1,0:T(8,128)(2,1)S(1)}, u32[]{:S(2)}, u32[]{:S(2)}) collective-permute-start(bf16[2,192,256]{2,1,0:T(8,128)(2,1)S(1)} %copy-done.35), channel_id=1, source_target_pairs={{0,2},{2,0},{4,6},{6,4},{8,10},{10,8},{12,14},{14,12},{1,3},{3,1},... | collective-permute-start | bytes 589832 | tf_op jit(solution)/shard_map/ppermute | solution.py:521
  65.7 70.8 %copy-start.23 = (bf16[2,48,256]{2,1,0:T(8,128)(2,1)}, bf16[2,48,256]{2,1,0:T(8,128)(2,1)S(1)}, u32[]{:S(2)}) copy-start(bf16[2,48,256]{2,1,0:T(8,128)(2,1)S(1)} %collective-permute-done.12.refs_3_) | copy-start | bytes 147460
  65.7 24.5 %collective-permute-start.17 = (bf16[2,192,256]{2,1,0:T(8,128)(2,1)S(1)}, bf16[2,192,256]{2,1,0:T(8,128)(2,1)S(1)}, u32[]{:S(2)}, u32[]{:S(2)}) collective-permute-start(bf16[2,192,256]{2,1,0:T(8,128)(2,1)S(1)} %copy-done.34), channel_id=1, source_target_pairs={{0,14},{2,4},{4,2},{6,8},{8,6},{10,12},{12,10},{14,0},{1,15},{3,5}... | collective-permute-start | bytes 589832 | tf_op jit(solution)/shard_map/ppermute | solution.py:521
  69.2 67.3 %copy-start.24 = (bf16[2,48,256]{2,1,0:T(8,128)(2,1)}, bf16[2,48,256]{2,1,0:T(8,128)(2,1)S(1)}, u32[]{:S(2)}) copy-start(bf16[2,48,256]{2,1,0:T(8,128)(2,1)S(1)} %collective-permute-done.13.refs_4_) | copy-start | bytes 147460
  69.2 8.3 %collective-permute-start.14 = (bf16[2,48,256]{2,1,0:T(8,128)(2,1)S(1)}, bf16[2,48,256]{2,1,0:T(8,128)(2,1)S(1)}, u32[]{:S(2)}, u32[]{:S(2)}) collective-permute-start(bf16[2,48,256]{2,1,0:T(8,128)(2,1)S(1)} %copy-done.38), channel_id=1, source_target_pairs={{0,10},{4,14},{10,0},{14,4},{1,11},{5,15},{11,1},{15,5},{16,26},{2... | collective-permute-start | bytes 147464 | tf_op jit(solution)/shard_map/ppermute | solution.py:521
  77.5 59.0 %copy-start.25 = (bf16[2,48,256]{2,1,0:T(8,128)(2,1)}, bf16[2,48,256]{2,1,0:T(8,128)(2,1)S(1)}, u32[]{:S(2)}) copy-start(bf16[2,48,256]{2,1,0:T(8,128)(2,1)S(1)} %collective-permute-done.14.refs_5_) | copy-start | bytes 147460
  77.5 5.9 %collective-permute-start.15 = (bf16[2,48,256]{2,1,0:T(8,128)(2,1)S(1)}, bf16[2,48,256]{2,1,0:T(8,128)(2,1)S(1)}, u32[]{:S(2)}, u32[]{:S(2)}) collective-permute-start(bf16[2,48,256]{2,1,0:T(8,128)(2,1)S(1)} %copy-done.37), channel_id=1, source_target_pairs={{0,12},{2,14},{4,8},{6,10},{8,4},{10,6},{12,0},{14,2},{1,13},{3,15... | collective-permute-start | bytes 147464 | tf_op jit(solution)/shard_map/ppermute | solution.py:521
  83.4 53.1 %copy-start.26 = (bf16[2,48,256]{2,1,0:T(8,128)(2,1)}, bf16[2,48,256]{2,1,0:T(8,128)(2,1)S(1)}, u32[]{:S(2)}) copy-start(bf16[2,48,256]{2,1,0:T(8,128)(2,1)S(1)} %collective-permute-done.15.refs_6_) | copy-start | bytes 147460
  83.4 6.8 %collective-permute-start.16 = (bf16[2,48,256]{2,1,0:T(8,128)(2,1)S(1)}, bf16[2,48,256]{2,1,0:T(8,128)(2,1)S(1)}, u32[]{:S(2)}, u32[]{:S(2)}) collective-permute-start(bf16[2,48,256]{2,1,0:T(8,128)(2,1)S(1)} %copy-done.36), channel_id=1, source_target_pairs={{0,14},{2,12},{4,10},{6,8},{8,6},{10,4},{12,2},{14,0},{1,15},{3,13... | collective-permute-start | bytes 147464 | tf_op jit(solution)/shard_map/ppermute | solution.py:521
  90.2 46.4 %copy-start.27 = (bf16[2,48,256]{2,1,0:T(8,128)(2,1)}, bf16[2,48,256]{2,1,0:T(8,128)(2,1)S(1)}, u32[]{:S(2)}) copy-start(bf16[2,48,256]{2,1,0:T(8,128)(2,1)S(1)} %collective-permute-done.16.refs_7_) | copy-start | bytes 147460
  90.2 46.4 %copy-start.12 = (bf16[2,192,256]{2,1,0:T(8,128)(2,1)}, bf16[2,192,256]{2,1,0:T(8,128)(2,1)S(1)}, u32[]{:S(2)}) copy-start(bf16[2,192,256]{2,1,0:T(8,128)(2,1)S(1)} %collective-permute-done.10.refs_1_) | copy-start | bytes 589828
  90.2 46.4 %copy-start.13 = (bf16[2,192,256]{2,1,0:T(8,128)(2,1)}, bf16[2,192,256]{2,1,0:T(8,128)(2,1)S(1)}, u32[]{:S(2)}) copy-start(bf16[2,192,256]{2,1,0:T(8,128)(2,1)S(1)} %collective-permute-done.17.refs_8_) | copy-start | bytes 589828
  92.9 7.8 %collective-permute-start.29 = (bf16[160,256]{1,0:T(8,128)(2,1)}, bf16[160,256]{1,0:T(8,128)(2,1)S(1)}, u32[]{:S(2)}, u32[]{:S(2)}) collective-permute-start(bf16[160,256]{1,0:T(8,128)(2,1)} %get-tuple-element.129), channel_id=1, source_target_pairs={{0,4},{2,6},{4,0},{6,2},{8,12},{10,14},{12,8},{14,10},{1,5},{3,7},... | collective-permute-start | bytes 245768 | tf_op jit(solution)/shard_map/ppermute | solution.py:569
  93.0 11.5 %collective-permute-start.30 = (bf16[160,256]{1,0:T(8,128)(2,1)}, bf16[160,256]{1,0:T(8,128)(2,1)S(1)}, u32[]{:S(2)}, u32[]{:S(2)}) collective-permute-start(bf16[160,256]{1,0:T(8,128)(2,1)} %get-tuple-element.130), channel_id=1, source_target_pairs={{0,8},{2,10},{4,12},{6,14},{8,0},{10,2},{12,4},{14,6},{1,9},{3,11}... | collective-permute-start | bytes 245768 | tf_op jit(solution)/shard_map/ppermute | solution.py:569
  93.6 10.8 %collective-permute-start.31 = (bf16[160,256]{1,0:T(8,128)(2,1)}, bf16[160,256]{1,0:T(8,128)(2,1)S(1)}, u32[]{:S(2)}, u32[]{:S(2)}) collective-permute-start(bf16[160,256]{1,0:T(8,128)(2,1)} %get-tuple-element.131), channel_id=1, source_target_pairs={{0,12},{2,14},{4,8},{6,10},{8,4},{10,6},{12,0},{14,2},{1,13},{3,15... | collective-permute-start | bytes 245768 | tf_op jit(solution)/shard_map/ppermute | solution.py:569
  100.0 9.4 %collective-permute-start.20 = (bf16[160,256]{1,0:T(8,128)(2,1)}, bf16[160,256]{1,0:T(8,128)(2,1)S(1)}, u32[]{:S(2)}, u32[]{:S(2)}) collective-permute-start(bf16[160,256]{1,0:T(8,128)(2,1)} %get-tuple-element.108), channel_id=1, source_target_pairs={{0,4},{2,6},{4,0},{6,2},{8,12},{10,14},{12,8},{14,10},{1,5},{3,7},... | collective-permute-start | bytes 245768 | tf_op jit(solution)/shard_map/ppermute | solution.py:569
  100.0 12.2 %collective-permute-start.21 = (bf16[160,256]{1,0:T(8,128)(2,1)}, bf16[160,256]{1,0:T(8,128)(2,1)S(1)}, u32[]{:S(2)}, u32[]{:S(2)}) collective-permute-start(bf16[160,256]{1,0:T(8,128)(2,1)} %get-tuple-element.109), channel_id=1, source_target_pairs={{0,8},{2,10},{4,12},{6,14},{8,0},{10,2},{12,4},{14,6},{1,9},{3,11}... | collective-permute-start | bytes 245768 | tf_op jit(solution)/shard_map/ppermute | solution.py:569
  100.7 3.7 %copy-start.18 = (bf16[160,256]{1,0:T(8,128)(2,1)}, bf16[160,256]{1,0:T(8,128)(2,1)S(1)}, u32[]{:S(2)}) copy-start(bf16[160,256]{1,0:T(8,128)(2,1)S(1)} %collective-permute-done.29.refs_0_) | copy-start | bytes 245764
  100.7 11.5 %collective-permute-start.22 = (bf16[160,256]{1,0:T(8,128)(2,1)}, bf16[160,256]{1,0:T(8,128)(2,1)S(1)}, u32[]{:S(2)}, u32[]{:S(2)}) collective-permute-start(bf16[160,256]{1,0:T(8,128)(2,1)} %get-tuple-element.110), channel_id=1, source_target_pairs={{0,12},{2,14},{4,8},{6,10},{8,4},{10,6},{12,0},{14,2},{1,13},{3,15... | collective-permute-start | bytes 245768 | tf_op jit(solution)/shard_map/ppermute | solution.py:569
  106.8 21.8 %collective-permute-start.34 = (bf16[144,256]{1,0:T(8,128)(2,1)}, bf16[144,256]{1,0:T(8,128)(2,1)S(1)}, u32[]{:S(2)}, u32[]{:S(2)}) collective-permute-start(bf16[144,256]{1,0:T(8,128)(2,1)} %get-tuple-element.132), channel_id=1, source_target_pairs={{0,12},{2,14},{4,8},{6,10},{8,4},{10,6},{12,0},{14,2},{1,13},{3,15... | collective-permute-start | bytes 221192 | tf_op jit(solution)/shard_map/ppermute | solution.py:569
  107.2 21.4 %collective-permute-start.33 = (bf16[144,256]{1,0:T(8,128)(2,1)}, bf16[144,256]{1,0:T(8,128)(2,1)S(1)}, u32[]{:S(2)}, u32[]{:S(2)}) collective-permute-start(bf16[144,256]{1,0:T(8,128)(2,1)} %get-tuple-element.132), channel_id=1, source_target_pairs={{0,8},{2,10},{4,12},{6,14},{8,0},{10,2},{12,4},{14,6},{1,9},{3,11}... | collective-permute-start | bytes 221192 | tf_op jit(solution)/shard_map/ppermute | solution.py:569
  109.5 2.7 %copy-start.16 = (bf16[160,256]{1,0:T(8,128)(2,1)}, bf16[160,256]{1,0:T(8,128)(2,1)S(1)}, u32[]{:S(2)}) copy-start(bf16[160,256]{1,0:T(8,128)(2,1)S(1)} %collective-permute-done.20.refs_0_) | copy-start | bytes 245764
  109.5 19.1 %collective-permute-start.32 = (bf16[144,256]{1,0:T(8,128)(2,1)}, bf16[144,256]{1,0:T(8,128)(2,1)S(1)}, u32[]{:S(2)}, u32[]{:S(2)}) collective-permute-start(bf16[144,256]{1,0:T(8,128)(2,1)} %get-tuple-element.132), channel_id=1, source_target_pairs={{0,4},{2,6},{4,0},{6,2},{8,12},{10,14},{12,8},{14,10},{1,5},{3,7},... | collective-permute-start | bytes 221192 | tf_op jit(solution)/shard_map/ppermute | solution.py:569
  114.6 11.0 %collective-permute-start.25 = (bf16[144,256]{1,0:T(8,128)(2,1)}, bf16[144,256]{1,0:T(8,128)(2,1)S(1)}, u32[]{:S(2)}, u32[]{:S(2)}) collective-permute-start(bf16[144,256]{1,0:T(8,128)(2,1)} %get-tuple-element.111), channel_id=1, source_target_pairs={{0,12},{2,14},{4,8},{6,10},{8,4},{10,6},{12,0},{14,2},{1,13},{3,15... | collective-permute-start | bytes 221192 | tf_op jit(solution)/shard_map/ppermute | solution.py:569
  114.9 5.2 %collective-permute-start.23 = (bf16[144,256]{1,0:T(8,128)(2,1)}, bf16[144,256]{1,0:T(8,128)(2,1)S(1)}, u32[]{:S(2)}, u32[]{:S(2)}) collective-permute-start(bf16[144,256]{1,0:T(8,128)(2,1)} %get-tuple-element.111), channel_id=1, source_target_pairs={{0,4},{2,6},{4,0},{6,2},{8,12},{10,14},{12,8},{14,10},{1,5},{3,7},... | collective-permute-start | bytes 221192 | tf_op jit(solution)/shard_map/ppermute | solution.py:569
  120.1 5.5 %collective-permute-start.24 = (bf16[144,256]{1,0:T(8,128)(2,1)}, bf16[144,256]{1,0:T(8,128)(2,1)S(1)}, u32[]{:S(2)}, u32[]{:S(2)}) collective-permute-start(bf16[144,256]{1,0:T(8,128)(2,1)} %get-tuple-element.111), channel_id=1, source_target_pairs={{0,8},{2,10},{4,12},{6,14},{8,0},{10,2},{12,4},{14,6},{1,9},{3,11}... | collective-permute-start | bytes 221192 | tf_op jit(solution)/shard_map/ppermute | solution.py:569
  125.6 18.1 %copy-start.3 = (bf16[576,256]{1,0:T(8,128)(2,1)}, bf16[576,256]{1,0:T(8,128)(2,1)S(1)}, u32[]{:S(2)}) copy-start(bf16[576,256]{1,0:T(8,128)(2,1)S(1)} %constant_dynamic-update-slice_fusion.a_ref) | copy-start | bytes 884740
  125.6 7.7 %collective-permute-start.26 = (bf16[576,256]{1,0:T(8,128)(2,1)S(1)}, bf16[576,256]{1,0:T(8,128)(2,1)S(1)}, u32[]{:S(2)}, u32[]{:S(2)}) collective-permute-start(bf16[576,256]{1,0:T(8,128)(2,1)S(1)} %constant_dynamic-update-slice_fusion.a_ref), channel_id=1, source_target_pairs={{0,2},{2,0},{4,6},{6,4},{8,10},{10,8},{12,14},{14,12},{1,3},{3,1},... | collective-permute-start | bytes 884744 | tf_op jit(solution)/shard_map/ppermute | solution.py:572
  128.7 15.0 %copy-start.2 = (bf16[576,256]{1,0:T(8,128)(2,1)}, bf16[576,256]{1,0:T(8,128)(2,1)S(1)}, u32[]{:S(2)}) copy-start(bf16[576,256]{1,0:T(8,128)(2,1)S(1)} %constant_dynamic-update-slice_fusion.4.a_ref) | copy-start | bytes 884740
  128.7 7.8 %collective-permute-start.35 = (bf16[576,256]{1,0:T(8,128)(2,1)S(1)}, bf16[576,256]{1,0:T(8,128)(2,1)S(1)}, u32[]{:S(2)}, u32[]{:S(2)}) collective-permute-start(bf16[576,256]{1,0:T(8,128)(2,1)S(1)} %constant_dynamic-update-slice_fusion.4.a_ref), channel_id=1, source_target_pairs={{0,2},{2,0},{4,6},{6,4},{8,10},{10,8},{12,14},{14,12},{1,3},{3,1},... | collective-permute-start | bytes 884744 | tf_op jit(solution)/shard_map/ppermute | solution.py:572
  128.8 15.0 %collective-permute-start.27 = (bf16[576,256]{1,0:T(8,128)(2,1)S(1)}, bf16[576,256]{1,0:T(8,128)(2,1)S(1)}, u32[]{:S(2)}, u32[]{:S(2)}) collective-permute-start(bf16[576,256]{1,0:T(8,128)(2,1)S(1)} %constant_dynamic-update-slice_fusion.a_ref), channel_id=1, source_target_pairs={{0,1},{1,0},{2,3},{3,2},{4,5},{5,4},{6,7},{7,6},{8,9},{9,8},{10,11... | collective-permute-start | bytes 884744 | tf_op jit(solution)/shard_map/ppermute | solution.py:526
  133.3 10.4 %copy-start.6 = (bf16[576,256]{1,0:T(8,128)(2,1)}, bf16[576,256]{1,0:T(8,128)(2,1)S(1)}, u32[]{:S(2)}) copy-start(bf16[576,256]{1,0:T(8,128)(2,1)S(1)} %collective-permute-done.26.b_ref) | copy-start | bytes 884740
  133.3 10.4 %collective-permute-start.28 = (bf16[576,256]{1,0:T(8,128)(2,1)S(1)}, bf16[576,256]{1,0:T(8,128)(2,1)S(1)}, u32[]{:S(2)}, u32[]{:S(2)}) collective-permute-start(bf16[576,256]{1,0:T(8,128)(2,1)S(1)} %collective-permute-done.26.b_ref), channel_id=1, source_target_pairs={{0,1},{1,0},{2,3},{3,2},{4,5},{5,4},{6,7},{7,6},{8,9},{9,8},{10,11... | collective-permute-start | bytes 884744 | tf_op jit(solution)/shard_map/ppermute | solution.py:526
  133.3 14.2 %collective-permute-start.36 = (bf16[576,256]{1,0:T(8,128)(2,1)S(1)}, bf16[576,256]{1,0:T(8,128)(2,1)S(1)}, u32[]{:S(2)}, u32[]{:S(2)}) collective-permute-start(bf16[576,256]{1,0:T(8,128)(2,1)S(1)} %constant_dynamic-update-slice_fusion.4.a_ref), channel_id=1, source_target_pairs={{0,1},{1,0},{2,3},{3,2},{4,5},{5,4},{6,7},{7,6},{8,9},{9,8},{10,11... | collective-permute-start | bytes 884744 | tf_op jit(solution)/shard_map/ppermute | solution.py:526
  136.5 7.3 %copy-start.7 = (bf16[576,256]{1,0:T(8,128)(2,1)}, bf16[576,256]{1,0:T(8,128)(2,1)S(1)}, u32[]{:S(2)}) copy-start(bf16[576,256]{1,0:T(8,128)(2,1)S(1)} %collective-permute-done.35.b_ref) | copy-start | bytes 884740
  136.5 11.1 %collective-permute-start.37 = (bf16[576,256]{1,0:T(8,128)(2,1)S(1)}, bf16[576,256]{1,0:T(8,128)(2,1)S(1)}, u32[]{:S(2)}, u32[]{:S(2)}) collective-permute-start(bf16[576,256]{1,0:T(8,128)(2,1)S(1)} %collective-permute-done.35.b_ref), channel_id=1, source_target_pairs={{0,1},{1,0},{2,3},{3,2},{4,5},{5,4},{6,7},{7,6},{8,9},{9,8},{10,11... | collective-permute-start | bytes 884744 | tf_op jit(solution)/shard_map/ppermute | solution.py:526
  (16 other events, 11.3 us)

commit v3 on v2

--- a/solution.py
+++ b/solution.py
@@ -19,38 +19,15 @@
         self.ROW = 6 * face
         self.SLOT = -(-(2 * rows + 2) // 8) * 8
         self.BASE = 6 * self.SLOT
-        self.MIR = 16 * rows
         self.o_msg = self.N
         self.o_mir = self.o_msg + tiles * self.BASE
-        self.o_row = self.o_mir + self.MIR
+        self.o_row = self.o_mir + self.BASE
         self.NT = self.o_row + 2 * self.ROW
         self.WE = 12 * 8
         self.S = self.WE + self.ROW
 
     def messages(self):
-        rows = [self.BASE] * (self.T - 1) + [self.MIR, self.BASE + self.ROW]
-        rows[1] += self.ROW
-        return rows
-
-    def table_parts(self):
-        parts = [(k, 0, self.BASE, self.o_msg + k * self.BASE) for k in range(self.T - 1)]
-        parts.append((self.T, 0, self.BASE, self.o_msg + (self.T - 1) * self.BASE))
-        parts.append((self.T - 1, 0, self.MIR, self.o_mir))
-        parts.append((1, self.BASE, self.ROW, self.o_row))
-        parts.append((self.T, self.BASE, self.ROW, self.o_row + self.ROW))
-        return parts
-
-    def pairs(self):
-        T = self.T
-        edges = (0, T - 1)
-
-        def needed(i, d):
-            return i in edges or d in edges or d in (T - 2 - i, T - i)
-
-        out = [[(i, i ^ k) for i in range(T) if k == 1 or needed(i, i ^ k)] for k in range(T - 1)]
-        out.append([(i, T - 1 - i) for i in range(T)])
-        out.append([(i, (i + 1) % T if i % 2 else (i - 1) % T) for i in range(T)])
-        return out
+        return [(self.T, 2, self.BASE, self.C), (2, self.ROW, self.C), (2, self.BASE + self.ROW, self.C)]
 
 
 def col_iota(n):
@@ -87,8 +64,15 @@
         gvalue = ep[f, far_edge]
         column = jnp.where(gvalue % 4 == 1, F - 1, 0) + (gvalue // 4) * (R * F)
         high = jnp.where(to_edge, column + F * i2, jnp.where(i2 < 2, sides + i2 * (F - 1), -1))
-        parts.append(jnp.where(i2 < 0, low, jnp.where(i2 < R, high, -1)))
+        strips = jnp.where(i2 < 0, low, jnp.where(i2 < R, high, -1))
+        mirror = (d == T - 1 - t) & jnp.logical_not(at_edge)
+        parts.append(jnp.where(mirror, mirror_slot(dm, f), strips))
     return parts
+
+
+def mirror_slot(dm, f):
+    i = col_iota(dm.SLOT)
+    return jnp.where(i < 2 * dm.R, (f * dm.R + i // 2) * dm.F + (i % 2) * (dm.F - 1), -1)
 
 
 def row_targets(dm, row):
@@ -96,27 +80,20 @@
     return [(f * dm.R + row) * dm.F + j for f in range(6)]
 
 
-def message_targets(dm, ep, t, k):
-    R, F, T = dm.R, dm.F, dm.T
-    if k == T - 1:
-        s = col_iota(16)
-        cells = (s // 2) * (R * F) + (s % 2) * (F - 1)
-        parts = [jnp.where(s < 12, cells + r * F, -1) for r in range(R)]
-    elif k == T:
-        parts = strip_targets(dm, ep, t, T - 1 - t)
-        parts += row_targets(dm, jnp.where(t % 2 == 1, R - 1, 0))
-    else:
-        parts = strip_targets(dm, ep, t, t ^ k)
-        if k == 1:
-            parts += row_targets(dm, jnp.where(t % 2 == 0, R - 1, 0))
-    return jnp.concatenate(parts, axis=0)
-
-
 def write_messages(dm, ep, t, sources, refs):
-    for k in range(dm.T + 1):
-        hot = one_hot(message_targets(dm, ep, t, k), dm.N)
-        for which, source in enumerate(sources):
-            refs[k][which] = jnp.dot(hot, source, preferred_element_type=F32).astype(BF)
+    R, T = dm.R, dm.T
+    strips_ref, pair_ref, ring_ref = refs
+
+    def pick(parts, which):
+        hot = one_hot(jnp.concatenate(parts, axis=0), dm.N)
+        return jnp.dot(hot, sources[which], preferred_element_type=F32).astype(BF)
+
+    for which in range(2):
+        for d in range(T):
+            strips_ref[d, which] = pick(strip_targets(dm, ep, t, d), which)
+        pair_ref[which] = pick(row_targets(dm, jnp.where(t % 2 == 0, R - 1, 0)), which)
+        mirror = [mirror_slot(dm, f) for f in range(6)]
+        ring_ref[which] = pick(mirror + row_targets(dm, jnp.where(t % 2 == 1, R - 1, 0)), which)
 
 
 def pack_kernel(dm, ep, x_ref, up_ref, *refs):
@@ -132,8 +109,9 @@
     inside = (q >= 0) & (q < F) & (m < R + 2)
     row_prev = dm.o_row + (1 - odd) * dm.ROW
     row_next = dm.o_row + odd * dm.ROW
-    side_first = dm.o_msg + (t ^ (T - t)) * dm.BASE + jnp.where(t == 1, R + 2, 0)
-    side_last = dm.o_msg + (t ^ (T - 2 - t)) * dm.BASE + jnp.where(t == T - 2, R + 2, 0)
+    side_first = dm.o_msg + (T - t) * dm.BASE + jnp.where(t == 1, R + 2, 0)
+    side_last = dm.o_msg + (T - 2 - t) * dm.BASE + jnp.where(t == T - 2, R + 2, 0)
+    mirror = jnp.where((t == 0) | (t == T - 1), dm.o_mir, dm.o_msg + (T - 1 - t) * dm.BASE)
     for f in range(6):
         for edge in (3, 1):
             value = ep[f, edge]
@@ -143,18 +121,16 @@
             is_col = (e2 % 2) == 1
             side = jnp.where(e2 == 1, 1, 0)
             column = side * (F - 1)
-            s = 2 * f2 + side
             slot = f2 * dm.SLOT + side
-            src_k = jnp.where(e2 == 0, t, t ^ (T - 1))
-            row = dm.o_msg + src_k * dm.BASE + f2 * dm.SLOT
+            row = dm.o_msg + jnp.where(e2 == 0, 0, T - 1) * dm.BASE + f2 * dm.SLOT
             i0 = jnp.where(is_col, jnp.where(reverse, side_first + slot, row_prev + f2 * F + column), row)
             i4 = jnp.where(
                 is_col, jnp.where(reverse, side_last + slot, row_next + f2 * F + column), row + R + 1
             )
             base = jnp.where(
-                is_col, jnp.where(reverse, dm.o_mir + 16 * R + s, (f2 * R - 1) * F + column), row
+                is_col, jnp.where(reverse, mirror + 2 * R + slot, (f2 * R - 1) * F + column), row
             )
-            step = jnp.where(is_col, jnp.where(reverse, -16, F), 1)
+            step = jnp.where(is_col, jnp.where(reverse, -2, F), 1)
             target = jnp.where(m == 0, i0, jnp.where(m == R + 1, i4, base + step * m))
             parts.append(jnp.where(inside, target, -1))
     j = col_iota(F)
@@ -179,9 +155,6 @@
             lin_step = jnp.where(reverse, -1, 1)
             k0 = jnp.where(reverse, T - 1, 0)
             ks = jnp.where(reverse, -1, 1)
-            if edge == 2:
-                k0 = T - 1 - k0
-                ks = -ks
             col_base = dm.o_msg + k0 * dm.BASE + f * dm.SLOT + R + 2 + jnp.where(reverse, R - 1, 0)
             base = jnp.where(is_col, col_base, lin_base)
             sj = jnp.where(is_col, 0, lin_step)
@@ -200,8 +173,12 @@
     out = []
     for which in range(2):
         table_ref[0 : dm.N] = own[which]
-        for k, row, count, at in dm.table_parts():
-            table_ref[at : at + count] = messages[k][which, row : row + count]
+        for k in range(dm.T):
+            at = dm.o_msg + k * dm.BASE
+            table_ref[at : at + dm.BASE] = messages[0][k, which]
+        table_ref[dm.o_mir : dm.o_row] = messages[2][which, : dm.BASE]
+        table_ref[dm.o_row : dm.o_row + dm.ROW] = messages[1][which]
+        table_ref[dm.o_row + dm.ROW :] = messages[2][which, dm.BASE :]
         out.append(jnp.dot(hot, table_ref[...], preferred_element_type=F32))
     return out
 
@@ -301,22 +278,23 @@
         acc_ref[(R - 1) * dm.ROW : R * dm.ROW] += strips[dm.WE :]
 
 
-def put_tap(send_ref, keep_ref, p, tap, value):
-    half = send_ref.shape[0] - EXTRA
-    unit = value.shape[0] // 2
-    for part in range(2):
-        row = tap * 2 * unit + part * unit
-        owner = row // half
-        at = row - owner * half
-        piece = value[part * unit : (part + 1) * unit]
-
-        @pl.when(p == owner)
+def put_tap(dm, send_ref, keep_ref, p, which, tap, value):
+    size = 9 * dm.C // (2 * dm.T)
+    start, stop = tap * dm.C, (tap + 1) * dm.C
+    for block in range(2 * dm.T):
+        low, high = max(start, block * size), min(stop, (block + 1) * size)
+        if low >= high:
+            continue
+        at = (block % dm.T) * 2 * size + which * size + low - block * size
+        piece = value[low - start : high - start]
+
+        @pl.when(p == block // dm.T)
         def _():
-            keep_ref[at : at + unit] = piece
-
-        @pl.when(p != owner)
+            keep_ref[at : at + high - low] = piece
+
+        @pl.when(p != block // dm.T)
         def _():
-            send_ref[at : at + unit] = piece.astype(BF)
+            send_ref[at : at + high - low] = piece.astype(BF)
 
 
 def put_extra(send_ref, keep_ref, row):
@@ -331,11 +309,10 @@
 
 def first_kernel(dm, ep, x_ref, up_ref, w1_ref, bias_ref, w2_ref, *refs):
     T, R, F, N, C = dm.T, dm.R, dm.F, dm.N, dm.C
-    M = T + 1
-    messages = refs[:M]
-    s1_ref, k1_ref, s2_ref, k2_ref, hid_ref, inner_ref = refs[M : M + 6]
-    out_messages = refs[M + 6 : 2 * M + 6]
-    table_ref, frame_ref, xs_ref, us_ref, z_ref, before_ref, acc_ref, hcat_ref = refs[2 * M + 6 :]
+    messages = refs[:3]
+    send_ref, keep_ref, hid_ref, inner_ref = refs[3:7]
+    out_messages = refs[7:10]
+    table_ref, frame_ref, xs_ref, us_ref, z_ref, before_ref, acc_ref, hcat_ref = refs[10:]
     t, p = lax.axis_index("tile"), lax.axis_index("dp")
     own = (x_ref[...].reshape(N, C), up_ref[...].reshape(N, C))
     gx, gu = gather_ghosts(dm, ep, t, own, messages, table_ref)
@@ -375,8 +352,7 @@
             main = us_ref[2 - b, (2 - a) * dm.ROW : (2 - a + R) * dm.ROW]
             grad = jnp.dot(hidden_t, main, preferred_element_type=F32)
             grad = grad + jnp.dot(edge_t, z_ref[3 * a + b].astype(BF), preferred_element_type=F32)
-            put_tap(s2_ref, k2_ref, p, 3 * a + b, grad)
-    put_extra(s2_ref, k2_ref, jnp.zeros((1, C), F32))
+            put_tap(dm, send_ref, keep_ref, p, 0, 3 * a + b, grad)
     for r in range(R):
         for f in range(6):
             at = (r * 6 + f) * F
@@ -395,8 +371,8 @@
                 (((0,), (0,)), ((), ())),
                 preferred_element_type=F32,
             )
-            put_tap(s1_ref, k1_ref, p, 3 * a + b, grad)
-    put_extra(s1_ref, k1_ref, jnp.sum(before_grad, axis=0, keepdims=True))
+            put_tap(dm, send_ref, keep_ref, p, 1, 3 * a + b, grad)
+    put_extra(send_ref, keep_ref, jnp.sum(before_grad, axis=0, keepdims=True))
     for r in range(R):
         for f in range(6):
             at = (r * 6 + f) * F
@@ -408,9 +384,9 @@
 
 def second_kernel(dm, ep, x_ref, d_ref, hid_ref, inner_ref, w1_ref, w2_ref, *refs):
     T, R, F, N, C = dm.T, dm.R, dm.F, dm.N, dm.C
-    messages = refs[: T + 1]
-    state_ref, grad_ref = refs[T + 1 : T + 3]
-    table_ref, frame_ref, shift_ref, z_ref, acc_ref = refs[T + 3 :]
+    messages = refs[:3]
+    state_ref, grad_ref = refs[3:5]
+    table_ref, frame_ref, shift_ref, z_ref, acc_ref = refs[5:]
     t = lax.axis_index("tile")
     own = (hid_ref[...].reshape(N, C), inner_ref[...].reshape(N, C))
     gh, gi = gather_ghosts(dm, ep, t, own, messages, table_ref)
@@ -446,55 +422,79 @@
     return keep[n : n + 1] + recv[n : n + 1].astype(F32) + recv[n + 1 : n + 2].astype(F32)
 
 
-def halve_kernel(pieces, shift, keep_ref, recv_ref, *refs):
-    out_keep, out_sends, sum_ref = refs[0], refs[1:pieces], refs[pieces]
-    n = keep_ref.shape[0] - EXTRA
-    size = n // pieces
-    t = lax.axis_index("tile")
-    own = t % 2 if shift == 0 else t // 2
-    sum_ref[...] = keep_ref[0:n] + recv_ref[0:n].astype(F32)
-    extra = extra_sum(keep_ref, recv_ref, n)
-    out_keep[0:size] = sum_ref[pl.ds(pl.multiple_of(own * size, 8), size)]
+def extra_rows(extra):
     i = lax.broadcasted_iota(jnp.int32, (EXTRA, extra.shape[1]), 0)
     high = extra.astype(BF).astype(F32)
-    out_keep[size:] = jnp.where(i == 0, extra, 0.0)
     tail = jnp.where(i == 0, high, jnp.where(i == 1, extra - high, 0.0)).astype(BF)
-    for j in range(1, pieces):
-        at = pl.multiple_of((own ^ j) * size, 8)
-        out_sends[j - 1][0:size] = sum_ref[pl.ds(at, size)].astype(BF)
-        out_sends[j - 1][size:] = tail
-
-
-def last_kernel(keep_ref, *refs):
-    recvs, (block_ref, extra_ref) = refs[:-2], refs[-2:]
+    return jnp.where(i == 0, extra, 0.0), tail
+
+
+def half_kernel(keep_ref, recv_ref, out_keep, out_send):
     n = keep_ref.shape[0] - EXTRA
+    size = n // 2
+    own = lax.axis_index("tile") % 2
+    mine = pl.multiple_of(own * size, 8)
+    far = pl.multiple_of((1 - own) * size, 8)
+    out_keep[0:size] = keep_ref[pl.ds(mine, size)] + recv_ref[pl.ds(mine, size)].astype(F32)
+    out_send[0:size] = (keep_ref[pl.ds(far, size)] + recv_ref[pl.ds(far, size)].astype(F32)).astype(BF)
+    keep, tail = extra_rows(extra_sum(keep_ref, recv_ref, n))
+    out_keep[size:] = keep
+    out_send[size:] = tail
+
+
+def block_kernel(zcount, keep_ref, recv_ref, out_keep, out_sends):
+    n = keep_ref.shape[0] - EXTRA
+    size = n // zcount
+    own = lax.axis_index("tile") // 2
+    keep, tail = extra_rows(extra_sum(keep_ref, recv_ref, n))
+    for j in range(zcount):
+        at = slice(j * size, (j + 1) * size)
+        total = keep_ref[at] + recv_ref[at].astype(F32)
+        out_sends[j, 0:size] = total.astype(BF)
+        out_sends[j, size:] = tail
+
+        @pl.when(own == j)
+        def _():
+            out_keep[0:size] = total
+
+    out_keep[size:] = keep
+
+
+def last_kernel(zcount, keep_ref, recv_ref, block_ref, extra_ref):
+    n = keep_ref.shape[0] - EXTRA
+    own = lax.axis_index("tile") // 2
     total = keep_ref[0:n]
     extra = keep_ref[n : n + 1]
-    for ref in recvs:
-        total = total + ref[0:n].astype(F32)
-        extra = extra + ref[n : n + 1].astype(F32) + ref[n + 1 : n + 2].astype(F32)
-    block_ref[...] = total.astype(BF)
-    extra_ref[...] = jnp.broadcast_to(extra, extra_ref.shape)
-
-
-def normal_kernel(zcount, a_ref, b_ref, c_ref, d_ref, extra_ref, out_ref, bias_ref):
+    for j in range(zcount):
+        far = own != j
+        total = total + jnp.where(far, recv_ref[j, 0:n].astype(F32), 0.0)
+        parts = recv_ref[j, n : n + 2].astype(F32)
+        extra = extra + jnp.where(far, parts[0:1] + parts[1:2], 0.0)
+    for j in range(zcount):
+        block_ref[j] = total.astype(BF)
+    extra_ref[...] = extra
+
+
+def normal_kernel(zcount, a_ref, b_ref, c_ref, d_ref, extra_ref, second_ref, first_ref, bias_ref):
     t, p = lax.axis_index("tile"), lax.axis_index("dp")
     refs = (a_ref, b_ref, c_ref, d_ref)
-    square = None
-    for ref in refs:
-        v = ref[...].astype(F32)
-        s = jnp.sum(v * v, axis=0, keepdims=True)
-        square = s if square is None else square + s
-    mean = jnp.sum(square, keepdims=True) / (out_ref.shape[0] * out_ref.shape[1])
-    scale = lax.rsqrt(mean + 1e-06)
-    size = a_ref.shape[0] // zcount
-    for index, ref in enumerate(refs):
-        block = (p ^ (index // 2)) * 2 + ((t % 2) ^ (index % 2))
-        for j in range(zcount):
-            at = (block * zcount + ((t // 2) ^ j)) * size
-            value = ref[j * size : (j + 1) * size].astype(F32) * scale
-            out_ref[pl.ds(pl.multiple_of(at, 8), size)] = value
-    extra = extra_ref[0:1]
+    size = a_ref.shape[1] // 2
+    for which, out_ref in enumerate((second_ref, first_ref)):
+        rows = slice(which * size, (which + 1) * size)
+        square = None
+        for ref in refs:
+            for j in range(zcount):
+                v = ref[j, rows].astype(F32)
+                s = jnp.sum(v * v, axis=0, keepdims=True)
+                square = s if square is None else square + s
+        mean = jnp.sum(square, keepdims=True) / (out_ref.shape[0] * out_ref.shape[1])
+        scale = lax.rsqrt(mean + 1e-06)
+        for index, ref in enumerate(refs):
+            block = (p ^ (index // 2)) * 2 + ((t % 2) ^ (index % 2))
+            for j in range(zcount):
+                at = pl.multiple_of((block * zcount + j) * size, 8)
+                out_ref[pl.ds(at, size)] = ref[j, rows].astype(F32) * scale
+    extra = extra_ref[...]
     bias_mean = jnp.mean(extra * extra, keepdims=True)
     bias_ref[...] = extra * lax.rsqrt(bias_mean + 1e-06)
 
@@ -516,9 +516,14 @@
     return run
 
 
-def exchange(dm, messages):
-    pairs = dm.pairs()
-    return [messages[0]] + [lax.ppermute(messages[k], "tile", pairs[k]) for k in range(1, dm.T + 1)]
+def exchange(tiles, messages):
+    strips, pair, ring = messages
+    other = [(i, (i + 1) % tiles if i % 2 else (i - 1) % tiles) for i in range(tiles)]
+    return [
+        lax.all_to_all(strips, "tile", 0, 0),
+        lax.ppermute(pair, "tile", [(i, i ^ 1) for i in range(tiles)]),
+        lax.ppermute(ring, "tile", other),
+    ]
 
 
 def swap_dp(v):
@@ -535,18 +540,18 @@
     d = state_cotangents[state_cotangents.shape[0] - 1].reshape(planes)
     w1 = w_first.reshape(9, channels, channels)
     w2 = w_second.reshape(9, channels, channels)
-    msg_shapes = [((2, n, channels), BF) for n in dm.messages()]
+    msg_shapes = [(shape, BF) for shape in dm.messages()]
     flat = (dm.N, channels)
     messages = call(functools.partial(pack_kernel, dm), msg_shapes, smem_first=True)(
         edge_partner, x.reshape(flat), d.reshape(flat)
     )
-    messages = exchange(dm, messages)
-    half = 9 * channels // 2
+    messages = exchange(tiles, messages)
+    half = 9 * channels
     shift_rows = (3, (rows + 2) * dm.ROW, channels)
     frame = (rows + 2, 6, face + 16, channels)
     outs = call(
         functools.partial(first_kernel, dm),
-        [((half + EXTRA, channels), BF), ((half + EXTRA, channels), F32)] * 2 + [(planes, BF)] * 2 + msg_shapes,
+        [((half + EXTRA, channels), BF), ((half + EXTRA, channels), F32)] + [(planes, BF)] * 2 + msg_shapes,
         [
             ((dm.NT, channels), BF),
             (frame, F32),
@@ -559,57 +564,35 @@
         ],
         smem_first=True,
     )(edge_partner, x, d, w1, bias.reshape(1, channels), w2, *messages)
-    send_first, keep_first, send_second, keep_second, hidden, inner = outs[:6]
+    send, keep, hidden, inner = outs[:4]
 
     zcount = tiles // 2
     n = half // 2
     m = n // zcount
-
-    def along_z(v, j):
-        return lax.ppermute(v, "tile", [(i, i ^ (2 * j)) for i in range(tiles)])
+    groups = [[h + 2 * z for z in range(zcount)] for h in range(2)]
 
     def along_y(v):
         return lax.ppermute(v, "tile", [(i, i ^ 1) for i in range(tiles)])
 
-    def reduce_y(keep, recv):
-        keep, send = call(
-            functools.partial(halve_kernel, 2, 0),
-            [((n + EXTRA, channels), F32), ((n + EXTRA, channels), BF)],
-            [((2 * n, channels), F32)],
-        )(keep, recv)
-        return keep, along_y(send)
-
-    def reduce_z(keep, recv):
-        keep, *sends = call(
-            functools.partial(halve_kernel, zcount, 1),
-            [((m + EXTRA, channels), F32)] + [((m + EXTRA, channels), BF)] * (zcount - 1),
-            [((n, channels), F32)],
-        )(keep, recv)
-        return keep, [along_z(v, j + 1) for j, v in enumerate(sends)]
-
-    def gather_z(keep, recvs):
-        block, extra = call(last_kernel, [((m, channels), BF), ((8, channels), F32)])(keep, *recvs)
-        return [block] + [along_z(block, j) for j in range(1, zcount)], extra
-
-    def finish(own, other, extra):
-        return call(
-            functools.partial(normal_kernel, zcount),
-            [((9 * channels, channels), F32), ((1, channels), F32)],
-        )(own, other, swap_dp(own), swap_dp(other), extra)
-
-    keep2, recv2 = reduce_y(keep_second, swap_dp(send_second))
-    messages = exchange(dm, outs[6:])
-    keep1, recv1 = reduce_y(keep_first, swap_dp(send_first))
-    (keep2, recv2), messages = lax.optimization_barrier(((keep2, recv2), messages))
-    keep2, recvs2 = reduce_z(keep2, recv2)
-    keep1, recvs1 = reduce_z(keep1, recv1)
-    blocks2, extra2 = gather_z(keep2, recvs2)
-    blocks1, extra1 = gather_z(keep1, recvs1)
-    own2 = jnp.concatenate(blocks2, axis=0)
-    other2 = along_y(own2)
-    own1 = jnp.concatenate(blocks1, axis=0)
-    other1 = along_y(own1)
-    messages, _ = lax.optimization_barrier((messages, own1))
+    def along_z(v):
+        return lax.all_to_all(v, "tile", 0, 0, axis_index_groups=groups)
+
+    keep, send = call(half_kernel, [((n + EXTRA, channels), F32), ((n + EXTRA, channels), BF)])(
+        keep, swap_dp(send)
+    )
+    recv = along_y(send)
+    messages = exchange(tiles, outs[4:])
+    recv, messages = lax.optimization_barrier((recv, messages))
+    keep, sends = call(
+        functools.partial(block_kernel, zcount),
+        [((m + EXTRA, channels), F32), ((zcount, m + EXTRA, channels), BF)],
+    )(keep, recv)
+    blocks, extra = call(
+        functools.partial(last_kernel, zcount), [((zcount, m, channels), BF), ((1, channels), F32)]
+    )(keep, along_z(sends))
+    own = along_z(blocks)
+    other = along_y(own)
+    messages, _ = lax.optimization_barrier((messages, own))
     state, grad = call(
         functools.partial(second_kernel, dm),
         [(planes, BF), (planes, F32)],
@@ -622,8 +605,10 @@
         ],
         smem_first=True,
     )(edge_partner, x, d, hidden, inner, w1, w2, *messages)
-    second_step, _ = finish(own2, other2, extra2)
-    first_step, bias_step = finish(own1, other1, extra1)
+    second_step, first_step, bias_step = call(
+        functools.partial(normal_kernel, zcount),
+        [((half, channels), F32)] * 2 + [((1, channels), F32)],
+    )(own, other, swap_dp(own), swap_dp(other), extra)
     return (
         state.reshape(initial_state.shape),
         grad.reshape(initial_state.shape),

time: 152 us -> 151 us (level)
  starting transfers between devices: 62.4 us -> 21.2 us
  blocking collectives: 0 us -> 40.6 us
  waiting for transfers between devices: 33.6 us -> 43.8 us
  Pallas kernels: 44.2 us -> 38.7 us
  local copies, waits for them, and re-layouts: 10 us -> 5.08 us
    ppermute x28 -> x4, starting transfers between devices: 54.7 us -> 8.02 us  [the longest x2 8.01 us: exchange(): lax.ppermute(ring, 'tile', other)]
    all_to_all x0 -> x2, blocking collectives: none -> 40.6 us  [along_z(): return lax.all_to_all(v, 'tile', 0, 0, axis_index_groups=groups)]
    all_to_all x0 -> x2, starting transfers between devices: none -> 10.7 us  [exchange(): lax.all_to_all(strips, 'tile', 0, 0)]
    ppermute x4 -> x2, waiting for transfers between devices: 7.12 us -> 13.6 us  [along_y(): return lax.ppermute(v, 'tile', [(i, i ^ 1) for i in range(tiles)])]
    pallas_call x11 -> x7, Pallas kernels: 44.2 us -> 38.7 us  [run(): pl.pallas_call(kernel, out_shape=[jax.ShapeDtypeStruct(s, dt) for s, dt i...]
    ppermute x28 -> x4, waiting for transfers between devices: 24.7 us -> 30.2 us  [the longest x2 27.2 us: exchange(): lax.ppermute(pair, 'tile', [(i, i ^ 1) for i in range(tiles)])]
    unnamed x91 -> x29, local copies, waits for them, and re-layouts: 9.98 us -> 5.08 us
    ppermute x4 -> x2, starting transfers between devices: 6.49 us -> 2.43 us  [along_y(): return lax.ppermute(v, 'tile', [(i, i ^ 1) for i in range(tiles)])]
  transfers between devices with their start and end apart: 38 -> 11, of which waited for: 9 -> 4; matrix products, arithmetic and copies ran while one was open for 1% -> 0% of each run, Pallas kernels for 15% -> 7%
where the time goes in v3:
time: 151 us; the launch traced here: 150 us
  waiting for transfers between devices  43.8 us (29%)
  blocking collectives  40.6 us (27%)
  Pallas kernels  38.7 us (26%)
  starting transfers between devices  21.2 us (14%)
  local copies, waits for them, and re-layouts  5.08 us (3%)
    all_to_all x2, blocking collectives, along_z(): return lax.all_to_all(v, 'tile', 0, 0, axis_index_groups=groups)  40.6 us
    pallas_call x7, Pallas kernels, run(): pl.pallas_call(kernel, out_shape=[jax.ShapeDtypeStruct(s, dt) for s, dt i...  38.7 us
    ppermute x2, waiting for transfers between devices, exchange(): lax.ppermute(pair, 'tile', [(i, i ^ 1) for i in range(tiles)])  27.2 us
    ppermute x2, waiting for transfers between devices, along_y(): return lax.ppermute(v, 'tile', [(i, i ^ 1) for i in range(tiles)])  13.6 us
    all_to_all x2, starting transfers between devices, exchange(): lax.all_to_all(strips, 'tile', 0, 0)  10.7 us
    ppermute x2, starting transfers between devices, exchange(): lax.ppermute(ring, 'tile', other)  8.01 us
    unnamed x29, local copies, waits for them, and re-layouts  5.08 us
  transfers between devices with their start and end apart: 11, of which 4 were waited for; matrix products, arithmetic and copies ran while one was open for 0% of the time, Pallas kernels for 7%

profile of v3, /device:TPU:0, one launch (start us, length us, event | category | flops | bytes accessed | tf_op | source)
XLA Modules:
  0.0 150.2 jit_solution(15185779677515247537)
XLA Ops:
  0.6 1.4 copy.13.ep
  2.0 3.3 %shard_map.101 = (bf16[8,2,48,256]{3,2,1,0:T(8,128)(2,1)}, bf16[2,144,256]{2,1,0:T(8,128)(2,1)}, bf16[2,192,256]{2,1,0:T(8,128)(2,1)}) custom-call(s32[6,4]{1,0:T(8,128)} %copy.13.ep, bf16[432,256]{1,0:T(8,128)(2,1)} %bitcast.16, bf16[432,256]{1,0:T(8,128)(2,1)} %bitcast.19), custom_call_target="tpu_custom_call" | custom-call | tf_op jit(solution)/shard_map/pallas_call | solution.py:507
  5.3 7.3 %all-to-all-start = ((bf16[8,2,48,256]{3,2,1,0:T(8,128)(2,1)}), bf16[8,2,48,256]{3,2,1,0:T(8,128)(2,1)S(1)}, u32[]{:S(2)}, u32[]{:S(2)}) async-start(bf16[8,2,48,256]{3,2,1,0:T(8,128)(2,1)} %get-tuple-element.33), calls=%async_computation | async-start | bytes 786432 | tf_op jit(solution)/shard_map/all_to_all | solution.py:523
  12.6 4.7 %collective-permute-start.1 = (bf16[2,192,256]{2,1,0:T(8,128)(2,1)}, bf16[2,192,256]{2,1,0:T(8,128)(2,1)S(1)}, u32[]{:S(2)}, u32[]{:S(2)}) collective-permute-start(bf16[2,192,256]{2,1,0:T(8,128)(2,1)} %get-tuple-element.35), channel_id=1, source_target_pairs={{0,14},{2,4},{4,2},{6,8},{8,6},{10,12},{12,10},{14,0},{1,15},{3,5}... | collective-permute-start | bytes 589832 | tf_op jit(solution)/shard_map/ppermute | solution.py:525
  17.3 0.0 collective-permute-start
  17.3 7.9 %collective-permute-done.refs_1_ = bf16[2,144,256]{2,1,0:T(8,128)(2,1)S(1)} collective-permute-done((bf16[2,144,256]{2,1,0:T(8,128)(2,1)}, bf16[2,144,256]{2,1,0:T(8,128)(2,1)S(1)}, u32[]{:S(2)}, u32[]{:S(2)}) %collective-permute-start) | collective-permute-done | bytes 147488 | tf_op jit(solution)/shard_map/ppermute | solution.py:524
  25.2 0.0 copy-start.11
  25.2 3.0 %collective-permute-done.1.refs_2_ = bf16[2,192,256]{2,1,0:T(8,128)(2,1)S(1)} collective-permute-done((bf16[2,192,256]{2,1,0:T(8,128)(2,1)}, bf16[2,192,256]{2,1,0:T(8,128)(2,1)S(1)}, u32[]{:S(2)}, u32[]{:S(2)}) %collective-permute-start.1) | collective-permute-done | bytes 196640 | tf_op jit(solution)/shard_map/ppermute | solution.py:525
  28.2 0.0 copy-start.9
  28.2 0.0 all-to-all-done.refs_0_
  28.2 0.0 copy-start.2
  28.2 0.0 copy-done.11
  28.2 0.7 copy-done.9
  28.8 0.1 copy-done.2
  29.0 15.7 %shard_map.102 = (bf16[2320,256]{1,0:T(8,128)(2,1)}, f32[2320,256]{1,0:T(8,128)}, bf16[18,24,256]{2,1,0:T(8,128)(2,1)}, bf16[18,24,256]{2,1,0:T(8,128)(2,1)}, bf...) custom-call(s32[6,4]{1,0:T(8,128)} %copy.13.ep, ...), custom_call_target="tpu_custom_call" | custom-call | tf_op jit(solution)/shard_map/pallas_call | solution.py:507
  44.7 0.0 collective-permute-start.2
  44.7 3.5 %all-to-all-start.1 = ((bf16[8,2,48,256]{3,2,1,0:T(8,128)(2,1)}), bf16[8,2,48,256]{3,2,1,0:T(8,128)(2,1)S(1)}, u32[]{:S(2)}, u32[]{:S(2)}) async-start(bf16[8,2,48,256]{3,2,1,0:T(8,128)(2,1)} %get-tuple-element.41), calls=%async_computation.1 | async-start | bytes 786432 | tf_op jit(solution)/shard_map/all_to_all | solution.py:523
  48.2 0.0 collective-permute-done.2.recv_ref
  48.2 0.0 copy-start.3
  48.2 1.0 copy-done.3
  49.2 0.0 copy-start.12
  49.2 0.0 copy-start.13
  49.2 3.5 %shard_map.103 = (f32[1168,256]{1,0:T(8,128)}, bf16[1168,256]{1,0:T(8,128)(2,1)}) custom-call(f32[2320,256]{1,0:T(8,128)} %get-tuple-element.38.keep_ref, bf16[2320,256]{1,0:T(8,128)(2,1)} %copy-done.3), custom_call_target="tpu_custom_call" | custom-call | tf_op jit(solution)/shard_map/pallas_call | solution.py:507
  52.7 1.9 %collective-permute-start.3 = (bf16[1168,256]{1,0:T(8,128)(2,1)}, bf16[1168,256]{1,0:T(8,128)(2,1)S(1)}, u32[]{:S(2)}, u32[]{:S(2)}) collective-permute-start(bf16[1168,256]{1,0:T(8,128)(2,1)} %get-tuple-element.40), channel_id=1, source_target_pairs={{0,2},{2,0},{4,6},{6,4},{8,10},{10,8},{12,14},{14,12},{1,3},{3,1},... | collective-permute-start | bytes 1794056 | tf_op jit(solution)/shard_map/ppermute | solution.py:575
  54.6 0.0 copy-done.12
  54.6 3.3 %collective-permute-start.5 = (bf16[2,192,256]{2,1,0:T(8,128)(2,1)S(1)}, bf16[2,192,256]{2,1,0:T(8,128)(2,1)S(1)}, u32[]{:S(2)}, u32[]{:S(2)}) collective-permute-start(bf16[2,192,256]{2,1,0:T(8,128)(2,1)S(1)} %copy-done.12), channel_id=1, source_target_pairs={{0,14},{2,4},{4,2},{6,8},{8,6},{10,12},{12,10},{14,0},{1,15},{3,5}... | collective-permute-start | bytes 589832 | tf_op jit(solution)/shard_map/ppermute | solution.py:525
  57.9 0.0 copy-done.13
  57.9 0.0 collective-permute-start.4
  57.9 19.3 %collective-permute-done.4.refs_1_ = bf16[2,144,256]{2,1,0:T(8,128)(2,1)S(1)} collective-permute-done((bf16[2,144,256]{2,1,0:T(8,128)(2,1)S(1)}, bf16[2,144,256]{2,1,0:T(8,128)(2,1)S(1)}, u32[]{:S(2)}, u32[]{:S(2)}) %collective-permute-start.4) | collective-permute-done | bytes 147488 | tf_op jit(solution)/shard_map/ppermute | solution.py:524
  77.2 0.0 copy-start.10
  77.2 0.0 collective-permute-done.5.refs_2_
  77.2 0.0 copy-start.8
  77.3 0.0 all-to-all-done.1.refs_0_
  77.3 0.0 copy-start.1
  77.3 0.0 collective-permute-done.3.recv_ref
  77.3 0.0 copy-start.4
  77.3 0.9 copy-done.4
  78.2 2.5 %shard_map.104 = (f32[304,256]{1,0:T(8,128)}, bf16[4,304,256]{2,1,0:T(8,128)(2,1)}) custom-call(f32[1168,256]{1,0:T(8,128)} %get-tuple-element.47.keep_ref, bf16[1168,256]{1,0:T(8,128)(2,1)} %copy-done.4), custom_call_target="tpu_custom_call" | custom-call | tf_op jit(solution)/shard_map/pallas_call | solution.py:507
  80.6 21.3 %all_to_all.20.recv_ref = bf16[4,304,256]{2,1,0:T(8,128)(2,1)} all-to-all(bf16[4,304,256]{2,1,0:T(8,128)(2,1)} %get-tuple-element.50), channel_id=1, replica_groups={{0,4,8,12},{2,6,10,14},{1,5,9,13},{3,7,11,15},{16,20,24,28},{18,22,26,3..., dimensions={0} | all-to-all | bytes 1245184 | tf_op jit(solution)/shard_map/all_to_all | solution.py:578
  102.0 0.0 copy-done.1
  102.0 2.1 %shard_map.105 = (bf16[4,288,256]{2,1,0:T(8,128)(2,1)}, f32[1,256]{1,0:T(1,128)}) custom-call(f32[304,256]{1,0:T(8,128)} %get-tuple-element.49.keep_ref, bf16[4,304,256]{2,1,0:T(8,128)(2,1)} %all_to_all.20.recv_ref), custom_call_target="tpu_custom_call" | custom-call | tf_op jit(solution)/shard_map/pallas_call | solution.py:507
  104.1 19.3 %all_to_all.21.a_ref = bf16[4,288,256]{2,1,0:T(8,128)(2,1)S(1)} all-to-all(bf16[4,288,256]{2,1,0:T(8,128)(2,1)} %get-tuple-element.51), channel_id=1, replica_groups={{0,4,8,12},{2,6,10,14},{1,5,9,13},{3,7,11,15},{16,20,24,28},{18,22,26,3..., dimensions={0} | all-to-all | bytes 1179648 | tf_op jit(solution)/shard_map/all_to_all | solution.py:578
  123.4 0.0 copy-start
  123.4 0.5 collective-permute-start.6
  123.9 0.0 collective-permute-start.7
  123.9 13.6 %collective-permute-done.6.b_ref = bf16[4,288,256]{2,1,0:T(8,128)(2,1)S(1)} collective-permute-done((bf16[4,288,256]{2,1,0:T(8,128)(2,1)S(1)}, bf16[4,288,256]{2,1,0:T(8,128)(2,1)S(1)}, u32[]{:S(2)}, u32[]{:S(2)}) %collective-permute-start.6) | collective-permute-done | bytes 589856 | tf_op jit(solution)/shard_map/ppermute | solution.py:575
  137.5 0.0 copy-start.5
  137.5 0.0 collective-permute-start.8
  137.5 0.0 copy-done.10
  137.6 0.0 copy-done.8
  137.6 7.3 %shard_map.106 = (bf16[18,24,256]{2,1,0:T(8,128)(2,1)}, f32[18,24,256]{2,1,0:T(8,128)}) custom-call(s32[6,4]{1,0:T(8,128)} %copy.13.ep, bf16[18,24,256]{2,1,0:T(8,128)(2,1)} %bitcast.18, bf16[18,24,256]{2,1,0:T(8,128)(2,1)} %bitcast.21, bf16[18,24,256]{2,1,0:T(8,128)(2,1)} %get-tuple-element.36.hid_ref, bf16[18,24,256]{2,1,0:T(8,128)(2,1)} %get-tuple-element.37.inner_ref, ...), custom_call_target="tpu_custom_call" | custom-call | tf_op jit(solution)/shard_map/pallas_call | solution.py:507
  144.9 0.0 copy-done
  144.9 0.0 copy-done.5
  144.9 0.0 collective-permute-done.7.c_ref
  144.9 0.0 copy-start.6
  144.9 0.0 collective-permute-done.8.d_ref
  144.9 0.0 copy-start.7
  144.9 0.8 copy-done.6
  145.7 0.2 copy-done.7
  145.9 4.2 %shard_map.107 = (f32[2304,256]{1,0:T(8,128)}, f32[2304,256]{1,0:T(8,128)}, f32[1,256]{1,0:T(1,128)}) custom-call(bf16[4,288,256]{2,1,0:T(8,128)(2,1)} %copy-done, bf16[4,288,256]{2,1,0:T(8,128)(2,1)} %copy-done.5, bf16[4,288,256]{2,1,0:T(8,128)(2,1)} %copy-done.6, bf16[4,288,256]{2,1,0:T(8,128)(2,1)} %copy-done.7, f32[1,256]{1,0:T(1,128)} %get-tuple-element.57.extra_ref), custom_call_target="tpu_custom_call" | custom-call | tf_op jit(solution)/shard_map/pallas_call | solution.py:507
Async XLA Ops:
  5.3 22.9 %all-to-all-start = ((bf16[8,2,48,256]{3,2,1,0:T(8,128)(2,1)}), bf16[8,2,48,256]{3,2,1,0:T(8,128)(2,1)S(1)}, u32[]{:S(2)}, u32[]{:S(2)}) async-start(bf16[8,2,48,256]{3,2,1,0:T(8,128)(2,1)} %get-tuple-element.33), calls=%async_computation | async-start | bytes 786432 | tf_op jit(solution)/shard_map/all_to_all | solution.py:523
  12.6 15.6 %collective-permute-start.1 = (bf16[2,192,256]{2,1,0:T(8,128)(2,1)}, bf16[2,192,256]{2,1,0:T(8,128)(2,1)S(1)}, u32[]{:S(2)}, u32[]{:S(2)}) collective-permute-start(bf16[2,192,256]{2,1,0:T(8,128)(2,1)} %get-tuple-element.35), channel_id=1, source_target_pairs={{0,14},{2,4},{4,2},{6,8},{8,6},{10,12},{12,10},{14,0},{1,15},{3,5}... | collective-permute-start | bytes 589832 | tf_op jit(solution)/shard_map/ppermute | solution.py:525
  17.3 7.9 %collective-permute-start = (bf16[2,144,256]{2,1,0:T(8,128)(2,1)}, bf16[2,144,256]{2,1,0:T(8,128)(2,1)S(1)}, u32[]{:S(2)}, u32[]{:S(2)}) collective-permute-start(bf16[2,144,256]{2,1,0:T(8,128)(2,1)} %get-tuple-element.34), channel_id=1, source_target_pairs={{0,2},{2,0},{4,6},{6,4},{8,10},{10,8},{12,14},{14,12},{1,3},{3,1},... | collective-permute-start | bytes 442376 | tf_op jit(solution)/shard_map/ppermute | solution.py:524
  25.2 3.0 %copy-start.11 = (bf16[2,144,256]{2,1,0:T(8,128)(2,1)}, bf16[2,144,256]{2,1,0:T(8,128)(2,1)S(1)}, u32[]{:S(2)}) copy-start(bf16[2,144,256]{2,1,0:T(8,128)(2,1)S(1)} %collective-permute-done.refs_1_) | copy-start | bytes 442372
  28.2 0.7 copy-start.9
  28.2 0.8 copy-start.2
  44.7 3.5 %collective-permute-start.2 = (bf16[2320,256]{1,0:T(8,128)(2,1)}, bf16[2320,256]{1,0:T(8,128)(2,1)S(1)}, u32[]{:S(2)}, u32[]{:S(2)}) collective-permute-start(bf16[2320,256]{1,0:T(8,128)(2,1)} %get-tuple-element.39), channel_id=1, source_target_pairs={{0,1},{1,0},{2,3},{3,2},{4,5},{5,4},{6,7},{7,6},{8,9},{9,8},{10,11... | collective-permute-start | bytes 3563528 | tf_op jit(solution)/shard_map/ppermute | solution.py:531
  44.7 32.5 %all-to-all-start.1 = ((bf16[8,2,48,256]{3,2,1,0:T(8,128)(2,1)}), bf16[8,2,48,256]{3,2,1,0:T(8,128)(2,1)S(1)}, u32[]{:S(2)}, u32[]{:S(2)}) async-start(bf16[8,2,48,256]{3,2,1,0:T(8,128)(2,1)} %get-tuple-element.41), calls=%async_computation.1 | async-start | bytes 786432 | tf_op jit(solution)/shard_map/all_to_all | solution.py:523
  48.2 1.0 copy-start.3
  49.2 5.4 %copy-start.12 = (bf16[2,192,256]{2,1,0:T(8,128)(2,1)S(1)}, bf16[2,192,256]{2,1,0:T(8,128)(2,1)}, u32[]{:S(2)}) copy-start(bf16[2,192,256]{2,1,0:T(8,128)(2,1)} %get-tuple-element.43) | copy-start | bytes 589828
  49.2 8.7 %copy-start.13 = (bf16[2,144,256]{2,1,0:T(8,128)(2,1)S(1)}, bf16[2,144,256]{2,1,0:T(8,128)(2,1)}, u32[]{:S(2)}) copy-start(bf16[2,144,256]{2,1,0:T(8,128)(2,1)} %get-tuple-element.42) | copy-start | bytes 442372
  52.7 24.6 %collective-permute-start.3 = (bf16[1168,256]{1,0:T(8,128)(2,1)}, bf16[1168,256]{1,0:T(8,128)(2,1)S(1)}, u32[]{:S(2)}, u32[]{:S(2)}) collective-permute-start(bf16[1168,256]{1,0:T(8,128)(2,1)} %get-tuple-element.40), channel_id=1, source_target_pairs={{0,2},{2,0},{4,6},{6,4},{8,10},{10,8},{12,14},{14,12},{1,3},{3,1},... | collective-permute-start | bytes 1794056 | tf_op jit(solution)/shard_map/ppermute | solution.py:575
  54.6 22.6 %collective-permute-start.5 = (bf16[2,192,256]{2,1,0:T(8,128)(2,1)S(1)}, bf16[2,192,256]{2,1,0:T(8,128)(2,1)S(1)}, u32[]{:S(2)}, u32[]{:S(2)}) collective-permute-start(bf16[2,192,256]{2,1,0:T(8,128)(2,1)S(1)} %copy-done.12), channel_id=1, source_target_pairs={{0,14},{2,4},{4,2},{6,8},{8,6},{10,12},{12,10},{14,0},{1,15},{3,5}... | collective-permute-start | bytes 589832 | tf_op jit(solution)/shard_map/ppermute | solution.py:525
  57.9 19.3 %collective-permute-start.4 = (bf16[2,144,256]{2,1,0:T(8,128)(2,1)S(1)}, bf16[2,144,256]{2,1,0:T(8,128)(2,1)S(1)}, u32[]{:S(2)}, u32[]{:S(2)}) collective-permute-start(bf16[2,144,256]{2,1,0:T(8,128)(2,1)S(1)} %copy-done.13), channel_id=1, source_target_pairs={{0,2},{2,0},{4,6},{6,4},{8,10},{10,8},{12,14},{14,12},{1,3},{3,1},... | collective-permute-start | bytes 442376 | tf_op jit(solution)/shard_map/ppermute | solution.py:524
  77.2 60.3 %copy-start.10 = (bf16[2,144,256]{2,1,0:T(8,128)(2,1)}, bf16[2,144,256]{2,1,0:T(8,128)(2,1)S(1)}, u32[]{:S(2)}) copy-start(bf16[2,144,256]{2,1,0:T(8,128)(2,1)S(1)} %collective-permute-done.4.refs_1_) | copy-start | bytes 442372
  77.2 60.3 %copy-start.8 = (bf16[2,192,256]{2,1,0:T(8,128)(2,1)}, bf16[2,192,256]{2,1,0:T(8,128)(2,1)S(1)}, u32[]{:S(2)}) copy-start(bf16[2,192,256]{2,1,0:T(8,128)(2,1)S(1)} %collective-permute-done.5.refs_2_) | copy-start | bytes 589828
  77.3 24.7 %copy-start.1 = (bf16[8,2,48,256]{3,2,1,0:T(8,128)(2,1)}, bf16[8,2,48,256]{3,2,1,0:T(8,128)(2,1)S(1)}, u32[]{:S(2)}) copy-start(bf16[8,2,48,256]{3,2,1,0:T(8,128)(2,1)S(1)} %all-to-all-done.1.refs_0_) | copy-start | bytes 1179652
  77.3 0.9 copy-start.4
  123.4 21.5 %copy-start = (bf16[4,288,256]{2,1,0:T(8,128)(2,1)}, bf16[4,288,256]{2,1,0:T(8,128)(2,1)S(1)}, u32[]{:S(2)}) copy-start(bf16[4,288,256]{2,1,0:T(8,128)(2,1)S(1)} %all_to_all.21.a_ref) | copy-start | bytes 1769476
  123.4 14.1 %collective-permute-start.6 = (bf16[4,288,256]{2,1,0:T(8,128)(2,1)S(1)}, bf16[4,288,256]{2,1,0:T(8,128)(2,1)S(1)}, u32[]{:S(2)}, u32[]{:S(2)}) collective-permute-start(bf16[4,288,256]{2,1,0:T(8,128)(2,1)S(1)} %all_to_all.21.a_ref), channel_id=1, source_target_pairs={{0,2},{2,0},{4,6},{6,4},{8,10},{10,8},{12,14},{14,12},{1,3},{3,1},... | collective-permute-start | bytes 1769480 | tf_op jit(solution)/shard_map/ppermute | solution.py:575
  123.9 21.0 %collective-permute-start.7 = (bf16[4,288,256]{2,1,0:T(8,128)(2,1)S(1)}, bf16[4,288,256]{2,1,0:T(8,128)(2,1)S(1)}, u32[]{:S(2)}, u32[]{:S(2)}) collective-permute-start(bf16[4,288,256]{2,1,0:T(8,128)(2,1)S(1)} %all_to_all.21.a_ref), channel_id=1, source_target_pairs={{0,1},{1,0},{2,3},{3,2},{4,5},{5,4},{6,7},{7,6},{8,9},{9,8},{10,11... | collective-permute-start | bytes 1769480 | tf_op jit(solution)/shard_map/ppermute | solution.py:531
  137.5 7.3 %copy-start.5 = (bf16[4,288,256]{2,1,0:T(8,128)(2,1)}, bf16[4,288,256]{2,1,0:T(8,128)(2,1)S(1)}, u32[]{:S(2)}) copy-start(bf16[4,288,256]{2,1,0:T(8,128)(2,1)S(1)} %collective-permute-done.6.b_ref) | copy-start | bytes 1769476
  137.5 7.4 %collective-permute-start.8 = (bf16[4,288,256]{2,1,0:T(8,128)(2,1)S(1)}, bf16[4,288,256]{2,1,0:T(8,128)(2,1)S(1)}, u32[]{:S(2)}, u32[]{:S(2)}) collective-permute-start(bf16[4,288,256]{2,1,0:T(8,128)(2,1)S(1)} %collective-permute-done.6.b_ref), channel_id=1, source_target_pairs={{0,1},{1,0},{2,3},{3,2},{4,5},{5,4},{6,7},{7,6},{8,9},{9,8},{10,11... | collective-permute-start | bytes 1769480 | tf_op jit(solution)/shard_map/ppermute | solution.py:531
  144.9 0.8 copy-start.6
  144.9 1.0 copy-start.7

commit v4 on v3

--- a/solution.py
+++ b/solution.py
@@ -20,14 +20,13 @@
         self.SLOT = -(-(2 * rows + 2) // 8) * 8
         self.BASE = 6 * self.SLOT
         self.o_msg = self.N
-        self.o_mir = self.o_msg + tiles * self.BASE
-        self.o_row = self.o_mir + self.BASE
+        self.o_row = self.o_msg + tiles * self.BASE
         self.NT = self.o_row + 2 * self.ROW
         self.WE = 12 * 8
         self.S = self.WE + self.ROW
 
     def messages(self):
-        return [(self.T, 2, self.BASE, self.C), (2, self.ROW, self.C), (2, self.BASE + self.ROW, self.C)]
+        return [(self.T, 2, self.BASE, self.C), (2, self.ROW, self.C), (2, self.ROW, self.C)]
 
 
 def col_iota(n):
@@ -65,8 +64,7 @@
         column = jnp.where(gvalue % 4 == 1, F - 1, 0) + (gvalue // 4) * (R * F)
         high = jnp.where(to_edge, column + F * i2, jnp.where(i2 < 2, sides + i2 * (F - 1), -1))
         strips = jnp.where(i2 < 0, low, jnp.where(i2 < R, high, -1))
-        mirror = (d == T - 1 - t) & jnp.logical_not(at_edge)
-        parts.append(jnp.where(mirror, mirror_slot(dm, f), strips))
+        parts.append(jnp.where(d == T - 1 - t, mirror_slot(dm, f), strips))
     return parts
 
 
@@ -92,8 +90,7 @@
         for d in range(T):
             strips_ref[d, which] = pick(strip_targets(dm, ep, t, d), which)
         pair_ref[which] = pick(row_targets(dm, jnp.where(t % 2 == 0, R - 1, 0)), which)
-        mirror = [mirror_slot(dm, f) for f in range(6)]
-        ring_ref[which] = pick(mirror + row_targets(dm, jnp.where(t % 2 == 1, R - 1, 0)), which)
+        ring_ref[which] = pick(row_targets(dm, jnp.where(t % 2 == 1, R - 1, 0)), which)
 
 
 def pack_kernel(dm, ep, x_ref, up_ref, *refs):
@@ -111,7 +108,7 @@
     row_next = dm.o_row + odd * dm.ROW
     side_first = dm.o_msg + (T - t) * dm.BASE + jnp.where(t == 1, R + 2, 0)
     side_last = dm.o_msg + (T - 2 - t) * dm.BASE + jnp.where(t == T - 2, R + 2, 0)
-    mirror = jnp.where((t == 0) | (t == T - 1), dm.o_mir, dm.o_msg + (T - 1 - t) * dm.BASE)
+    mirror = dm.o_msg + (T - 1 - t) * dm.BASE
     for f in range(6):
         for edge in (3, 1):
             value = ep[f, edge]
@@ -123,14 +120,18 @@
             column = side * (F - 1)
             slot = f2 * dm.SLOT + side
             row = dm.o_msg + jnp.where(e2 == 0, 0, T - 1) * dm.BASE + f2 * dm.SLOT
+            facing = jnp.where(e2 == 0, t == T - 1, t == 0)
+            whole = dm.o_row + dm.ROW + f2 * F + jnp.where(reverse, F - R * t, R * t - 1)
+            row = jnp.where(facing, whole, row)
+            along = jnp.where(facing & reverse, -1, 1)
             i0 = jnp.where(is_col, jnp.where(reverse, side_first + slot, row_prev + f2 * F + column), row)
             i4 = jnp.where(
-                is_col, jnp.where(reverse, side_last + slot, row_next + f2 * F + column), row + R + 1
+                is_col, jnp.where(reverse, side_last + slot, row_next + f2 * F + column), row + along * (R + 1)
             )
             base = jnp.where(
                 is_col, jnp.where(reverse, mirror + 2 * R + slot, (f2 * R - 1) * F + column), row
             )
-            step = jnp.where(is_col, jnp.where(reverse, -2, F), 1)
+            step = jnp.where(is_col, jnp.where(reverse, -2, F), along)
             target = jnp.where(m == 0, i0, jnp.where(m == R + 1, i4, base + step * m))
             parts.append(jnp.where(inside, target, -1))
     j = col_iota(F)
@@ -164,7 +165,12 @@
             sj = jnp.where(at_edge, sj, 1)
             st = jnp.where(at_edge, st, 0)
             sr = jnp.where(at_edge, sr, 0)
-            parts.append(base + sj * j + st * jt + sr * jr)
+            target = base + sj * j + st * jt + sr * jr
+            far_tile = T - 1 if edge == 0 else 0
+            from_mirror = is_col & at_edge & (jnp.where(reverse, T - 1 - jt, jt) == far_tile)
+            side = jnp.where(e2 == 1, 1, 0)
+            cells = mirror + f2 * dm.SLOT + side + 2 * jnp.where(reverse, R - 1 - jr, jr)
+            parts.append(jnp.where(from_mirror, cells, target))
     return jnp.concatenate(parts, axis=0)
 
 
@@ -176,14 +182,13 @@
         for k in range(dm.T):
             at = dm.o_msg + k * dm.BASE
             table_ref[at : at + dm.BASE] = messages[0][k, which]
-        table_ref[dm.o_mir : dm.o_row] = messages[2][which, : dm.BASE]
         table_ref[dm.o_row : dm.o_row + dm.ROW] = messages[1][which]
-        table_ref[dm.o_row + dm.ROW :] = messages[2][which, dm.BASE :]
+        table_ref[dm.o_row + dm.ROW :] = messages[2][which]
         out.append(jnp.dot(hot, table_ref[...], preferred_element_type=F32))
     return out
 
 
-def build_shifts(dm, field_ref, ghosts, top, bottom, frame_ref, shift_ref):
+def build_taps(dm, field_ref, ghosts, top, bottom, frame_ref, taps_ref, adjoint):
     R, F, C = dm.R, dm.F, dm.C
     for f in range(6):
         for r in range(R):
@@ -202,8 +207,12 @@
             frame_ref[m, f, 8 + F : 9 + F] = east
     for m in range(R + 2):
         for b in range(3):
-            plane = frame_ref[m, :, 7 + b : 7 + b + F].reshape(dm.ROW, C)
-            shift_ref[b, m * dm.ROW : (m + 1) * dm.ROW] = plane.astype(BF)
+            plane = frame_ref[m, :, 7 + b : 7 + b + F].reshape(dm.ROW, C).astype(BF)
+            for a in range(3):
+                r = m - 2 + a if adjoint else m - a
+                tap = 3 * a + (2 - b if adjoint else b)
+                if 0 <= r < R:
+                    taps_ref[r * dm.ROW : (r + 1) * dm.ROW, tap * C : (tap + 1) * C] = plane
 
 
 def build_strip_terms(dm, ep, t, ghosts, top, bottom, z_ref):
@@ -248,20 +257,13 @@
         add_rows(2, bottom)
 
 
-def adjoint(dm, t, u_ref, z_ref, w_ref, acc_ref):
-    R, F = dm.R, dm.F
-    total = None
-    strips = None
-    for a in range(3):
-        for b in range(3):
-            main = u_ref[2 - b, (2 - a) * dm.ROW : (2 - a + R) * dm.ROW]
-            w = w_ref[3 * a + b]
-            dims = (((1,), (1,)), ((), ()))
-            term = lax.dot_general(main, w, dims, preferred_element_type=F32)
-            strip = lax.dot_general(z_ref[3 * a + b].astype(BF), w, dims, preferred_element_type=F32)
-            total = term if total is None else total + term
-            strips = strip if strips is None else strips + strip
-    acc_ref[...] = total
+def adjoint(dm, t, taps_ref, z_ref, wt_ref, acc_ref):
+    R, F, C, N = dm.R, dm.F, dm.C, dm.N
+    for tap in range(9):
+        taps_ref[N:, tap * C : (tap + 1) * C] = z_ref[tap].astype(BF)
+    total = jnp.dot(taps_ref[...], wt_ref[...], preferred_element_type=F32)
+    acc_ref[...] = total[:N]
+    strips = total[N:]
     for f in range(6):
         for side in range(2):
             for r in range(R):
@@ -276,6 +278,12 @@
     @pl.when(t == dm.T - 1)
     def _():
         acc_ref[(R - 1) * dm.ROW : R * dm.ROW] += strips[dm.WE :]
+
+
+def turn_kernel(w1_ref, w2_ref, w1t_ref, w2t_ref):
+    for w_ref, wt_ref in ((w1_ref, w1t_ref), (w2_ref, w2t_ref)):
+        for tap in range(9):
+            wt_ref[tap] = w_ref[tap].T
 
 
 def put_tap(dm, send_ref, keep_ref, p, which, tap, value):
@@ -307,7 +315,7 @@
     send_ref[n:] = jnp.where(i == 0, high.astype(F32), jnp.where(i == 1, low, 0.0)).astype(BF)
 
 
-def first_kernel(dm, ep, x_ref, up_ref, w1_ref, bias_ref, w2_ref, *refs):
+def first_kernel(dm, ep, x_ref, up_ref, w1_ref, bias_ref, w2t_ref, *refs):
     T, R, F, N, C = dm.T, dm.R, dm.F, dm.N, dm.C
     messages = refs[:3]
     send_ref, keep_ref, hid_ref, inner_ref = refs[3:7]
@@ -317,61 +325,48 @@
     own = (x_ref[...].reshape(N, C), up_ref[...].reshape(N, C))
     gx, gu = gather_ghosts(dm, ep, t, own, messages, table_ref)
     top, bottom = dm.WE, dm.WE + dm.ROW
-    build_shifts(dm, x_ref, gx[:top], gx[top:bottom], gx[bottom:], frame_ref, xs_ref)
-    total = None
-    for a in range(3):
-        for b in range(3):
-            term = jnp.dot(
-                xs_ref[b, a * dm.ROW : (a + R) * dm.ROW], w1_ref[3 * a + b], preferred_element_type=F32
-            )
-            total = term if total is None else total + term
-    before = total + bias_ref[...]
+    build_taps(dm, x_ref, gx[:top], gx[top:bottom], gx[bottom:], frame_ref, xs_ref, False)
+    before = jnp.dot(xs_ref[...], w1_ref[...], preferred_element_type=F32) + bias_ref[...]
     before_ref[...] = before
     sig = 1.0 / (1.0 + jnp.exp(-before))
-    hidden = before * sig
-    acc_ref[...] = hidden
-    hidden_bf = hidden.astype(BF)
+    acc_ref[...] = before * sig
     up_top = jnp.where(t == 0, 0.0, gu[top:bottom])
     up_bottom = jnp.where(t == T - 1, 0.0, gu[bottom:])
-    build_shifts(dm, up_ref, None, up_top, up_bottom, frame_ref, us_ref)
+    build_taps(dm, up_ref, None, up_top, up_bottom, frame_ref, us_ref, True)
     build_strip_terms(dm, ep, t, gu[:top], gu[top:bottom], gu[bottom:], z_ref)
-    hcat_ref[...] = jnp.zeros(hcat_ref.shape, F32)
+    hcat_ref[0:N] = acc_ref[...]
+    hcat_ref[N:] = jnp.zeros((dm.S, C), F32)
     for f in range(6):
         for side in range(2):
             for r in range(R):
                 at = (r * 6 + f) * F + side * (F - 1)
-                row = 16 * f + 8 * side + r
+                row = N + 16 * f + 8 * side + r
                 hcat_ref[row : row + 1] = acc_ref[at : at + 1]
     first_row = acc_ref[0 : dm.ROW]
     last_row = acc_ref[(R - 1) * dm.ROW : R * dm.ROW]
-    hcat_ref[dm.WE :] = jnp.where(t == 0, first_row, last_row)
-    hidden_t = hidden_bf.T
-    edge_t = hcat_ref[...].astype(BF).T
-    for a in range(3):
-        for b in range(3):
-            main = us_ref[2 - b, (2 - a) * dm.ROW : (2 - a + R) * dm.ROW]
-            grad = jnp.dot(hidden_t, main, preferred_element_type=F32)
-            grad = grad + jnp.dot(edge_t, z_ref[3 * a + b].astype(BF), preferred_element_type=F32)
-            put_tap(dm, send_ref, keep_ref, p, 0, 3 * a + b, grad)
+    hcat_ref[N + dm.WE :] = jnp.where(t == 0, first_row, last_row)
     for r in range(R):
         for f in range(6):
             at = (r * 6 + f) * F
             hid_ref[f * R + r] = acc_ref[at : at + F].astype(BF)
-    adjoint(dm, t, us_ref, z_ref, w2_ref, acc_ref)
+    adjoint(dm, t, us_ref, z_ref, w2t_ref, acc_ref)
+    hidden_t = hcat_ref[...].astype(BF).T
+    for tap in range(9):
+        grad = jnp.dot(hidden_t, us_ref[:, tap * C : (tap + 1) * C], preferred_element_type=F32)
+        put_tap(dm, send_ref, keep_ref, p, 0, tap, grad)
     before = before_ref[...]
     sig = 1.0 / (1.0 + jnp.exp(-before))
     before_grad = acc_ref[...] * (sig * (1.0 + before * (1.0 - sig)))
     acc_ref[...] = before_grad
     inner = before_grad.astype(BF)
-    for a in range(3):
-        for b in range(3):
-            grad = lax.dot_general(
-                xs_ref[b, a * dm.ROW : (a + R) * dm.ROW],
-                inner,
-                (((0,), (0,)), ((), ())),
-                preferred_element_type=F32,
-            )
-            put_tap(dm, send_ref, keep_ref, p, 1, 3 * a + b, grad)
+    for tap in range(9):
+        grad = lax.dot_general(
+            xs_ref[:, tap * C : (tap + 1) * C],
+            inner,
+            (((0,), (0,)), ((), ())),
+            preferred_element_type=F32,
+        )
+        put_tap(dm, send_ref, keep_ref, p, 1, tap, grad)
     put_extra(send_ref, keep_ref, jnp.sum(before_grad, axis=0, keepdims=True))
     for r in range(R):
         for f in range(6):
@@ -382,26 +377,17 @@
     )
 
 
-def second_kernel(dm, ep, x_ref, d_ref, hid_ref, inner_ref, w1_ref, w2_ref, *refs):
+def second_kernel(dm, ep, x_ref, d_ref, hid_ref, inner_ref, w1t_ref, w2_ref, *refs):
     T, R, F, N, C = dm.T, dm.R, dm.F, dm.N, dm.C
     messages = refs[:3]
     state_ref, grad_ref = refs[3:5]
-    table_ref, frame_ref, shift_ref, z_ref, acc_ref = refs[5:]
+    table_ref, frame_ref, hs_ref, is_ref, z_ref, acc_ref = refs[5:]
     t = lax.axis_index("tile")
     own = (hid_ref[...].reshape(N, C), inner_ref[...].reshape(N, C))
     gh, gi = gather_ghosts(dm, ep, t, own, messages, table_ref)
     top, bottom = dm.WE, dm.WE + dm.ROW
-    build_shifts(dm, hid_ref, gh[:top], gh[top:bottom], gh[bottom:], frame_ref, shift_ref)
-    total = None
-    for a in range(3):
-        for b in range(3):
-            term = jnp.dot(
-                shift_ref[b, a * dm.ROW : (a + R) * dm.ROW],
-                w2_ref[3 * a + b],
-                preferred_element_type=F32,
-            )
-            total = term if total is None else total + term
-    acc_ref[...] = total
+    build_taps(dm, hid_ref, gh[:top], gh[top:bottom], gh[bottom:], frame_ref, hs_ref, False)
+    acc_ref[...] = jnp.dot(hs_ref[...], w2_ref[...], preferred_element_type=F32)
     for r in range(R):
         for f in range(6):
             at = (r * 6 + f) * F
@@ -409,9 +395,9 @@
             state_ref[f * R + r] = value.astype(BF)
     in_top = jnp.where(t == 0, 0.0, gi[top:bottom])
     in_bottom = jnp.where(t == T - 1, 0.0, gi[bottom:])
-    build_shifts(dm, inner_ref, None, in_top, in_bottom, frame_ref, shift_ref)
+    build_taps(dm, inner_ref, None, in_top, in_bottom, frame_ref, is_ref, True)
     build_strip_terms(dm, ep, t, gi[:top], gi[top:bottom], gi[bottom:], z_ref)
-    adjoint(dm, t, shift_ref, z_ref, w1_ref, acc_ref)
+    adjoint(dm, t, is_ref, z_ref, w1t_ref, acc_ref)
     for r in range(R):
         for f in range(6):
             at = (r * 6 + f) * F
@@ -538,8 +524,12 @@
     planes = (6 * rows, face, channels)
     x = initial_state.reshape(planes)
     d = state_cotangents[state_cotangents.shape[0] - 1].reshape(planes)
-    w1 = w_first.reshape(9, channels, channels)
-    w2 = w_second.reshape(9, channels, channels)
+    taps = (9, channels, channels)
+    w1 = w_first.reshape(9 * channels, channels)
+    w2 = w_second.reshape(9 * channels, channels)
+    w1t, w2t = call(turn_kernel, [(taps, BF)] * 2)(w_first.reshape(taps), w_second.reshape(taps))
+    w1t = w1t.reshape(w1.shape)
+    w2t = w2t.reshape(w2.shape)
     msg_shapes = [(shape, BF) for shape in dm.messages()]
     flat = (dm.N, channels)
     messages = call(functools.partial(pack_kernel, dm), msg_shapes, smem_first=True)(
@@ -547,7 +537,7 @@
     )
     messages = exchange(tiles, messages)
     half = 9 * channels
-    shift_rows = (3, (rows + 2) * dm.ROW, channels)
+    wide = 9 * channels
     frame = (rows + 2, 6, face + 16, channels)
     outs = call(
         functools.partial(first_kernel, dm),
@@ -555,15 +545,15 @@
         [
             ((dm.NT, channels), BF),
             (frame, F32),
-            (shift_rows, BF),
-            (shift_rows, BF),
+            ((dm.N, wide), BF),
+            ((dm.N + dm.S, wide), BF),
             ((9, dm.S, channels), F32),
             (flat, F32),
             (flat, F32),
-            ((dm.S, channels), F32),
+            ((dm.N + dm.S, channels), F32),
         ],
         smem_first=True,
-    )(edge_partner, x, d, w1, bias.reshape(1, channels), w2, *messages)
+    )(edge_partner, x, d, w1, bias.reshape(1, channels), w2t, *messages)
     send, keep, hidden, inner = outs[:4]
 
     zcount = tiles // 2
@@ -599,12 +589,14 @@
         [
             ((dm.NT, channels), BF),
             (frame, F32),
-            (shift_rows, BF),
+            ((dm.N, wide), BF),
+            ((dm.N + dm.S, wide), BF),
             ((9, dm.S, channels), F32),
             (flat, F32),
         ],
         smem_first=True,
-    )(edge_partner, x, d, hidden, inner, w1, w2, *messages)
+    )(edge_partner, x, d, hidden, inner, w1t, w2, *messages)
+    other, state, grad = lax.optimization_barrier((other, state, grad))
     second_step, first_step, bias_step = call(
         functools.partial(normal_kernel, zcount),
         [((half, channels), F32)] * 2 + [((1, channels), F32)],

time: 151 us -> 144 us (0.954)
  waiting for transfers between devices: 43.8 us -> 31.3 us
  Pallas kernels: 38.7 us -> 42.3 us
  starting transfers between devices: 21.2 us -> 23.2 us
    ppermute x2, waiting for transfers between devices: 27.2 us -> 19.6 us  [exchange(): lax.ppermute(pair, 'tile', [(i, i ^ 1) for i in range(tiles)])]
    ppermute x2, waiting for transfers between devices: 13.6 us -> 6.62 us  [along_y(): return lax.ppermute(v, 'tile', [(i, i ^ 1) for i in range(tiles)])]
    pallas_call x7 -> x8, Pallas kernels: 38.7 us -> 42.3 us  [run(): pl.pallas_call(kernel, out_shape=[jax.ShapeDtypeStruct(s, dt) for s, dt i...]
    ppermute x2, starting transfers between devices: 0.01 us -> 2.14 us  [exchange(): lax.ppermute(pair, 'tile', [(i, i ^ 1) for i in range(tiles)])]
    ppermute x3, waiting for transfers between devices: 0.01 us -> 1.99 us  [swap_dp(): return lax.ppermute(v, 'dp', [(i, count - 1 - i) for i in range(count)])]
  transfers between devices with their start and end apart: 11 -> 11, of which waited for: 4 -> 5; matrix products, arithmetic and copies ran while one was open for 0% -> 0% of each run, Pallas kernels for 7% -> 10%
where the time goes in v4:
time: 144 us; the launch traced here: 143 us
  Pallas kernels  42.3 us (29%)
  blocking collectives  40.7 us (28%)
  waiting for transfers between devices  31.3 us (22%)
  starting transfers between devices  23.2 us (16%)
  local copies, waits for them, and re-layouts  4.89 us (3%)
    pallas_call x8, Pallas kernels, run(): pl.pallas_call(kernel, out_shape=[jax.ShapeDtypeStruct(s, dt) for s, dt i...  42.3 us
    all_to_all x2, blocking collectives, along_z(): return lax.all_to_all(v, 'tile', 0, 0, axis_index_groups=groups)  40.7 us
    ppermute x2, waiting for transfers between devices, exchange(): lax.ppermute(pair, 'tile', [(i, i ^ 1) for i in range(tiles)])  19.6 us
    all_to_all x2, starting transfers between devices, exchange(): lax.all_to_all(strips, 'tile', 0, 0)  10.7 us
    ppermute x2, starting transfers between devices, exchange(): lax.ppermute(ring, 'tile', other)  7.91 us
    ppermute x2, waiting for transfers between devices, along_y(): return lax.ppermute(v, 'tile', [(i, i ^ 1) for i in range(tiles)])  6.62 us
    unnamed x29, local copies, waits for them, and re-layouts  4.89 us
    ppermute x2, waiting for transfers between devices, exchange(): lax.ppermute(ring, 'tile', other)  3.09 us
  transfers between devices with their start and end apart: 11, of which 5 were waited for; matrix products, arithmetic and copies ran while one was open for 0% of the time, Pallas kernels for 10%

profile of v4, /device:TPU:0, one launch (start us, length us, event | category | flops | bytes accessed | tf_op | source)
XLA Modules:
  0.0 143.0 jit_solution(13053752279606948865)
XLA Ops:
  0.6 1.4 copy.12.ep
  2.0 3.3 %shard_map.102 = (bf16[8,2,48,256]{3,2,1,0:T(8,128)(2,1)}, bf16[2,144,256]{2,1,0:T(8,128)(2,1)}, bf16[2,144,256]{2,1,0:T(8,128)(2,1)}) custom-call(s32[6,4]{1,0:T(8,128)} %copy.12.ep, bf16[432,256]{1,0:T(8,128)(2,1)} %bitcast.20, bf16[432,256]{1,0:T(8,128)(2,1)} %bitcast.23), custom_call_target="tpu_custom_call" | custom-call | tf_op jit(solution)/shard_map/pallas_call | solution.py:493
  5.3 7.3 %all-to-all-start = ((bf16[8,2,48,256]{3,2,1,0:T(8,128)(2,1)}), bf16[8,2,48,256]{3,2,1,0:T(8,128)(2,1)S(1)}, u32[]{:S(2)}, u32[]{:S(2)}) async-start(bf16[8,2,48,256]{3,2,1,0:T(8,128)(2,1)} %get-tuple-element.39), calls=%async_computation | async-start | bytes 786432 | tf_op jit(solution)/shard_map/all_to_all | solution.py:509
  12.5 2.0 %collective-permute-start = (bf16[2,144,256]{2,1,0:T(8,128)(2,1)}, bf16[2,144,256]{2,1,0:T(8,128)(2,1)S(1)}, u32[]{:S(2)}, u32[]{:S(2)}) collective-permute-start(bf16[2,144,256]{2,1,0:T(8,128)(2,1)} %get-tuple-element.40), channel_id=1, source_target_pairs={{0,2},{2,0},{4,6},{6,4},{8,10},{10,8},{12,14},{14,12},{1,3},{3,1},... | collective-permute-start | bytes 442376 | tf_op jit(solution)/shard_map/ppermute | solution.py:510
  14.6 3.3 %collective-permute-start.1 = (bf16[2,144,256]{2,1,0:T(8,128)(2,1)}, bf16[2,144,256]{2,1,0:T(8,128)(2,1)S(1)}, u32[]{:S(2)}, u32[]{:S(2)}) collective-permute-start(bf16[2,144,256]{2,1,0:T(8,128)(2,1)} %get-tuple-element.41), channel_id=1, source_target_pairs={{0,14},{2,4},{4,2},{6,8},{8,6},{10,12},{12,10},{14,0},{1,15},{3,5}... | collective-permute-start | bytes 442376 | tf_op jit(solution)/shard_map/ppermute | solution.py:511
  17.8 3.4 %shard_map.101 = (bf16[9,256,256]{2,1,0:T(8,128)(2,1)}, bf16[9,256,256]{2,1,0:T(8,128)(2,1)}) custom-call(bf16[9,256,256]{2,1,0:T(8,128)(2,1)} %bitcast.16, bf16[9,256,256]{2,1,0:T(8,128)(2,1)} %bitcast.18), custom_call_target="tpu_custom_call" | custom-call | tf_op jit(solution)/shard_map/pallas_call | solution.py:493
  21.2 2.8 %collective-permute-done.refs_1_ = bf16[2,144,256]{2,1,0:T(8,128)(2,1)S(1)} collective-permute-done((bf16[2,144,256]{2,1,0:T(8,128)(2,1)}, bf16[2,144,256]{2,1,0:T(8,128)(2,1)S(1)}, u32[]{:S(2)}, u32[]{:S(2)}) %collective-permute-start) | collective-permute-done | bytes 147488 | tf_op jit(solution)/shard_map/ppermute | solution.py:510
  24.0 0.0 copy-start.10
  24.0 3.1 %collective-permute-done.1.refs_2_ = bf16[2,144,256]{2,1,0:T(8,128)(2,1)S(1)} collective-permute-done((bf16[2,144,256]{2,1,0:T(8,128)(2,1)}, bf16[2,144,256]{2,1,0:T(8,128)(2,1)S(1)}, u32[]{:S(2)}, u32[]{:S(2)}) %collective-permute-start.1) | collective-permute-done | bytes 147488 | tf_op jit(solution)/shard_map/ppermute | solution.py:511
  27.1 0.0 copy-start.11
  27.1 0.0 all-to-all-done.refs_0_
  27.1 0.0 copy-start.2
  27.1 0.0 copy-done.10
  27.1 0.6 copy-done.11
  27.7 0.1 copy-done.2
  27.9 16.2 %shard_map.103 = (bf16[2320,256]{1,0:T(8,128)(2,1)}, f32[2320,256]{1,0:T(8,128)}, bf16[18,24,256]{2,1,0:T(8,128)(2,1)}, bf16[18,24,256]{2,1,0:T(8,128)(2,1)}, bf...) custom-call(s32[6,4]{1,0:T(8,128)} %copy.12.ep, ...), custom_call_target="tpu_custom_call" | custom-call | tf_op jit(solution)/shard_map/pallas_call | solution.py:493
  44.1 0.0 collective-permute-start.2
  44.1 3.5 %all-to-all-start.1 = ((bf16[8,2,48,256]{3,2,1,0:T(8,128)(2,1)}), bf16[8,2,48,256]{3,2,1,0:T(8,128)(2,1)S(1)}, u32[]{:S(2)}, u32[]{:S(2)}) async-start(bf16[8,2,48,256]{3,2,1,0:T(8,128)(2,1)} %get-tuple-element.46), calls=%async_computation.1 | async-start | bytes 786432 | tf_op jit(solution)/shard_map/all_to_all | solution.py:509
  47.6 0.0 collective-permute-done.2.recv_ref
  47.6 0.0 copy-start.3
  47.6 1.0 copy-done.3
  48.6 0.0 copy-start.13
  48.6 0.0 copy-start.12
  48.7 3.4 %shard_map.104 = (f32[1168,256]{1,0:T(8,128)}, bf16[1168,256]{1,0:T(8,128)(2,1)}) custom-call(f32[2320,256]{1,0:T(8,128)} %get-tuple-element.42.keep_ref, bf16[2320,256]{1,0:T(8,128)(2,1)} %copy-done.3), custom_call_target="tpu_custom_call" | custom-call | tf_op jit(solution)/shard_map/pallas_call | solution.py:493
  52.1 1.9 %collective-permute-start.3 = (bf16[1168,256]{1,0:T(8,128)(2,1)}, bf16[1168,256]{1,0:T(8,128)(2,1)S(1)}, u32[]{:S(2)}, u32[]{:S(2)}) collective-permute-start(bf16[1168,256]{1,0:T(8,128)(2,1)} %get-tuple-element.45), channel_id=1, source_target_pairs={{0,2},{2,0},{4,6},{6,4},{8,10},{10,8},{12,14},{14,12},{1,3},{3,1},... | collective-permute-start | bytes 1794056 | tf_op jit(solution)/shard_map/ppermute | solution.py:565
  54.0 0.0 copy-done.13
  54.0 0.1 collective-permute-start.4
  54.1 0.0 copy-done.12
  54.1 4.6 %collective-permute-start.5 = (bf16[2,144,256]{2,1,0:T(8,128)(2,1)S(1)}, bf16[2,144,256]{2,1,0:T(8,128)(2,1)S(1)}, u32[]{:S(2)}, u32[]{:S(2)}) collective-permute-start(bf16[2,144,256]{2,1,0:T(8,128)(2,1)S(1)} %copy-done.12), channel_id=1, source_target_pairs={{0,14},{2,4},{4,2},{6,8},{8,6},{10,12},{12,10},{14,0},{1,15},{3,5}... | collective-permute-start | bytes 442376 | tf_op jit(solution)/shard_map/ppermute | solution.py:511
  58.8 16.8 %collective-permute-done.4.refs_1_ = bf16[2,144,256]{2,1,0:T(8,128)(2,1)S(1)} collective-permute-done((bf16[2,144,256]{2,1,0:T(8,128)(2,1)S(1)}, bf16[2,144,256]{2,1,0:T(8,128)(2,1)S(1)}, u32[]{:S(2)}, u32[]{:S(2)}) %collective-permute-start.4) | collective-permute-done | bytes 147488 | tf_op jit(solution)/shard_map/ppermute | solution.py:510
  75.6 0.0 copy-start.8
  75.6 0.0 collective-permute-done.5.refs_2_
  75.6 0.0 copy-start.9
  75.6 0.0 all-to-all-done.1.refs_0_
  75.6 0.0 copy-start.1
  75.6 0.0 collective-permute-done.3.recv_ref
  75.6 0.0 copy-start.4
  75.6 0.9 copy-done.4
  76.5 2.5 %shard_map.105 = (f32[304,256]{1,0:T(8,128)}, bf16[4,304,256]{2,1,0:T(8,128)(2,1)}) custom-call(f32[1168,256]{1,0:T(8,128)} %get-tuple-element.44.keep_ref, bf16[1168,256]{1,0:T(8,128)(2,1)} %copy-done.4), custom_call_target="tpu_custom_call" | custom-call | tf_op jit(solution)/shard_map/pallas_call | solution.py:493
  79.0 21.4 %all_to_all.20.recv_ref = bf16[4,304,256]{2,1,0:T(8,128)(2,1)} all-to-all(bf16[4,304,256]{2,1,0:T(8,128)(2,1)} %get-tuple-element.51), channel_id=1, replica_groups={{0,4,8,12},{2,6,10,14},{1,5,9,13},{3,7,11,15},{16,20,24,28},{18,22,26,3..., dimensions={0} | all-to-all | bytes 1245184 | tf_op jit(solution)/shard_map/all_to_all | solution.py:568
  100.3 0.0 copy-done.1
  100.3 2.1 %shard_map.106 = (bf16[4,288,256]{2,1,0:T(8,128)(2,1)}, f32[1,256]{1,0:T(1,128)}) custom-call(f32[304,256]{1,0:T(8,128)} %get-tuple-element.50.keep_ref, bf16[4,304,256]{2,1,0:T(8,128)(2,1)} %all_to_all.20.recv_ref), custom_call_target="tpu_custom_call" | custom-call | tf_op jit(solution)/shard_map/pallas_call | solution.py:493
  102.5 19.3 %all_to_all.21.a_ref = bf16[4,288,256]{2,1,0:T(8,128)(2,1)S(1)} all-to-all(bf16[4,288,256]{2,1,0:T(8,128)(2,1)} %get-tuple-element.52), channel_id=1, replica_groups={{0,4,8,12},{2,6,10,14},{1,5,9,13},{3,7,11,15},{16,20,24,28},{18,22,26,3..., dimensions={0} | all-to-all | bytes 1179648 | tf_op jit(solution)/shard_map/all_to_all | solution.py:568
  121.8 0.0 copy-start
  121.8 0.5 collective-permute-start.6
  122.2 0.0 copy-done.8
  122.2 0.0 copy-done.9
  122.2 7.1 %shard_map.107 = (bf16[18,24,256]{2,1,0:T(8,128)(2,1)}, f32[18,24,256]{2,1,0:T(8,128)}) custom-call(s32[6,4]{1,0:T(8,128)} %copy.12.ep, bf16[18,24,256]{2,1,0:T(8,128)(2,1)} %bitcast.22, bf16[18,24,256]{2,1,0:T(8,128)(2,1)} %bitcast.25, bf16[18,24,256]{2,1,0:T(8,128)(2,1)} %get-tuple-element.53.hid_ref, bf16[18,24,256]{2,1,0:T(8,128)(2,1)} %get-tuple-element.54.inner_ref, ...), custom_call_target="tpu_custom_call" | custom-call | tf_op jit(solution)/shard_map/pallas_call | solution.py:493
  129.3 0.0 copy-done
  129.3 0.0 collective-permute-start.7
  129.3 6.6 %collective-permute-done.6.b_ref = bf16[4,288,256]{2,1,0:T(8,128)(2,1)S(1)} collective-permute-done((bf16[4,288,256]{2,1,0:T(8,128)(2,1)S(1)}, bf16[4,288,256]{2,1,0:T(8,128)(2,1)S(1)}, u32[]{:S(2)}, u32[]{:S(2)}) %collective-permute-start.6) | collective-permute-done | bytes 589856 | tf_op jit(solution)/shard_map/ppermute | solution.py:565
  135.9 0.0 copy-start.5
  135.9 0.0 collective-permute-start.8
  135.9 0.0 collective-permute-done.7.c_ref
  135.9 0.0 copy-start.6
  135.9 2.0 %collective-permute-done.8.d_ref = bf16[4,288,256]{2,1,0:T(8,128)(2,1)S(1)} collective-permute-done((bf16[4,288,256]{2,1,0:T(8,128)(2,1)S(1)}, bf16[4,288,256]{2,1,0:T(8,128)(2,1)S(1)}, u32[]{:S(2)}, u32[]{:S(2)}) %collective-permute-start.8) | collective-permute-done | bytes 589856 | tf_op jit(solution)/shard_map/ppermute | solution.py:517
  137.9 0.0 copy-start.7
  137.9 0.0 copy-done.5
  137.9 0.0 copy-done.6
  137.9 0.8 copy-done.7
  138.8 4.2 %shard_map.108 = (f32[2304,256]{1,0:T(8,128)}, f32[2304,256]{1,0:T(8,128)}, f32[1,256]{1,0:T(1,128)}) custom-call(bf16[4,288,256]{2,1,0:T(8,128)(2,1)} %copy-done, bf16[4,288,256]{2,1,0:T(8,128)(2,1)} %copy-done.5, bf16[4,288,256]{2,1,0:T(8,128)(2,1)} %copy-done.6, bf16[4,288,256]{2,1,0:T(8,128)(2,1)} %copy-done.7, f32[1,256]{1,0:T(1,128)} %get-tuple-element.67.extra_ref), custom_call_target="tpu_custom_call" | custom-call | tf_op jit(solution)/shard_map/pallas_call | solution.py:493
Async XLA Ops:
  5.3 21.8 %all-to-all-start = ((bf16[8,2,48,256]{3,2,1,0:T(8,128)(2,1)}), bf16[8,2,48,256]{3,2,1,0:T(8,128)(2,1)S(1)}, u32[]{:S(2)}, u32[]{:S(2)}) async-start(bf16[8,2,48,256]{3,2,1,0:T(8,128)(2,1)} %get-tuple-element.39), calls=%async_computation | async-start | bytes 786432 | tf_op jit(solution)/shard_map/all_to_all | solution.py:509
  12.5 11.4 %collective-permute-start = (bf16[2,144,256]{2,1,0:T(8,128)(2,1)}, bf16[2,144,256]{2,1,0:T(8,128)(2,1)S(1)}, u32[]{:S(2)}, u32[]{:S(2)}) collective-permute-start(bf16[2,144,256]{2,1,0:T(8,128)(2,1)} %get-tuple-element.40), channel_id=1, source_target_pairs={{0,2},{2,0},{4,6},{6,4},{8,10},{10,8},{12,14},{14,12},{1,3},{3,1},... | collective-permute-start | bytes 442376 | tf_op jit(solution)/shard_map/ppermute | solution.py:510
  14.6 12.5 %collective-permute-start.1 = (bf16[2,144,256]{2,1,0:T(8,128)(2,1)}, bf16[2,144,256]{2,1,0:T(8,128)(2,1)S(1)}, u32[]{:S(2)}, u32[]{:S(2)}) collective-permute-start(bf16[2,144,256]{2,1,0:T(8,128)(2,1)} %get-tuple-element.41), channel_id=1, source_target_pairs={{0,14},{2,4},{4,2},{6,8},{8,6},{10,12},{12,10},{14,0},{1,15},{3,5}... | collective-permute-start | bytes 442376 | tf_op jit(solution)/shard_map/ppermute | solution.py:511
  24.0 3.1 %copy-start.10 = (bf16[2,144,256]{2,1,0:T(8,128)(2,1)}, bf16[2,144,256]{2,1,0:T(8,128)(2,1)S(1)}, u32[]{:S(2)}) copy-start(bf16[2,144,256]{2,1,0:T(8,128)(2,1)S(1)} %collective-permute-done.refs_1_) | copy-start | bytes 442372
  27.1 0.7 copy-start.11
  27.1 0.8 copy-start.2
  44.1 3.5 %collective-permute-start.2 = (bf16[2320,256]{1,0:T(8,128)(2,1)}, bf16[2320,256]{1,0:T(8,128)(2,1)S(1)}, u32[]{:S(2)}, u32[]{:S(2)}) collective-permute-start(bf16[2320,256]{1,0:T(8,128)(2,1)} %get-tuple-element.43), channel_id=1, source_target_pairs={{0,1},{1,0},{2,3},{3,2},{4,5},{5,4},{6,7},{7,6},{8,9},{9,8},{10,11... | collective-permute-start | bytes 3563528 | tf_op jit(solution)/shard_map/ppermute | solution.py:517
  44.1 31.4 %all-to-all-start.1 = ((bf16[8,2,48,256]{3,2,1,0:T(8,128)(2,1)}), bf16[8,2,48,256]{3,2,1,0:T(8,128)(2,1)S(1)}, u32[]{:S(2)}, u32[]{:S(2)}) async-start(bf16[8,2,48,256]{3,2,1,0:T(8,128)(2,1)} %get-tuple-element.46), calls=%async_computation.1 | async-start | bytes 786432 | tf_op jit(solution)/shard_map/all_to_all | solution.py:509
  47.6 1.0 copy-start.3
  48.6 5.4 %copy-start.13 = (bf16[2,144,256]{2,1,0:T(8,128)(2,1)S(1)}, bf16[2,144,256]{2,1,0:T(8,128)(2,1)}, u32[]{:S(2)}) copy-start(bf16[2,144,256]{2,1,0:T(8,128)(2,1)} %get-tuple-element.47) | copy-start | bytes 442372
  48.6 5.5 %copy-start.12 = (bf16[2,144,256]{2,1,0:T(8,128)(2,1)S(1)}, bf16[2,144,256]{2,1,0:T(8,128)(2,1)}, u32[]{:S(2)}) copy-start(bf16[2,144,256]{2,1,0:T(8,128)(2,1)} %get-tuple-element.48) | copy-start | bytes 442372
  52.1 23.5 %collective-permute-start.3 = (bf16[1168,256]{1,0:T(8,128)(2,1)}, bf16[1168,256]{1,0:T(8,128)(2,1)S(1)}, u32[]{:S(2)}, u32[]{:S(2)}) collective-permute-start(bf16[1168,256]{1,0:T(8,128)(2,1)} %get-tuple-element.45), channel_id=1, source_target_pairs={{0,2},{2,0},{4,6},{6,4},{8,10},{10,8},{12,14},{14,12},{1,3},{3,1},... | collective-permute-start | bytes 1794056 | tf_op jit(solution)/shard_map/ppermute | solution.py:565
  54.0 21.6 %collective-permute-start.4 = (bf16[2,144,256]{2,1,0:T(8,128)(2,1)S(1)}, bf16[2,144,256]{2,1,0:T(8,128)(2,1)S(1)}, u32[]{:S(2)}, u32[]{:S(2)}) collective-permute-start(bf16[2,144,256]{2,1,0:T(8,128)(2,1)S(1)} %copy-done.13), channel_id=1, source_target_pairs={{0,2},{2,0},{4,6},{6,4},{8,10},{10,8},{12,14},{14,12},{1,3},{3,1},... | collective-permute-start | bytes 442376 | tf_op jit(solution)/shard_map/ppermute | solution.py:510
  54.1 21.5 %collective-permute-start.5 = (bf16[2,144,256]{2,1,0:T(8,128)(2,1)S(1)}, bf16[2,144,256]{2,1,0:T(8,128)(2,1)S(1)}, u32[]{:S(2)}, u32[]{:S(2)}) collective-permute-start(bf16[2,144,256]{2,1,0:T(8,128)(2,1)S(1)} %copy-done.12), channel_id=1, source_target_pairs={{0,14},{2,4},{4,2},{6,8},{8,6},{10,12},{12,10},{14,0},{1,15},{3,5}... | collective-permute-start | bytes 442376 | tf_op jit(solution)/shard_map/ppermute | solution.py:511
  75.6 46.6 %copy-start.8 = (bf16[2,144,256]{2,1,0:T(8,128)(2,1)}, bf16[2,144,256]{2,1,0:T(8,128)(2,1)S(1)}, u32[]{:S(2)}) copy-start(bf16[2,144,256]{2,1,0:T(8,128)(2,1)S(1)} %collective-permute-done.4.refs_1_) | copy-start | bytes 442372
  75.6 46.6 %copy-start.9 = (bf16[2,144,256]{2,1,0:T(8,128)(2,1)}, bf16[2,144,256]{2,1,0:T(8,128)(2,1)S(1)}, u32[]{:S(2)}) copy-start(bf16[2,144,256]{2,1,0:T(8,128)(2,1)S(1)} %collective-permute-done.5.refs_2_) | copy-start | bytes 442372
  75.6 24.8 %copy-start.1 = (bf16[8,2,48,256]{3,2,1,0:T(8,128)(2,1)}, bf16[8,2,48,256]{3,2,1,0:T(8,128)(2,1)S(1)}, u32[]{:S(2)}) copy-start(bf16[8,2,48,256]{3,2,1,0:T(8,128)(2,1)S(1)} %all-to-all-done.1.refs_0_) | copy-start | bytes 1179652
  75.6 0.9 copy-start.4
  121.8 7.5 %copy-start = (bf16[4,288,256]{2,1,0:T(8,128)(2,1)}, bf16[4,288,256]{2,1,0:T(8,128)(2,1)S(1)}, u32[]{:S(2)}) copy-start(bf16[4,288,256]{2,1,0:T(8,128)(2,1)S(1)} %all_to_all.21.a_ref) | copy-start | bytes 1769476
  121.8 14.2 %collective-permute-start.6 = (bf16[4,288,256]{2,1,0:T(8,128)(2,1)S(1)}, bf16[4,288,256]{2,1,0:T(8,128)(2,1)S(1)}, u32[]{:S(2)}, u32[]{:S(2)}) collective-permute-start(bf16[4,288,256]{2,1,0:T(8,128)(2,1)S(1)} %all_to_all.21.a_ref), channel_id=1, source_target_pairs={{0,2},{2,0},{4,6},{6,4},{8,10},{10,8},{12,14},{14,12},{1,3},{3,1},... | collective-permute-start | bytes 1769480 | tf_op jit(solution)/shard_map/ppermute | solution.py:565
  129.3 6.6 %collective-permute-start.7 = (bf16[4,288,256]{2,1,0:T(8,128)(2,1)S(1)}, bf16[4,288,256]{2,1,0:T(8,128)(2,1)S(1)}, u32[]{:S(2)}, u32[]{:S(2)}) collective-permute-start(bf16[4,288,256]{2,1,0:T(8,128)(2,1)S(1)} %all_to_all.21.a_ref), channel_id=1, source_target_pairs={{0,1},{1,0},{2,3},{3,2},{4,5},{5,4},{6,7},{7,6},{8,9},{9,8},{10,11... | collective-permute-start | bytes 1769480 | tf_op jit(solution)/shard_map/ppermute | solution.py:517
  135.9 2.0 %copy-start.5 = (bf16[4,288,256]{2,1,0:T(8,128)(2,1)}, bf16[4,288,256]{2,1,0:T(8,128)(2,1)S(1)}, u32[]{:S(2)}) copy-start(bf16[4,288,256]{2,1,0:T(8,128)(2,1)S(1)} %collective-permute-done.6.b_ref) | copy-start | bytes 1769476
  135.9 2.0 %collective-permute-start.8 = (bf16[4,288,256]{2,1,0:T(8,128)(2,1)S(1)}, bf16[4,288,256]{2,1,0:T(8,128)(2,1)S(1)}, u32[]{:S(2)}, u32[]{:S(2)}) collective-permute-start(bf16[4,288,256]{2,1,0:T(8,128)(2,1)S(1)} %collective-permute-done.6.b_ref), channel_id=1, source_target_pairs={{0,1},{1,0},{2,3},{3,2},{4,5},{5,4},{6,7},{7,6},{8,9},{9,8},{10,11... | collective-permute-start | bytes 1769480 | tf_op jit(solution)/shard_map/ppermute | solution.py:517
  135.9 2.0 %copy-start.6 = (bf16[4,288,256]{2,1,0:T(8,128)(2,1)}, bf16[4,288,256]{2,1,0:T(8,128)(2,1)S(1)}, u32[]{:S(2)}) copy-start(bf16[4,288,256]{2,1,0:T(8,128)(2,1)S(1)} %collective-permute-done.7.c_ref) | copy-start | bytes 1769476
  137.9 0.8 copy-start.7

commit v5 on v4

--- a/solution.py
+++ b/solution.py
@@ -10,6 +10,7 @@
 BF = jnp.bfloat16
 F32 = jnp.float32
 EXTRA = 16
+LIMIT = 40
 
 
 class Dims:
@@ -188,7 +189,13 @@
     return out
 
 
-def build_taps(dm, field_ref, ghosts, top, bottom, frame_ref, taps_ref, adjoint):
+def own_first(value, p):
+    half = value.shape[1] // 2
+    low, high = value[:, :half], value[:, half:]
+    return jnp.concatenate([jnp.where(p == 0, low, high), jnp.where(p == 0, high, low)], axis=1)
+
+
+def build_taps(dm, field_ref, ghosts, top, bottom, frame_ref, taps_ref, adjoint, p=None):
     R, F, C = dm.R, dm.F, dm.C
     for f in range(6):
         for r in range(R):
@@ -207,7 +214,10 @@
             frame_ref[m, f, 8 + F : 9 + F] = east
     for m in range(R + 2):
         for b in range(3):
-            plane = frame_ref[m, :, 7 + b : 7 + b + F].reshape(dm.ROW, C).astype(BF)
+            plane = frame_ref[m, :, 7 + b : 7 + b + F].reshape(dm.ROW, C)
+            if p is not None:
+                plane = own_first(plane, p)
+            plane = plane.astype(BF)
             for a in range(3):
                 r = m - 2 + a if adjoint else m - a
                 tap = 3 * a + (2 - b if adjoint else b)
@@ -280,52 +290,40 @@
         acc_ref[(R - 1) * dm.ROW : R * dm.ROW] += strips[dm.WE :]
 
 
-def turn_kernel(w1_ref, w2_ref, w1t_ref, w2t_ref):
-    for w_ref, wt_ref in ((w1_ref, w1t_ref), (w2_ref, w2t_ref)):
-        for tap in range(9):
-            wt_ref[tap] = w_ref[tap].T
-
-
-def put_tap(dm, send_ref, keep_ref, p, which, tap, value):
-    size = 9 * dm.C // (2 * dm.T)
-    start, stop = tap * dm.C, (tap + 1) * dm.C
-    for block in range(2 * dm.T):
-        low, high = max(start, block * size), min(stop, (block + 1) * size)
-        if low >= high:
-            continue
-        at = (block % dm.T) * 2 * size + which * size + low - block * size
-        piece = value[low - start : high - start]
-
-        @pl.when(p == block // dm.T)
-        def _():
-            keep_ref[at : at + high - low] = piece
-
-        @pl.when(p != block // dm.T)
-        def _():
-            send_ref[at : at + high - low] = piece.astype(BF)
-
-
-def put_extra(send_ref, keep_ref, row):
-    c = row.shape[1]
-    n = send_ref.shape[0] - EXTRA
-    i = lax.broadcasted_iota(jnp.int32, (EXTRA, c), 0)
-    high = row.astype(BF)
-    low = (row - high.astype(F32)).astype(BF).astype(F32)
-    keep_ref[n:] = jnp.where(i == 0, row, 0.0)
-    send_ref[n:] = jnp.where(i == 0, high.astype(F32), jnp.where(i == 1, low, 0.0)).astype(BF)
+def turn_kernel(w1_ref, w2_ref, w1s_ref, w1t_ref, w2t_ref):
+    p = lax.axis_index("dp")
+    half = w1_ref.shape[1] // 2
+    for tap in range(9):
+        w1t_ref[tap] = w1_ref[tap].T
+        w2t_ref[tap] = w2_ref[tap].T
+        w1s_ref[tap, :half] = w1_ref[tap, pl.ds(pl.multiple_of(p * half, half), half)]
+        w1s_ref[tap, half:] = w1_ref[tap, pl.ds(pl.multiple_of((1 - p) * half, half), half)]
+
+
+def put_taps(send_ref, keep_ref, which, taps, value):
+    half = value.shape[0] // (2 * len(taps))
+    for i, tap in enumerate(taps):
+        keep_ref[which, tap] = value[2 * i * half : (2 * i + 1) * half]
+        send_ref[which, tap] = value[(2 * i + 1) * half : (2 * i + 2) * half].astype(BF)
+
+
+def high_low(row):
+    i = lax.broadcasted_iota(jnp.int32, (EXTRA, row.shape[1]), 0)
+    high = row.astype(BF).astype(F32)
+    return jnp.where(i == 0, high, jnp.where(i == 1, row - high, 0.0)).astype(BF)
 
 
 def first_kernel(dm, ep, x_ref, up_ref, w1_ref, bias_ref, w2t_ref, *refs):
     T, R, F, N, C = dm.T, dm.R, dm.F, dm.N, dm.C
     messages = refs[:3]
-    send_ref, keep_ref, hid_ref, inner_ref = refs[3:7]
-    out_messages = refs[7:10]
-    table_ref, frame_ref, xs_ref, us_ref, z_ref, before_ref, acc_ref, hcat_ref = refs[10:]
+    send_ref, send_bias_ref, keep_ref, bias_sum_ref, hid_ref, inner_ref = refs[3:9]
+    out_messages = refs[9:12]
+    table_ref, frame_ref, xs_ref, us_ref, z_ref, before_ref, acc_ref, hcat_ref = refs[12:]
     t, p = lax.axis_index("tile"), lax.axis_index("dp")
     own = (x_ref[...].reshape(N, C), up_ref[...].reshape(N, C))
     gx, gu = gather_ghosts(dm, ep, t, own, messages, table_ref)
     top, bottom = dm.WE, dm.WE + dm.ROW
-    build_taps(dm, x_ref, gx[:top], gx[top:bottom], gx[bottom:], frame_ref, xs_ref, False)
+    build_taps(dm, x_ref, gx[:top], gx[top:bottom], gx[bottom:], frame_ref, xs_ref, False, p)
     before = jnp.dot(xs_ref[...], w1_ref[...], preferred_element_type=F32) + bias_ref[...]
     before_ref[...] = before
     sig = 1.0 / (1.0 + jnp.exp(-before))
@@ -350,24 +348,26 @@
             at = (r * 6 + f) * F
             hid_ref[f * R + r] = acc_ref[at : at + F].astype(BF)
     adjoint(dm, t, us_ref, z_ref, w2t_ref, acc_ref)
-    hidden_t = hcat_ref[...].astype(BF).T
+    hidden_t = own_first(hcat_ref[...], p).astype(BF).T
     for tap in range(9):
         grad = jnp.dot(hidden_t, us_ref[:, tap * C : (tap + 1) * C], preferred_element_type=F32)
-        put_tap(dm, send_ref, keep_ref, p, 0, tap, grad)
+        put_taps(send_ref, keep_ref, 0, [tap], grad)
     before = before_ref[...]
     sig = 1.0 / (1.0 + jnp.exp(-before))
     before_grad = acc_ref[...] * (sig * (1.0 + before * (1.0 - sig)))
     acc_ref[...] = before_grad
     inner = before_grad.astype(BF)
-    for tap in range(9):
+    for taps in ((0, 1, 2), (3, 4, 5), (6, 7, 8)):
         grad = lax.dot_general(
-            xs_ref[:, tap * C : (tap + 1) * C],
+            xs_ref[:, taps[0] * C : (taps[-1] + 1) * C],
             inner,
             (((0,), (0,)), ((), ())),
             preferred_element_type=F32,
         )
-        put_tap(dm, send_ref, keep_ref, p, 1, tap, grad)
-    put_extra(send_ref, keep_ref, jnp.sum(before_grad, axis=0, keepdims=True))
+        put_taps(send_ref, keep_ref, 1, taps, grad)
+    bias_sum = jnp.sum(before_grad, axis=0, keepdims=True)
+    bias_sum_ref[...] = bias_sum
+    send_bias_ref[...] = high_low(bias_sum)
     for r in range(R):
         for f in range(6):
             at = (r * 6 + f) * F
@@ -404,88 +404,87 @@
             grad_ref[f * R + r] = d_ref[f * R + r].astype(F32) + acc_ref[at : at + F]
 
 
-def extra_sum(keep, recv, n):
-    return keep[n : n + 1] + recv[n : n + 1].astype(F32) + recv[n + 1 : n + 2].astype(F32)
-
-
-def extra_rows(extra):
-    i = lax.broadcasted_iota(jnp.int32, (EXTRA, extra.shape[1]), 0)
-    high = extra.astype(BF).astype(F32)
-    tail = jnp.where(i == 0, high, jnp.where(i == 1, extra - high, 0.0)).astype(BF)
-    return jnp.where(i == 0, extra, 0.0), tail
-
-
-def half_kernel(keep_ref, recv_ref, out_keep, out_send):
-    n = keep_ref.shape[0] - EXTRA
-    size = n // 2
+def both(pair):
+    return pair[0:1].astype(F32) + pair[1:2].astype(F32)
+
+
+def half_kernel(keep_ref, bias_ref, recv_ref, recv_bias_ref, out_keep, out_bias, out_send, out_send_bias):
+    size = keep_ref.shape[2] // 2
     own = lax.axis_index("tile") % 2
-    mine = pl.multiple_of(own * size, 8)
-    far = pl.multiple_of((1 - own) * size, 8)
-    out_keep[0:size] = keep_ref[pl.ds(mine, size)] + recv_ref[pl.ds(mine, size)].astype(F32)
-    out_send[0:size] = (keep_ref[pl.ds(far, size)] + recv_ref[pl.ds(far, size)].astype(F32)).astype(BF)
-    keep, tail = extra_rows(extra_sum(keep_ref, recv_ref, n))
-    out_keep[size:] = keep
-    out_send[size:] = tail
-
-
-def block_kernel(zcount, keep_ref, recv_ref, out_keep, out_sends):
-    n = keep_ref.shape[0] - EXTRA
-    size = n // zcount
+    mine = pl.ds(pl.multiple_of(own * size, size), size)
+    far = pl.ds(pl.multiple_of((1 - own) * size, size), size)
+    for which in range(2):
+        for tap in range(9):
+            out_keep[which, tap] = keep_ref[which, tap, mine] + recv_ref[which, tap, mine].astype(F32)
+            out = keep_ref[which, tap, far] + recv_ref[which, tap, far].astype(F32)
+            out_send[which, tap] = out.astype(BF)
+    bias = bias_ref[...] + both(recv_bias_ref)
+    out_bias[...] = bias
+    out_send_bias[...] = high_low(bias)
+
+
+def block_kernel(zcount, keep_ref, bias_ref, recv_ref, recv_bias_ref, out_keep, out_bias, out_sends):
+    size = keep_ref.shape[2] // zcount
     own = lax.axis_index("tile") // 2
-    keep, tail = extra_rows(extra_sum(keep_ref, recv_ref, n))
+    bias = bias_ref[...] + both(recv_bias_ref)
+    out_bias[...] = bias
+    tail = high_low(bias)
     for j in range(zcount):
-        at = slice(j * size, (j + 1) * size)
-        total = keep_ref[at] + recv_ref[at].astype(F32)
-        out_sends[j, 0:size] = total.astype(BF)
-        out_sends[j, size:] = tail
-
-        @pl.when(own == j)
-        def _():
-            out_keep[0:size] = total
-
-    out_keep[size:] = keep
-
-
-def last_kernel(zcount, keep_ref, recv_ref, block_ref, extra_ref):
-    n = keep_ref.shape[0] - EXTRA
+        rows = slice(j * size, (j + 1) * size)
+        for which in range(2):
+            for tap in range(9):
+                total = keep_ref[which, tap, rows] + recv_ref[which, tap, rows].astype(F32)
+                at = (9 * which + tap) * size
+                out_sends[j, at : at + size] = total.astype(BF)
+        out_sends[j, 18 * size :] = tail
+    mine = pl.ds(pl.multiple_of(own * size, size), size)
+    for which in range(2):
+        for tap in range(9):
+            at = (9 * which + tap) * size
+            out_keep[at : at + size] = keep_ref[which, tap, mine] + recv_ref[which, tap, mine].astype(F32)
+
+
+def last_kernel(zcount, keep_ref, bias_ref, recv_ref, block_ref, bias_sum_ref):
+    n = keep_ref.shape[0]
     own = lax.axis_index("tile") // 2
-    total = keep_ref[0:n]
-    extra = keep_ref[n : n + 1]
+    total = keep_ref[...]
+    bias = bias_ref[...]
     for j in range(zcount):
         far = own != j
         total = total + jnp.where(far, recv_ref[j, 0:n].astype(F32), 0.0)
-        parts = recv_ref[j, n : n + 2].astype(F32)
-        extra = extra + jnp.where(far, parts[0:1] + parts[1:2], 0.0)
+        bias = bias + jnp.where(far, both(recv_ref[j, n : n + 2]), 0.0)
     for j in range(zcount):
         block_ref[j] = total.astype(BF)
-    extra_ref[...] = extra
-
-
-def normal_kernel(zcount, a_ref, b_ref, c_ref, d_ref, extra_ref, second_ref, first_ref, bias_ref):
+    bias_sum_ref[...] = bias
+
+
+def normal_kernel(zcount, a_ref, b_ref, c_ref, d_ref, bias_sum_ref, second_ref, first_ref, bias_ref):
     t, p = lax.axis_index("tile"), lax.axis_index("dp")
     refs = (a_ref, b_ref, c_ref, d_ref)
-    size = a_ref.shape[1] // 2
+    size = a_ref.shape[1] // 18
     for which, out_ref in enumerate((second_ref, first_ref)):
-        rows = slice(which * size, (which + 1) * size)
+        rows = slice(which * 9 * size, (which + 1) * 9 * size)
         square = None
         for ref in refs:
             for j in range(zcount):
                 v = ref[j, rows].astype(F32)
                 s = jnp.sum(v * v, axis=0, keepdims=True)
                 square = s if square is None else square + s
-        mean = jnp.sum(square, keepdims=True) / (out_ref.shape[0] * out_ref.shape[1])
+        mean = jnp.sum(square, keepdims=True) / (9 * out_ref.shape[1] * out_ref.shape[2])
         scale = lax.rsqrt(mean + 1e-06)
         for index, ref in enumerate(refs):
             block = (p ^ (index // 2)) * 2 + ((t % 2) ^ (index % 2))
             for j in range(zcount):
-                at = pl.multiple_of((block * zcount + j) * size, 8)
-                out_ref[pl.ds(at, size)] = ref[j, rows].astype(F32) * scale
-    extra = extra_ref[...]
-    bias_mean = jnp.mean(extra * extra, keepdims=True)
-    bias_ref[...] = extra * lax.rsqrt(bias_mean + 1e-06)
-
-
-def call(kernel, out_shapes, scratch=(), smem_first=False):
+                at = pl.ds(pl.multiple_of((block * zcount + j) * size, size), size)
+                for tap in range(9):
+                    row = (9 * which + tap) * size
+                    out_ref[tap, at] = ref[j, row : row + size].astype(F32) * scale
+    total = bias_sum_ref[...]
+    bias_mean = jnp.mean(total * total, keepdims=True)
+    bias_ref[...] = total * lax.rsqrt(bias_mean + 1e-06)
+
+
+def call(kernel, out_shapes, scratch=(), smem_first=False, limit=16):
     def run(*args):
         vmem = pl.BlockSpec(memory_space=pltpu.VMEM)
         smem = pl.BlockSpec(memory_space=pltpu.SMEM)
@@ -496,7 +495,7 @@
             in_specs=specs,
             out_specs=[vmem] * len(out_shapes),
             scratch_shapes=[pltpu.VMEM(s, dt) for s, dt in scratch],
-            compiler_params=pltpu.CompilerParams(vmem_limit_bytes=56 << 20),
+            compiler_params=pltpu.CompilerParams(vmem_limit_bytes=limit << 20),
         )(*args)
 
     return run
@@ -527,7 +526,8 @@
     taps = (9, channels, channels)
     w1 = w_first.reshape(9 * channels, channels)
     w2 = w_second.reshape(9 * channels, channels)
-    w1t, w2t = call(turn_kernel, [(taps, BF)] * 2)(w_first.reshape(taps), w_second.reshape(taps))
+    w1s, w1t, w2t = call(turn_kernel, [(taps, BF)] * 3)(w_first.reshape(taps), w_second.reshape(taps))
+    w1s = w1s.reshape(w1.shape)
     w1t = w1t.reshape(w1.shape)
     w2t = w2t.reshape(w2.shape)
     msg_shapes = [(shape, BF) for shape in dm.messages()]
@@ -536,12 +536,20 @@
         edge_partner, x.reshape(flat), d.reshape(flat)
     )
     messages = exchange(tiles, messages)
-    half = 9 * channels
+    half = channels // 2
     wide = 9 * channels
     frame = (rows + 2, 6, face + 16, channels)
     outs = call(
         functools.partial(first_kernel, dm),
-        [((half + EXTRA, channels), BF), ((half + EXTRA, channels), F32)] + [(planes, BF)] * 2 + msg_shapes,
+        [
+            ((2, 9, half, channels), BF),
+            ((EXTRA, channels), BF),
+            ((2, 9, half, channels), F32),
+            ((1, channels), F32),
+            (planes, BF),
+            (planes, BF),
+        ]
+        + msg_shapes,
         [
             ((dm.NT, channels), BF),
             (frame, F32),
@@ -553,8 +561,9 @@
             ((dm.N + dm.S, channels), F32),
         ],
         smem_first=True,
-    )(edge_partner, x, d, w1, bias.reshape(1, channels), w2t, *messages)
-    send, keep, hidden, inner = outs[:4]
+        limit=LIMIT,
+    )(edge_partner, x, d, w1s, bias.reshape(1, channels), w2t, *messages)
+    send, send_bias, keep, bias_sum, hidden, inner = outs[:6]
 
     zcount = tiles // 2
     n = half // 2
@@ -567,19 +576,25 @@
     def along_z(v):
         return lax.all_to_all(v, "tile", 0, 0, axis_index_groups=groups)
 
-    keep, send = call(half_kernel, [((n + EXTRA, channels), F32), ((n + EXTRA, channels), BF)])(
-        keep, swap_dp(send)
-    )
-    recv = along_y(send)
-    messages = exchange(tiles, outs[4:])
+    keep, bias_sum, send, send_bias = call(
+        half_kernel,
+        [
+            ((2, 9, n, channels), F32),
+            ((1, channels), F32),
+            ((2, 9, n, channels), BF),
+            ((EXTRA, channels), BF),
+        ],
+    )(keep, bias_sum, swap_dp(send), swap_dp(send_bias))
+    recv, recv_bias = along_y(send), along_y(send_bias)
+    messages = exchange(tiles, outs[6:])
     recv, messages = lax.optimization_barrier((recv, messages))
-    keep, sends = call(
+    keep, bias_sum, sends = call(
         functools.partial(block_kernel, zcount),
-        [((m + EXTRA, channels), F32), ((zcount, m + EXTRA, channels), BF)],
-    )(keep, recv)
-    blocks, extra = call(
-        functools.partial(last_kernel, zcount), [((zcount, m, channels), BF), ((1, channels), F32)]
-    )(keep, along_z(sends))
+        [((18 * m, channels), F32), ((1, channels), F32), ((zcount, 18 * m + EXTRA, channels), BF)],
+    )(keep, bias_sum, recv, recv_bias)
+    blocks, bias_sum = call(
+        functools.partial(last_kernel, zcount), [((zcount, 18 * m, channels), BF), ((1, channels), F32)]
+    )(keep, bias_sum, along_z(sends))
     own = along_z(blocks)
     other = along_y(own)
     messages, _ = lax.optimization_barrier((messages, own))
@@ -595,12 +610,14 @@
             (flat, F32),
         ],
         smem_first=True,
+        limit=LIMIT,
     )(edge_partner, x, d, hidden, inner, w1t, w2, *messages)
     other, state, grad = lax.optimization_barrier((other, state, grad))
     second_step, first_step, bias_step = call(
         functools.partial(normal_kernel, zcount),
-        [((half, channels), F32)] * 2 + [((1, channels), F32)],
-    )(own, other, swap_dp(own), swap_dp(other), extra)
+        [(taps, F32)] * 2 + [((1, channels), F32)],
+        limit=24,
+    )(own, other, swap_dp(own), swap_dp(other), bias_sum)
     return (
         state.reshape(initial_state.shape),
         grad.reshape(initial_state.shape),

time: 144 us -> 141 us (0.979)
  Pallas kernels: 42.3 us -> 22.9 us
  local copies, waits for them, and re-layouts: 4.89 us -> 22.7 us
  starting transfers between devices: 23.2 us -> 25.8 us
  blocking collectives: 40.7 us -> 38.4 us
  waiting for transfers between devices: 31.3 us -> 29.8 us
    pallas_call x8, Pallas kernels: 42.3 us -> 22.9 us  [run(): pl.pallas_call(kernel, out_shape=[jax.ShapeDtypeStruct(s, dt) for s, dt i...]
    unnamed x29 -> x67, local copies, waits for them, and re-layouts: 4.89 us -> 22.7 us
    all_to_all x2, blocking collectives: 40.7 us -> 38.4 us  [along_z(): return lax.all_to_all(v, 'tile', 0, 0, axis_index_groups=groups)]
    ppermute x2, waiting for transfers between devices: 19.6 us -> 17.8 us  [exchange(): lax.ppermute(pair, 'tile', [(i, i ^ 1) for i in range(tiles)])]
    ppermute x2 -> x3, starting transfers between devices: 2.37 us -> 3.78 us  [along_y(): return lax.ppermute(v, 'tile', [(i, i ^ 1) for i in range(tiles)])]
    ppermute x3 -> x4, waiting for transfers between devices: 1.99 us -> 3.04 us  [swap_dp(): return lax.ppermute(v, 'dp', [(i, count - 1 - i) for i in range(count)])]
    ppermute x2 -> x3, waiting for transfers between devices: 6.62 us -> 6.39 us  [along_y(): return lax.ppermute(v, 'tile', [(i, i ^ 1) for i in range(tiles)])]
  transfers between devices with their start and end apart: 11 -> 13, of which waited for: 5 -> 7; matrix products, arithmetic and copies ran while one was open for 0% -> 0% of each run, Pallas kernels for 10% -> 6%
where the time goes in v5:
time: 141 us; the launch traced here: 140 us
  blocking collectives  38.4 us (27%)
  waiting for transfers between devices  29.8 us (21%)
  starting transfers between devices  25.8 us (18%)
  Pallas kernels  22.9 us (16%)
  local copies, waits for them, and re-layouts  22.7 us (16%)
    all_to_all x2, blocking collectives, along_z(): return lax.all_to_all(v, 'tile', 0, 0, axis_index_groups=groups)  38.4 us
    pallas_call x8, Pallas kernels, run(): pl.pallas_call(kernel, out_shape=[jax.ShapeDtypeStruct(s, dt) for s, dt i...  22.9 us
    unnamed x67, local copies, waits for them, and re-layouts  22.7 us
    ppermute x2, waiting for transfers between devices, exchange(): lax.ppermute(pair, 'tile', [(i, i ^ 1) for i in range(tiles)])  17.8 us
    all_to_all x2, starting transfers between devices, exchange(): lax.all_to_all(strips, 'tile', 0, 0)  11.4 us
    ppermute x2, starting transfers between devices, exchange(): lax.ppermute(ring, 'tile', other)  7.67 us
    ppermute x3, waiting for transfers between devices, along_y(): return lax.ppermute(v, 'tile', [(i, i ^ 1) for i in range(tiles)])  6.39 us
    ppermute x3, starting transfers between devices, along_y(): return lax.ppermute(v, 'tile', [(i, i ^ 1) for i in range(tiles)])  3.78 us
  transfers between devices with their start and end apart: 13, of which 7 were waited for; matrix products, arithmetic and copies ran while one was open for 0% of the time, Pallas kernels for 6%

profile of v5, /device:TPU:0, one launch (start us, length us, event | category | flops | bytes accessed | tf_op | source)
XLA Modules:
  0.0 140.3 jit_solution(9515194777664441371)
XLA Ops:
  0.6 0.9 copy.12.ep
  1.5 0.9 copy-done.1
  2.4 0.9 copy-done.4
  3.4 2.7 %shard_map.102 = (bf16[8,2,48,256]{3,2,1,0:T(8,128)(2,1)}, bf16[2,144,256]{2,1,0:T(8,128)(2,1)S(1)}, bf16[2,144,256]{2,1,0:T(8,128)(2,1)S(1)}) custom-call(s32[6,4]{1,0:T(8,128)S(1)} %copy.12.ep, bf16[432,256]{1,0:T(8,128)(2,1)S(1)} %bitcast.18, bf16[432,256]{1,0:T(8,128)(2,1)S(1)} %bitcast.21), custom_call_target="tpu_custom_call" | custom-call | tf_op jit(solution)/shard_map/pallas_call | solution.py:492
  6.1 7.3 %all-to-all-start = ((bf16[8,2,48,256]{3,2,1,0:T(8,128)(2,1)}), bf16[8,2,48,256]{3,2,1,0:T(8,128)(2,1)S(1)}, u32[]{:S(2)}, u32[]{:S(2)}) async-start(bf16[8,2,48,256]{3,2,1,0:T(8,128)(2,1)} %get-tuple-element.46), calls=%async_computation | async-start | bytes 786432 | tf_op jit(solution)/shard_map/all_to_all | solution.py:508
  13.4 2.0 %collective-permute-start = (bf16[2,144,256]{2,1,0:T(8,128)(2,1)S(1)}, bf16[2,144,256]{2,1,0:T(8,128)(2,1)S(1)}, u32[]{:S(2)}, u32[]{:S(2)}) collective-permute-start(bf16[2,144,256]{2,1,0:T(8,128)(2,1)S(1)} %get-tuple-element.47), channel_id=1, source_target_pairs={{0,2},{2,0},{4,6},{6,4},{8,10},{10,8},{12,14},{14,12},{1,3},{3,1},... | collective-permute-start | bytes 442376 | tf_op jit(solution)/shard_map/ppermute | solution.py:509
  15.4 3.3 %collective-permute-start.1 = (bf16[2,144,256]{2,1,0:T(8,128)(2,1)S(1)}, bf16[2,144,256]{2,1,0:T(8,128)(2,1)S(1)}, u32[]{:S(2)}, u32[]{:S(2)}) collective-permute-start(bf16[2,144,256]{2,1,0:T(8,128)(2,1)S(1)} %get-tuple-element.48), channel_id=1, source_target_pairs={{0,14},{2,4},{4,2},{6,8},{8,6},{10,12},{12,10},{14,0},{1,15},{3,5}... | collective-permute-start | bytes 442376 | tf_op jit(solution)/shard_map/ppermute | solution.py:510
  18.7 1.3 copy-done.15
  20.0 0.7 shard_map.101
  20.6 0.0 copy-start.9
  20.7 1.1 copy-done.9
  21.7 1.0 copy-done.11
  22.7 1.0 copy-done.13
  23.7 1.0 collective-permute-done.refs_1_
  24.7 0.7 copy-done.23
  25.4 2.6 %collective-permute-done.1.refs_2_ = bf16[2,144,256]{2,1,0:T(8,128)(2,1)S(1)} collective-permute-done((bf16[2,144,256]{2,1,0:T(8,128)(2,1)S(1)}, bf16[2,144,256]{2,1,0:T(8,128)(2,1)S(1)}, u32[]{:S(2)}, u32[]{:S(2)}) %collective-permute-start.1) | collective-permute-done | bytes 147488 | tf_op jit(solution)/shard_map/ppermute | solution.py:510
  27.9 0.7 copy-done.25
  28.6 0.0 all-to-all-done.refs_0_
  28.6 0.7 copy-done.7
  29.4 0.9 copy-done.2
  30.3 0.9 copy-done.5
  31.2 1.0 copy-done.8
  32.2 1.3 copy-done.12
  33.5 1.3 copy-done.14
  34.8 0.9 copy-done.24
  35.7 0.9 copy-done.26
  36.6 8.3 %shard_map.103 = (bf16[2,9,128,256]{3,2,1,0:T(8,128)(2,1)}, bf16[16,256]{1,0:T(8,128)(2,1)S(1)}, f32[2,9,128,256]{3,2,1,0:T(8,128)S(1)}, f32[1,256]{1,0:T(1,128)...) custom-call(s32[6,4]{1,0:T(8,128)S(1)} %copy.12.ep, ...), custom_call_target="tpu_custom_call" | custom-call | tf_op jit(solution)/shard_map/pallas_call | solution.py:492
  44.9 0.7 copy-done.18
  45.6 0.7 copy-done.19
  46.3 0.7 copy-done.21
  47.0 0.6 copy-done.28
  47.7 0.7 copy-done.30
  48.3 0.6 copy-done.32
  48.9 0.0 collective-permute-start.2
  48.9 4.1 %all-to-all-start.1 = ((bf16[8,2,48,256]{3,2,1,0:T(8,128)(2,1)}), bf16[8,2,48,256]{3,2,1,0:T(8,128)(2,1)}, u32[]{:S(2)}, u32[]{:S(2)}) async-start(bf16[8,2,48,256]{3,2,1,0:T(8,128)(2,1)} %copy-done.18), calls=%async_computation.1 | async-start | bytes 786432 | tf_op jit(solution)/shard_map/all_to_all | solution.py:508
  53.0 0.6 collective-permute-start.3
  53.6 1.0 collective-permute-done.3.recv_bias_ref
  54.7 0.0 collective-permute-done.2.recv_ref
  54.7 2.3 %shard_map.104 = (f32[2,9,64,256]{3,2,1,0:T(8,128)S(1)}, f32[1,256]{1,0:T(1,128)S(1)}, bf16[2,9,64,256]{3,2,1,0:T(8,128)(2,1)}, bf16[16,256]{1,0:T(8,128)(2,1)}) custom-call(f32[2,9,128,256]{3,2,1,0:T(8,128)S(1)} %get-tuple-element.49.keep_ref, f32[1,256]{1,0:T(1,128)S(1)} %get-tuple-element.50.bias_ref, ...), custom_call_target="tpu_custom_call" | custom-call | tf_op jit(solution)/shard_map/pallas_call | solution.py:492
  57.0 1.0 copy-done.16
  58.0 1.7 %collective-permute-start.4 = (bf16[2,9,64,256]{3,2,1,0:T(8,128)(2,1)}, bf16[2,9,64,256]{3,2,1,0:T(8,128)(2,1)S(1)}, u32[]{:S(2)}, u32[]{:S(2)}) collective-permute-start(bf16[2,9,64,256]{3,2,1,0:T(8,128)(2,1)} %get-tuple-element.55), channel_id=1, source_target_pairs={{0,2},{2,0},{4,6},{6,4},{8,10},{10,8},{12,14},{14,12},{1,3},{3,1},... | collective-permute-start | bytes 1769480 | tf_op jit(solution)/shard_map/ppermute | solution.py:574
  59.6 0.0 copy-done.31
  59.6 0.4 collective-permute-start.5
  60.0 4.4 %collective-permute-start.6 = (bf16[2,144,256]{2,1,0:T(8,128)(2,1)S(1)}, bf16[2,144,256]{2,1,0:T(8,128)(2,1)S(1)}, u32[]{:S(2)}, u32[]{:S(2)}) collective-permute-start(bf16[2,144,256]{2,1,0:T(8,128)(2,1)S(1)} %copy-done.29), channel_id=1, source_target_pairs={{0,14},{2,4},{4,2},{6,8},{8,6},{10,12},{12,10},{14,0},{1,15},{3,5}... | collective-permute-start | bytes 442376 | tf_op jit(solution)/shard_map/ppermute | solution.py:510
  64.4 0.0 collective-permute-start.7
  64.4 16.8 %collective-permute-done.5.refs_1_ = bf16[2,144,256]{2,1,0:T(8,128)(2,1)S(1)} collective-permute-done((bf16[2,144,256]{2,1,0:T(8,128)(2,1)S(1)}, bf16[2,144,256]{2,1,0:T(8,128)(2,1)S(1)}, u32[]{:S(2)}, u32[]{:S(2)}) %collective-permute-start.5) | collective-permute-done | bytes 147488 | tf_op jit(solution)/shard_map/ppermute | solution.py:509
  81.2 0.0 collective-permute-done.6.refs_2_
  81.2 0.0 all-to-all-done.1.refs_0_
  81.2 0.0 collective-permute-done.4.recv_ref
  81.2 0.1 collective-permute-done.7.recv_bias_ref
  81.3 1.3 copy-done.17
  82.6 0.1 shard_map.105
  82.7 20.3 %all_to_all.20.recv_ref = bf16[4,304,256]{2,1,0:T(8,128)(2,1)S(1)} all-to-all(bf16[4,304,256]{2,1,0:T(8,128)(2,1)S(1)} %get-tuple-element.63), channel_id=1, replica_groups={{0,4,8,12},{2,6,10,14},{1,5,9,13},{3,7,11,15},{16,20,24,28},{18,22,26,3..., dimensions={0} | all-to-all | bytes 1245184 | tf_op jit(solution)/shard_map/all_to_all | solution.py:577
  103.0 0.0 copy-start.22
  103.0 0.2 shard_map.106
  103.2 18.1 %all_to_all.21.a_ref = bf16[4,288,256]{2,1,0:T(8,128)(2,1)S(1)} all-to-all(bf16[4,288,256]{2,1,0:T(8,128)(2,1)S(1)} %get-tuple-element.64), channel_id=1, replica_groups={{0,4,8,12},{2,6,10,14},{1,5,9,13},{3,7,11,15},{16,20,24,28},{18,22,26,3..., dimensions={0} | all-to-all | bytes 1179648 | tf_op jit(solution)/shard_map/all_to_all | solution.py:577
  121.2 2.1 %collective-permute-start.8 = (bf16[4,288,256]{2,1,0:T(8,128)(2,1)S(1)}, bf16[4,288,256]{2,1,0:T(8,128)(2,1)S(1)}, u32[]{:S(2)}, u32[]{:S(2)}) collective-permute-start(bf16[4,288,256]{2,1,0:T(8,128)(2,1)S(1)} %all_to_all.21.a_ref), channel_id=1, source_target_pairs={{0,2},{2,0},{4,6},{6,4},{8,10},{10,8},{12,14},{14,12},{1,3},{3,1},... | collective-permute-start | bytes 1769480 | tf_op jit(solution)/shard_map/ppermute | solution.py:574
  123.4 6.0 %shard_map.107 = (bf16[18,24,256]{2,1,0:T(8,128)(2,1)}, f32[18,24,256]{2,1,0:T(8,128)}) custom-call(s32[6,4]{1,0:T(8,128)S(1)} %copy.12.ep, bf16[18,24,256]{2,1,0:T(8,128)(2,1)S(1)} %bitcast.20, bf16[18,24,256]{2,1,0:T(8,128)(2,1)S(1)} %bitcast.23, bf16[18,24,256]{2,1,0:T(8,128)(2,1)S(1)} %copy-done.20, bf16[18,24,256]{2,1,0:T(8,128)(2,1)S(1)} %copy-done.22, ...), custom_call_target="tpu_custom_call" | custom-call | tf_op jit(solution)/shard_map/pallas_call | solution.py:492
  129.3 0.0 collective-permute-start.9
  129.3 6.3 %collective-permute-done.8.b_ref = bf16[4,288,256]{2,1,0:T(8,128)(2,1)S(1)} collective-permute-done((bf16[4,288,256]{2,1,0:T(8,128)(2,1)S(1)}, bf16[4,288,256]{2,1,0:T(8,128)(2,1)S(1)}, u32[]{:S(2)}, u32[]{:S(2)}) %collective-permute-start.8) | collective-permute-done | bytes 589856 | tf_op jit(solution)/shard_map/ppermute | solution.py:574
  135.6 0.0 collective-permute-start.10
  135.7 0.0 collective-permute-done.9.c_ref
  135.7 2.0 %collective-permute-done.10.d_ref = bf16[4,288,256]{2,1,0:T(8,128)(2,1)S(1)} collective-permute-done((bf16[4,288,256]{2,1,0:T(8,128)(2,1)S(1)}, bf16[4,288,256]{2,1,0:T(8,128)(2,1)S(1)}, u32[]{:S(2)}, u32[]{:S(2)}) %collective-permute-start.10) | collective-permute-done | bytes 589856 | tf_op jit(solution)/shard_map/ppermute | solution.py:516
  137.7 2.6 %shard_map.108 = (f32[9,256,256]{2,1,0:T(8,128)}, f32[9,256,256]{2,1,0:T(8,128)}, f32[1,256]{1,0:T(1,128)}) custom-call(bf16[4,288,256]{2,1,0:T(8,128)(2,1)S(1)} %all_to_all.21.a_ref, bf16[4,288,256]{2,1,0:T(8,128)(2,1)S(1)} %collective-permute-done.8.b_ref, bf16[4,288,256]{2,1,0:T(8,128)(2,1)S(1)} %collective-permute-done.9.c_ref, ...), custom_call_target="tpu_custom_call" | custom-call | tf_op jit(solution)/shard_map/pallas_call | solution.py:492
  (39 shorter events, 0.1 us)
Async XLA Ops:
  0.6 18.1 %copy-start = (bf16[3,3,256,256]{3,2,1,0:T(8,128)(2,1)S(1)}, bf16[3,3,256,256]{3,2,1,0:T(8,128)(2,1)}, u32[]{:S(2)}) copy-start(bf16[3,3,256,256]{3,2,1,0:T(8,128)(2,1)} %param.10) | copy-start | bytes 3538948
  1.5 0.9 copy-start.1
  2.4 0.9 copy-start.4
  6.1 22.5 %all-to-all-start = ((bf16[8,2,48,256]{3,2,1,0:T(8,128)(2,1)}), bf16[8,2,48,256]{3,2,1,0:T(8,128)(2,1)S(1)}, u32[]{:S(2)}, u32[]{:S(2)}) async-start(bf16[8,2,48,256]{3,2,1,0:T(8,128)(2,1)} %get-tuple-element.46), calls=%async_computation | async-start | bytes 786432 | tf_op jit(solution)/shard_map/all_to_all | solution.py:508
  13.4 11.3 %collective-permute-start = (bf16[2,144,256]{2,1,0:T(8,128)(2,1)S(1)}, bf16[2,144,256]{2,1,0:T(8,128)(2,1)S(1)}, u32[]{:S(2)}, u32[]{:S(2)}) collective-permute-start(bf16[2,144,256]{2,1,0:T(8,128)(2,1)S(1)} %get-tuple-element.47), channel_id=1, source_target_pairs={{0,2},{2,0},{4,6},{6,4},{8,10},{10,8},{12,14},{14,12},{1,3},{3,1},... | collective-permute-start | bytes 442376 | tf_op jit(solution)/shard_map/ppermute | solution.py:509
  15.4 12.5 %collective-permute-start.1 = (bf16[2,144,256]{2,1,0:T(8,128)(2,1)S(1)}, bf16[2,144,256]{2,1,0:T(8,128)(2,1)S(1)}, u32[]{:S(2)}, u32[]{:S(2)}) collective-permute-start(bf16[2,144,256]{2,1,0:T(8,128)(2,1)S(1)} %get-tuple-element.48), channel_id=1, source_target_pairs={{0,14},{2,4},{4,2},{6,8},{8,6},{10,12},{12,10},{14,0},{1,15},{3,5}... | collective-permute-start | bytes 442376 | tf_op jit(solution)/shard_map/ppermute | solution.py:510
  18.7 1.3 copy-start.15
  20.0 9.4 %copy-start.27 = (f32[256]{0:T(256)S(1)}, f32[256]{0:T(256)}, u32[]{:S(2)}) copy-start(f32[256]{0:T(256)} %param.9) | copy-start | bytes 3076
  20.6 1.1 copy-start.9
  21.7 1.0 copy-start.11
  22.7 1.0 copy-start.13
  24.7 0.7 copy-start.23
  27.9 0.7 copy-start.25
  28.6 0.7 copy-start.7
  29.4 0.9 copy-start.2
  30.3 0.9 copy-start.5
  31.2 1.0 copy-start.8
  32.2 1.3 copy-start.12
  33.5 1.3 copy-start.14
  34.8 0.9 copy-start.24
  35.7 0.9 copy-start.26
  44.9 0.7 copy-start.18
  45.6 0.7 copy-start.19
  46.3 0.7 copy-start.21
  47.0 0.6 copy-start.28
  47.7 0.7 copy-start.30
  48.3 0.6 copy-start.32
  48.9 5.7 %collective-permute-start.2 = (bf16[2,9,128,256]{3,2,1,0:T(8,128)(2,1)}, bf16[2,9,128,256]{3,2,1,0:T(8,128)(2,1)}, u32[]{:S(2)}, u32[]{:S(2)}) collective-permute-start(bf16[2,9,128,256]{3,2,1,0:T(8,128)(2,1)} %get-tuple-element.51), channel_id=1, source_target_pairs={{0,1},{1,0},{2,3},{3,2},{4,5},{5,4},{6,7},{7,6},{8,9},{9,8},{10,11... | collective-permute-start | bytes 3538952 | tf_op jit(solution)/shard_map/ppermute | solution.py:516
  48.9 32.3 %all-to-all-start.1 = ((bf16[8,2,48,256]{3,2,1,0:T(8,128)(2,1)}), bf16[8,2,48,256]{3,2,1,0:T(8,128)(2,1)}, u32[]{:S(2)}, u32[]{:S(2)}) async-start(bf16[8,2,48,256]{3,2,1,0:T(8,128)(2,1)} %copy-done.18), calls=%async_computation.1 | async-start | bytes 786432 | tf_op jit(solution)/shard_map/all_to_all | solution.py:508
  53.0 1.6 %collective-permute-start.3 = (bf16[16,256]{1,0:T(8,128)(2,1)}, bf16[16,256]{1,0:T(8,128)(2,1)S(1)}, u32[]{:S(2)}, u32[]{:S(2)}) collective-permute-start(bf16[16,256]{1,0:T(8,128)(2,1)} %copy-done.32), channel_id=1, source_target_pairs={{0,1},{1,0},{2,3},{3,2},{4,5},{5,4},{6,7},{7,6},{8,9},{9,8},{10,11... | collective-permute-start | bytes 24584 | tf_op jit(solution)/shard_map/ppermute | solution.py:516
  54.7 5.0 %copy-start.31 = (bf16[2,144,256]{2,1,0:T(8,128)(2,1)S(1)}, bf16[2,144,256]{2,1,0:T(8,128)(2,1)}, u32[]{:S(2)}) copy-start(bf16[2,144,256]{2,1,0:T(8,128)(2,1)} %copy-done.30) | copy-start | bytes 442372
  54.7 5.3 %copy-start.29 = (bf16[2,144,256]{2,1,0:T(8,128)(2,1)S(1)}, bf16[2,144,256]{2,1,0:T(8,128)(2,1)}, u32[]{:S(2)}) copy-start(bf16[2,144,256]{2,1,0:T(8,128)(2,1)} %copy-done.28) | copy-start | bytes 442372
  57.0 1.0 copy-start.16
  58.0 23.3 %collective-permute-start.4 = (bf16[2,9,64,256]{3,2,1,0:T(8,128)(2,1)}, bf16[2,9,64,256]{3,2,1,0:T(8,128)(2,1)S(1)}, u32[]{:S(2)}, u32[]{:S(2)}) collective-permute-start(bf16[2,9,64,256]{3,2,1,0:T(8,128)(2,1)} %get-tuple-element.55), channel_id=1, source_target_pairs={{0,2},{2,0},{4,6},{6,4},{8,10},{10,8},{12,14},{14,12},{1,3},{3,1},... | collective-permute-start | bytes 1769480 | tf_op jit(solution)/shard_map/ppermute | solution.py:574
  59.6 21.6 %collective-permute-start.5 = (bf16[2,144,256]{2,1,0:T(8,128)(2,1)S(1)}, bf16[2,144,256]{2,1,0:T(8,128)(2,1)S(1)}, u32[]{:S(2)}, u32[]{:S(2)}) collective-permute-start(bf16[2,144,256]{2,1,0:T(8,128)(2,1)S(1)} %copy-done.31), channel_id=1, source_target_pairs={{0,2},{2,0},{4,6},{6,4},{8,10},{10,8},{12,14},{14,12},{1,3},{3,1},... | collective-permute-start | bytes 442376 | tf_op jit(solution)/shard_map/ppermute | solution.py:509
  60.0 21.2 %collective-permute-start.6 = (bf16[2,144,256]{2,1,0:T(8,128)(2,1)S(1)}, bf16[2,144,256]{2,1,0:T(8,128)(2,1)S(1)}, u32[]{:S(2)}, u32[]{:S(2)}) collective-permute-start(bf16[2,144,256]{2,1,0:T(8,128)(2,1)S(1)} %copy-done.29), channel_id=1, source_target_pairs={{0,14},{2,4},{4,2},{6,8},{8,6},{10,12},{12,10},{14,0},{1,15},{3,5}... | collective-permute-start | bytes 442376 | tf_op jit(solution)/shard_map/ppermute | solution.py:510
  64.4 16.9 %collective-permute-start.7 = (bf16[16,256]{1,0:T(8,128)(2,1)}, bf16[16,256]{1,0:T(8,128)(2,1)S(1)}, u32[]{:S(2)}, u32[]{:S(2)}) collective-permute-start(bf16[16,256]{1,0:T(8,128)(2,1)} %get-tuple-element.60), channel_id=1, source_target_pairs={{0,2},{2,0},{4,6},{6,4},{8,10},{10,8},{12,14},{14,12},{1,3},{3,1},... | collective-permute-start | bytes 24584 | tf_op jit(solution)/shard_map/ppermute | solution.py:574
  81.3 1.3 copy-start.17
  103.0 20.4 %copy-start.3 = (bf16[1,6,3,24,256]{4,3,2,1,0:T(8,128)(2,1)S(1)}, bf16[1,6,3,24,256]{4,3,2,1,0:T(8,128)(2,1)}, u32[]{:S(2)}) copy-start(bf16[1,6,3,24,256]{4,3,2,1,0:T(8,128)(2,1)} %param.6) | copy-start | bytes 663556
  103.0 20.4 %copy-start.6 = (bf16[1,1,6,3,24,256]{5,4,3,2,1,0:T(8,128)(2,1)S(1)}, bf16[1,1,6,3,24,256]{5,4,3,2,1,0:T(8,128)(2,1)}, u32[]{:S(2)}) copy-start(bf16[1,1,6,3,24,256]{5,4,3,2,1,0:T(8,128)(2,1)} %param.7) | copy-start | bytes 663556
  103.0 20.4 %copy-start.10 = (bf16[9,256,256]{2,1,0:T(8,128)(2,1)S(1)}, bf16[9,256,256]{2,1,0:T(8,128)(2,1)}, u32[]{:S(2)}) copy-start(bf16[9,256,256]{2,1,0:T(8,128)(2,1)} %copy-done.9) | copy-start | bytes 3538948
  103.0 20.4 %copy-start.20 = (bf16[18,24,256]{2,1,0:T(8,128)(2,1)S(1)}, bf16[18,24,256]{2,1,0:T(8,128)(2,1)}, u32[]{:S(2)}) copy-start(bf16[18,24,256]{2,1,0:T(8,128)(2,1)} %copy-done.19) | copy-start | bytes 663556
  103.0 20.4 %copy-start.22 = (bf16[18,24,256]{2,1,0:T(8,128)(2,1)S(1)}, bf16[18,24,256]{2,1,0:T(8,128)(2,1)}, u32[]{:S(2)}) copy-start(bf16[18,24,256]{2,1,0:T(8,128)(2,1)} %copy-done.21) | copy-start | bytes 663556
  121.2 14.4 %collective-permute-start.8 = (bf16[4,288,256]{2,1,0:T(8,128)(2,1)S(1)}, bf16[4,288,256]{2,1,0:T(8,128)(2,1)S(1)}, u32[]{:S(2)}, u32[]{:S(2)}) collective-permute-start(bf16[4,288,256]{2,1,0:T(8,128)(2,1)S(1)} %all_to_all.21.a_ref), channel_id=1, source_target_pairs={{0,2},{2,0},{4,6},{6,4},{8,10},{10,8},{12,14},{14,12},{1,3},{3,1},... | collective-permute-start | bytes 1769480 | tf_op jit(solution)/shard_map/ppermute | solution.py:574
  129.3 6.3 %collective-permute-start.9 = (bf16[4,288,256]{2,1,0:T(8,128)(2,1)S(1)}, bf16[4,288,256]{2,1,0:T(8,128)(2,1)S(1)}, u32[]{:S(2)}, u32[]{:S(2)}) collective-permute-start(bf16[4,288,256]{2,1,0:T(8,128)(2,1)S(1)} %all_to_all.21.a_ref), channel_id=1, source_target_pairs={{0,1},{1,0},{2,3},{3,2},{4,5},{5,4},{6,7},{7,6},{8,9},{9,8},{10,11... | collective-permute-start | bytes 1769480 | tf_op jit(solution)/shard_map/ppermute | solution.py:516
  135.6 2.0 %collective-permute-start.10 = (bf16[4,288,256]{2,1,0:T(8,128)(2,1)S(1)}, bf16[4,288,256]{2,1,0:T(8,128)(2,1)S(1)}, u32[]{:S(2)}, u32[]{:S(2)}) collective-permute-start(bf16[4,288,256]{2,1,0:T(8,128)(2,1)S(1)} %collective-permute-done.8.b_ref), channel_id=1, source_target_pairs={{0,1},{1,0},{2,3},{3,2},{4,5},{5,4},{6,7},{7,6},{8,9},{9,8},{10,11... | collective-permute-start | bytes 1769480 | tf_op jit(solution)/shard_map/ppermute | solution.py:516

commit v6 on v5

--- a/solution.py
+++ b/solution.py
@@ -9,7 +9,6 @@
 
 BF = jnp.bfloat16
 F32 = jnp.float32
-EXTRA = 16
 LIMIT = 40
 
 
@@ -27,7 +26,19 @@
         self.S = self.WE + self.ROW
 
     def messages(self):
-        return [(self.T, 2, self.BASE, self.C), (2, self.ROW, self.C), (2, self.ROW, self.C)]
+        rows = [self.BASE] * self.T + [self.ROW]
+        rows[1] += self.ROW
+        return [(2, n, self.C) for n in rows]
+
+    def pairs(self):
+        T = self.T
+
+        def needed(i, d):
+            return i in (0, T - 1) or d in (0, T - 1) or d in (T - 2 - i, T - i)
+
+        out = [[(i, i ^ k) for i in range(T) if k in (1, T - 1) or needed(i, i ^ k)] for k in range(T)]
+        out.append([(i, (i + 1) % T if i % 2 else (i - 1) % T) for i in range(T)])
+        return out
 
 
 def col_iota(n):
@@ -80,18 +91,16 @@
 
 
 def write_messages(dm, ep, t, sources, refs):
-    R, T = dm.R, dm.T
-    strips_ref, pair_ref, ring_ref = refs
-
-    def pick(parts, which):
+    R = dm.R
+    for k in range(dm.T + 1):
+        parts = strip_targets(dm, ep, t, t ^ k) if k < dm.T else []
+        if k == 1:
+            parts = parts + row_targets(dm, jnp.where(t % 2 == 0, R - 1, 0))
+        if k == dm.T:
+            parts = row_targets(dm, jnp.where(t % 2 == 1, R - 1, 0))
         hot = one_hot(jnp.concatenate(parts, axis=0), dm.N)
-        return jnp.dot(hot, sources[which], preferred_element_type=F32).astype(BF)
-
-    for which in range(2):
-        for d in range(T):
-            strips_ref[d, which] = pick(strip_targets(dm, ep, t, d), which)
-        pair_ref[which] = pick(row_targets(dm, jnp.where(t % 2 == 0, R - 1, 0)), which)
-        ring_ref[which] = pick(row_targets(dm, jnp.where(t % 2 == 1, R - 1, 0)), which)
+        for which in range(2):
+            refs[k][which] = jnp.dot(hot, sources[which], preferred_element_type=F32).astype(BF)
 
 
 def pack_kernel(dm, ep, x_ref, up_ref, *refs):
@@ -107,9 +116,9 @@
     inside = (q >= 0) & (q < F) & (m < R + 2)
     row_prev = dm.o_row + (1 - odd) * dm.ROW
     row_next = dm.o_row + odd * dm.ROW
-    side_first = dm.o_msg + (T - t) * dm.BASE + jnp.where(t == 1, R + 2, 0)
-    side_last = dm.o_msg + (T - 2 - t) * dm.BASE + jnp.where(t == T - 2, R + 2, 0)
-    mirror = dm.o_msg + (T - 1 - t) * dm.BASE
+    side_first = dm.o_msg + (t ^ (T - t)) * dm.BASE + jnp.where(t == 1, R + 2, 0)
+    side_last = dm.o_msg + (t ^ (T - 2 - t)) * dm.BASE + jnp.where(t == T - 2, R + 2, 0)
+    mirror = dm.o_msg + (T - 1) * dm.BASE
     for f in range(6):
         for edge in (3, 1):
             value = ep[f, edge]
@@ -120,7 +129,7 @@
             side = jnp.where(e2 == 1, 1, 0)
             column = side * (F - 1)
             slot = f2 * dm.SLOT + side
-            row = dm.o_msg + jnp.where(e2 == 0, 0, T - 1) * dm.BASE + f2 * dm.SLOT
+            row = dm.o_msg + (t ^ jnp.where(e2 == 0, 0, T - 1)) * dm.BASE + f2 * dm.SLOT
             facing = jnp.where(e2 == 0, t == T - 1, t == 0)
             whole = dm.o_row + dm.ROW + f2 * F + jnp.where(reverse, F - R * t, R * t - 1)
             row = jnp.where(facing, whole, row)
@@ -157,6 +166,9 @@
             lin_step = jnp.where(reverse, -1, 1)
             k0 = jnp.where(reverse, T - 1, 0)
             ks = jnp.where(reverse, -1, 1)
+            if edge == 2:
+                k0 = T - 1 - k0
+                ks = -ks
             col_base = dm.o_msg + k0 * dm.BASE + f * dm.SLOT + R + 2 + jnp.where(reverse, R - 1, 0)
             base = jnp.where(is_col, col_base, lin_base)
             sj = jnp.where(is_col, 0, lin_step)
@@ -182,9 +194,9 @@
         table_ref[0 : dm.N] = own[which]
         for k in range(dm.T):
             at = dm.o_msg + k * dm.BASE
-            table_ref[at : at + dm.BASE] = messages[0][k, which]
-        table_ref[dm.o_row : dm.o_row + dm.ROW] = messages[1][which]
-        table_ref[dm.o_row + dm.ROW :] = messages[2][which]
+            table_ref[at : at + dm.BASE] = messages[k][which, : dm.BASE]
+        table_ref[dm.o_row : dm.o_row + dm.ROW] = messages[1][which, dm.BASE :]
+        table_ref[dm.o_row + dm.ROW :] = messages[dm.T][which]
         out.append(jnp.dot(hot, table_ref[...], preferred_element_type=F32))
     return out
 
@@ -300,25 +312,20 @@
         w1s_ref[tap, half:] = w1_ref[tap, pl.ds(pl.multiple_of((1 - p) * half, half), half)]
 
 
-def put_taps(send_ref, keep_ref, which, taps, value):
-    half = value.shape[0] // (2 * len(taps))
-    for i, tap in enumerate(taps):
-        keep_ref[which, tap] = value[2 * i * half : (2 * i + 1) * half]
-        send_ref[which, tap] = value[(2 * i + 1) * half : (2 * i + 2) * half].astype(BF)
-
-
-def high_low(row):
-    i = lax.broadcasted_iota(jnp.int32, (EXTRA, row.shape[1]), 0)
-    high = row.astype(BF).astype(F32)
-    return jnp.where(i == 0, high, jnp.where(i == 1, row - high, 0.0)).astype(BF)
+def put_taps(send_ref, keep_ref, first_tap, value):
+    half = keep_ref.shape[1]
+    for i in range(value.shape[0] // (2 * half)):
+        keep_ref[first_tap + i] = value[2 * i * half : (2 * i + 1) * half]
+        send_ref[first_tap + i] = value[(2 * i + 1) * half : (2 * i + 2) * half].astype(BF)
 
 
 def first_kernel(dm, ep, x_ref, up_ref, w1_ref, bias_ref, w2t_ref, *refs):
     T, R, F, N, C = dm.T, dm.R, dm.F, dm.N, dm.C
-    messages = refs[:3]
-    send_ref, send_bias_ref, keep_ref, bias_sum_ref, hid_ref, inner_ref = refs[3:9]
-    out_messages = refs[9:12]
-    table_ref, frame_ref, xs_ref, us_ref, z_ref, before_ref, acc_ref, hcat_ref = refs[12:]
+    M = T + 1
+    messages = refs[:M]
+    send1_ref, keep1_ref, send2_ref, keep2_ref, bias_sum_ref, hid_ref, inner_ref = refs[M : M + 7]
+    out_messages = refs[M + 7 : 2 * M + 7]
+    table_ref, frame_ref, xs_ref, us_ref, z_ref, before_ref, acc_ref, hcat_ref = refs[2 * M + 7 :]
     t, p = lax.axis_index("tile"), lax.axis_index("dp")
     own = (x_ref[...].reshape(N, C), up_ref[...].reshape(N, C))
     gx, gu = gather_ghosts(dm, ep, t, own, messages, table_ref)
@@ -351,23 +358,21 @@
     hidden_t = own_first(hcat_ref[...], p).astype(BF).T
     for tap in range(9):
         grad = jnp.dot(hidden_t, us_ref[:, tap * C : (tap + 1) * C], preferred_element_type=F32)
-        put_taps(send_ref, keep_ref, 0, [tap], grad)
+        put_taps(send2_ref, keep2_ref, tap, grad)
     before = before_ref[...]
     sig = 1.0 / (1.0 + jnp.exp(-before))
     before_grad = acc_ref[...] * (sig * (1.0 + before * (1.0 - sig)))
     acc_ref[...] = before_grad
     inner = before_grad.astype(BF)
-    for taps in ((0, 1, 2), (3, 4, 5), (6, 7, 8)):
+    for tap in (0, 3, 6):
         grad = lax.dot_general(
-            xs_ref[:, taps[0] * C : (taps[-1] + 1) * C],
+            xs_ref[:, tap * C : (tap + 3) * C],
             inner,
             (((0,), (0,)), ((), ())),
             preferred_element_type=F32,
         )
-        put_taps(send_ref, keep_ref, 1, taps, grad)
-    bias_sum = jnp.sum(before_grad, axis=0, keepdims=True)
-    bias_sum_ref[...] = bias_sum
-    send_bias_ref[...] = high_low(bias_sum)
+        put_taps(send1_ref, keep1_ref, tap, grad)
+    bias_sum_ref[...] = jnp.sum(before_grad, axis=0, keepdims=True)
     for r in range(R):
         for f in range(6):
             at = (r * 6 + f) * F
@@ -379,9 +384,9 @@
 
 def second_kernel(dm, ep, x_ref, d_ref, hid_ref, inner_ref, w1t_ref, w2_ref, *refs):
     T, R, F, N, C = dm.T, dm.R, dm.F, dm.N, dm.C
-    messages = refs[:3]
-    state_ref, grad_ref = refs[3:5]
-    table_ref, frame_ref, hs_ref, is_ref, z_ref, acc_ref = refs[5:]
+    messages = refs[: T + 1]
+    state_ref, grad_ref = refs[T + 1 : T + 3]
+    table_ref, frame_ref, hs_ref, is_ref, z_ref, acc_ref = refs[T + 3 :]
     t = lax.axis_index("tile")
     own = (hid_ref[...].reshape(N, C), inner_ref[...].reshape(N, C))
     gh, gi = gather_ghosts(dm, ep, t, own, messages, table_ref)
@@ -404,81 +409,58 @@
             grad_ref[f * R + r] = d_ref[f * R + r].astype(F32) + acc_ref[at : at + F]
 
 
-def both(pair):
-    return pair[0:1].astype(F32) + pair[1:2].astype(F32)
-
-
-def half_kernel(keep_ref, bias_ref, recv_ref, recv_bias_ref, out_keep, out_bias, out_send, out_send_bias):
-    size = keep_ref.shape[2] // 2
+def half_kernel(zcount, keep2_ref, keep1_ref, recv2_ref, recv1_ref, out_keep, *out_sends):
+    size = keep1_ref.shape[1] // 2
     own = lax.axis_index("tile") % 2
     mine = pl.ds(pl.multiple_of(own * size, size), size)
     far = pl.ds(pl.multiple_of((1 - own) * size, size), size)
-    for which in range(2):
+    part = size // zcount
+    for which, (keep_ref, recv_ref) in enumerate(((keep2_ref, recv2_ref), (keep1_ref, recv1_ref))):
         for tap in range(9):
-            out_keep[which, tap] = keep_ref[which, tap, mine] + recv_ref[which, tap, mine].astype(F32)
-            out = keep_ref[which, tap, far] + recv_ref[which, tap, far].astype(F32)
-            out_send[which, tap] = out.astype(BF)
-    bias = bias_ref[...] + both(recv_bias_ref)
-    out_bias[...] = bias
-    out_send_bias[...] = high_low(bias)
-
-
-def block_kernel(zcount, keep_ref, bias_ref, recv_ref, recv_bias_ref, out_keep, out_bias, out_sends):
-    size = keep_ref.shape[2] // zcount
+            kept = keep_ref[tap, mine] + recv_ref[tap, mine].astype(F32)
+            sent = keep_ref[tap, far] + recv_ref[tap, far].astype(F32)
+            at = (9 * which + tap) * part
+            for j in range(zcount):
+                out_keep[j, at : at + part] = kept[j * part : (j + 1) * part]
+                out_sends[j][at : at + part] = sent[j * part : (j + 1) * part].astype(BF)
+
+
+def block_kernel(zcount, keep_ref, *refs):
+    recvs, (out_keep, *out_sends), sum_ref = refs[:zcount], refs[zcount : 2 * zcount], refs[2 * zcount]
     own = lax.axis_index("tile") // 2
-    bias = bias_ref[...] + both(recv_bias_ref)
-    out_bias[...] = bias
-    tail = high_low(bias)
     for j in range(zcount):
-        rows = slice(j * size, (j + 1) * size)
-        for which in range(2):
-            for tap in range(9):
-                total = keep_ref[which, tap, rows] + recv_ref[which, tap, rows].astype(F32)
-                at = (9 * which + tap) * size
-                out_sends[j, at : at + size] = total.astype(BF)
-        out_sends[j, 18 * size :] = tail
-    mine = pl.ds(pl.multiple_of(own * size, size), size)
-    for which in range(2):
-        for tap in range(9):
-            at = (9 * which + tap) * size
-            out_keep[at : at + size] = keep_ref[which, tap, mine] + recv_ref[which, tap, mine].astype(F32)
-
-
-def last_kernel(zcount, keep_ref, bias_ref, recv_ref, block_ref, bias_sum_ref):
-    n = keep_ref.shape[0]
-    own = lax.axis_index("tile") // 2
+        sum_ref[j] = keep_ref[j] + recvs[j][...].astype(F32)
+    out_keep[...] = sum_ref[own]
+    for j in range(1, zcount):
+        out_sends[j - 1][...] = sum_ref[own ^ j].astype(BF)
+
+
+def last_kernel(keep_ref, *refs):
     total = keep_ref[...]
-    bias = bias_ref[...]
-    for j in range(zcount):
-        far = own != j
-        total = total + jnp.where(far, recv_ref[j, 0:n].astype(F32), 0.0)
-        bias = bias + jnp.where(far, both(recv_ref[j, n : n + 2]), 0.0)
-    for j in range(zcount):
-        block_ref[j] = total.astype(BF)
-    bias_sum_ref[...] = bias
-
-
-def normal_kernel(zcount, a_ref, b_ref, c_ref, d_ref, bias_sum_ref, second_ref, first_ref, bias_ref):
+    for ref in refs[:-1]:
+        total = total + ref[...].astype(F32)
+    refs[-1][...] = total.astype(BF)
+
+
+def normal_kernel(zcount, bias_sum_ref, *refs):
+    blocks, (second_ref, first_ref, bias_ref) = refs[: 4 * zcount], refs[4 * zcount :]
     t, p = lax.axis_index("tile"), lax.axis_index("dp")
-    refs = (a_ref, b_ref, c_ref, d_ref)
-    size = a_ref.shape[1] // 18
+    n = blocks[0].shape[0] // 2
+    size = n // 9
     for which, out_ref in enumerate((second_ref, first_ref)):
-        rows = slice(which * 9 * size, (which + 1) * 9 * size)
         square = None
-        for ref in refs:
-            for j in range(zcount):
-                v = ref[j, rows].astype(F32)
-                s = jnp.sum(v * v, axis=0, keepdims=True)
-                square = s if square is None else square + s
+        for ref in blocks:
+            v = ref[which * n : (which + 1) * n].astype(F32)
+            square = v * v if square is None else square + v * v
         mean = jnp.sum(square, keepdims=True) / (9 * out_ref.shape[1] * out_ref.shape[2])
         scale = lax.rsqrt(mean + 1e-06)
-        for index, ref in enumerate(refs):
-            block = (p ^ (index // 2)) * 2 + ((t % 2) ^ (index % 2))
-            for j in range(zcount):
-                at = pl.ds(pl.multiple_of((block * zcount + j) * size, size), size)
-                for tap in range(9):
-                    row = (9 * which + tap) * size
-                    out_ref[tap, at] = ref[j, row : row + size].astype(F32) * scale
+        for index, ref in enumerate(blocks):
+            group, j = index // zcount, index % zcount
+            block = (p ^ (group // 2)) * 2 + ((t % 2) ^ (group % 2))
+            at = pl.ds(pl.multiple_of((block * zcount + ((t // 2) ^ j)) * size, size), size)
+            for tap in range(9):
+                row = which * n + tap * size
+                out_ref[tap, at] = ref[row : row + size].astype(F32) * scale
     total = bias_sum_ref[...]
     bias_mean = jnp.mean(total * total, keepdims=True)
     bias_ref[...] = total * lax.rsqrt(bias_mean + 1e-06)
@@ -499,16 +481,6 @@
         )(*args)
 
     return run
-
-
-def exchange(tiles, messages):
-    strips, pair, ring = messages
-    other = [(i, (i + 1) % tiles if i % 2 else (i - 1) % tiles) for i in range(tiles)]
-    return [
-        lax.all_to_all(strips, "tile", 0, 0),
-        lax.ppermute(pair, "tile", [(i, i ^ 1) for i in range(tiles)]),
-        lax.ppermute(ring, "tile", other),
-    ]
 
 
 def swap_dp(v):
@@ -535,16 +507,22 @@
     messages = call(functools.partial(pack_kernel, dm), msg_shapes, smem_first=True)(
         edge_partner, x.reshape(flat), d.reshape(flat)
     )
-    messages = exchange(tiles, messages)
+    pairs = dm.pairs()
+
+    def send_message(messages, k):
+        return messages[k] if k == 0 else lax.ppermute(messages[k], "tile", pairs[k])
+
+    messages = [send_message(messages, k) for k in range(tiles + 1)]
     half = channels // 2
     wide = 9 * channels
     frame = (rows + 2, 6, face + 16, channels)
     outs = call(
         functools.partial(first_kernel, dm),
         [
-            ((2, 9, half, channels), BF),
-            ((EXTRA, channels), BF),
-            ((2, 9, half, channels), F32),
+            ((9, half, channels), BF),
+            ((9, half, channels), F32),
+            ((9, half, channels), BF),
+            ((9, half, channels), F32),
             ((1, channels), F32),
             (planes, BF),
             (planes, BF),
@@ -563,41 +541,56 @@
         smem_first=True,
         limit=LIMIT,
     )(edge_partner, x, d, w1s, bias.reshape(1, channels), w2t, *messages)
-    send, send_bias, keep, bias_sum, hidden, inner = outs[:6]
+    send1, keep1, send2, keep2, bias_sum, hidden, inner = outs[:7]
+    packed = list(outs[7:])
+    bias_sum = lax.psum(bias_sum, ("tile", "dp"))
 
     zcount = tiles // 2
-    n = half // 2
-    m = n // zcount
-    groups = [[h + 2 * z for z in range(zcount)] for h in range(2)]
+    block = (18 * half // tiles, channels)
+    barrier = lax.optimization_barrier
 
     def along_y(v):
         return lax.ppermute(v, "tile", [(i, i ^ 1) for i in range(tiles)])
 
-    def along_z(v):
-        return lax.all_to_all(v, "tile", 0, 0, axis_index_groups=groups)
-
-    keep, bias_sum, send, send_bias = call(
-        half_kernel,
-        [
-            ((2, 9, n, channels), F32),
-            ((1, channels), F32),
-            ((2, 9, n, channels), BF),
-            ((EXTRA, channels), BF),
-        ],
-    )(keep, bias_sum, swap_dp(send), swap_dp(send_bias))
-    recv, recv_bias = along_y(send), along_y(send_bias)
-    messages = exchange(tiles, outs[6:])
-    recv, messages = lax.optimization_barrier((recv, messages))
-    keep, bias_sum, sends = call(
+    def along_z(v, j):
+        return lax.ppermute(v, "tile", [(i, i ^ (2 * j)) for i in range(tiles)])
+
+    early = [k for k in range(2, tiles - 1) if k % 2 == 0]
+    middle = [k for k in range(1, tiles - 1) if k % 2 == 1]
+    late = [tiles - 1, tiles]
+    messages = list(packed)
+
+    keep, *sends = call(
+        functools.partial(half_kernel, zcount), [((zcount,) + block, F32)] + [(block, BF)] * zcount
+    )(keep2, keep1, swap_dp(send2), swap_dp(send1))
+    recvs = [along_y(v) for v in sends]
+    got = [send_message(packed, k) for k in early]
+    recvs, got = barrier((recvs, got))
+    for k, v in zip(early, got):
+        messages[k] = v
+
+    keep, *sends = call(
         functools.partial(block_kernel, zcount),
-        [((18 * m, channels), F32), ((1, channels), F32), ((zcount, 18 * m + EXTRA, channels), BF)],
-    )(keep, bias_sum, recv, recv_bias)
-    blocks, bias_sum = call(
-        functools.partial(last_kernel, zcount), [((zcount, 18 * m, channels), BF), ((1, channels), F32)]
-    )(keep, bias_sum, along_z(sends))
-    own = along_z(blocks)
-    other = along_y(own)
-    messages, _ = lax.optimization_barrier((messages, own))
+        [(block, F32)] + [(block, BF)] * (zcount - 1),
+        [((zcount,) + block, F32)],
+    )(keep, *recvs)
+    sends, todo = barrier((sends, [packed[k] for k in middle]))
+    recvs = [along_z(v, j + 1) for j, v in enumerate(sends)]
+    got = [lax.ppermute(v, "tile", pairs[k]) for k, v in zip(middle, todo)]
+    recvs, got = barrier((recvs, got))
+    for k, v in zip(middle, got):
+        messages[k] = v
+
+    (own,) = call(last_kernel, [(block, BF)])(keep, *recvs)
+    own, todo = barrier((own, [packed[k] for k in late]))
+    own = [own] + [along_z(own, j) for j in range(1, zcount)]
+    got = [lax.ppermute(v, "tile", pairs[k]) for k, v in zip(late, todo)]
+    own[-1], got = barrier((own[-1], got))
+    for k, v in zip(late, got):
+        messages[k] = v
+    other = [along_y(v) for v in own]
+    blocks = own + other
+    blocks = blocks + [swap_dp(v) for v in blocks]
     state, grad = call(
         functools.partial(second_kernel, dm),
         [(planes, BF), (planes, F32)],
@@ -612,12 +605,11 @@
         smem_first=True,
         limit=LIMIT,
     )(edge_partner, x, d, hidden, inner, w1t, w2, *messages)
-    other, state, grad = lax.optimization_barrier((other, state, grad))
     second_step, first_step, bias_step = call(
         functools.partial(normal_kernel, zcount),
         [(taps, F32)] * 2 + [((1, channels), F32)],
         limit=24,
-    )(own, other, swap_dp(own), swap_dp(other), bias_sum)
+    )(bias_sum, *blocks)
     return (
         state.reshape(initial_state.shape),
         grad.reshape(initial_state.shape),

time: 141 us -> 160 us (1.13)
  starting transfers between devices: 25.8 us -> 51.6 us
  blocking collectives: 38.4 us -> 32.1 us
  waiting for transfers between devices: 29.8 us -> 33.8 us
  local copies, waits for them, and re-layouts: 22.7 us -> 19.1 us
    all_to_all x2 -> x0, blocking collectives: 38.4 us -> none  [along_z(): return lax.all_to_all(v, 'tile', 0, 0, axis_index_groups=groups)]
    psum x0 -> x1, blocking collectives: none -> 32.1 us  [on_device(): bias_sum = lax.psum(bias_sum, ('tile', 'dp'))]
    ppermute x4 -> x22, starting transfers between devices: 10 us -> 39.6 us  [the longest x11 25.1 us: send_message(): lax.ppermute(messages[k], 'tile', pairs[k])]
    all_to_all x2 -> x0, starting transfers between devices: 11.4 us -> none  [exchange(): lax.all_to_all(strips, 'tile', 0, 0)]
    ppermute x4 -> x22, waiting for transfers between devices: 20.3 us -> 28 us  [the longest x3 13.2 us: on_device(): got = [lax.ppermute(v, 'tile', pairs[k]) for k, v in zip(middle, todo)]]
    ppermute x3 -> x8, starting transfers between devices: 3.78 us -> 10.9 us  [along_y(): return lax.ppermute(v, 'tile', [(i, i ^ 1) for i in range(tiles)])]
    unnamed x67 -> x73, local copies, waits for them, and re-layouts: 22.7 us -> 19.1 us
    ppermute x4 -> x10, waiting for transfers between devices: 3.04 us -> 0.03 us  [swap_dp(): return lax.ppermute(v, 'dp', [(i, count - 1 - i) for i in range(count)])]
  transfers between devices with their start and end apart: 13 -> 40, of which waited for: 7 -> 11; matrix products, arithmetic and copies ran while one was open for 0% -> 0% of each run, Pallas kernels for 6% -> 4%
where the time goes in v6:
time: 160 us; the launch traced here: 159 us
  starting transfers between devices  51.6 us (32%)
  waiting for transfers between devices  33.8 us (21%)
  blocking collectives  32.1 us (20%)
  Pallas kernels  21.3 us (13%)
  local copies, waits for them, and re-layouts  19.1 us (12%)
    psum x1, blocking collectives, on_device(): bias_sum = lax.psum(bias_sum, ('tile', 'dp'))  32.1 us
    ppermute x11, starting transfers between devices, send_message(): lax.ppermute(messages[k], 'tile', pairs[k])  25.1 us
    pallas_call x8, Pallas kernels, run(): pl.pallas_call(kernel, out_shape=[jax.ShapeDtypeStruct(s, dt) for s, dt i...  21.3 us
    unnamed x73, local copies, waits for them, and re-layouts  19.1 us
    ppermute x3, waiting for transfers between devices, on_device(): got = [lax.ppermute(v, 'tile', pairs[k]) for k, v in zip(middle, todo)]  13.2 us
    ppermute x8, starting transfers between devices, along_y(): return lax.ppermute(v, 'tile', [(i, i ^ 1) for i in range(tiles)])  10.9 us
    ppermute x11, waiting for transfers between devices, send_message(): lax.ppermute(messages[k], 'tile', pairs[k])  9.51 us
    ppermute x8, waiting for transfers between devices, along_y(): return lax.ppermute(v, 'tile', [(i, i ^ 1) for i in range(tiles)])  5.76 us
  transfers between devices with their start and end apart: 40, of which 11 were waited for; matrix products, arithmetic and copies ran while one was open for 0% of the time, Pallas kernels for 4%

profile of v6, /device:TPU:0, one launch (start us, length us, event | category | flops | bytes accessed | tf_op | source)
XLA Modules:
  0.0 158.9 jit_solution(13493498501051849555)
XLA Ops:
  0.6 0.8 copy.13.ep
  1.4 0.9 copy-done.2
  2.3 0.9 copy-done.4
  3.3 2.1 %shard_map.102 = (bf16[2,48,256]{2,1,0:T(8,128)(2,1)S(1)}, bf16[2,192,256]{2,1,0:T(8,128)(2,1)S(1)}, bf16[2,48,256]{2,1,0:T(8,128)(2,1)S(1)}, bf16[2,48,256]{2,1...) custom-call(s32[6,4]{1,0:T(8,128)S(1)} %copy.13.ep, ...), custom_call_target="tpu_custom_call" | custom-call | tf_op jit(solution)/shard_map/pallas_call | solution.py:474
  5.4 3.0 %collective-permute-start = (bf16[2,192,256]{2,1,0:T(8,128)(2,1)S(1)}, bf16[2,192,256]{2,1,0:T(8,128)(2,1)S(1)}, u32[]{:S(2)}, u32[]{:S(2)}) collective-permute-start(bf16[2,192,256]{2,1,0:T(8,128)(2,1)S(1)} %get-tuple-element.75), channel_id=1, source_target_pairs={{0,2},{2,0},{4,6},{6,4},{8,10},{10,8},{12,14},{14,12},{1,3},{3,1},... | collective-permute-start | bytes 589832 | tf_op jit(solution)/shard_map/ppermute | solution.py:513
  8.4 3.5 %collective-permute-start.7 = (bf16[2,144,256]{2,1,0:T(8,128)(2,1)S(1)}, bf16[2,144,256]{2,1,0:T(8,128)(2,1)S(1)}, u32[]{:S(2)}, u32[]{:S(2)}) collective-permute-start(bf16[2,144,256]{2,1,0:T(8,128)(2,1)S(1)} %get-tuple-element.82), channel_id=1, source_target_pairs={{0,14},{2,4},{4,2},{6,8},{8,6},{10,12},{12,10},{14,0},{1,15},{3,5}... | collective-permute-start | bytes 442376 | tf_op jit(solution)/shard_map/ppermute | solution.py:513
  12.0 1.9 %collective-permute-start.1 = (bf16[2,48,256]{2,1,0:T(8,128)(2,1)S(1)}, bf16[2,48,256]{2,1,0:T(8,128)(2,1)S(1)}, u32[]{:S(2)}, u32[]{:S(2)}) collective-permute-start(bf16[2,48,256]{2,1,0:T(8,128)(2,1)S(1)} %get-tuple-element.76), channel_id=1, source_target_pairs={{0,4},{4,0},{10,14},{14,10},{1,5},{5,1},{11,15},{15,11},{16,20},{2... | collective-permute-start | bytes 147464 | tf_op jit(solution)/shard_map/ppermute | solution.py:513
  13.9 1.9 %collective-permute-start.2 = (bf16[2,48,256]{2,1,0:T(8,128)(2,1)S(1)}, bf16[2,48,256]{2,1,0:T(8,128)(2,1)S(1)}, u32[]{:S(2)}, u32[]{:S(2)}) collective-permute-start(bf16[2,48,256]{2,1,0:T(8,128)(2,1)S(1)} %get-tuple-element.77), channel_id=1, source_target_pairs={{0,6},{6,0},{8,14},{14,8},{1,7},{7,1},{9,15},{15,9},{16,22},{22,16... | collective-permute-start | bytes 147464 | tf_op jit(solution)/shard_map/ppermute | solution.py:513
  15.8 3.6 %collective-permute-start.3 = (bf16[2,48,256]{2,1,0:T(8,128)(2,1)S(1)}, bf16[2,48,256]{2,1,0:T(8,128)(2,1)S(1)}, u32[]{:S(2)}, u32[]{:S(2)}) collective-permute-start(bf16[2,48,256]{2,1,0:T(8,128)(2,1)S(1)} %get-tuple-element.78), channel_id=1, source_target_pairs={{0,8},{2,10},{4,12},{6,14},{8,0},{10,2},{12,4},{14,6},{1,9},{3,11}... | collective-permute-start | bytes 147464 | tf_op jit(solution)/shard_map/ppermute | solution.py:513
  19.4 2.2 %collective-permute-start.4 = (bf16[2,48,256]{2,1,0:T(8,128)(2,1)S(1)}, bf16[2,48,256]{2,1,0:T(8,128)(2,1)S(1)}, u32[]{:S(2)}, u32[]{:S(2)}) collective-permute-start(bf16[2,48,256]{2,1,0:T(8,128)(2,1)S(1)} %get-tuple-element.79), channel_id=1, source_target_pairs={{0,10},{4,14},{10,0},{14,4},{1,11},{5,15},{11,1},{15,5},{16,26},{2... | collective-permute-start | bytes 147464 | tf_op jit(solution)/shard_map/ppermute | solution.py:513
  21.8 2.2 %collective-permute-start.6 = (bf16[2,48,256]{2,1,0:T(8,128)(2,1)S(1)}, bf16[2,48,256]{2,1,0:T(8,128)(2,1)S(1)}, u32[]{:S(2)}, u32[]{:S(2)}) collective-permute-start(bf16[2,48,256]{2,1,0:T(8,128)(2,1)S(1)} %get-tuple-element.81), channel_id=1, source_target_pairs={{0,14},{2,12},{4,10},{6,8},{8,6},{10,4},{12,2},{14,0},{1,15},{3,13... | collective-permute-start | bytes 147464 | tf_op jit(solution)/shard_map/ppermute | solution.py:513
  24.0 1.3 copy-done
  25.3 1.3 copy-done.6
  26.5 0.7 shard_map.101
  27.2 0.7 collective-permute-done.4.refs_5_
  28.0 0.8 collective-permute-done.6.refs_7_
  28.8 8.2 %shard_map.103 = (bf16[9,128,256]{2,1,0:T(8,128)(2,1)S(1)}, f32[9,128,256]{2,1,0:T(8,128)S(1)}, bf16[9,128,256]{2,1,0:T(8,128)(2,1)S(1)}, f32[9,128,256]{2,1,0:T...) custom-call(s32[6,4]{1,0:T(8,128)S(1)} %copy.13.ep, ...), custom_call_target="tpu_custom_call" | custom-call | tf_op jit(solution)/shard_map/pallas_call | solution.py:474
  37.5 3.2 %collective-permute-start.14 = (bf16[2,48,256]{2,1,0:T(8,128)(2,1)S(1)}, bf16[2,48,256]{2,1,0:T(8,128)(2,1)S(1)}, u32[]{:S(2)}, u32[]{:S(2)}) collective-permute-start(bf16[2,48,256]{2,1,0:T(8,128)(2,1)S(1)} %get-tuple-element.96), channel_id=1, source_target_pairs={{0,4},{4,0},{10,14},{14,10},{1,5},{5,1},{11,15},{15,11},{16,20},{2... | collective-permute-start | bytes 147464 | tf_op jit(solution)/shard_map/ppermute | solution.py:513
  41.0 1.6 %collective-permute-start.10 = (bf16[288,256]{1,0:T(8,128)(2,1)S(1)}, bf16[288,256]{1,0:T(8,128)(2,1)S(1)}, u32[]{:S(2)}, u32[]{:S(2)}) collective-permute-start(bf16[288,256]{1,0:T(8,128)(2,1)S(1)} %get-tuple-element.92), channel_id=1, source_target_pairs={{0,2},{2,0},{4,6},{6,4},{8,10},{10,8},{12,14},{14,12},{1,3},{3,1},... | collective-permute-start | bytes 442376 | tf_op jit(solution)/shard_map/ppermute | solution.py:553
  43.1 1.6 collective-permute-start.12
  45.1 1.0 collective-permute-start.15
  46.1 4.5 %collective-permute-done.15.refs_4_ = bf16[2,48,256]{2,1,0:T(8,128)(2,1)S(1)} collective-permute-done((bf16[2,48,256]{2,1,0:T(8,128)(2,1)S(1)}, bf16[2,48,256]{2,1,0:T(8,128)(2,1)S(1)}, u32[]{:S(2)}, u32[]{:S(2)}) %collective-permute-start.15) | collective-permute-done | bytes 49184 | tf_op jit(solution)/shard_map/ppermute | solution.py:513
  50.6 2.4 %collective-permute-start.16 = (bf16[2,48,256]{2,1,0:T(8,128)(2,1)S(1)}, bf16[2,48,256]{2,1,0:T(8,128)(2,1)S(1)}, u32[]{:S(2)}, u32[]{:S(2)}) collective-permute-start(bf16[2,48,256]{2,1,0:T(8,128)(2,1)S(1)} %get-tuple-element.98), channel_id=1, source_target_pairs={{0,12},{2,14},{4,8},{6,10},{8,4},{10,6},{12,0},{14,2},{1,13},{3,15... | collective-permute-start | bytes 147464 | tf_op jit(solution)/shard_map/ppermute | solution.py:513
  53.0 3.5 %collective-permute-done.16.refs_6_ = bf16[2,48,256]{2,1,0:T(8,128)(2,1)S(1)} collective-permute-done((bf16[2,48,256]{2,1,0:T(8,128)(2,1)S(1)}, bf16[2,48,256]{2,1,0:T(8,128)(2,1)S(1)}, u32[]{:S(2)}, u32[]{:S(2)}) %collective-permute-start.16) | collective-permute-done | bytes 49184 | tf_op jit(solution)/shard_map/ppermute | solution.py:513
  56.7 1.5 collective-permute-start.20
  58.3 2.1 %collective-permute-start.18 = (bf16[288,256]{1,0:T(8,128)(2,1)S(1)}, bf16[288,256]{1,0:T(8,128)(2,1)S(1)}, u32[]{:S(2)}, u32[]{:S(2)}) collective-permute-start(bf16[288,256]{1,0:T(8,128)(2,1)S(1)} %get-tuple-element.110), channel_id=1, source_target_pairs={{0,8},{2,10},{4,12},{6,14},{8,0},{10,2},{12,4},{14,6},{1,9},{3,11}... | collective-permute-start | bytes 442376 | tf_op jit(solution)/shard_map/ppermute | solution.py:556
  60.4 2.3 %collective-permute-start.19 = (bf16[288,256]{1,0:T(8,128)(2,1)S(1)}, bf16[288,256]{1,0:T(8,128)(2,1)S(1)}, u32[]{:S(2)}, u32[]{:S(2)}) collective-permute-start(bf16[288,256]{1,0:T(8,128)(2,1)S(1)} %get-tuple-element.111), channel_id=1, source_target_pairs={{0,12},{2,14},{4,8},{6,10},{8,4},{10,6},{12,0},{14,2},{1,13},{3,15... | collective-permute-start | bytes 442376 | tf_op jit(solution)/shard_map/ppermute | solution.py:556
  62.6 1.9 %collective-permute-start.21 = (bf16[2,48,256]{2,1,0:T(8,128)(2,1)S(1)}, bf16[2,48,256]{2,1,0:T(8,128)(2,1)S(1)}, u32[]{:S(2)}, u32[]{:S(2)}) collective-permute-start(bf16[2,48,256]{2,1,0:T(8,128)(2,1)S(1)} %get-tuple-element.113), channel_id=1, source_target_pairs={{0,6},{6,0},{8,14},{14,8},{1,7},{7,1},{9,15},{15,9},{16,22},{22,16... | collective-permute-start | bytes 147464 | tf_op jit(solution)/shard_map/ppermute | solution.py:579
  64.5 6.9 %collective-permute-done.21.refs_3_ = bf16[2,48,256]{2,1,0:T(8,128)(2,1)S(1)} collective-permute-done((bf16[2,48,256]{2,1,0:T(8,128)(2,1)S(1)}, bf16[2,48,256]{2,1,0:T(8,128)(2,1)S(1)}, u32[]{:S(2)}, u32[]{:S(2)}) %collective-permute-start.21) | collective-permute-done | bytes 49184 | tf_op jit(solution)/shard_map/ppermute | solution.py:579
  71.5 0.6 copy-done.29
  72.1 1.9 %collective-permute-start.22 = (bf16[2,48,256]{2,1,0:T(8,128)(2,1)S(1)}, bf16[2,48,256]{2,1,0:T(8,128)(2,1)S(1)}, u32[]{:S(2)}, u32[]{:S(2)}) collective-permute-start(bf16[2,48,256]{2,1,0:T(8,128)(2,1)S(1)} %get-tuple-element.114), channel_id=1, source_target_pairs={{0,10},{4,14},{10,0},{14,4},{1,11},{5,15},{11,1},{15,5},{16,26},{2... | collective-permute-start | bytes 147464 | tf_op jit(solution)/shard_map/ppermute | solution.py:579
  74.0 6.3 %collective-permute-done.22.refs_5_ = bf16[2,48,256]{2,1,0:T(8,128)(2,1)S(1)} collective-permute-done((bf16[2,48,256]{2,1,0:T(8,128)(2,1)S(1)}, bf16[2,48,256]{2,1,0:T(8,128)(2,1)S(1)}, u32[]{:S(2)}, u32[]{:S(2)}) %collective-permute-start.22) | collective-permute-done | bytes 49184 | tf_op jit(solution)/shard_map/ppermute | solution.py:579
  80.3 0.6 copy-done.31
  81.0 0.7 copy-done.7
  81.7 2.5 %collective-permute-start.25 = (bf16[2,144,256]{2,1,0:T(8,128)(2,1)S(1)}, bf16[2,144,256]{2,1,0:T(8,128)(2,1)S(1)}, u32[]{:S(2)}, u32[]{:S(2)}) collective-permute-start(bf16[2,144,256]{2,1,0:T(8,128)(2,1)S(1)} %get-tuple-element.129), channel_id=1, source_target_pairs={{0,14},{2,4},{4,2},{6,8},{8,6},{10,12},{12,10},{14,0},{1,15},{3,5}... | collective-permute-start | bytes 442376 | tf_op jit(solution)/shard_map/ppermute | solution.py:587
  84.2 2.3 %collective-permute-start.24 = (bf16[2,48,256]{2,1,0:T(8,128)(2,1)S(1)}, bf16[2,48,256]{2,1,0:T(8,128)(2,1)S(1)}, u32[]{:S(2)}, u32[]{:S(2)}) collective-permute-start(bf16[2,48,256]{2,1,0:T(8,128)(2,1)S(1)} %get-tuple-element.128), channel_id=1, source_target_pairs={{0,14},{2,12},{4,10},{6,8},{8,6},{10,4},{12,2},{14,0},{1,15},{3,13... | collective-permute-start | bytes 147464 | tf_op jit(solution)/shard_map/ppermute | solution.py:587
  86.5 3.0 %collective-permute-start.28 = (bf16[288,256]{1,0:T(8,128)(2,1)S(1)}, bf16[288,256]{1,0:T(8,128)(2,1)S(1)}, u32[]{:S(2)}, u32[]{:S(2)}) collective-permute-start(bf16[288,256]{1,0:T(8,128)(2,1)S(1)} %shard_map.106.refs_0_), channel_id=1, source_target_pairs={{0,2},{2,0},{4,6},{6,4},{8,10},{10,8},{12,14},{14,12},{1,3},{3,1},... | collective-permute-start | bytes 442376 | tf_op jit(solution)/shard_map/ppermute | solution.py:553
  89.5 2.1 %collective-permute-done.24.refs_7_ = bf16[2,48,256]{2,1,0:T(8,128)(2,1)S(1)} collective-permute-done((bf16[2,48,256]{2,1,0:T(8,128)(2,1)S(1)}, bf16[2,48,256]{2,1,0:T(8,128)(2,1)S(1)}, u32[]{:S(2)}, u32[]{:S(2)}) %collective-permute-start.24) | collective-permute-done | bytes 49184 | tf_op jit(solution)/shard_map/ppermute | solution.py:587
  91.6 0.6 copy-done.33
  92.2 0.7 copy-done.13
  92.9 0.6 collective-permute-done.23.refs_3_
  93.5 0.7 copy-done.9
  94.1 2.6 %collective-permute-done.27.refs_2_ = bf16[288,256]{1,0:T(8,128)(2,1)S(1)} collective-permute-done((bf16[288,256]{1,0:T(8,128)(2,1)S(1)}, bf16[288,256]{1,0:T(8,128)(2,1)S(1)}, u32[]{:S(2)}, u32[]{:S(2)}) %collective-permute-start.27) | collective-permute-done | bytes 147488 | tf_op jit(solution)/shard_map/ppermute | solution.py:556
  96.7 1.8 %collective-permute-start.30 = (bf16[288,256]{1,0:T(8,128)(2,1)S(1)}, bf16[288,256]{1,0:T(8,128)(2,1)}, u32[]{:S(2)}, u32[]{:S(2)}) collective-permute-start(bf16[288,256]{1,0:T(8,128)(2,1)S(1)} %collective-permute-done.27.refs_2_), channel_id=1, source_target_pairs={{0,2},{2,0},{4,6},{6,4},{8,10},{10,8},{12,14},{14,12},{1,3},{3,1},... | collective-permute-start | bytes 442376 | tf_op jit(solution)/shard_map/ppermute | solution.py:553
  98.5 0.7 copy-done.11
  99.4 0.7 copy-done.15
  100.1 1.8 %collective-permute-start.31 = (bf16[288,256]{1,0:T(8,128)(2,1)S(1)}, bf16[288,256]{1,0:T(8,128)(2,1)}, u32[]{:S(2)}, u32[]{:S(2)}) collective-permute-start(bf16[288,256]{1,0:T(8,128)(2,1)S(1)} %collective-permute-done.23.refs_3_), channel_id=1, source_target_pairs={{0,2},{2,0},{4,6},{6,4},{8,10},{10,8},{12,14},{14,12},{1,3},{3,1},... | collective-permute-start | bytes 442376 | tf_op jit(solution)/shard_map/ppermute | solution.py:553
  101.9 0.7 copy-done.17
  102.5 0.7 copy-done.19
  103.2 0.5 collective-permute-start.33
  103.7 2.9 %collective-permute-done.29.refs_5_ = bf16[288,256]{1,0:T(8,128)(2,1)} collective-permute-done((bf16[288,256]{1,0:T(8,128)(2,1)}, bf16[288,256]{1,0:T(8,128)(2,1)}, u32[]{:S(2)}, u32[]{:S(2)}) %collective-permute-start.29) | collective-permute-done | bytes 147488 | tf_op jit(solution)/shard_map/ppermute | solution.py:553
  106.6 2.8 %collective-permute-done.31.refs_7_ = bf16[288,256]{1,0:T(8,128)(2,1)} collective-permute-done((bf16[288,256]{1,0:T(8,128)(2,1)S(1)}, bf16[288,256]{1,0:T(8,128)(2,1)}, u32[]{:S(2)}, u32[]{:S(2)}) %collective-permute-start.31) | collective-permute-done | bytes 147488 | tf_op jit(solution)/shard_map/ppermute | solution.py:553
  109.4 32.1 %psum.7.bias_sum_ref = f32[1,256]{1,0:T(1,128)S(1)} all-reduce(f32[1,256]{1,0:T(1,128)S(1)} %get-tuple-element.134), channel_id=1, replica_groups=mesh['groups'=2,'tile'=8,'dp'=2] {'tile','dp'}, use_global_device_ids=true, to_apply=%region_0.0 | all-reduce | flops 256 | bytes 2048 | tf_op jit(solution)/shard_map/psum | solution.py:546
  141.6 0.9 copy-done.8
  142.5 0.9 copy-done.14
  143.4 0.8 copy-done.22
  144.2 0.8 copy-done.24
  145.0 0.8 copy-done.26
  145.8 0.8 copy-done.28
  146.6 0.8 copy-done.30
  147.4 0.8 copy-done.32
  148.2 0.8 copy-done.34
  149.0 5.5 %shard_map.107 = (bf16[18,24,256]{2,1,0:T(8,128)(2,1)}, f32[18,24,256]{2,1,0:T(8,128)}) custom-call(s32[6,4]{1,0:T(8,128)S(1)} %copy.13.ep, bf16[18,24,256]{2,1,0:T(8,128)(2,1)S(1)} %bitcast.20, bf16[18,24,256]{2,1,0:T(8,128)(2,1)S(1)} %bitcast.23, bf16[18,24,256]{2,1,0:T(8,128)(2,1)S(1)} %get-tuple-element.83.hid_ref, ...), custom_call_target="tpu_custom_call" | custom-call | tf_op jit(solution)/shard_map/pallas_call | solution.py:474
  154.6 4.3 %shard_map.108 = (f32[9,256,256]{2,1,0:T(8,128)}, f32[9,256,256]{2,1,0:T(8,128)}, f32[1,256]{1,0:T(1,128)}) custom-call(f32[1,256]{1,0:T(1,128)S(1)} %psum.7.bias_sum_ref, bf16[288,256]{1,0:T(8,128)(2,1)S(1)} %shard_map.106.refs_0_, bf16[288,256]{1,0:T(8,128)(2,1)} %collective-permute-done.26.refs_1_, bf16[288,256]{1,0:T(8,128)(2,1)S(1)} %copy-done.12, ...), custom_call_target="tpu_custom_call" | custom-call | tf_op jit(solution)/shard_map/pallas_call | solution.py:474
  (98 shorter events, 2.5 us)
Async XLA Ops:
  1.4 0.9 copy-start.2
  2.3 0.9 copy-start.4
  5.4 23.3 %collective-permute-start = (bf16[2,192,256]{2,1,0:T(8,128)(2,1)S(1)}, bf16[2,192,256]{2,1,0:T(8,128)(2,1)S(1)}, u32[]{:S(2)}, u32[]{:S(2)}) collective-permute-start(bf16[2,192,256]{2,1,0:T(8,128)(2,1)S(1)} %get-tuple-element.75), channel_id=1, source_target_pairs={{0,2},{2,0},{4,6},{6,4},{8,10},{10,8},{12,14},{14,12},{1,3},{3,1},... | collective-permute-start | bytes 589832 | tf_op jit(solution)/shard_map/ppermute | solution.py:513
  8.4 20.3 %collective-permute-start.7 = (bf16[2,144,256]{2,1,0:T(8,128)(2,1)S(1)}, bf16[2,144,256]{2,1,0:T(8,128)(2,1)S(1)}, u32[]{:S(2)}, u32[]{:S(2)}) collective-permute-start(bf16[2,144,256]{2,1,0:T(8,128)(2,1)S(1)} %get-tuple-element.82), channel_id=1, source_target_pairs={{0,14},{2,4},{4,2},{6,8},{8,6},{10,12},{12,10},{14,0},{1,15},{3,5}... | collective-permute-start | bytes 442376 | tf_op jit(solution)/shard_map/ppermute | solution.py:513
  12.0 7.4 %collective-permute-start.1 = (bf16[2,48,256]{2,1,0:T(8,128)(2,1)S(1)}, bf16[2,48,256]{2,1,0:T(8,128)(2,1)S(1)}, u32[]{:S(2)}, u32[]{:S(2)}) collective-permute-start(bf16[2,48,256]{2,1,0:T(8,128)(2,1)S(1)} %get-tuple-element.76), channel_id=1, source_target_pairs={{0,4},{4,0},{10,14},{14,10},{1,5},{5,1},{11,15},{15,11},{16,20},{2... | collective-permute-start | bytes 147464 | tf_op jit(solution)/shard_map/ppermute | solution.py:513
  13.9 7.8 %collective-permute-start.2 = (bf16[2,48,256]{2,1,0:T(8,128)(2,1)S(1)}, bf16[2,48,256]{2,1,0:T(8,128)(2,1)S(1)}, u32[]{:S(2)}, u32[]{:S(2)}) collective-permute-start(bf16[2,48,256]{2,1,0:T(8,128)(2,1)S(1)} %get-tuple-element.77), channel_id=1, source_target_pairs={{0,6},{6,0},{8,14},{14,8},{1,7},{7,1},{9,15},{15,9},{16,22},{22,16... | collective-permute-start | bytes 147464 | tf_op jit(solution)/shard_map/ppermute | solution.py:513
  15.8 5.9 %collective-permute-start.3 = (bf16[2,48,256]{2,1,0:T(8,128)(2,1)S(1)}, bf16[2,48,256]{2,1,0:T(8,128)(2,1)S(1)}, u32[]{:S(2)}, u32[]{:S(2)}) collective-permute-start(bf16[2,48,256]{2,1,0:T(8,128)(2,1)S(1)} %get-tuple-element.78), channel_id=1, source_target_pairs={{0,8},{2,10},{4,12},{6,14},{8,0},{10,2},{12,4},{14,6},{1,9},{3,11}... | collective-permute-start | bytes 147464 | tf_op jit(solution)/shard_map/ppermute | solution.py:513
  19.4 8.6 %collective-permute-start.4 = (bf16[2,48,256]{2,1,0:T(8,128)(2,1)S(1)}, bf16[2,48,256]{2,1,0:T(8,128)(2,1)S(1)}, u32[]{:S(2)}, u32[]{:S(2)}) collective-permute-start(bf16[2,48,256]{2,1,0:T(8,128)(2,1)S(1)} %get-tuple-element.79), channel_id=1, source_target_pairs={{0,10},{4,14},{10,0},{14,4},{1,11},{5,15},{11,1},{15,5},{16,26},{2... | collective-permute-start | bytes 147464 | tf_op jit(solution)/shard_map/ppermute | solution.py:513
  21.7 6.3 %collective-permute-start.5 = (bf16[2,48,256]{2,1,0:T(8,128)(2,1)S(1)}, bf16[2,48,256]{2,1,0:T(8,128)(2,1)S(1)}, u32[]{:S(2)}, u32[]{:S(2)}) collective-permute-start(bf16[2,48,256]{2,1,0:T(8,128)(2,1)S(1)} %get-tuple-element.80), channel_id=1, source_target_pairs={{0,12},{2,14},{4,8},{6,10},{8,4},{10,6},{12,0},{14,2},{1,13},{3,15... | collective-permute-start | bytes 147464 | tf_op jit(solution)/shard_map/ppermute | solution.py:513
  21.8 7.0 %collective-permute-start.6 = (bf16[2,48,256]{2,1,0:T(8,128)(2,1)S(1)}, bf16[2,48,256]{2,1,0:T(8,128)(2,1)S(1)}, u32[]{:S(2)}, u32[]{:S(2)}) collective-permute-start(bf16[2,48,256]{2,1,0:T(8,128)(2,1)S(1)} %get-tuple-element.81), channel_id=1, source_target_pairs={{0,14},{2,12},{4,10},{6,8},{8,6},{10,4},{12,2},{14,0},{1,15},{3,13... | collective-permute-start | bytes 147464 | tf_op jit(solution)/shard_map/ppermute | solution.py:513
  24.0 1.3 copy-start
  25.3 1.3 copy-start.6
  26.5 2.2 %copy-start.3 = (bf16[1,6,3,24,256]{4,3,2,1,0:T(8,128)(2,1)S(1)}, bf16[1,6,3,24,256]{4,3,2,1,0:T(8,128)(2,1)}, u32[]{:S(2)}) copy-start(bf16[1,6,3,24,256]{4,3,2,1,0:T(8,128)(2,1)} %param.6) | copy-start | bytes 663556
  26.5 2.2 %copy-start.5 = (bf16[1,1,6,3,24,256]{5,4,3,2,1,0:T(8,128)(2,1)S(1)}, bf16[1,1,6,3,24,256]{5,4,3,2,1,0:T(8,128)(2,1)}, u32[]{:S(2)}) copy-start(bf16[1,1,6,3,24,256]{5,4,3,2,1,0:T(8,128)(2,1)} %param.7) | copy-start | bytes 663556
  26.5 2.2 %copy-start.35 = (f32[256]{0:T(256)S(1)}, f32[256]{0:T(256)}, u32[]{:S(2)}) copy-start(f32[256]{0:T(256)} %param.9) | copy-start | bytes 3076
  36.9 4.0 %copy-start.21 = (bf16[2,48,256]{2,1,0:T(8,128)(2,1)}, bf16[2,48,256]{2,1,0:T(8,128)(2,1)S(1)}, u32[]{:S(2)}) copy-start(bf16[2,48,256]{2,1,0:T(8,128)(2,1)S(1)} %get-tuple-element.86.refs_0_) | copy-start | bytes 147460
  36.9 3.8 %collective-permute-start.8 = (bf16[9,128,256]{2,1,0:T(8,128)(2,1)S(1)}, bf16[9,128,256]{2,1,0:T(8,128)(2,1)S(1)}, u32[]{:S(2)}, u32[]{:S(2)}) collective-permute-start(bf16[9,128,256]{2,1,0:T(8,128)(2,1)S(1)} %get-tuple-element.89), channel_id=1, source_target_pairs={{0,1},{1,0},{2,3},{3,2},{4,5},{5,4},{6,7},{7,6},{8,9},{9,8},{10,11... | collective-permute-start | bytes 1769480 | tf_op jit(solution)/shard_map/ppermute | solution.py:488
  37.0 3.7 %collective-permute-start.9 = (bf16[9,128,256]{2,1,0:T(8,128)(2,1)S(1)}, bf16[9,128,256]{2,1,0:T(8,128)(2,1)S(1)}, u32[]{:S(2)}, u32[]{:S(2)}) collective-permute-start(bf16[9,128,256]{2,1,0:T(8,128)(2,1)S(1)} %get-tuple-element.90), channel_id=1, source_target_pairs={{0,1},{1,0},{2,3},{3,2},{4,5},{5,4},{6,7},{7,6},{8,9},{9,8},{10,11... | collective-permute-start | bytes 1769480 | tf_op jit(solution)/shard_map/ppermute | solution.py:488
  37.5 7.6 %collective-permute-start.14 = (bf16[2,48,256]{2,1,0:T(8,128)(2,1)S(1)}, bf16[2,48,256]{2,1,0:T(8,128)(2,1)S(1)}, u32[]{:S(2)}, u32[]{:S(2)}) collective-permute-start(bf16[2,48,256]{2,1,0:T(8,128)(2,1)S(1)} %get-tuple-element.96), channel_id=1, source_target_pairs={{0,4},{4,0},{10,14},{14,10},{1,5},{5,1},{11,15},{15,11},{16,20},{2... | collective-permute-start | bytes 147464 | tf_op jit(solution)/shard_map/ppermute | solution.py:513
  41.0 15.5 %collective-permute-start.10 = (bf16[288,256]{1,0:T(8,128)(2,1)S(1)}, bf16[288,256]{1,0:T(8,128)(2,1)S(1)}, u32[]{:S(2)}, u32[]{:S(2)}) collective-permute-start(bf16[288,256]{1,0:T(8,128)(2,1)S(1)} %get-tuple-element.92), channel_id=1, source_target_pairs={{0,2},{2,0},{4,6},{6,4},{8,10},{10,8},{12,14},{14,12},{1,3},{3,1},... | collective-permute-start | bytes 442376 | tf_op jit(solution)/shard_map/ppermute | solution.py:553
  42.6 13.9 %collective-permute-start.11 = (bf16[288,256]{1,0:T(8,128)(2,1)S(1)}, bf16[288,256]{1,0:T(8,128)(2,1)S(1)}, u32[]{:S(2)}, u32[]{:S(2)}) collective-permute-start(bf16[288,256]{1,0:T(8,128)(2,1)S(1)} %get-tuple-element.93), channel_id=1, source_target_pairs={{0,2},{2,0},{4,6},{6,4},{8,10},{10,8},{12,14},{14,12},{1,3},{3,1},... | collective-permute-start | bytes 442376 | tf_op jit(solution)/shard_map/ppermute | solution.py:553
  43.1 13.5 %collective-permute-start.12 = (bf16[288,256]{1,0:T(8,128)(2,1)S(1)}, bf16[288,256]{1,0:T(8,128)(2,1)S(1)}, u32[]{:S(2)}, u32[]{:S(2)}) collective-permute-start(bf16[288,256]{1,0:T(8,128)(2,1)S(1)} %get-tuple-element.94), channel_id=1, source_target_pairs={{0,2},{2,0},{4,6},{6,4},{8,10},{10,8},{12,14},{14,12},{1,3},{3,1},... | collective-permute-start | bytes 442376 | tf_op jit(solution)/shard_map/ppermute | solution.py:553
  44.7 11.9 %collective-permute-start.13 = (bf16[288,256]{1,0:T(8,128)(2,1)S(1)}, bf16[288,256]{1,0:T(8,128)(2,1)S(1)}, u32[]{:S(2)}, u32[]{:S(2)}) collective-permute-start(bf16[288,256]{1,0:T(8,128)(2,1)S(1)} %get-tuple-element.95), channel_id=1, source_target_pairs={{0,2},{2,0},{4,6},{6,4},{8,10},{10,8},{12,14},{14,12},{1,3},{3,1},... | collective-permute-start | bytes 442376 | tf_op jit(solution)/shard_map/ppermute | solution.py:553
  45.1 36.6 %copy-start.23 = (bf16[2,48,256]{2,1,0:T(8,128)(2,1)}, bf16[2,48,256]{2,1,0:T(8,128)(2,1)S(1)}, u32[]{:S(2)}) copy-start(bf16[2,48,256]{2,1,0:T(8,128)(2,1)S(1)} %collective-permute-done.14.refs_2_) | copy-start | bytes 147460
  45.1 5.5 %collective-permute-start.15 = (bf16[2,48,256]{2,1,0:T(8,128)(2,1)S(1)}, bf16[2,48,256]{2,1,0:T(8,128)(2,1)S(1)}, u32[]{:S(2)}, u32[]{:S(2)}) collective-permute-start(bf16[2,48,256]{2,1,0:T(8,128)(2,1)S(1)} %get-tuple-element.97), channel_id=1, source_target_pairs={{0,8},{2,10},{4,12},{6,14},{8,0},{10,2},{12,4},{14,6},{1,9},{3,11}... | collective-permute-start | bytes 147464 | tf_op jit(solution)/shard_map/ppermute | solution.py:513
  50.6 31.1 %copy-start.25 = (bf16[2,48,256]{2,1,0:T(8,128)(2,1)}, bf16[2,48,256]{2,1,0:T(8,128)(2,1)S(1)}, u32[]{:S(2)}) copy-start(bf16[2,48,256]{2,1,0:T(8,128)(2,1)S(1)} %collective-permute-done.15.refs_4_) | copy-start | bytes 147460
  50.6 5.9 %collective-permute-start.16 = (bf16[2,48,256]{2,1,0:T(8,128)(2,1)S(1)}, bf16[2,48,256]{2,1,0:T(8,128)(2,1)S(1)}, u32[]{:S(2)}, u32[]{:S(2)}) collective-permute-start(bf16[2,48,256]{2,1,0:T(8,128)(2,1)S(1)} %get-tuple-element.98), channel_id=1, source_target_pairs={{0,12},{2,14},{4,8},{6,10},{8,4},{10,6},{12,0},{14,2},{1,13},{3,15... | collective-permute-start | bytes 147464 | tf_op jit(solution)/shard_map/ppermute | solution.py:513
  56.5 25.2 %copy-start.27 = (bf16[2,48,256]{2,1,0:T(8,128)(2,1)}, bf16[2,48,256]{2,1,0:T(8,128)(2,1)S(1)}, u32[]{:S(2)}) copy-start(bf16[2,48,256]{2,1,0:T(8,128)(2,1)S(1)} %collective-permute-done.16.refs_6_) | copy-start | bytes 147460
  56.5 85.0 %copy-start.1 = (bf16[3,3,256,256]{3,2,1,0:T(8,128)(2,1)S(1)}, bf16[3,3,256,256]{3,2,1,0:T(8,128)(2,1)}, u32[]{:S(2)}) copy-start(bf16[3,3,256,256]{3,2,1,0:T(8,128)(2,1)} %param.10) | copy-start | bytes 3538948
  56.7 24.2 %collective-permute-start.20 = (bf16[2,192,256]{2,1,0:T(8,128)(2,1)S(1)}, bf16[2,192,256]{2,1,0:T(8,128)(2,1)S(1)}, u32[]{:S(2)}, u32[]{:S(2)}) collective-permute-start(bf16[2,192,256]{2,1,0:T(8,128)(2,1)S(1)} %get-tuple-element.112), channel_id=1, source_target_pairs={{0,2},{2,0},{4,6},{6,4},{8,10},{10,8},{12,14},{14,12},{1,3},{3,1},... | collective-permute-start | bytes 589832 | tf_op jit(solution)/shard_map/ppermute | solution.py:579
  58.2 22.7 %collective-permute-start.17 = (bf16[288,256]{1,0:T(8,128)(2,1)S(1)}, bf16[288,256]{1,0:T(8,128)(2,1)S(1)}, u32[]{:S(2)}, u32[]{:S(2)}) collective-permute-start(bf16[288,256]{1,0:T(8,128)(2,1)S(1)} %get-tuple-element.109), channel_id=1, source_target_pairs={{0,4},{2,6},{4,0},{6,2},{8,12},{10,14},{12,8},{14,10},{1,5},{3,7},... | collective-permute-start | bytes 442376 | tf_op jit(solution)/shard_map/ppermute | solution.py:556
  58.3 22.6 %collective-permute-start.18 = (bf16[288,256]{1,0:T(8,128)(2,1)S(1)}, bf16[288,256]{1,0:T(8,128)(2,1)S(1)}, u32[]{:S(2)}, u32[]{:S(2)}) collective-permute-start(bf16[288,256]{1,0:T(8,128)(2,1)S(1)} %get-tuple-element.110), channel_id=1, source_target_pairs={{0,8},{2,10},{4,12},{6,14},{8,0},{10,2},{12,4},{14,6},{1,9},{3,11}... | collective-permute-start | bytes 442376 | tf_op jit(solution)/shard_map/ppermute | solution.py:556
  60.4 20.6 %collective-permute-start.19 = (bf16[288,256]{1,0:T(8,128)(2,1)S(1)}, bf16[288,256]{1,0:T(8,128)(2,1)S(1)}, u32[]{:S(2)}, u32[]{:S(2)}) collective-permute-start(bf16[288,256]{1,0:T(8,128)(2,1)S(1)} %get-tuple-element.111), channel_id=1, source_target_pairs={{0,12},{2,14},{4,8},{6,10},{8,4},{10,6},{12,0},{14,2},{1,13},{3,15... | collective-permute-start | bytes 442376 | tf_op jit(solution)/shard_map/ppermute | solution.py:556
  62.6 8.8 %collective-permute-start.21 = (bf16[2,48,256]{2,1,0:T(8,128)(2,1)S(1)}, bf16[2,48,256]{2,1,0:T(8,128)(2,1)S(1)}, u32[]{:S(2)}, u32[]{:S(2)}) collective-permute-start(bf16[2,48,256]{2,1,0:T(8,128)(2,1)S(1)} %get-tuple-element.113), channel_id=1, source_target_pairs={{0,6},{6,0},{8,14},{14,8},{1,7},{7,1},{9,15},{15,9},{16,22},{22,16... | collective-permute-start | bytes 147464 | tf_op jit(solution)/shard_map/ppermute | solution.py:579
  72.1 8.2 %collective-permute-start.22 = (bf16[2,48,256]{2,1,0:T(8,128)(2,1)S(1)}, bf16[2,48,256]{2,1,0:T(8,128)(2,1)S(1)}, u32[]{:S(2)}, u32[]{:S(2)}) collective-permute-start(bf16[2,48,256]{2,1,0:T(8,128)(2,1)S(1)} %get-tuple-element.114), channel_id=1, source_target_pairs={{0,10},{4,14},{10,0},{14,4},{1,11},{5,15},{11,1},{15,5},{16,26},{2... | collective-permute-start | bytes 147464 | tf_op jit(solution)/shard_map/ppermute | solution.py:579
  81.7 10.5 %collective-permute-start.25 = (bf16[2,144,256]{2,1,0:T(8,128)(2,1)S(1)}, bf16[2,144,256]{2,1,0:T(8,128)(2,1)S(1)}, u32[]{:S(2)}, u32[]{:S(2)}) collective-permute-start(bf16[2,144,256]{2,1,0:T(8,128)(2,1)S(1)} %get-tuple-element.129), channel_id=1, source_target_pairs={{0,14},{2,4},{4,2},{6,8},{8,6},{10,12},{12,10},{14,0},{1,15},{3,5}... | collective-permute-start | bytes 442376 | tf_op jit(solution)/shard_map/ppermute | solution.py:587
  84.2 7.4 %collective-permute-start.24 = (bf16[2,48,256]{2,1,0:T(8,128)(2,1)S(1)}, bf16[2,48,256]{2,1,0:T(8,128)(2,1)S(1)}, u32[]{:S(2)}, u32[]{:S(2)}) collective-permute-start(bf16[2,48,256]{2,1,0:T(8,128)(2,1)S(1)} %get-tuple-element.128), channel_id=1, source_target_pairs={{0,14},{2,12},{4,10},{6,8},{8,6},{10,4},{12,2},{14,0},{1,15},{3,13... | collective-permute-start | bytes 147464 | tf_op jit(solution)/shard_map/ppermute | solution.py:587
  86.5 6.9 %collective-permute-start.23 = (bf16[288,256]{1,0:T(8,128)(2,1)S(1)}, bf16[288,256]{1,0:T(8,128)(2,1)S(1)}, u32[]{:S(2)}, u32[]{:S(2)}) collective-permute-start(bf16[288,256]{1,0:T(8,128)(2,1)S(1)} %shard_map.106.refs_0_), channel_id=1, source_target_pairs={{0,12},{2,14},{4,8},{6,10},{8,4},{10,6},{12,0},{14,2},{1,13},{3,15... | collective-permute-start | bytes 442376 | tf_op jit(solution)/shard_map/ppermute | solution.py:556
  86.5 6.9 %collective-permute-start.28 = (bf16[288,256]{1,0:T(8,128)(2,1)S(1)}, bf16[288,256]{1,0:T(8,128)(2,1)S(1)}, u32[]{:S(2)}, u32[]{:S(2)}) collective-permute-start(bf16[288,256]{1,0:T(8,128)(2,1)S(1)} %shard_map.106.refs_0_), channel_id=1, source_target_pairs={{0,2},{2,0},{4,6},{6,4},{8,10},{10,8},{12,14},{14,12},{1,3},{3,1},... | collective-permute-start | bytes 442376 | tf_op jit(solution)/shard_map/ppermute | solution.py:553
  89.5 7.2 %collective-permute-start.27 = (bf16[288,256]{1,0:T(8,128)(2,1)S(1)}, bf16[288,256]{1,0:T(8,128)(2,1)S(1)}, u32[]{:S(2)}, u32[]{:S(2)}) collective-permute-start(bf16[288,256]{1,0:T(8,128)(2,1)S(1)} %shard_map.106.refs_0_), channel_id=1, source_target_pairs={{0,8},{2,10},{4,12},{6,14},{8,0},{10,2},{12,4},{14,6},{1,9},{3,11}... | collective-permute-start | bytes 442376 | tf_op jit(solution)/shard_map/ppermute | solution.py:556
  92.2 6.9 %collective-permute-start.26 = (bf16[288,256]{1,0:T(8,128)(2,1)S(1)}, bf16[288,256]{1,0:T(8,128)(2,1)}, u32[]{:S(2)}, u32[]{:S(2)}) collective-permute-start(bf16[288,256]{1,0:T(8,128)(2,1)S(1)} %shard_map.106.refs_0_), channel_id=1, source_target_pairs={{0,4},{2,6},{4,0},{6,2},{8,12},{10,14},{12,8},{14,10},{1,5},{3,7},... | collective-permute-start | bytes 442376 | tf_op jit(solution)/shard_map/ppermute | solution.py:556
  92.9 6.5 %collective-permute-start.32 = (bf16[288,256]{1,0:T(8,128)(2,1)S(1)}, bf16[288,256]{1,0:T(8,128)(2,1)S(1)}, u32[]{:S(2)}, u32[]{:S(2)}) collective-permute-start(bf16[288,256]{1,0:T(8,128)(2,1)S(1)} %shard_map.106.refs_0_), channel_id=1, source_target_pairs={{0,1},{1,0},{2,3},{3,2},{4,5},{5,4},{6,7},{7,6},{8,9},{9,8},{10,11... | collective-permute-start | bytes 442376 | tf_op jit(solution)/shard_map/ppermute | solution.py:488
  93.5 8.4 %collective-permute-start.36 = (bf16[288,256]{1,0:T(8,128)(2,1)S(1)}, bf16[288,256]{1,0:T(8,128)(2,1)S(1)}, u32[]{:S(2)}, u32[]{:S(2)}) collective-permute-start(bf16[288,256]{1,0:T(8,128)(2,1)S(1)} %collective-permute-done.28.refs_4_), channel_id=1, source_target_pairs={{0,1},{1,0},{2,3},{3,2},{4,5},{5,4},{6,7},{7,6},{8,9},{9,8},{10,11... | collective-permute-start | bytes 442376 | tf_op jit(solution)/shard_map/ppermute | solution.py:488
  96.7 5.8 %collective-permute-start.34 = (bf16[288,256]{1,0:T(8,128)(2,1)S(1)}, bf16[288,256]{1,0:T(8,128)(2,1)S(1)}, u32[]{:S(2)}, u32[]{:S(2)}) collective-permute-start(bf16[288,256]{1,0:T(8,128)(2,1)S(1)} %collective-permute-done.27.refs_2_), channel_id=1, source_target_pairs={{0,1},{1,0},{2,3},{3,2},{4,5},{5,4},{6,7},{7,6},{8,9},{9,8},{10,11... | collective-permute-start | bytes 442376 | tf_op jit(solution)/shard_map/ppermute | solution.py:488
  96.7 7.0 %collective-permute-start.30 = (bf16[288,256]{1,0:T(8,128)(2,1)S(1)}, bf16[288,256]{1,0:T(8,128)(2,1)}, u32[]{:S(2)}, u32[]{:S(2)}) collective-permute-start(bf16[288,256]{1,0:T(8,128)(2,1)S(1)} %collective-permute-done.27.refs_2_), channel_id=1, source_target_pairs={{0,2},{2,0},{4,6},{6,4},{8,10},{10,8},{12,14},{14,12},{1,3},{3,1},... | collective-permute-start | bytes 442376 | tf_op jit(solution)/shard_map/ppermute | solution.py:553
  99.2 7.5 %collective-permute-start.29 = (bf16[288,256]{1,0:T(8,128)(2,1)}, bf16[288,256]{1,0:T(8,128)(2,1)}, u32[]{:S(2)}, u32[]{:S(2)}) collective-permute-start(bf16[288,256]{1,0:T(8,128)(2,1)} %collective-permute-done.26.refs_1_), channel_id=1, source_target_pairs={{0,2},{2,0},{4,6},{6,4},{8,10},{10,8},{12,14},{14,12},{1,3},{3,1},... | collective-permute-start | bytes 442376 | tf_op jit(solution)/shard_map/ppermute | solution.py:553
  100.1 9.4 %collective-permute-start.31 = (bf16[288,256]{1,0:T(8,128)(2,1)S(1)}, bf16[288,256]{1,0:T(8,128)(2,1)}, u32[]{:S(2)}, u32[]{:S(2)}) collective-permute-start(bf16[288,256]{1,0:T(8,128)(2,1)S(1)} %collective-permute-done.23.refs_3_), channel_id=1, source_target_pairs={{0,2},{2,0},{4,6},{6,4},{8,10},{10,8},{12,14},{14,12},{1,3},{3,1},... | collective-permute-start | bytes 442376 | tf_op jit(solution)/shard_map/ppermute | solution.py:553
  102.5 52.1 %collective-permute-start.35 = (bf16[288,256]{1,0:T(8,128)(2,1)S(1)}, bf16[288,256]{1,0:T(8,128)(2,1)}, u32[]{:S(2)}, u32[]{:S(2)}) collective-permute-start(bf16[288,256]{1,0:T(8,128)(2,1)S(1)} %collective-permute-done.23.refs_3_), channel_id=1, source_target_pairs={{0,1},{1,0},{2,3},{3,2},{4,5},{5,4},{6,7},{7,6},{8,9},{9,8},{10,11... | collective-permute-start | bytes 442376 | tf_op jit(solution)/shard_map/ppermute | solution.py:488
  103.2 51.4 %collective-permute-start.33 = (bf16[288,256]{1,0:T(8,128)(2,1)}, bf16[288,256]{1,0:T(8,128)(2,1)}, u32[]{:S(2)}, u32[]{:S(2)}) collective-permute-start(bf16[288,256]{1,0:T(8,128)(2,1)} %collective-permute-done.26.refs_1_), channel_id=1, source_target_pairs={{0,1},{1,0},{2,3},{3,2},{4,5},{5,4},{6,7},{7,6},{8,9},{9,8},{10,11... | collective-permute-start | bytes 442376 | tf_op jit(solution)/shard_map/ppermute | solution.py:488
  103.7 50.9 %collective-permute-start.38 = (bf16[288,256]{1,0:T(8,128)(2,1)}, bf16[288,256]{1,0:T(8,128)(2,1)}, u32[]{:S(2)}, u32[]{:S(2)}) collective-permute-start(bf16[288,256]{1,0:T(8,128)(2,1)} %collective-permute-done.30.refs_6_), channel_id=1, source_target_pairs={{0,1},{1,0},{2,3},{3,2},{4,5},{5,4},{6,7},{7,6},{8,9},{9,8},{10,11... | collective-permute-start | bytes 442376 | tf_op jit(solution)/shard_map/ppermute | solution.py:488
  106.6 48.0 %collective-permute-start.37 = (bf16[288,256]{1,0:T(8,128)(2,1)}, bf16[288,256]{1,0:T(8,128)(2,1)}, u32[]{:S(2)}, u32[]{:S(2)}) collective-permute-start(bf16[288,256]{1,0:T(8,128)(2,1)} %collective-permute-done.29.refs_5_), channel_id=1, source_target_pairs={{0,1},{1,0},{2,3},{3,2},{4,5},{5,4},{6,7},{7,6},{8,9},{9,8},{10,11... | collective-permute-start | bytes 442376 | tf_op jit(solution)/shard_map/ppermute | solution.py:488
  109.4 45.1 %collective-permute-start.39 = (bf16[288,256]{1,0:T(8,128)(2,1)}, bf16[288,256]{1,0:T(8,128)(2,1)}, u32[]{:S(2)}, u32[]{:S(2)}) collective-permute-start(bf16[288,256]{1,0:T(8,128)(2,1)} %collective-permute-done.31.refs_7_), channel_id=1, source_target_pairs={{0,1},{1,0},{2,3},{3,2},{4,5},{5,4},{6,7},{7,6},{8,9},{9,8},{10,11... | collective-permute-start | bytes 442376 | tf_op jit(solution)/shard_map/ppermute | solution.py:488
  141.6 0.9 copy-start.8
  142.5 0.9 copy-start.14
  143.4 0.8 copy-start.22
  144.2 0.8 copy-start.24
  145.0 0.8 copy-start.26
  145.8 0.8 copy-start.28
  146.6 0.8 copy-start.30
  149.0 5.6 %copy-start.10 = (bf16[288,256]{1,0:T(8,128)(2,1)S(1)}, bf16[288,256]{1,0:T(8,128)(2,1)}, u32[]{:S(2)}) copy-start(bf16[288,256]{1,0:T(8,128)(2,1)} %copy-done.9) | copy-start | bytes 442372
  149.0 5.6 %copy-start.12 = (bf16[288,256]{1,0:T(8,128)(2,1)S(1)}, bf16[288,256]{1,0:T(8,128)(2,1)}, u32[]{:S(2)}) copy-start(bf16[288,256]{1,0:T(8,128)(2,1)} %copy-done.11) | copy-start | bytes 442372
  149.0 5.6 %copy-start.16 = (bf16[288,256]{1,0:T(8,128)(2,1)S(1)}, bf16[288,256]{1,0:T(8,128)(2,1)}, u32[]{:S(2)}) copy-start(bf16[288,256]{1,0:T(8,128)(2,1)} %copy-done.15) | copy-start | bytes 442372
  149.0 5.6 %copy-start.18 = (bf16[288,256]{1,0:T(8,128)(2,1)S(1)}, bf16[288,256]{1,0:T(8,128)(2,1)}, u32[]{:S(2)}) copy-start(bf16[288,256]{1,0:T(8,128)(2,1)} %copy-done.17) | copy-start | bytes 442372
  149.0 5.6 %copy-start.20 = (bf16[288,256]{1,0:T(8,128)(2,1)S(1)}, bf16[288,256]{1,0:T(8,128)(2,1)}, u32[]{:S(2)}) copy-start(bf16[288,256]{1,0:T(8,128)(2,1)} %copy-done.19) | copy-start | bytes 442372
  (12 other events, 8.1 us)

commit v7 on v6

--- a/solution.py
+++ b/solution.py
@@ -9,7 +9,8 @@
 
 BF = jnp.bfloat16
 F32 = jnp.float32
-LIMIT = 40
+EXTRA = 8
+LIMIT = 24
 
 
 class Dims:
@@ -25,18 +26,18 @@
         self.WE = 12 * 8
         self.S = self.WE + self.ROW
 
-    def messages(self):
-        rows = [self.BASE] * self.T + [self.ROW]
+    def messages(self, extra=0):
+        rows = [self.BASE + extra] * self.T + [self.ROW]
         rows[1] += self.ROW
         return [(2, n, self.C) for n in rows]
 
-    def pairs(self):
+    def pairs(self, every=False):
         T = self.T
 
         def needed(i, d):
             return i in (0, T - 1) or d in (0, T - 1) or d in (T - 2 - i, T - i)
 
-        out = [[(i, i ^ k) for i in range(T) if k in (1, T - 1) or needed(i, i ^ k)] for k in range(T)]
+        out = [[(i, i ^ k) for i in range(T) if every or k in (1, T - 1) or needed(i, i ^ k)] for k in range(T)]
         out.append([(i, (i + 1) % T if i % 2 else (i - 1) % T) for i in range(T)])
         return out
 
@@ -100,7 +101,8 @@
             parts = row_targets(dm, jnp.where(t % 2 == 1, R - 1, 0))
         hot = one_hot(jnp.concatenate(parts, axis=0), dm.N)
         for which in range(2):
-            refs[k][which] = jnp.dot(hot, sources[which], preferred_element_type=F32).astype(BF)
+            rows = jnp.dot(hot, sources[which], preferred_element_type=F32).astype(BF)
+            refs[k][which, : rows.shape[0]] = rows
 
 
 def pack_kernel(dm, ep, x_ref, up_ref, *refs):
@@ -195,7 +197,7 @@
         for k in range(dm.T):
             at = dm.o_msg + k * dm.BASE
             table_ref[at : at + dm.BASE] = messages[k][which, : dm.BASE]
-        table_ref[dm.o_row : dm.o_row + dm.ROW] = messages[1][which, dm.BASE :]
+        table_ref[dm.o_row : dm.o_row + dm.ROW] = messages[1][which, dm.BASE : dm.BASE + dm.ROW]
         table_ref[dm.o_row + dm.ROW :] = messages[dm.T][which]
         out.append(jnp.dot(hot, table_ref[...], preferred_element_type=F32))
     return out
@@ -323,9 +325,9 @@
     T, R, F, N, C = dm.T, dm.R, dm.F, dm.N, dm.C
     M = T + 1
     messages = refs[:M]
-    send1_ref, keep1_ref, send2_ref, keep2_ref, bias_sum_ref, hid_ref, inner_ref = refs[M : M + 7]
-    out_messages = refs[M + 7 : 2 * M + 7]
-    table_ref, frame_ref, xs_ref, us_ref, z_ref, before_ref, acc_ref, hcat_ref = refs[2 * M + 7 :]
+    send1_ref, keep1_ref, send2_ref, keep2_ref, hid_ref, inner_ref = refs[M : M + 6]
+    out_messages = refs[M + 6 : 2 * M + 6]
+    table_ref, frame_ref, xs_ref, us_ref, z_ref, before_ref, acc_ref, hcat_ref = refs[2 * M + 6 :]
     t, p = lax.axis_index("tile"), lax.axis_index("dp")
     own = (x_ref[...].reshape(N, C), up_ref[...].reshape(N, C))
     gx, gu = gather_ghosts(dm, ep, t, own, messages, table_ref)
@@ -372,7 +374,12 @@
             preferred_element_type=F32,
         )
         put_taps(send1_ref, keep1_ref, tap, grad)
-    bias_sum_ref[...] = jnp.sum(before_grad, axis=0, keepdims=True)
+    bias_sum = jnp.sum(before_grad, axis=0, keepdims=True)
+    high = bias_sum.astype(BF).astype(F32)
+    for k in range(T):
+        for which, value in enumerate((high, bias_sum - high)):
+            at = out_messages[k].shape[1] - EXTRA
+            out_messages[k][which, at:] = jnp.broadcast_to(value, (EXTRA, C)).astype(BF)
     for r in range(R):
         for f in range(6):
             at = (r * 6 + f) * F
@@ -385,8 +392,14 @@
 def second_kernel(dm, ep, x_ref, d_ref, hid_ref, inner_ref, w1t_ref, w2_ref, *refs):
     T, R, F, N, C = dm.T, dm.R, dm.F, dm.N, dm.C
     messages = refs[: T + 1]
-    state_ref, grad_ref = refs[T + 1 : T + 3]
-    table_ref, frame_ref, hs_ref, is_ref, z_ref, acc_ref = refs[T + 3 :]
+    state_ref, grad_ref, bias_ref = refs[T + 1 : T + 4]
+    table_ref, frame_ref, hs_ref, is_ref, z_ref, acc_ref = refs[T + 4 :]
+    bias_sum = jnp.zeros((1, C), F32)
+    for k in range(T):
+        at = messages[k].shape[1] - EXTRA
+        for which in range(2):
+            bias_sum = bias_sum + messages[k][which, at : at + 1].astype(F32)
+    bias_ref[...] = jnp.broadcast_to(bias_sum, bias_ref.shape)
     t = lax.axis_index("tile")
     own = (hid_ref[...].reshape(N, C), inner_ref[...].reshape(N, C))
     gh, gi = gather_ghosts(dm, ep, t, own, messages, table_ref)
@@ -442,26 +455,30 @@
     refs[-1][...] = total.astype(BF)
 
 
-def normal_kernel(zcount, bias_sum_ref, *refs):
-    blocks, (second_ref, first_ref, bias_ref) = refs[: 4 * zcount], refs[4 * zcount :]
+def normal_kernel(zcount, bias1_ref, bias2_ref, *refs):
+    sources, (second_ref, first_ref, bias_ref) = refs[:4], refs[4:]
     t, p = lax.axis_index("tile"), lax.axis_index("dp")
-    n = blocks[0].shape[0] // 2
+    rows = sources[0].shape[0] // zcount
+    n = rows // 2
     size = n // 9
     for which, out_ref in enumerate((second_ref, first_ref)):
         square = None
-        for ref in blocks:
-            v = ref[which * n : (which + 1) * n].astype(F32)
-            square = v * v if square is None else square + v * v
+        for ref in sources:
+            for j in range(zcount):
+                at = j * rows + which * n
+                v = ref[at : at + n].astype(F32)
+                part = jnp.sum(v * v, axis=0, keepdims=True)
+                square = part if square is None else square + part
         mean = jnp.sum(square, keepdims=True) / (9 * out_ref.shape[1] * out_ref.shape[2])
         scale = lax.rsqrt(mean + 1e-06)
-        for index, ref in enumerate(blocks):
-            group, j = index // zcount, index % zcount
+        for group, ref in enumerate(sources):
             block = (p ^ (group // 2)) * 2 + ((t % 2) ^ (group % 2))
-            at = pl.ds(pl.multiple_of((block * zcount + ((t // 2) ^ j)) * size, size), size)
-            for tap in range(9):
-                row = which * n + tap * size
-                out_ref[tap, at] = ref[row : row + size].astype(F32) * scale
-    total = bias_sum_ref[...]
+            for j in range(zcount):
+                at = pl.ds(pl.multiple_of((block * zcount + ((t // 2) ^ j)) * size, size), size)
+                for tap in range(9):
+                    row = j * rows + which * n + tap * size
+                    out_ref[tap, at] = ref[row : row + size].astype(F32) * scale
+    total = bias1_ref[0:1] + bias2_ref[0:1]
     bias_mean = jnp.mean(total * total, keepdims=True)
     bias_ref[...] = total * lax.rsqrt(bias_mean + 1e-06)
 
@@ -523,11 +540,10 @@
             ((9, half, channels), F32),
             ((9, half, channels), BF),
             ((9, half, channels), F32),
-            ((1, channels), F32),
             (planes, BF),
             (planes, BF),
         ]
-        + msg_shapes,
+        + [(shape, BF) for shape in dm.messages(EXTRA)],
         [
             ((dm.NT, channels), BF),
             (frame, F32),
@@ -541,9 +557,9 @@
         smem_first=True,
         limit=LIMIT,
     )(edge_partner, x, d, w1s, bias.reshape(1, channels), w2t, *messages)
-    send1, keep1, send2, keep2, bias_sum, hidden, inner = outs[:7]
-    packed = list(outs[7:])
-    bias_sum = lax.psum(bias_sum, ("tile", "dp"))
+    send1, keep1, send2, keep2, hidden, inner = outs[:6]
+    packed = list(outs[6:])
+    pairs = dm.pairs(True)
 
     zcount = tiles // 2
     block = (18 * half // tiles, channels)
@@ -564,7 +580,7 @@
         functools.partial(half_kernel, zcount), [((zcount,) + block, F32)] + [(block, BF)] * zcount
     )(keep2, keep1, swap_dp(send2), swap_dp(send1))
     recvs = [along_y(v) for v in sends]
-    got = [send_message(packed, k) for k in early]
+    got = [lax.ppermute(packed[k], "tile", pairs[k]) for k in early]
     recvs, got = barrier((recvs, got))
     for k, v in zip(early, got):
         messages[k] = v
@@ -588,12 +604,12 @@
     own[-1], got = barrier((own[-1], got))
     for k, v in zip(late, got):
         messages[k] = v
-    other = [along_y(v) for v in own]
-    blocks = own + other
-    blocks = blocks + [swap_dp(v) for v in blocks]
-    state, grad = call(
+    own = jnp.concatenate(own, axis=0)
+    other = along_y(own)
+    own, messages = barrier((own, messages))
+    state, grad, bias_sum = call(
         functools.partial(second_kernel, dm),
-        [(planes, BF), (planes, F32)],
+        [(planes, BF), (planes, F32), ((8, channels), F32)],
         [
             ((dm.NT, channels), BF),
             (frame, F32),
@@ -605,11 +621,12 @@
         smem_first=True,
         limit=LIMIT,
     )(edge_partner, x, d, hidden, inner, w1t, w2, *messages)
+    other, bias_sum = barrier((other, bias_sum))
     second_step, first_step, bias_step = call(
         functools.partial(normal_kernel, zcount),
         [(taps, F32)] * 2 + [((1, channels), F32)],
         limit=24,
-    )(bias_sum, *blocks)
+    )(bias_sum, swap_dp(bias_sum), own, other, swap_dp(own), swap_dp(other))
     return (
         state.reshape(initial_state.shape),
         grad.reshape(initial_state.shape),

time: 160 us -> 114 us (0.71)
  blocking collectives: 32.1 us -> 0 us
  local copies, waits for them, and re-layouts: 19.1 us -> 5.24 us
  waiting for transfers between devices: 33.8 us -> 36.9 us
    psum x1 -> x0, blocking collectives: 32.1 us -> none  [on_device(): bias_sum = lax.psum(bias_sum, ('tile', 'dp'))]
    unnamed x73 -> x20, local copies, waits for them, and re-layouts: 19.1 us -> 5.23 us
    ppermute x11 -> x8, waiting for transfers between devices: 9.51 us -> 1.51 us  [send_message(): lax.ppermute(messages[k], 'tile', pairs[k])]
    ppermute x0 -> x3, waiting for transfers between devices: none -> 7.53 us  [on_device(): got = [lax.ppermute(packed[k], 'tile', pairs[k]) for k in early]]
    ppermute x11 -> x8, starting transfers between devices: 25.1 us -> 18.5 us  [send_message(): lax.ppermute(messages[k], 'tile', pairs[k])]
    ppermute x2, waiting for transfers between devices: 2.12 us -> 7.82 us  [on_device(): got = [lax.ppermute(v, 'tile', pairs[k]) for k, v in zip(late, todo)]]
    ppermute x0 -> x3, starting transfers between devices: none -> 5.43 us  [on_device(): got = [lax.ppermute(packed[k], 'tile', pairs[k]) for k in early]]
    ppermute x8 -> x5, starting transfers between devices: 10.9 us -> 6.41 us  [along_y(): return lax.ppermute(v, 'tile', [(i, i ^ 1) for i in range(tiles)])]
  transfers between devices with their start and end apart: 40 -> 32, of which waited for: 11 -> 12; matrix products, arithmetic and copies ran while one was open for 0% -> 0% of each run, Pallas kernels for 4% -> 6%
where the time goes in v7:
time: 114 us; the launch traced here: 113 us
  starting transfers between devices  50.7 us (44%)
  waiting for transfers between devices  36.9 us (32%)
  Pallas kernels  19.8 us (17%)
  local copies, waits for them, and re-layouts  5.24 us (5%)
    pallas_call x8, Pallas kernels, run(): pl.pallas_call(kernel, out_shape=[jax.ShapeDtypeStruct(s, dt) for s, dt i...  19.8 us
    ppermute x8, starting transfers between devices, send_message(): lax.ppermute(messages[k], 'tile', pairs[k])  18.5 us
    ppermute x6, starting transfers between devices, along_z(): return lax.ppermute(v, 'tile', [(i, i ^ 2 * j) for i in range(tiles)])  8.77 us
    ppermute x3, waiting for transfers between devices, on_device(): got = [lax.ppermute(v, 'tile', pairs[k]) for k, v in zip(middle, todo)]  8.76 us
    ppermute x2, waiting for transfers between devices, on_device(): got = [lax.ppermute(v, 'tile', pairs[k]) for k, v in zip(late, todo)]  7.82 us
    ppermute x3, waiting for transfers between devices, on_device(): got = [lax.ppermute(packed[k], 'tile', pairs[k]) for k in early]  7.53 us
    ppermute x5, waiting for transfers between devices, along_y(): return lax.ppermute(v, 'tile', [(i, i ^ 1) for i in range(tiles)])  6.56 us
    ppermute x5, starting transfers between devices, along_y(): return lax.ppermute(v, 'tile', [(i, i ^ 1) for i in range(tiles)])  6.41 us
  transfers between devices with their start and end apart: 32, of which 12 were waited for; matrix products, arithmetic and copies ran while one was open for 0% of the time, Pallas kernels for 6%

profile of v7, /device:TPU:0, one launch (start us, length us, event | category | flops | bytes accessed | tf_op | source)
XLA Modules:
  0.0 113.4 jit_solution(17143918607541710945)
XLA Ops:
  0.6 0.8 copy.13.ep
  1.4 0.9 copy-done.2
  2.3 0.9 copy-done.4
  3.3 2.1 %shard_map.102 = (bf16[2,48,256]{2,1,0:T(8,128)(2,1)S(1)}, bf16[2,192,256]{2,1,0:T(8,128)(2,1)S(1)}, bf16[2,48,256]{2,1,0:T(8,128)(2,1)S(1)}, bf16[2,48,256]{2,1...) custom-call(s32[6,4]{1,0:T(8,128)S(1)} %copy.13.ep, ...), custom_call_target="tpu_custom_call" | custom-call | tf_op jit(solution)/shard_map/pallas_call | solution.py:491
  5.4 3.0 %collective-permute-start = (bf16[2,192,256]{2,1,0:T(8,128)(2,1)S(1)}, bf16[2,192,256]{2,1,0:T(8,128)(2,1)S(1)}, u32[]{:S(2)}, u32[]{:S(2)}) collective-permute-start(bf16[2,192,256]{2,1,0:T(8,128)(2,1)S(1)} %get-tuple-element.87), channel_id=1, source_target_pairs={{0,2},{2,0},{4,6},{6,4},{8,10},{10,8},{12,14},{14,12},{1,3},{3,1},... | collective-permute-start | bytes 589832 | tf_op jit(solution)/shard_map/ppermute | solution.py:530
  8.4 3.5 %collective-permute-start.7 = (bf16[2,144,256]{2,1,0:T(8,128)(2,1)S(1)}, bf16[2,144,256]{2,1,0:T(8,128)(2,1)S(1)}, u32[]{:S(2)}, u32[]{:S(2)}) collective-permute-start(bf16[2,144,256]{2,1,0:T(8,128)(2,1)S(1)} %get-tuple-element.94), channel_id=1, source_target_pairs={{0,14},{2,4},{4,2},{6,8},{8,6},{10,12},{12,10},{14,0},{1,15},{3,5}... | collective-permute-start | bytes 442376 | tf_op jit(solution)/shard_map/ppermute | solution.py:530
  12.0 1.9 %collective-permute-start.1 = (bf16[2,48,256]{2,1,0:T(8,128)(2,1)S(1)}, bf16[2,48,256]{2,1,0:T(8,128)(2,1)S(1)}, u32[]{:S(2)}, u32[]{:S(2)}) collective-permute-start(bf16[2,48,256]{2,1,0:T(8,128)(2,1)S(1)} %get-tuple-element.88), channel_id=1, source_target_pairs={{0,4},{4,0},{10,14},{14,10},{1,5},{5,1},{11,15},{15,11},{16,20},{2... | collective-permute-start | bytes 147464 | tf_op jit(solution)/shard_map/ppermute | solution.py:530
  13.9 1.9 %collective-permute-start.2 = (bf16[2,48,256]{2,1,0:T(8,128)(2,1)S(1)}, bf16[2,48,256]{2,1,0:T(8,128)(2,1)S(1)}, u32[]{:S(2)}, u32[]{:S(2)}) collective-permute-start(bf16[2,48,256]{2,1,0:T(8,128)(2,1)S(1)} %get-tuple-element.89), channel_id=1, source_target_pairs={{0,6},{6,0},{8,14},{14,8},{1,7},{7,1},{9,15},{15,9},{16,22},{22,16... | collective-permute-start | bytes 147464 | tf_op jit(solution)/shard_map/ppermute | solution.py:530
  15.8 3.6 %collective-permute-start.3 = (bf16[2,48,256]{2,1,0:T(8,128)(2,1)S(1)}, bf16[2,48,256]{2,1,0:T(8,128)(2,1)S(1)}, u32[]{:S(2)}, u32[]{:S(2)}) collective-permute-start(bf16[2,48,256]{2,1,0:T(8,128)(2,1)S(1)} %get-tuple-element.90), channel_id=1, source_target_pairs={{0,8},{2,10},{4,12},{6,14},{8,0},{10,2},{12,4},{14,6},{1,9},{3,11}... | collective-permute-start | bytes 147464 | tf_op jit(solution)/shard_map/ppermute | solution.py:530
  19.4 0.0 collective-permute-done.1.refs_2_
  19.4 2.2 %collective-permute-start.4 = (bf16[2,48,256]{2,1,0:T(8,128)(2,1)S(1)}, bf16[2,48,256]{2,1,0:T(8,128)(2,1)S(1)}, u32[]{:S(2)}, u32[]{:S(2)}) collective-permute-start(bf16[2,48,256]{2,1,0:T(8,128)(2,1)S(1)} %get-tuple-element.91), channel_id=1, source_target_pairs={{0,10},{4,14},{10,0},{14,4},{1,11},{5,15},{11,1},{15,5},{16,26},{2... | collective-permute-start | bytes 147464 | tf_op jit(solution)/shard_map/ppermute | solution.py:530
  21.7 0.0 collective-permute-done.2.refs_3_
  21.7 0.1 collective-permute-start.5
  21.8 2.2 %collective-permute-start.6 = (bf16[2,48,256]{2,1,0:T(8,128)(2,1)S(1)}, bf16[2,48,256]{2,1,0:T(8,128)(2,1)S(1)}, u32[]{:S(2)}, u32[]{:S(2)}) collective-permute-start(bf16[2,48,256]{2,1,0:T(8,128)(2,1)S(1)} %get-tuple-element.93), channel_id=1, source_target_pairs={{0,14},{2,12},{4,10},{6,8},{8,6},{10,4},{12,2},{14,0},{1,15},{3,13... | collective-permute-start | bytes 147464 | tf_op jit(solution)/shard_map/ppermute | solution.py:530
  24.0 1.3 %copy-done = bf16[3,3,256,256]{3,2,1,0:T(8,128)(2,1)S(1)} copy-done((bf16[3,3,256,256]{3,2,1,0:T(8,128)(2,1)S(1)}, bf16[3,3,256,256]{3,2,1,0:T(8,128)(2,1)}, u32[]{:S(2)}) %copy-start) | copy-done | bytes 1179672
  25.3 1.3 %copy-done.6 = bf16[3,3,256,256]{3,2,1,0:T(8,128)(2,1)S(1)} copy-done((bf16[3,3,256,256]{3,2,1,0:T(8,128)(2,1)S(1)}, bf16[3,3,256,256]{3,2,1,0:T(8,128)(2,1)}, u32[]{:S(2)}) %copy-start.6) | copy-done | bytes 1179672
  26.5 0.7 shard_map.101
  27.2 0.7 collective-permute-done.4.refs_5_
  28.0 0.8 collective-permute-done.6.refs_7_
  28.7 0.0 collective-permute-done.7.refs_8_
  28.8 8.3 %shard_map.103 = (bf16[9,128,256]{2,1,0:T(8,128)(2,1)S(1)}, f32[9,128,256]{2,1,0:T(8,128)S(1)}, bf16[9,128,256]{2,1,0:T(8,128)(2,1)S(1)}, f32[9,128,256]{2,1,0:T...) custom-call(s32[6,4]{1,0:T(8,128)S(1)} %copy.13.ep, ...), custom_call_target="tpu_custom_call" | custom-call | tf_op jit(solution)/shard_map/pallas_call | solution.py:491
  37.1 0.1 collective-permute-start.8
  37.2 0.5 collective-permute-start.9
  37.7 1.3 %collective-permute-start.14 = (bf16[2,56,256]{2,1,0:T(8,128)(2,1)S(1)}, bf16[2,56,256]{2,1,0:T(8,128)(2,1)S(1)}, u32[]{:S(2)}, u32[]{:S(2)}) collective-permute-start(bf16[2,56,256]{2,1,0:T(8,128)(2,1)S(1)} %get-tuple-element.107), channel_id=1, source_target_pairs={{0,4},{2,6},{4,0},{6,2},{8,12},{10,14},{12,8},{14,10},{1,5},{3,7},... | collective-permute-start | bytes 172040 | tf_op jit(solution)/shard_map/ppermute | solution.py:583
  39.0 0.2 collective-permute-done.8.recv2_ref
  39.2 0.8 collective-permute-done.9.recv1_ref
  40.0 0.2 shard_map.104
  40.2 2.5 %collective-permute-start.10 = (bf16[288,256]{1,0:T(8,128)(2,1)S(1)}, bf16[288,256]{1,0:T(8,128)(2,1)S(1)}, u32[]{:S(2)}, u32[]{:S(2)}) collective-permute-start(bf16[288,256]{1,0:T(8,128)(2,1)S(1)} %get-tuple-element.103), channel_id=1, source_target_pairs={{0,2},{2,0},{4,6},{6,4},{8,10},{10,8},{12,14},{14,12},{1,3},{3,1},... | collective-permute-start | bytes 442376 | tf_op jit(solution)/shard_map/ppermute | solution.py:569
  42.8 0.1 collective-permute-start.11
  42.9 1.9 %collective-permute-start.12 = (bf16[288,256]{1,0:T(8,128)(2,1)S(1)}, bf16[288,256]{1,0:T(8,128)(2,1)S(1)}, u32[]{:S(2)}, u32[]{:S(2)}) collective-permute-start(bf16[288,256]{1,0:T(8,128)(2,1)S(1)} %get-tuple-element.105), channel_id=1, source_target_pairs={{0,2},{2,0},{4,6},{6,4},{8,10},{10,8},{12,14},{14,12},{1,3},{3,1},... | collective-permute-start | bytes 442376 | tf_op jit(solution)/shard_map/ppermute | solution.py:569
  44.8 0.1 collective-permute-start.13
  44.9 1.4 %collective-permute-start.15 = (bf16[2,56,256]{2,1,0:T(8,128)(2,1)S(1)}, bf16[2,56,256]{2,1,0:T(8,128)(2,1)S(1)}, u32[]{:S(2)}, u32[]{:S(2)}) collective-permute-start(bf16[2,56,256]{2,1,0:T(8,128)(2,1)S(1)} %get-tuple-element.108), channel_id=1, source_target_pairs={{0,8},{2,10},{4,12},{6,14},{8,0},{10,2},{12,4},{14,6},{1,9},{3,11}... | collective-permute-start | bytes 172040 | tf_op jit(solution)/shard_map/ppermute | solution.py:583
  46.3 4.3 %collective-permute-done.15.refs_4_ = bf16[2,56,256]{2,1,0:T(8,128)(2,1)S(1)} collective-permute-done((bf16[2,56,256]{2,1,0:T(8,128)(2,1)S(1)}, bf16[2,56,256]{2,1,0:T(8,128)(2,1)S(1)}, u32[]{:S(2)}, u32[]{:S(2)}) %collective-permute-start.15) | collective-permute-done | bytes 57376 | tf_op jit(solution)/shard_map/ppermute | solution.py:583
  50.6 2.7 %collective-permute-start.16 = (bf16[2,56,256]{2,1,0:T(8,128)(2,1)S(1)}, bf16[2,56,256]{2,1,0:T(8,128)(2,1)S(1)}, u32[]{:S(2)}, u32[]{:S(2)}) collective-permute-start(bf16[2,56,256]{2,1,0:T(8,128)(2,1)S(1)} %get-tuple-element.109), channel_id=1, source_target_pairs={{0,12},{2,14},{4,8},{6,10},{8,4},{10,6},{12,0},{14,2},{1,13},{3,15... | collective-permute-start | bytes 172040 | tf_op jit(solution)/shard_map/ppermute | solution.py:583
  53.3 3.2 %collective-permute-done.16.refs_6_ = bf16[2,56,256]{2,1,0:T(8,128)(2,1)S(1)} collective-permute-done((bf16[2,56,256]{2,1,0:T(8,128)(2,1)S(1)}, bf16[2,56,256]{2,1,0:T(8,128)(2,1)S(1)}, u32[]{:S(2)}, u32[]{:S(2)}) %collective-permute-start.16) | collective-permute-done | bytes 57376 | tf_op jit(solution)/shard_map/ppermute | solution.py:583
  56.6 0.0 collective-permute-done.12.refs_2_
  56.6 0.0 collective-permute-done.13.refs_3_
  56.6 0.2 shard_map.105
  56.8 0.0 copy-start.1
  56.8 1.7 %collective-permute-start.20 = (bf16[2,200,256]{2,1,0:T(8,128)(2,1)S(1)}, bf16[2,200,256]{2,1,0:T(8,128)(2,1)S(1)}, u32[]{:S(2)}, u32[]{:S(2)}) collective-permute-start(bf16[2,200,256]{2,1,0:T(8,128)(2,1)S(1)} %get-tuple-element.124), channel_id=1, source_target_pairs={{0,2},{2,0},{4,6},{6,4},{8,10},{10,8},{12,14},{14,12},{1,3},{3,1},... | collective-permute-start | bytes 614408 | tf_op jit(solution)/shard_map/ppermute | solution.py:595
  58.5 0.0 collective-permute-start.17
  58.5 2.0 %collective-permute-start.18 = (bf16[288,256]{1,0:T(8,128)(2,1)S(1)}, bf16[288,256]{1,0:T(8,128)(2,1)S(1)}, u32[]{:S(2)}, u32[]{:S(2)}) collective-permute-start(bf16[288,256]{1,0:T(8,128)(2,1)S(1)} %get-tuple-element.122), channel_id=1, source_target_pairs={{0,8},{2,10},{4,12},{6,14},{8,0},{10,2},{12,4},{14,6},{1,9},{3,11}... | collective-permute-start | bytes 442376 | tf_op jit(solution)/shard_map/ppermute | solution.py:572
  60.5 2.4 %collective-permute-start.19 = (bf16[288,256]{1,0:T(8,128)(2,1)S(1)}, bf16[288,256]{1,0:T(8,128)(2,1)S(1)}, u32[]{:S(2)}, u32[]{:S(2)}) collective-permute-start(bf16[288,256]{1,0:T(8,128)(2,1)S(1)} %get-tuple-element.123), channel_id=1, source_target_pairs={{0,12},{2,14},{4,8},{6,10},{8,4},{10,6},{12,0},{14,2},{1,13},{3,15... | collective-permute-start | bytes 442376 | tf_op jit(solution)/shard_map/ppermute | solution.py:572
  62.9 0.0 collective-permute-start.21
  62.9 5.7 %collective-permute-done.21.refs_3_ = bf16[2,56,256]{2,1,0:T(8,128)(2,1)S(1)} collective-permute-done((bf16[2,56,256]{2,1,0:T(8,128)(2,1)S(1)}, bf16[2,56,256]{2,1,0:T(8,128)(2,1)S(1)}, u32[]{:S(2)}, u32[]{:S(2)}) %collective-permute-start.21) | collective-permute-done | bytes 57376 | tf_op jit(solution)/shard_map/ppermute | solution.py:595
  68.6 4.0 %collective-permute-start.22 = (bf16[2,56,256]{2,1,0:T(8,128)(2,1)S(1)}, bf16[2,56,256]{2,1,0:T(8,128)(2,1)S(1)}, u32[]{:S(2)}, u32[]{:S(2)}) collective-permute-start(bf16[2,56,256]{2,1,0:T(8,128)(2,1)S(1)} %get-tuple-element.126), channel_id=1, source_target_pairs={{0,10},{2,8},{4,14},{6,12},{8,2},{10,0},{12,6},{14,4},{1,11},{3,9}... | collective-permute-start | bytes 172040 | tf_op jit(solution)/shard_map/ppermute | solution.py:595
  72.6 3.0 %collective-permute-done.22.refs_5_ = bf16[2,56,256]{2,1,0:T(8,128)(2,1)S(1)} collective-permute-done((bf16[2,56,256]{2,1,0:T(8,128)(2,1)S(1)}, bf16[2,56,256]{2,1,0:T(8,128)(2,1)S(1)}, u32[]{:S(2)}, u32[]{:S(2)}) %collective-permute-start.22) | collective-permute-done | bytes 57376 | tf_op jit(solution)/shard_map/ppermute | solution.py:595
  75.6 0.0 collective-permute-done.17.refs_0_
  75.6 0.0 collective-permute-done.18.refs_1_
  75.6 0.0 collective-permute-done.19.refs_2_
  75.6 0.1 shard_map.106
  75.7 2.5 %collective-permute-start.27 = (bf16[2,144,256]{2,1,0:T(8,128)(2,1)S(1)}, bf16[2,144,256]{2,1,0:T(8,128)(2,1)S(1)}, u32[]{:S(2)}, u32[]{:S(2)}) collective-permute-start(bf16[2,144,256]{2,1,0:T(8,128)(2,1)S(1)} %get-tuple-element.134), channel_id=1, source_target_pairs={{0,14},{2,4},{4,2},{6,8},{8,6},{10,12},{12,10},{14,0},{1,15},{3,5}... | collective-permute-start | bytes 442376 | tf_op jit(solution)/shard_map/ppermute | solution.py:603
  78.2 1.9 %collective-permute-start.25 = (bf16[288,256]{1,0:T(8,128)(2,1)S(1)}, bf16[288,256]{1,0:T(8,128)(2,1)S(1)}, u32[]{:S(2)}, u32[]{:S(2)}) collective-permute-start(bf16[288,256]{1,0:T(8,128)(2,1)S(1)} %shard_map.106), channel_id=1, source_target_pairs={{0,12},{2,14},{4,8},{6,10},{8,4},{10,6},{12,0},{14,2},{1,13},{3,15... | collective-permute-start | bytes 442376 | tf_op jit(solution)/shard_map/ppermute | solution.py:572
  80.2 2.4 %collective-permute-start.24 = (bf16[288,256]{1,0:T(8,128)(2,1)S(1)}, bf16[288,256]{1,0:T(8,128)(2,1)S(1)}, u32[]{:S(2)}, u32[]{:S(2)}) collective-permute-start(bf16[288,256]{1,0:T(8,128)(2,1)S(1)} %shard_map.106), channel_id=1, source_target_pairs={{0,8},{2,10},{4,12},{6,14},{8,0},{10,2},{12,4},{14,6},{1,9},{3,11}... | collective-permute-start | bytes 442376 | tf_op jit(solution)/shard_map/ppermute | solution.py:572
  82.6 2.3 %collective-permute-start.26 = (bf16[2,56,256]{2,1,0:T(8,128)(2,1)S(1)}, bf16[2,56,256]{2,1,0:T(8,128)(2,1)S(1)}, u32[]{:S(2)}, u32[]{:S(2)}) collective-permute-start(bf16[2,56,256]{2,1,0:T(8,128)(2,1)S(1)} %get-tuple-element.133), channel_id=1, source_target_pairs={{0,14},{2,12},{4,10},{6,8},{8,6},{10,4},{12,2},{14,0},{1,15},{3,13... | collective-permute-start | bytes 172040 | tf_op jit(solution)/shard_map/ppermute | solution.py:603
  84.9 7.8 %collective-permute-done.26.refs_7_ = bf16[2,56,256]{2,1,0:T(8,128)(2,1)S(1)} collective-permute-done((bf16[2,56,256]{2,1,0:T(8,128)(2,1)S(1)}, bf16[2,56,256]{2,1,0:T(8,128)(2,1)S(1)}, u32[]{:S(2)}, u32[]{:S(2)}) %collective-permute-start.26) | collective-permute-done | bytes 57376 | tf_op jit(solution)/shard_map/ppermute | solution.py:603
  92.7 0.0 collective-permute-done.27.refs_8_
  92.8 2.1 %collective-permute-done.24 = bf16[288,256]{1,0:T(8,128)(2,1)S(1)} collective-permute-done((bf16[288,256]{1,0:T(8,128)(2,1)S(1)}, bf16[288,256]{1,0:T(8,128)(2,1)S(1)}, u32[]{:S(2)}, u32[]{:S(2)}) %collective-permute-start.24) | collective-permute-done | bytes 147488 | tf_op jit(solution)/shard_map/ppermute | solution.py:572
  94.9 1.8 %collective-permute-start.28 = (bf16[1152,256]{1,0:T(8,128)(2,1)S(1)}, bf16[1152,256]{1,0:T(8,128)(2,1)S(1)}, u32[]{:S(2)}, u32[]{:S(2)}) collective-permute-start(bf16[1152,256]{1,0:T(8,128)(2,1)S(1)} %constant_dynamic-update-slice_fusion.refs_0_), channel_id=1, source_target_pairs={{0,2},{2,0},{4,6},{6,4},{8,10},{10,8},{12,14},{14,12},{1,3},{3,1},... | collective-permute-start | bytes 1769480 | tf_op jit(solution)/shard_map/ppermute | solution.py:569
  96.7 5.5 %shard_map.107 = (bf16[18,24,256]{2,1,0:T(8,128)(2,1)}, f32[18,24,256]{2,1,0:T(8,128)}, f32[8,256]{1,0:T(8,128)S(1)}) custom-call(s32[6,4]{1,0:T(8,128)S(1)} %copy.13.ep, bf16[18,24,256]{2,1,0:T(8,128)(2,1)S(1)} %bitcast.20, bf16[18,24,256]{2,1,0:T(8,128)(2,1)S(1)} %bitcast.23, bf16[18,24,256]{2,1,0:T(8,128)(2,1)S(1)} %get-tuple-element.95.hid_ref, ...), custom_call_target="tpu_custom_call" | custom-call | tf_op jit(solution)/shard_map/pallas_call | solution.py:491
  102.2 6.5 %collective-permute-done.28.refs_1_ = bf16[1152,256]{1,0:T(8,128)(2,1)S(1)} collective-permute-done((bf16[1152,256]{1,0:T(8,128)(2,1)S(1)}, bf16[1152,256]{1,0:T(8,128)(2,1)S(1)}, u32[]{:S(2)}, u32[]{:S(2)}) %collective-permute-start.28) | collective-permute-done | bytes 589856 | tf_op jit(solution)/shard_map/ppermute | solution.py:569
  108.8 0.5 collective-permute-start.29
  109.3 1.5 %collective-permute-done.29.bias2_ref = f32[8,256]{1,0:T(8,128)S(1)} collective-permute-done((f32[8,256]{1,0:T(8,128)S(1)}, f32[8,256]{1,0:T(8,128)S(1)}, u32[]{:S(2)}, u32[]{:S(2)}) %collective-permute-start.29) | collective-permute-done | bytes 8224 | tf_op jit(solution)/shard_map/ppermute | solution.py:505
  110.8 2.6 %shard_map.108 = (f32[9,256,256]{2,1,0:T(8,128)}, f32[9,256,256]{2,1,0:T(8,128)}, f32[1,256]{1,0:T(1,128)}) custom-call(f32[8,256]{1,0:T(8,128)S(1)} %get-tuple-element.157.bias1_ref, f32[8,256]{1,0:T(8,128)S(1)} %collective-permute-done.29.bias2_ref, bf16[1152,256]{1,0:T(8,128)(2,1)S(1)} %constant_dynamic-update-slice_fusion.refs_0_, ...), custom_call_target="tpu_custom_call" | custom-call | tf_op jit(solution)/shard_map/pallas_call | solution.py:491
  (29 shorter events, 0.1 us)
Async XLA Ops:
  1.4 0.9 copy-start.2
  2.3 0.9 copy-start.4
  5.4 23.3 %collective-permute-start = (bf16[2,192,256]{2,1,0:T(8,128)(2,1)S(1)}, bf16[2,192,256]{2,1,0:T(8,128)(2,1)S(1)}, u32[]{:S(2)}, u32[]{:S(2)}) collective-permute-start(bf16[2,192,256]{2,1,0:T(8,128)(2,1)S(1)} %get-tuple-element.87), channel_id=1, source_target_pairs={{0,2},{2,0},{4,6},{6,4},{8,10},{10,8},{12,14},{14,12},{1,3},{3,1},... | collective-permute-start | bytes 589832 | tf_op jit(solution)/shard_map/ppermute | solution.py:530
  8.4 20.3 %collective-permute-start.7 = (bf16[2,144,256]{2,1,0:T(8,128)(2,1)S(1)}, bf16[2,144,256]{2,1,0:T(8,128)(2,1)S(1)}, u32[]{:S(2)}, u32[]{:S(2)}) collective-permute-start(bf16[2,144,256]{2,1,0:T(8,128)(2,1)S(1)} %get-tuple-element.94), channel_id=1, source_target_pairs={{0,14},{2,4},{4,2},{6,8},{8,6},{10,12},{12,10},{14,0},{1,15},{3,5}... | collective-permute-start | bytes 442376 | tf_op jit(solution)/shard_map/ppermute | solution.py:530
  12.0 7.4 %collective-permute-start.1 = (bf16[2,48,256]{2,1,0:T(8,128)(2,1)S(1)}, bf16[2,48,256]{2,1,0:T(8,128)(2,1)S(1)}, u32[]{:S(2)}, u32[]{:S(2)}) collective-permute-start(bf16[2,48,256]{2,1,0:T(8,128)(2,1)S(1)} %get-tuple-element.88), channel_id=1, source_target_pairs={{0,4},{4,0},{10,14},{14,10},{1,5},{5,1},{11,15},{15,11},{16,20},{2... | collective-permute-start | bytes 147464 | tf_op jit(solution)/shard_map/ppermute | solution.py:530
  13.9 7.8 %collective-permute-start.2 = (bf16[2,48,256]{2,1,0:T(8,128)(2,1)S(1)}, bf16[2,48,256]{2,1,0:T(8,128)(2,1)S(1)}, u32[]{:S(2)}, u32[]{:S(2)}) collective-permute-start(bf16[2,48,256]{2,1,0:T(8,128)(2,1)S(1)} %get-tuple-element.89), channel_id=1, source_target_pairs={{0,6},{6,0},{8,14},{14,8},{1,7},{7,1},{9,15},{15,9},{16,22},{22,16... | collective-permute-start | bytes 147464 | tf_op jit(solution)/shard_map/ppermute | solution.py:530
  15.8 5.9 %collective-permute-start.3 = (bf16[2,48,256]{2,1,0:T(8,128)(2,1)S(1)}, bf16[2,48,256]{2,1,0:T(8,128)(2,1)S(1)}, u32[]{:S(2)}, u32[]{:S(2)}) collective-permute-start(bf16[2,48,256]{2,1,0:T(8,128)(2,1)S(1)} %get-tuple-element.90), channel_id=1, source_target_pairs={{0,8},{2,10},{4,12},{6,14},{8,0},{10,2},{12,4},{14,6},{1,9},{3,11}... | collective-permute-start | bytes 147464 | tf_op jit(solution)/shard_map/ppermute | solution.py:530
  19.4 8.6 %collective-permute-start.4 = (bf16[2,48,256]{2,1,0:T(8,128)(2,1)S(1)}, bf16[2,48,256]{2,1,0:T(8,128)(2,1)S(1)}, u32[]{:S(2)}, u32[]{:S(2)}) collective-permute-start(bf16[2,48,256]{2,1,0:T(8,128)(2,1)S(1)} %get-tuple-element.91), channel_id=1, source_target_pairs={{0,10},{4,14},{10,0},{14,4},{1,11},{5,15},{11,1},{15,5},{16,26},{2... | collective-permute-start | bytes 147464 | tf_op jit(solution)/shard_map/ppermute | solution.py:530
  21.7 6.3 %collective-permute-start.5 = (bf16[2,48,256]{2,1,0:T(8,128)(2,1)S(1)}, bf16[2,48,256]{2,1,0:T(8,128)(2,1)S(1)}, u32[]{:S(2)}, u32[]{:S(2)}) collective-permute-start(bf16[2,48,256]{2,1,0:T(8,128)(2,1)S(1)} %get-tuple-element.92), channel_id=1, source_target_pairs={{0,12},{2,14},{4,8},{6,10},{8,4},{10,6},{12,0},{14,2},{1,13},{3,15... | collective-permute-start | bytes 147464 | tf_op jit(solution)/shard_map/ppermute | solution.py:530
  21.8 7.0 %collective-permute-start.6 = (bf16[2,48,256]{2,1,0:T(8,128)(2,1)S(1)}, bf16[2,48,256]{2,1,0:T(8,128)(2,1)S(1)}, u32[]{:S(2)}, u32[]{:S(2)}) collective-permute-start(bf16[2,48,256]{2,1,0:T(8,128)(2,1)S(1)} %get-tuple-element.93), channel_id=1, source_target_pairs={{0,14},{2,12},{4,10},{6,8},{8,6},{10,4},{12,2},{14,0},{1,15},{3,13... | collective-permute-start | bytes 147464 | tf_op jit(solution)/shard_map/ppermute | solution.py:530
  24.0 1.3 %copy-start = (bf16[3,3,256,256]{3,2,1,0:T(8,128)(2,1)S(1)}, bf16[3,3,256,256]{3,2,1,0:T(8,128)(2,1)}, u32[]{:S(2)}) copy-start(bf16[3,3,256,256]{3,2,1,0:T(8,128)(2,1)} %param.10) | copy-start | bytes 3538948
  25.3 1.3 %copy-start.6 = (bf16[3,3,256,256]{3,2,1,0:T(8,128)(2,1)S(1)}, bf16[3,3,256,256]{3,2,1,0:T(8,128)(2,1)}, u32[]{:S(2)}) copy-start(bf16[3,3,256,256]{3,2,1,0:T(8,128)(2,1)} %param.8) | copy-start | bytes 3538948
  26.5 2.2 %copy-start.3 = (bf16[1,6,3,24,256]{4,3,2,1,0:T(8,128)(2,1)S(1)}, bf16[1,6,3,24,256]{4,3,2,1,0:T(8,128)(2,1)}, u32[]{:S(2)}) copy-start(bf16[1,6,3,24,256]{4,3,2,1,0:T(8,128)(2,1)} %param.6) | copy-start | bytes 663556
  26.5 2.2 %copy-start.5 = (bf16[1,1,6,3,24,256]{5,4,3,2,1,0:T(8,128)(2,1)S(1)}, bf16[1,1,6,3,24,256]{5,4,3,2,1,0:T(8,128)(2,1)}, u32[]{:S(2)}) copy-start(bf16[1,1,6,3,24,256]{5,4,3,2,1,0:T(8,128)(2,1)} %param.7) | copy-start | bytes 663556
  26.5 2.2 %copy-start.7 = (f32[256]{0:T(256)S(1)}, f32[256]{0:T(256)}, u32[]{:S(2)}) copy-start(f32[256]{0:T(256)} %param.9) | copy-start | bytes 3076
  37.1 2.1 %collective-permute-start.8 = (bf16[9,128,256]{2,1,0:T(8,128)(2,1)S(1)}, bf16[9,128,256]{2,1,0:T(8,128)(2,1)S(1)}, u32[]{:S(2)}, u32[]{:S(2)}) collective-permute-start(bf16[9,128,256]{2,1,0:T(8,128)(2,1)S(1)} %get-tuple-element.100), channel_id=1, source_target_pairs={{0,1},{1,0},{2,3},{3,2},{4,5},{5,4},{6,7},{7,6},{8,9},{9,8},{10,11... | collective-permute-start | bytes 1769480 | tf_op jit(solution)/shard_map/ppermute | solution.py:505
  37.2 2.8 %collective-permute-start.9 = (bf16[9,128,256]{2,1,0:T(8,128)(2,1)S(1)}, bf16[9,128,256]{2,1,0:T(8,128)(2,1)S(1)}, u32[]{:S(2)}, u32[]{:S(2)}) collective-permute-start(bf16[9,128,256]{2,1,0:T(8,128)(2,1)S(1)} %get-tuple-element.101), channel_id=1, source_target_pairs={{0,1},{1,0},{2,3},{3,2},{4,5},{5,4},{6,7},{7,6},{8,9},{9,8},{10,11... | collective-permute-start | bytes 1769480 | tf_op jit(solution)/shard_map/ppermute | solution.py:505
  37.7 7.2 %collective-permute-start.14 = (bf16[2,56,256]{2,1,0:T(8,128)(2,1)S(1)}, bf16[2,56,256]{2,1,0:T(8,128)(2,1)S(1)}, u32[]{:S(2)}, u32[]{:S(2)}) collective-permute-start(bf16[2,56,256]{2,1,0:T(8,128)(2,1)S(1)} %get-tuple-element.107), channel_id=1, source_target_pairs={{0,4},{2,6},{4,0},{6,2},{8,12},{10,14},{12,8},{14,10},{1,5},{3,7},... | collective-permute-start | bytes 172040 | tf_op jit(solution)/shard_map/ppermute | solution.py:583
  40.2 16.3 %collective-permute-start.10 = (bf16[288,256]{1,0:T(8,128)(2,1)S(1)}, bf16[288,256]{1,0:T(8,128)(2,1)S(1)}, u32[]{:S(2)}, u32[]{:S(2)}) collective-permute-start(bf16[288,256]{1,0:T(8,128)(2,1)S(1)} %get-tuple-element.103), channel_id=1, source_target_pairs={{0,2},{2,0},{4,6},{6,4},{8,10},{10,8},{12,14},{14,12},{1,3},{3,1},... | collective-permute-start | bytes 442376 | tf_op jit(solution)/shard_map/ppermute | solution.py:569
  42.8 13.8 %collective-permute-start.11 = (bf16[288,256]{1,0:T(8,128)(2,1)S(1)}, bf16[288,256]{1,0:T(8,128)(2,1)S(1)}, u32[]{:S(2)}, u32[]{:S(2)}) collective-permute-start(bf16[288,256]{1,0:T(8,128)(2,1)S(1)} %get-tuple-element.104), channel_id=1, source_target_pairs={{0,2},{2,0},{4,6},{6,4},{8,10},{10,8},{12,14},{14,12},{1,3},{3,1},... | collective-permute-start | bytes 442376 | tf_op jit(solution)/shard_map/ppermute | solution.py:569
  42.9 13.7 %collective-permute-start.12 = (bf16[288,256]{1,0:T(8,128)(2,1)S(1)}, bf16[288,256]{1,0:T(8,128)(2,1)S(1)}, u32[]{:S(2)}, u32[]{:S(2)}) collective-permute-start(bf16[288,256]{1,0:T(8,128)(2,1)S(1)} %get-tuple-element.105), channel_id=1, source_target_pairs={{0,2},{2,0},{4,6},{6,4},{8,10},{10,8},{12,14},{14,12},{1,3},{3,1},... | collective-permute-start | bytes 442376 | tf_op jit(solution)/shard_map/ppermute | solution.py:569
  44.8 11.8 %collective-permute-start.13 = (bf16[288,256]{1,0:T(8,128)(2,1)S(1)}, bf16[288,256]{1,0:T(8,128)(2,1)S(1)}, u32[]{:S(2)}, u32[]{:S(2)}) collective-permute-start(bf16[288,256]{1,0:T(8,128)(2,1)S(1)} %get-tuple-element.106), channel_id=1, source_target_pairs={{0,2},{2,0},{4,6},{6,4},{8,10},{10,8},{12,14},{14,12},{1,3},{3,1},... | collective-permute-start | bytes 442376 | tf_op jit(solution)/shard_map/ppermute | solution.py:569
  44.9 5.7 %collective-permute-start.15 = (bf16[2,56,256]{2,1,0:T(8,128)(2,1)S(1)}, bf16[2,56,256]{2,1,0:T(8,128)(2,1)S(1)}, u32[]{:S(2)}, u32[]{:S(2)}) collective-permute-start(bf16[2,56,256]{2,1,0:T(8,128)(2,1)S(1)} %get-tuple-element.108), channel_id=1, source_target_pairs={{0,8},{2,10},{4,12},{6,14},{8,0},{10,2},{12,4},{14,6},{1,9},{3,11}... | collective-permute-start | bytes 172040 | tf_op jit(solution)/shard_map/ppermute | solution.py:583
  50.6 6.0 %collective-permute-start.16 = (bf16[2,56,256]{2,1,0:T(8,128)(2,1)S(1)}, bf16[2,56,256]{2,1,0:T(8,128)(2,1)S(1)}, u32[]{:S(2)}, u32[]{:S(2)}) collective-permute-start(bf16[2,56,256]{2,1,0:T(8,128)(2,1)S(1)} %get-tuple-element.109), channel_id=1, source_target_pairs={{0,12},{2,14},{4,8},{6,10},{8,4},{10,6},{12,0},{14,2},{1,13},{3,15... | collective-permute-start | bytes 172040 | tf_op jit(solution)/shard_map/ppermute | solution.py:583
  56.8 39.9 %copy-start.1 = (bf16[3,3,256,256]{3,2,1,0:T(8,128)(2,1)S(1)}, bf16[3,3,256,256]{3,2,1,0:T(8,128)(2,1)}, u32[]{:S(2)}) copy-start(bf16[3,3,256,256]{3,2,1,0:T(8,128)(2,1)} %param.10) | copy-start | bytes 3538948
  56.8 18.9 %collective-permute-start.20 = (bf16[2,200,256]{2,1,0:T(8,128)(2,1)S(1)}, bf16[2,200,256]{2,1,0:T(8,128)(2,1)S(1)}, u32[]{:S(2)}, u32[]{:S(2)}) collective-permute-start(bf16[2,200,256]{2,1,0:T(8,128)(2,1)S(1)} %get-tuple-element.124), channel_id=1, source_target_pairs={{0,2},{2,0},{4,6},{6,4},{8,10},{10,8},{12,14},{14,12},{1,3},{3,1},... | collective-permute-start | bytes 614408 | tf_op jit(solution)/shard_map/ppermute | solution.py:595
  58.5 17.1 %collective-permute-start.17 = (bf16[288,256]{1,0:T(8,128)(2,1)S(1)}, bf16[288,256]{1,0:T(8,128)(2,1)S(1)}, u32[]{:S(2)}, u32[]{:S(2)}) collective-permute-start(bf16[288,256]{1,0:T(8,128)(2,1)S(1)} %get-tuple-element.121), channel_id=1, source_target_pairs={{0,4},{2,6},{4,0},{6,2},{8,12},{10,14},{12,8},{14,10},{1,5},{3,7},... | collective-permute-start | bytes 442376 | tf_op jit(solution)/shard_map/ppermute | solution.py:572
  58.5 17.1 %collective-permute-start.18 = (bf16[288,256]{1,0:T(8,128)(2,1)S(1)}, bf16[288,256]{1,0:T(8,128)(2,1)S(1)}, u32[]{:S(2)}, u32[]{:S(2)}) collective-permute-start(bf16[288,256]{1,0:T(8,128)(2,1)S(1)} %get-tuple-element.122), channel_id=1, source_target_pairs={{0,8},{2,10},{4,12},{6,14},{8,0},{10,2},{12,4},{14,6},{1,9},{3,11}... | collective-permute-start | bytes 442376 | tf_op jit(solution)/shard_map/ppermute | solution.py:572
  60.5 15.1 %collective-permute-start.19 = (bf16[288,256]{1,0:T(8,128)(2,1)S(1)}, bf16[288,256]{1,0:T(8,128)(2,1)S(1)}, u32[]{:S(2)}, u32[]{:S(2)}) collective-permute-start(bf16[288,256]{1,0:T(8,128)(2,1)S(1)} %get-tuple-element.123), channel_id=1, source_target_pairs={{0,12},{2,14},{4,8},{6,10},{8,4},{10,6},{12,0},{14,2},{1,13},{3,15... | collective-permute-start | bytes 442376 | tf_op jit(solution)/shard_map/ppermute | solution.py:572
  62.9 5.7 %collective-permute-start.21 = (bf16[2,56,256]{2,1,0:T(8,128)(2,1)S(1)}, bf16[2,56,256]{2,1,0:T(8,128)(2,1)S(1)}, u32[]{:S(2)}, u32[]{:S(2)}) collective-permute-start(bf16[2,56,256]{2,1,0:T(8,128)(2,1)S(1)} %get-tuple-element.125), channel_id=1, source_target_pairs={{0,6},{2,4},{4,2},{6,0},{8,14},{10,12},{12,10},{14,8},{1,7},{3,5},... | collective-permute-start | bytes 172040 | tf_op jit(solution)/shard_map/ppermute | solution.py:595
  68.6 7.0 %collective-permute-start.22 = (bf16[2,56,256]{2,1,0:T(8,128)(2,1)S(1)}, bf16[2,56,256]{2,1,0:T(8,128)(2,1)S(1)}, u32[]{:S(2)}, u32[]{:S(2)}) collective-permute-start(bf16[2,56,256]{2,1,0:T(8,128)(2,1)S(1)} %get-tuple-element.126), channel_id=1, source_target_pairs={{0,10},{2,8},{4,14},{6,12},{8,2},{10,0},{12,6},{14,4},{1,11},{3,9}... | collective-permute-start | bytes 172040 | tf_op jit(solution)/shard_map/ppermute | solution.py:595
  75.7 17.0 %collective-permute-start.27 = (bf16[2,144,256]{2,1,0:T(8,128)(2,1)S(1)}, bf16[2,144,256]{2,1,0:T(8,128)(2,1)S(1)}, u32[]{:S(2)}, u32[]{:S(2)}) collective-permute-start(bf16[2,144,256]{2,1,0:T(8,128)(2,1)S(1)} %get-tuple-element.134), channel_id=1, source_target_pairs={{0,14},{2,4},{4,2},{6,8},{8,6},{10,12},{12,10},{14,0},{1,15},{3,5}... | collective-permute-start | bytes 442376 | tf_op jit(solution)/shard_map/ppermute | solution.py:603
  78.2 14.5 %collective-permute-start.25 = (bf16[288,256]{1,0:T(8,128)(2,1)S(1)}, bf16[288,256]{1,0:T(8,128)(2,1)S(1)}, u32[]{:S(2)}, u32[]{:S(2)}) collective-permute-start(bf16[288,256]{1,0:T(8,128)(2,1)S(1)} %shard_map.106), channel_id=1, source_target_pairs={{0,12},{2,14},{4,8},{6,10},{8,4},{10,6},{12,0},{14,2},{1,13},{3,15... | collective-permute-start | bytes 442376 | tf_op jit(solution)/shard_map/ppermute | solution.py:572
  80.2 12.6 %collective-permute-start.23 = (bf16[288,256]{1,0:T(8,128)(2,1)S(1)}, bf16[288,256]{1,0:T(8,128)(2,1)S(1)}, u32[]{:S(2)}, u32[]{:S(2)}) collective-permute-start(bf16[288,256]{1,0:T(8,128)(2,1)S(1)} %shard_map.106), channel_id=1, source_target_pairs={{0,4},{2,6},{4,0},{6,2},{8,12},{10,14},{12,8},{14,10},{1,5},{3,7},... | collective-permute-start | bytes 442376 | tf_op jit(solution)/shard_map/ppermute | solution.py:572
  80.2 14.7 %collective-permute-start.24 = (bf16[288,256]{1,0:T(8,128)(2,1)S(1)}, bf16[288,256]{1,0:T(8,128)(2,1)S(1)}, u32[]{:S(2)}, u32[]{:S(2)}) collective-permute-start(bf16[288,256]{1,0:T(8,128)(2,1)S(1)} %shard_map.106), channel_id=1, source_target_pairs={{0,8},{2,10},{4,12},{6,14},{8,0},{10,2},{12,4},{14,6},{1,9},{3,11}... | collective-permute-start | bytes 442376 | tf_op jit(solution)/shard_map/ppermute | solution.py:572
  82.6 10.1 %collective-permute-start.26 = (bf16[2,56,256]{2,1,0:T(8,128)(2,1)S(1)}, bf16[2,56,256]{2,1,0:T(8,128)(2,1)S(1)}, u32[]{:S(2)}, u32[]{:S(2)}) collective-permute-start(bf16[2,56,256]{2,1,0:T(8,128)(2,1)S(1)} %get-tuple-element.133), channel_id=1, source_target_pairs={{0,14},{2,12},{4,10},{6,8},{8,6},{10,4},{12,2},{14,0},{1,15},{3,13... | collective-permute-start | bytes 172040 | tf_op jit(solution)/shard_map/ppermute | solution.py:603
  94.9 13.8 %collective-permute-start.28 = (bf16[1152,256]{1,0:T(8,128)(2,1)S(1)}, bf16[1152,256]{1,0:T(8,128)(2,1)S(1)}, u32[]{:S(2)}, u32[]{:S(2)}) collective-permute-start(bf16[1152,256]{1,0:T(8,128)(2,1)S(1)} %constant_dynamic-update-slice_fusion.refs_0_), channel_id=1, source_target_pairs={{0,2},{2,0},{4,6},{6,4},{8,10},{10,8},{12,14},{14,12},{1,3},{3,1},... | collective-permute-start | bytes 1769480 | tf_op jit(solution)/shard_map/ppermute | solution.py:569
  96.7 12.6 %collective-permute-start.30 = (bf16[1152,256]{1,0:T(8,128)(2,1)S(1)}, bf16[1152,256]{1,0:T(8,128)(2,1)S(1)}, u32[]{:S(2)}, u32[]{:S(2)}) collective-permute-start(bf16[1152,256]{1,0:T(8,128)(2,1)S(1)} %constant_dynamic-update-slice_fusion.refs_0_), channel_id=1, source_target_pairs={{0,1},{1,0},{2,3},{3,2},{4,5},{5,4},{6,7},{7,6},{8,9},{9,8},{10,11... | collective-permute-start | bytes 1769480 | tf_op jit(solution)/shard_map/ppermute | solution.py:505
  108.8 2.0 %collective-permute-start.31 = (bf16[1152,256]{1,0:T(8,128)(2,1)S(1)}, bf16[1152,256]{1,0:T(8,128)(2,1)S(1)}, u32[]{:S(2)}, u32[]{:S(2)}) collective-permute-start(bf16[1152,256]{1,0:T(8,128)(2,1)S(1)} %collective-permute-done.28.refs_1_), channel_id=1, source_target_pairs={{0,1},{1,0},{2,3},{3,2},{4,5},{5,4},{6,7},{7,6},{8,9},{9,8},{10,11... | collective-permute-start | bytes 1769480 | tf_op jit(solution)/shard_map/ppermute | solution.py:505
  108.8 2.0 %collective-permute-start.29 = (f32[8,256]{1,0:T(8,128)S(1)}, f32[8,256]{1,0:T(8,128)S(1)}, u32[]{:S(2)}, u32[]{:S(2)}) collective-permute-start(f32[8,256]{1,0:T(8,128)S(1)} %get-tuple-element.157.bias1_ref), channel_id=1, source_target_pairs={{0,1},{1,0},{2,3},{3,2},{4,5},{5,4},{6,7},{7,6},{8,9},{9,8},{10,11... | collective-permute-start | bytes 24584 | tf_op jit(solution)/shard_map/ppermute | solution.py:505

commit v8 on v6

--- a/solution.py
+++ b/solution.py
@@ -9,7 +9,8 @@
 
 BF = jnp.bfloat16
 F32 = jnp.float32
-LIMIT = 40
+EXTRA = 8
+LIMIT = 24
 
 
 class Dims:
@@ -19,24 +20,32 @@
         self.ROW = 6 * face
         self.SLOT = -(-(2 * rows + 2) // 8) * 8
         self.BASE = 6 * self.SLOT
+        self.MIX = tiles // 2 - 1
         self.o_msg = self.N
         self.o_row = self.o_msg + tiles * self.BASE
         self.NT = self.o_row + 2 * self.ROW
         self.WE = 12 * 8
         self.S = self.WE + self.ROW
 
+    def partner(self, t, k):
+        if k == self.MIX:
+            ends = (t == 0) | (t == self.MIX) | (t == self.MIX + 1) | (t == self.T - 1)
+            return jnp.where(ends, t ^ k, self.T - 1 - t)
+        return t ^ k
+
     def messages(self):
-        rows = [self.BASE] * self.T + [self.ROW]
+        rows = [self.BASE] * (self.T - 1) + [self.BASE + self.ROW]
         rows[1] += self.ROW
         return [(2, n, self.C) for n in rows]
 
     def pairs(self):
-        T = self.T
+        T, mix = self.T, self.MIX
 
         def needed(i, d):
             return i in (0, T - 1) or d in (0, T - 1) or d in (T - 2 - i, T - i)
 
-        out = [[(i, i ^ k) for i in range(T) if k in (1, T - 1) or needed(i, i ^ k)] for k in range(T)]
+        out = [[(i, i ^ k) for i in range(T) if k == 1 or needed(i, i ^ k)] for k in range(T - 1)]
+        out[mix] = [(i, i ^ mix if i in (0, mix, mix + 1, T - 1) else T - 1 - i) for i in range(T)]
         out.append([(i, (i + 1) % T if i % 2 else (i - 1) % T) for i in range(T)])
         return out
 
@@ -92,12 +101,14 @@
 
 def write_messages(dm, ep, t, sources, refs):
     R = dm.R
-    for k in range(dm.T + 1):
-        parts = strip_targets(dm, ep, t, t ^ k) if k < dm.T else []
-        if k == 1:
-            parts = parts + row_targets(dm, jnp.where(t % 2 == 0, R - 1, 0))
-        if k == dm.T:
-            parts = row_targets(dm, jnp.where(t % 2 == 1, R - 1, 0))
+    for k in range(dm.T):
+        if k < dm.T - 1:
+            parts = strip_targets(dm, ep, t, dm.partner(t, k))
+            if k == 1:
+                parts = parts + row_targets(dm, jnp.where(t % 2 == 0, R - 1, 0))
+        else:
+            parts = [mirror_slot(dm, f) for f in range(6)]
+            parts = parts + row_targets(dm, jnp.where(t % 2 == 1, R - 1, 0))
         hot = one_hot(jnp.concatenate(parts, axis=0), dm.N)
         for which in range(2):
             refs[k][which] = jnp.dot(hot, sources[which], preferred_element_type=F32).astype(BF)
@@ -118,7 +129,8 @@
     row_next = dm.o_row + odd * dm.ROW
     side_first = dm.o_msg + (t ^ (T - t)) * dm.BASE + jnp.where(t == 1, R + 2, 0)
     side_last = dm.o_msg + (t ^ (T - 2 - t)) * dm.BASE + jnp.where(t == T - 2, R + 2, 0)
-    mirror = dm.o_msg + (T - 1) * dm.BASE
+    ends = (t == 0) | (t == dm.MIX) | (t == dm.MIX + 1) | (t == T - 1)
+    mirror = dm.o_msg + jnp.where(ends, T - 1, dm.MIX) * dm.BASE
     for f in range(6):
         for edge in (3, 1):
             value = ep[f, edge]
@@ -196,7 +208,7 @@
             at = dm.o_msg + k * dm.BASE
             table_ref[at : at + dm.BASE] = messages[k][which, : dm.BASE]
         table_ref[dm.o_row : dm.o_row + dm.ROW] = messages[1][which, dm.BASE :]
-        table_ref[dm.o_row + dm.ROW :] = messages[dm.T][which]
+        table_ref[dm.o_row + dm.ROW :] = messages[dm.T - 1][which, dm.BASE :]
         out.append(jnp.dot(hot, table_ref[...], preferred_element_type=F32))
     return out
 
@@ -319,13 +331,22 @@
         send_ref[first_tap + i] = value[(2 * i + 1) * half : (2 * i + 2) * half].astype(BF)
 
 
+def high_low(row):
+    i = lax.broadcasted_iota(jnp.int32, (EXTRA, row.shape[1]), 0)
+    high = row.astype(BF).astype(F32)
+    return jnp.where(i == 0, high, jnp.where(i == 1, row - high, 0.0)).astype(BF)
+
+
+def both(pair):
+    return pair[0:1].astype(F32) + pair[1:2].astype(F32)
+
+
 def first_kernel(dm, ep, x_ref, up_ref, w1_ref, bias_ref, w2t_ref, *refs):
     T, R, F, N, C = dm.T, dm.R, dm.F, dm.N, dm.C
-    M = T + 1
-    messages = refs[:M]
-    send1_ref, keep1_ref, send2_ref, keep2_ref, bias_sum_ref, hid_ref, inner_ref = refs[M : M + 7]
-    out_messages = refs[M + 7 : 2 * M + 7]
-    table_ref, frame_ref, xs_ref, us_ref, z_ref, before_ref, acc_ref, hcat_ref = refs[2 * M + 7 :]
+    messages = refs[:T]
+    send1_ref, keep1_ref, send2_ref, keep2_ref, hid_ref, inner_ref, bias_sum_ref, send_bias_ref = refs[T : T + 8]
+    out_messages = refs[T + 8 : 2 * T + 8]
+    table_ref, frame_ref, xs_ref, us_ref, z_ref, before_ref, acc_ref, hcat_ref = refs[2 * T + 8 :]
     t, p = lax.axis_index("tile"), lax.axis_index("dp")
     own = (x_ref[...].reshape(N, C), up_ref[...].reshape(N, C))
     gx, gu = gather_ghosts(dm, ep, t, own, messages, table_ref)
@@ -372,7 +393,9 @@
             preferred_element_type=F32,
         )
         put_taps(send1_ref, keep1_ref, tap, grad)
-    bias_sum_ref[...] = jnp.sum(before_grad, axis=0, keepdims=True)
+    bias_sum = jnp.sum(before_grad, axis=0, keepdims=True)
+    bias_sum_ref[...] = bias_sum
+    send_bias_ref[...] = high_low(bias_sum)
     for r in range(R):
         for f in range(6):
             at = (r * 6 + f) * F
@@ -384,9 +407,9 @@
 
 def second_kernel(dm, ep, x_ref, d_ref, hid_ref, inner_ref, w1t_ref, w2_ref, *refs):
     T, R, F, N, C = dm.T, dm.R, dm.F, dm.N, dm.C
-    messages = refs[: T + 1]
-    state_ref, grad_ref = refs[T + 1 : T + 3]
-    table_ref, frame_ref, hs_ref, is_ref, z_ref, acc_ref = refs[T + 3 :]
+    messages = refs[:T]
+    state_ref, grad_ref = refs[T : T + 2]
+    table_ref, frame_ref, hs_ref, is_ref, z_ref, acc_ref = refs[T + 2 :]
     t = lax.axis_index("tile")
     own = (hid_ref[...].reshape(N, C), inner_ref[...].reshape(N, C))
     gh, gi = gather_ghosts(dm, ep, t, own, messages, table_ref)
@@ -409,61 +432,90 @@
             grad_ref[f * R + r] = d_ref[f * R + r].astype(F32) + acc_ref[at : at + F]
 
 
-def half_kernel(zcount, keep2_ref, keep1_ref, recv2_ref, recv1_ref, out_keep, *out_sends):
-    size = keep1_ref.shape[1] // 2
+def half_kernel(zcount, keep_ref, recv_ref, *refs):
+    size = keep_ref.shape[1] // 2
     own = lax.axis_index("tile") % 2
     mine = pl.ds(pl.multiple_of(own * size, size), size)
     far = pl.ds(pl.multiple_of((1 - own) * size, size), size)
     part = size // zcount
-    for which, (keep_ref, recv_ref) in enumerate(((keep2_ref, recv2_ref), (keep1_ref, recv1_ref))):
-        for tap in range(9):
-            kept = keep_ref[tap, mine] + recv_ref[tap, mine].astype(F32)
-            sent = keep_ref[tap, far] + recv_ref[tap, far].astype(F32)
-            at = (9 * which + tap) * part
-            for j in range(zcount):
-                out_keep[j, at : at + part] = kept[j * part : (j + 1) * part]
-                out_sends[j][at : at + part] = sent[j * part : (j + 1) * part].astype(BF)
-
-
-def block_kernel(zcount, keep_ref, *refs):
-    recvs, (out_keep, *out_sends), sum_ref = refs[:zcount], refs[zcount : 2 * zcount], refs[2 * zcount]
+    if len(refs) > 2:
+        bias_ref, recv_bias_ref, out_keep, out_send, out_bias = refs
+        bias = bias_ref[...] + both(recv_bias_ref)
+        out_bias[...] = bias
+        out_send[9 * size :] = high_low(bias)
+    else:
+        out_keep, out_send = refs
+    for tap in range(9):
+        kept = keep_ref[tap, mine] + recv_ref[tap, mine].astype(F32)
+        sent = keep_ref[tap, far] + recv_ref[tap, far].astype(F32)
+        for j in range(zcount):
+            at = j * 9 * part + tap * part
+            out_keep[j, tap * part : (tap + 1) * part] = kept[j * part : (j + 1) * part]
+            out_send[at : at + part] = sent[j * part : (j + 1) * part].astype(BF)
+
+
+def block_kernel(zcount, keep_ref, recv_ref, *refs):
     own = lax.axis_index("tile") // 2
+    n = keep_ref.shape[1]
+    if len(refs) > zcount + 1:
+        bias_ref, out_keep, *out_sends, out_bias, sum_ref = refs
+        bias = bias_ref[...] + both(recv_ref[zcount * n : zcount * n + 2])
+        out_bias[...] = bias
+        tail = high_low(bias)
+    else:
+        out_keep, *out_sends, sum_ref = refs
+        tail = None
     for j in range(zcount):
-        sum_ref[j] = keep_ref[j] + recvs[j][...].astype(F32)
+        sum_ref[j] = keep_ref[j] + recv_ref[j * n : (j + 1) * n].astype(F32)
     out_keep[...] = sum_ref[own]
     for j in range(1, zcount):
-        out_sends[j - 1][...] = sum_ref[own ^ j].astype(BF)
-
-
-def last_kernel(keep_ref, *refs):
+        out_sends[j - 1][0:n] = sum_ref[own ^ j].astype(BF)
+        if tail is not None:
+            out_sends[j - 1][n:] = tail
+
+
+def last_kernel(zcount, keep_ref, *refs):
+    recvs = refs[: zcount - 1]
+    n = keep_ref.shape[0]
     total = keep_ref[...]
-    for ref in refs[:-1]:
-        total = total + ref[...].astype(F32)
-    refs[-1][...] = total.astype(BF)
-
-
-def normal_kernel(zcount, bias_sum_ref, *refs):
-    blocks, (second_ref, first_ref, bias_ref) = refs[: 4 * zcount], refs[4 * zcount :]
+    for ref in recvs:
+        total = total + ref[0:n].astype(F32)
+    if len(refs) > zcount:
+        bias_ref, block_ref, out_bias = refs[zcount - 1 :]
+        bias = bias_ref[...]
+        for ref in recvs:
+            bias = bias + both(ref[n : n + 2])
+        out_bias[...] = bias
+    else:
+        block_ref = refs[-1]
+    block_ref[...] = total.astype(BF)
+
+
+def normal_kernel(zcount, *refs):
+    sources, out_ref = refs[:4], refs[4]
+    if len(refs) > 5:
+        bias_ref, out_ref, out_bias = refs[4:]
+        bias = bias_ref[...]
+        bias_mean = jnp.mean(bias * bias, keepdims=True)
+        out_bias[...] = bias * lax.rsqrt(bias_mean + 1e-06)
     t, p = lax.axis_index("tile"), lax.axis_index("dp")
-    n = blocks[0].shape[0] // 2
+    n = sources[0].shape[0] // zcount
     size = n // 9
-    for which, out_ref in enumerate((second_ref, first_ref)):
-        square = None
-        for ref in blocks:
-            v = ref[which * n : (which + 1) * n].astype(F32)
-            square = v * v if square is None else square + v * v
-        mean = jnp.sum(square, keepdims=True) / (9 * out_ref.shape[1] * out_ref.shape[2])
-        scale = lax.rsqrt(mean + 1e-06)
-        for index, ref in enumerate(blocks):
-            group, j = index // zcount, index % zcount
-            block = (p ^ (group // 2)) * 2 + ((t % 2) ^ (group % 2))
+    square = None
+    for ref in sources:
+        for j in range(zcount):
+            v = ref[j * n : (j + 1) * n].astype(F32)
+            part = jnp.sum(v * v, axis=0, keepdims=True)
+            square = part if square is None else square + part
+    mean = jnp.sum(square, keepdims=True) / (9 * out_ref.shape[1] * out_ref.shape[2])
+    scale = lax.rsqrt(mean + 1e-06)
+    for group, ref in enumerate(sources):
+        block = (p ^ (group // 2)) * 2 + ((t % 2) ^ (group % 2))
+        for j in range(zcount):
             at = pl.ds(pl.multiple_of((block * zcount + ((t // 2) ^ j)) * size, size), size)
             for tap in range(9):
-                row = which * n + tap * size
+                row = j * n + tap * size
                 out_ref[tap, at] = ref[row : row + size].astype(F32) * scale
-    total = bias_sum_ref[...]
-    bias_mean = jnp.mean(total * total, keepdims=True)
-    bias_ref[...] = total * lax.rsqrt(bias_mean + 1e-06)
 
 
 def call(kernel, out_shapes, scratch=(), smem_first=False, limit=16):
@@ -512,7 +564,7 @@
     def send_message(messages, k):
         return messages[k] if k == 0 else lax.ppermute(messages[k], "tile", pairs[k])
 
-    messages = [send_message(messages, k) for k in range(tiles + 1)]
+    messages = [send_message(messages, k) for k in range(tiles)]
     half = channels // 2
     wide = 9 * channels
     frame = (rows + 2, 6, face + 16, channels)
@@ -523,9 +575,10 @@
             ((9, half, channels), F32),
             ((9, half, channels), BF),
             ((9, half, channels), F32),
-            ((1, channels), F32),
             (planes, BF),
             (planes, BF),
+            ((1, channels), F32),
+            ((EXTRA, channels), BF),
         ]
         + msg_shapes,
         [
@@ -541,12 +594,12 @@
         smem_first=True,
         limit=LIMIT,
     )(edge_partner, x, d, w1s, bias.reshape(1, channels), w2t, *messages)
-    send1, keep1, send2, keep2, bias_sum, hidden, inner = outs[:7]
-    packed = list(outs[7:])
-    bias_sum = lax.psum(bias_sum, ("tile", "dp"))
+    send1, keep1, send2, keep2, hidden, inner, bias_sum, send_bias = outs[:8]
+    packed = list(outs[8:])
 
     zcount = tiles // 2
-    block = (18 * half // tiles, channels)
+    n = 9 * half // tiles
+    one = ((1, channels), F32)
     barrier = lax.optimization_barrier
 
     def along_y(v):
@@ -555,42 +608,64 @@
     def along_z(v, j):
         return lax.ppermute(v, "tile", [(i, i ^ (2 * j)) for i in range(tiles)])
 
+    def sum_dp(keep, recv, *bias):
+        extra = EXTRA if bias else 0
+        return call(
+            functools.partial(half_kernel, zcount),
+            [((zcount, n, channels), F32), ((zcount * n + extra, channels), BF)] + [one] * bool(bias),
+        )(keep, recv, *bias)
+
+    def sum_y(keep, recv, *bias):
+        extra = EXTRA if bias else 0
+        keep, *out = call(
+            functools.partial(block_kernel, zcount),
+            [((n, channels), F32)] + [((n + extra, channels), BF)] * (zcount - 1) + [one] * bool(bias),
+            [((zcount, n, channels), F32)],
+        )(keep, recv, *bias)
+        return keep, out[: zcount - 1], out[zcount - 1 :]
+
+    def sum_z(keep, recvs, *bias):
+        return call(
+            functools.partial(last_kernel, zcount), [((n, channels), BF)] + [one] * bool(bias)
+        )(keep, *recvs, *bias)
+
     early = [k for k in range(2, tiles - 1) if k % 2 == 0]
     middle = [k for k in range(1, tiles - 1) if k % 2 == 1]
-    late = [tiles - 1, tiles]
     messages = list(packed)
 
-    keep, *sends = call(
-        functools.partial(half_kernel, zcount), [((zcount,) + block, F32)] + [(block, BF)] * zcount
-    )(keep2, keep1, swap_dp(send2), swap_dp(send1))
-    recvs = [along_y(v) for v in sends]
-    got = [send_message(packed, k) for k in early]
-    recvs, got = barrier((recvs, got))
+    keep2, send2 = sum_dp(keep2, swap_dp(send2))
+    recv2 = along_y(send2)
+    keep1, send1, bias_sum = sum_dp(keep1, swap_dp(send1), bias_sum, swap_dp(send_bias))
+    recv1 = along_y(send1)
+    got = [lax.ppermute(packed[k], "tile", pairs[k]) for k in early]
+
+    keep2, sends2, _ = sum_y(keep2, recv2)
+    recvs2 = [along_z(v, j + 1) for j, v in enumerate(sends2)]
+    recv1, got = barrier((recv1, got))
     for k, v in zip(early, got):
         messages[k] = v
 
-    keep, *sends = call(
-        functools.partial(block_kernel, zcount),
-        [(block, F32)] + [(block, BF)] * (zcount - 1),
-        [((zcount,) + block, F32)],
-    )(keep, *recvs)
-    sends, todo = barrier((sends, [packed[k] for k in middle]))
-    recvs = [along_z(v, j + 1) for j, v in enumerate(sends)]
+    keep1, sends1, (bias_sum,) = sum_y(keep1, recv1, bias_sum)
+    sends1, todo = barrier((sends1, [packed[k] for k in middle]))
+    recvs1 = [along_z(v, j + 1) for j, v in enumerate(sends1)]
     got = [lax.ppermute(v, "tile", pairs[k]) for k, v in zip(middle, todo)]
-    recvs, got = barrier((recvs, got))
+
+    (own2,) = sum_z(keep2, recvs2)
+    own2 = [own2] + [along_z(own2, j) for j in range(1, zcount)]
+    recvs1, got = barrier((recvs1, got))
     for k, v in zip(middle, got):
         messages[k] = v
 
-    (own,) = call(last_kernel, [(block, BF)])(keep, *recvs)
-    own, todo = barrier((own, [packed[k] for k in late]))
-    own = [own] + [along_z(own, j) for j in range(1, zcount)]
-    got = [lax.ppermute(v, "tile", pairs[k]) for k, v in zip(late, todo)]
-    own[-1], got = barrier((own[-1], got))
-    for k, v in zip(late, got):
-        messages[k] = v
-    other = [along_y(v) for v in own]
-    blocks = own + other
-    blocks = blocks + [swap_dp(v) for v in blocks]
+    own1, bias_sum = sum_z(keep1, recvs1, bias_sum)
+    own1, last = barrier((own1, packed[tiles - 1]))
+    own1 = [own1] + [along_z(own1, j) for j in range(1, zcount)]
+    last = lax.ppermute(last, "tile", pairs[tiles - 1])
+    own2 = jnp.concatenate(own2, axis=0)
+    other2 = along_y(own2)
+    own1[-1], messages[tiles - 1] = barrier((own1[-1], last))
+    own1 = jnp.concatenate(own1, axis=0)
+    other1 = along_y(own1)
+    own1, messages = barrier((own1, messages))
     state, grad = call(
         functools.partial(second_kernel, dm),
         [(planes, BF), (planes, F32)],
@@ -605,11 +680,13 @@
         smem_first=True,
         limit=LIMIT,
     )(edge_partner, x, d, hidden, inner, w1t, w2, *messages)
-    second_step, first_step, bias_step = call(
-        functools.partial(normal_kernel, zcount),
-        [(taps, F32)] * 2 + [((1, channels), F32)],
-        limit=24,
-    )(bias_sum, *blocks)
+    other1, state, grad = barrier((other1, state, grad))
+    (second_step,) = call(functools.partial(normal_kernel, zcount), [(taps, F32)])(
+        own2, other2, swap_dp(own2), swap_dp(other2)
+    )
+    first_step, bias_step = call(functools.partial(normal_kernel, zcount), [(taps, F32), one])(
+        own1, other1, swap_dp(own1), swap_dp(other1), bias_sum
+    )
     return (
         state.reshape(initial_state.shape),
         grad.reshape(initial_state.shape),

time: 160 us -> 109 us (0.68)
  blocking collectives: 32.1 us -> 0 us
  local copies, waits for them, and re-layouts: 19.1 us -> 5.22 us
  starting transfers between devices: 51.6 us -> 49.5 us
    psum x1 -> x0, blocking collectives: 32.1 us -> none  [on_device(): bias_sum = lax.psum(bias_sum, ('tile', 'dp'))]
    unnamed x73 -> x20, local copies, waits for them, and re-layouts: 19.1 us -> 5.21 us
    ppermute x6 -> x12, starting transfers between devices: 4.39 us -> 17.8 us  [along_z(): return lax.ppermute(v, 'tile', [(i, i ^ 2 * j) for i in range(tiles)])]
    ppermute x11 -> x7, starting transfers between devices: 25.1 us -> 15.7 us  [send_message(): lax.ppermute(messages[k], 'tile', pairs[k])]
    ppermute x8 -> x4, starting transfers between devices: 10.9 us -> 2.32 us  [along_y(): return lax.ppermute(v, 'tile', [(i, i ^ 1) for i in range(tiles)])]
    ppermute x3, waiting for transfers between devices: 13.2 us -> 4.74 us  [on_device(): got = [lax.ppermute(v, 'tile', pairs[k]) for k, v in zip(middle, todo)]]
    ppermute x2 -> x4, waiting for transfers between devices: 2.12 us -> 8.29 us  [the longest x1 4.33 us: on_device(): last = lax.ppermute(last, 'tile', pairs[tiles - 1])]
    ppermute x11 -> x7, waiting for transfers between devices: 9.51 us -> 3.7 us  [send_message(): lax.ppermute(messages[k], 'tile', pairs[k])]
  transfers between devices with their start and end apart: 40 -> 37, of which waited for: 11 -> 13; matrix products, arithmetic and copies ran while one was open for 0% -> 0% of each run, Pallas kernels for 4% -> 8%
where the time goes in v8:
time: 109 us; the launch traced here: 108 us
  starting transfers between devices  49.5 us (45%)
  waiting for transfers between devices  32.5 us (30%)
  Pallas kernels  20.3 us (19%)
  local copies, waits for them, and re-layouts  5.22 us (5%)
    pallas_call x12, Pallas kernels, run(): pl.pallas_call(kernel, out_shape=[jax.ShapeDtypeStruct(s, dt) for s, dt i...  20.3 us
    ppermute x12, starting transfers between devices, along_z(): return lax.ppermute(v, 'tile', [(i, i ^ 2 * j) for i in range(tiles)])  17.8 us
    ppermute x7, starting transfers between devices, send_message(): lax.ppermute(messages[k], 'tile', pairs[k])  15.7 us
    ppermute x12, waiting for transfers between devices, along_z(): return lax.ppermute(v, 'tile', [(i, i ^ 2 * j) for i in range(tiles)])  8.06 us
    ppermute x3, starting transfers between devices, on_device(): got = [lax.ppermute(v, 'tile', pairs[k]) for k, v in zip(middle, todo)]  5.37 us
    unnamed x20, local copies, waits for them, and re-layouts  5.21 us
    ppermute x3, starting transfers between devices, on_device(): got = [lax.ppermute(packed[k], 'tile', pairs[k]) for k in early]  4.95 us
    ppermute x3, waiting for transfers between devices, on_device(): got = [lax.ppermute(v, 'tile', pairs[k]) for k, v in zip(middle, todo)]  4.74 us
  transfers between devices with their start and end apart: 37, of which 13 were waited for; matrix products, arithmetic and copies ran while one was open for 0% of the time, Pallas kernels for 8%

profile of v8, /device:TPU:0, one launch (start us, length us, event | category | flops | bytes accessed | tf_op | source)
XLA Modules:
  0.0 108.4 jit_solution(10175447724723589117)
XLA Ops:
  0.6 0.8 copy.12.ep
  1.4 0.9 copy-done.2
  2.3 0.9 copy-done.4
  3.3 2.0 %shard_map.102 = (bf16[2,48,256]{2,1,0:T(8,128)(2,1)S(1)}, bf16[2,192,256]{2,1,0:T(8,128)(2,1)S(1)}, bf16[2,48,256]{2,1,0:T(8,128)(2,1)S(1)}, bf16[2,48,256]{2,1...) custom-call(s32[6,4]{1,0:T(8,128)S(1)} %copy.12.ep, ...), custom_call_target="tpu_custom_call" | custom-call | tf_op jit(solution)/shard_map/pallas_call | solution.py:526
  5.3 3.0 %collective-permute-start = (bf16[2,192,256]{2,1,0:T(8,128)(2,1)S(1)}, bf16[2,192,256]{2,1,0:T(8,128)(2,1)S(1)}, u32[]{:S(2)}, u32[]{:S(2)}) collective-permute-start(bf16[2,192,256]{2,1,0:T(8,128)(2,1)S(1)} %get-tuple-element.87), channel_id=1, source_target_pairs={{0,2},{2,0},{4,6},{6,4},{8,10},{10,8},{12,14},{14,12},{1,3},{3,1},... | collective-permute-start | bytes 589832 | tf_op jit(solution)/shard_map/ppermute | solution.py:565
  8.3 3.5 %collective-permute-start.6 = (bf16[2,192,256]{2,1,0:T(8,128)(2,1)S(1)}, bf16[2,192,256]{2,1,0:T(8,128)(2,1)S(1)}, u32[]{:S(2)}, u32[]{:S(2)}) collective-permute-start(bf16[2,192,256]{2,1,0:T(8,128)(2,1)S(1)} %get-tuple-element.93), channel_id=1, source_target_pairs={{0,14},{2,4},{4,2},{6,8},{8,6},{10,12},{12,10},{14,0},{1,15},{3,5}... | collective-permute-start | bytes 589832 | tf_op jit(solution)/shard_map/ppermute | solution.py:565
  11.8 1.9 %collective-permute-start.1 = (bf16[2,48,256]{2,1,0:T(8,128)(2,1)S(1)}, bf16[2,48,256]{2,1,0:T(8,128)(2,1)S(1)}, u32[]{:S(2)}, u32[]{:S(2)}) collective-permute-start(bf16[2,48,256]{2,1,0:T(8,128)(2,1)S(1)} %get-tuple-element.88), channel_id=1, source_target_pairs={{0,4},{4,0},{10,14},{14,10},{1,5},{5,1},{11,15},{15,11},{16,20},{2... | collective-permute-start | bytes 147464 | tf_op jit(solution)/shard_map/ppermute | solution.py:565
  13.7 0.1 collective-permute-start.2
  13.8 3.5 %collective-permute-start.3 = (bf16[2,48,256]{2,1,0:T(8,128)(2,1)S(1)}, bf16[2,48,256]{2,1,0:T(8,128)(2,1)S(1)}, u32[]{:S(2)}, u32[]{:S(2)}) collective-permute-start(bf16[2,48,256]{2,1,0:T(8,128)(2,1)S(1)} %get-tuple-element.90), channel_id=1, source_target_pairs={{0,8},{2,10},{4,12},{6,14},{8,0},{10,2},{12,4},{14,6},{1,9},{3,11}... | collective-permute-start | bytes 147464 | tf_op jit(solution)/shard_map/ppermute | solution.py:565
  17.3 1.0 collective-permute-done.1.refs_2_
  18.4 3.5 %collective-permute-start.4 = (bf16[2,48,256]{2,1,0:T(8,128)(2,1)S(1)}, bf16[2,48,256]{2,1,0:T(8,128)(2,1)S(1)}, u32[]{:S(2)}, u32[]{:S(2)}) collective-permute-start(bf16[2,48,256]{2,1,0:T(8,128)(2,1)S(1)} %get-tuple-element.91), channel_id=1, source_target_pairs={{0,10},{4,14},{10,0},{14,4},{1,11},{5,15},{11,1},{15,5},{16,26},{2... | collective-permute-start | bytes 147464 | tf_op jit(solution)/shard_map/ppermute | solution.py:565
  21.9 0.1 collective-permute-start.5
  22.0 0.0 copy-start
  22.0 1.3 %copy-done = bf16[3,3,256,256]{3,2,1,0:T(8,128)(2,1)S(1)} copy-done((bf16[3,3,256,256]{3,2,1,0:T(8,128)(2,1)S(1)}, bf16[3,3,256,256]{3,2,1,0:T(8,128)(2,1)}, u32[]{:S(2)}) %copy-start) | copy-done | bytes 1179672
  23.3 1.3 %copy-done.6 = bf16[3,3,256,256]{3,2,1,0:T(8,128)(2,1)S(1)} copy-done((bf16[3,3,256,256]{3,2,1,0:T(8,128)(2,1)S(1)}, bf16[3,3,256,256]{3,2,1,0:T(8,128)(2,1)}, u32[]{:S(2)}) %copy-start.6) | copy-done | bytes 1179672
  24.5 0.7 shard_map.101
  25.2 0.9 collective-permute-done.4.refs_5_
  26.1 1.8 %collective-permute-done.5.refs_6_ = bf16[2,48,256]{2,1,0:T(8,128)(2,1)S(1)} collective-permute-done((bf16[2,48,256]{2,1,0:T(8,128)(2,1)S(1)}, bf16[2,48,256]{2,1,0:T(8,128)(2,1)S(1)}, u32[]{:S(2)}, u32[]{:S(2)}) %collective-permute-start.5) | collective-permute-done | bytes 49184 | tf_op jit(solution)/shard_map/ppermute | solution.py:565
  27.9 8.1 %shard_map.103 = (bf16[9,128,256]{2,1,0:T(8,128)(2,1)S(1)}, f32[9,128,256]{2,1,0:T(8,128)S(1)}, bf16[9,128,256]{2,1,0:T(8,128)(2,1)S(1)}, f32[9,128,256]{2,1,0:T...) custom-call(s32[6,4]{1,0:T(8,128)S(1)} %copy.12.ep, ...), custom_call_target="tpu_custom_call" | custom-call | tf_op jit(solution)/shard_map/pallas_call | solution.py:526
  36.0 0.1 collective-permute-start.26
  36.1 0.5 collective-permute-start.7
  36.6 1.5 %collective-permute-done.26.recv_ref = bf16[9,128,256]{2,1,0:T(8,128)(2,1)S(1)} collective-permute-done((bf16[9,128,256]{2,1,0:T(8,128)(2,1)S(1)}, bf16[9,128,256]{2,1,0:T(8,128)(2,1)S(1)}, u32[]{:S(2)}, u32[]{:S(2)}) %collective-permute-start.26) | collective-permute-done | bytes 589856 | tf_op jit(solution)/shard_map/ppermute | solution.py:540
  38.1 0.1 shard_map.109
  38.2 1.7 %collective-permute-start.27 = (bf16[576,256]{1,0:T(8,128)(2,1)S(1)}, bf16[576,256]{1,0:T(8,128)(2,1)S(1)}, u32[]{:S(2)}, u32[]{:S(2)}) collective-permute-start(bf16[576,256]{1,0:T(8,128)(2,1)S(1)} %get-tuple-element.158), channel_id=1, source_target_pairs={{0,2},{2,0},{4,6},{6,4},{8,10},{10,8},{12,14},{14,12},{1,3},{3,1},... | collective-permute-start | bytes 884744 | tf_op jit(solution)/shard_map/ppermute | solution.py:606
  39.9 1.2 %collective-permute-done.8.refs_1_ = bf16[8,256]{1,0:T(8,128)(2,1)S(1)} collective-permute-done((bf16[8,256]{1,0:T(8,128)(2,1)S(1)}, bf16[8,256]{1,0:T(8,128)(2,1)S(1)}, u32[]{:S(2)}, u32[]{:S(2)}) %collective-permute-start.8) | collective-permute-done | bytes 4128 | tf_op jit(solution)/shard_map/ppermute | solution.py:540
  41.0 0.1 shard_map.104
  41.1 0.5 collective-permute-start.9
  41.6 2.8 %collective-permute-start.10 = (bf16[2,48,256]{2,1,0:T(8,128)(2,1)S(1)}, bf16[2,48,256]{2,1,0:T(8,128)(2,1)S(1)}, u32[]{:S(2)}, u32[]{:S(2)}) collective-permute-start(bf16[2,48,256]{2,1,0:T(8,128)(2,1)S(1)} %get-tuple-element.100), channel_id=1, source_target_pairs={{0,4},{4,0},{10,14},{14,10},{1,5},{5,1},{11,15},{15,11},{16,20},{2... | collective-permute-start | bytes 147464 | tf_op jit(solution)/shard_map/ppermute | solution.py:640
  44.5 0.1 collective-permute-start.11
  44.5 3.6 %collective-permute-done.27.recv_ref = bf16[576,256]{1,0:T(8,128)(2,1)S(1)} collective-permute-done((bf16[576,256]{1,0:T(8,128)(2,1)S(1)}, bf16[576,256]{1,0:T(8,128)(2,1)S(1)}, u32[]{:S(2)}, u32[]{:S(2)}) %collective-permute-start.27) | collective-permute-done | bytes 294944 | tf_op jit(solution)/shard_map/ppermute | solution.py:606
  48.1 0.1 shard_map.110
  48.2 1.0 collective-permute-start.28
  49.2 1.7 %collective-permute-start.29 = (bf16[144,256]{1,0:T(8,128)(2,1)S(1)}, bf16[144,256]{1,0:T(8,128)(2,1)S(1)}, u32[]{:S(2)}, u32[]{:S(2)}) collective-permute-start(bf16[144,256]{1,0:T(8,128)(2,1)S(1)} %get-tuple-element.161), channel_id=1, source_target_pairs={{0,8},{2,10},{4,12},{6,14},{8,0},{10,2},{12,4},{14,6},{1,9},{3,11}... | collective-permute-start | bytes 221192 | tf_op jit(solution)/shard_map/ppermute | solution.py:609
  50.9 1.8 %collective-permute-start.30 = (bf16[144,256]{1,0:T(8,128)(2,1)S(1)}, bf16[144,256]{1,0:T(8,128)(2,1)S(1)}, u32[]{:S(2)}, u32[]{:S(2)}) collective-permute-start(bf16[144,256]{1,0:T(8,128)(2,1)S(1)} %get-tuple-element.162), channel_id=1, source_target_pairs={{0,12},{2,14},{4,8},{6,10},{8,4},{10,6},{12,0},{14,2},{1,13},{3,15... | collective-permute-start | bytes 221192 | tf_op jit(solution)/shard_map/ppermute | solution.py:609
  52.7 2.0 %collective-permute-start.12 = (bf16[2,48,256]{2,1,0:T(8,128)(2,1)S(1)}, bf16[2,48,256]{2,1,0:T(8,128)(2,1)S(1)}, u32[]{:S(2)}, u32[]{:S(2)}) collective-permute-start(bf16[2,48,256]{2,1,0:T(8,128)(2,1)S(1)} %get-tuple-element.102), channel_id=1, source_target_pairs={{0,12},{2,14},{4,8},{6,10},{8,4},{10,6},{12,0},{14,2},{1,13},{3,15... | collective-permute-start | bytes 147464 | tf_op jit(solution)/shard_map/ppermute | solution.py:640
  54.7 4.0 %collective-permute-done.12.refs_6_ = bf16[2,48,256]{2,1,0:T(8,128)(2,1)S(1)} collective-permute-done((bf16[2,48,256]{2,1,0:T(8,128)(2,1)S(1)}, bf16[2,48,256]{2,1,0:T(8,128)(2,1)S(1)}, u32[]{:S(2)}, u32[]{:S(2)}) %collective-permute-start.12) | collective-permute-done | bytes 49184 | tf_op jit(solution)/shard_map/ppermute | solution.py:640
  58.6 0.1 shard_map.105
  58.8 0.0 copy-start.1
  58.8 1.6 %collective-permute-start.16 = (bf16[2,192,256]{2,1,0:T(8,128)(2,1)S(1)}, bf16[2,192,256]{2,1,0:T(8,128)(2,1)S(1)}, u32[]{:S(2)}, u32[]{:S(2)}) collective-permute-start(bf16[2,192,256]{2,1,0:T(8,128)(2,1)S(1)} %get-tuple-element.115), channel_id=1, source_target_pairs={{0,2},{2,0},{4,6},{6,4},{8,10},{10,8},{12,14},{14,12},{1,3},{3,1},... | collective-permute-start | bytes 589832 | tf_op jit(solution)/shard_map/ppermute | solution.py:651
  60.4 2.6 %collective-permute-start.33 = (bf16[144,256]{1,0:T(8,128)(2,1)S(1)}, bf16[144,256]{1,0:T(8,128)(2,1)S(1)}, u32[]{:S(2)}, u32[]{:S(2)}) collective-permute-start(bf16[144,256]{1,0:T(8,128)(2,1)S(1)} %shard_map.111), channel_id=1, source_target_pairs={{0,12},{2,14},{4,8},{6,10},{8,4},{10,6},{12,0},{14,2},{1,13},{3,15... | collective-permute-start | bytes 221192 | tf_op jit(solution)/shard_map/ppermute | solution.py:609
  63.1 1.8 %collective-permute-start.31 = (bf16[144,256]{1,0:T(8,128)(2,1)S(1)}, bf16[144,256]{1,0:T(8,128)(2,1)S(1)}, u32[]{:S(2)}, u32[]{:S(2)}) collective-permute-start(bf16[144,256]{1,0:T(8,128)(2,1)S(1)} %shard_map.111), channel_id=1, source_target_pairs={{0,4},{2,6},{4,0},{6,2},{8,12},{10,14},{12,8},{14,10},{1,5},{3,7},... | collective-permute-start | bytes 221192 | tf_op jit(solution)/shard_map/ppermute | solution.py:609
  64.9 0.3 collective-permute-start.17
  65.2 4.7 %collective-permute-done.17.refs_3_ = bf16[2,48,256]{2,1,0:T(8,128)(2,1)S(1)} collective-permute-done((bf16[2,48,256]{2,1,0:T(8,128)(2,1)S(1)}, bf16[2,48,256]{2,1,0:T(8,128)(2,1)S(1)}, u32[]{:S(2)}, u32[]{:S(2)}) %collective-permute-start.17) | collective-permute-done | bytes 49184 | tf_op jit(solution)/shard_map/ppermute | solution.py:651
  69.9 3.5 %collective-permute-start.18 = (bf16[2,48,256]{2,1,0:T(8,128)(2,1)S(1)}, bf16[2,48,256]{2,1,0:T(8,128)(2,1)S(1)}, u32[]{:S(2)}, u32[]{:S(2)}) collective-permute-start(bf16[2,48,256]{2,1,0:T(8,128)(2,1)S(1)} %get-tuple-element.117), channel_id=1, source_target_pairs={{0,10},{4,14},{10,0},{14,4},{1,11},{5,15},{11,1},{15,5},{16,26},{2... | collective-permute-start | bytes 147464 | tf_op jit(solution)/shard_map/ppermute | solution.py:651
  73.4 1.5 %collective-permute-start.13 = (bf16[152,256]{1,0:T(8,128)(2,1)S(1)}, bf16[152,256]{1,0:T(8,128)(2,1)S(1)}, u32[]{:S(2)}, u32[]{:S(2)}) collective-permute-start(bf16[152,256]{1,0:T(8,128)(2,1)S(1)} %get-tuple-element.112), channel_id=1, source_target_pairs={{0,4},{2,6},{4,0},{6,2},{8,12},{10,14},{12,8},{14,10},{1,5},{3,7},... | collective-permute-start | bytes 233480 | tf_op jit(solution)/shard_map/ppermute | solution.py:609
  74.9 0.9 collective-permute-start.14
  75.8 2.1 %collective-permute-start.15 = (bf16[152,256]{1,0:T(8,128)(2,1)S(1)}, bf16[152,256]{1,0:T(8,128)(2,1)S(1)}, u32[]{:S(2)}, u32[]{:S(2)}) collective-permute-start(bf16[152,256]{1,0:T(8,128)(2,1)S(1)} %get-tuple-element.114), channel_id=1, source_target_pairs={{0,12},{2,14},{4,8},{6,10},{8,4},{10,6},{12,0},{14,2},{1,13},{3,15... | collective-permute-start | bytes 233480 | tf_op jit(solution)/shard_map/ppermute | solution.py:609
  77.9 0.0 collective-permute-done.18.refs_5_
  77.9 0.2 collective-permute-start.34
  78.1 6.2 %collective-permute-done.14.refs_1_ = bf16[152,256]{1,0:T(8,128)(2,1)S(1)} collective-permute-done((bf16[152,256]{1,0:T(8,128)(2,1)S(1)}, bf16[152,256]{1,0:T(8,128)(2,1)S(1)}, u32[]{:S(2)}, u32[]{:S(2)}) %collective-permute-start.14) | collective-permute-done | bytes 77856 | tf_op jit(solution)/shard_map/ppermute | solution.py:609
  84.3 0.8 collective-permute-start.21
  85.1 3.0 %collective-permute-start.20 = (bf16[144,256]{1,0:T(8,128)(2,1)S(1)}, bf16[144,256]{1,0:T(8,128)(2,1)S(1)}, u32[]{:S(2)}, u32[]{:S(2)}) collective-permute-start(bf16[144,256]{1,0:T(8,128)(2,1)S(1)} %get-tuple-element.124), channel_id=1, source_target_pairs={{0,8},{2,10},{4,12},{6,14},{8,0},{10,2},{12,4},{14,6},{1,9},{3,11}... | collective-permute-start | bytes 221192 | tf_op jit(solution)/shard_map/ppermute | solution.py:609
  88.1 0.7 collective-permute-start.19
  88.8 2.1 %collective-permute-start.22 = (bf16[2,192,256]{2,1,0:T(8,128)(2,1)S(1)}, bf16[2,192,256]{2,1,0:T(8,128)(2,1)S(1)}, u32[]{:S(2)}, u32[]{:S(2)}) collective-permute-start(bf16[2,192,256]{2,1,0:T(8,128)(2,1)S(1)} %get-tuple-element.125), channel_id=1, source_target_pairs={{0,14},{2,4},{4,2},{6,8},{8,6},{10,12},{12,10},{14,0},{1,15},{3,5}... | collective-permute-start | bytes 589832 | tf_op jit(solution)/shard_map/ppermute | solution.py:662
  90.9 1.9 %collective-permute-done.19 = bf16[144,256]{1,0:T(8,128)(2,1)S(1)} collective-permute-done((bf16[144,256]{1,0:T(8,128)(2,1)S(1)}, bf16[144,256]{1,0:T(8,128)(2,1)S(1)}, u32[]{:S(2)}, u32[]{:S(2)}) %collective-permute-start.19) | collective-permute-done | bytes 73760 | tf_op jit(solution)/shard_map/ppermute | solution.py:609
  92.8 4.3 %collective-permute-done.22.refs_7_ = bf16[2,192,256]{2,1,0:T(8,128)(2,1)S(1)} collective-permute-done((bf16[2,192,256]{2,1,0:T(8,128)(2,1)S(1)}, bf16[2,192,256]{2,1,0:T(8,128)(2,1)S(1)}, u32[]{:S(2)}, u32[]{:S(2)}) %collective-permute-start.22) | collective-permute-done | bytes 196640 | tf_op jit(solution)/shard_map/ppermute | solution.py:662
  97.1 0.1 collective-permute-start.35
  97.2 0.5 collective-permute-start.24
  97.7 5.5 %shard_map.107 = (bf16[18,24,256]{2,1,0:T(8,128)(2,1)}, f32[18,24,256]{2,1,0:T(8,128)}) custom-call(s32[6,4]{1,0:T(8,128)S(1)} %copy.12.ep, bf16[18,24,256]{2,1,0:T(8,128)(2,1)S(1)} %bitcast.20, bf16[18,24,256]{2,1,0:T(8,128)(2,1)S(1)} %bitcast.23, bf16[18,24,256]{2,1,0:T(8,128)(2,1)S(1)} %get-tuple-element.127.hid_ref, ...), custom_call_target="tpu_custom_call" | custom-call | tf_op jit(solution)/shard_map/pallas_call | solution.py:526
  103.3 0.1 collective-permute-start.36
  103.4 0.5 collective-permute-done.23.refs_1_
  103.9 1.0 collective-permute-done.36.refs_3_
  104.9 1.8 %shard_map.112 = f32[9,256,256]{2,1,0:T(8,128)} custom-call(bf16[576,256]{1,0:T(8,128)(2,1)S(1)} %pad_maximum_fusion.refs_0_, bf16[576,256]{1,0:T(8,128)(2,1)S(1)} %collective-permute-done.34.refs_1_, bf16[576,256]{1,0:T(8,128)(2,1)S(1)} %collective-permute-done.35.refs_2_, bf16[576,256]{1,0:T(8,128)(2,1)S(1)} %collective-permute-done.36.refs_3_), custom_call_target="tpu_custom_call" | custom-call | tf_op jit(solution)/shard_map/pallas_call | solution.py:526
  106.6 1.8 %shard_map.108 = (f32[9,256,256]{2,1,0:T(8,128)}, f32[1,256]{1,0:T(1,128)}) custom-call(bf16[576,256]{1,0:T(8,128)(2,1)S(1)} %constant_dynamic-update-slice_fusion.refs_0_, bf16[576,256]{1,0:T(8,128)(2,1)S(1)} %collective-permute-done.23.refs_1_, bf16[576,256]{1,0:T(8,128)(2,1)S(1)} %collective-permute-done.24.refs_2_, ...), custom_call_target="tpu_custom_call" | custom-call | tf_op jit(solution)/shard_map/pallas_call | solution.py:526
  (44 shorter events, 0.2 us)
Async XLA Ops:
  1.4 0.9 copy-start.2
  2.3 0.9 copy-start.4
  5.3 22.6 %collective-permute-start = (bf16[2,192,256]{2,1,0:T(8,128)(2,1)S(1)}, bf16[2,192,256]{2,1,0:T(8,128)(2,1)S(1)}, u32[]{:S(2)}, u32[]{:S(2)}) collective-permute-start(bf16[2,192,256]{2,1,0:T(8,128)(2,1)S(1)} %get-tuple-element.87), channel_id=1, source_target_pairs={{0,2},{2,0},{4,6},{6,4},{8,10},{10,8},{12,14},{14,12},{1,3},{3,1},... | collective-permute-start | bytes 589832 | tf_op jit(solution)/shard_map/ppermute | solution.py:565
  8.3 19.6 %collective-permute-start.6 = (bf16[2,192,256]{2,1,0:T(8,128)(2,1)S(1)}, bf16[2,192,256]{2,1,0:T(8,128)(2,1)S(1)}, u32[]{:S(2)}, u32[]{:S(2)}) collective-permute-start(bf16[2,192,256]{2,1,0:T(8,128)(2,1)S(1)} %get-tuple-element.93), channel_id=1, source_target_pairs={{0,14},{2,4},{4,2},{6,8},{8,6},{10,12},{12,10},{14,0},{1,15},{3,5}... | collective-permute-start | bytes 589832 | tf_op jit(solution)/shard_map/ppermute | solution.py:565
  11.8 6.5 %collective-permute-start.1 = (bf16[2,48,256]{2,1,0:T(8,128)(2,1)S(1)}, bf16[2,48,256]{2,1,0:T(8,128)(2,1)S(1)}, u32[]{:S(2)}, u32[]{:S(2)}) collective-permute-start(bf16[2,48,256]{2,1,0:T(8,128)(2,1)S(1)} %get-tuple-element.88), channel_id=1, source_target_pairs={{0,4},{4,0},{10,14},{14,10},{1,5},{5,1},{11,15},{15,11},{16,20},{2... | collective-permute-start | bytes 147464 | tf_op jit(solution)/shard_map/ppermute | solution.py:565
  13.7 8.1 %collective-permute-start.2 = (bf16[2,48,256]{2,1,0:T(8,128)(2,1)S(1)}, bf16[2,48,256]{2,1,0:T(8,128)(2,1)S(1)}, u32[]{:S(2)}, u32[]{:S(2)}) collective-permute-start(bf16[2,48,256]{2,1,0:T(8,128)(2,1)S(1)} %get-tuple-element.89), channel_id=1, source_target_pairs={{0,6},{2,12},{4,10},{6,0},{8,14},{10,4},{12,2},{14,8},{1,7},{3,13}... | collective-permute-start | bytes 147464 | tf_op jit(solution)/shard_map/ppermute | solution.py:565
  13.8 11.4 %collective-permute-start.3 = (bf16[2,48,256]{2,1,0:T(8,128)(2,1)S(1)}, bf16[2,48,256]{2,1,0:T(8,128)(2,1)S(1)}, u32[]{:S(2)}, u32[]{:S(2)}) collective-permute-start(bf16[2,48,256]{2,1,0:T(8,128)(2,1)S(1)} %get-tuple-element.90), channel_id=1, source_target_pairs={{0,8},{2,10},{4,12},{6,14},{8,0},{10,2},{12,4},{14,6},{1,9},{3,11}... | collective-permute-start | bytes 147464 | tf_op jit(solution)/shard_map/ppermute | solution.py:565
  18.4 7.8 %collective-permute-start.4 = (bf16[2,48,256]{2,1,0:T(8,128)(2,1)S(1)}, bf16[2,48,256]{2,1,0:T(8,128)(2,1)S(1)}, u32[]{:S(2)}, u32[]{:S(2)}) collective-permute-start(bf16[2,48,256]{2,1,0:T(8,128)(2,1)S(1)} %get-tuple-element.91), channel_id=1, source_target_pairs={{0,10},{4,14},{10,0},{14,4},{1,11},{5,15},{11,1},{15,5},{16,26},{2... | collective-permute-start | bytes 147464 | tf_op jit(solution)/shard_map/ppermute | solution.py:565
  21.9 6.0 %collective-permute-start.5 = (bf16[2,48,256]{2,1,0:T(8,128)(2,1)S(1)}, bf16[2,48,256]{2,1,0:T(8,128)(2,1)S(1)}, u32[]{:S(2)}, u32[]{:S(2)}) collective-permute-start(bf16[2,48,256]{2,1,0:T(8,128)(2,1)S(1)} %get-tuple-element.92), channel_id=1, source_target_pairs={{0,12},{2,14},{4,8},{6,10},{8,4},{10,6},{12,0},{14,2},{1,13},{3,15... | collective-permute-start | bytes 147464 | tf_op jit(solution)/shard_map/ppermute | solution.py:565
  22.0 1.3 %copy-start = (bf16[3,3,256,256]{3,2,1,0:T(8,128)(2,1)S(1)}, bf16[3,3,256,256]{3,2,1,0:T(8,128)(2,1)}, u32[]{:S(2)}) copy-start(bf16[3,3,256,256]{3,2,1,0:T(8,128)(2,1)} %param.10) | copy-start | bytes 3538948
  23.2 1.3 %copy-start.6 = (bf16[3,3,256,256]{3,2,1,0:T(8,128)(2,1)S(1)}, bf16[3,3,256,256]{3,2,1,0:T(8,128)(2,1)}, u32[]{:S(2)}) copy-start(bf16[3,3,256,256]{3,2,1,0:T(8,128)(2,1)} %param.8) | copy-start | bytes 3538948
  24.5 3.4 %copy-start.3 = (bf16[1,6,3,24,256]{4,3,2,1,0:T(8,128)(2,1)S(1)}, bf16[1,6,3,24,256]{4,3,2,1,0:T(8,128)(2,1)}, u32[]{:S(2)}) copy-start(bf16[1,6,3,24,256]{4,3,2,1,0:T(8,128)(2,1)} %param.6) | copy-start | bytes 663556
  24.5 3.4 %copy-start.5 = (bf16[1,1,6,3,24,256]{5,4,3,2,1,0:T(8,128)(2,1)S(1)}, bf16[1,1,6,3,24,256]{5,4,3,2,1,0:T(8,128)(2,1)}, u32[]{:S(2)}) copy-start(bf16[1,1,6,3,24,256]{5,4,3,2,1,0:T(8,128)(2,1)} %param.7) | copy-start | bytes 663556
  24.5 3.4 %copy-start.7 = (f32[256]{0:T(256)S(1)}, f32[256]{0:T(256)}, u32[]{:S(2)}) copy-start(f32[256]{0:T(256)} %param.9) | copy-start | bytes 3076
  36.0 2.1 %collective-permute-start.26 = (bf16[9,128,256]{2,1,0:T(8,128)(2,1)S(1)}, bf16[9,128,256]{2,1,0:T(8,128)(2,1)S(1)}, u32[]{:S(2)}, u32[]{:S(2)}) collective-permute-start(bf16[9,128,256]{2,1,0:T(8,128)(2,1)S(1)} %get-tuple-element.156), channel_id=1, source_target_pairs={{0,1},{1,0},{2,3},{3,2},{4,5},{5,4},{6,7},{7,6},{8,9},{9,8},{10,11... | collective-permute-start | bytes 1769480 | tf_op jit(solution)/shard_map/ppermute | solution.py:540
  36.1 4.9 %collective-permute-start.7 = (bf16[9,128,256]{2,1,0:T(8,128)(2,1)S(1)}, bf16[9,128,256]{2,1,0:T(8,128)(2,1)S(1)}, u32[]{:S(2)}, u32[]{:S(2)}) collective-permute-start(bf16[9,128,256]{2,1,0:T(8,128)(2,1)S(1)} %get-tuple-element.95), channel_id=1, source_target_pairs={{0,1},{1,0},{2,3},{3,2},{4,5},{5,4},{6,7},{7,6},{8,9},{9,8},{10,11... | collective-permute-start | bytes 1769480 | tf_op jit(solution)/shard_map/ppermute | solution.py:540
  38.2 9.9 %collective-permute-start.27 = (bf16[576,256]{1,0:T(8,128)(2,1)S(1)}, bf16[576,256]{1,0:T(8,128)(2,1)S(1)}, u32[]{:S(2)}, u32[]{:S(2)}) collective-permute-start(bf16[576,256]{1,0:T(8,128)(2,1)S(1)} %get-tuple-element.158), channel_id=1, source_target_pairs={{0,2},{2,0},{4,6},{6,4},{8,10},{10,8},{12,14},{14,12},{1,3},{3,1},... | collective-permute-start | bytes 884744 | tf_op jit(solution)/shard_map/ppermute | solution.py:606
  39.9 1.2 %collective-permute-start.8 = (bf16[8,256]{1,0:T(8,128)(2,1)S(1)}, bf16[8,256]{1,0:T(8,128)(2,1)S(1)}, u32[]{:S(2)}, u32[]{:S(2)}) collective-permute-start(bf16[8,256]{1,0:T(8,128)(2,1)S(1)} %get-tuple-element.97), channel_id=1, source_target_pairs={{0,1},{1,0},{2,3},{3,2},{4,5},{5,4},{6,7},{7,6},{8,9},{9,8},{10,11... | collective-permute-start | bytes 12296 | tf_op jit(solution)/shard_map/ppermute | solution.py:540
  41.1 17.5 %collective-permute-start.9 = (bf16[584,256]{1,0:T(8,128)(2,1)S(1)}, bf16[584,256]{1,0:T(8,128)(2,1)S(1)}, u32[]{:S(2)}, u32[]{:S(2)}) collective-permute-start(bf16[584,256]{1,0:T(8,128)(2,1)S(1)} %get-tuple-element.99), channel_id=1, source_target_pairs={{0,2},{2,0},{4,6},{6,4},{8,10},{10,8},{12,14},{14,12},{1,3},{3,1},... | collective-permute-start | bytes 897032 | tf_op jit(solution)/shard_map/ppermute | solution.py:606
  41.6 9.3 %collective-permute-start.10 = (bf16[2,48,256]{2,1,0:T(8,128)(2,1)S(1)}, bf16[2,48,256]{2,1,0:T(8,128)(2,1)S(1)}, u32[]{:S(2)}, u32[]{:S(2)}) collective-permute-start(bf16[2,48,256]{2,1,0:T(8,128)(2,1)S(1)} %get-tuple-element.100), channel_id=1, source_target_pairs={{0,4},{4,0},{10,14},{14,10},{1,5},{5,1},{11,15},{15,11},{16,20},{2... | collective-permute-start | bytes 147464 | tf_op jit(solution)/shard_map/ppermute | solution.py:640
  44.5 8.2 %collective-permute-start.11 = (bf16[2,48,256]{2,1,0:T(8,128)(2,1)S(1)}, bf16[2,48,256]{2,1,0:T(8,128)(2,1)S(1)}, u32[]{:S(2)}, u32[]{:S(2)}) collective-permute-start(bf16[2,48,256]{2,1,0:T(8,128)(2,1)S(1)} %get-tuple-element.101), channel_id=1, source_target_pairs={{0,8},{2,10},{4,12},{6,14},{8,0},{10,2},{12,4},{14,6},{1,9},{3,11}... | collective-permute-start | bytes 147464 | tf_op jit(solution)/shard_map/ppermute | solution.py:640
  48.2 12.2 %collective-permute-start.28 = (bf16[144,256]{1,0:T(8,128)(2,1)S(1)}, bf16[144,256]{1,0:T(8,128)(2,1)S(1)}, u32[]{:S(2)}, u32[]{:S(2)}) collective-permute-start(bf16[144,256]{1,0:T(8,128)(2,1)S(1)} %get-tuple-element.160), channel_id=1, source_target_pairs={{0,4},{2,6},{4,0},{6,2},{8,12},{10,14},{12,8},{14,10},{1,5},{3,7},... | collective-permute-start | bytes 221192 | tf_op jit(solution)/shard_map/ppermute | solution.py:609
  49.2 11.2 %collective-permute-start.29 = (bf16[144,256]{1,0:T(8,128)(2,1)S(1)}, bf16[144,256]{1,0:T(8,128)(2,1)S(1)}, u32[]{:S(2)}, u32[]{:S(2)}) collective-permute-start(bf16[144,256]{1,0:T(8,128)(2,1)S(1)} %get-tuple-element.161), channel_id=1, source_target_pairs={{0,8},{2,10},{4,12},{6,14},{8,0},{10,2},{12,4},{14,6},{1,9},{3,11}... | collective-permute-start | bytes 221192 | tf_op jit(solution)/shard_map/ppermute | solution.py:609
  50.9 9.5 %collective-permute-start.30 = (bf16[144,256]{1,0:T(8,128)(2,1)S(1)}, bf16[144,256]{1,0:T(8,128)(2,1)S(1)}, u32[]{:S(2)}, u32[]{:S(2)}) collective-permute-start(bf16[144,256]{1,0:T(8,128)(2,1)S(1)} %get-tuple-element.162), channel_id=1, source_target_pairs={{0,12},{2,14},{4,8},{6,10},{8,4},{10,6},{12,0},{14,2},{1,13},{3,15... | collective-permute-start | bytes 221192 | tf_op jit(solution)/shard_map/ppermute | solution.py:609
  52.7 6.0 %collective-permute-start.12 = (bf16[2,48,256]{2,1,0:T(8,128)(2,1)S(1)}, bf16[2,48,256]{2,1,0:T(8,128)(2,1)S(1)}, u32[]{:S(2)}, u32[]{:S(2)}) collective-permute-start(bf16[2,48,256]{2,1,0:T(8,128)(2,1)S(1)} %get-tuple-element.102), channel_id=1, source_target_pairs={{0,12},{2,14},{4,8},{6,10},{8,4},{10,6},{12,0},{14,2},{1,13},{3,15... | collective-permute-start | bytes 147464 | tf_op jit(solution)/shard_map/ppermute | solution.py:640
  58.8 39.0 %copy-start.1 = (bf16[3,3,256,256]{3,2,1,0:T(8,128)(2,1)S(1)}, bf16[3,3,256,256]{3,2,1,0:T(8,128)(2,1)}, u32[]{:S(2)}) copy-start(bf16[3,3,256,256]{3,2,1,0:T(8,128)(2,1)} %param.10) | copy-start | bytes 3538948
  58.8 25.5 %collective-permute-start.16 = (bf16[2,192,256]{2,1,0:T(8,128)(2,1)S(1)}, bf16[2,192,256]{2,1,0:T(8,128)(2,1)S(1)}, u32[]{:S(2)}, u32[]{:S(2)}) collective-permute-start(bf16[2,192,256]{2,1,0:T(8,128)(2,1)S(1)} %get-tuple-element.115), channel_id=1, source_target_pairs={{0,2},{2,0},{4,6},{6,4},{8,10},{10,8},{12,14},{14,12},{1,3},{3,1},... | collective-permute-start | bytes 589832 | tf_op jit(solution)/shard_map/ppermute | solution.py:651
  60.4 12.9 %collective-permute-start.33 = (bf16[144,256]{1,0:T(8,128)(2,1)S(1)}, bf16[144,256]{1,0:T(8,128)(2,1)S(1)}, u32[]{:S(2)}, u32[]{:S(2)}) collective-permute-start(bf16[144,256]{1,0:T(8,128)(2,1)S(1)} %shard_map.111), channel_id=1, source_target_pairs={{0,12},{2,14},{4,8},{6,10},{8,4},{10,6},{12,0},{14,2},{1,13},{3,15... | collective-permute-start | bytes 221192 | tf_op jit(solution)/shard_map/ppermute | solution.py:609
  63.0 11.9 %collective-permute-start.32 = (bf16[144,256]{1,0:T(8,128)(2,1)S(1)}, bf16[144,256]{1,0:T(8,128)(2,1)S(1)}, u32[]{:S(2)}, u32[]{:S(2)}) collective-permute-start(bf16[144,256]{1,0:T(8,128)(2,1)S(1)} %shard_map.111), channel_id=1, source_target_pairs={{0,8},{2,10},{4,12},{6,14},{8,0},{10,2},{12,4},{14,6},{1,9},{3,11}... | collective-permute-start | bytes 221192 | tf_op jit(solution)/shard_map/ppermute | solution.py:609
  63.1 12.8 %collective-permute-start.31 = (bf16[144,256]{1,0:T(8,128)(2,1)S(1)}, bf16[144,256]{1,0:T(8,128)(2,1)S(1)}, u32[]{:S(2)}, u32[]{:S(2)}) collective-permute-start(bf16[144,256]{1,0:T(8,128)(2,1)S(1)} %shard_map.111), channel_id=1, source_target_pairs={{0,4},{2,6},{4,0},{6,2},{8,12},{10,14},{12,8},{14,10},{1,5},{3,7},... | collective-permute-start | bytes 221192 | tf_op jit(solution)/shard_map/ppermute | solution.py:609
  64.9 5.0 %collective-permute-start.17 = (bf16[2,48,256]{2,1,0:T(8,128)(2,1)S(1)}, bf16[2,48,256]{2,1,0:T(8,128)(2,1)S(1)}, u32[]{:S(2)}, u32[]{:S(2)}) collective-permute-start(bf16[2,48,256]{2,1,0:T(8,128)(2,1)S(1)} %get-tuple-element.116), channel_id=1, source_target_pairs={{0,6},{2,12},{4,10},{6,0},{8,14},{10,4},{12,2},{14,8},{1,7},{3,13}... | collective-permute-start | bytes 147464 | tf_op jit(solution)/shard_map/ppermute | solution.py:651
  69.9 8.0 %collective-permute-start.18 = (bf16[2,48,256]{2,1,0:T(8,128)(2,1)S(1)}, bf16[2,48,256]{2,1,0:T(8,128)(2,1)S(1)}, u32[]{:S(2)}, u32[]{:S(2)}) collective-permute-start(bf16[2,48,256]{2,1,0:T(8,128)(2,1)S(1)} %get-tuple-element.117), channel_id=1, source_target_pairs={{0,10},{4,14},{10,0},{14,4},{1,11},{5,15},{11,1},{15,5},{16,26},{2... | collective-permute-start | bytes 147464 | tf_op jit(solution)/shard_map/ppermute | solution.py:651
  73.4 4.7 %collective-permute-start.13 = (bf16[152,256]{1,0:T(8,128)(2,1)S(1)}, bf16[152,256]{1,0:T(8,128)(2,1)S(1)}, u32[]{:S(2)}, u32[]{:S(2)}) collective-permute-start(bf16[152,256]{1,0:T(8,128)(2,1)S(1)} %get-tuple-element.112), channel_id=1, source_target_pairs={{0,4},{2,6},{4,0},{6,2},{8,12},{10,14},{12,8},{14,10},{1,5},{3,7},... | collective-permute-start | bytes 233480 | tf_op jit(solution)/shard_map/ppermute | solution.py:609
  74.9 9.3 %collective-permute-start.14 = (bf16[152,256]{1,0:T(8,128)(2,1)S(1)}, bf16[152,256]{1,0:T(8,128)(2,1)S(1)}, u32[]{:S(2)}, u32[]{:S(2)}) collective-permute-start(bf16[152,256]{1,0:T(8,128)(2,1)S(1)} %get-tuple-element.113), channel_id=1, source_target_pairs={{0,8},{2,10},{4,12},{6,14},{8,0},{10,2},{12,4},{14,6},{1,9},{3,11}... | collective-permute-start | bytes 233480 | tf_op jit(solution)/shard_map/ppermute | solution.py:609
  75.8 8.4 %collective-permute-start.15 = (bf16[152,256]{1,0:T(8,128)(2,1)S(1)}, bf16[152,256]{1,0:T(8,128)(2,1)S(1)}, u32[]{:S(2)}, u32[]{:S(2)}) collective-permute-start(bf16[152,256]{1,0:T(8,128)(2,1)S(1)} %get-tuple-element.114), channel_id=1, source_target_pairs={{0,12},{2,14},{4,8},{6,10},{8,4},{10,6},{12,0},{14,2},{1,13},{3,15... | collective-permute-start | bytes 233480 | tf_op jit(solution)/shard_map/ppermute | solution.py:609
  77.9 25.4 %collective-permute-start.34 = (bf16[576,256]{1,0:T(8,128)(2,1)S(1)}, bf16[576,256]{1,0:T(8,128)(2,1)S(1)}, u32[]{:S(2)}, u32[]{:S(2)}) collective-permute-start(bf16[576,256]{1,0:T(8,128)(2,1)S(1)} %pad_maximum_fusion.refs_0_), channel_id=1, source_target_pairs={{0,2},{2,0},{4,6},{6,4},{8,10},{10,8},{12,14},{14,12},{1,3},{3,1},... | collective-permute-start | bytes 884744 | tf_op jit(solution)/shard_map/ppermute | solution.py:606
  84.3 8.5 %collective-permute-start.21 = (bf16[144,256]{1,0:T(8,128)(2,1)S(1)}, bf16[144,256]{1,0:T(8,128)(2,1)S(1)}, u32[]{:S(2)}, u32[]{:S(2)}) collective-permute-start(bf16[144,256]{1,0:T(8,128)(2,1)S(1)} %get-tuple-element.124), channel_id=1, source_target_pairs={{0,12},{2,14},{4,8},{6,10},{8,4},{10,6},{12,0},{14,2},{1,13},{3,15... | collective-permute-start | bytes 221192 | tf_op jit(solution)/shard_map/ppermute | solution.py:609
  85.1 7.7 %collective-permute-start.20 = (bf16[144,256]{1,0:T(8,128)(2,1)S(1)}, bf16[144,256]{1,0:T(8,128)(2,1)S(1)}, u32[]{:S(2)}, u32[]{:S(2)}) collective-permute-start(bf16[144,256]{1,0:T(8,128)(2,1)S(1)} %get-tuple-element.124), channel_id=1, source_target_pairs={{0,8},{2,10},{4,12},{6,14},{8,0},{10,2},{12,4},{14,6},{1,9},{3,11}... | collective-permute-start | bytes 221192 | tf_op jit(solution)/shard_map/ppermute | solution.py:609
  88.1 4.7 %collective-permute-start.19 = (bf16[144,256]{1,0:T(8,128)(2,1)S(1)}, bf16[144,256]{1,0:T(8,128)(2,1)S(1)}, u32[]{:S(2)}, u32[]{:S(2)}) collective-permute-start(bf16[144,256]{1,0:T(8,128)(2,1)S(1)} %get-tuple-element.124), channel_id=1, source_target_pairs={{0,4},{2,6},{4,0},{6,2},{8,12},{10,14},{12,8},{14,10},{1,5},{3,7},... | collective-permute-start | bytes 221192 | tf_op jit(solution)/shard_map/ppermute | solution.py:609
  88.8 8.4 %collective-permute-start.22 = (bf16[2,192,256]{2,1,0:T(8,128)(2,1)S(1)}, bf16[2,192,256]{2,1,0:T(8,128)(2,1)S(1)}, u32[]{:S(2)}, u32[]{:S(2)}) collective-permute-start(bf16[2,192,256]{2,1,0:T(8,128)(2,1)S(1)} %get-tuple-element.125), channel_id=1, source_target_pairs={{0,14},{2,4},{4,2},{6,8},{8,6},{10,12},{12,10},{14,0},{1,15},{3,5}... | collective-permute-start | bytes 589832 | tf_op jit(solution)/shard_map/ppermute | solution.py:662
  97.1 6.7 %collective-permute-start.23 = (bf16[576,256]{1,0:T(8,128)(2,1)S(1)}, bf16[576,256]{1,0:T(8,128)(2,1)S(1)}, u32[]{:S(2)}, u32[]{:S(2)}) collective-permute-start(bf16[576,256]{1,0:T(8,128)(2,1)S(1)} %constant_dynamic-update-slice_fusion.refs_0_), channel_id=1, source_target_pairs={{0,2},{2,0},{4,6},{6,4},{8,10},{10,8},{12,14},{14,12},{1,3},{3,1},... | collective-permute-start | bytes 884744 | tf_op jit(solution)/shard_map/ppermute | solution.py:606
  97.1 6.7 %collective-permute-start.35 = (bf16[576,256]{1,0:T(8,128)(2,1)S(1)}, bf16[576,256]{1,0:T(8,128)(2,1)S(1)}, u32[]{:S(2)}, u32[]{:S(2)}) collective-permute-start(bf16[576,256]{1,0:T(8,128)(2,1)S(1)} %pad_maximum_fusion.refs_0_), channel_id=1, source_target_pairs={{0,1},{1,0},{2,3},{3,2},{4,5},{5,4},{6,7},{7,6},{8,9},{9,8},{10,11... | collective-permute-start | bytes 884744 | tf_op jit(solution)/shard_map/ppermute | solution.py:540
  97.2 9.4 %collective-permute-start.24 = (bf16[576,256]{1,0:T(8,128)(2,1)S(1)}, bf16[576,256]{1,0:T(8,128)(2,1)S(1)}, u32[]{:S(2)}, u32[]{:S(2)}) collective-permute-start(bf16[576,256]{1,0:T(8,128)(2,1)S(1)} %constant_dynamic-update-slice_fusion.refs_0_), channel_id=1, source_target_pairs={{0,1},{1,0},{2,3},{3,2},{4,5},{5,4},{6,7},{7,6},{8,9},{9,8},{10,11... | collective-permute-start | bytes 884744 | tf_op jit(solution)/shard_map/ppermute | solution.py:540
  103.3 1.6 %collective-permute-start.36 = (bf16[576,256]{1,0:T(8,128)(2,1)S(1)}, bf16[576,256]{1,0:T(8,128)(2,1)S(1)}, u32[]{:S(2)}, u32[]{:S(2)}) collective-permute-start(bf16[576,256]{1,0:T(8,128)(2,1)S(1)} %collective-permute-done.34.refs_1_), channel_id=1, source_target_pairs={{0,1},{1,0},{2,3},{3,2},{4,5},{5,4},{6,7},{7,6},{8,9},{9,8},{10,11... | collective-permute-start | bytes 884744 | tf_op jit(solution)/shard_map/ppermute | solution.py:540
  103.9 2.8 %collective-permute-start.25 = (bf16[576,256]{1,0:T(8,128)(2,1)S(1)}, bf16[576,256]{1,0:T(8,128)(2,1)S(1)}, u32[]{:S(2)}, u32[]{:S(2)}) collective-permute-start(bf16[576,256]{1,0:T(8,128)(2,1)S(1)} %collective-permute-done.23.refs_1_), channel_id=1, source_target_pairs={{0,1},{1,0},{2,3},{3,2},{4,5},{5,4},{6,7},{7,6},{8,9},{9,8},{10,11... | collective-permute-start | bytes 884744 | tf_op jit(solution)/shard_map/ppermute | solution.py:540

commit v9 on v8

--- a/solution.py
+++ b/solution.py
@@ -33,10 +33,17 @@
             return jnp.where(ends, t ^ k, self.T - 1 - t)
         return t ^ k
 
-    def messages(self):
-        rows = [self.BASE] * (self.T - 1) + [self.BASE + self.ROW]
-        rows[1] += self.ROW
-        return [(2, n, self.C) for n in rows]
+    def steps(self):
+        rest = [k for k in range(2, self.T - 1)]
+        evens = [k for k in rest if k % 2 == 0]
+        odds = [k for k in rest if k % 2 == 1]
+        rest = evens + odds
+        if len(rest) % 2:
+            rest = rest[:-1] + [None, rest[-1]]
+        return [(1, self.T - 1)] + [(rest[i], rest[i + 1]) for i in range(0, len(rest), 2)]
+
+    def rows(self, step):
+        return self.BASE + (self.ROW if step == 0 else 0)
 
     def pairs(self):
         T, mix = self.T, self.MIX
@@ -47,7 +54,10 @@
         out = [[(i, i ^ k) for i in range(T) if k == 1 or needed(i, i ^ k)] for k in range(T - 1)]
         out[mix] = [(i, i ^ mix if i in (0, mix, mix + 1, T - 1) else T - 1 - i) for i in range(T)]
         out.append([(i, (i + 1) % T if i % 2 else (i - 1) % T) for i in range(T)])
-        return out
+        return [
+            [(2 * i + core, 2 * d + core) for core in range(2) if ks[core] is not None for i, d in out[ks[core]]]
+            for ks in self.steps()
+        ]
 
 
 def col_iota(n):
@@ -99,23 +109,50 @@
     return [(f * dm.R + row) * dm.F + j for f in range(6)]
 
 
-def write_messages(dm, ep, t, sources, refs):
+def write_messages(dm, ep, t, p, sources, refs):
     R = dm.R
-    for k in range(dm.T):
-        if k < dm.T - 1:
-            parts = strip_targets(dm, ep, t, dm.partner(t, k))
-            if k == 1:
-                parts = parts + row_targets(dm, jnp.where(t % 2 == 0, R - 1, 0))
-        else:
-            parts = [mirror_slot(dm, f) for f in range(6)]
-            parts = parts + row_targets(dm, jnp.where(t % 2 == 1, R - 1, 0))
-        hot = one_hot(jnp.concatenate(parts, axis=0), dm.N)
-        for which in range(2):
-            refs[k][which] = jnp.dot(hot, sources[which], preferred_element_type=F32).astype(BF)
-
-
-def pack_kernel(dm, ep, x_ref, up_ref, *refs):
-    write_messages(dm, ep, lax.axis_index("tile"), (x_ref[...], up_ref[...]), refs)
+    steps = dm.steps()
+    for other in range(2):
+        core = p ^ other
+        for step, ks in enumerate(steps):
+            if step == 0:
+                strips = strip_targets(dm, ep, t, t ^ 1)
+                parts = [jnp.where(core == 0, strips[f], mirror_slot(dm, f)) for f in range(6)]
+                parts = parts + row_targets(dm, jnp.where((t + core) % 2 == 0, R - 1, 0))
+            else:
+                ds = [dm.partner(t, k) for k in ks if k is not None]
+                parts = strip_targets(dm, ep, t, jnp.where(core == 0, ds[0], ds[-1]))
+            hot = one_hot(jnp.concatenate(parts, axis=0), dm.N)
+            for which in range(2):
+                rows = jnp.dot(hot, sources[which], preferred_element_type=F32).astype(BF)
+                refs[other * len(steps) + step][which] = rows
+
+
+def write_self(dm, ep, t, sources, ref):
+    hot = one_hot(jnp.concatenate(strip_targets(dm, ep, t, t), axis=0), dm.N)
+    for which in range(2):
+        ref[which] = jnp.dot(hot, sources[which], preferred_element_type=F32).astype(BF)
+
+
+def pack_kernel(dm, ep, x_hbm, up_hbm, *refs):
+    *refs, self_ref, x_ref, up_ref, sems = refs
+    copies = [
+        pltpu.make_async_copy(x_hbm, x_ref, sems.at[0]),
+        pltpu.make_async_copy(up_hbm, up_ref, sems.at[1]),
+    ]
+    for copy in copies:
+        copy.start()
+    for copy in copies:
+        copy.wait()
+    t, p = lax.axis_index("tile"), lax.axis_index("dp")
+    write_messages(dm, ep, t, p, (x_ref[...], up_ref[...]), refs)
+    write_self(dm, ep, t, (x_ref[...], up_ref[...]), self_ref)
+
+
+def merge_kernel(count, *refs):
+    for i in range(count):
+        refs[2 * count + i][0] = refs[i][...]
+        refs[2 * count + i][1] = refs[count + i][...]
 
 
 def ghost_targets(dm, ep, t):
@@ -199,16 +236,24 @@
     return jnp.concatenate(parts, axis=0)
 
 
-def gather_ghosts(dm, ep, t, own, messages, table_ref):
+def gather_ghosts(dm, ep, t, p, own, messages, table_ref):
     hot = one_hot(ghost_targets(dm, ep, t), dm.NT)
     out = []
     for which in range(2):
         table_ref[0 : dm.N] = own[which]
-        for k in range(dm.T):
-            at = dm.o_msg + k * dm.BASE
-            table_ref[at : at + dm.BASE] = messages[k][which, : dm.BASE]
-        table_ref[dm.o_row : dm.o_row + dm.ROW] = messages[1][which, dm.BASE :]
-        table_ref[dm.o_row + dm.ROW :] = messages[dm.T - 1][which, dm.BASE :]
+        table_ref[dm.o_msg : dm.o_msg + dm.BASE] = messages[-1][which]
+        for step, ks in enumerate(dm.steps()):
+            here = messages[2 * step][0, which].astype(F32)
+            there = messages[2 * step + 1][1, which].astype(F32)
+            for core, k in enumerate(ks):
+                if k is None:
+                    continue
+                value = jnp.where(p == core, here, there).astype(BF)
+                at = dm.o_msg + k * dm.BASE
+                table_ref[at : at + dm.BASE] = value[: dm.BASE]
+                if step == 0:
+                    at = dm.o_row + core * dm.ROW
+                    table_ref[at : at + dm.ROW] = value[dm.BASE :]
         out.append(jnp.dot(hot, table_ref[...], preferred_element_type=F32))
     return out
 
@@ -343,13 +388,15 @@
 
 def first_kernel(dm, ep, x_ref, up_ref, w1_ref, bias_ref, w2t_ref, *refs):
     T, R, F, N, C = dm.T, dm.R, dm.F, dm.N, dm.C
-    messages = refs[:T]
-    send1_ref, keep1_ref, send2_ref, keep2_ref, hid_ref, inner_ref, bias_sum_ref, send_bias_ref = refs[T : T + 8]
-    out_messages = refs[T + 8 : 2 * T + 8]
-    table_ref, frame_ref, xs_ref, us_ref, z_ref, before_ref, acc_ref, hcat_ref = refs[2 * T + 8 :]
+    M = 2 * len(dm.steps())
+    messages = refs[: M + 1]
+    refs = refs[M + 1 :]
+    send1_ref, keep1_ref, send2_ref, keep2_ref, hid_ref, inner_ref, bias_sum_ref, send_bias_ref = refs[:8]
+    out_messages, self_ref = refs[8 : M + 8], refs[M + 8]
+    table_ref, frame_ref, xs_ref, us_ref, z_ref, before_ref, acc_ref, hcat_ref = refs[M + 9 :]
     t, p = lax.axis_index("tile"), lax.axis_index("dp")
     own = (x_ref[...].reshape(N, C), up_ref[...].reshape(N, C))
-    gx, gu = gather_ghosts(dm, ep, t, own, messages, table_ref)
+    gx, gu = gather_ghosts(dm, ep, t, p, own, messages, table_ref)
     top, bottom = dm.WE, dm.WE + dm.ROW
     build_taps(dm, x_ref, gx[:top], gx[top:bottom], gx[bottom:], frame_ref, xs_ref, False, p)
     before = jnp.dot(xs_ref[...], w1_ref[...], preferred_element_type=F32) + bias_ref[...]
@@ -400,19 +447,20 @@
         for f in range(6):
             at = (r * 6 + f) * F
             inner_ref[f * R + r] = acc_ref[at : at + F].astype(BF)
-    write_messages(
-        dm, ep, t, (hid_ref[...].reshape(N, C), inner_ref[...].reshape(N, C)), out_messages
-    )
+    fields = (hid_ref[...].reshape(N, C), inner_ref[...].reshape(N, C))
+    write_messages(dm, ep, t, p, fields, out_messages)
+    write_self(dm, ep, t, fields, self_ref)
 
 
 def second_kernel(dm, ep, x_ref, d_ref, hid_ref, inner_ref, w1t_ref, w2_ref, *refs):
     T, R, F, N, C = dm.T, dm.R, dm.F, dm.N, dm.C
-    messages = refs[:T]
-    state_ref, grad_ref = refs[T : T + 2]
-    table_ref, frame_ref, hs_ref, is_ref, z_ref, acc_ref = refs[T + 2 :]
-    t = lax.axis_index("tile")
+    M = 2 * len(dm.steps()) + 1
+    messages = refs[:M]
+    state_ref, grad_ref = refs[M : M + 2]
+    table_ref, frame_ref, hs_ref, is_ref, z_ref, acc_ref = refs[M + 2 :]
+    t, p = lax.axis_index("tile"), lax.axis_index("dp")
     own = (hid_ref[...].reshape(N, C), inner_ref[...].reshape(N, C))
-    gh, gi = gather_ghosts(dm, ep, t, own, messages, table_ref)
+    gh, gi = gather_ghosts(dm, ep, t, p, own, messages, table_ref)
     top, bottom = dm.WE, dm.WE + dm.ROW
     build_taps(dm, hid_ref, gh[:top], gh[top:bottom], gh[bottom:], frame_ref, hs_ref, False)
     acc_ref[...] = jnp.dot(hs_ref[...], w2_ref[...], preferred_element_type=F32)
@@ -518,17 +566,18 @@
                 out_ref[tap, at] = ref[row : row + size].astype(F32) * scale
 
 
-def call(kernel, out_shapes, scratch=(), smem_first=False, limit=16):
+def call(kernel, out_shapes, scratch=(), smem_first=False, limit=16, raw=()):
     def run(*args):
         vmem = pl.BlockSpec(memory_space=pltpu.VMEM)
         smem = pl.BlockSpec(memory_space=pltpu.SMEM)
-        specs = [smem if smem_first and i == 0 else vmem for i in range(len(args))]
+        hbm = pl.BlockSpec(memory_space=pl.ANY)
+        specs = [smem if smem_first and i == 0 else hbm if i in raw else vmem for i in range(len(args))]
         return pl.pallas_call(
             kernel,
             out_shape=[jax.ShapeDtypeStruct(s, dt) for s, dt in out_shapes],
             in_specs=specs,
             out_specs=[vmem] * len(out_shapes),
-            scratch_shapes=[pltpu.VMEM(s, dt) for s, dt in scratch],
+            scratch_shapes=[pltpu.VMEM(s, dt) for s, dt in scratch] + [pltpu.SemaphoreType.DMA((2,))] * bool(raw),
             compiler_params=pltpu.CompilerParams(vmem_limit_bytes=limit << 20),
         )(*args)
 
@@ -554,17 +603,29 @@
     w1s = w1s.reshape(w1.shape)
     w1t = w1t.reshape(w1.shape)
     w2t = w2t.reshape(w2.shape)
-    msg_shapes = [(shape, BF) for shape in dm.messages()]
+    steps = range(len(dm.steps()))
+    pairs = dm.pairs()
+    msg_shapes = [((2, dm.rows(i), channels), BF) for i in steps] * 2 + [((2, dm.BASE, channels), BF)]
     flat = (dm.N, channels)
-    messages = call(functools.partial(pack_kernel, dm), msg_shapes, smem_first=True)(
-        edge_partner, x.reshape(flat), d.reshape(flat)
-    )
-    pairs = dm.pairs()
-
-    def send_message(messages, k):
-        return messages[k] if k == 0 else lax.ppermute(messages[k], "tile", pairs[k])
-
-    messages = [send_message(messages, k) for k in range(tiles)]
+
+    def merged(packed):
+        count = len(steps)
+        own, give = packed[:count], [swap_dp(v) for v in packed[count : 2 * count]]
+        return call(
+            functools.partial(merge_kernel, count), [((2,) + v.shape, BF) for v in own]
+        )(*own, *give)
+
+    def across(v, step):
+        return lax.ppermute(v, ("tile", "dp"), pairs[step])
+
+    packed = call(
+        functools.partial(pack_kernel, dm), msg_shapes, [(flat, BF)] * 2, smem_first=True, raw=(1, 2)
+    )(edge_partner, x.reshape(flat), d.reshape(flat))
+    messages = []
+    for i, v in enumerate(merged(packed)):
+        v = across(v, i)
+        messages += [v, swap_dp(v)]
+    messages.append(packed[-1])
     half = channels // 2
     wide = 9 * channels
     frame = (rows + 2, 6, face + 16, channels)
@@ -629,42 +690,42 @@
             functools.partial(last_kernel, zcount), [((n, channels), BF)] + [one] * bool(bias)
         )(keep, *recvs, *bias)
 
-    early = [k for k in range(2, tiles - 1) if k % 2 == 0]
-    middle = [k for k in range(1, tiles - 1) if k % 2 == 1]
-    messages = list(packed)
+    joined = merged(packed)
+    early = list(steps)[1 : 1 + len(steps) // 2]
+    middle = [i for i in steps if i not in early]
+    came = {}
 
     keep2, send2 = sum_dp(keep2, swap_dp(send2))
     recv2 = along_y(send2)
     keep1, send1, bias_sum = sum_dp(keep1, swap_dp(send1), bias_sum, swap_dp(send_bias))
     recv1 = along_y(send1)
-    got = [lax.ppermute(packed[k], "tile", pairs[k]) for k in early]
+    got = [across(joined[i], i) for i in early]
 
     keep2, sends2, _ = sum_y(keep2, recv2)
     recvs2 = [along_z(v, j + 1) for j, v in enumerate(sends2)]
     recv1, got = barrier((recv1, got))
-    for k, v in zip(early, got):
-        messages[k] = v
+    came.update(zip(early, got))
 
     keep1, sends1, (bias_sum,) = sum_y(keep1, recv1, bias_sum)
-    sends1, todo = barrier((sends1, [packed[k] for k in middle]))
+    sends1, todo = barrier((sends1, [joined[i] for i in middle]))
     recvs1 = [along_z(v, j + 1) for j, v in enumerate(sends1)]
-    got = [lax.ppermute(v, "tile", pairs[k]) for k, v in zip(middle, todo)]
+    got = [across(v, i) for i, v in zip(middle, todo)]
 
     (own2,) = sum_z(keep2, recvs2)
     own2 = [own2] + [along_z(own2, j) for j in range(1, zcount)]
     recvs1, got = barrier((recvs1, got))
-    for k, v in zip(middle, got):
-        messages[k] = v
+    came.update(zip(middle, got))
 
     own1, bias_sum = sum_z(keep1, recvs1, bias_sum)
-    own1, last = barrier((own1, packed[tiles - 1]))
     own1 = [own1] + [along_z(own1, j) for j in range(1, zcount)]
-    last = lax.ppermute(last, "tile", pairs[tiles - 1])
     own2 = jnp.concatenate(own2, axis=0)
     other2 = along_y(own2)
-    own1[-1], messages[tiles - 1] = barrier((own1[-1], last))
     own1 = jnp.concatenate(own1, axis=0)
     other1 = along_y(own1)
+    messages = []
+    for i in steps:
+        messages += [came[i], swap_dp(came[i])]
+    messages.append(packed[-1])
     own1, messages = barrier((own1, messages))
     state, grad = call(
         functools.partial(second_kernel, dm),

time: 109 us -> 120 us (1.10)
  waiting for transfers between devices: 32.5 us -> 39.9 us
  starting transfers between devices: 49.5 us -> 51.7 us
    ppermute x14 -> x8, starting transfers between devices: 28.1 us -> 11.1 us  [across(): return lax.ppermute(v, ('tile', 'dp'), pairs[step])]
    ppermute x7 -> x23, starting transfers between devices: 1.23 us -> 14.1 us  [swap_dp(): return lax.ppermute(v, 'dp', [(i, count - 1 - i) for i in range(count)])]
    ppermute x12, starting transfers between devices: 17.8 us -> 22.7 us  [along_z(): return lax.ppermute(v, 'tile', [(i, i ^ 2 * j) for i in range(tiles)])]
    ppermute x12, waiting for transfers between devices: 8.06 us -> 12 us  [along_z(): return lax.ppermute(v, 'tile', [(i, i ^ 2 * j) for i in range(tiles)])]
    ppermute x14 -> x8, waiting for transfers between devices: 16.7 us -> 19.6 us  [across(): return lax.ppermute(v, ('tile', 'dp'), pairs[step])]
    ppermute x7 -> x23, waiting for transfers between devices: 3.66 us -> 5.75 us  [swap_dp(): return lax.ppermute(v, 'dp', [(i, count - 1 - i) for i in range(count)])]
    ppermute x4, waiting for transfers between devices: 4.06 us -> 2.51 us  [along_y(): return lax.ppermute(v, 'tile', [(i, i ^ 1) for i in range(tiles)])]
    ppermute x4, starting transfers between devices: 2.32 us -> 3.77 us  [along_y(): return lax.ppermute(v, 'tile', [(i, i ^ 1) for i in range(tiles)])]
  transfers between devices with their start and end apart: 37 -> 47, of which waited for: 13 -> 19; matrix products, arithmetic and copies ran while one was open for 0% -> 0% of each run, Pallas kernels for 8% -> 7%
where the time goes in v9:
time: 120 us; the launch traced here: 119 us
  starting transfers between devices  51.7 us (43%)
  waiting for transfers between devices  39.9 us (33%)
  Pallas kernels  21.4 us (18%)
  local copies, waits for them, and re-layouts  5.53 us (5%)
    ppermute x12, starting transfers between devices, along_z(): return lax.ppermute(v, 'tile', [(i, i ^ 2 * j) for i in range(tiles)])  22.7 us
    pallas_call x14, Pallas kernels, run(): pl.pallas_call(kernel, out_shape=[jax.ShapeDtypeStruct(s, dt) for s, dt i...  21.4 us
    ppermute x8, waiting for transfers between devices, across(): return lax.ppermute(v, ('tile', 'dp'), pairs[step])  19.6 us
    ppermute x23, starting transfers between devices, swap_dp(): return lax.ppermute(v, 'dp', [(i, count - 1 - i) for i in range(count)])  14.1 us
    ppermute x12, waiting for transfers between devices, along_z(): return lax.ppermute(v, 'tile', [(i, i ^ 2 * j) for i in range(tiles)])  12 us
    ppermute x8, starting transfers between devices, across(): return lax.ppermute(v, ('tile', 'dp'), pairs[step])  11.1 us
    ppermute x23, waiting for transfers between devices, swap_dp(): return lax.ppermute(v, 'dp', [(i, count - 1 - i) for i in range(count)])  5.75 us
    unnamed x20, local copies, waits for them, and re-layouts  5.52 us
  transfers between devices with their start and end apart: 47, of which 19 were waited for; matrix products, arithmetic and copies ran while one was open for 0% of the time, Pallas kernels for 7%

profile of v9, /device:TPU:0, one launch (start us, length us, event | category | flops | bytes accessed | tf_op | source)
XLA Modules:
  0.0 119.4 jit_solution(1889003747316916978)
XLA Ops:
  0.6 0.8 copy.12.ep
  1.4 0.9 copy-done.2
  2.3 0.9 copy-done.4
  3.3 2.7 %shard_map.102 = (bf16[2,192,256]{2,1,0:T(8,128)(2,1)S(1)}, bf16[2,48,256]{2,1,0:T(8,128)(2,1)S(1)}, bf16[2,48,256]{2,1,0:T(8,128)(2,1)S(1)}, bf16[2,48,256]{2,1...) custom-call(s32[6,4]{1,0:T(8,128)S(1)} %copy.12.ep, ...), custom_call_target="tpu_custom_call" | custom-call | tf_op jit(solution)/shard_map/pallas_call | solution.py:575
  6.0 0.5 collective-permute-start
  6.6 0.4 collective-permute-start.2
  7.1 0.6 collective-permute-done.1.refs_5_
  7.8 0.2 collective-permute-done.2.refs_6_
  7.9 0.3 collective-permute-done.3.refs_7_
  8.3 2.7 %collective-permute-start.4 = (bf16[2,2,192,256]{3,2,1,0:T(8,128)(2,1)S(1)}, bf16[2,2,192,256]{3,2,1,0:T(8,128)(2,1)S(1)}, u32[]{:S(2)}, u32[]{:S(2)}) collective-permute-start(bf16[2,2,192,256]{3,2,1,0:T(8,128)(2,1)S(1)} %get-tuple-element.98), channel_id=1, source_target_pairs={{0,2},{2,0},{4,6},{6,4},{8,10},{10,8},{12,14},{14,12},{1,15},{3,5}... | collective-permute-start | bytes 1179656 | tf_op jit(solution)/shard_map/ppermute | solution.py:619
  11.1 10.0 %collective-permute-done.4.refs_0_ = bf16[2,2,192,256]{3,2,1,0:T(8,128)(2,1)S(1)} collective-permute-done((bf16[2,2,192,256]{3,2,1,0:T(8,128)(2,1)S(1)}, bf16[2,2,192,256]{3,2,1,0:T(8,128)(2,1)S(1)}, u32[]{:S(2)}, u32[]{:S(2)}) %collective-permute-start.4) | collective-permute-done | bytes 393248 | tf_op jit(solution)/shard_map/ppermute | solution.py:619
  21.0 4.0 %collective-permute-start.6 = (bf16[2,2,48,256]{3,2,1,0:T(8,128)(2,1)S(1)}, bf16[2,2,48,256]{3,2,1,0:T(8,128)(2,1)S(1)}, u32[]{:S(2)}, u32[]{:S(2)}) collective-permute-start(bf16[2,2,48,256]{3,2,1,0:T(8,128)(2,1)S(1)} %get-tuple-element.99), channel_id=1, source_target_pairs={{0,4},{4,0},{10,14},{14,10},{1,9},{3,11},{5,13},{7,15},{9,1},{11,3... | collective-permute-start | bytes 294920 | tf_op jit(solution)/shard_map/ppermute | solution.py:619
  25.0 0.9 collective-permute-start.8
  25.9 0.7 collective-permute-start.10
  26.5 1.9 %collective-permute-done.6.refs_2_ = bf16[2,2,48,256]{3,2,1,0:T(8,128)(2,1)S(1)} collective-permute-done((bf16[2,2,48,256]{3,2,1,0:T(8,128)(2,1)S(1)}, bf16[2,2,48,256]{3,2,1,0:T(8,128)(2,1)S(1)}, u32[]{:S(2)}, u32[]{:S(2)}) %collective-permute-start.6) | collective-permute-done | bytes 98336 | tf_op jit(solution)/shard_map/ppermute | solution.py:619
  28.5 3.2 %collective-permute-start.7 = (bf16[2,2,48,256]{3,2,1,0:T(8,128)(2,1)S(1)}, bf16[2,2,48,256]{3,2,1,0:T(8,128)(2,1)S(1)}, u32[]{:S(2)}, u32[]{:S(2)}) collective-permute-start(bf16[2,2,48,256]{3,2,1,0:T(8,128)(2,1)S(1)} %collective-permute-done.6.refs_2_), channel_id=1, source_target_pairs={{0,1},{1,0},{2,3},{3,2},{4,5},{5,4},{6,7},{7,6},{8,9},{9,8},{10,11... | collective-permute-start | bytes 294920 | tf_op jit(solution)/shard_map/ppermute | solution.py:589
  31.8 3.9 %collective-permute-start.11 = (bf16[2,2,48,256]{3,2,1,0:T(8,128)(2,1)S(1)}, bf16[2,2,48,256]{3,2,1,0:T(8,128)(2,1)S(1)}, u32[]{:S(2)}, u32[]{:S(2)}) collective-permute-start(bf16[2,2,48,256]{3,2,1,0:T(8,128)(2,1)S(1)} %collective-permute-done.10.refs_6_), channel_id=1, source_target_pairs={{0,1},{1,0},{2,3},{3,2},{4,5},{5,4},{6,7},{7,6},{8,9},{9,8},{10,11... | collective-permute-start | bytes 294920 | tf_op jit(solution)/shard_map/ppermute | solution.py:589
  35.7 1.3 %copy-done = bf16[3,3,256,256]{3,2,1,0:T(8,128)(2,1)S(1)} copy-done((bf16[3,3,256,256]{3,2,1,0:T(8,128)(2,1)S(1)}, bf16[3,3,256,256]{3,2,1,0:T(8,128)(2,1)}, u32[]{:S(2)}) %copy-start) | copy-done | bytes 1179672
  37.0 1.3 %copy-done.6 = bf16[3,3,256,256]{3,2,1,0:T(8,128)(2,1)S(1)} copy-done((bf16[3,3,256,256]{3,2,1,0:T(8,128)(2,1)S(1)}, bf16[3,3,256,256]{3,2,1,0:T(8,128)(2,1)}, u32[]{:S(2)}) %copy-start.6) | copy-done | bytes 1179672
  38.3 0.7 shard_map.101
  39.0 0.2 copy-done.3
  39.3 8.2 %shard_map.104 = (bf16[9,128,256]{2,1,0:T(8,128)(2,1)S(1)}, f32[9,128,256]{2,1,0:T(8,128)S(1)}, bf16[9,128,256]{2,1,0:T(8,128)(2,1)S(1)}, f32[9,128,256]{2,1,0:T...) custom-call(s32[6,4]{1,0:T(8,128)S(1)} %copy.12.ep, ...), custom_call_target="tpu_custom_call" | custom-call | tf_op jit(solution)/shard_map/pallas_call | solution.py:575
  47.6 0.5 collective-permute-start.36
  48.2 2.3 %collective-permute-done.13.refs_1_ = bf16[8,256]{1,0:T(8,128)(2,1)S(1)} collective-permute-done((bf16[8,256]{1,0:T(8,128)(2,1)S(1)}, bf16[8,256]{1,0:T(8,128)(2,1)S(1)}, u32[]{:S(2)}, u32[]{:S(2)}) %collective-permute-start.13) | collective-permute-done | bytes 4128 | tf_op jit(solution)/shard_map/ppermute | solution.py:589
  50.7 0.2 collective-permute-start.15
  50.9 0.4 collective-permute-start.16
  51.4 2.0 %collective-permute-start.37 = (bf16[576,256]{1,0:T(8,128)(2,1)S(1)}, bf16[576,256]{1,0:T(8,128)(2,1)S(1)}, u32[]{:S(2)}, u32[]{:S(2)}) collective-permute-start(bf16[576,256]{1,0:T(8,128)(2,1)S(1)} %get-tuple-element.166), channel_id=1, source_target_pairs={{0,2},{2,0},{4,6},{6,4},{8,10},{10,8},{12,14},{14,12},{1,3},{3,1},... | collective-permute-start | bytes 884744 | tf_op jit(solution)/shard_map/ppermute | solution.py:667
  53.4 0.5 collective-permute-start.18
  53.9 0.7 collective-permute-done.17.refs_6_
  54.6 0.2 collective-permute-done.18.refs_7_
  54.8 1.9 %collective-permute-start.19 = (bf16[2,2,48,256]{3,2,1,0:T(8,128)(2,1)S(1)}, bf16[2,2,48,256]{3,2,1,0:T(8,128)(2,1)S(1)}, u32[]{:S(2)}, u32[]{:S(2)}) collective-permute-start(bf16[2,2,48,256]{3,2,1,0:T(8,128)(2,1)S(1)} %get-tuple-element.117), channel_id=1, source_target_pairs={{0,4},{4,0},{10,14},{14,10},{1,9},{3,11},{5,13},{7,15},{9,1},{11,3... | collective-permute-start | bytes 294920 | tf_op jit(solution)/shard_map/ppermute | solution.py:619
  56.8 7.7 %collective-permute-done.19.refs_2_ = bf16[2,2,48,256]{3,2,1,0:T(8,128)(2,1)S(1)} collective-permute-done((bf16[2,2,48,256]{3,2,1,0:T(8,128)(2,1)S(1)}, bf16[2,2,48,256]{3,2,1,0:T(8,128)(2,1)S(1)}, u32[]{:S(2)}, u32[]{:S(2)}) %collective-permute-start.19) | collective-permute-done | bytes 98336 | tf_op jit(solution)/shard_map/ppermute | solution.py:619
  64.7 2.5 %collective-permute-done.37.recv_ref = bf16[576,256]{1,0:T(8,128)(2,1)S(1)} collective-permute-done((bf16[576,256]{1,0:T(8,128)(2,1)S(1)}, bf16[576,256]{1,0:T(8,128)(2,1)S(1)}, u32[]{:S(2)}, u32[]{:S(2)}) %collective-permute-start.37) | collective-permute-done | bytes 294944 | tf_op jit(solution)/shard_map/ppermute | solution.py:667
  67.4 1.0 collective-permute-start.39
  68.4 3.3 %collective-permute-start.40 = (bf16[144,256]{1,0:T(8,128)(2,1)S(1)}, bf16[144,256]{1,0:T(8,128)(2,1)S(1)}, u32[]{:S(2)}, u32[]{:S(2)}) collective-permute-start(bf16[144,256]{1,0:T(8,128)(2,1)S(1)} %get-tuple-element.170), channel_id=1, source_target_pairs={{0,12},{2,14},{4,8},{6,10},{8,4},{10,6},{12,0},{14,2},{1,13},{3,15... | collective-permute-start | bytes 221192 | tf_op jit(solution)/shard_map/ppermute | solution.py:670
  71.7 2.4 %collective-permute-done.38.refs_0_ = bf16[144,256]{1,0:T(8,128)(2,1)S(1)} collective-permute-done((bf16[144,256]{1,0:T(8,128)(2,1)S(1)}, bf16[144,256]{1,0:T(8,128)(2,1)S(1)}, u32[]{:S(2)}, u32[]{:S(2)}) %collective-permute-start.38) | collective-permute-done | bytes 73760 | tf_op jit(solution)/shard_map/ppermute | solution.py:670
  74.1 2.4 %collective-permute-done.40.refs_2_ = bf16[144,256]{1,0:T(8,128)(2,1)S(1)} collective-permute-done((bf16[144,256]{1,0:T(8,128)(2,1)S(1)}, bf16[144,256]{1,0:T(8,128)(2,1)S(1)}, u32[]{:S(2)}, u32[]{:S(2)}) %collective-permute-start.40) | collective-permute-done | bytes 73760 | tf_op jit(solution)/shard_map/ppermute | solution.py:670
  76.5 4.0 %collective-permute-start.43 = (bf16[144,256]{1,0:T(8,128)(2,1)S(1)}, bf16[144,256]{1,0:T(8,128)(2,1)S(1)}, u32[]{:S(2)}, u32[]{:S(2)}) collective-permute-start(bf16[144,256]{1,0:T(8,128)(2,1)S(1)} %shard_map.113), channel_id=1, source_target_pairs={{0,12},{2,14},{4,8},{6,10},{8,4},{10,6},{12,0},{14,2},{1,13},{3,15... | collective-permute-start | bytes 221192 | tf_op jit(solution)/shard_map/ppermute | solution.py:670
  80.6 0.5 collective-permute-start.42
  81.0 0.5 collective-permute-start.41
  81.5 1.5 %collective-permute-start.21 = (bf16[152,256]{1,0:T(8,128)(2,1)S(1)}, bf16[152,256]{1,0:T(8,128)(2,1)S(1)}, u32[]{:S(2)}, u32[]{:S(2)}) collective-permute-start(bf16[152,256]{1,0:T(8,128)(2,1)S(1)} %get-tuple-element.127), channel_id=1, source_target_pairs={{0,4},{2,6},{4,0},{6,2},{8,12},{10,14},{12,8},{14,10},{1,5},{3,7},... | collective-permute-start | bytes 233480 | tf_op jit(solution)/shard_map/ppermute | solution.py:670
  83.1 0.7 collective-permute-done.43
  83.7 4.7 %collective-permute-start.22 = (bf16[152,256]{1,0:T(8,128)(2,1)S(1)}, bf16[152,256]{1,0:T(8,128)(2,1)S(1)}, u32[]{:S(2)}, u32[]{:S(2)}) collective-permute-start(bf16[152,256]{1,0:T(8,128)(2,1)S(1)} %get-tuple-element.128), channel_id=1, source_target_pairs={{0,8},{2,10},{4,12},{6,14},{8,0},{10,2},{12,4},{14,6},{1,9},{3,11}... | collective-permute-start | bytes 233480 | tf_op jit(solution)/shard_map/ppermute | solution.py:670
  88.4 2.6 %collective-permute-start.23 = (bf16[152,256]{1,0:T(8,128)(2,1)S(1)}, bf16[152,256]{1,0:T(8,128)(2,1)S(1)}, u32[]{:S(2)}, u32[]{:S(2)}) collective-permute-start(bf16[152,256]{1,0:T(8,128)(2,1)S(1)} %get-tuple-element.129), channel_id=1, source_target_pairs={{0,12},{2,14},{4,8},{6,10},{8,4},{10,6},{12,0},{14,2},{1,13},{3,15... | collective-permute-start | bytes 233480 | tf_op jit(solution)/shard_map/ppermute | solution.py:670
  91.0 0.8 collective-permute-start.25
  91.9 0.2 collective-permute-start.44
  92.1 1.2 %collective-permute-done.22.refs_1_ = bf16[152,256]{1,0:T(8,128)(2,1)S(1)} collective-permute-done((bf16[152,256]{1,0:T(8,128)(2,1)S(1)}, bf16[152,256]{1,0:T(8,128)(2,1)S(1)}, u32[]{:S(2)}, u32[]{:S(2)}) %collective-permute-start.22) | collective-permute-done | bytes 77856 | tf_op jit(solution)/shard_map/ppermute | solution.py:670
  93.3 1.4 %collective-permute-done.23.refs_2_ = bf16[152,256]{1,0:T(8,128)(2,1)S(1)} collective-permute-done((bf16[152,256]{1,0:T(8,128)(2,1)S(1)}, bf16[152,256]{1,0:T(8,128)(2,1)S(1)}, u32[]{:S(2)}, u32[]{:S(2)}) %collective-permute-start.23) | collective-permute-done | bytes 77856 | tf_op jit(solution)/shard_map/ppermute | solution.py:670
  94.7 3.0 %collective-permute-start.28 = (bf16[144,256]{1,0:T(8,128)(2,1)S(1)}, bf16[144,256]{1,0:T(8,128)(2,1)S(1)}, u32[]{:S(2)}, u32[]{:S(2)}) collective-permute-start(bf16[144,256]{1,0:T(8,128)(2,1)S(1)} %get-tuple-element.136), channel_id=1, source_target_pairs={{0,12},{2,14},{4,8},{6,10},{8,4},{10,6},{12,0},{14,2},{1,13},{3,15... | collective-permute-start | bytes 221192 | tf_op jit(solution)/shard_map/ppermute | solution.py:670
  97.8 1.4 %collective-permute-start.26 = (bf16[144,256]{1,0:T(8,128)(2,1)S(1)}, bf16[144,256]{1,0:T(8,128)(2,1)S(1)}, u32[]{:S(2)}, u32[]{:S(2)}) collective-permute-start(bf16[144,256]{1,0:T(8,128)(2,1)S(1)} %get-tuple-element.136), channel_id=1, source_target_pairs={{0,4},{2,6},{4,0},{6,2},{8,12},{10,14},{12,8},{14,10},{1,5},{3,7},... | collective-permute-start | bytes 221192 | tf_op jit(solution)/shard_map/ppermute | solution.py:670
  99.2 2.4 %collective-permute-start.30 = (bf16[2,2,192,256]{3,2,1,0:T(8,128)(2,1)S(1)}, bf16[2,2,192,256]{3,2,1,0:T(8,128)(2,1)S(1)}, u32[]{:S(2)}, u32[]{:S(2)}) collective-permute-start(bf16[2,2,192,256]{3,2,1,0:T(8,128)(2,1)S(1)} %collective-permute-done.24.refs_0_), channel_id=1, source_target_pairs={{0,1},{1,0},{2,3},{3,2},{4,5},{5,4},{6,7},{7,6},{8,9},{9,8},{10,11... | collective-permute-start | bytes 1179656 | tf_op jit(solution)/shard_map/ppermute | solution.py:589
  101.6 1.7 %collective-permute-done.26 = bf16[144,256]{1,0:T(8,128)(2,1)S(1)} collective-permute-done((bf16[144,256]{1,0:T(8,128)(2,1)S(1)}, bf16[144,256]{1,0:T(8,128)(2,1)S(1)}, u32[]{:S(2)}, u32[]{:S(2)}) %collective-permute-start.26) | collective-permute-done | bytes 73760 | tf_op jit(solution)/shard_map/ppermute | solution.py:670
  103.3 2.2 %collective-permute-done.27 = bf16[144,256]{1,0:T(8,128)(2,1)S(1)} collective-permute-done((bf16[144,256]{1,0:T(8,128)(2,1)S(1)}, bf16[144,256]{1,0:T(8,128)(2,1)S(1)}, u32[]{:S(2)}, u32[]{:S(2)}) %collective-permute-start.27) | collective-permute-done | bytes 73760 | tf_op jit(solution)/shard_map/ppermute | solution.py:670
  105.6 1.5 %collective-permute-start.29 = (bf16[576,256]{1,0:T(8,128)(2,1)S(1)}, bf16[576,256]{1,0:T(8,128)(2,1)S(1)}, u32[]{:S(2)}, u32[]{:S(2)}) collective-permute-start(bf16[576,256]{1,0:T(8,128)(2,1)S(1)} %constant_dynamic-update-slice_fusion.refs_0_), channel_id=1, source_target_pairs={{0,2},{2,0},{4,6},{6,4},{8,10},{10,8},{12,14},{14,12},{1,3},{3,1},... | collective-permute-start | bytes 884744 | tf_op jit(solution)/shard_map/ppermute | solution.py:667
  107.0 0.5 collective-permute-start.32
  107.5 0.8 collective-permute-done.31.refs_3_
  108.3 0.2 collective-permute-start.33
  108.5 0.4 collective-permute-start.45
  108.8 0.2 collective-permute-start.46
  109.0 0.6 collective-permute-done.33.refs_7_
  109.6 5.6 %shard_map.109 = (bf16[18,24,256]{2,1,0:T(8,128)(2,1)}, f32[18,24,256]{2,1,0:T(8,128)}) custom-call(s32[6,4]{1,0:T(8,128)S(1)} %copy.12.ep, bf16[18,24,256]{2,1,0:T(8,128)(2,1)S(1)} %bitcast.20, bf16[18,24,256]{2,1,0:T(8,128)(2,1)S(1)} %bitcast.23, bf16[18,24,256]{2,1,0:T(8,128)(2,1)S(1)} %get-tuple-element.137.hid_ref, ...), custom_call_target="tpu_custom_call" | custom-call | tf_op jit(solution)/shard_map/pallas_call | solution.py:575
  115.4 0.4 collective-permute-start.34
  115.8 1.8 %shard_map.114 = f32[9,256,256]{2,1,0:T(8,128)} custom-call(bf16[576,256]{1,0:T(8,128)(2,1)S(1)} %pad_maximum_fusion.refs_0_, bf16[576,256]{1,0:T(8,128)(2,1)S(1)} %collective-permute-done.44.refs_1_, bf16[576,256]{1,0:T(8,128)(2,1)S(1)} %collective-permute-done.45.refs_2_, bf16[576,256]{1,0:T(8,128)(2,1)S(1)} %collective-permute-done.46.refs_3_), custom_call_target="tpu_custom_call" | custom-call | tf_op jit(solution)/shard_map/pallas_call | solution.py:575
  117.6 1.8 %shard_map.110 = (f32[9,256,256]{2,1,0:T(8,128)}, f32[1,256]{1,0:T(1,128)}) custom-call(bf16[576,256]{1,0:T(8,128)(2,1)S(1)} %constant_dynamic-update-slice_fusion.refs_0_, bf16[576,256]{1,0:T(8,128)(2,1)S(1)} %collective-permute-done.29.refs_1_, bf16[576,256]{1,0:T(8,128)(2,1)S(1)} %collective-permute-done.34.refs_2_, ...), custom_call_target="tpu_custom_call" | custom-call | tf_op jit(solution)/shard_map/pallas_call | solution.py:575
  (66 shorter events, 1.7 us)
Async XLA Ops:
  1.4 0.9 copy-start.2
  2.3 0.9 copy-start.4
  6.0 2.3 %collective-permute-start = (bf16[2,192,256]{2,1,0:T(8,128)(2,1)S(1)}, bf16[2,192,256]{2,1,0:T(8,128)(2,1)S(1)}, u32[]{:S(2)}, u32[]{:S(2)}) collective-permute-start(bf16[2,192,256]{2,1,0:T(8,128)(2,1)S(1)} %get-tuple-element.94), channel_id=1, source_target_pairs={{0,1},{1,0},{2,3},{3,2},{4,5},{5,4},{6,7},{7,6},{8,9},{9,8},{10,11... | collective-permute-start | bytes 589832 | tf_op jit(solution)/shard_map/ppermute | solution.py:589
  6.5 1.2 %collective-permute-start.1 = (bf16[2,48,256]{2,1,0:T(8,128)(2,1)S(1)}, bf16[2,48,256]{2,1,0:T(8,128)(2,1)S(1)}, u32[]{:S(2)}, u32[]{:S(2)}) collective-permute-start(bf16[2,48,256]{2,1,0:T(8,128)(2,1)S(1)} %get-tuple-element.95), channel_id=1, source_target_pairs={{0,1},{1,0},{2,3},{3,2},{4,5},{5,4},{6,7},{7,6},{8,9},{9,8},{10,11... | collective-permute-start | bytes 147464 | tf_op jit(solution)/shard_map/ppermute | solution.py:589
  6.6 1.3 %collective-permute-start.2 = (bf16[2,48,256]{2,1,0:T(8,128)(2,1)S(1)}, bf16[2,48,256]{2,1,0:T(8,128)(2,1)S(1)}, u32[]{:S(2)}, u32[]{:S(2)}) collective-permute-start(bf16[2,48,256]{2,1,0:T(8,128)(2,1)S(1)} %get-tuple-element.96), channel_id=1, source_target_pairs={{0,1},{1,0},{2,3},{3,2},{4,5},{5,4},{6,7},{7,6},{8,9},{9,8},{10,11... | collective-permute-start | bytes 147464 | tf_op jit(solution)/shard_map/ppermute | solution.py:589
  7.0 1.2 %collective-permute-start.3 = (bf16[2,48,256]{2,1,0:T(8,128)(2,1)S(1)}, bf16[2,48,256]{2,1,0:T(8,128)(2,1)S(1)}, u32[]{:S(2)}, u32[]{:S(2)}) collective-permute-start(bf16[2,48,256]{2,1,0:T(8,128)(2,1)S(1)} %get-tuple-element.97), channel_id=1, source_target_pairs={{0,1},{1,0},{2,3},{3,2},{4,5},{5,4},{6,7},{7,6},{8,9},{9,8},{10,11... | collective-permute-start | bytes 147464 | tf_op jit(solution)/shard_map/ppermute | solution.py:589
  8.3 12.7 %collective-permute-start.4 = (bf16[2,2,192,256]{3,2,1,0:T(8,128)(2,1)S(1)}, bf16[2,2,192,256]{3,2,1,0:T(8,128)(2,1)S(1)}, u32[]{:S(2)}, u32[]{:S(2)}) collective-permute-start(bf16[2,2,192,256]{3,2,1,0:T(8,128)(2,1)S(1)} %get-tuple-element.98), channel_id=1, source_target_pairs={{0,2},{2,0},{4,6},{6,4},{8,10},{10,8},{12,14},{14,12},{1,15},{3,5}... | collective-permute-start | bytes 1179656 | tf_op jit(solution)/shard_map/ppermute | solution.py:619
  21.0 18.0 %collective-permute-start.5 = (bf16[2,2,192,256]{3,2,1,0:T(8,128)(2,1)S(1)}, bf16[2,2,192,256]{3,2,1,0:T(8,128)(2,1)S(1)}, u32[]{:S(2)}, u32[]{:S(2)}) collective-permute-start(bf16[2,2,192,256]{3,2,1,0:T(8,128)(2,1)S(1)} %collective-permute-done.4.refs_0_), channel_id=1, source_target_pairs={{0,1},{1,0},{2,3},{3,2},{4,5},{5,4},{6,7},{7,6},{8,9},{9,8},{10,11... | collective-permute-start | bytes 1179656 | tf_op jit(solution)/shard_map/ppermute | solution.py:589
  21.0 7.4 %collective-permute-start.6 = (bf16[2,2,48,256]{3,2,1,0:T(8,128)(2,1)S(1)}, bf16[2,2,48,256]{3,2,1,0:T(8,128)(2,1)S(1)}, u32[]{:S(2)}, u32[]{:S(2)}) collective-permute-start(bf16[2,2,48,256]{3,2,1,0:T(8,128)(2,1)S(1)} %get-tuple-element.99), channel_id=1, source_target_pairs={{0,4},{4,0},{10,14},{14,10},{1,9},{3,11},{5,13},{7,15},{9,1},{11,3... | collective-permute-start | bytes 294920 | tf_op jit(solution)/shard_map/ppermute | solution.py:619
  25.0 6.7 %collective-permute-start.8 = (bf16[2,2,48,256]{3,2,1,0:T(8,128)(2,1)S(1)}, bf16[2,2,48,256]{3,2,1,0:T(8,128)(2,1)S(1)}, u32[]{:S(2)}, u32[]{:S(2)}) collective-permute-start(bf16[2,2,48,256]{3,2,1,0:T(8,128)(2,1)S(1)} %get-tuple-element.100), channel_id=1, source_target_pairs={{0,12},{2,14},{4,8},{6,10},{8,4},{10,6},{12,0},{14,2},{1,7},{3,13}... | collective-permute-start | bytes 294920 | tf_op jit(solution)/shard_map/ppermute | solution.py:619
  25.9 5.9 %collective-permute-start.10 = (bf16[2,2,48,256]{3,2,1,0:T(8,128)(2,1)S(1)}, bf16[2,2,48,256]{3,2,1,0:T(8,128)(2,1)S(1)}, u32[]{:S(2)}, u32[]{:S(2)}) collective-permute-start(bf16[2,2,48,256]{3,2,1,0:T(8,128)(2,1)S(1)} %get-tuple-element.101), channel_id=1, source_target_pairs={{1,11},{5,15},{11,1},{15,5},{17,27},{21,31},{27,17},{31,21}} | collective-permute-start | bytes 294920 | tf_op jit(solution)/shard_map/ppermute | solution.py:619
  28.5 10.5 %collective-permute-start.7 = (bf16[2,2,48,256]{3,2,1,0:T(8,128)(2,1)S(1)}, bf16[2,2,48,256]{3,2,1,0:T(8,128)(2,1)S(1)}, u32[]{:S(2)}, u32[]{:S(2)}) collective-permute-start(bf16[2,2,48,256]{3,2,1,0:T(8,128)(2,1)S(1)} %collective-permute-done.6.refs_2_), channel_id=1, source_target_pairs={{0,1},{1,0},{2,3},{3,2},{4,5},{5,4},{6,7},{7,6},{8,9},{9,8},{10,11... | collective-permute-start | bytes 294920 | tf_op jit(solution)/shard_map/ppermute | solution.py:589
  31.7 7.3 %collective-permute-start.9 = (bf16[2,2,48,256]{3,2,1,0:T(8,128)(2,1)S(1)}, bf16[2,2,48,256]{3,2,1,0:T(8,128)(2,1)S(1)}, u32[]{:S(2)}, u32[]{:S(2)}) collective-permute-start(bf16[2,2,48,256]{3,2,1,0:T(8,128)(2,1)S(1)} %collective-permute-done.8.refs_4_), channel_id=1, source_target_pairs={{0,1},{1,0},{2,3},{3,2},{4,5},{5,4},{6,7},{7,6},{8,9},{9,8},{10,11... | collective-permute-start | bytes 294920 | tf_op jit(solution)/shard_map/ppermute | solution.py:589
  31.8 7.2 %collective-permute-start.11 = (bf16[2,2,48,256]{3,2,1,0:T(8,128)(2,1)S(1)}, bf16[2,2,48,256]{3,2,1,0:T(8,128)(2,1)S(1)}, u32[]{:S(2)}, u32[]{:S(2)}) collective-permute-start(bf16[2,2,48,256]{3,2,1,0:T(8,128)(2,1)S(1)} %collective-permute-done.10.refs_6_), channel_id=1, source_target_pairs={{0,1},{1,0},{2,3},{3,2},{4,5},{5,4},{6,7},{7,6},{8,9},{9,8},{10,11... | collective-permute-start | bytes 294920 | tf_op jit(solution)/shard_map/ppermute | solution.py:589
  35.7 1.3 %copy-start = (bf16[3,3,256,256]{3,2,1,0:T(8,128)(2,1)S(1)}, bf16[3,3,256,256]{3,2,1,0:T(8,128)(2,1)}, u32[]{:S(2)}) copy-start(bf16[3,3,256,256]{3,2,1,0:T(8,128)(2,1)} %param.10) | copy-start | bytes 3538948
  37.0 1.3 %copy-start.6 = (bf16[3,3,256,256]{3,2,1,0:T(8,128)(2,1)S(1)}, bf16[3,3,256,256]{3,2,1,0:T(8,128)(2,1)}, u32[]{:S(2)}) copy-start(bf16[3,3,256,256]{3,2,1,0:T(8,128)(2,1)} %param.8) | copy-start | bytes 3538948
  38.3 0.9 copy-start.3
  38.3 1.0 copy-start.5
  38.3 1.0 copy-start.7
  47.5 2.9 %collective-permute-start.12 = (bf16[9,128,256]{2,1,0:T(8,128)(2,1)S(1)}, bf16[9,128,256]{2,1,0:T(8,128)(2,1)S(1)}, u32[]{:S(2)}, u32[]{:S(2)}) collective-permute-start(bf16[9,128,256]{2,1,0:T(8,128)(2,1)S(1)} %get-tuple-element.104), channel_id=1, source_target_pairs={{0,1},{1,0},{2,3},{3,2},{4,5},{5,4},{6,7},{7,6},{8,9},{9,8},{10,11... | collective-permute-start | bytes 1769480 | tf_op jit(solution)/shard_map/ppermute | solution.py:589
  47.6 3.6 %collective-permute-start.36 = (bf16[9,128,256]{2,1,0:T(8,128)(2,1)S(1)}, bf16[9,128,256]{2,1,0:T(8,128)(2,1)S(1)}, u32[]{:S(2)}, u32[]{:S(2)}) collective-permute-start(bf16[9,128,256]{2,1,0:T(8,128)(2,1)S(1)} %get-tuple-element.164), channel_id=1, source_target_pairs={{0,1},{1,0},{2,3},{3,2},{4,5},{5,4},{6,7},{7,6},{8,9},{9,8},{10,11... | collective-permute-start | bytes 1769480 | tf_op jit(solution)/shard_map/ppermute | solution.py:589
  48.1 2.3 %collective-permute-start.13 = (bf16[8,256]{1,0:T(8,128)(2,1)S(1)}, bf16[8,256]{1,0:T(8,128)(2,1)S(1)}, u32[]{:S(2)}, u32[]{:S(2)}) collective-permute-start(bf16[8,256]{1,0:T(8,128)(2,1)S(1)} %get-tuple-element.106), channel_id=1, source_target_pairs={{0,1},{1,0},{2,3},{3,2},{4,5},{5,4},{6,7},{7,6},{8,9},{9,8},{10,11... | collective-permute-start | bytes 12296 | tf_op jit(solution)/shard_map/ppermute | solution.py:589
  50.6 13.9 %collective-permute-start.14 = (bf16[584,256]{1,0:T(8,128)(2,1)S(1)}, bf16[584,256]{1,0:T(8,128)(2,1)S(1)}, u32[]{:S(2)}, u32[]{:S(2)}) collective-permute-start(bf16[584,256]{1,0:T(8,128)(2,1)S(1)} %get-tuple-element.108), channel_id=1, source_target_pairs={{0,2},{2,0},{4,6},{6,4},{8,10},{10,8},{12,14},{14,12},{1,3},{3,1},... | collective-permute-start | bytes 897032 | tf_op jit(solution)/shard_map/ppermute | solution.py:667
  50.7 4.1 %collective-permute-start.15 = (bf16[2,192,256]{2,1,0:T(8,128)(2,1)S(1)}, bf16[2,192,256]{2,1,0:T(8,128)(2,1)S(1)}, u32[]{:S(2)}, u32[]{:S(2)}) collective-permute-start(bf16[2,192,256]{2,1,0:T(8,128)(2,1)S(1)} %get-tuple-element.113), channel_id=1, source_target_pairs={{0,1},{1,0},{2,3},{3,2},{4,5},{5,4},{6,7},{7,6},{8,9},{9,8},{10,11... | collective-permute-start | bytes 589832 | tf_op jit(solution)/shard_map/ppermute | solution.py:589
  50.9 2.5 %collective-permute-start.16 = (bf16[2,48,256]{2,1,0:T(8,128)(2,1)S(1)}, bf16[2,48,256]{2,1,0:T(8,128)(2,1)S(1)}, u32[]{:S(2)}, u32[]{:S(2)}) collective-permute-start(bf16[2,48,256]{2,1,0:T(8,128)(2,1)S(1)} %get-tuple-element.114), channel_id=1, source_target_pairs={{0,1},{1,0},{2,3},{3,2},{4,5},{5,4},{6,7},{7,6},{8,9},{9,8},{10,11... | collective-permute-start | bytes 147464 | tf_op jit(solution)/shard_map/ppermute | solution.py:589
  51.4 15.8 %collective-permute-start.37 = (bf16[576,256]{1,0:T(8,128)(2,1)S(1)}, bf16[576,256]{1,0:T(8,128)(2,1)S(1)}, u32[]{:S(2)}, u32[]{:S(2)}) collective-permute-start(bf16[576,256]{1,0:T(8,128)(2,1)S(1)} %get-tuple-element.166), channel_id=1, source_target_pairs={{0,2},{2,0},{4,6},{6,4},{8,10},{10,8},{12,14},{14,12},{1,3},{3,1},... | collective-permute-start | bytes 884744 | tf_op jit(solution)/shard_map/ppermute | solution.py:667
  53.4 1.2 %collective-permute-start.17 = (bf16[2,48,256]{2,1,0:T(8,128)(2,1)S(1)}, bf16[2,48,256]{2,1,0:T(8,128)(2,1)S(1)}, u32[]{:S(2)}, u32[]{:S(2)}) collective-permute-start(bf16[2,48,256]{2,1,0:T(8,128)(2,1)S(1)} %get-tuple-element.115), channel_id=1, source_target_pairs={{0,1},{1,0},{2,3},{3,2},{4,5},{5,4},{6,7},{7,6},{8,9},{9,8},{10,11... | collective-permute-start | bytes 147464 | tf_op jit(solution)/shard_map/ppermute | solution.py:589
  53.4 1.4 %collective-permute-start.18 = (bf16[2,48,256]{2,1,0:T(8,128)(2,1)S(1)}, bf16[2,48,256]{2,1,0:T(8,128)(2,1)S(1)}, u32[]{:S(2)}, u32[]{:S(2)}) collective-permute-start(bf16[2,48,256]{2,1,0:T(8,128)(2,1)S(1)} %get-tuple-element.116), channel_id=1, source_target_pairs={{0,1},{1,0},{2,3},{3,2},{4,5},{5,4},{6,7},{7,6},{8,9},{9,8},{10,11... | collective-permute-start | bytes 147464 | tf_op jit(solution)/shard_map/ppermute | solution.py:589
  54.8 9.7 %collective-permute-start.19 = (bf16[2,2,48,256]{3,2,1,0:T(8,128)(2,1)S(1)}, bf16[2,2,48,256]{3,2,1,0:T(8,128)(2,1)S(1)}, u32[]{:S(2)}, u32[]{:S(2)}) collective-permute-start(bf16[2,2,48,256]{3,2,1,0:T(8,128)(2,1)S(1)} %get-tuple-element.117), channel_id=1, source_target_pairs={{0,4},{4,0},{10,14},{14,10},{1,9},{3,11},{5,13},{7,15},{9,1},{11,3... | collective-permute-start | bytes 294920 | tf_op jit(solution)/shard_map/ppermute | solution.py:619
  56.8 7.7 %collective-permute-start.20 = (bf16[2,2,48,256]{3,2,1,0:T(8,128)(2,1)S(1)}, bf16[2,2,48,256]{3,2,1,0:T(8,128)(2,1)S(1)}, u32[]{:S(2)}, u32[]{:S(2)}) collective-permute-start(bf16[2,2,48,256]{3,2,1,0:T(8,128)(2,1)S(1)} %get-tuple-element.118), channel_id=1, source_target_pairs={{0,12},{2,14},{4,8},{6,10},{8,4},{10,6},{12,0},{14,2},{1,7},{3,13}... | collective-permute-start | bytes 294920 | tf_op jit(solution)/shard_map/ppermute | solution.py:619
  64.6 30.1 %collective-permute-start.24 = (bf16[2,2,192,256]{3,2,1,0:T(8,128)(2,1)S(1)}, bf16[2,2,192,256]{3,2,1,0:T(8,128)(2,1)S(1)}, u32[]{:S(2)}, u32[]{:S(2)}) collective-permute-start(bf16[2,2,192,256]{3,2,1,0:T(8,128)(2,1)S(1)} %get-tuple-element.130), channel_id=1, source_target_pairs={{0,2},{2,0},{4,6},{6,4},{8,10},{10,8},{12,14},{14,12},{1,15},{3,5}... | collective-permute-start | bytes 1179656 | tf_op jit(solution)/shard_map/ppermute | solution.py:619
  67.3 42.4 %copy-start.1 = (bf16[3,3,256,256]{3,2,1,0:T(8,128)(2,1)S(1)}, bf16[3,3,256,256]{3,2,1,0:T(8,128)(2,1)}, u32[]{:S(2)}) copy-start(bf16[3,3,256,256]{3,2,1,0:T(8,128)(2,1)} %param.10) | copy-start | bytes 3538948
  67.3 6.9 %collective-permute-start.38 = (bf16[144,256]{1,0:T(8,128)(2,1)S(1)}, bf16[144,256]{1,0:T(8,128)(2,1)S(1)}, u32[]{:S(2)}, u32[]{:S(2)}) collective-permute-start(bf16[144,256]{1,0:T(8,128)(2,1)S(1)} %get-tuple-element.168), channel_id=1, source_target_pairs={{0,4},{2,6},{4,0},{6,2},{8,12},{10,14},{12,8},{14,10},{1,5},{3,7},... | collective-permute-start | bytes 221192 | tf_op jit(solution)/shard_map/ppermute | solution.py:670
  67.4 6.8 %collective-permute-start.39 = (bf16[144,256]{1,0:T(8,128)(2,1)S(1)}, bf16[144,256]{1,0:T(8,128)(2,1)S(1)}, u32[]{:S(2)}, u32[]{:S(2)}) collective-permute-start(bf16[144,256]{1,0:T(8,128)(2,1)S(1)} %get-tuple-element.169), channel_id=1, source_target_pairs={{0,8},{2,10},{4,12},{6,14},{8,0},{10,2},{12,4},{14,6},{1,9},{3,11}... | collective-permute-start | bytes 221192 | tf_op jit(solution)/shard_map/ppermute | solution.py:670
  68.4 8.1 %collective-permute-start.40 = (bf16[144,256]{1,0:T(8,128)(2,1)S(1)}, bf16[144,256]{1,0:T(8,128)(2,1)S(1)}, u32[]{:S(2)}, u32[]{:S(2)}) collective-permute-start(bf16[144,256]{1,0:T(8,128)(2,1)S(1)} %get-tuple-element.170), channel_id=1, source_target_pairs={{0,12},{2,14},{4,8},{6,10},{8,4},{10,6},{12,0},{14,2},{1,13},{3,15... | collective-permute-start | bytes 221192 | tf_op jit(solution)/shard_map/ppermute | solution.py:670
  76.5 7.2 %collective-permute-start.43 = (bf16[144,256]{1,0:T(8,128)(2,1)S(1)}, bf16[144,256]{1,0:T(8,128)(2,1)S(1)}, u32[]{:S(2)}, u32[]{:S(2)}) collective-permute-start(bf16[144,256]{1,0:T(8,128)(2,1)S(1)} %shard_map.113), channel_id=1, source_target_pairs={{0,12},{2,14},{4,8},{6,10},{8,4},{10,6},{12,0},{14,2},{1,13},{3,15... | collective-permute-start | bytes 221192 | tf_op jit(solution)/shard_map/ppermute | solution.py:670
  80.6 7.8 %collective-permute-start.42 = (bf16[144,256]{1,0:T(8,128)(2,1)S(1)}, bf16[144,256]{1,0:T(8,128)(2,1)S(1)}, u32[]{:S(2)}, u32[]{:S(2)}) collective-permute-start(bf16[144,256]{1,0:T(8,128)(2,1)S(1)} %shard_map.113), channel_id=1, source_target_pairs={{0,8},{2,10},{4,12},{6,14},{8,0},{10,2},{12,4},{14,6},{1,9},{3,11}... | collective-permute-start | bytes 221192 | tf_op jit(solution)/shard_map/ppermute | solution.py:670
  81.0 9.9 %collective-permute-start.41 = (bf16[144,256]{1,0:T(8,128)(2,1)S(1)}, bf16[144,256]{1,0:T(8,128)(2,1)S(1)}, u32[]{:S(2)}, u32[]{:S(2)}) collective-permute-start(bf16[144,256]{1,0:T(8,128)(2,1)S(1)} %shard_map.113), channel_id=1, source_target_pairs={{0,4},{2,6},{4,0},{6,2},{8,12},{10,14},{12,8},{14,10},{1,5},{3,7},... | collective-permute-start | bytes 221192 | tf_op jit(solution)/shard_map/ppermute | solution.py:670
  81.5 10.3 %collective-permute-start.21 = (bf16[152,256]{1,0:T(8,128)(2,1)S(1)}, bf16[152,256]{1,0:T(8,128)(2,1)S(1)}, u32[]{:S(2)}, u32[]{:S(2)}) collective-permute-start(bf16[152,256]{1,0:T(8,128)(2,1)S(1)} %get-tuple-element.127), channel_id=1, source_target_pairs={{0,4},{2,6},{4,0},{6,2},{8,12},{10,14},{12,8},{14,10},{1,5},{3,7},... | collective-permute-start | bytes 233480 | tf_op jit(solution)/shard_map/ppermute | solution.py:670
  83.7 9.6 %collective-permute-start.22 = (bf16[152,256]{1,0:T(8,128)(2,1)S(1)}, bf16[152,256]{1,0:T(8,128)(2,1)S(1)}, u32[]{:S(2)}, u32[]{:S(2)}) collective-permute-start(bf16[152,256]{1,0:T(8,128)(2,1)S(1)} %get-tuple-element.128), channel_id=1, source_target_pairs={{0,8},{2,10},{4,12},{6,14},{8,0},{10,2},{12,4},{14,6},{1,9},{3,11}... | collective-permute-start | bytes 233480 | tf_op jit(solution)/shard_map/ppermute | solution.py:670
  88.4 6.3 %collective-permute-start.23 = (bf16[152,256]{1,0:T(8,128)(2,1)S(1)}, bf16[152,256]{1,0:T(8,128)(2,1)S(1)}, u32[]{:S(2)}, u32[]{:S(2)}) collective-permute-start(bf16[152,256]{1,0:T(8,128)(2,1)S(1)} %get-tuple-element.129), channel_id=1, source_target_pairs={{0,12},{2,14},{4,8},{6,10},{8,4},{10,6},{12,0},{14,2},{1,13},{3,15... | collective-permute-start | bytes 233480 | tf_op jit(solution)/shard_map/ppermute | solution.py:670
  91.0 3.7 %collective-permute-start.25 = (bf16[2,2,48,256]{3,2,1,0:T(8,128)(2,1)S(1)}, bf16[2,2,48,256]{3,2,1,0:T(8,128)(2,1)S(1)}, u32[]{:S(2)}, u32[]{:S(2)}) collective-permute-start(bf16[2,2,48,256]{3,2,1,0:T(8,128)(2,1)S(1)} %get-tuple-element.131), channel_id=1, source_target_pairs={{1,11},{5,15},{11,1},{15,5},{17,27},{21,31},{27,17},{31,21}} | collective-permute-start | bytes 294920 | tf_op jit(solution)/shard_map/ppermute | solution.py:619
  91.9 17.0 %collective-permute-start.44 = (bf16[576,256]{1,0:T(8,128)(2,1)S(1)}, bf16[576,256]{1,0:T(8,128)(2,1)S(1)}, u32[]{:S(2)}, u32[]{:S(2)}) collective-permute-start(bf16[576,256]{1,0:T(8,128)(2,1)S(1)} %pad_maximum_fusion.refs_0_), channel_id=1, source_target_pairs={{0,2},{2,0},{4,6},{6,4},{8,10},{10,8},{12,14},{14,12},{1,3},{3,1},... | collective-permute-start | bytes 884744 | tf_op jit(solution)/shard_map/ppermute | solution.py:667
  94.7 10.8 %collective-permute-start.28 = (bf16[144,256]{1,0:T(8,128)(2,1)S(1)}, bf16[144,256]{1,0:T(8,128)(2,1)S(1)}, u32[]{:S(2)}, u32[]{:S(2)}) collective-permute-start(bf16[144,256]{1,0:T(8,128)(2,1)S(1)} %get-tuple-element.136), channel_id=1, source_target_pairs={{0,12},{2,14},{4,8},{6,10},{8,4},{10,6},{12,0},{14,2},{1,13},{3,15... | collective-permute-start | bytes 221192 | tf_op jit(solution)/shard_map/ppermute | solution.py:670
  97.8 7.7 %collective-permute-start.27 = (bf16[144,256]{1,0:T(8,128)(2,1)S(1)}, bf16[144,256]{1,0:T(8,128)(2,1)S(1)}, u32[]{:S(2)}, u32[]{:S(2)}) collective-permute-start(bf16[144,256]{1,0:T(8,128)(2,1)S(1)} %get-tuple-element.136), channel_id=1, source_target_pairs={{0,8},{2,10},{4,12},{6,14},{8,0},{10,2},{12,4},{14,6},{1,9},{3,11}... | collective-permute-start | bytes 221192 | tf_op jit(solution)/shard_map/ppermute | solution.py:670
  97.8 5.5 %collective-permute-start.26 = (bf16[144,256]{1,0:T(8,128)(2,1)S(1)}, bf16[144,256]{1,0:T(8,128)(2,1)S(1)}, u32[]{:S(2)}, u32[]{:S(2)}) collective-permute-start(bf16[144,256]{1,0:T(8,128)(2,1)S(1)} %get-tuple-element.136), channel_id=1, source_target_pairs={{0,4},{2,6},{4,0},{6,2},{8,12},{10,14},{12,8},{14,10},{1,5},{3,7},... | collective-permute-start | bytes 221192 | tf_op jit(solution)/shard_map/ppermute | solution.py:670
  99.2 10.4 %collective-permute-start.30 = (bf16[2,2,192,256]{3,2,1,0:T(8,128)(2,1)S(1)}, bf16[2,2,192,256]{3,2,1,0:T(8,128)(2,1)S(1)}, u32[]{:S(2)}, u32[]{:S(2)}) collective-permute-start(bf16[2,2,192,256]{3,2,1,0:T(8,128)(2,1)S(1)} %collective-permute-done.24.refs_0_), channel_id=1, source_target_pairs={{0,1},{1,0},{2,3},{3,2},{4,5},{5,4},{6,7},{7,6},{8,9},{9,8},{10,11... | collective-permute-start | bytes 1179656 | tf_op jit(solution)/shard_map/ppermute | solution.py:589
  105.6 9.7 %collective-permute-start.29 = (bf16[576,256]{1,0:T(8,128)(2,1)S(1)}, bf16[576,256]{1,0:T(8,128)(2,1)S(1)}, u32[]{:S(2)}, u32[]{:S(2)}) collective-permute-start(bf16[576,256]{1,0:T(8,128)(2,1)S(1)} %constant_dynamic-update-slice_fusion.refs_0_), channel_id=1, source_target_pairs={{0,2},{2,0},{4,6},{6,4},{8,10},{10,8},{12,14},{14,12},{1,3},{3,1},... | collective-permute-start | bytes 884744 | tf_op jit(solution)/shard_map/ppermute | solution.py:667
  107.0 1.3 %collective-permute-start.31 = (bf16[2,2,48,256]{3,2,1,0:T(8,128)(2,1)S(1)}, bf16[2,2,48,256]{3,2,1,0:T(8,128)(2,1)S(1)}, u32[]{:S(2)}, u32[]{:S(2)}) collective-permute-start(bf16[2,2,48,256]{3,2,1,0:T(8,128)(2,1)S(1)} %collective-permute-done.19.refs_2_), channel_id=1, source_target_pairs={{0,1},{1,0},{2,3},{3,2},{4,5},{5,4},{6,7},{7,6},{8,9},{9,8},{10,11... | collective-permute-start | bytes 294920 | tf_op jit(solution)/shard_map/ppermute | solution.py:589
  107.0 1.5 %collective-permute-start.32 = (bf16[2,2,48,256]{3,2,1,0:T(8,128)(2,1)S(1)}, bf16[2,2,48,256]{3,2,1,0:T(8,128)(2,1)S(1)}, u32[]{:S(2)}, u32[]{:S(2)}) collective-permute-start(bf16[2,2,48,256]{3,2,1,0:T(8,128)(2,1)S(1)} %collective-permute-done.20.refs_4_), channel_id=1, source_target_pairs={{0,1},{1,0},{2,3},{3,2},{4,5},{5,4},{6,7},{7,6},{8,9},{9,8},{10,11... | collective-permute-start | bytes 294920 | tf_op jit(solution)/shard_map/ppermute | solution.py:589
  108.3 1.3 %collective-permute-start.33 = (bf16[2,2,48,256]{3,2,1,0:T(8,128)(2,1)S(1)}, bf16[2,2,48,256]{3,2,1,0:T(8,128)(2,1)S(1)}, u32[]{:S(2)}, u32[]{:S(2)}) collective-permute-start(bf16[2,2,48,256]{3,2,1,0:T(8,128)(2,1)S(1)} %collective-permute-done.25.refs_6_), channel_id=1, source_target_pairs={{0,1},{1,0},{2,3},{3,2},{4,5},{5,4},{6,7},{7,6},{8,9},{9,8},{10,11... | collective-permute-start | bytes 294920 | tf_op jit(solution)/shard_map/ppermute | solution.py:589
  108.5 7.3 %collective-permute-start.45 = (bf16[576,256]{1,0:T(8,128)(2,1)S(1)}, bf16[576,256]{1,0:T(8,128)(2,1)S(1)}, u32[]{:S(2)}, u32[]{:S(2)}) collective-permute-start(bf16[576,256]{1,0:T(8,128)(2,1)S(1)} %pad_maximum_fusion.refs_0_), channel_id=1, source_target_pairs={{0,1},{1,0},{2,3},{3,2},{4,5},{5,4},{6,7},{7,6},{8,9},{9,8},{10,11... | collective-permute-start | bytes 884744 | tf_op jit(solution)/shard_map/ppermute | solution.py:589
  108.8 7.0 %collective-permute-start.46 = (bf16[576,256]{1,0:T(8,128)(2,1)S(1)}, bf16[576,256]{1,0:T(8,128)(2,1)S(1)}, u32[]{:S(2)}, u32[]{:S(2)}) collective-permute-start(bf16[576,256]{1,0:T(8,128)(2,1)S(1)} %collective-permute-done.44.refs_1_), channel_id=1, source_target_pairs={{0,1},{1,0},{2,3},{3,2},{4,5},{5,4},{6,7},{7,6},{8,9},{9,8},{10,11... | collective-permute-start | bytes 884744 | tf_op jit(solution)/shard_map/ppermute | solution.py:589
  115.3 2.3 %collective-permute-start.35 = (bf16[576,256]{1,0:T(8,128)(2,1)S(1)}, bf16[576,256]{1,0:T(8,128)(2,1)S(1)}, u32[]{:S(2)}, u32[]{:S(2)}) collective-permute-start(bf16[576,256]{1,0:T(8,128)(2,1)S(1)} %collective-permute-done.29.refs_1_), channel_id=1, source_target_pairs={{0,1},{1,0},{2,3},{3,2},{4,5},{5,4},{6,7},{7,6},{8,9},{9,8},{10,11... | collective-permute-start | bytes 884744 | tf_op jit(solution)/shard_map/ppermute | solution.py:589
  115.4 2.2 %collective-permute-start.34 = (bf16[576,256]{1,0:T(8,128)(2,1)S(1)}, bf16[576,256]{1,0:T(8,128)(2,1)S(1)}, u32[]{:S(2)}, u32[]{:S(2)}) collective-permute-start(bf16[576,256]{1,0:T(8,128)(2,1)S(1)} %constant_dynamic-update-slice_fusion.refs_0_), channel_id=1, source_target_pairs={{0,1},{1,0},{2,3},{3,2},{4,5},{5,4},{6,7},{7,6},{8,9},{9,8},{10,11... | collective-permute-start | bytes 884744 | tf_op jit(solution)/shard_map/ppermute | solution.py:589

commit v10 on v9

--- a/solution.py
+++ b/solution.py
@@ -134,19 +134,11 @@
         ref[which] = jnp.dot(hot, sources[which], preferred_element_type=F32).astype(BF)
 
 
-def pack_kernel(dm, ep, x_hbm, up_hbm, *refs):
-    *refs, self_ref, x_ref, up_ref, sems = refs
-    copies = [
-        pltpu.make_async_copy(x_hbm, x_ref, sems.at[0]),
-        pltpu.make_async_copy(up_hbm, up_ref, sems.at[1]),
-    ]
-    for copy in copies:
-        copy.start()
-    for copy in copies:
-        copy.wait()
+def pack_kernel(dm, ep, x_ref, up_ref, *refs):
     t, p = lax.axis_index("tile"), lax.axis_index("dp")
-    write_messages(dm, ep, t, p, (x_ref[...], up_ref[...]), refs)
-    write_self(dm, ep, t, (x_ref[...], up_ref[...]), self_ref)
+    fields = (x_ref[...], up_ref[...])
+    write_messages(dm, ep, t, p, fields, refs[:-1])
+    write_self(dm, ep, t, fields, refs[-1])
 
 
 def merge_kernel(count, *refs):
@@ -566,18 +558,17 @@
                 out_ref[tap, at] = ref[row : row + size].astype(F32) * scale
 
 
-def call(kernel, out_shapes, scratch=(), smem_first=False, limit=16, raw=()):
+def call(kernel, out_shapes, scratch=(), smem_first=False, limit=16):
     def run(*args):
         vmem = pl.BlockSpec(memory_space=pltpu.VMEM)
         smem = pl.BlockSpec(memory_space=pltpu.SMEM)
-        hbm = pl.BlockSpec(memory_space=pl.ANY)
-        specs = [smem if smem_first and i == 0 else hbm if i in raw else vmem for i in range(len(args))]
+        specs = [smem if smem_first and i == 0 else vmem for i in range(len(args))]
         return pl.pallas_call(
             kernel,
             out_shape=[jax.ShapeDtypeStruct(s, dt) for s, dt in out_shapes],
             in_specs=specs,
             out_specs=[vmem] * len(out_shapes),
-            scratch_shapes=[pltpu.VMEM(s, dt) for s, dt in scratch] + [pltpu.SemaphoreType.DMA((2,))] * bool(raw),
+            scratch_shapes=[pltpu.VMEM(s, dt) for s, dt in scratch],
             compiler_params=pltpu.CompilerParams(vmem_limit_bytes=limit << 20),
         )(*args)
 
@@ -619,11 +610,12 @@
         return lax.ppermute(v, ("tile", "dp"), pairs[step])
 
     packed = call(
-        functools.partial(pack_kernel, dm), msg_shapes, [(flat, BF)] * 2, smem_first=True, raw=(1, 2)
+        functools.partial(pack_kernel, dm), msg_shapes, smem_first=True
     )(edge_partner, x.reshape(flat), d.reshape(flat))
+    came = [across(v, i) for i, v in enumerate(merged(packed))]
+    came, w1s, w1t, w2t = lax.optimization_barrier((came, w1s, w1t, w2t))
     messages = []
-    for i, v in enumerate(merged(packed)):
-        v = across(v, i)
+    for v in came:
         messages += [v, swap_dp(v)]
     messages.append(packed[-1])
     half = channels // 2

time: 120 us -> 108 us (0.900)
  waiting for transfers between devices: 39.9 us -> 29.2 us
    ppermute x8, waiting for transfers between devices: 19.6 us -> 8.5 us  [across(): return lax.ppermute(v, ('tile', 'dp'), pairs[step])]
    ppermute x8, starting transfers between devices: 11.1 us -> 15.5 us  [across(): return lax.ppermute(v, ('tile', 'dp'), pairs[step])]
    ppermute x23, starting transfers between devices: 14.1 us -> 11.4 us  [swap_dp(): return lax.ppermute(v, 'dp', [(i, count - 1 - i) for i in range(count)])]
    ppermute x4, waiting for transfers between devices: 2.51 us -> 0.03 us  [along_y(): return lax.ppermute(v, 'tile', [(i, i ^ 1) for i in range(tiles)])]
    ppermute x12, waiting for transfers between devices: 12 us -> 13.9 us  [along_z(): return lax.ppermute(v, 'tile', [(i, i ^ 2 * j) for i in range(tiles)])]
    ppermute x4, starting transfers between devices: 3.77 us -> 2.23 us  [along_y(): return lax.ppermute(v, 'tile', [(i, i ^ 1) for i in range(tiles)])]
  transfers between devices with their start and end apart: 47 -> 47, of which waited for: 19 -> 22; matrix products, arithmetic and copies ran while one was open for 0% -> 0% of each run, Pallas kernels for 7% -> 8%
where the time goes in v10:
time: 108 us
  starting transfers between devices  51.7 us (48%)
  waiting for transfers between devices  29.2 us (27%)
  Pallas kernels  20.9 us (19%)
  local copies, waits for them, and re-layouts  5.22 us (5%)
    ppermute x12, starting transfers between devices, along_z(): return lax.ppermute(v, 'tile', [(i, i ^ 2 * j) for i in range(tiles)])  22.7 us
    pallas_call x14, Pallas kernels, run(): pl.pallas_call(kernel, out_shape=[jax.ShapeDtypeStruct(s, dt) for s, dt i...  20.9 us
    ppermute x8, starting transfers between devices, across(): return lax.ppermute(v, ('tile', 'dp'), pairs[step])  15.5 us
    ppermute x12, waiting for transfers between devices, along_z(): return lax.ppermute(v, 'tile', [(i, i ^ 2 * j) for i in range(tiles)])  13.9 us
    ppermute x23, starting transfers between devices, swap_dp(): return lax.ppermute(v, 'dp', [(i, count - 1 - i) for i in range(count)])  11.4 us
    ppermute x8, waiting for transfers between devices, across(): return lax.ppermute(v, ('tile', 'dp'), pairs[step])  8.5 us
    ppermute x23, waiting for transfers between devices, swap_dp(): return lax.ppermute(v, 'dp', [(i, count - 1 - i) for i in range(count)])  6.79 us
    unnamed x20, local copies, waits for them, and re-layouts  5.21 us
  transfers between devices with their start and end apart: 47, of which 22 were waited for; matrix products, arithmetic and copies ran while one was open for 0% of the time, Pallas kernels for 8%

profile of v10, /device:TPU:0, one launch (start us, length us, event | category | flops | bytes accessed | tf_op | source)
XLA Modules:
  0.0 107.9 jit_solution(5245187919419210917)
XLA Ops:
  0.6 0.8 copy.12.ep
  1.4 0.9 copy-done.2
  2.3 0.9 copy-done.4
  3.3 2.2 %shard_map.101 = (bf16[2,192,256]{2,1,0:T(8,128)(2,1)S(1)}, bf16[2,48,256]{2,1,0:T(8,128)(2,1)S(1)}, bf16[2,48,256]{2,1,0:T(8,128)(2,1)S(1)}, bf16[2,48,256]{2,1...) custom-call(s32[6,4]{1,0:T(8,128)S(1)} %copy.12.ep, ...), custom_call_target="tpu_custom_call" | custom-call | tf_op jit(solution)/shard_map/pallas_call | solution.py:566
  5.4 0.5 collective-permute-start
  6.0 0.4 collective-permute-start.2
  6.5 0.6 collective-permute-done.1.refs_5_
  7.3 0.3 collective-permute-done.3.refs_7_
  7.7 2.7 %collective-permute-start.4 = (bf16[2,2,192,256]{3,2,1,0:T(8,128)(2,1)S(1)}, bf16[2,2,192,256]{3,2,1,0:T(8,128)(2,1)S(1)}, u32[]{:S(2)}, u32[]{:S(2)}) collective-permute-start(bf16[2,2,192,256]{3,2,1,0:T(8,128)(2,1)S(1)} %get-tuple-element.103), channel_id=1, source_target_pairs={{0,2},{2,0},{4,6},{6,4},{8,10},{10,8},{12,14},{14,12},{1,15},{3,5}... | collective-permute-start | bytes 1179656 | tf_op jit(solution)/shard_map/ppermute | solution.py:610
  10.5 3.5 %collective-permute-start.5 = (bf16[2,2,48,256]{3,2,1,0:T(8,128)(2,1)S(1)}, bf16[2,2,48,256]{3,2,1,0:T(8,128)(2,1)S(1)}, u32[]{:S(2)}, u32[]{:S(2)}) collective-permute-start(bf16[2,2,48,256]{3,2,1,0:T(8,128)(2,1)S(1)} %get-tuple-element.104), channel_id=1, source_target_pairs={{0,4},{4,0},{10,14},{14,10},{1,9},{3,11},{5,13},{7,15},{9,1},{11,3... | collective-permute-start | bytes 294920 | tf_op jit(solution)/shard_map/ppermute | solution.py:610
  14.0 0.9 collective-permute-start.6
  14.8 0.7 collective-permute-start.7
  15.5 1.3 %copy-done = bf16[3,3,256,256]{3,2,1,0:T(8,128)(2,1)S(1)} copy-done((bf16[3,3,256,256]{3,2,1,0:T(8,128)(2,1)S(1)}, bf16[3,3,256,256]{3,2,1,0:T(8,128)(2,1)}, u32[]{:S(2)}) %copy-start) | copy-done | bytes 1179672
  16.8 1.3 %copy-done.6 = bf16[3,3,256,256]{3,2,1,0:T(8,128)(2,1)S(1)} copy-done((bf16[3,3,256,256]{3,2,1,0:T(8,128)(2,1)S(1)}, bf16[3,3,256,256]{3,2,1,0:T(8,128)(2,1)}, u32[]{:S(2)}) %copy-start.6) | copy-done | bytes 1179672
  18.0 0.7 shard_map.103
  18.7 2.9 %collective-permute-done.6.refs_4_ = bf16[2,2,48,256]{3,2,1,0:T(8,128)(2,1)S(1)} collective-permute-done((bf16[2,2,48,256]{3,2,1,0:T(8,128)(2,1)S(1)}, bf16[2,2,48,256]{3,2,1,0:T(8,128)(2,1)S(1)}, u32[]{:S(2)}, u32[]{:S(2)}) %collective-permute-start.6) | collective-permute-done | bytes 98336 | tf_op jit(solution)/shard_map/ppermute | solution.py:610
  21.7 4.5 %collective-permute-start.8 = (bf16[2,2,192,256]{3,2,1,0:T(8,128)(2,1)S(1)}, bf16[2,2,192,256]{3,2,1,0:T(8,128)(2,1)S(1)}, u32[]{:S(2)}, u32[]{:S(2)}) collective-permute-start(bf16[2,2,192,256]{3,2,1,0:T(8,128)(2,1)S(1)} %collective-permute-done.4.refs_0_), channel_id=1, source_target_pairs={{0,1},{1,0},{2,3},{3,2},{4,5},{5,4},{6,7},{7,6},{8,9},{9,8},{10,11... | collective-permute-start | bytes 1179656 | tf_op jit(solution)/shard_map/ppermute | solution.py:580
  26.2 0.5 collective-permute-start.10
  26.7 1.0 collective-permute-done.9.refs_3_
  27.8 0.2 collective-permute-done.11.refs_7_
  28.0 8.3 %shard_map.104 = (bf16[9,128,256]{2,1,0:T(8,128)(2,1)S(1)}, f32[9,128,256]{2,1,0:T(8,128)S(1)}, bf16[9,128,256]{2,1,0:T(8,128)(2,1)S(1)}, f32[9,128,256]{2,1,0:T...) custom-call(s32[6,4]{1,0:T(8,128)S(1)} %copy.12.ep, ...), custom_call_target="tpu_custom_call" | custom-call | tf_op jit(solution)/shard_map/pallas_call | solution.py:566
  36.3 0.4 collective-permute-start.12
  36.7 0.2 collective-permute-start.36
  36.8 0.3 collective-permute-start.13
  37.2 2.0 %collective-permute-done.13.refs_1_ = bf16[8,256]{1,0:T(8,128)(2,1)S(1)} collective-permute-done((bf16[8,256]{1,0:T(8,128)(2,1)S(1)}, bf16[8,256]{1,0:T(8,128)(2,1)S(1)}, u32[]{:S(2)}, u32[]{:S(2)}) %collective-permute-start.13) | collective-permute-done | bytes 4128 | tf_op jit(solution)/shard_map/ppermute | solution.py:580
  39.4 0.4 collective-permute-start.15
  39.8 0.2 collective-permute-start.16
  40.1 2.0 %collective-permute-start.37 = (bf16[576,256]{1,0:T(8,128)(2,1)S(1)}, bf16[576,256]{1,0:T(8,128)(2,1)S(1)}, u32[]{:S(2)}, u32[]{:S(2)}) collective-permute-start(bf16[576,256]{1,0:T(8,128)(2,1)S(1)} %get-tuple-element.180), channel_id=1, source_target_pairs={{0,2},{2,0},{4,6},{6,4},{8,10},{10,8},{12,14},{14,12},{1,3},{3,1},... | collective-permute-start | bytes 884744 | tf_op jit(solution)/shard_map/ppermute | solution.py:659
  42.1 0.5 collective-permute-start.18
  42.6 0.7 collective-permute-done.17.refs_6_
  43.6 2.8 %collective-permute-start.19 = (bf16[2,2,48,256]{3,2,1,0:T(8,128)(2,1)S(1)}, bf16[2,2,48,256]{3,2,1,0:T(8,128)(2,1)S(1)}, u32[]{:S(2)}, u32[]{:S(2)}) collective-permute-start(bf16[2,2,48,256]{3,2,1,0:T(8,128)(2,1)S(1)} %get-tuple-element.131), channel_id=1, source_target_pairs={{0,4},{4,0},{10,14},{14,10},{1,9},{3,11},{5,13},{7,15},{9,1},{11,3... | collective-permute-start | bytes 294920 | tf_op jit(solution)/shard_map/ppermute | solution.py:610
  46.4 1.6 %collective-permute-start.20 = (bf16[2,2,48,256]{3,2,1,0:T(8,128)(2,1)S(1)}, bf16[2,2,48,256]{3,2,1,0:T(8,128)(2,1)S(1)}, u32[]{:S(2)}, u32[]{:S(2)}) collective-permute-start(bf16[2,2,48,256]{3,2,1,0:T(8,128)(2,1)S(1)} %get-tuple-element.132), channel_id=1, source_target_pairs={{0,12},{2,14},{4,8},{6,10},{8,4},{10,6},{12,0},{14,2},{1,7},{3,13}... | collective-permute-start | bytes 294920 | tf_op jit(solution)/shard_map/ppermute | solution.py:610
  48.0 3.1 %collective-permute-done.19.refs_2_ = bf16[2,2,48,256]{3,2,1,0:T(8,128)(2,1)S(1)} collective-permute-done((bf16[2,2,48,256]{3,2,1,0:T(8,128)(2,1)S(1)}, bf16[2,2,48,256]{3,2,1,0:T(8,128)(2,1)S(1)}, u32[]{:S(2)}, u32[]{:S(2)}) %collective-permute-start.19) | collective-permute-done | bytes 98336 | tf_op jit(solution)/shard_map/ppermute | solution.py:610
  51.1 2.4 %collective-permute-done.20.refs_4_ = bf16[2,2,48,256]{3,2,1,0:T(8,128)(2,1)S(1)} collective-permute-done((bf16[2,2,48,256]{3,2,1,0:T(8,128)(2,1)S(1)}, bf16[2,2,48,256]{3,2,1,0:T(8,128)(2,1)S(1)}, u32[]{:S(2)}, u32[]{:S(2)}) %collective-permute-start.20) | collective-permute-done | bytes 98336 | tf_op jit(solution)/shard_map/ppermute | solution.py:610
  53.6 2.5 %collective-permute-start.24 = (bf16[2,2,192,256]{3,2,1,0:T(8,128)(2,1)S(1)}, bf16[2,2,192,256]{3,2,1,0:T(8,128)(2,1)S(1)}, u32[]{:S(2)}, u32[]{:S(2)}) collective-permute-start(bf16[2,2,192,256]{3,2,1,0:T(8,128)(2,1)S(1)} %get-tuple-element.144), channel_id=1, source_target_pairs={{0,2},{2,0},{4,6},{6,4},{8,10},{10,8},{12,14},{14,12},{1,15},{3,5}... | collective-permute-start | bytes 1179656 | tf_op jit(solution)/shard_map/ppermute | solution.py:610
  56.3 0.9 collective-permute-start.38
  57.2 2.9 %collective-permute-start.39 = (bf16[144,256]{1,0:T(8,128)(2,1)S(1)}, bf16[144,256]{1,0:T(8,128)(2,1)S(1)}, u32[]{:S(2)}, u32[]{:S(2)}) collective-permute-start(bf16[144,256]{1,0:T(8,128)(2,1)S(1)} %get-tuple-element.183), channel_id=1, source_target_pairs={{0,8},{2,10},{4,12},{6,14},{8,0},{10,2},{12,4},{14,6},{1,9},{3,11}... | collective-permute-start | bytes 221192 | tf_op jit(solution)/shard_map/ppermute | solution.py:662
  60.1 0.6 collective-permute-start.40
  60.7 0.8 collective-permute-done.38.refs_0_
  61.5 2.4 %collective-permute-done.39.refs_1_ = bf16[144,256]{1,0:T(8,128)(2,1)S(1)} collective-permute-done((bf16[144,256]{1,0:T(8,128)(2,1)S(1)}, bf16[144,256]{1,0:T(8,128)(2,1)S(1)}, u32[]{:S(2)}, u32[]{:S(2)}) %collective-permute-start.39) | collective-permute-done | bytes 73760 | tf_op jit(solution)/shard_map/ppermute | solution.py:662
  64.0 3.2 %collective-permute-done.40.refs_2_ = bf16[144,256]{1,0:T(8,128)(2,1)S(1)} collective-permute-done((bf16[144,256]{1,0:T(8,128)(2,1)S(1)}, bf16[144,256]{1,0:T(8,128)(2,1)S(1)}, u32[]{:S(2)}, u32[]{:S(2)}) %collective-permute-start.40) | collective-permute-done | bytes 73760 | tf_op jit(solution)/shard_map/ppermute | solution.py:662
  67.2 4.2 %collective-permute-start.43 = (bf16[144,256]{1,0:T(8,128)(2,1)S(1)}, bf16[144,256]{1,0:T(8,128)(2,1)S(1)}, u32[]{:S(2)}, u32[]{:S(2)}) collective-permute-start(bf16[144,256]{1,0:T(8,128)(2,1)S(1)} %shard_map.113), channel_id=1, source_target_pairs={{0,12},{2,14},{4,8},{6,10},{8,4},{10,6},{12,0},{14,2},{1,13},{3,15... | collective-permute-start | bytes 221192 | tf_op jit(solution)/shard_map/ppermute | solution.py:662
  71.4 0.2 collective-permute-start.42
  71.6 0.5 collective-permute-start.41
  72.1 1.5 %collective-permute-start.21 = (bf16[152,256]{1,0:T(8,128)(2,1)S(1)}, bf16[152,256]{1,0:T(8,128)(2,1)S(1)}, u32[]{:S(2)}, u32[]{:S(2)}) collective-permute-start(bf16[152,256]{1,0:T(8,128)(2,1)S(1)} %get-tuple-element.141), channel_id=1, source_target_pairs={{0,4},{2,6},{4,0},{6,2},{8,12},{10,14},{12,8},{14,10},{1,5},{3,7},... | collective-permute-start | bytes 233480 | tf_op jit(solution)/shard_map/ppermute | solution.py:662
  73.6 0.5 collective-permute-done.43
  74.1 4.7 %collective-permute-start.22 = (bf16[152,256]{1,0:T(8,128)(2,1)S(1)}, bf16[152,256]{1,0:T(8,128)(2,1)S(1)}, u32[]{:S(2)}, u32[]{:S(2)}) collective-permute-start(bf16[152,256]{1,0:T(8,128)(2,1)S(1)} %get-tuple-element.142), channel_id=1, source_target_pairs={{0,8},{2,10},{4,12},{6,14},{8,0},{10,2},{12,4},{14,6},{1,9},{3,11}... | collective-permute-start | bytes 233480 | tf_op jit(solution)/shard_map/ppermute | solution.py:662
  78.9 2.6 %collective-permute-start.23 = (bf16[152,256]{1,0:T(8,128)(2,1)S(1)}, bf16[152,256]{1,0:T(8,128)(2,1)S(1)}, u32[]{:S(2)}, u32[]{:S(2)}) collective-permute-start(bf16[152,256]{1,0:T(8,128)(2,1)S(1)} %get-tuple-element.143), channel_id=1, source_target_pairs={{0,12},{2,14},{4,8},{6,10},{8,4},{10,6},{12,0},{14,2},{1,13},{3,15... | collective-permute-start | bytes 233480 | tf_op jit(solution)/shard_map/ppermute | solution.py:662
  81.5 0.8 collective-permute-start.25
  82.4 0.8 collective-permute-done.22.refs_1_
  83.3 1.8 %collective-permute-done.23.refs_2_ = bf16[152,256]{1,0:T(8,128)(2,1)S(1)} collective-permute-done((bf16[152,256]{1,0:T(8,128)(2,1)S(1)}, bf16[152,256]{1,0:T(8,128)(2,1)S(1)}, u32[]{:S(2)}, u32[]{:S(2)}) %collective-permute-start.23) | collective-permute-done | bytes 77856 | tf_op jit(solution)/shard_map/ppermute | solution.py:662
  85.1 3.6 %collective-permute-start.28 = (bf16[144,256]{1,0:T(8,128)(2,1)S(1)}, bf16[144,256]{1,0:T(8,128)(2,1)S(1)}, u32[]{:S(2)}, u32[]{:S(2)}) collective-permute-start(bf16[144,256]{1,0:T(8,128)(2,1)S(1)} %get-tuple-element.150), channel_id=1, source_target_pairs={{0,12},{2,14},{4,8},{6,10},{8,4},{10,6},{12,0},{14,2},{1,13},{3,15... | collective-permute-start | bytes 221192 | tf_op jit(solution)/shard_map/ppermute | solution.py:662
  88.7 0.9 collective-permute-start.26
  89.6 1.5 %collective-permute-start.30 = (bf16[2,2,192,256]{3,2,1,0:T(8,128)(2,1)S(1)}, bf16[2,2,192,256]{3,2,1,0:T(8,128)(2,1)S(1)}, u32[]{:S(2)}, u32[]{:S(2)}) collective-permute-start(bf16[2,2,192,256]{3,2,1,0:T(8,128)(2,1)S(1)} %collective-permute-done.24.refs_0_), channel_id=1, source_target_pairs={{0,1},{1,0},{2,3},{3,2},{4,5},{5,4},{6,7},{7,6},{8,9},{9,8},{10,11... | collective-permute-start | bytes 1179656 | tf_op jit(solution)/shard_map/ppermute | solution.py:580
  91.1 3.3 %collective-permute-done.26 = bf16[144,256]{1,0:T(8,128)(2,1)S(1)} collective-permute-done((bf16[144,256]{1,0:T(8,128)(2,1)S(1)}, bf16[144,256]{1,0:T(8,128)(2,1)S(1)}, u32[]{:S(2)}, u32[]{:S(2)}) %collective-permute-start.26) | collective-permute-done | bytes 73760 | tf_op jit(solution)/shard_map/ppermute | solution.py:662
  94.5 1.0 collective-permute-done.27
  95.6 0.5 collective-permute-start.32
  96.1 0.8 collective-permute-done.31.refs_3_
  97.0 0.4 collective-permute-start.45
  97.6 0.6 collective-permute-done.33.refs_7_
  98.2 5.6 %shard_map.109 = (bf16[18,24,256]{2,1,0:T(8,128)(2,1)}, f32[18,24,256]{2,1,0:T(8,128)}) custom-call(s32[6,4]{1,0:T(8,128)S(1)} %copy.12.ep, bf16[18,24,256]{2,1,0:T(8,128)(2,1)S(1)} %bitcast.20, bf16[18,24,256]{2,1,0:T(8,128)(2,1)S(1)} %bitcast.23, bf16[18,24,256]{2,1,0:T(8,128)(2,1)S(1)} %get-tuple-element.151.hid_ref, ...), custom_call_target="tpu_custom_call" | custom-call | tf_op jit(solution)/shard_map/pallas_call | solution.py:566
  104.0 0.4 collective-permute-start.34
  104.4 1.8 %shard_map.114 = f32[9,256,256]{2,1,0:T(8,128)} custom-call(bf16[576,256]{1,0:T(8,128)(2,1)S(1)} %pad_maximum_fusion.refs_0_, bf16[576,256]{1,0:T(8,128)(2,1)S(1)} %collective-permute-done.44.refs_1_, bf16[576,256]{1,0:T(8,128)(2,1)S(1)} %collective-permute-done.45.refs_2_, bf16[576,256]{1,0:T(8,128)(2,1)S(1)} %collective-permute-done.46.refs_3_), custom_call_target="tpu_custom_call" | custom-call | tf_op jit(solution)/shard_map/pallas_call | solution.py:566
  106.2 1.8 %shard_map.110 = (f32[9,256,256]{2,1,0:T(8,128)}, f32[1,256]{1,0:T(1,128)}) custom-call(bf16[576,256]{1,0:T(8,128)(2,1)S(1)} %constant_dynamic-update-slice_fusion.refs_0_, bf16[576,256]{1,0:T(8,128)(2,1)S(1)} %collective-permute-done.29.refs_1_, bf16[576,256]{1,0:T(8,128)(2,1)S(1)} %collective-permute-done.34.refs_2_, ...), custom_call_target="tpu_custom_call" | custom-call | tf_op jit(solution)/shard_map/pallas_call | solution.py:566
  (66 shorter events, 2.1 us)
Async XLA Ops:
  1.4 0.9 copy-start.2
  2.3 0.9 copy-start.4
  5.4 2.3 %collective-permute-start = (bf16[2,192,256]{2,1,0:T(8,128)(2,1)S(1)}, bf16[2,192,256]{2,1,0:T(8,128)(2,1)S(1)}, u32[]{:S(2)}, u32[]{:S(2)}) collective-permute-start(bf16[2,192,256]{2,1,0:T(8,128)(2,1)S(1)} %get-tuple-element.99), channel_id=1, source_target_pairs={{0,1},{1,0},{2,3},{3,2},{4,5},{5,4},{6,7},{7,6},{8,9},{9,8},{10,11... | collective-permute-start | bytes 589832 | tf_op jit(solution)/shard_map/ppermute | solution.py:580
  6.0 1.2 %collective-permute-start.1 = (bf16[2,48,256]{2,1,0:T(8,128)(2,1)S(1)}, bf16[2,48,256]{2,1,0:T(8,128)(2,1)S(1)}, u32[]{:S(2)}, u32[]{:S(2)}) collective-permute-start(bf16[2,48,256]{2,1,0:T(8,128)(2,1)S(1)} %get-tuple-element.100), channel_id=1, source_target_pairs={{0,1},{1,0},{2,3},{3,2},{4,5},{5,4},{6,7},{7,6},{8,9},{9,8},{10,11... | collective-permute-start | bytes 147464 | tf_op jit(solution)/shard_map/ppermute | solution.py:580
  6.0 1.3 %collective-permute-start.2 = (bf16[2,48,256]{2,1,0:T(8,128)(2,1)S(1)}, bf16[2,48,256]{2,1,0:T(8,128)(2,1)S(1)}, u32[]{:S(2)}, u32[]{:S(2)}) collective-permute-start(bf16[2,48,256]{2,1,0:T(8,128)(2,1)S(1)} %get-tuple-element.101), channel_id=1, source_target_pairs={{0,1},{1,0},{2,3},{3,2},{4,5},{5,4},{6,7},{7,6},{8,9},{9,8},{10,11... | collective-permute-start | bytes 147464 | tf_op jit(solution)/shard_map/ppermute | solution.py:580
  6.5 1.2 %collective-permute-start.3 = (bf16[2,48,256]{2,1,0:T(8,128)(2,1)S(1)}, bf16[2,48,256]{2,1,0:T(8,128)(2,1)S(1)}, u32[]{:S(2)}, u32[]{:S(2)}) collective-permute-start(bf16[2,48,256]{2,1,0:T(8,128)(2,1)S(1)} %get-tuple-element.102), channel_id=1, source_target_pairs={{0,1},{1,0},{2,3},{3,2},{4,5},{5,4},{6,7},{7,6},{8,9},{9,8},{10,11... | collective-permute-start | bytes 147464 | tf_op jit(solution)/shard_map/ppermute | solution.py:580
  7.7 13.9 %collective-permute-start.4 = (bf16[2,2,192,256]{3,2,1,0:T(8,128)(2,1)S(1)}, bf16[2,2,192,256]{3,2,1,0:T(8,128)(2,1)S(1)}, u32[]{:S(2)}, u32[]{:S(2)}) collective-permute-start(bf16[2,2,192,256]{3,2,1,0:T(8,128)(2,1)S(1)} %get-tuple-element.103), channel_id=1, source_target_pairs={{0,2},{2,0},{4,6},{6,4},{8,10},{10,8},{12,14},{14,12},{1,15},{3,5}... | collective-permute-start | bytes 1179656 | tf_op jit(solution)/shard_map/ppermute | solution.py:610
  10.5 8.2 %collective-permute-start.5 = (bf16[2,2,48,256]{3,2,1,0:T(8,128)(2,1)S(1)}, bf16[2,2,48,256]{3,2,1,0:T(8,128)(2,1)S(1)}, u32[]{:S(2)}, u32[]{:S(2)}) collective-permute-start(bf16[2,2,48,256]{3,2,1,0:T(8,128)(2,1)S(1)} %get-tuple-element.104), channel_id=1, source_target_pairs={{0,4},{4,0},{10,14},{14,10},{1,9},{3,11},{5,13},{7,15},{9,1},{11,3... | collective-permute-start | bytes 294920 | tf_op jit(solution)/shard_map/ppermute | solution.py:610
  14.0 7.7 %collective-permute-start.6 = (bf16[2,2,48,256]{3,2,1,0:T(8,128)(2,1)S(1)}, bf16[2,2,48,256]{3,2,1,0:T(8,128)(2,1)S(1)}, u32[]{:S(2)}, u32[]{:S(2)}) collective-permute-start(bf16[2,2,48,256]{3,2,1,0:T(8,128)(2,1)S(1)} %get-tuple-element.105), channel_id=1, source_target_pairs={{0,12},{2,14},{4,8},{6,10},{8,4},{10,6},{12,0},{14,2},{1,7},{3,13}... | collective-permute-start | bytes 294920 | tf_op jit(solution)/shard_map/ppermute | solution.py:610
  14.8 6.8 %collective-permute-start.7 = (bf16[2,2,48,256]{3,2,1,0:T(8,128)(2,1)S(1)}, bf16[2,2,48,256]{3,2,1,0:T(8,128)(2,1)S(1)}, u32[]{:S(2)}, u32[]{:S(2)}) collective-permute-start(bf16[2,2,48,256]{3,2,1,0:T(8,128)(2,1)S(1)} %get-tuple-element.106), channel_id=1, source_target_pairs={{1,11},{5,15},{11,1},{15,5},{17,27},{21,31},{27,17},{31,21}} | collective-permute-start | bytes 294920 | tf_op jit(solution)/shard_map/ppermute | solution.py:610
  15.5 1.3 %copy-start = (bf16[3,3,256,256]{3,2,1,0:T(8,128)(2,1)S(1)}, bf16[3,3,256,256]{3,2,1,0:T(8,128)(2,1)}, u32[]{:S(2)}) copy-start(bf16[3,3,256,256]{3,2,1,0:T(8,128)(2,1)} %param.10) | copy-start | bytes 3538948
  16.8 1.3 %copy-start.6 = (bf16[3,3,256,256]{3,2,1,0:T(8,128)(2,1)S(1)}, bf16[3,3,256,256]{3,2,1,0:T(8,128)(2,1)}, u32[]{:S(2)}) copy-start(bf16[3,3,256,256]{3,2,1,0:T(8,128)(2,1)} %param.8) | copy-start | bytes 3538948
  18.0 9.9 %copy-start.3 = (bf16[1,6,3,24,256]{4,3,2,1,0:T(8,128)(2,1)S(1)}, bf16[1,6,3,24,256]{4,3,2,1,0:T(8,128)(2,1)}, u32[]{:S(2)}) copy-start(bf16[1,6,3,24,256]{4,3,2,1,0:T(8,128)(2,1)} %param.6) | copy-start | bytes 663556
  18.0 9.9 %copy-start.5 = (bf16[1,1,6,3,24,256]{5,4,3,2,1,0:T(8,128)(2,1)S(1)}, bf16[1,1,6,3,24,256]{5,4,3,2,1,0:T(8,128)(2,1)}, u32[]{:S(2)}) copy-start(bf16[1,1,6,3,24,256]{5,4,3,2,1,0:T(8,128)(2,1)} %param.7) | copy-start | bytes 663556
  18.0 9.9 %copy-start.7 = (f32[256]{0:T(256)S(1)}, f32[256]{0:T(256)}, u32[]{:S(2)}) copy-start(f32[256]{0:T(256)} %param.9) | copy-start | bytes 3076
  21.7 6.3 %collective-permute-start.8 = (bf16[2,2,192,256]{3,2,1,0:T(8,128)(2,1)S(1)}, bf16[2,2,192,256]{3,2,1,0:T(8,128)(2,1)S(1)}, u32[]{:S(2)}, u32[]{:S(2)}) collective-permute-start(bf16[2,2,192,256]{3,2,1,0:T(8,128)(2,1)S(1)} %collective-permute-done.4.refs_0_), channel_id=1, source_target_pairs={{0,1},{1,0},{2,3},{3,2},{4,5},{5,4},{6,7},{7,6},{8,9},{9,8},{10,11... | collective-permute-start | bytes 1179656 | tf_op jit(solution)/shard_map/ppermute | solution.py:580
  26.1 1.5 %collective-permute-start.9 = (bf16[2,2,48,256]{3,2,1,0:T(8,128)(2,1)S(1)}, bf16[2,2,48,256]{3,2,1,0:T(8,128)(2,1)S(1)}, u32[]{:S(2)}, u32[]{:S(2)}) collective-permute-start(bf16[2,2,48,256]{3,2,1,0:T(8,128)(2,1)S(1)} %collective-permute-done.5.refs_2_), channel_id=1, source_target_pairs={{0,1},{1,0},{2,3},{3,2},{4,5},{5,4},{6,7},{7,6},{8,9},{9,8},{10,11... | collective-permute-start | bytes 294920 | tf_op jit(solution)/shard_map/ppermute | solution.py:580
  26.2 1.6 %collective-permute-start.10 = (bf16[2,2,48,256]{3,2,1,0:T(8,128)(2,1)S(1)}, bf16[2,2,48,256]{3,2,1,0:T(8,128)(2,1)S(1)}, u32[]{:S(2)}, u32[]{:S(2)}) collective-permute-start(bf16[2,2,48,256]{3,2,1,0:T(8,128)(2,1)S(1)} %collective-permute-done.6.refs_4_), channel_id=1, source_target_pairs={{0,1},{1,0},{2,3},{3,2},{4,5},{5,4},{6,7},{7,6},{8,9},{9,8},{10,11... | collective-permute-start | bytes 294920 | tf_op jit(solution)/shard_map/ppermute | solution.py:580
  26.7 1.3 %collective-permute-start.11 = (bf16[2,2,48,256]{3,2,1,0:T(8,128)(2,1)S(1)}, bf16[2,2,48,256]{3,2,1,0:T(8,128)(2,1)S(1)}, u32[]{:S(2)}, u32[]{:S(2)}) collective-permute-start(bf16[2,2,48,256]{3,2,1,0:T(8,128)(2,1)S(1)} %collective-permute-done.7.refs_6_), channel_id=1, source_target_pairs={{0,1},{1,0},{2,3},{3,2},{4,5},{5,4},{6,7},{7,6},{8,9},{9,8},{10,11... | collective-permute-start | bytes 294920 | tf_op jit(solution)/shard_map/ppermute | solution.py:580
  36.3 2.9 %collective-permute-start.12 = (bf16[9,128,256]{2,1,0:T(8,128)(2,1)S(1)}, bf16[9,128,256]{2,1,0:T(8,128)(2,1)S(1)}, u32[]{:S(2)}, u32[]{:S(2)}) collective-permute-start(bf16[9,128,256]{2,1,0:T(8,128)(2,1)S(1)} %get-tuple-element.118), channel_id=1, source_target_pairs={{0,1},{1,0},{2,3},{3,2},{4,5},{5,4},{6,7},{7,6},{8,9},{9,8},{10,11... | collective-permute-start | bytes 1769480 | tf_op jit(solution)/shard_map/ppermute | solution.py:580
  36.7 3.3 %collective-permute-start.36 = (bf16[9,128,256]{2,1,0:T(8,128)(2,1)S(1)}, bf16[9,128,256]{2,1,0:T(8,128)(2,1)S(1)}, u32[]{:S(2)}, u32[]{:S(2)}) collective-permute-start(bf16[9,128,256]{2,1,0:T(8,128)(2,1)S(1)} %get-tuple-element.178), channel_id=1, source_target_pairs={{0,1},{1,0},{2,3},{3,2},{4,5},{5,4},{6,7},{7,6},{8,9},{9,8},{10,11... | collective-permute-start | bytes 1769480 | tf_op jit(solution)/shard_map/ppermute | solution.py:580
  36.8 2.3 %collective-permute-start.13 = (bf16[8,256]{1,0:T(8,128)(2,1)S(1)}, bf16[8,256]{1,0:T(8,128)(2,1)S(1)}, u32[]{:S(2)}, u32[]{:S(2)}) collective-permute-start(bf16[8,256]{1,0:T(8,128)(2,1)S(1)} %get-tuple-element.120), channel_id=1, source_target_pairs={{0,1},{1,0},{2,3},{3,2},{4,5},{5,4},{6,7},{7,6},{8,9},{9,8},{10,11... | collective-permute-start | bytes 12296 | tf_op jit(solution)/shard_map/ppermute | solution.py:580
  39.3 14.2 %collective-permute-start.14 = (bf16[584,256]{1,0:T(8,128)(2,1)S(1)}, bf16[584,256]{1,0:T(8,128)(2,1)S(1)}, u32[]{:S(2)}, u32[]{:S(2)}) collective-permute-start(bf16[584,256]{1,0:T(8,128)(2,1)S(1)} %get-tuple-element.122), channel_id=1, source_target_pairs={{0,2},{2,0},{4,6},{6,4},{8,10},{10,8},{12,14},{14,12},{1,3},{3,1},... | collective-permute-start | bytes 897032 | tf_op jit(solution)/shard_map/ppermute | solution.py:659
  39.4 4.1 %collective-permute-start.15 = (bf16[2,192,256]{2,1,0:T(8,128)(2,1)S(1)}, bf16[2,192,256]{2,1,0:T(8,128)(2,1)S(1)}, u32[]{:S(2)}, u32[]{:S(2)}) collective-permute-start(bf16[2,192,256]{2,1,0:T(8,128)(2,1)S(1)} %get-tuple-element.127), channel_id=1, source_target_pairs={{0,1},{1,0},{2,3},{3,2},{4,5},{5,4},{6,7},{7,6},{8,9},{9,8},{10,11... | collective-permute-start | bytes 589832 | tf_op jit(solution)/shard_map/ppermute | solution.py:580
  39.8 2.3 %collective-permute-start.16 = (bf16[2,48,256]{2,1,0:T(8,128)(2,1)S(1)}, bf16[2,48,256]{2,1,0:T(8,128)(2,1)S(1)}, u32[]{:S(2)}, u32[]{:S(2)}) collective-permute-start(bf16[2,48,256]{2,1,0:T(8,128)(2,1)S(1)} %get-tuple-element.128), channel_id=1, source_target_pairs={{0,1},{1,0},{2,3},{3,2},{4,5},{5,4},{6,7},{7,6},{8,9},{9,8},{10,11... | collective-permute-start | bytes 147464 | tf_op jit(solution)/shard_map/ppermute | solution.py:580
  40.1 16.1 %collective-permute-start.37 = (bf16[576,256]{1,0:T(8,128)(2,1)S(1)}, bf16[576,256]{1,0:T(8,128)(2,1)S(1)}, u32[]{:S(2)}, u32[]{:S(2)}) collective-permute-start(bf16[576,256]{1,0:T(8,128)(2,1)S(1)} %get-tuple-element.180), channel_id=1, source_target_pairs={{0,2},{2,0},{4,6},{6,4},{8,10},{10,8},{12,14},{14,12},{1,3},{3,1},... | collective-permute-start | bytes 884744 | tf_op jit(solution)/shard_map/ppermute | solution.py:659
  42.1 1.2 %collective-permute-start.17 = (bf16[2,48,256]{2,1,0:T(8,128)(2,1)S(1)}, bf16[2,48,256]{2,1,0:T(8,128)(2,1)S(1)}, u32[]{:S(2)}, u32[]{:S(2)}) collective-permute-start(bf16[2,48,256]{2,1,0:T(8,128)(2,1)S(1)} %get-tuple-element.129), channel_id=1, source_target_pairs={{0,1},{1,0},{2,3},{3,2},{4,5},{5,4},{6,7},{7,6},{8,9},{9,8},{10,11... | collective-permute-start | bytes 147464 | tf_op jit(solution)/shard_map/ppermute | solution.py:580
  42.1 1.4 %collective-permute-start.18 = (bf16[2,48,256]{2,1,0:T(8,128)(2,1)S(1)}, bf16[2,48,256]{2,1,0:T(8,128)(2,1)S(1)}, u32[]{:S(2)}, u32[]{:S(2)}) collective-permute-start(bf16[2,48,256]{2,1,0:T(8,128)(2,1)S(1)} %get-tuple-element.130), channel_id=1, source_target_pairs={{0,1},{1,0},{2,3},{3,2},{4,5},{5,4},{6,7},{7,6},{8,9},{9,8},{10,11... | collective-permute-start | bytes 147464 | tf_op jit(solution)/shard_map/ppermute | solution.py:580
  43.6 7.5 %collective-permute-start.19 = (bf16[2,2,48,256]{3,2,1,0:T(8,128)(2,1)S(1)}, bf16[2,2,48,256]{3,2,1,0:T(8,128)(2,1)S(1)}, u32[]{:S(2)}, u32[]{:S(2)}) collective-permute-start(bf16[2,2,48,256]{3,2,1,0:T(8,128)(2,1)S(1)} %get-tuple-element.131), channel_id=1, source_target_pairs={{0,4},{4,0},{10,14},{14,10},{1,9},{3,11},{5,13},{7,15},{9,1},{11,3... | collective-permute-start | bytes 294920 | tf_op jit(solution)/shard_map/ppermute | solution.py:610
  46.4 7.1 %collective-permute-start.20 = (bf16[2,2,48,256]{3,2,1,0:T(8,128)(2,1)S(1)}, bf16[2,2,48,256]{3,2,1,0:T(8,128)(2,1)S(1)}, u32[]{:S(2)}, u32[]{:S(2)}) collective-permute-start(bf16[2,2,48,256]{3,2,1,0:T(8,128)(2,1)S(1)} %get-tuple-element.132), channel_id=1, source_target_pairs={{0,12},{2,14},{4,8},{6,10},{8,4},{10,6},{12,0},{14,2},{1,7},{3,13}... | collective-permute-start | bytes 294920 | tf_op jit(solution)/shard_map/ppermute | solution.py:610
  53.6 31.5 %collective-permute-start.24 = (bf16[2,2,192,256]{3,2,1,0:T(8,128)(2,1)S(1)}, bf16[2,2,192,256]{3,2,1,0:T(8,128)(2,1)S(1)}, u32[]{:S(2)}, u32[]{:S(2)}) collective-permute-start(bf16[2,2,192,256]{3,2,1,0:T(8,128)(2,1)S(1)} %get-tuple-element.144), channel_id=1, source_target_pairs={{0,2},{2,0},{4,6},{6,4},{8,10},{10,8},{12,14},{14,12},{1,15},{3,5}... | collective-permute-start | bytes 1179656 | tf_op jit(solution)/shard_map/ppermute | solution.py:610
  56.2 42.0 %copy-start.1 = (bf16[3,3,256,256]{3,2,1,0:T(8,128)(2,1)S(1)}, bf16[3,3,256,256]{3,2,1,0:T(8,128)(2,1)}, u32[]{:S(2)}) copy-start(bf16[3,3,256,256]{3,2,1,0:T(8,128)(2,1)} %param.10) | copy-start | bytes 3538948
  56.3 5.3 %collective-permute-start.38 = (bf16[144,256]{1,0:T(8,128)(2,1)S(1)}, bf16[144,256]{1,0:T(8,128)(2,1)S(1)}, u32[]{:S(2)}, u32[]{:S(2)}) collective-permute-start(bf16[144,256]{1,0:T(8,128)(2,1)S(1)} %get-tuple-element.182), channel_id=1, source_target_pairs={{0,4},{2,6},{4,0},{6,2},{8,12},{10,14},{12,8},{14,10},{1,5},{3,7},... | collective-permute-start | bytes 221192 | tf_op jit(solution)/shard_map/ppermute | solution.py:662
  57.2 6.8 %collective-permute-start.39 = (bf16[144,256]{1,0:T(8,128)(2,1)S(1)}, bf16[144,256]{1,0:T(8,128)(2,1)S(1)}, u32[]{:S(2)}, u32[]{:S(2)}) collective-permute-start(bf16[144,256]{1,0:T(8,128)(2,1)S(1)} %get-tuple-element.183), channel_id=1, source_target_pairs={{0,8},{2,10},{4,12},{6,14},{8,0},{10,2},{12,4},{14,6},{1,9},{3,11}... | collective-permute-start | bytes 221192 | tf_op jit(solution)/shard_map/ppermute | solution.py:662
  60.1 7.0 %collective-permute-start.40 = (bf16[144,256]{1,0:T(8,128)(2,1)S(1)}, bf16[144,256]{1,0:T(8,128)(2,1)S(1)}, u32[]{:S(2)}, u32[]{:S(2)}) collective-permute-start(bf16[144,256]{1,0:T(8,128)(2,1)S(1)} %get-tuple-element.184), channel_id=1, source_target_pairs={{0,12},{2,14},{4,8},{6,10},{8,4},{10,6},{12,0},{14,2},{1,13},{3,15... | collective-permute-start | bytes 221192 | tf_op jit(solution)/shard_map/ppermute | solution.py:662
  67.2 7.0 %collective-permute-start.43 = (bf16[144,256]{1,0:T(8,128)(2,1)S(1)}, bf16[144,256]{1,0:T(8,128)(2,1)S(1)}, u32[]{:S(2)}, u32[]{:S(2)}) collective-permute-start(bf16[144,256]{1,0:T(8,128)(2,1)S(1)} %shard_map.113), channel_id=1, source_target_pairs={{0,12},{2,14},{4,8},{6,10},{8,4},{10,6},{12,0},{14,2},{1,13},{3,15... | collective-permute-start | bytes 221192 | tf_op jit(solution)/shard_map/ppermute | solution.py:662
  71.4 7.5 %collective-permute-start.42 = (bf16[144,256]{1,0:T(8,128)(2,1)S(1)}, bf16[144,256]{1,0:T(8,128)(2,1)S(1)}, u32[]{:S(2)}, u32[]{:S(2)}) collective-permute-start(bf16[144,256]{1,0:T(8,128)(2,1)S(1)} %shard_map.113), channel_id=1, source_target_pairs={{0,8},{2,10},{4,12},{6,14},{8,0},{10,2},{12,4},{14,6},{1,9},{3,11}... | collective-permute-start | bytes 221192 | tf_op jit(solution)/shard_map/ppermute | solution.py:662
  71.6 9.9 %collective-permute-start.41 = (bf16[144,256]{1,0:T(8,128)(2,1)S(1)}, bf16[144,256]{1,0:T(8,128)(2,1)S(1)}, u32[]{:S(2)}, u32[]{:S(2)}) collective-permute-start(bf16[144,256]{1,0:T(8,128)(2,1)S(1)} %shard_map.113), channel_id=1, source_target_pairs={{0,4},{2,6},{4,0},{6,2},{8,12},{10,14},{12,8},{14,10},{1,5},{3,7},... | collective-permute-start | bytes 221192 | tf_op jit(solution)/shard_map/ppermute | solution.py:662
  72.1 10.3 %collective-permute-start.21 = (bf16[152,256]{1,0:T(8,128)(2,1)S(1)}, bf16[152,256]{1,0:T(8,128)(2,1)S(1)}, u32[]{:S(2)}, u32[]{:S(2)}) collective-permute-start(bf16[152,256]{1,0:T(8,128)(2,1)S(1)} %get-tuple-element.141), channel_id=1, source_target_pairs={{0,4},{2,6},{4,0},{6,2},{8,12},{10,14},{12,8},{14,10},{1,5},{3,7},... | collective-permute-start | bytes 233480 | tf_op jit(solution)/shard_map/ppermute | solution.py:662
  74.1 9.1 %collective-permute-start.22 = (bf16[152,256]{1,0:T(8,128)(2,1)S(1)}, bf16[152,256]{1,0:T(8,128)(2,1)S(1)}, u32[]{:S(2)}, u32[]{:S(2)}) collective-permute-start(bf16[152,256]{1,0:T(8,128)(2,1)S(1)} %get-tuple-element.142), channel_id=1, source_target_pairs={{0,8},{2,10},{4,12},{6,14},{8,0},{10,2},{12,4},{14,6},{1,9},{3,11}... | collective-permute-start | bytes 233480 | tf_op jit(solution)/shard_map/ppermute | solution.py:662
  78.9 6.2 %collective-permute-start.23 = (bf16[152,256]{1,0:T(8,128)(2,1)S(1)}, bf16[152,256]{1,0:T(8,128)(2,1)S(1)}, u32[]{:S(2)}, u32[]{:S(2)}) collective-permute-start(bf16[152,256]{1,0:T(8,128)(2,1)S(1)} %get-tuple-element.143), channel_id=1, source_target_pairs={{0,12},{2,14},{4,8},{6,10},{8,4},{10,6},{12,0},{14,2},{1,13},{3,15... | collective-permute-start | bytes 233480 | tf_op jit(solution)/shard_map/ppermute | solution.py:662
  81.5 3.6 %collective-permute-start.25 = (bf16[2,2,48,256]{3,2,1,0:T(8,128)(2,1)S(1)}, bf16[2,2,48,256]{3,2,1,0:T(8,128)(2,1)S(1)}, u32[]{:S(2)}, u32[]{:S(2)}) collective-permute-start(bf16[2,2,48,256]{3,2,1,0:T(8,128)(2,1)S(1)} %get-tuple-element.145), channel_id=1, source_target_pairs={{1,11},{5,15},{11,1},{15,5},{17,27},{21,31},{27,17},{31,21}} | collective-permute-start | bytes 294920 | tf_op jit(solution)/shard_map/ppermute | solution.py:610
  82.4 15.1 %collective-permute-start.44 = (bf16[576,256]{1,0:T(8,128)(2,1)S(1)}, bf16[576,256]{1,0:T(8,128)(2,1)S(1)}, u32[]{:S(2)}, u32[]{:S(2)}) collective-permute-start(bf16[576,256]{1,0:T(8,128)(2,1)S(1)} %pad_maximum_fusion.refs_0_), channel_id=1, source_target_pairs={{0,2},{2,0},{4,6},{6,4},{8,10},{10,8},{12,14},{14,12},{1,3},{3,1},... | collective-permute-start | bytes 884744 | tf_op jit(solution)/shard_map/ppermute | solution.py:659
  85.1 10.3 %collective-permute-start.28 = (bf16[144,256]{1,0:T(8,128)(2,1)S(1)}, bf16[144,256]{1,0:T(8,128)(2,1)S(1)}, u32[]{:S(2)}, u32[]{:S(2)}) collective-permute-start(bf16[144,256]{1,0:T(8,128)(2,1)S(1)} %get-tuple-element.150), channel_id=1, source_target_pairs={{0,12},{2,14},{4,8},{6,10},{8,4},{10,6},{12,0},{14,2},{1,13},{3,15... | collective-permute-start | bytes 221192 | tf_op jit(solution)/shard_map/ppermute | solution.py:662
  88.7 6.7 %collective-permute-start.27 = (bf16[144,256]{1,0:T(8,128)(2,1)S(1)}, bf16[144,256]{1,0:T(8,128)(2,1)S(1)}, u32[]{:S(2)}, u32[]{:S(2)}) collective-permute-start(bf16[144,256]{1,0:T(8,128)(2,1)S(1)} %get-tuple-element.150), channel_id=1, source_target_pairs={{0,8},{2,10},{4,12},{6,14},{8,0},{10,2},{12,4},{14,6},{1,9},{3,11}... | collective-permute-start | bytes 221192 | tf_op jit(solution)/shard_map/ppermute | solution.py:662
  88.7 5.7 %collective-permute-start.26 = (bf16[144,256]{1,0:T(8,128)(2,1)S(1)}, bf16[144,256]{1,0:T(8,128)(2,1)S(1)}, u32[]{:S(2)}, u32[]{:S(2)}) collective-permute-start(bf16[144,256]{1,0:T(8,128)(2,1)S(1)} %get-tuple-element.150), channel_id=1, source_target_pairs={{0,4},{2,6},{4,0},{6,2},{8,12},{10,14},{12,8},{14,10},{1,5},{3,7},... | collective-permute-start | bytes 221192 | tf_op jit(solution)/shard_map/ppermute | solution.py:662
  89.6 8.6 %collective-permute-start.30 = (bf16[2,2,192,256]{3,2,1,0:T(8,128)(2,1)S(1)}, bf16[2,2,192,256]{3,2,1,0:T(8,128)(2,1)S(1)}, u32[]{:S(2)}, u32[]{:S(2)}) collective-permute-start(bf16[2,2,192,256]{3,2,1,0:T(8,128)(2,1)S(1)} %collective-permute-done.24.refs_0_), channel_id=1, source_target_pairs={{0,1},{1,0},{2,3},{3,2},{4,5},{5,4},{6,7},{7,6},{8,9},{9,8},{10,11... | collective-permute-start | bytes 1179656 | tf_op jit(solution)/shard_map/ppermute | solution.py:580
  95.4 8.4 %collective-permute-start.29 = (bf16[576,256]{1,0:T(8,128)(2,1)S(1)}, bf16[576,256]{1,0:T(8,128)(2,1)S(1)}, u32[]{:S(2)}, u32[]{:S(2)}) collective-permute-start(bf16[576,256]{1,0:T(8,128)(2,1)S(1)} %constant_dynamic-update-slice_fusion.refs_0_), channel_id=1, source_target_pairs={{0,2},{2,0},{4,6},{6,4},{8,10},{10,8},{12,14},{14,12},{1,3},{3,1},... | collective-permute-start | bytes 884744 | tf_op jit(solution)/shard_map/ppermute | solution.py:659
  95.5 1.4 %collective-permute-start.31 = (bf16[2,2,48,256]{3,2,1,0:T(8,128)(2,1)S(1)}, bf16[2,2,48,256]{3,2,1,0:T(8,128)(2,1)S(1)}, u32[]{:S(2)}, u32[]{:S(2)}) collective-permute-start(bf16[2,2,48,256]{3,2,1,0:T(8,128)(2,1)S(1)} %collective-permute-done.19.refs_2_), channel_id=1, source_target_pairs={{0,1},{1,0},{2,3},{3,2},{4,5},{5,4},{6,7},{7,6},{8,9},{9,8},{10,11... | collective-permute-start | bytes 294920 | tf_op jit(solution)/shard_map/ppermute | solution.py:580
  95.6 1.4 %collective-permute-start.32 = (bf16[2,2,48,256]{3,2,1,0:T(8,128)(2,1)S(1)}, bf16[2,2,48,256]{3,2,1,0:T(8,128)(2,1)S(1)}, u32[]{:S(2)}, u32[]{:S(2)}) collective-permute-start(bf16[2,2,48,256]{3,2,1,0:T(8,128)(2,1)S(1)} %collective-permute-done.20.refs_4_), channel_id=1, source_target_pairs={{0,1},{1,0},{2,3},{3,2},{4,5},{5,4},{6,7},{7,6},{8,9},{9,8},{10,11... | collective-permute-start | bytes 294920 | tf_op jit(solution)/shard_map/ppermute | solution.py:580
  96.9 1.3 %collective-permute-start.33 = (bf16[2,2,48,256]{3,2,1,0:T(8,128)(2,1)S(1)}, bf16[2,2,48,256]{3,2,1,0:T(8,128)(2,1)S(1)}, u32[]{:S(2)}, u32[]{:S(2)}) collective-permute-start(bf16[2,2,48,256]{3,2,1,0:T(8,128)(2,1)S(1)} %collective-permute-done.25.refs_6_), channel_id=1, source_target_pairs={{0,1},{1,0},{2,3},{3,2},{4,5},{5,4},{6,7},{7,6},{8,9},{9,8},{10,11... | collective-permute-start | bytes 294920 | tf_op jit(solution)/shard_map/ppermute | solution.py:580
  97.0 7.3 %collective-permute-start.45 = (bf16[576,256]{1,0:T(8,128)(2,1)S(1)}, bf16[576,256]{1,0:T(8,128)(2,1)S(1)}, u32[]{:S(2)}, u32[]{:S(2)}) collective-permute-start(bf16[576,256]{1,0:T(8,128)(2,1)S(1)} %pad_maximum_fusion.refs_0_), channel_id=1, source_target_pairs={{0,1},{1,0},{2,3},{3,2},{4,5},{5,4},{6,7},{7,6},{8,9},{9,8},{10,11... | collective-permute-start | bytes 884744 | tf_op jit(solution)/shard_map/ppermute | solution.py:580
  97.4 7.0 %collective-permute-start.46 = (bf16[576,256]{1,0:T(8,128)(2,1)S(1)}, bf16[576,256]{1,0:T(8,128)(2,1)S(1)}, u32[]{:S(2)}, u32[]{:S(2)}) collective-permute-start(bf16[576,256]{1,0:T(8,128)(2,1)S(1)} %collective-permute-done.44.refs_1_), channel_id=1, source_target_pairs={{0,1},{1,0},{2,3},{3,2},{4,5},{5,4},{6,7},{7,6},{8,9},{9,8},{10,11... | collective-permute-start | bytes 884744 | tf_op jit(solution)/shard_map/ppermute | solution.py:580
  103.9 2.3 %collective-permute-start.35 = (bf16[576,256]{1,0:T(8,128)(2,1)S(1)}, bf16[576,256]{1,0:T(8,128)(2,1)S(1)}, u32[]{:S(2)}, u32[]{:S(2)}) collective-permute-start(bf16[576,256]{1,0:T(8,128)(2,1)S(1)} %collective-permute-done.29.refs_1_), channel_id=1, source_target_pairs={{0,1},{1,0},{2,3},{3,2},{4,5},{5,4},{6,7},{7,6},{8,9},{9,8},{10,11... | collective-permute-start | bytes 884744 | tf_op jit(solution)/shard_map/ppermute | solution.py:580
  104.0 2.2 %collective-permute-start.34 = (bf16[576,256]{1,0:T(8,128)(2,1)S(1)}, bf16[576,256]{1,0:T(8,128)(2,1)S(1)}, u32[]{:S(2)}, u32[]{:S(2)}) collective-permute-start(bf16[576,256]{1,0:T(8,128)(2,1)S(1)} %constant_dynamic-update-slice_fusion.refs_0_), channel_id=1, source_target_pairs={{0,1},{1,0},{2,3},{3,2},{4,5},{5,4},{6,7},{7,6},{8,9},{9,8},{10,11... | collective-permute-start | bytes 884744 | tf_op jit(solution)/shard_map/ppermute | solution.py:580

commit v11 on v10

--- a/solution.py
+++ b/solution.py
@@ -683,7 +683,7 @@
         )(keep, *recvs, *bias)
 
     joined = merged(packed)
-    early = list(steps)[1 : 1 + len(steps) // 2]
+    early = list(steps)[1:]
     middle = [i for i in steps if i not in early]
     came = {}
 
@@ -703,9 +703,9 @@
     recvs1 = [along_z(v, j + 1) for j, v in enumerate(sends1)]
     got = [across(v, i) for i, v in zip(middle, todo)]
 
+    recvs2, recvs1 = barrier((recvs2, recvs1))
     (own2,) = sum_z(keep2, recvs2)
     own2 = [own2] + [along_z(own2, j) for j in range(1, zcount)]
-    recvs1, got = barrier((recvs1, got))
     came.update(zip(middle, got))
 
     own1, bias_sum = sum_z(keep1, recvs1, bias_sum)

time: 108 us -> 109 us (level)
  starting transfers between devices: 51.7 us -> 54.7 us
  waiting for transfers between devices: 29.2 us -> 26.8 us
    ppermute x4, starting transfers between devices: 2.23 us -> 7.83 us  [along_y(): return lax.ppermute(v, 'tile', [(i, i ^ 1) for i in range(tiles)])]
    ppermute x12, waiting for transfers between devices: 13.9 us -> 10.2 us  [along_z(): return lax.ppermute(v, 'tile', [(i, i ^ 2 * j) for i in range(tiles)])]
    ppermute x23, starting transfers between devices: 11.4 us -> 9.61 us  [swap_dp(): return lax.ppermute(v, 'dp', [(i, count - 1 - i) for i in range(count)])]
    ppermute x23, waiting for transfers between devices: 6.79 us -> 8.17 us  [swap_dp(): return lax.ppermute(v, 'dp', [(i, count - 1 - i) for i in range(count)])]
  transfers between devices with their start and end apart: 47 -> 47, of which waited for: 22 -> 19; matrix products, arithmetic and copies ran while one was open for 0% -> 0% of each run, Pallas kernels for 8% -> 8%
where the time goes in v11:
time: 109 us
  starting transfers between devices  54.7 us (50%)
  waiting for transfers between devices  26.8 us (25%)
  Pallas kernels  20.9 us (19%)
  local copies, waits for them, and re-layouts  5.22 us (5%)
    ppermute x12, starting transfers between devices, along_z(): return lax.ppermute(v, 'tile', [(i, i ^ 2 * j) for i in range(tiles)])  22 us
    pallas_call x14, Pallas kernels, run(): pl.pallas_call(kernel, out_shape=[jax.ShapeDtypeStruct(s, dt) for s, dt i...  20.9 us
    ppermute x8, starting transfers between devices, across(): return lax.ppermute(v, ('tile', 'dp'), pairs[step])  15.2 us
    ppermute x12, waiting for transfers between devices, along_z(): return lax.ppermute(v, 'tile', [(i, i ^ 2 * j) for i in range(tiles)])  10.2 us
    ppermute x23, starting transfers between devices, swap_dp(): return lax.ppermute(v, 'dp', [(i, count - 1 - i) for i in range(count)])  9.61 us
    ppermute x23, waiting for transfers between devices, swap_dp(): return lax.ppermute(v, 'dp', [(i, count - 1 - i) for i in range(count)])  8.17 us
    ppermute x8, waiting for transfers between devices, across(): return lax.ppermute(v, ('tile', 'dp'), pairs[step])  8.08 us
    ppermute x4, starting transfers between devices, along_y(): return lax.ppermute(v, 'tile', [(i, i ^ 1) for i in range(tiles)])  7.83 us
  transfers between devices with their start and end apart: 47, of which 19 were waited for; matrix products, arithmetic and copies ran while one was open for 0% of the time, Pallas kernels for 8%

profile of v11, /device:TPU:0, one launch (start us, length us, event | category | flops | bytes accessed | tf_op | source)
XLA Modules:
  0.0 108.5 jit_solution(4008319656682168223)
XLA Ops:
  0.6 0.8 copy.12.ep
  1.4 0.9 copy-done.2
  2.3 0.9 copy-done.4
  3.3 2.2 %shard_map.101 = (bf16[2,192,256]{2,1,0:T(8,128)(2,1)S(1)}, bf16[2,48,256]{2,1,0:T(8,128)(2,1)S(1)}, bf16[2,48,256]{2,1,0:T(8,128)(2,1)S(1)}, bf16[2,48,256]{2,1...) custom-call(s32[6,4]{1,0:T(8,128)S(1)} %copy.12.ep, ...), custom_call_target="tpu_custom_call" | custom-call | tf_op jit(solution)/shard_map/pallas_call | solution.py:566
  5.4 0.5 collective-permute-start
  6.0 0.4 collective-permute-start.2
  6.5 0.6 collective-permute-done.1.refs_5_
  7.3 0.3 collective-permute-done.3.refs_7_
  7.7 2.7 %collective-permute-start.4 = (bf16[2,2,192,256]{3,2,1,0:T(8,128)(2,1)S(1)}, bf16[2,2,192,256]{3,2,1,0:T(8,128)(2,1)S(1)}, u32[]{:S(2)}, u32[]{:S(2)}) collective-permute-start(bf16[2,2,192,256]{3,2,1,0:T(8,128)(2,1)S(1)} %get-tuple-element.104), channel_id=1, source_target_pairs={{0,2},{2,0},{4,6},{6,4},{8,10},{10,8},{12,14},{14,12},{1,15},{3,5}... | collective-permute-start | bytes 1179656 | tf_op jit(solution)/shard_map/ppermute | solution.py:610
  10.5 3.5 %collective-permute-start.5 = (bf16[2,2,48,256]{3,2,1,0:T(8,128)(2,1)S(1)}, bf16[2,2,48,256]{3,2,1,0:T(8,128)(2,1)S(1)}, u32[]{:S(2)}, u32[]{:S(2)}) collective-permute-start(bf16[2,2,48,256]{3,2,1,0:T(8,128)(2,1)S(1)} %get-tuple-element.105), channel_id=1, source_target_pairs={{0,4},{4,0},{10,14},{14,10},{1,9},{3,11},{5,13},{7,15},{9,1},{11,3... | collective-permute-start | bytes 294920 | tf_op jit(solution)/shard_map/ppermute | solution.py:610
  14.0 0.9 collective-permute-start.6
  14.8 0.7 collective-permute-start.7
  15.5 1.3 %copy-done = bf16[3,3,256,256]{3,2,1,0:T(8,128)(2,1)S(1)} copy-done((bf16[3,3,256,256]{3,2,1,0:T(8,128)(2,1)S(1)}, bf16[3,3,256,256]{3,2,1,0:T(8,128)(2,1)}, u32[]{:S(2)}) %copy-start) | copy-done | bytes 1179672
  16.8 1.3 %copy-done.6 = bf16[3,3,256,256]{3,2,1,0:T(8,128)(2,1)S(1)} copy-done((bf16[3,3,256,256]{3,2,1,0:T(8,128)(2,1)S(1)}, bf16[3,3,256,256]{3,2,1,0:T(8,128)(2,1)}, u32[]{:S(2)}) %copy-start.6) | copy-done | bytes 1179672
  18.0 0.7 shard_map.103
  18.7 2.9 %collective-permute-done.6.refs_4_ = bf16[2,2,48,256]{3,2,1,0:T(8,128)(2,1)S(1)} collective-permute-done((bf16[2,2,48,256]{3,2,1,0:T(8,128)(2,1)S(1)}, bf16[2,2,48,256]{3,2,1,0:T(8,128)(2,1)S(1)}, u32[]{:S(2)}, u32[]{:S(2)}) %collective-permute-start.6) | collective-permute-done | bytes 98336 | tf_op jit(solution)/shard_map/ppermute | solution.py:610
  21.7 4.5 %collective-permute-start.8 = (bf16[2,2,192,256]{3,2,1,0:T(8,128)(2,1)S(1)}, bf16[2,2,192,256]{3,2,1,0:T(8,128)(2,1)S(1)}, u32[]{:S(2)}, u32[]{:S(2)}) collective-permute-start(bf16[2,2,192,256]{3,2,1,0:T(8,128)(2,1)S(1)} %collective-permute-done.4.refs_0_), channel_id=1, source_target_pairs={{0,1},{1,0},{2,3},{3,2},{4,5},{5,4},{6,7},{7,6},{8,9},{9,8},{10,11... | collective-permute-start | bytes 1179656 | tf_op jit(solution)/shard_map/ppermute | solution.py:580
  26.2 0.5 collective-permute-start.10
  26.7 1.0 collective-permute-done.9.refs_3_
  27.8 0.2 collective-permute-done.11.refs_7_
  28.0 8.3 %shard_map.104 = (bf16[9,128,256]{2,1,0:T(8,128)(2,1)S(1)}, f32[9,128,256]{2,1,0:T(8,128)S(1)}, bf16[9,128,256]{2,1,0:T(8,128)(2,1)S(1)}, f32[9,128,256]{2,1,0:T...) custom-call(s32[6,4]{1,0:T(8,128)S(1)} %copy.12.ep, ...), custom_call_target="tpu_custom_call" | custom-call | tf_op jit(solution)/shard_map/pallas_call | solution.py:566
  36.3 0.4 collective-permute-start.22
  36.8 1.5 %collective-permute-done.22.recv_ref = bf16[9,128,256]{2,1,0:T(8,128)(2,1)S(1)} collective-permute-done((bf16[9,128,256]{2,1,0:T(8,128)(2,1)S(1)}, bf16[9,128,256]{2,1,0:T(8,128)(2,1)S(1)}, u32[]{:S(2)}, u32[]{:S(2)}) %collective-permute-start.22) | collective-permute-done | bytes 589856 | tf_op jit(solution)/shard_map/ppermute | solution.py:580
  38.6 0.4 collective-permute-start.13
  38.9 0.8 collective-permute-done.13.refs_1_
  39.9 2.0 %collective-permute-start.14 = (bf16[584,256]{1,0:T(8,128)(2,1)S(1)}, bf16[584,256]{1,0:T(8,128)(2,1)S(1)}, u32[]{:S(2)}, u32[]{:S(2)}) collective-permute-start(bf16[584,256]{1,0:T(8,128)(2,1)S(1)} %get-tuple-element.123), channel_id=1, source_target_pairs={{0,2},{2,0},{4,6},{6,4},{8,10},{10,8},{12,14},{14,12},{1,3},{3,1},... | collective-permute-start | bytes 897032 | tf_op jit(solution)/shard_map/ppermute | solution.py:659
  41.9 0.5 collective-permute-start.16
  42.4 1.0 collective-permute-done.16.refs_5_
  43.4 0.2 collective-permute-start.18
  43.7 1.0 collective-permute-done.18.refs_7_
  44.7 2.8 %collective-permute-start.19 = (bf16[2,2,48,256]{3,2,1,0:T(8,128)(2,1)S(1)}, bf16[2,2,48,256]{3,2,1,0:T(8,128)(2,1)S(1)}, u32[]{:S(2)}, u32[]{:S(2)}) collective-permute-start(bf16[2,2,48,256]{3,2,1,0:T(8,128)(2,1)S(1)} %get-tuple-element.132), channel_id=1, source_target_pairs={{0,4},{4,0},{10,14},{14,10},{1,9},{3,11},{5,13},{7,15},{9,1},{11,3... | collective-permute-start | bytes 294920 | tf_op jit(solution)/shard_map/ppermute | solution.py:610
  47.5 1.0 collective-permute-start.20
  48.5 0.8 collective-permute-start.21
  49.5 0.3 collective-permute-start.24
  49.8 2.0 %collective-permute-done.19.refs_2_ = bf16[2,2,48,256]{3,2,1,0:T(8,128)(2,1)S(1)} collective-permute-done((bf16[2,2,48,256]{3,2,1,0:T(8,128)(2,1)S(1)}, bf16[2,2,48,256]{3,2,1,0:T(8,128)(2,1)S(1)}, u32[]{:S(2)}, u32[]{:S(2)}) %collective-permute-start.19) | collective-permute-done | bytes 98336 | tf_op jit(solution)/shard_map/ppermute | solution.py:610
  51.7 3.1 %collective-permute-done.20.refs_4_ = bf16[2,2,48,256]{3,2,1,0:T(8,128)(2,1)S(1)} collective-permute-done((bf16[2,2,48,256]{3,2,1,0:T(8,128)(2,1)S(1)}, bf16[2,2,48,256]{3,2,1,0:T(8,128)(2,1)S(1)}, u32[]{:S(2)}, u32[]{:S(2)}) %collective-permute-start.20) | collective-permute-done | bytes 98336 | tf_op jit(solution)/shard_map/ppermute | solution.py:610
  54.9 0.3 collective-permute-done.14.recv_ref
  55.4 1.0 collective-permute-start.27
  56.3 3.2 %collective-permute-start.28 = (bf16[152,256]{1,0:T(8,128)(2,1)S(1)}, bf16[152,256]{1,0:T(8,128)(2,1)S(1)}, u32[]{:S(2)}, u32[]{:S(2)}) collective-permute-start(bf16[152,256]{1,0:T(8,128)(2,1)S(1)} %get-tuple-element.150), channel_id=1, source_target_pairs={{0,8},{2,10},{4,12},{6,14},{8,0},{10,2},{12,4},{14,6},{1,9},{3,11}... | collective-permute-start | bytes 233480 | tf_op jit(solution)/shard_map/ppermute | solution.py:662
  59.6 0.2 collective-permute-start.29
  59.8 1.3 %collective-permute-start.25 = (bf16[144,256]{1,0:T(8,128)(2,1)S(1)}, bf16[144,256]{1,0:T(8,128)(2,1)S(1)}, u32[]{:S(2)}, u32[]{:S(2)}) collective-permute-start(bf16[144,256]{1,0:T(8,128)(2,1)S(1)} %get-tuple-element.143), channel_id=1, source_target_pairs={{0,8},{2,10},{4,12},{6,14},{8,0},{10,2},{12,4},{14,6},{1,9},{3,11}... | collective-permute-start | bytes 221192 | tf_op jit(solution)/shard_map/ppermute | solution.py:662
  61.1 2.3 %collective-permute-start.26 = (bf16[144,256]{1,0:T(8,128)(2,1)S(1)}, bf16[144,256]{1,0:T(8,128)(2,1)S(1)}, u32[]{:S(2)}, u32[]{:S(2)}) collective-permute-start(bf16[144,256]{1,0:T(8,128)(2,1)S(1)} %get-tuple-element.144), channel_id=1, source_target_pairs={{0,12},{2,14},{4,8},{6,10},{8,4},{10,6},{12,0},{14,2},{1,13},{3,15... | collective-permute-start | bytes 221192 | tf_op jit(solution)/shard_map/ppermute | solution.py:662
  63.4 8.5 %collective-permute-done.25.refs_1_ = bf16[144,256]{1,0:T(8,128)(2,1)S(1)} collective-permute-done((bf16[144,256]{1,0:T(8,128)(2,1)S(1)}, bf16[144,256]{1,0:T(8,128)(2,1)S(1)}, u32[]{:S(2)}, u32[]{:S(2)}) %collective-permute-start.25) | collective-permute-done | bytes 73760 | tf_op jit(solution)/shard_map/ppermute | solution.py:662
  71.9 2.9 %collective-permute-start.34 = (bf16[2,2,192,256]{3,2,1,0:T(8,128)(2,1)S(1)}, bf16[2,2,192,256]{3,2,1,0:T(8,128)(2,1)S(1)}, u32[]{:S(2)}, u32[]{:S(2)}) collective-permute-start(bf16[2,2,192,256]{3,2,1,0:T(8,128)(2,1)S(1)} %get-tuple-element.160), channel_id=1, source_target_pairs={{0,2},{2,0},{4,6},{6,4},{8,10},{10,8},{12,14},{14,12},{1,15},{3,5}... | collective-permute-start | bytes 1179656 | tf_op jit(solution)/shard_map/ppermute | solution.py:610
  74.8 2.4 %collective-permute-start.43 = (bf16[144,256]{1,0:T(8,128)(2,1)S(1)}, bf16[144,256]{1,0:T(8,128)(2,1)S(1)}, u32[]{:S(2)}, u32[]{:S(2)}) collective-permute-start(bf16[144,256]{1,0:T(8,128)(2,1)S(1)} %shard_map.113), channel_id=1, source_target_pairs={{0,12},{2,14},{4,8},{6,10},{8,4},{10,6},{12,0},{14,2},{1,13},{3,15... | collective-permute-start | bytes 221192 | tf_op jit(solution)/shard_map/ppermute | solution.py:662
  77.3 2.0 %collective-permute-start.41 = (bf16[144,256]{1,0:T(8,128)(2,1)S(1)}, bf16[144,256]{1,0:T(8,128)(2,1)S(1)}, u32[]{:S(2)}, u32[]{:S(2)}) collective-permute-start(bf16[144,256]{1,0:T(8,128)(2,1)S(1)} %shard_map.113), channel_id=1, source_target_pairs={{0,4},{2,6},{4,0},{6,2},{8,12},{10,14},{12,8},{14,10},{1,5},{3,7},... | collective-permute-start | bytes 221192 | tf_op jit(solution)/shard_map/ppermute | solution.py:662
  79.3 2.4 %collective-permute-start.32 = (bf16[144,256]{1,0:T(8,128)(2,1)S(1)}, bf16[144,256]{1,0:T(8,128)(2,1)S(1)}, u32[]{:S(2)}, u32[]{:S(2)}) collective-permute-start(bf16[144,256]{1,0:T(8,128)(2,1)S(1)} %get-tuple-element.156), channel_id=1, source_target_pairs={{0,12},{2,14},{4,8},{6,10},{8,4},{10,6},{12,0},{14,2},{1,13},{3,15... | collective-permute-start | bytes 221192 | tf_op jit(solution)/shard_map/ppermute | solution.py:662
  81.8 0.3 collective-permute-done.43
  82.0 6.8 %collective-permute-start.31 = (bf16[144,256]{1,0:T(8,128)(2,1)S(1)}, bf16[144,256]{1,0:T(8,128)(2,1)S(1)}, u32[]{:S(2)}, u32[]{:S(2)}) collective-permute-start(bf16[144,256]{1,0:T(8,128)(2,1)S(1)} %get-tuple-element.156), channel_id=1, source_target_pairs={{0,8},{2,10},{4,12},{6,14},{8,0},{10,2},{12,4},{14,6},{1,9},{3,11}... | collective-permute-start | bytes 221192 | tf_op jit(solution)/shard_map/ppermute | solution.py:662
  88.9 2.9 %collective-permute-start.44 = (bf16[576,256]{1,0:T(8,128)(2,1)S(1)}, bf16[576,256]{1,0:T(8,128)(2,1)S(1)}, u32[]{:S(2)}, u32[]{:S(2)}) collective-permute-start(bf16[576,256]{1,0:T(8,128)(2,1)S(1)} %pad_maximum_fusion.refs_0_), channel_id=1, source_target_pairs={{0,2},{2,0},{4,6},{6,4},{8,10},{10,8},{12,14},{14,12},{1,3},{3,1},... | collective-permute-start | bytes 884744 | tf_op jit(solution)/shard_map/ppermute | solution.py:659
  91.8 1.4 %collective-permute-done.30 = bf16[144,256]{1,0:T(8,128)(2,1)S(1)} collective-permute-done((bf16[144,256]{1,0:T(8,128)(2,1)S(1)}, bf16[144,256]{1,0:T(8,128)(2,1)S(1)}, u32[]{:S(2)}, u32[]{:S(2)}) %collective-permute-start.30) | collective-permute-done | bytes 73760 | tf_op jit(solution)/shard_map/ppermute | solution.py:662
  93.3 2.9 %collective-permute-start.33 = (bf16[576,256]{1,0:T(8,128)(2,1)S(1)}, bf16[576,256]{1,0:T(8,128)(2,1)S(1)}, u32[]{:S(2)}, u32[]{:S(2)}) collective-permute-start(bf16[576,256]{1,0:T(8,128)(2,1)S(1)} %constant_dynamic-update-slice_fusion.refs_0_), channel_id=1, source_target_pairs={{0,2},{2,0},{4,6},{6,4},{8,10},{10,8},{12,14},{14,12},{1,3},{3,1},... | collective-permute-start | bytes 884744 | tf_op jit(solution)/shard_map/ppermute | solution.py:659
  96.2 0.2 collective-permute-start.36
  96.4 0.3 collective-permute-start.37
  96.7 0.8 collective-permute-done.36.refs_3_
  97.5 0.2 collective-permute-start.38
  97.7 0.3 collective-permute-start.45
  98.0 0.2 collective-permute-start.46
  98.2 0.6 collective-permute-done.38.refs_7_
  98.8 0.2 collective-permute-start.39
  99.0 5.6 %shard_map.111 = (bf16[18,24,256]{2,1,0:T(8,128)(2,1)}, f32[18,24,256]{2,1,0:T(8,128)}) custom-call(s32[6,4]{1,0:T(8,128)S(1)} %copy.12.ep, bf16[18,24,256]{2,1,0:T(8,128)(2,1)S(1)} %bitcast.20, bf16[18,24,256]{2,1,0:T(8,128)(2,1)S(1)} %bitcast.23, bf16[18,24,256]{2,1,0:T(8,128)(2,1)S(1)} %get-tuple-element.157.hid_ref, ...), custom_call_target="tpu_custom_call" | custom-call | tf_op jit(solution)/shard_map/pallas_call | solution.py:566
  104.7 0.3 collective-permute-start.40
  105.0 1.8 %shard_map.114 = f32[9,256,256]{2,1,0:T(8,128)} custom-call(bf16[576,256]{1,0:T(8,128)(2,1)S(1)} %pad_maximum_fusion.refs_0_, bf16[576,256]{1,0:T(8,128)(2,1)S(1)} %collective-permute-done.44.refs_1_, bf16[576,256]{1,0:T(8,128)(2,1)S(1)} %collective-permute-done.45.refs_2_, bf16[576,256]{1,0:T(8,128)(2,1)S(1)} %collective-permute-done.46.refs_3_), custom_call_target="tpu_custom_call" | custom-call | tf_op jit(solution)/shard_map/pallas_call | solution.py:566
  106.8 1.8 %shard_map.112 = (f32[9,256,256]{2,1,0:T(8,128)}, f32[1,256]{1,0:T(1,128)}) custom-call(bf16[576,256]{1,0:T(8,128)(2,1)S(1)} %constant_dynamic-update-slice_fusion.refs_0_, bf16[576,256]{1,0:T(8,128)(2,1)S(1)} %collective-permute-done.33.refs_1_, bf16[576,256]{1,0:T(8,128)(2,1)S(1)} %collective-permute-done.39.refs_2_, ...), custom_call_target="tpu_custom_call" | custom-call | tf_op jit(solution)/shard_map/pallas_call | solution.py:566
  (66 shorter events, 1.5 us)
Async XLA Ops:
  1.4 0.9 copy-start.2
  2.3 0.9 copy-start.4
  5.4 2.3 %collective-permute-start = (bf16[2,192,256]{2,1,0:T(8,128)(2,1)S(1)}, bf16[2,192,256]{2,1,0:T(8,128)(2,1)S(1)}, u32[]{:S(2)}, u32[]{:S(2)}) collective-permute-start(bf16[2,192,256]{2,1,0:T(8,128)(2,1)S(1)} %get-tuple-element.100), channel_id=1, source_target_pairs={{0,1},{1,0},{2,3},{3,2},{4,5},{5,4},{6,7},{7,6},{8,9},{9,8},{10,11... | collective-permute-start | bytes 589832 | tf_op jit(solution)/shard_map/ppermute | solution.py:580
  6.0 1.2 %collective-permute-start.1 = (bf16[2,48,256]{2,1,0:T(8,128)(2,1)S(1)}, bf16[2,48,256]{2,1,0:T(8,128)(2,1)S(1)}, u32[]{:S(2)}, u32[]{:S(2)}) collective-permute-start(bf16[2,48,256]{2,1,0:T(8,128)(2,1)S(1)} %get-tuple-element.101), channel_id=1, source_target_pairs={{0,1},{1,0},{2,3},{3,2},{4,5},{5,4},{6,7},{7,6},{8,9},{9,8},{10,11... | collective-permute-start | bytes 147464 | tf_op jit(solution)/shard_map/ppermute | solution.py:580
  6.0 1.3 %collective-permute-start.2 = (bf16[2,48,256]{2,1,0:T(8,128)(2,1)S(1)}, bf16[2,48,256]{2,1,0:T(8,128)(2,1)S(1)}, u32[]{:S(2)}, u32[]{:S(2)}) collective-permute-start(bf16[2,48,256]{2,1,0:T(8,128)(2,1)S(1)} %get-tuple-element.102), channel_id=1, source_target_pairs={{0,1},{1,0},{2,3},{3,2},{4,5},{5,4},{6,7},{7,6},{8,9},{9,8},{10,11... | collective-permute-start | bytes 147464 | tf_op jit(solution)/shard_map/ppermute | solution.py:580
  6.5 1.2 %collective-permute-start.3 = (bf16[2,48,256]{2,1,0:T(8,128)(2,1)S(1)}, bf16[2,48,256]{2,1,0:T(8,128)(2,1)S(1)}, u32[]{:S(2)}, u32[]{:S(2)}) collective-permute-start(bf16[2,48,256]{2,1,0:T(8,128)(2,1)S(1)} %get-tuple-element.103), channel_id=1, source_target_pairs={{0,1},{1,0},{2,3},{3,2},{4,5},{5,4},{6,7},{7,6},{8,9},{9,8},{10,11... | collective-permute-start | bytes 147464 | tf_op jit(solution)/shard_map/ppermute | solution.py:580
  7.7 13.9 %collective-permute-start.4 = (bf16[2,2,192,256]{3,2,1,0:T(8,128)(2,1)S(1)}, bf16[2,2,192,256]{3,2,1,0:T(8,128)(2,1)S(1)}, u32[]{:S(2)}, u32[]{:S(2)}) collective-permute-start(bf16[2,2,192,256]{3,2,1,0:T(8,128)(2,1)S(1)} %get-tuple-element.104), channel_id=1, source_target_pairs={{0,2},{2,0},{4,6},{6,4},{8,10},{10,8},{12,14},{14,12},{1,15},{3,5}... | collective-permute-start | bytes 1179656 | tf_op jit(solution)/shard_map/ppermute | solution.py:610
  10.5 8.2 %collective-permute-start.5 = (bf16[2,2,48,256]{3,2,1,0:T(8,128)(2,1)S(1)}, bf16[2,2,48,256]{3,2,1,0:T(8,128)(2,1)S(1)}, u32[]{:S(2)}, u32[]{:S(2)}) collective-permute-start(bf16[2,2,48,256]{3,2,1,0:T(8,128)(2,1)S(1)} %get-tuple-element.105), channel_id=1, source_target_pairs={{0,4},{4,0},{10,14},{14,10},{1,9},{3,11},{5,13},{7,15},{9,1},{11,3... | collective-permute-start | bytes 294920 | tf_op jit(solution)/shard_map/ppermute | solution.py:610
  14.0 7.7 %collective-permute-start.6 = (bf16[2,2,48,256]{3,2,1,0:T(8,128)(2,1)S(1)}, bf16[2,2,48,256]{3,2,1,0:T(8,128)(2,1)S(1)}, u32[]{:S(2)}, u32[]{:S(2)}) collective-permute-start(bf16[2,2,48,256]{3,2,1,0:T(8,128)(2,1)S(1)} %get-tuple-element.106), channel_id=1, source_target_pairs={{0,12},{2,14},{4,8},{6,10},{8,4},{10,6},{12,0},{14,2},{1,7},{3,13}... | collective-permute-start | bytes 294920 | tf_op jit(solution)/shard_map/ppermute | solution.py:610
  14.8 6.8 %collective-permute-start.7 = (bf16[2,2,48,256]{3,2,1,0:T(8,128)(2,1)S(1)}, bf16[2,2,48,256]{3,2,1,0:T(8,128)(2,1)S(1)}, u32[]{:S(2)}, u32[]{:S(2)}) collective-permute-start(bf16[2,2,48,256]{3,2,1,0:T(8,128)(2,1)S(1)} %get-tuple-element.107), channel_id=1, source_target_pairs={{1,11},{5,15},{11,1},{15,5},{17,27},{21,31},{27,17},{31,21}} | collective-permute-start | bytes 294920 | tf_op jit(solution)/shard_map/ppermute | solution.py:610
  15.5 1.3 %copy-start = (bf16[3,3,256,256]{3,2,1,0:T(8,128)(2,1)S(1)}, bf16[3,3,256,256]{3,2,1,0:T(8,128)(2,1)}, u32[]{:S(2)}) copy-start(bf16[3,3,256,256]{3,2,1,0:T(8,128)(2,1)} %param.10) | copy-start | bytes 3538948
  16.8 1.3 %copy-start.6 = (bf16[3,3,256,256]{3,2,1,0:T(8,128)(2,1)S(1)}, bf16[3,3,256,256]{3,2,1,0:T(8,128)(2,1)}, u32[]{:S(2)}) copy-start(bf16[3,3,256,256]{3,2,1,0:T(8,128)(2,1)} %param.8) | copy-start | bytes 3538948
  18.0 9.9 %copy-start.3 = (bf16[1,6,3,24,256]{4,3,2,1,0:T(8,128)(2,1)S(1)}, bf16[1,6,3,24,256]{4,3,2,1,0:T(8,128)(2,1)}, u32[]{:S(2)}) copy-start(bf16[1,6,3,24,256]{4,3,2,1,0:T(8,128)(2,1)} %param.6) | copy-start | bytes 663556
  18.0 9.9 %copy-start.5 = (bf16[1,1,6,3,24,256]{5,4,3,2,1,0:T(8,128)(2,1)S(1)}, bf16[1,1,6,3,24,256]{5,4,3,2,1,0:T(8,128)(2,1)}, u32[]{:S(2)}) copy-start(bf16[1,1,6,3,24,256]{5,4,3,2,1,0:T(8,128)(2,1)} %param.7) | copy-start | bytes 663556
  18.0 9.9 %copy-start.7 = (f32[256]{0:T(256)S(1)}, f32[256]{0:T(256)}, u32[]{:S(2)}) copy-start(f32[256]{0:T(256)} %param.9) | copy-start | bytes 3076
  21.7 6.3 %collective-permute-start.8 = (bf16[2,2,192,256]{3,2,1,0:T(8,128)(2,1)S(1)}, bf16[2,2,192,256]{3,2,1,0:T(8,128)(2,1)S(1)}, u32[]{:S(2)}, u32[]{:S(2)}) collective-permute-start(bf16[2,2,192,256]{3,2,1,0:T(8,128)(2,1)S(1)} %collective-permute-done.4.refs_0_), channel_id=1, source_target_pairs={{0,1},{1,0},{2,3},{3,2},{4,5},{5,4},{6,7},{7,6},{8,9},{9,8},{10,11... | collective-permute-start | bytes 1179656 | tf_op jit(solution)/shard_map/ppermute | solution.py:580
  26.1 1.5 %collective-permute-start.9 = (bf16[2,2,48,256]{3,2,1,0:T(8,128)(2,1)S(1)}, bf16[2,2,48,256]{3,2,1,0:T(8,128)(2,1)S(1)}, u32[]{:S(2)}, u32[]{:S(2)}) collective-permute-start(bf16[2,2,48,256]{3,2,1,0:T(8,128)(2,1)S(1)} %collective-permute-done.5.refs_2_), channel_id=1, source_target_pairs={{0,1},{1,0},{2,3},{3,2},{4,5},{5,4},{6,7},{7,6},{8,9},{9,8},{10,11... | collective-permute-start | bytes 294920 | tf_op jit(solution)/shard_map/ppermute | solution.py:580
  26.2 1.6 %collective-permute-start.10 = (bf16[2,2,48,256]{3,2,1,0:T(8,128)(2,1)S(1)}, bf16[2,2,48,256]{3,2,1,0:T(8,128)(2,1)S(1)}, u32[]{:S(2)}, u32[]{:S(2)}) collective-permute-start(bf16[2,2,48,256]{3,2,1,0:T(8,128)(2,1)S(1)} %collective-permute-done.6.refs_4_), channel_id=1, source_target_pairs={{0,1},{1,0},{2,3},{3,2},{4,5},{5,4},{6,7},{7,6},{8,9},{9,8},{10,11... | collective-permute-start | bytes 294920 | tf_op jit(solution)/shard_map/ppermute | solution.py:580
  26.7 1.3 %collective-permute-start.11 = (bf16[2,2,48,256]{3,2,1,0:T(8,128)(2,1)S(1)}, bf16[2,2,48,256]{3,2,1,0:T(8,128)(2,1)S(1)}, u32[]{:S(2)}, u32[]{:S(2)}) collective-permute-start(bf16[2,2,48,256]{3,2,1,0:T(8,128)(2,1)S(1)} %collective-permute-done.7.refs_6_), channel_id=1, source_target_pairs={{0,1},{1,0},{2,3},{3,2},{4,5},{5,4},{6,7},{7,6},{8,9},{9,8},{10,11... | collective-permute-start | bytes 294920 | tf_op jit(solution)/shard_map/ppermute | solution.py:580
  36.3 2.1 %collective-permute-start.22 = (bf16[9,128,256]{2,1,0:T(8,128)(2,1)S(1)}, bf16[9,128,256]{2,1,0:T(8,128)(2,1)S(1)}, u32[]{:S(2)}, u32[]{:S(2)}) collective-permute-start(bf16[9,128,256]{2,1,0:T(8,128)(2,1)S(1)} %get-tuple-element.139), channel_id=1, source_target_pairs={{0,1},{1,0},{2,3},{3,2},{4,5},{5,4},{6,7},{7,6},{8,9},{9,8},{10,11... | collective-permute-start | bytes 1769480 | tf_op jit(solution)/shard_map/ppermute | solution.py:580
  36.7 3.1 %collective-permute-start.12 = (bf16[9,128,256]{2,1,0:T(8,128)(2,1)S(1)}, bf16[9,128,256]{2,1,0:T(8,128)(2,1)S(1)}, u32[]{:S(2)}, u32[]{:S(2)}) collective-permute-start(bf16[9,128,256]{2,1,0:T(8,128)(2,1)S(1)} %get-tuple-element.119), channel_id=1, source_target_pairs={{0,1},{1,0},{2,3},{3,2},{4,5},{5,4},{6,7},{7,6},{8,9},{9,8},{10,11... | collective-permute-start | bytes 1769480 | tf_op jit(solution)/shard_map/ppermute | solution.py:580
  38.5 10.9 %collective-permute-start.23 = (bf16[576,256]{1,0:T(8,128)(2,1)S(1)}, bf16[576,256]{1,0:T(8,128)(2,1)S(1)}, u32[]{:S(2)}, u32[]{:S(2)}) collective-permute-start(bf16[576,256]{1,0:T(8,128)(2,1)S(1)} %get-tuple-element.141), channel_id=1, source_target_pairs={{0,2},{2,0},{4,6},{6,4},{8,10},{10,8},{12,14},{14,12},{1,3},{3,1},... | collective-permute-start | bytes 884744 | tf_op jit(solution)/shard_map/ppermute | solution.py:659
  38.6 1.2 %collective-permute-start.13 = (bf16[8,256]{1,0:T(8,128)(2,1)S(1)}, bf16[8,256]{1,0:T(8,128)(2,1)S(1)}, u32[]{:S(2)}, u32[]{:S(2)}) collective-permute-start(bf16[8,256]{1,0:T(8,128)(2,1)S(1)} %get-tuple-element.121), channel_id=1, source_target_pairs={{0,1},{1,0},{2,3},{3,2},{4,5},{5,4},{6,7},{7,6},{8,9},{9,8},{10,11... | collective-permute-start | bytes 12296 | tf_op jit(solution)/shard_map/ppermute | solution.py:580
  39.9 15.3 %collective-permute-start.14 = (bf16[584,256]{1,0:T(8,128)(2,1)S(1)}, bf16[584,256]{1,0:T(8,128)(2,1)S(1)}, u32[]{:S(2)}, u32[]{:S(2)}) collective-permute-start(bf16[584,256]{1,0:T(8,128)(2,1)S(1)} %get-tuple-element.123), channel_id=1, source_target_pairs={{0,2},{2,0},{4,6},{6,4},{8,10},{10,8},{12,14},{14,12},{1,3},{3,1},... | collective-permute-start | bytes 897032 | tf_op jit(solution)/shard_map/ppermute | solution.py:659
  41.9 2.7 %collective-permute-start.15 = (bf16[2,192,256]{2,1,0:T(8,128)(2,1)S(1)}, bf16[2,192,256]{2,1,0:T(8,128)(2,1)S(1)}, u32[]{:S(2)}, u32[]{:S(2)}) collective-permute-start(bf16[2,192,256]{2,1,0:T(8,128)(2,1)S(1)} %get-tuple-element.128), channel_id=1, source_target_pairs={{0,1},{1,0},{2,3},{3,2},{4,5},{5,4},{6,7},{7,6},{8,9},{9,8},{10,11... | collective-permute-start | bytes 589832 | tf_op jit(solution)/shard_map/ppermute | solution.py:580
  41.9 1.5 %collective-permute-start.16 = (bf16[2,48,256]{2,1,0:T(8,128)(2,1)S(1)}, bf16[2,48,256]{2,1,0:T(8,128)(2,1)S(1)}, u32[]{:S(2)}, u32[]{:S(2)}) collective-permute-start(bf16[2,48,256]{2,1,0:T(8,128)(2,1)S(1)} %get-tuple-element.129), channel_id=1, source_target_pairs={{0,1},{1,0},{2,3},{3,2},{4,5},{5,4},{6,7},{7,6},{8,9},{9,8},{10,11... | collective-permute-start | bytes 147464 | tf_op jit(solution)/shard_map/ppermute | solution.py:580
  42.4 1.2 %collective-permute-start.17 = (bf16[2,48,256]{2,1,0:T(8,128)(2,1)S(1)}, bf16[2,48,256]{2,1,0:T(8,128)(2,1)S(1)}, u32[]{:S(2)}, u32[]{:S(2)}) collective-permute-start(bf16[2,48,256]{2,1,0:T(8,128)(2,1)S(1)} %get-tuple-element.130), channel_id=1, source_target_pairs={{0,1},{1,0},{2,3},{3,2},{4,5},{5,4},{6,7},{7,6},{8,9},{9,8},{10,11... | collective-permute-start | bytes 147464 | tf_op jit(solution)/shard_map/ppermute | solution.py:580
  43.4 1.2 %collective-permute-start.18 = (bf16[2,48,256]{2,1,0:T(8,128)(2,1)S(1)}, bf16[2,48,256]{2,1,0:T(8,128)(2,1)S(1)}, u32[]{:S(2)}, u32[]{:S(2)}) collective-permute-start(bf16[2,48,256]{2,1,0:T(8,128)(2,1)S(1)} %get-tuple-element.131), channel_id=1, source_target_pairs={{0,1},{1,0},{2,3},{3,2},{4,5},{5,4},{6,7},{7,6},{8,9},{9,8},{10,11... | collective-permute-start | bytes 147464 | tf_op jit(solution)/shard_map/ppermute | solution.py:580
  44.7 7.0 %collective-permute-start.19 = (bf16[2,2,48,256]{3,2,1,0:T(8,128)(2,1)S(1)}, bf16[2,2,48,256]{3,2,1,0:T(8,128)(2,1)S(1)}, u32[]{:S(2)}, u32[]{:S(2)}) collective-permute-start(bf16[2,2,48,256]{3,2,1,0:T(8,128)(2,1)S(1)} %get-tuple-element.132), channel_id=1, source_target_pairs={{0,4},{4,0},{10,14},{14,10},{1,9},{3,11},{5,13},{7,15},{9,1},{11,3... | collective-permute-start | bytes 294920 | tf_op jit(solution)/shard_map/ppermute | solution.py:610
  47.5 7.4 %collective-permute-start.20 = (bf16[2,2,48,256]{3,2,1,0:T(8,128)(2,1)S(1)}, bf16[2,2,48,256]{3,2,1,0:T(8,128)(2,1)S(1)}, u32[]{:S(2)}, u32[]{:S(2)}) collective-permute-start(bf16[2,2,48,256]{3,2,1,0:T(8,128)(2,1)S(1)} %get-tuple-element.133), channel_id=1, source_target_pairs={{0,12},{2,14},{4,8},{6,10},{8,4},{10,6},{12,0},{14,2},{1,7},{3,13}... | collective-permute-start | bytes 294920 | tf_op jit(solution)/shard_map/ppermute | solution.py:610
  48.5 6.4 %collective-permute-start.21 = (bf16[2,2,48,256]{3,2,1,0:T(8,128)(2,1)S(1)}, bf16[2,2,48,256]{3,2,1,0:T(8,128)(2,1)S(1)}, u32[]{:S(2)}, u32[]{:S(2)}) collective-permute-start(bf16[2,2,48,256]{3,2,1,0:T(8,128)(2,1)S(1)} %get-tuple-element.134), channel_id=1, source_target_pairs={{1,11},{5,15},{11,1},{15,5},{17,27},{21,31},{27,17},{31,21}} | collective-permute-start | bytes 294920 | tf_op jit(solution)/shard_map/ppermute | solution.py:610
  49.5 11.7 %collective-permute-start.24 = (bf16[144,256]{1,0:T(8,128)(2,1)S(1)}, bf16[144,256]{1,0:T(8,128)(2,1)S(1)}, u32[]{:S(2)}, u32[]{:S(2)}) collective-permute-start(bf16[144,256]{1,0:T(8,128)(2,1)S(1)} %get-tuple-element.142), channel_id=1, source_target_pairs={{0,4},{2,6},{4,0},{6,2},{8,12},{10,14},{12,8},{14,10},{1,5},{3,7},... | collective-permute-start | bytes 221192 | tf_op jit(solution)/shard_map/ppermute | solution.py:662
  55.3 43.7 %copy-start.1 = (bf16[3,3,256,256]{3,2,1,0:T(8,128)(2,1)S(1)}, bf16[3,3,256,256]{3,2,1,0:T(8,128)(2,1)}, u32[]{:S(2)}) copy-start(bf16[3,3,256,256]{3,2,1,0:T(8,128)(2,1)} %param.10) | copy-start | bytes 3538948
  55.4 19.4 %collective-permute-start.27 = (bf16[152,256]{1,0:T(8,128)(2,1)S(1)}, bf16[152,256]{1,0:T(8,128)(2,1)S(1)}, u32[]{:S(2)}, u32[]{:S(2)}) collective-permute-start(bf16[152,256]{1,0:T(8,128)(2,1)S(1)} %get-tuple-element.149), channel_id=1, source_target_pairs={{0,4},{2,6},{4,0},{6,2},{8,12},{10,14},{12,8},{14,10},{1,5},{3,7},... | collective-permute-start | bytes 233480 | tf_op jit(solution)/shard_map/ppermute | solution.py:662
  56.3 18.4 %collective-permute-start.28 = (bf16[152,256]{1,0:T(8,128)(2,1)S(1)}, bf16[152,256]{1,0:T(8,128)(2,1)S(1)}, u32[]{:S(2)}, u32[]{:S(2)}) collective-permute-start(bf16[152,256]{1,0:T(8,128)(2,1)S(1)} %get-tuple-element.150), channel_id=1, source_target_pairs={{0,8},{2,10},{4,12},{6,14},{8,0},{10,2},{12,4},{14,6},{1,9},{3,11}... | collective-permute-start | bytes 233480 | tf_op jit(solution)/shard_map/ppermute | solution.py:662
  59.6 15.2 %collective-permute-start.29 = (bf16[152,256]{1,0:T(8,128)(2,1)S(1)}, bf16[152,256]{1,0:T(8,128)(2,1)S(1)}, u32[]{:S(2)}, u32[]{:S(2)}) collective-permute-start(bf16[152,256]{1,0:T(8,128)(2,1)S(1)} %get-tuple-element.151), channel_id=1, source_target_pairs={{0,12},{2,14},{4,8},{6,10},{8,4},{10,6},{12,0},{14,2},{1,13},{3,15... | collective-permute-start | bytes 233480 | tf_op jit(solution)/shard_map/ppermute | solution.py:662
  59.8 12.0 %collective-permute-start.25 = (bf16[144,256]{1,0:T(8,128)(2,1)S(1)}, bf16[144,256]{1,0:T(8,128)(2,1)S(1)}, u32[]{:S(2)}, u32[]{:S(2)}) collective-permute-start(bf16[144,256]{1,0:T(8,128)(2,1)S(1)} %get-tuple-element.143), channel_id=1, source_target_pairs={{0,8},{2,10},{4,12},{6,14},{8,0},{10,2},{12,4},{14,6},{1,9},{3,11}... | collective-permute-start | bytes 221192 | tf_op jit(solution)/shard_map/ppermute | solution.py:662
  61.1 13.6 %collective-permute-start.26 = (bf16[144,256]{1,0:T(8,128)(2,1)S(1)}, bf16[144,256]{1,0:T(8,128)(2,1)S(1)}, u32[]{:S(2)}, u32[]{:S(2)}) collective-permute-start(bf16[144,256]{1,0:T(8,128)(2,1)S(1)} %get-tuple-element.144), channel_id=1, source_target_pairs={{0,12},{2,14},{4,8},{6,10},{8,4},{10,6},{12,0},{14,2},{1,13},{3,15... | collective-permute-start | bytes 221192 | tf_op jit(solution)/shard_map/ppermute | solution.py:662
  71.9 21.4 %collective-permute-start.34 = (bf16[2,2,192,256]{3,2,1,0:T(8,128)(2,1)S(1)}, bf16[2,2,192,256]{3,2,1,0:T(8,128)(2,1)S(1)}, u32[]{:S(2)}, u32[]{:S(2)}) collective-permute-start(bf16[2,2,192,256]{3,2,1,0:T(8,128)(2,1)S(1)} %get-tuple-element.160), channel_id=1, source_target_pairs={{0,2},{2,0},{4,6},{6,4},{8,10},{10,8},{12,14},{14,12},{1,15},{3,5}... | collective-permute-start | bytes 1179656 | tf_op jit(solution)/shard_map/ppermute | solution.py:610
  74.8 7.2 %collective-permute-start.43 = (bf16[144,256]{1,0:T(8,128)(2,1)S(1)}, bf16[144,256]{1,0:T(8,128)(2,1)S(1)}, u32[]{:S(2)}, u32[]{:S(2)}) collective-permute-start(bf16[144,256]{1,0:T(8,128)(2,1)S(1)} %shard_map.113), channel_id=1, source_target_pairs={{0,12},{2,14},{4,8},{6,10},{8,4},{10,6},{12,0},{14,2},{1,13},{3,15... | collective-permute-start | bytes 221192 | tf_op jit(solution)/shard_map/ppermute | solution.py:662
  77.3 11.6 %collective-permute-start.42 = (bf16[144,256]{1,0:T(8,128)(2,1)S(1)}, bf16[144,256]{1,0:T(8,128)(2,1)S(1)}, u32[]{:S(2)}, u32[]{:S(2)}) collective-permute-start(bf16[144,256]{1,0:T(8,128)(2,1)S(1)} %shard_map.113), channel_id=1, source_target_pairs={{0,8},{2,10},{4,12},{6,14},{8,0},{10,2},{12,4},{14,6},{1,9},{3,11}... | collective-permute-start | bytes 221192 | tf_op jit(solution)/shard_map/ppermute | solution.py:662
  77.3 11.6 %collective-permute-start.41 = (bf16[144,256]{1,0:T(8,128)(2,1)S(1)}, bf16[144,256]{1,0:T(8,128)(2,1)S(1)}, u32[]{:S(2)}, u32[]{:S(2)}) collective-permute-start(bf16[144,256]{1,0:T(8,128)(2,1)S(1)} %shard_map.113), channel_id=1, source_target_pairs={{0,4},{2,6},{4,0},{6,2},{8,12},{10,14},{12,8},{14,10},{1,5},{3,7},... | collective-permute-start | bytes 221192 | tf_op jit(solution)/shard_map/ppermute | solution.py:662
  79.3 14.0 %collective-permute-start.32 = (bf16[144,256]{1,0:T(8,128)(2,1)S(1)}, bf16[144,256]{1,0:T(8,128)(2,1)S(1)}, u32[]{:S(2)}, u32[]{:S(2)}) collective-permute-start(bf16[144,256]{1,0:T(8,128)(2,1)S(1)} %get-tuple-element.156), channel_id=1, source_target_pairs={{0,12},{2,14},{4,8},{6,10},{8,4},{10,6},{12,0},{14,2},{1,13},{3,15... | collective-permute-start | bytes 221192 | tf_op jit(solution)/shard_map/ppermute | solution.py:662
  82.0 11.2 %collective-permute-start.31 = (bf16[144,256]{1,0:T(8,128)(2,1)S(1)}, bf16[144,256]{1,0:T(8,128)(2,1)S(1)}, u32[]{:S(2)}, u32[]{:S(2)}) collective-permute-start(bf16[144,256]{1,0:T(8,128)(2,1)S(1)} %get-tuple-element.156), channel_id=1, source_target_pairs={{0,8},{2,10},{4,12},{6,14},{8,0},{10,2},{12,4},{14,6},{1,9},{3,11}... | collective-permute-start | bytes 221192 | tf_op jit(solution)/shard_map/ppermute | solution.py:662
  88.8 4.4 %collective-permute-start.30 = (bf16[144,256]{1,0:T(8,128)(2,1)S(1)}, bf16[144,256]{1,0:T(8,128)(2,1)S(1)}, u32[]{:S(2)}, u32[]{:S(2)}) collective-permute-start(bf16[144,256]{1,0:T(8,128)(2,1)S(1)} %get-tuple-element.156), channel_id=1, source_target_pairs={{0,4},{2,6},{4,0},{6,2},{8,12},{10,14},{12,8},{14,10},{1,5},{3,7},... | collective-permute-start | bytes 221192 | tf_op jit(solution)/shard_map/ppermute | solution.py:662
  88.9 9.2 %collective-permute-start.44 = (bf16[576,256]{1,0:T(8,128)(2,1)S(1)}, bf16[576,256]{1,0:T(8,128)(2,1)S(1)}, u32[]{:S(2)}, u32[]{:S(2)}) collective-permute-start(bf16[576,256]{1,0:T(8,128)(2,1)S(1)} %pad_maximum_fusion.refs_0_), channel_id=1, source_target_pairs={{0,2},{2,0},{4,6},{6,4},{8,10},{10,8},{12,14},{14,12},{1,3},{3,1},... | collective-permute-start | bytes 884744 | tf_op jit(solution)/shard_map/ppermute | solution.py:659
  93.2 5.6 %collective-permute-start.35 = (bf16[2,2,192,256]{3,2,1,0:T(8,128)(2,1)S(1)}, bf16[2,2,192,256]{3,2,1,0:T(8,128)(2,1)S(1)}, u32[]{:S(2)}, u32[]{:S(2)}) collective-permute-start(bf16[2,2,192,256]{3,2,1,0:T(8,128)(2,1)S(1)} %collective-permute-done.34.refs_0_), channel_id=1, source_target_pairs={{0,1},{1,0},{2,3},{3,2},{4,5},{5,4},{6,7},{7,6},{8,9},{9,8},{10,11... | collective-permute-start | bytes 1179656 | tf_op jit(solution)/shard_map/ppermute | solution.py:580
  93.3 11.3 %collective-permute-start.33 = (bf16[576,256]{1,0:T(8,128)(2,1)S(1)}, bf16[576,256]{1,0:T(8,128)(2,1)S(1)}, u32[]{:S(2)}, u32[]{:S(2)}) collective-permute-start(bf16[576,256]{1,0:T(8,128)(2,1)S(1)} %constant_dynamic-update-slice_fusion.refs_0_), channel_id=1, source_target_pairs={{0,2},{2,0},{4,6},{6,4},{8,10},{10,8},{12,14},{14,12},{1,3},{3,1},... | collective-permute-start | bytes 884744 | tf_op jit(solution)/shard_map/ppermute | solution.py:659
  96.2 1.3 %collective-permute-start.36 = (bf16[2,2,48,256]{3,2,1,0:T(8,128)(2,1)S(1)}, bf16[2,2,48,256]{3,2,1,0:T(8,128)(2,1)S(1)}, u32[]{:S(2)}, u32[]{:S(2)}) collective-permute-start(bf16[2,2,48,256]{3,2,1,0:T(8,128)(2,1)S(1)} %collective-permute-done.19.refs_2_), channel_id=1, source_target_pairs={{0,1},{1,0},{2,3},{3,2},{4,5},{5,4},{6,7},{7,6},{8,9},{9,8},{10,11... | collective-permute-start | bytes 294920 | tf_op jit(solution)/shard_map/ppermute | solution.py:580
  96.4 1.3 %collective-permute-start.37 = (bf16[2,2,48,256]{3,2,1,0:T(8,128)(2,1)S(1)}, bf16[2,2,48,256]{3,2,1,0:T(8,128)(2,1)S(1)}, u32[]{:S(2)}, u32[]{:S(2)}) collective-permute-start(bf16[2,2,48,256]{3,2,1,0:T(8,128)(2,1)S(1)} %collective-permute-done.20.refs_4_), channel_id=1, source_target_pairs={{0,1},{1,0},{2,3},{3,2},{4,5},{5,4},{6,7},{7,6},{8,9},{9,8},{10,11... | collective-permute-start | bytes 294920 | tf_op jit(solution)/shard_map/ppermute | solution.py:580
  97.5 1.3 %collective-permute-start.38 = (bf16[2,2,48,256]{3,2,1,0:T(8,128)(2,1)S(1)}, bf16[2,2,48,256]{3,2,1,0:T(8,128)(2,1)S(1)}, u32[]{:S(2)}, u32[]{:S(2)}) collective-permute-start(bf16[2,2,48,256]{3,2,1,0:T(8,128)(2,1)S(1)} %collective-permute-done.21.refs_6_), channel_id=1, source_target_pairs={{0,1},{1,0},{2,3},{3,2},{4,5},{5,4},{6,7},{7,6},{8,9},{9,8},{10,11... | collective-permute-start | bytes 294920 | tf_op jit(solution)/shard_map/ppermute | solution.py:580
  97.7 7.3 %collective-permute-start.45 = (bf16[576,256]{1,0:T(8,128)(2,1)S(1)}, bf16[576,256]{1,0:T(8,128)(2,1)S(1)}, u32[]{:S(2)}, u32[]{:S(2)}) collective-permute-start(bf16[576,256]{1,0:T(8,128)(2,1)S(1)} %pad_maximum_fusion.refs_0_), channel_id=1, source_target_pairs={{0,1},{1,0},{2,3},{3,2},{4,5},{5,4},{6,7},{7,6},{8,9},{9,8},{10,11... | collective-permute-start | bytes 884744 | tf_op jit(solution)/shard_map/ppermute | solution.py:580
  98.0 7.0 %collective-permute-start.46 = (bf16[576,256]{1,0:T(8,128)(2,1)S(1)}, bf16[576,256]{1,0:T(8,128)(2,1)S(1)}, u32[]{:S(2)}, u32[]{:S(2)}) collective-permute-start(bf16[576,256]{1,0:T(8,128)(2,1)S(1)} %collective-permute-done.44.refs_1_), channel_id=1, source_target_pairs={{0,1},{1,0},{2,3},{3,2},{4,5},{5,4},{6,7},{7,6},{8,9},{9,8},{10,11... | collective-permute-start | bytes 884744 | tf_op jit(solution)/shard_map/ppermute | solution.py:580
  98.8 7.9 %collective-permute-start.39 = (bf16[576,256]{1,0:T(8,128)(2,1)S(1)}, bf16[576,256]{1,0:T(8,128)(2,1)S(1)}, u32[]{:S(2)}, u32[]{:S(2)}) collective-permute-start(bf16[576,256]{1,0:T(8,128)(2,1)S(1)} %constant_dynamic-update-slice_fusion.refs_0_), channel_id=1, source_target_pairs={{0,1},{1,0},{2,3},{3,2},{4,5},{5,4},{6,7},{7,6},{8,9},{9,8},{10,11... | collective-permute-start | bytes 884744 | tf_op jit(solution)/shard_map/ppermute | solution.py:580
  104.7 2.1 %collective-permute-start.40 = (bf16[576,256]{1,0:T(8,128)(2,1)S(1)}, bf16[576,256]{1,0:T(8,128)(2,1)S(1)}, u32[]{:S(2)}, u32[]{:S(2)}) collective-permute-start(bf16[576,256]{1,0:T(8,128)(2,1)S(1)} %collective-permute-done.33.refs_1_), channel_id=1, source_target_pairs={{0,1},{1,0},{2,3},{3,2},{4,5},{5,4},{6,7},{7,6},{8,9},{9,8},{10,11... | collective-permute-start | bytes 884744 | tf_op jit(solution)/shard_map/ppermute | solution.py:580

commit v12 on v11

--- a/solution.py
+++ b/solution.py
@@ -690,13 +690,13 @@
     keep2, send2 = sum_dp(keep2, swap_dp(send2))
     recv2 = along_y(send2)
     keep1, send1, bias_sum = sum_dp(keep1, swap_dp(send1), bias_sum, swap_dp(send_bias))
+    got = [across(joined[i], i) for i in early]
+    recv2, send1, got = barrier((recv2, send1, got))
+    came.update(zip(early, got))
     recv1 = along_y(send1)
-    got = [across(joined[i], i) for i in early]
 
     keep2, sends2, _ = sum_y(keep2, recv2)
     recvs2 = [along_z(v, j + 1) for j, v in enumerate(sends2)]
-    recv1, got = barrier((recv1, got))
-    came.update(zip(early, got))
 
     keep1, sends1, (bias_sum,) = sum_y(keep1, recv1, bias_sum)
     sends1, todo = barrier((sends1, [joined[i] for i in middle]))

time: 109 us -> 114 us (1.046)
  waiting for transfers between devices: 26.8 us -> 32.1 us
    ppermute x4, waiting for transfers between devices: 0.35 us -> 7.46 us  [along_y(): return lax.ppermute(v, 'tile', [(i, i ^ 1) for i in range(tiles)])]
    ppermute x4, starting transfers between devices: 7.83 us -> 4.92 us  [along_y(): return lax.ppermute(v, 'tile', [(i, i ^ 1) for i in range(tiles)])]
    ppermute x23, waiting for transfers between devices: 8.17 us -> 5.87 us  [swap_dp(): return lax.ppermute(v, 'dp', [(i, count - 1 - i) for i in range(count)])]
    ppermute x12, starting transfers between devices: 22 us -> 24.2 us  [along_z(): return lax.ppermute(v, 'tile', [(i, i ^ 2 * j) for i in range(tiles)])]
    ppermute x12, waiting for transfers between devices: 10.2 us -> 12.1 us  [along_z(): return lax.ppermute(v, 'tile', [(i, i ^ 2 * j) for i in range(tiles)])]
    ppermute x8, waiting for transfers between devices: 8.08 us -> 6.68 us  [across(): return lax.ppermute(v, ('tile', 'dp'), pairs[step])]
  transfers between devices with their start and end apart: 47 -> 47, of which waited for: 19 -> 18; matrix products, arithmetic and copies ran while one was open for 0% -> 0% of each run, Pallas kernels for 8% -> 8%
where the time goes in v12:
time: 114 us
  starting transfers between devices  54.9 us (48%)
  waiting for transfers between devices  32.1 us (28%)
  Pallas kernels  20.9 us (18%)
  local copies, waits for them, and re-layouts  5.22 us (5%)
    ppermute x12, starting transfers between devices, along_z(): return lax.ppermute(v, 'tile', [(i, i ^ 2 * j) for i in range(tiles)])  24.2 us
    pallas_call x14, Pallas kernels, run(): pl.pallas_call(kernel, out_shape=[jax.ShapeDtypeStruct(s, dt) for s, dt i...  20.9 us
    ppermute x8, starting transfers between devices, across(): return lax.ppermute(v, ('tile', 'dp'), pairs[step])  16 us
    ppermute x12, waiting for transfers between devices, along_z(): return lax.ppermute(v, 'tile', [(i, i ^ 2 * j) for i in range(tiles)])  12.1 us
    ppermute x23, starting transfers between devices, swap_dp(): return lax.ppermute(v, 'dp', [(i, count - 1 - i) for i in range(count)])  9.83 us
    ppermute x4, waiting for transfers between devices, along_y(): return lax.ppermute(v, 'tile', [(i, i ^ 1) for i in range(tiles)])  7.46 us
    ppermute x8, waiting for transfers between devices, across(): return lax.ppermute(v, ('tile', 'dp'), pairs[step])  6.68 us
    ppermute x23, waiting for transfers between devices, swap_dp(): return lax.ppermute(v, 'dp', [(i, count - 1 - i) for i in range(count)])  5.87 us
  transfers between devices with their start and end apart: 47, of which 18 were waited for; matrix products, arithmetic and copies ran while one was open for 0% of the time, Pallas kernels for 8%

profile of v12, /device:TPU:0, one launch (start us, length us, event | category | flops | bytes accessed | tf_op | source)
XLA Modules:
  0.0 114.1 jit_solution(15442848470632262312)
XLA Ops:
  0.6 0.8 copy.12.ep
  1.4 0.9 copy-done.2
  2.3 0.9 copy-done.4
  3.3 2.2 %shard_map.101 = (bf16[2,192,256]{2,1,0:T(8,128)(2,1)S(1)}, bf16[2,48,256]{2,1,0:T(8,128)(2,1)S(1)}, bf16[2,48,256]{2,1,0:T(8,128)(2,1)S(1)}, bf16[2,48,256]{2,1...) custom-call(s32[6,4]{1,0:T(8,128)S(1)} %copy.12.ep, ...), custom_call_target="tpu_custom_call" | custom-call | tf_op jit(solution)/shard_map/pallas_call | solution.py:566
  5.4 0.5 collective-permute-start
  6.0 0.4 collective-permute-start.2
  6.5 0.6 collective-permute-done.1.refs_5_
  7.3 0.3 collective-permute-done.3.refs_7_
  7.7 2.7 %collective-permute-start.4 = (bf16[2,2,192,256]{3,2,1,0:T(8,128)(2,1)S(1)}, bf16[2,2,192,256]{3,2,1,0:T(8,128)(2,1)S(1)}, u32[]{:S(2)}, u32[]{:S(2)}) collective-permute-start(bf16[2,2,192,256]{3,2,1,0:T(8,128)(2,1)S(1)} %get-tuple-element.105), channel_id=1, source_target_pairs={{0,2},{2,0},{4,6},{6,4},{8,10},{10,8},{12,14},{14,12},{1,15},{3,5}... | collective-permute-start | bytes 1179656 | tf_op jit(solution)/shard_map/ppermute | solution.py:610
  10.5 3.5 %collective-permute-start.5 = (bf16[2,2,48,256]{3,2,1,0:T(8,128)(2,1)S(1)}, bf16[2,2,48,256]{3,2,1,0:T(8,128)(2,1)S(1)}, u32[]{:S(2)}, u32[]{:S(2)}) collective-permute-start(bf16[2,2,48,256]{3,2,1,0:T(8,128)(2,1)S(1)} %get-tuple-element.106), channel_id=1, source_target_pairs={{0,4},{4,0},{10,14},{14,10},{1,9},{3,11},{5,13},{7,15},{9,1},{11,3... | collective-permute-start | bytes 294920 | tf_op jit(solution)/shard_map/ppermute | solution.py:610
  14.0 0.9 collective-permute-start.6
  14.8 0.7 collective-permute-start.7
  15.5 1.3 %copy-done = bf16[3,3,256,256]{3,2,1,0:T(8,128)(2,1)S(1)} copy-done((bf16[3,3,256,256]{3,2,1,0:T(8,128)(2,1)S(1)}, bf16[3,3,256,256]{3,2,1,0:T(8,128)(2,1)}, u32[]{:S(2)}) %copy-start) | copy-done | bytes 1179672
  16.8 1.3 %copy-done.6 = bf16[3,3,256,256]{3,2,1,0:T(8,128)(2,1)S(1)} copy-done((bf16[3,3,256,256]{3,2,1,0:T(8,128)(2,1)S(1)}, bf16[3,3,256,256]{3,2,1,0:T(8,128)(2,1)}, u32[]{:S(2)}) %copy-start.6) | copy-done | bytes 1179672
  18.0 0.7 shard_map.103
  18.7 2.9 %collective-permute-done.6.refs_4_ = bf16[2,2,48,256]{3,2,1,0:T(8,128)(2,1)S(1)} collective-permute-done((bf16[2,2,48,256]{3,2,1,0:T(8,128)(2,1)S(1)}, bf16[2,2,48,256]{3,2,1,0:T(8,128)(2,1)S(1)}, u32[]{:S(2)}, u32[]{:S(2)}) %collective-permute-start.6) | collective-permute-done | bytes 98336 | tf_op jit(solution)/shard_map/ppermute | solution.py:610
  21.7 4.5 %collective-permute-start.8 = (bf16[2,2,192,256]{3,2,1,0:T(8,128)(2,1)S(1)}, bf16[2,2,192,256]{3,2,1,0:T(8,128)(2,1)S(1)}, u32[]{:S(2)}, u32[]{:S(2)}) collective-permute-start(bf16[2,2,192,256]{3,2,1,0:T(8,128)(2,1)S(1)} %collective-permute-done.4.refs_0_), channel_id=1, source_target_pairs={{0,1},{1,0},{2,3},{3,2},{4,5},{5,4},{6,7},{7,6},{8,9},{9,8},{10,11... | collective-permute-start | bytes 1179656 | tf_op jit(solution)/shard_map/ppermute | solution.py:580
  26.2 0.5 collective-permute-start.10
  26.7 1.0 collective-permute-done.9.refs_3_
  27.8 0.2 collective-permute-done.11.refs_7_
  28.0 8.3 %shard_map.104 = (bf16[9,128,256]{2,1,0:T(8,128)(2,1)S(1)}, f32[9,128,256]{2,1,0:T(8,128)S(1)}, bf16[9,128,256]{2,1,0:T(8,128)(2,1)S(1)}, f32[9,128,256]{2,1,0:T...) custom-call(s32[6,4]{1,0:T(8,128)S(1)} %copy.12.ep, ...), custom_call_target="tpu_custom_call" | custom-call | tf_op jit(solution)/shard_map/pallas_call | solution.py:566
  36.3 0.4 collective-permute-start.14
  36.7 0.2 collective-permute-start.12
  36.8 0.3 collective-permute-start.16
  37.2 1.2 %collective-permute-done.14.recv_ref = bf16[9,128,256]{2,1,0:T(8,128)(2,1)S(1)} collective-permute-done((bf16[9,128,256]{2,1,0:T(8,128)(2,1)S(1)}, bf16[9,128,256]{2,1,0:T(8,128)(2,1)S(1)}, u32[]{:S(2)}, u32[]{:S(2)}) %collective-permute-start.14) | collective-permute-done | bytes 589856 | tf_op jit(solution)/shard_map/ppermute | solution.py:580
  38.6 0.4 collective-permute-start.17
  38.9 0.2 collective-permute-start.18
  39.1 0.7 collective-permute-done.17.refs_5_
  39.8 0.3 collective-permute-start.19
  40.2 0.2 collective-permute-start.13
  40.4 0.7 collective-permute-done.19.refs_7_
  41.1 2.8 %collective-permute-start.20 = (bf16[2,2,48,256]{3,2,1,0:T(8,128)(2,1)S(1)}, bf16[2,2,48,256]{3,2,1,0:T(8,128)(2,1)S(1)}, u32[]{:S(2)}, u32[]{:S(2)}) collective-permute-start(bf16[2,2,48,256]{3,2,1,0:T(8,128)(2,1)S(1)} %get-tuple-element.136), channel_id=1, source_target_pairs={{0,4},{4,0},{10,14},{14,10},{1,9},{3,11},{5,13},{7,15},{9,1},{11,3... | collective-permute-start | bytes 294920 | tf_op jit(solution)/shard_map/ppermute | solution.py:610
  44.0 2.8 %collective-permute-start.21 = (bf16[2,2,48,256]{3,2,1,0:T(8,128)(2,1)S(1)}, bf16[2,2,48,256]{3,2,1,0:T(8,128)(2,1)S(1)}, u32[]{:S(2)}, u32[]{:S(2)}) collective-permute-start(bf16[2,2,48,256]{3,2,1,0:T(8,128)(2,1)S(1)} %get-tuple-element.137), channel_id=1, source_target_pairs={{0,12},{2,14},{4,8},{6,10},{8,4},{10,6},{12,0},{14,2},{1,7},{3,13}... | collective-permute-start | bytes 294920 | tf_op jit(solution)/shard_map/ppermute | solution.py:610
  46.8 0.8 collective-permute-start.22
  47.8 0.9 collective-permute-done.20.refs_2_
  48.7 2.8 %collective-permute-done.21.refs_4_ = bf16[2,2,48,256]{3,2,1,0:T(8,128)(2,1)S(1)} collective-permute-done((bf16[2,2,48,256]{3,2,1,0:T(8,128)(2,1)S(1)}, bf16[2,2,48,256]{3,2,1,0:T(8,128)(2,1)S(1)}, u32[]{:S(2)}, u32[]{:S(2)}) %collective-permute-start.21) | collective-permute-done | bytes 98336 | tf_op jit(solution)/shard_map/ppermute | solution.py:610
  51.5 2.0 %collective-permute-start.23 = (bf16[584,256]{1,0:T(8,128)(2,1)S(1)}, bf16[584,256]{1,0:T(8,128)(2,1)S(1)}, u32[]{:S(2)}, u32[]{:S(2)}) collective-permute-start(bf16[584,256]{1,0:T(8,128)(2,1)S(1)} %get-tuple-element.139), channel_id=1, source_target_pairs={{0,2},{2,0},{4,6},{6,4},{8,10},{10,8},{12,14},{14,12},{1,3},{3,1},... | collective-permute-start | bytes 897032 | tf_op jit(solution)/shard_map/ppermute | solution.py:659
  53.7 5.8 %collective-permute-done.23.recv_ref = bf16[584,256]{1,0:T(8,128)(2,1)S(1)} collective-permute-done((bf16[584,256]{1,0:T(8,128)(2,1)S(1)}, bf16[584,256]{1,0:T(8,128)(2,1)S(1)}, u32[]{:S(2)}, u32[]{:S(2)}) %collective-permute-start.23) | collective-permute-done | bytes 299040 | tf_op jit(solution)/shard_map/ppermute | solution.py:659
  59.6 1.5 %collective-permute-start.27 = (bf16[152,256]{1,0:T(8,128)(2,1)S(1)}, bf16[152,256]{1,0:T(8,128)(2,1)S(1)}, u32[]{:S(2)}, u32[]{:S(2)}) collective-permute-start(bf16[152,256]{1,0:T(8,128)(2,1)S(1)} %get-tuple-element.151), channel_id=1, source_target_pairs={{0,4},{2,6},{4,0},{6,2},{8,12},{10,14},{12,8},{14,10},{1,5},{3,7},... | collective-permute-start | bytes 233480 | tf_op jit(solution)/shard_map/ppermute | solution.py:662
  61.1 3.2 %collective-permute-start.28 = (bf16[152,256]{1,0:T(8,128)(2,1)S(1)}, bf16[152,256]{1,0:T(8,128)(2,1)S(1)}, u32[]{:S(2)}, u32[]{:S(2)}) collective-permute-start(bf16[152,256]{1,0:T(8,128)(2,1)S(1)} %get-tuple-element.152), channel_id=1, source_target_pairs={{0,8},{2,10},{4,12},{6,14},{8,0},{10,2},{12,4},{14,6},{1,9},{3,11}... | collective-permute-start | bytes 233480 | tf_op jit(solution)/shard_map/ppermute | solution.py:662
  64.3 1.5 %collective-permute-start.25 = (bf16[144,256]{1,0:T(8,128)(2,1)S(1)}, bf16[144,256]{1,0:T(8,128)(2,1)S(1)}, u32[]{:S(2)}, u32[]{:S(2)}) collective-permute-start(bf16[144,256]{1,0:T(8,128)(2,1)S(1)} %get-tuple-element.145), channel_id=1, source_target_pairs={{0,8},{2,10},{4,12},{6,14},{8,0},{10,2},{12,4},{14,6},{1,9},{3,11}... | collective-permute-start | bytes 221192 | tf_op jit(solution)/shard_map/ppermute | solution.py:662
  65.9 2.3 %collective-permute-start.26 = (bf16[144,256]{1,0:T(8,128)(2,1)S(1)}, bf16[144,256]{1,0:T(8,128)(2,1)S(1)}, u32[]{:S(2)}, u32[]{:S(2)}) collective-permute-start(bf16[144,256]{1,0:T(8,128)(2,1)S(1)} %get-tuple-element.146), channel_id=1, source_target_pairs={{0,12},{2,14},{4,8},{6,10},{8,4},{10,6},{12,0},{14,2},{1,13},{3,15... | collective-permute-start | bytes 221192 | tf_op jit(solution)/shard_map/ppermute | solution.py:662
  68.2 8.9 %collective-permute-done.25.refs_1_ = bf16[144,256]{1,0:T(8,128)(2,1)S(1)} collective-permute-done((bf16[144,256]{1,0:T(8,128)(2,1)S(1)}, bf16[144,256]{1,0:T(8,128)(2,1)S(1)}, u32[]{:S(2)}, u32[]{:S(2)}) %collective-permute-start.25) | collective-permute-done | bytes 73760 | tf_op jit(solution)/shard_map/ppermute | solution.py:662
  77.0 1.8 %collective-permute-start.34 = (bf16[2,2,192,256]{3,2,1,0:T(8,128)(2,1)S(1)}, bf16[2,2,192,256]{3,2,1,0:T(8,128)(2,1)S(1)}, u32[]{:S(2)}, u32[]{:S(2)}) collective-permute-start(bf16[2,2,192,256]{3,2,1,0:T(8,128)(2,1)S(1)} %get-tuple-element.162), channel_id=1, source_target_pairs={{0,2},{2,0},{4,6},{6,4},{8,10},{10,8},{12,14},{14,12},{1,15},{3,5}... | collective-permute-start | bytes 1179656 | tf_op jit(solution)/shard_map/ppermute | solution.py:610
  78.9 3.0 %collective-permute-start.43 = (bf16[144,256]{1,0:T(8,128)(2,1)S(1)}, bf16[144,256]{1,0:T(8,128)(2,1)S(1)}, u32[]{:S(2)}, u32[]{:S(2)}) collective-permute-start(bf16[144,256]{1,0:T(8,128)(2,1)S(1)} %shard_map.113), channel_id=1, source_target_pairs={{0,12},{2,14},{4,8},{6,10},{8,4},{10,6},{12,0},{14,2},{1,13},{3,15... | collective-permute-start | bytes 221192 | tf_op jit(solution)/shard_map/ppermute | solution.py:662
  81.9 1.5 %collective-permute-start.41 = (bf16[144,256]{1,0:T(8,128)(2,1)S(1)}, bf16[144,256]{1,0:T(8,128)(2,1)S(1)}, u32[]{:S(2)}, u32[]{:S(2)}) collective-permute-start(bf16[144,256]{1,0:T(8,128)(2,1)S(1)} %shard_map.113), channel_id=1, source_target_pairs={{0,4},{2,6},{4,0},{6,2},{8,12},{10,14},{12,8},{14,10},{1,5},{3,7},... | collective-permute-start | bytes 221192 | tf_op jit(solution)/shard_map/ppermute | solution.py:662
  83.4 3.0 %collective-permute-start.32 = (bf16[144,256]{1,0:T(8,128)(2,1)S(1)}, bf16[144,256]{1,0:T(8,128)(2,1)S(1)}, u32[]{:S(2)}, u32[]{:S(2)}) collective-permute-start(bf16[144,256]{1,0:T(8,128)(2,1)S(1)} %get-tuple-element.158), channel_id=1, source_target_pairs={{0,12},{2,14},{4,8},{6,10},{8,4},{10,6},{12,0},{14,2},{1,13},{3,15... | collective-permute-start | bytes 221192 | tf_op jit(solution)/shard_map/ppermute | solution.py:662
  86.4 4.2 %collective-permute-start.31 = (bf16[144,256]{1,0:T(8,128)(2,1)S(1)}, bf16[144,256]{1,0:T(8,128)(2,1)S(1)}, u32[]{:S(2)}, u32[]{:S(2)}) collective-permute-start(bf16[144,256]{1,0:T(8,128)(2,1)S(1)} %get-tuple-element.158), channel_id=1, source_target_pairs={{0,8},{2,10},{4,12},{6,14},{8,0},{10,2},{12,4},{14,6},{1,9},{3,11}... | collective-permute-start | bytes 221192 | tf_op jit(solution)/shard_map/ppermute | solution.py:662
  90.5 0.3 collective-permute-done.42
  90.9 4.0 %collective-permute-start.30 = (bf16[144,256]{1,0:T(8,128)(2,1)S(1)}, bf16[144,256]{1,0:T(8,128)(2,1)S(1)}, u32[]{:S(2)}, u32[]{:S(2)}) collective-permute-start(bf16[144,256]{1,0:T(8,128)(2,1)S(1)} %get-tuple-element.158), channel_id=1, source_target_pairs={{0,4},{2,6},{4,0},{6,2},{8,12},{10,14},{12,8},{14,10},{1,5},{3,7},... | collective-permute-start | bytes 221192 | tf_op jit(solution)/shard_map/ppermute | solution.py:662
  94.9 0.6 collective-permute-start.44
  95.5 2.9 %collective-permute-done.30 = bf16[144,256]{1,0:T(8,128)(2,1)S(1)} collective-permute-done((bf16[144,256]{1,0:T(8,128)(2,1)S(1)}, bf16[144,256]{1,0:T(8,128)(2,1)S(1)}, u32[]{:S(2)}, u32[]{:S(2)}) %collective-permute-start.30) | collective-permute-done | bytes 73760 | tf_op jit(solution)/shard_map/ppermute | solution.py:662
  98.4 0.2 collective-permute-start.35
  98.6 2.2 %collective-permute-start.33 = (bf16[576,256]{1,0:T(8,128)(2,1)S(1)}, bf16[576,256]{1,0:T(8,128)(2,1)S(1)}, u32[]{:S(2)}, u32[]{:S(2)}) collective-permute-start(bf16[576,256]{1,0:T(8,128)(2,1)S(1)} %constant_dynamic-update-slice_fusion.refs_0_), channel_id=1, source_target_pairs={{0,2},{2,0},{4,6},{6,4},{8,10},{10,8},{12,14},{14,12},{1,3},{3,1},... | collective-permute-start | bytes 884744 | tf_op jit(solution)/shard_map/ppermute | solution.py:659
  100.8 0.2 collective-permute-start.36
  101.0 0.3 collective-permute-start.37
  101.3 0.8 collective-permute-done.36.refs_3_
  102.1 0.2 collective-permute-start.38
  102.3 0.3 collective-permute-start.45
  102.6 1.7 %collective-permute-done.44.refs_1_ = bf16[576,256]{1,0:T(8,128)(2,1)S(1)} collective-permute-done((bf16[576,256]{1,0:T(8,128)(2,1)S(1)}, bf16[576,256]{1,0:T(8,128)(2,1)S(1)}, u32[]{:S(2)}, u32[]{:S(2)}) %collective-permute-start.44) | collective-permute-done | bytes 294944 | tf_op jit(solution)/shard_map/ppermute | solution.py:659
  104.3 5.6 %shard_map.111 = (bf16[18,24,256]{2,1,0:T(8,128)(2,1)}, f32[18,24,256]{2,1,0:T(8,128)}) custom-call(s32[6,4]{1,0:T(8,128)S(1)} %copy.12.ep, bf16[18,24,256]{2,1,0:T(8,128)(2,1)S(1)} %bitcast.20, bf16[18,24,256]{2,1,0:T(8,128)(2,1)S(1)} %bitcast.23, bf16[18,24,256]{2,1,0:T(8,128)(2,1)S(1)} %get-tuple-element.159.hid_ref, ...), custom_call_target="tpu_custom_call" | custom-call | tf_op jit(solution)/shard_map/pallas_call | solution.py:566
  110.0 0.5 collective-permute-start.40
  110.5 1.8 %shard_map.114 = f32[9,256,256]{2,1,0:T(8,128)} custom-call(bf16[576,256]{1,0:T(8,128)(2,1)S(1)} %pad_maximum_fusion.refs_0_, bf16[576,256]{1,0:T(8,128)(2,1)S(1)} %collective-permute-done.44.refs_1_, bf16[576,256]{1,0:T(8,128)(2,1)S(1)} %collective-permute-done.45.refs_2_, bf16[576,256]{1,0:T(8,128)(2,1)S(1)} %collective-permute-done.46.refs_3_), custom_call_target="tpu_custom_call" | custom-call | tf_op jit(solution)/shard_map/pallas_call | solution.py:566
  112.3 1.8 %shard_map.112 = (f32[9,256,256]{2,1,0:T(8,128)}, f32[1,256]{1,0:T(1,128)}) custom-call(bf16[576,256]{1,0:T(8,128)(2,1)S(1)} %constant_dynamic-update-slice_fusion.refs_0_, bf16[576,256]{1,0:T(8,128)(2,1)S(1)} %collective-permute-done.33.refs_1_, bf16[576,256]{1,0:T(8,128)(2,1)S(1)} %collective-permute-done.39.refs_2_, ...), custom_call_target="tpu_custom_call" | custom-call | tf_op jit(solution)/shard_map/pallas_call | solution.py:566
  (66 shorter events, 1.4 us)
Async XLA Ops:
  1.4 0.9 copy-start.2
  2.3 0.9 copy-start.4
  5.4 2.3 %collective-permute-start = (bf16[2,192,256]{2,1,0:T(8,128)(2,1)S(1)}, bf16[2,192,256]{2,1,0:T(8,128)(2,1)S(1)}, u32[]{:S(2)}, u32[]{:S(2)}) collective-permute-start(bf16[2,192,256]{2,1,0:T(8,128)(2,1)S(1)} %get-tuple-element.101), channel_id=1, source_target_pairs={{0,1},{1,0},{2,3},{3,2},{4,5},{5,4},{6,7},{7,6},{8,9},{9,8},{10,11... | collective-permute-start | bytes 589832 | tf_op jit(solution)/shard_map/ppermute | solution.py:580
  6.0 1.2 %collective-permute-start.1 = (bf16[2,48,256]{2,1,0:T(8,128)(2,1)S(1)}, bf16[2,48,256]{2,1,0:T(8,128)(2,1)S(1)}, u32[]{:S(2)}, u32[]{:S(2)}) collective-permute-start(bf16[2,48,256]{2,1,0:T(8,128)(2,1)S(1)} %get-tuple-element.102), channel_id=1, source_target_pairs={{0,1},{1,0},{2,3},{3,2},{4,5},{5,4},{6,7},{7,6},{8,9},{9,8},{10,11... | collective-permute-start | bytes 147464 | tf_op jit(solution)/shard_map/ppermute | solution.py:580
  6.0 1.3 %collective-permute-start.2 = (bf16[2,48,256]{2,1,0:T(8,128)(2,1)S(1)}, bf16[2,48,256]{2,1,0:T(8,128)(2,1)S(1)}, u32[]{:S(2)}, u32[]{:S(2)}) collective-permute-start(bf16[2,48,256]{2,1,0:T(8,128)(2,1)S(1)} %get-tuple-element.103), channel_id=1, source_target_pairs={{0,1},{1,0},{2,3},{3,2},{4,5},{5,4},{6,7},{7,6},{8,9},{9,8},{10,11... | collective-permute-start | bytes 147464 | tf_op jit(solution)/shard_map/ppermute | solution.py:580
  6.5 1.2 %collective-permute-start.3 = (bf16[2,48,256]{2,1,0:T(8,128)(2,1)S(1)}, bf16[2,48,256]{2,1,0:T(8,128)(2,1)S(1)}, u32[]{:S(2)}, u32[]{:S(2)}) collective-permute-start(bf16[2,48,256]{2,1,0:T(8,128)(2,1)S(1)} %get-tuple-element.104), channel_id=1, source_target_pairs={{0,1},{1,0},{2,3},{3,2},{4,5},{5,4},{6,7},{7,6},{8,9},{9,8},{10,11... | collective-permute-start | bytes 147464 | tf_op jit(solution)/shard_map/ppermute | solution.py:580
  7.7 13.9 %collective-permute-start.4 = (bf16[2,2,192,256]{3,2,1,0:T(8,128)(2,1)S(1)}, bf16[2,2,192,256]{3,2,1,0:T(8,128)(2,1)S(1)}, u32[]{:S(2)}, u32[]{:S(2)}) collective-permute-start(bf16[2,2,192,256]{3,2,1,0:T(8,128)(2,1)S(1)} %get-tuple-element.105), channel_id=1, source_target_pairs={{0,2},{2,0},{4,6},{6,4},{8,10},{10,8},{12,14},{14,12},{1,15},{3,5}... | collective-permute-start | bytes 1179656 | tf_op jit(solution)/shard_map/ppermute | solution.py:610
  10.5 8.2 %collective-permute-start.5 = (bf16[2,2,48,256]{3,2,1,0:T(8,128)(2,1)S(1)}, bf16[2,2,48,256]{3,2,1,0:T(8,128)(2,1)S(1)}, u32[]{:S(2)}, u32[]{:S(2)}) collective-permute-start(bf16[2,2,48,256]{3,2,1,0:T(8,128)(2,1)S(1)} %get-tuple-element.106), channel_id=1, source_target_pairs={{0,4},{4,0},{10,14},{14,10},{1,9},{3,11},{5,13},{7,15},{9,1},{11,3... | collective-permute-start | bytes 294920 | tf_op jit(solution)/shard_map/ppermute | solution.py:610
  14.0 7.7 %collective-permute-start.6 = (bf16[2,2,48,256]{3,2,1,0:T(8,128)(2,1)S(1)}, bf16[2,2,48,256]{3,2,1,0:T(8,128)(2,1)S(1)}, u32[]{:S(2)}, u32[]{:S(2)}) collective-permute-start(bf16[2,2,48,256]{3,2,1,0:T(8,128)(2,1)S(1)} %get-tuple-element.107), channel_id=1, source_target_pairs={{0,12},{2,14},{4,8},{6,10},{8,4},{10,6},{12,0},{14,2},{1,7},{3,13}... | collective-permute-start | bytes 294920 | tf_op jit(solution)/shard_map/ppermute | solution.py:610
  14.8 6.8 %collective-permute-start.7 = (bf16[2,2,48,256]{3,2,1,0:T(8,128)(2,1)S(1)}, bf16[2,2,48,256]{3,2,1,0:T(8,128)(2,1)S(1)}, u32[]{:S(2)}, u32[]{:S(2)}) collective-permute-start(bf16[2,2,48,256]{3,2,1,0:T(8,128)(2,1)S(1)} %get-tuple-element.108), channel_id=1, source_target_pairs={{1,11},{5,15},{11,1},{15,5},{17,27},{21,31},{27,17},{31,21}} | collective-permute-start | bytes 294920 | tf_op jit(solution)/shard_map/ppermute | solution.py:610
  15.5 1.3 %copy-start = (bf16[3,3,256,256]{3,2,1,0:T(8,128)(2,1)S(1)}, bf16[3,3,256,256]{3,2,1,0:T(8,128)(2,1)}, u32[]{:S(2)}) copy-start(bf16[3,3,256,256]{3,2,1,0:T(8,128)(2,1)} %param.10) | copy-start | bytes 3538948
  16.8 1.3 %copy-start.6 = (bf16[3,3,256,256]{3,2,1,0:T(8,128)(2,1)S(1)}, bf16[3,3,256,256]{3,2,1,0:T(8,128)(2,1)}, u32[]{:S(2)}) copy-start(bf16[3,3,256,256]{3,2,1,0:T(8,128)(2,1)} %param.8) | copy-start | bytes 3538948
  18.0 9.9 %copy-start.3 = (bf16[1,6,3,24,256]{4,3,2,1,0:T(8,128)(2,1)S(1)}, bf16[1,6,3,24,256]{4,3,2,1,0:T(8,128)(2,1)}, u32[]{:S(2)}) copy-start(bf16[1,6,3,24,256]{4,3,2,1,0:T(8,128)(2,1)} %param.6) | copy-start | bytes 663556
  18.0 9.9 %copy-start.5 = (bf16[1,1,6,3,24,256]{5,4,3,2,1,0:T(8,128)(2,1)S(1)}, bf16[1,1,6,3,24,256]{5,4,3,2,1,0:T(8,128)(2,1)}, u32[]{:S(2)}) copy-start(bf16[1,1,6,3,24,256]{5,4,3,2,1,0:T(8,128)(2,1)} %param.7) | copy-start | bytes 663556
  18.0 9.9 %copy-start.7 = (f32[256]{0:T(256)S(1)}, f32[256]{0:T(256)}, u32[]{:S(2)}) copy-start(f32[256]{0:T(256)} %param.9) | copy-start | bytes 3076
  21.7 6.3 %collective-permute-start.8 = (bf16[2,2,192,256]{3,2,1,0:T(8,128)(2,1)S(1)}, bf16[2,2,192,256]{3,2,1,0:T(8,128)(2,1)S(1)}, u32[]{:S(2)}, u32[]{:S(2)}) collective-permute-start(bf16[2,2,192,256]{3,2,1,0:T(8,128)(2,1)S(1)} %collective-permute-done.4.refs_0_), channel_id=1, source_target_pairs={{0,1},{1,0},{2,3},{3,2},{4,5},{5,4},{6,7},{7,6},{8,9},{9,8},{10,11... | collective-permute-start | bytes 1179656 | tf_op jit(solution)/shard_map/ppermute | solution.py:580
  26.1 1.5 %collective-permute-start.9 = (bf16[2,2,48,256]{3,2,1,0:T(8,128)(2,1)S(1)}, bf16[2,2,48,256]{3,2,1,0:T(8,128)(2,1)S(1)}, u32[]{:S(2)}, u32[]{:S(2)}) collective-permute-start(bf16[2,2,48,256]{3,2,1,0:T(8,128)(2,1)S(1)} %collective-permute-done.5.refs_2_), channel_id=1, source_target_pairs={{0,1},{1,0},{2,3},{3,2},{4,5},{5,4},{6,7},{7,6},{8,9},{9,8},{10,11... | collective-permute-start | bytes 294920 | tf_op jit(solution)/shard_map/ppermute | solution.py:580
  26.2 1.6 %collective-permute-start.10 = (bf16[2,2,48,256]{3,2,1,0:T(8,128)(2,1)S(1)}, bf16[2,2,48,256]{3,2,1,0:T(8,128)(2,1)S(1)}, u32[]{:S(2)}, u32[]{:S(2)}) collective-permute-start(bf16[2,2,48,256]{3,2,1,0:T(8,128)(2,1)S(1)} %collective-permute-done.6.refs_4_), channel_id=1, source_target_pairs={{0,1},{1,0},{2,3},{3,2},{4,5},{5,4},{6,7},{7,6},{8,9},{9,8},{10,11... | collective-permute-start | bytes 294920 | tf_op jit(solution)/shard_map/ppermute | solution.py:580
  26.7 1.3 %collective-permute-start.11 = (bf16[2,2,48,256]{3,2,1,0:T(8,128)(2,1)S(1)}, bf16[2,2,48,256]{3,2,1,0:T(8,128)(2,1)S(1)}, u32[]{:S(2)}, u32[]{:S(2)}) collective-permute-start(bf16[2,2,48,256]{3,2,1,0:T(8,128)(2,1)S(1)} %collective-permute-done.7.refs_6_), channel_id=1, source_target_pairs={{0,1},{1,0},{2,3},{3,2},{4,5},{5,4},{6,7},{7,6},{8,9},{9,8},{10,11... | collective-permute-start | bytes 294920 | tf_op jit(solution)/shard_map/ppermute | solution.py:580
  36.3 2.1 %collective-permute-start.14 = (bf16[9,128,256]{2,1,0:T(8,128)(2,1)S(1)}, bf16[9,128,256]{2,1,0:T(8,128)(2,1)S(1)}, u32[]{:S(2)}, u32[]{:S(2)}) collective-permute-start(bf16[9,128,256]{2,1,0:T(8,128)(2,1)S(1)} %get-tuple-element.125), channel_id=1, source_target_pairs={{0,1},{1,0},{2,3},{3,2},{4,5},{5,4},{6,7},{7,6},{8,9},{9,8},{10,11... | collective-permute-start | bytes 1769480 | tf_op jit(solution)/shard_map/ppermute | solution.py:580
  36.7 11.0 %collective-permute-start.12 = (bf16[9,128,256]{2,1,0:T(8,128)(2,1)S(1)}, bf16[9,128,256]{2,1,0:T(8,128)(2,1)S(1)}, u32[]{:S(2)}, u32[]{:S(2)}) collective-permute-start(bf16[9,128,256]{2,1,0:T(8,128)(2,1)S(1)} %get-tuple-element.120), channel_id=1, source_target_pairs={{0,1},{1,0},{2,3},{3,2},{4,5},{5,4},{6,7},{7,6},{8,9},{9,8},{10,11... | collective-permute-start | bytes 1769480 | tf_op jit(solution)/shard_map/ppermute | solution.py:580
  36.8 4.2 %collective-permute-start.16 = (bf16[2,192,256]{2,1,0:T(8,128)(2,1)S(1)}, bf16[2,192,256]{2,1,0:T(8,128)(2,1)S(1)}, u32[]{:S(2)}, u32[]{:S(2)}) collective-permute-start(bf16[2,192,256]{2,1,0:T(8,128)(2,1)S(1)} %get-tuple-element.132), channel_id=1, source_target_pairs={{0,1},{1,0},{2,3},{3,2},{4,5},{5,4},{6,7},{7,6},{8,9},{9,8},{10,11... | collective-permute-start | bytes 589832 | tf_op jit(solution)/shard_map/ppermute | solution.py:580
  38.5 13.0 %collective-permute-start.15 = (bf16[576,256]{1,0:T(8,128)(2,1)S(1)}, bf16[576,256]{1,0:T(8,128)(2,1)S(1)}, u32[]{:S(2)}, u32[]{:S(2)}) collective-permute-start(bf16[576,256]{1,0:T(8,128)(2,1)S(1)} %get-tuple-element.126), channel_id=1, source_target_pairs={{0,2},{2,0},{4,6},{6,4},{8,10},{10,8},{12,14},{14,12},{1,3},{3,1},... | collective-permute-start | bytes 884744 | tf_op jit(solution)/shard_map/ppermute | solution.py:659
  38.6 1.3 %collective-permute-start.17 = (bf16[2,48,256]{2,1,0:T(8,128)(2,1)S(1)}, bf16[2,48,256]{2,1,0:T(8,128)(2,1)S(1)}, u32[]{:S(2)}, u32[]{:S(2)}) collective-permute-start(bf16[2,48,256]{2,1,0:T(8,128)(2,1)S(1)} %get-tuple-element.133), channel_id=1, source_target_pairs={{0,1},{1,0},{2,3},{3,2},{4,5},{5,4},{6,7},{7,6},{8,9},{9,8},{10,11... | collective-permute-start | bytes 147464 | tf_op jit(solution)/shard_map/ppermute | solution.py:580
  38.9 1.2 %collective-permute-start.18 = (bf16[2,48,256]{2,1,0:T(8,128)(2,1)S(1)}, bf16[2,48,256]{2,1,0:T(8,128)(2,1)S(1)}, u32[]{:S(2)}, u32[]{:S(2)}) collective-permute-start(bf16[2,48,256]{2,1,0:T(8,128)(2,1)S(1)} %get-tuple-element.134), channel_id=1, source_target_pairs={{0,1},{1,0},{2,3},{3,2},{4,5},{5,4},{6,7},{7,6},{8,9},{9,8},{10,11... | collective-permute-start | bytes 147464 | tf_op jit(solution)/shard_map/ppermute | solution.py:580
  39.8 1.2 %collective-permute-start.19 = (bf16[2,48,256]{2,1,0:T(8,128)(2,1)S(1)}, bf16[2,48,256]{2,1,0:T(8,128)(2,1)S(1)}, u32[]{:S(2)}, u32[]{:S(2)}) collective-permute-start(bf16[2,48,256]{2,1,0:T(8,128)(2,1)S(1)} %get-tuple-element.135), channel_id=1, source_target_pairs={{0,1},{1,0},{2,3},{3,2},{4,5},{5,4},{6,7},{7,6},{8,9},{9,8},{10,11... | collective-permute-start | bytes 147464 | tf_op jit(solution)/shard_map/ppermute | solution.py:580
  40.2 6.6 %collective-permute-start.13 = (bf16[8,256]{1,0:T(8,128)(2,1)S(1)}, bf16[8,256]{1,0:T(8,128)(2,1)S(1)}, u32[]{:S(2)}, u32[]{:S(2)}) collective-permute-start(bf16[8,256]{1,0:T(8,128)(2,1)S(1)} %get-tuple-element.122), channel_id=1, source_target_pairs={{0,1},{1,0},{2,3},{3,2},{4,5},{5,4},{6,7},{7,6},{8,9},{9,8},{10,11... | collective-permute-start | bytes 12296 | tf_op jit(solution)/shard_map/ppermute | solution.py:580
  41.1 7.6 %collective-permute-start.20 = (bf16[2,2,48,256]{3,2,1,0:T(8,128)(2,1)S(1)}, bf16[2,2,48,256]{3,2,1,0:T(8,128)(2,1)S(1)}, u32[]{:S(2)}, u32[]{:S(2)}) collective-permute-start(bf16[2,2,48,256]{3,2,1,0:T(8,128)(2,1)S(1)} %get-tuple-element.136), channel_id=1, source_target_pairs={{0,4},{4,0},{10,14},{14,10},{1,9},{3,11},{5,13},{7,15},{9,1},{11,3... | collective-permute-start | bytes 294920 | tf_op jit(solution)/shard_map/ppermute | solution.py:610
  44.0 7.5 %collective-permute-start.21 = (bf16[2,2,48,256]{3,2,1,0:T(8,128)(2,1)S(1)}, bf16[2,2,48,256]{3,2,1,0:T(8,128)(2,1)S(1)}, u32[]{:S(2)}, u32[]{:S(2)}) collective-permute-start(bf16[2,2,48,256]{3,2,1,0:T(8,128)(2,1)S(1)} %get-tuple-element.137), channel_id=1, source_target_pairs={{0,12},{2,14},{4,8},{6,10},{8,4},{10,6},{12,0},{14,2},{1,7},{3,13}... | collective-permute-start | bytes 294920 | tf_op jit(solution)/shard_map/ppermute | solution.py:610
  46.8 4.7 %collective-permute-start.22 = (bf16[2,2,48,256]{3,2,1,0:T(8,128)(2,1)S(1)}, bf16[2,2,48,256]{3,2,1,0:T(8,128)(2,1)S(1)}, u32[]{:S(2)}, u32[]{:S(2)}) collective-permute-start(bf16[2,2,48,256]{3,2,1,0:T(8,128)(2,1)S(1)} %get-tuple-element.138), channel_id=1, source_target_pairs={{1,11},{5,15},{11,1},{15,5},{17,27},{21,31},{27,17},{31,21}} | collective-permute-start | bytes 294920 | tf_op jit(solution)/shard_map/ppermute | solution.py:610
  51.5 8.0 %collective-permute-start.23 = (bf16[584,256]{1,0:T(8,128)(2,1)S(1)}, bf16[584,256]{1,0:T(8,128)(2,1)S(1)}, u32[]{:S(2)}, u32[]{:S(2)}) collective-permute-start(bf16[584,256]{1,0:T(8,128)(2,1)S(1)} %get-tuple-element.139), channel_id=1, source_target_pairs={{0,2},{2,0},{4,6},{6,4},{8,10},{10,8},{12,14},{14,12},{1,3},{3,1},... | collective-permute-start | bytes 897032 | tf_op jit(solution)/shard_map/ppermute | solution.py:659
  53.6 12.2 %collective-permute-start.24 = (bf16[144,256]{1,0:T(8,128)(2,1)S(1)}, bf16[144,256]{1,0:T(8,128)(2,1)S(1)}, u32[]{:S(2)}, u32[]{:S(2)}) collective-permute-start(bf16[144,256]{1,0:T(8,128)(2,1)S(1)} %get-tuple-element.144), channel_id=1, source_target_pairs={{0,4},{2,6},{4,0},{6,2},{8,12},{10,14},{12,8},{14,10},{1,5},{3,7},... | collective-permute-start | bytes 221192 | tf_op jit(solution)/shard_map/ppermute | solution.py:662
  59.6 44.7 %copy-start.1 = (bf16[3,3,256,256]{3,2,1,0:T(8,128)(2,1)S(1)}, bf16[3,3,256,256]{3,2,1,0:T(8,128)(2,1)}, u32[]{:S(2)}) copy-start(bf16[3,3,256,256]{3,2,1,0:T(8,128)(2,1)} %param.10) | copy-start | bytes 3538948
  59.6 19.2 %collective-permute-start.27 = (bf16[152,256]{1,0:T(8,128)(2,1)S(1)}, bf16[152,256]{1,0:T(8,128)(2,1)S(1)}, u32[]{:S(2)}, u32[]{:S(2)}) collective-permute-start(bf16[152,256]{1,0:T(8,128)(2,1)S(1)} %get-tuple-element.151), channel_id=1, source_target_pairs={{0,4},{2,6},{4,0},{6,2},{8,12},{10,14},{12,8},{14,10},{1,5},{3,7},... | collective-permute-start | bytes 233480 | tf_op jit(solution)/shard_map/ppermute | solution.py:662
  61.1 17.7 %collective-permute-start.28 = (bf16[152,256]{1,0:T(8,128)(2,1)S(1)}, bf16[152,256]{1,0:T(8,128)(2,1)S(1)}, u32[]{:S(2)}, u32[]{:S(2)}) collective-permute-start(bf16[152,256]{1,0:T(8,128)(2,1)S(1)} %get-tuple-element.152), channel_id=1, source_target_pairs={{0,8},{2,10},{4,12},{6,14},{8,0},{10,2},{12,4},{14,6},{1,9},{3,11}... | collective-permute-start | bytes 233480 | tf_op jit(solution)/shard_map/ppermute | solution.py:662
  64.3 14.5 %collective-permute-start.29 = (bf16[152,256]{1,0:T(8,128)(2,1)S(1)}, bf16[152,256]{1,0:T(8,128)(2,1)S(1)}, u32[]{:S(2)}, u32[]{:S(2)}) collective-permute-start(bf16[152,256]{1,0:T(8,128)(2,1)S(1)} %get-tuple-element.153), channel_id=1, source_target_pairs={{0,12},{2,14},{4,8},{6,10},{8,4},{10,6},{12,0},{14,2},{1,13},{3,15... | collective-permute-start | bytes 233480 | tf_op jit(solution)/shard_map/ppermute | solution.py:662
  64.3 12.7 %collective-permute-start.25 = (bf16[144,256]{1,0:T(8,128)(2,1)S(1)}, bf16[144,256]{1,0:T(8,128)(2,1)S(1)}, u32[]{:S(2)}, u32[]{:S(2)}) collective-permute-start(bf16[144,256]{1,0:T(8,128)(2,1)S(1)} %get-tuple-element.145), channel_id=1, source_target_pairs={{0,8},{2,10},{4,12},{6,14},{8,0},{10,2},{12,4},{14,6},{1,9},{3,11}... | collective-permute-start | bytes 221192 | tf_op jit(solution)/shard_map/ppermute | solution.py:662
  65.9 13.0 %collective-permute-start.26 = (bf16[144,256]{1,0:T(8,128)(2,1)S(1)}, bf16[144,256]{1,0:T(8,128)(2,1)S(1)}, u32[]{:S(2)}, u32[]{:S(2)}) collective-permute-start(bf16[144,256]{1,0:T(8,128)(2,1)S(1)} %get-tuple-element.146), channel_id=1, source_target_pairs={{0,12},{2,14},{4,8},{6,10},{8,4},{10,6},{12,0},{14,2},{1,13},{3,15... | collective-permute-start | bytes 221192 | tf_op jit(solution)/shard_map/ppermute | solution.py:662
  77.0 21.4 %collective-permute-start.34 = (bf16[2,2,192,256]{3,2,1,0:T(8,128)(2,1)S(1)}, bf16[2,2,192,256]{3,2,1,0:T(8,128)(2,1)S(1)}, u32[]{:S(2)}, u32[]{:S(2)}) collective-permute-start(bf16[2,2,192,256]{3,2,1,0:T(8,128)(2,1)S(1)} %get-tuple-element.162), channel_id=1, source_target_pairs={{0,2},{2,0},{4,6},{6,4},{8,10},{10,8},{12,14},{14,12},{1,15},{3,5}... | collective-permute-start | bytes 1179656 | tf_op jit(solution)/shard_map/ppermute | solution.py:610
  78.9 7.5 %collective-permute-start.43 = (bf16[144,256]{1,0:T(8,128)(2,1)S(1)}, bf16[144,256]{1,0:T(8,128)(2,1)S(1)}, u32[]{:S(2)}, u32[]{:S(2)}) collective-permute-start(bf16[144,256]{1,0:T(8,128)(2,1)S(1)} %shard_map.113), channel_id=1, source_target_pairs={{0,12},{2,14},{4,8},{6,10},{8,4},{10,6},{12,0},{14,2},{1,13},{3,15... | collective-permute-start | bytes 221192 | tf_op jit(solution)/shard_map/ppermute | solution.py:662
  81.9 9.0 %collective-permute-start.42 = (bf16[144,256]{1,0:T(8,128)(2,1)S(1)}, bf16[144,256]{1,0:T(8,128)(2,1)S(1)}, u32[]{:S(2)}, u32[]{:S(2)}) collective-permute-start(bf16[144,256]{1,0:T(8,128)(2,1)S(1)} %shard_map.113), channel_id=1, source_target_pairs={{0,8},{2,10},{4,12},{6,14},{8,0},{10,2},{12,4},{14,6},{1,9},{3,11}... | collective-permute-start | bytes 221192 | tf_op jit(solution)/shard_map/ppermute | solution.py:662
  81.9 13.0 %collective-permute-start.41 = (bf16[144,256]{1,0:T(8,128)(2,1)S(1)}, bf16[144,256]{1,0:T(8,128)(2,1)S(1)}, u32[]{:S(2)}, u32[]{:S(2)}) collective-permute-start(bf16[144,256]{1,0:T(8,128)(2,1)S(1)} %shard_map.113), channel_id=1, source_target_pairs={{0,4},{2,6},{4,0},{6,2},{8,12},{10,14},{12,8},{14,10},{1,5},{3,7},... | collective-permute-start | bytes 221192 | tf_op jit(solution)/shard_map/ppermute | solution.py:662
  83.4 15.2 %collective-permute-start.32 = (bf16[144,256]{1,0:T(8,128)(2,1)S(1)}, bf16[144,256]{1,0:T(8,128)(2,1)S(1)}, u32[]{:S(2)}, u32[]{:S(2)}) collective-permute-start(bf16[144,256]{1,0:T(8,128)(2,1)S(1)} %get-tuple-element.158), channel_id=1, source_target_pairs={{0,12},{2,14},{4,8},{6,10},{8,4},{10,6},{12,0},{14,2},{1,13},{3,15... | collective-permute-start | bytes 221192 | tf_op jit(solution)/shard_map/ppermute | solution.py:662
  86.4 12.0 %collective-permute-start.31 = (bf16[144,256]{1,0:T(8,128)(2,1)S(1)}, bf16[144,256]{1,0:T(8,128)(2,1)S(1)}, u32[]{:S(2)}, u32[]{:S(2)}) collective-permute-start(bf16[144,256]{1,0:T(8,128)(2,1)S(1)} %get-tuple-element.158), channel_id=1, source_target_pairs={{0,8},{2,10},{4,12},{6,14},{8,0},{10,2},{12,4},{14,6},{1,9},{3,11}... | collective-permute-start | bytes 221192 | tf_op jit(solution)/shard_map/ppermute | solution.py:662
  90.9 7.5 %collective-permute-start.30 = (bf16[144,256]{1,0:T(8,128)(2,1)S(1)}, bf16[144,256]{1,0:T(8,128)(2,1)S(1)}, u32[]{:S(2)}, u32[]{:S(2)}) collective-permute-start(bf16[144,256]{1,0:T(8,128)(2,1)S(1)} %get-tuple-element.158), channel_id=1, source_target_pairs={{0,4},{2,6},{4,0},{6,2},{8,12},{10,14},{12,8},{14,10},{1,5},{3,7},... | collective-permute-start | bytes 221192 | tf_op jit(solution)/shard_map/ppermute | solution.py:662
  94.9 9.4 %collective-permute-start.44 = (bf16[576,256]{1,0:T(8,128)(2,1)S(1)}, bf16[576,256]{1,0:T(8,128)(2,1)S(1)}, u32[]{:S(2)}, u32[]{:S(2)}) collective-permute-start(bf16[576,256]{1,0:T(8,128)(2,1)S(1)} %pad_maximum_fusion.refs_0_), channel_id=1, source_target_pairs={{0,2},{2,0},{4,6},{6,4},{8,10},{10,8},{12,14},{14,12},{1,3},{3,1},... | collective-permute-start | bytes 884744 | tf_op jit(solution)/shard_map/ppermute | solution.py:659
  98.4 5.9 %collective-permute-start.35 = (bf16[2,2,192,256]{3,2,1,0:T(8,128)(2,1)S(1)}, bf16[2,2,192,256]{3,2,1,0:T(8,128)(2,1)S(1)}, u32[]{:S(2)}, u32[]{:S(2)}) collective-permute-start(bf16[2,2,192,256]{3,2,1,0:T(8,128)(2,1)S(1)} %collective-permute-done.34.refs_0_), channel_id=1, source_target_pairs={{0,1},{1,0},{2,3},{3,2},{4,5},{5,4},{6,7},{7,6},{8,9},{9,8},{10,11... | collective-permute-start | bytes 1179656 | tf_op jit(solution)/shard_map/ppermute | solution.py:580
  98.6 11.4 %collective-permute-start.33 = (bf16[576,256]{1,0:T(8,128)(2,1)S(1)}, bf16[576,256]{1,0:T(8,128)(2,1)S(1)}, u32[]{:S(2)}, u32[]{:S(2)}) collective-permute-start(bf16[576,256]{1,0:T(8,128)(2,1)S(1)} %constant_dynamic-update-slice_fusion.refs_0_), channel_id=1, source_target_pairs={{0,2},{2,0},{4,6},{6,4},{8,10},{10,8},{12,14},{14,12},{1,3},{3,1},... | collective-permute-start | bytes 884744 | tf_op jit(solution)/shard_map/ppermute | solution.py:659
  100.8 1.3 %collective-permute-start.36 = (bf16[2,2,48,256]{3,2,1,0:T(8,128)(2,1)S(1)}, bf16[2,2,48,256]{3,2,1,0:T(8,128)(2,1)S(1)}, u32[]{:S(2)}, u32[]{:S(2)}) collective-permute-start(bf16[2,2,48,256]{3,2,1,0:T(8,128)(2,1)S(1)} %collective-permute-done.20.refs_2_), channel_id=1, source_target_pairs={{0,1},{1,0},{2,3},{3,2},{4,5},{5,4},{6,7},{7,6},{8,9},{9,8},{10,11... | collective-permute-start | bytes 294920 | tf_op jit(solution)/shard_map/ppermute | solution.py:580
  101.0 1.3 %collective-permute-start.37 = (bf16[2,2,48,256]{3,2,1,0:T(8,128)(2,1)S(1)}, bf16[2,2,48,256]{3,2,1,0:T(8,128)(2,1)S(1)}, u32[]{:S(2)}, u32[]{:S(2)}) collective-permute-start(bf16[2,2,48,256]{3,2,1,0:T(8,128)(2,1)S(1)} %collective-permute-done.21.refs_4_), channel_id=1, source_target_pairs={{0,1},{1,0},{2,3},{3,2},{4,5},{5,4},{6,7},{7,6},{8,9},{9,8},{10,11... | collective-permute-start | bytes 294920 | tf_op jit(solution)/shard_map/ppermute | solution.py:580
  102.1 2.2 %collective-permute-start.38 = (bf16[2,2,48,256]{3,2,1,0:T(8,128)(2,1)S(1)}, bf16[2,2,48,256]{3,2,1,0:T(8,128)(2,1)S(1)}, u32[]{:S(2)}, u32[]{:S(2)}) collective-permute-start(bf16[2,2,48,256]{3,2,1,0:T(8,128)(2,1)S(1)} %collective-permute-done.22.refs_6_), channel_id=1, source_target_pairs={{0,1},{1,0},{2,3},{3,2},{4,5},{5,4},{6,7},{7,6},{8,9},{9,8},{10,11... | collective-permute-start | bytes 294920 | tf_op jit(solution)/shard_map/ppermute | solution.py:580
  102.3 8.2 %collective-permute-start.45 = (bf16[576,256]{1,0:T(8,128)(2,1)S(1)}, bf16[576,256]{1,0:T(8,128)(2,1)S(1)}, u32[]{:S(2)}, u32[]{:S(2)}) collective-permute-start(bf16[576,256]{1,0:T(8,128)(2,1)S(1)} %pad_maximum_fusion.refs_0_), channel_id=1, source_target_pairs={{0,1},{1,0},{2,3},{3,2},{4,5},{5,4},{6,7},{7,6},{8,9},{9,8},{10,11... | collective-permute-start | bytes 884744 | tf_op jit(solution)/shard_map/ppermute | solution.py:580
  104.3 6.2 %collective-permute-start.46 = (bf16[576,256]{1,0:T(8,128)(2,1)S(1)}, bf16[576,256]{1,0:T(8,128)(2,1)S(1)}, u32[]{:S(2)}, u32[]{:S(2)}) collective-permute-start(bf16[576,256]{1,0:T(8,128)(2,1)S(1)} %collective-permute-done.44.refs_1_), channel_id=1, source_target_pairs={{0,1},{1,0},{2,3},{3,2},{4,5},{5,4},{6,7},{7,6},{8,9},{9,8},{10,11... | collective-permute-start | bytes 884744 | tf_op jit(solution)/shard_map/ppermute | solution.py:580
  110.0 2.3 %collective-permute-start.40 = (bf16[576,256]{1,0:T(8,128)(2,1)S(1)}, bf16[576,256]{1,0:T(8,128)(2,1)S(1)}, u32[]{:S(2)}, u32[]{:S(2)}) collective-permute-start(bf16[576,256]{1,0:T(8,128)(2,1)S(1)} %collective-permute-done.33.refs_1_), channel_id=1, source_target_pairs={{0,1},{1,0},{2,3},{3,2},{4,5},{5,4},{6,7},{7,6},{8,9},{9,8},{10,11... | collective-permute-start | bytes 884744 | tf_op jit(solution)/shard_map/ppermute | solution.py:580
  110.5 1.8 %collective-permute-start.39 = (bf16[576,256]{1,0:T(8,128)(2,1)S(1)}, bf16[576,256]{1,0:T(8,128)(2,1)S(1)}, u32[]{:S(2)}, u32[]{:S(2)}) collective-permute-start(bf16[576,256]{1,0:T(8,128)(2,1)S(1)} %constant_dynamic-update-slice_fusion.refs_0_), channel_id=1, source_target_pairs={{0,1},{1,0},{2,3},{3,2},{4,5},{5,4},{6,7},{7,6},{8,9},{9,8},{10,11... | collective-permute-start | bytes 884744 | tf_op jit(solution)/shard_map/ppermute | solution.py:580

commit v13 on v12

--- a/solution.py
+++ b/solution.py
@@ -697,28 +697,28 @@
 
     keep2, sends2, _ = sum_y(keep2, recv2)
     recvs2 = [along_z(v, j + 1) for j, v in enumerate(sends2)]
+    recv1, recvs2 = barrier((recv1, recvs2))
 
     keep1, sends1, (bias_sum,) = sum_y(keep1, recv1, bias_sum)
-    sends1, todo = barrier((sends1, [joined[i] for i in middle]))
+    (own2,) = sum_z(keep2, recvs2)
+    sends1, own2, todo = barrier((sends1, own2, [joined[i] for i in middle]))
     recvs1 = [along_z(v, j + 1) for j, v in enumerate(sends1)]
+    own2 = [own2] + [along_z(own2, j) for j in range(1, zcount)]
     got = [across(v, i) for i, v in zip(middle, todo)]
-
-    recvs2, recvs1 = barrier((recvs2, recvs1))
-    (own2,) = sum_z(keep2, recvs2)
-    own2 = [own2] + [along_z(own2, j) for j in range(1, zcount)]
+    recvs1, own2, got = barrier((recvs1, own2, got))
     came.update(zip(middle, got))
 
     own1, bias_sum = sum_z(keep1, recvs1, bias_sum)
     own1 = [own1] + [along_z(own1, j) for j in range(1, zcount)]
     own2 = jnp.concatenate(own2, axis=0)
     other2 = along_y(own2)
-    own1 = jnp.concatenate(own1, axis=0)
-    other1 = along_y(own1)
     messages = []
     for i in steps:
         messages += [came[i], swap_dp(came[i])]
     messages.append(packed[-1])
-    own1, messages = barrier((own1, messages))
+    own1, other2, messages = barrier((own1, other2, messages))
+    own1 = jnp.concatenate(own1, axis=0)
+    other1 = along_y(own1)
     state, grad = call(
         functools.partial(second_kernel, dm),
         [(planes, BF), (planes, F32)],

time: 114 us -> 112 us (0.982)
  waiting for transfers between devices: 32.1 us -> 29 us
    ppermute x4, waiting for transfers between devices: 7.46 us -> 2.36 us  [along_y(): return lax.ppermute(v, 'tile', [(i, i ^ 1) for i in range(tiles)])]
    ppermute x12, waiting for transfers between devices: 12.1 us -> 14.2 us  [along_z(): return lax.ppermute(v, 'tile', [(i, i ^ 2 * j) for i in range(tiles)])]
    ppermute x12, starting transfers between devices: 24.2 us -> 25.9 us  [along_z(): return lax.ppermute(v, 'tile', [(i, i ^ 2 * j) for i in range(tiles)])]
    ppermute x8, starting transfers between devices: 16 us -> 14.3 us  [across(): return lax.ppermute(v, ('tile', 'dp'), pairs[step])]
    unnamed x20 -> x23, local copies, waits for them, and re-layouts: 5.21 us -> 5.23 us
  transfers between devices with their start and end apart: 47 -> 47, of which waited for: 18 -> 21; matrix products, arithmetic and copies ran while one was open for 0% -> 0% of each run, Pallas kernels for 8% -> 8%
where the time goes in v13:
time: 112 us
  starting transfers between devices  55.7 us (50%)
  waiting for transfers between devices  29 us (26%)
  Pallas kernels  20.9 us (19%)
  local copies, waits for them, and re-layouts  5.25 us (5%)
    ppermute x12, starting transfers between devices, along_z(): return lax.ppermute(v, 'tile', [(i, i ^ 2 * j) for i in range(tiles)])  25.9 us
    pallas_call x14, Pallas kernels, run(): pl.pallas_call(kernel, out_shape=[jax.ShapeDtypeStruct(s, dt) for s, dt i...  20.9 us
    ppermute x8, starting transfers between devices, across(): return lax.ppermute(v, ('tile', 'dp'), pairs[step])  14.3 us
    ppermute x12, waiting for transfers between devices, along_z(): return lax.ppermute(v, 'tile', [(i, i ^ 2 * j) for i in range(tiles)])  14.2 us
    ppermute x23, starting transfers between devices, swap_dp(): return lax.ppermute(v, 'dp', [(i, count - 1 - i) for i in range(count)])  9.87 us
    ppermute x8, waiting for transfers between devices, across(): return lax.ppermute(v, ('tile', 'dp'), pairs[step])  6.68 us
    ppermute x23, waiting for transfers between devices, swap_dp(): return lax.ppermute(v, 'dp', [(i, count - 1 - i) for i in range(count)])  5.75 us
    ppermute x4, starting transfers between devices, along_y(): return lax.ppermute(v, 'tile', [(i, i ^ 1) for i in range(tiles)])  5.7 us
  transfers between devices with their start and end apart: 47, of which 21 were waited for; matrix products, arithmetic and copies ran while one was open for 0% of the time, Pallas kernels for 8%

profile of v13, /device:TPU:0, one launch (start us, length us, event | category | flops | bytes accessed | tf_op | source)
XLA Modules:
  0.0 111.8 jit_solution(3559811128049446794)
XLA Ops:
  0.6 0.8 copy.12.ep
  1.4 0.9 copy-done.2
  2.3 0.9 copy-done.4
  3.3 2.2 %shard_map.101 = (bf16[2,192,256]{2,1,0:T(8,128)(2,1)S(1)}, bf16[2,48,256]{2,1,0:T(8,128)(2,1)S(1)}, bf16[2,48,256]{2,1,0:T(8,128)(2,1)S(1)}, bf16[2,48,256]{2,1...) custom-call(s32[6,4]{1,0:T(8,128)S(1)} %copy.12.ep, ...), custom_call_target="tpu_custom_call" | custom-call | tf_op jit(solution)/shard_map/pallas_call | solution.py:566
  5.4 0.5 collective-permute-start
  6.0 0.4 collective-permute-start.2
  6.5 0.6 collective-permute-done.1.refs_5_
  7.3 0.3 collective-permute-done.3.refs_7_
  7.7 2.7 %collective-permute-start.4 = (bf16[2,2,192,256]{3,2,1,0:T(8,128)(2,1)S(1)}, bf16[2,2,192,256]{3,2,1,0:T(8,128)(2,1)S(1)}, u32[]{:S(2)}, u32[]{:S(2)}) collective-permute-start(bf16[2,2,192,256]{3,2,1,0:T(8,128)(2,1)S(1)} %get-tuple-element.116), channel_id=1, source_target_pairs={{0,2},{2,0},{4,6},{6,4},{8,10},{10,8},{12,14},{14,12},{1,15},{3,5}... | collective-permute-start | bytes 1179656 | tf_op jit(solution)/shard_map/ppermute | solution.py:610
  10.5 3.5 %collective-permute-start.5 = (bf16[2,2,48,256]{3,2,1,0:T(8,128)(2,1)S(1)}, bf16[2,2,48,256]{3,2,1,0:T(8,128)(2,1)S(1)}, u32[]{:S(2)}, u32[]{:S(2)}) collective-permute-start(bf16[2,2,48,256]{3,2,1,0:T(8,128)(2,1)S(1)} %get-tuple-element.117), channel_id=1, source_target_pairs={{0,4},{4,0},{10,14},{14,10},{1,9},{3,11},{5,13},{7,15},{9,1},{11,3... | collective-permute-start | bytes 294920 | tf_op jit(solution)/shard_map/ppermute | solution.py:610
  14.0 0.9 collective-permute-start.6
  14.8 0.7 collective-permute-start.7
  15.5 1.3 %copy-done = bf16[3,3,256,256]{3,2,1,0:T(8,128)(2,1)S(1)} copy-done((bf16[3,3,256,256]{3,2,1,0:T(8,128)(2,1)S(1)}, bf16[3,3,256,256]{3,2,1,0:T(8,128)(2,1)}, u32[]{:S(2)}) %copy-start) | copy-done | bytes 1179672
  16.8 1.3 %copy-done.6 = bf16[3,3,256,256]{3,2,1,0:T(8,128)(2,1)S(1)} copy-done((bf16[3,3,256,256]{3,2,1,0:T(8,128)(2,1)S(1)}, bf16[3,3,256,256]{3,2,1,0:T(8,128)(2,1)}, u32[]{:S(2)}) %copy-start.6) | copy-done | bytes 1179672
  18.0 0.7 shard_map.103
  18.7 2.9 %collective-permute-done.6.refs_4_ = bf16[2,2,48,256]{3,2,1,0:T(8,128)(2,1)S(1)} collective-permute-done((bf16[2,2,48,256]{3,2,1,0:T(8,128)(2,1)S(1)}, bf16[2,2,48,256]{3,2,1,0:T(8,128)(2,1)S(1)}, u32[]{:S(2)}, u32[]{:S(2)}) %collective-permute-start.6) | collective-permute-done | bytes 98336 | tf_op jit(solution)/shard_map/ppermute | solution.py:610
  21.7 4.5 %collective-permute-start.8 = (bf16[2,2,192,256]{3,2,1,0:T(8,128)(2,1)S(1)}, bf16[2,2,192,256]{3,2,1,0:T(8,128)(2,1)S(1)}, u32[]{:S(2)}, u32[]{:S(2)}) collective-permute-start(bf16[2,2,192,256]{3,2,1,0:T(8,128)(2,1)S(1)} %collective-permute-done.4.refs_0_), channel_id=1, source_target_pairs={{0,1},{1,0},{2,3},{3,2},{4,5},{5,4},{6,7},{7,6},{8,9},{9,8},{10,11... | collective-permute-start | bytes 1179656 | tf_op jit(solution)/shard_map/ppermute | solution.py:580
  26.2 0.5 collective-permute-start.10
  26.7 1.0 collective-permute-done.9.refs_3_
  27.8 0.2 collective-permute-done.11.refs_7_
  28.0 8.3 %shard_map.104 = (bf16[9,128,256]{2,1,0:T(8,128)(2,1)S(1)}, f32[9,128,256]{2,1,0:T(8,128)S(1)}, bf16[9,128,256]{2,1,0:T(8,128)(2,1)S(1)}, f32[9,128,256]{2,1,0:T...) custom-call(s32[6,4]{1,0:T(8,128)S(1)} %copy.12.ep, ...), custom_call_target="tpu_custom_call" | custom-call | tf_op jit(solution)/shard_map/pallas_call | solution.py:566
  36.3 0.4 collective-permute-start.14
  36.7 0.2 collective-permute-start.12
  36.8 0.3 collective-permute-start.16
  37.2 1.2 %collective-permute-done.14.recv_ref = bf16[9,128,256]{2,1,0:T(8,128)(2,1)S(1)} collective-permute-done((bf16[9,128,256]{2,1,0:T(8,128)(2,1)S(1)}, bf16[9,128,256]{2,1,0:T(8,128)(2,1)S(1)}, u32[]{:S(2)}, u32[]{:S(2)}) %collective-permute-start.14) | collective-permute-done | bytes 589856 | tf_op jit(solution)/shard_map/ppermute | solution.py:580
  38.6 0.4 collective-permute-start.17
  38.9 0.2 collective-permute-start.18
  39.1 0.7 collective-permute-done.17.refs_5_
  39.8 0.3 collective-permute-start.19
  40.2 0.2 collective-permute-start.13
  40.4 0.7 collective-permute-done.19.refs_7_
  41.1 2.8 %collective-permute-start.20 = (bf16[2,2,48,256]{3,2,1,0:T(8,128)(2,1)S(1)}, bf16[2,2,48,256]{3,2,1,0:T(8,128)(2,1)S(1)}, u32[]{:S(2)}, u32[]{:S(2)}) collective-permute-start(bf16[2,2,48,256]{3,2,1,0:T(8,128)(2,1)S(1)} %get-tuple-element.147), channel_id=1, source_target_pairs={{0,4},{4,0},{10,14},{14,10},{1,9},{3,11},{5,13},{7,15},{9,1},{11,3... | collective-permute-start | bytes 294920 | tf_op jit(solution)/shard_map/ppermute | solution.py:610
  44.0 2.8 %collective-permute-start.21 = (bf16[2,2,48,256]{3,2,1,0:T(8,128)(2,1)S(1)}, bf16[2,2,48,256]{3,2,1,0:T(8,128)(2,1)S(1)}, u32[]{:S(2)}, u32[]{:S(2)}) collective-permute-start(bf16[2,2,48,256]{3,2,1,0:T(8,128)(2,1)S(1)} %get-tuple-element.148), channel_id=1, source_target_pairs={{0,12},{2,14},{4,8},{6,10},{8,4},{10,6},{12,0},{14,2},{1,7},{3,13}... | collective-permute-start | bytes 294920 | tf_op jit(solution)/shard_map/ppermute | solution.py:610
  46.8 0.8 collective-permute-start.22
  47.8 0.9 collective-permute-done.20.refs_2_
  48.7 2.8 %collective-permute-done.21.refs_4_ = bf16[2,2,48,256]{3,2,1,0:T(8,128)(2,1)S(1)} collective-permute-done((bf16[2,2,48,256]{3,2,1,0:T(8,128)(2,1)S(1)}, bf16[2,2,48,256]{3,2,1,0:T(8,128)(2,1)S(1)}, u32[]{:S(2)}, u32[]{:S(2)}) %collective-permute-start.21) | collective-permute-done | bytes 98336 | tf_op jit(solution)/shard_map/ppermute | solution.py:610
  51.5 2.0 %collective-permute-start.23 = (bf16[584,256]{1,0:T(8,128)(2,1)S(1)}, bf16[584,256]{1,0:T(8,128)(2,1)S(1)}, u32[]{:S(2)}, u32[]{:S(2)}) collective-permute-start(bf16[584,256]{1,0:T(8,128)(2,1)S(1)} %get-tuple-element.150), channel_id=1, source_target_pairs={{0,2},{2,0},{4,6},{6,4},{8,10},{10,8},{12,14},{14,12},{1,3},{3,1},... | collective-permute-start | bytes 897032 | tf_op jit(solution)/shard_map/ppermute | solution.py:659
  53.7 2.9 %collective-permute-start.25 = (bf16[144,256]{1,0:T(8,128)(2,1)S(1)}, bf16[144,256]{1,0:T(8,128)(2,1)S(1)}, u32[]{:S(2)}, u32[]{:S(2)}) collective-permute-start(bf16[144,256]{1,0:T(8,128)(2,1)S(1)} %get-tuple-element.154), channel_id=1, source_target_pairs={{0,8},{2,10},{4,12},{6,14},{8,0},{10,2},{12,4},{14,6},{1,9},{3,11}... | collective-permute-start | bytes 221192 | tf_op jit(solution)/shard_map/ppermute | solution.py:662
  56.6 1.5 %collective-permute-start.26 = (bf16[144,256]{1,0:T(8,128)(2,1)S(1)}, bf16[144,256]{1,0:T(8,128)(2,1)S(1)}, u32[]{:S(2)}, u32[]{:S(2)}) collective-permute-start(bf16[144,256]{1,0:T(8,128)(2,1)S(1)} %get-tuple-element.155), channel_id=1, source_target_pairs={{0,12},{2,14},{4,8},{6,10},{8,4},{10,6},{12,0},{14,2},{1,13},{3,15... | collective-permute-start | bytes 221192 | tf_op jit(solution)/shard_map/ppermute | solution.py:662
  58.1 0.9 collective-permute-done.25.refs_1_
  59.0 4.3 %collective-permute-done.26.refs_2_ = bf16[144,256]{1,0:T(8,128)(2,1)S(1)} collective-permute-done((bf16[144,256]{1,0:T(8,128)(2,1)S(1)}, bf16[144,256]{1,0:T(8,128)(2,1)S(1)}, u32[]{:S(2)}, u32[]{:S(2)}) %collective-permute-start.26) | collective-permute-done | bytes 73760 | tf_op jit(solution)/shard_map/ppermute | solution.py:662
  63.6 2.3 %collective-permute-start.32 = (bf16[144,256]{1,0:T(8,128)(2,1)S(1)}, bf16[144,256]{1,0:T(8,128)(2,1)S(1)}, u32[]{:S(2)}, u32[]{:S(2)}) collective-permute-start(bf16[144,256]{1,0:T(8,128)(2,1)S(1)} %shard_map.110), channel_id=1, source_target_pairs={{0,12},{2,14},{4,8},{6,10},{8,4},{10,6},{12,0},{14,2},{1,13},{3,15... | collective-permute-start | bytes 221192 | tf_op jit(solution)/shard_map/ppermute | solution.py:662
  65.9 1.0 collective-permute-start.31
  66.9 1.1 %collective-permute-start.27 = (bf16[152,256]{1,0:T(8,128)(2,1)S(1)}, bf16[152,256]{1,0:T(8,128)(2,1)S(1)}, u32[]{:S(2)}, u32[]{:S(2)}) collective-permute-start(bf16[152,256]{1,0:T(8,128)(2,1)S(1)} %get-tuple-element.167), channel_id=1, source_target_pairs={{0,4},{2,6},{4,0},{6,2},{8,12},{10,14},{12,8},{14,10},{1,5},{3,7},... | collective-permute-start | bytes 233480 | tf_op jit(solution)/shard_map/ppermute | solution.py:662
  68.1 2.0 %collective-permute-start.28 = (bf16[152,256]{1,0:T(8,128)(2,1)S(1)}, bf16[152,256]{1,0:T(8,128)(2,1)S(1)}, u32[]{:S(2)}, u32[]{:S(2)}) collective-permute-start(bf16[152,256]{1,0:T(8,128)(2,1)S(1)} %get-tuple-element.168), channel_id=1, source_target_pairs={{0,8},{2,10},{4,12},{6,14},{8,0},{10,2},{12,4},{14,6},{1,9},{3,11}... | collective-permute-start | bytes 233480 | tf_op jit(solution)/shard_map/ppermute | solution.py:662
  70.1 0.5 collective-permute-done.32
  70.6 2.4 %collective-permute-start.29 = (bf16[152,256]{1,0:T(8,128)(2,1)S(1)}, bf16[152,256]{1,0:T(8,128)(2,1)S(1)}, u32[]{:S(2)}, u32[]{:S(2)}) collective-permute-start(bf16[152,256]{1,0:T(8,128)(2,1)S(1)} %get-tuple-element.169), channel_id=1, source_target_pairs={{0,12},{2,14},{4,8},{6,10},{8,4},{10,6},{12,0},{14,2},{1,13},{3,15... | collective-permute-start | bytes 233480 | tf_op jit(solution)/shard_map/ppermute | solution.py:662
  73.1 8.1 %collective-permute-start.30 = (bf16[144,256]{1,0:T(8,128)(2,1)S(1)}, bf16[144,256]{1,0:T(8,128)(2,1)S(1)}, u32[]{:S(2)}, u32[]{:S(2)}) collective-permute-start(bf16[144,256]{1,0:T(8,128)(2,1)S(1)} %shard_map.110), channel_id=1, source_target_pairs={{0,4},{2,6},{4,0},{6,2},{8,12},{10,14},{12,8},{14,10},{1,5},{3,7},... | collective-permute-start | bytes 221192 | tf_op jit(solution)/shard_map/ppermute | solution.py:662
  81.3 3.0 %collective-permute-done.30 = bf16[144,256]{1,0:T(8,128)(2,1)S(1)} collective-permute-done((bf16[144,256]{1,0:T(8,128)(2,1)S(1)}, bf16[144,256]{1,0:T(8,128)(2,1)S(1)}, u32[]{:S(2)}, u32[]{:S(2)}) %collective-permute-start.30) | collective-permute-done | bytes 73760 | tf_op jit(solution)/shard_map/ppermute | solution.py:662
  84.3 0.7 collective-permute-start.38
  85.0 3.2 %collective-permute-start.37 = (bf16[576,256]{1,0:T(8,128)(2,1)S(1)}, bf16[576,256]{1,0:T(8,128)(2,1)S(1)}, u32[]{:S(2)}, u32[]{:S(2)}) collective-permute-start(bf16[576,256]{1,0:T(8,128)(2,1)S(1)} %constant_dynamic-update-slice_fusion.refs_0_), channel_id=1, source_target_pairs={{0,2},{2,0},{4,6},{6,4},{8,10},{10,8},{12,14},{14,12},{1,3},{3,1},... | collective-permute-start | bytes 884744 | tf_op jit(solution)/shard_map/ppermute | solution.py:659
  88.4 0.4 collective-permute-start.40
  88.9 0.7 collective-permute-done.39.refs_3_
  89.6 2.4 %collective-permute-start.36 = (bf16[144,256]{1,0:T(8,128)(2,1)S(1)}, bf16[144,256]{1,0:T(8,128)(2,1)S(1)}, u32[]{:S(2)}, u32[]{:S(2)}) collective-permute-start(bf16[144,256]{1,0:T(8,128)(2,1)S(1)} %get-tuple-element.186), channel_id=1, source_target_pairs={{0,12},{2,14},{4,8},{6,10},{8,4},{10,6},{12,0},{14,2},{1,13},{3,15... | collective-permute-start | bytes 221192 | tf_op jit(solution)/shard_map/ppermute | solution.py:662
  92.0 0.2 collective-permute-start.35
  92.2 1.8 %collective-permute-start.34 = (bf16[144,256]{1,0:T(8,128)(2,1)S(1)}, bf16[144,256]{1,0:T(8,128)(2,1)S(1)}, u32[]{:S(2)}, u32[]{:S(2)}) collective-permute-start(bf16[144,256]{1,0:T(8,128)(2,1)S(1)} %get-tuple-element.186), channel_id=1, source_target_pairs={{0,4},{2,6},{4,0},{6,2},{8,12},{10,14},{12,8},{14,10},{1,5},{3,7},... | collective-permute-start | bytes 221192 | tf_op jit(solution)/shard_map/ppermute | solution.py:662
  94.0 2.6 %collective-permute-done.36 = bf16[144,256]{1,0:T(8,128)(2,1)S(1)} collective-permute-done((bf16[144,256]{1,0:T(8,128)(2,1)S(1)}, bf16[144,256]{1,0:T(8,128)(2,1)S(1)}, u32[]{:S(2)}, u32[]{:S(2)}) %collective-permute-start.36) | collective-permute-done | bytes 73760 | tf_op jit(solution)/shard_map/ppermute | solution.py:662
  96.6 2.7 %collective-permute-done.35 = bf16[144,256]{1,0:T(8,128)(2,1)S(1)} collective-permute-done((bf16[144,256]{1,0:T(8,128)(2,1)S(1)}, bf16[144,256]{1,0:T(8,128)(2,1)S(1)}, u32[]{:S(2)}, u32[]{:S(2)}) %collective-permute-start.35) | collective-permute-done | bytes 73760 | tf_op jit(solution)/shard_map/ppermute | solution.py:662
  99.3 0.4 collective-permute-start.42
  99.7 0.5 collective-permute-start.43
  100.2 5.6 %shard_map.112 = (bf16[18,24,256]{2,1,0:T(8,128)(2,1)}, f32[18,24,256]{2,1,0:T(8,128)}) custom-call(s32[6,4]{1,0:T(8,128)S(1)} %copy.12.ep, bf16[18,24,256]{2,1,0:T(8,128)(2,1)S(1)} %bitcast.20, bf16[18,24,256]{2,1,0:T(8,128)(2,1)S(1)} %bitcast.23, bf16[18,24,256]{2,1,0:T(8,128)(2,1)S(1)} %get-tuple-element.190.hid_ref, ...), custom_call_target="tpu_custom_call" | custom-call | tf_op jit(solution)/shard_map/pallas_call | solution.py:566
  105.8 2.4 %collective-permute-done.42.refs_1_ = bf16[576,256]{1,0:T(8,128)(2,1)S(1)} collective-permute-done((bf16[576,256]{1,0:T(8,128)(2,1)S(1)}, bf16[576,256]{1,0:T(8,128)(2,1)S(1)}, u32[]{:S(2)}, u32[]{:S(2)}) %collective-permute-start.42) | collective-permute-done | bytes 294944 | tf_op jit(solution)/shard_map/ppermute | solution.py:659
  108.2 1.8 %shard_map.114 = f32[9,256,256]{2,1,0:T(8,128)} custom-call(bf16[576,256]{1,0:T(8,128)(2,1)S(1)} %constant_dynamic-update-slice_fusion.refs_0_, bf16[576,256]{1,0:T(8,128)(2,1)S(1)} %collective-permute-done.37.refs_1_, bf16[576,256]{1,0:T(8,128)(2,1)S(1)} %collective-permute-done.45.refs_2_, bf16[576,256]{1,0:T(8,128)(2,1)S(1)} %collective-permute-done.46.refs_3_), custom_call_target="tpu_custom_call" | custom-call | tf_op jit(solution)/shard_map/pallas_call | solution.py:566
  110.0 1.8 %shard_map.113 = (f32[9,256,256]{2,1,0:T(8,128)}, f32[1,256]{1,0:T(1,128)}) custom-call(bf16[576,256]{1,0:T(8,128)(2,1)S(1)} %constant_dynamic-update-slice_fusion.4.refs_0_, bf16[576,256]{1,0:T(8,128)(2,1)S(1)} %collective-permute-done.42.refs_1_, bf16[576,256]{1,0:T(8,128)(2,1)S(1)} %collective-permute-done.43.refs_2_, ...), custom_call_target="tpu_custom_call" | custom-call | tf_op jit(solution)/shard_map/pallas_call | solution.py:566
  (69 shorter events, 1.7 us)
Async XLA Ops:
  1.4 0.9 copy-start.2
  2.3 0.9 copy-start.4
  5.4 2.3 %collective-permute-start = (bf16[2,192,256]{2,1,0:T(8,128)(2,1)S(1)}, bf16[2,192,256]{2,1,0:T(8,128)(2,1)S(1)}, u32[]{:S(2)}, u32[]{:S(2)}) collective-permute-start(bf16[2,192,256]{2,1,0:T(8,128)(2,1)S(1)} %get-tuple-element.112), channel_id=1, source_target_pairs={{0,1},{1,0},{2,3},{3,2},{4,5},{5,4},{6,7},{7,6},{8,9},{9,8},{10,11... | collective-permute-start | bytes 589832 | tf_op jit(solution)/shard_map/ppermute | solution.py:580
  6.0 1.2 %collective-permute-start.1 = (bf16[2,48,256]{2,1,0:T(8,128)(2,1)S(1)}, bf16[2,48,256]{2,1,0:T(8,128)(2,1)S(1)}, u32[]{:S(2)}, u32[]{:S(2)}) collective-permute-start(bf16[2,48,256]{2,1,0:T(8,128)(2,1)S(1)} %get-tuple-element.113), channel_id=1, source_target_pairs={{0,1},{1,0},{2,3},{3,2},{4,5},{5,4},{6,7},{7,6},{8,9},{9,8},{10,11... | collective-permute-start | bytes 147464 | tf_op jit(solution)/shard_map/ppermute | solution.py:580
  6.0 1.3 %collective-permute-start.2 = (bf16[2,48,256]{2,1,0:T(8,128)(2,1)S(1)}, bf16[2,48,256]{2,1,0:T(8,128)(2,1)S(1)}, u32[]{:S(2)}, u32[]{:S(2)}) collective-permute-start(bf16[2,48,256]{2,1,0:T(8,128)(2,1)S(1)} %get-tuple-element.114), channel_id=1, source_target_pairs={{0,1},{1,0},{2,3},{3,2},{4,5},{5,4},{6,7},{7,6},{8,9},{9,8},{10,11... | collective-permute-start | bytes 147464 | tf_op jit(solution)/shard_map/ppermute | solution.py:580
  6.5 1.2 %collective-permute-start.3 = (bf16[2,48,256]{2,1,0:T(8,128)(2,1)S(1)}, bf16[2,48,256]{2,1,0:T(8,128)(2,1)S(1)}, u32[]{:S(2)}, u32[]{:S(2)}) collective-permute-start(bf16[2,48,256]{2,1,0:T(8,128)(2,1)S(1)} %get-tuple-element.115), channel_id=1, source_target_pairs={{0,1},{1,0},{2,3},{3,2},{4,5},{5,4},{6,7},{7,6},{8,9},{9,8},{10,11... | collective-permute-start | bytes 147464 | tf_op jit(solution)/shard_map/ppermute | solution.py:580
  7.7 13.9 %collective-permute-start.4 = (bf16[2,2,192,256]{3,2,1,0:T(8,128)(2,1)S(1)}, bf16[2,2,192,256]{3,2,1,0:T(8,128)(2,1)S(1)}, u32[]{:S(2)}, u32[]{:S(2)}) collective-permute-start(bf16[2,2,192,256]{3,2,1,0:T(8,128)(2,1)S(1)} %get-tuple-element.116), channel_id=1, source_target_pairs={{0,2},{2,0},{4,6},{6,4},{8,10},{10,8},{12,14},{14,12},{1,15},{3,5}... | collective-permute-start | bytes 1179656 | tf_op jit(solution)/shard_map/ppermute | solution.py:610
  10.5 8.2 %collective-permute-start.5 = (bf16[2,2,48,256]{3,2,1,0:T(8,128)(2,1)S(1)}, bf16[2,2,48,256]{3,2,1,0:T(8,128)(2,1)S(1)}, u32[]{:S(2)}, u32[]{:S(2)}) collective-permute-start(bf16[2,2,48,256]{3,2,1,0:T(8,128)(2,1)S(1)} %get-tuple-element.117), channel_id=1, source_target_pairs={{0,4},{4,0},{10,14},{14,10},{1,9},{3,11},{5,13},{7,15},{9,1},{11,3... | collective-permute-start | bytes 294920 | tf_op jit(solution)/shard_map/ppermute | solution.py:610
  14.0 7.7 %collective-permute-start.6 = (bf16[2,2,48,256]{3,2,1,0:T(8,128)(2,1)S(1)}, bf16[2,2,48,256]{3,2,1,0:T(8,128)(2,1)S(1)}, u32[]{:S(2)}, u32[]{:S(2)}) collective-permute-start(bf16[2,2,48,256]{3,2,1,0:T(8,128)(2,1)S(1)} %get-tuple-element.118), channel_id=1, source_target_pairs={{0,12},{2,14},{4,8},{6,10},{8,4},{10,6},{12,0},{14,2},{1,7},{3,13}... | collective-permute-start | bytes 294920 | tf_op jit(solution)/shard_map/ppermute | solution.py:610
  14.8 6.8 %collective-permute-start.7 = (bf16[2,2,48,256]{3,2,1,0:T(8,128)(2,1)S(1)}, bf16[2,2,48,256]{3,2,1,0:T(8,128)(2,1)S(1)}, u32[]{:S(2)}, u32[]{:S(2)}) collective-permute-start(bf16[2,2,48,256]{3,2,1,0:T(8,128)(2,1)S(1)} %get-tuple-element.119), channel_id=1, source_target_pairs={{1,11},{5,15},{11,1},{15,5},{17,27},{21,31},{27,17},{31,21}} | collective-permute-start | bytes 294920 | tf_op jit(solution)/shard_map/ppermute | solution.py:610
  15.5 1.3 %copy-start = (bf16[3,3,256,256]{3,2,1,0:T(8,128)(2,1)S(1)}, bf16[3,3,256,256]{3,2,1,0:T(8,128)(2,1)}, u32[]{:S(2)}) copy-start(bf16[3,3,256,256]{3,2,1,0:T(8,128)(2,1)} %param.10) | copy-start | bytes 3538948
  16.8 1.3 %copy-start.6 = (bf16[3,3,256,256]{3,2,1,0:T(8,128)(2,1)S(1)}, bf16[3,3,256,256]{3,2,1,0:T(8,128)(2,1)}, u32[]{:S(2)}) copy-start(bf16[3,3,256,256]{3,2,1,0:T(8,128)(2,1)} %param.8) | copy-start | bytes 3538948
  18.0 9.9 %copy-start.3 = (bf16[1,6,3,24,256]{4,3,2,1,0:T(8,128)(2,1)S(1)}, bf16[1,6,3,24,256]{4,3,2,1,0:T(8,128)(2,1)}, u32[]{:S(2)}) copy-start(bf16[1,6,3,24,256]{4,3,2,1,0:T(8,128)(2,1)} %param.6) | copy-start | bytes 663556
  18.0 9.9 %copy-start.5 = (bf16[1,1,6,3,24,256]{5,4,3,2,1,0:T(8,128)(2,1)S(1)}, bf16[1,1,6,3,24,256]{5,4,3,2,1,0:T(8,128)(2,1)}, u32[]{:S(2)}) copy-start(bf16[1,1,6,3,24,256]{5,4,3,2,1,0:T(8,128)(2,1)} %param.7) | copy-start | bytes 663556
  18.0 9.9 %copy-start.7 = (f32[256]{0:T(256)S(1)}, f32[256]{0:T(256)}, u32[]{:S(2)}) copy-start(f32[256]{0:T(256)} %param.9) | copy-start | bytes 3076
  21.7 6.3 %collective-permute-start.8 = (bf16[2,2,192,256]{3,2,1,0:T(8,128)(2,1)S(1)}, bf16[2,2,192,256]{3,2,1,0:T(8,128)(2,1)S(1)}, u32[]{:S(2)}, u32[]{:S(2)}) collective-permute-start(bf16[2,2,192,256]{3,2,1,0:T(8,128)(2,1)S(1)} %collective-permute-done.4.refs_0_), channel_id=1, source_target_pairs={{0,1},{1,0},{2,3},{3,2},{4,5},{5,4},{6,7},{7,6},{8,9},{9,8},{10,11... | collective-permute-start | bytes 1179656 | tf_op jit(solution)/shard_map/ppermute | solution.py:580
  26.1 1.5 %collective-permute-start.9 = (bf16[2,2,48,256]{3,2,1,0:T(8,128)(2,1)S(1)}, bf16[2,2,48,256]{3,2,1,0:T(8,128)(2,1)S(1)}, u32[]{:S(2)}, u32[]{:S(2)}) collective-permute-start(bf16[2,2,48,256]{3,2,1,0:T(8,128)(2,1)S(1)} %collective-permute-done.5.refs_2_), channel_id=1, source_target_pairs={{0,1},{1,0},{2,3},{3,2},{4,5},{5,4},{6,7},{7,6},{8,9},{9,8},{10,11... | collective-permute-start | bytes 294920 | tf_op jit(solution)/shard_map/ppermute | solution.py:580
  26.2 1.6 %collective-permute-start.10 = (bf16[2,2,48,256]{3,2,1,0:T(8,128)(2,1)S(1)}, bf16[2,2,48,256]{3,2,1,0:T(8,128)(2,1)S(1)}, u32[]{:S(2)}, u32[]{:S(2)}) collective-permute-start(bf16[2,2,48,256]{3,2,1,0:T(8,128)(2,1)S(1)} %collective-permute-done.6.refs_4_), channel_id=1, source_target_pairs={{0,1},{1,0},{2,3},{3,2},{4,5},{5,4},{6,7},{7,6},{8,9},{9,8},{10,11... | collective-permute-start | bytes 294920 | tf_op jit(solution)/shard_map/ppermute | solution.py:580
  26.7 1.3 %collective-permute-start.11 = (bf16[2,2,48,256]{3,2,1,0:T(8,128)(2,1)S(1)}, bf16[2,2,48,256]{3,2,1,0:T(8,128)(2,1)S(1)}, u32[]{:S(2)}, u32[]{:S(2)}) collective-permute-start(bf16[2,2,48,256]{3,2,1,0:T(8,128)(2,1)S(1)} %collective-permute-done.7.refs_6_), channel_id=1, source_target_pairs={{0,1},{1,0},{2,3},{3,2},{4,5},{5,4},{6,7},{7,6},{8,9},{9,8},{10,11... | collective-permute-start | bytes 294920 | tf_op jit(solution)/shard_map/ppermute | solution.py:580
  36.3 2.1 %collective-permute-start.14 = (bf16[9,128,256]{2,1,0:T(8,128)(2,1)S(1)}, bf16[9,128,256]{2,1,0:T(8,128)(2,1)S(1)}, u32[]{:S(2)}, u32[]{:S(2)}) collective-permute-start(bf16[9,128,256]{2,1,0:T(8,128)(2,1)S(1)} %get-tuple-element.136), channel_id=1, source_target_pairs={{0,1},{1,0},{2,3},{3,2},{4,5},{5,4},{6,7},{7,6},{8,9},{9,8},{10,11... | collective-permute-start | bytes 1769480 | tf_op jit(solution)/shard_map/ppermute | solution.py:580
  36.7 11.0 %collective-permute-start.12 = (bf16[9,128,256]{2,1,0:T(8,128)(2,1)S(1)}, bf16[9,128,256]{2,1,0:T(8,128)(2,1)S(1)}, u32[]{:S(2)}, u32[]{:S(2)}) collective-permute-start(bf16[9,128,256]{2,1,0:T(8,128)(2,1)S(1)} %get-tuple-element.131), channel_id=1, source_target_pairs={{0,1},{1,0},{2,3},{3,2},{4,5},{5,4},{6,7},{7,6},{8,9},{9,8},{10,11... | collective-permute-start | bytes 1769480 | tf_op jit(solution)/shard_map/ppermute | solution.py:580
  36.8 4.2 %collective-permute-start.16 = (bf16[2,192,256]{2,1,0:T(8,128)(2,1)S(1)}, bf16[2,192,256]{2,1,0:T(8,128)(2,1)S(1)}, u32[]{:S(2)}, u32[]{:S(2)}) collective-permute-start(bf16[2,192,256]{2,1,0:T(8,128)(2,1)S(1)} %get-tuple-element.143), channel_id=1, source_target_pairs={{0,1},{1,0},{2,3},{3,2},{4,5},{5,4},{6,7},{7,6},{8,9},{9,8},{10,11... | collective-permute-start | bytes 589832 | tf_op jit(solution)/shard_map/ppermute | solution.py:580
  38.5 13.0 %collective-permute-start.15 = (bf16[576,256]{1,0:T(8,128)(2,1)S(1)}, bf16[576,256]{1,0:T(8,128)(2,1)S(1)}, u32[]{:S(2)}, u32[]{:S(2)}) collective-permute-start(bf16[576,256]{1,0:T(8,128)(2,1)S(1)} %get-tuple-element.137), channel_id=1, source_target_pairs={{0,2},{2,0},{4,6},{6,4},{8,10},{10,8},{12,14},{14,12},{1,3},{3,1},... | collective-permute-start | bytes 884744 | tf_op jit(solution)/shard_map/ppermute | solution.py:659
  38.6 1.3 %collective-permute-start.17 = (bf16[2,48,256]{2,1,0:T(8,128)(2,1)S(1)}, bf16[2,48,256]{2,1,0:T(8,128)(2,1)S(1)}, u32[]{:S(2)}, u32[]{:S(2)}) collective-permute-start(bf16[2,48,256]{2,1,0:T(8,128)(2,1)S(1)} %get-tuple-element.144), channel_id=1, source_target_pairs={{0,1},{1,0},{2,3},{3,2},{4,5},{5,4},{6,7},{7,6},{8,9},{9,8},{10,11... | collective-permute-start | bytes 147464 | tf_op jit(solution)/shard_map/ppermute | solution.py:580
  38.9 1.2 %collective-permute-start.18 = (bf16[2,48,256]{2,1,0:T(8,128)(2,1)S(1)}, bf16[2,48,256]{2,1,0:T(8,128)(2,1)S(1)}, u32[]{:S(2)}, u32[]{:S(2)}) collective-permute-start(bf16[2,48,256]{2,1,0:T(8,128)(2,1)S(1)} %get-tuple-element.145), channel_id=1, source_target_pairs={{0,1},{1,0},{2,3},{3,2},{4,5},{5,4},{6,7},{7,6},{8,9},{9,8},{10,11... | collective-permute-start | bytes 147464 | tf_op jit(solution)/shard_map/ppermute | solution.py:580
  39.8 1.2 %collective-permute-start.19 = (bf16[2,48,256]{2,1,0:T(8,128)(2,1)S(1)}, bf16[2,48,256]{2,1,0:T(8,128)(2,1)S(1)}, u32[]{:S(2)}, u32[]{:S(2)}) collective-permute-start(bf16[2,48,256]{2,1,0:T(8,128)(2,1)S(1)} %get-tuple-element.146), channel_id=1, source_target_pairs={{0,1},{1,0},{2,3},{3,2},{4,5},{5,4},{6,7},{7,6},{8,9},{9,8},{10,11... | collective-permute-start | bytes 147464 | tf_op jit(solution)/shard_map/ppermute | solution.py:580
  40.2 6.6 %collective-permute-start.13 = (bf16[8,256]{1,0:T(8,128)(2,1)S(1)}, bf16[8,256]{1,0:T(8,128)(2,1)S(1)}, u32[]{:S(2)}, u32[]{:S(2)}) collective-permute-start(bf16[8,256]{1,0:T(8,128)(2,1)S(1)} %get-tuple-element.133), channel_id=1, source_target_pairs={{0,1},{1,0},{2,3},{3,2},{4,5},{5,4},{6,7},{7,6},{8,9},{9,8},{10,11... | collective-permute-start | bytes 12296 | tf_op jit(solution)/shard_map/ppermute | solution.py:580
  41.1 7.6 %collective-permute-start.20 = (bf16[2,2,48,256]{3,2,1,0:T(8,128)(2,1)S(1)}, bf16[2,2,48,256]{3,2,1,0:T(8,128)(2,1)S(1)}, u32[]{:S(2)}, u32[]{:S(2)}) collective-permute-start(bf16[2,2,48,256]{3,2,1,0:T(8,128)(2,1)S(1)} %get-tuple-element.147), channel_id=1, source_target_pairs={{0,4},{4,0},{10,14},{14,10},{1,9},{3,11},{5,13},{7,15},{9,1},{11,3... | collective-permute-start | bytes 294920 | tf_op jit(solution)/shard_map/ppermute | solution.py:610
  44.0 7.5 %collective-permute-start.21 = (bf16[2,2,48,256]{3,2,1,0:T(8,128)(2,1)S(1)}, bf16[2,2,48,256]{3,2,1,0:T(8,128)(2,1)S(1)}, u32[]{:S(2)}, u32[]{:S(2)}) collective-permute-start(bf16[2,2,48,256]{3,2,1,0:T(8,128)(2,1)S(1)} %get-tuple-element.148), channel_id=1, source_target_pairs={{0,12},{2,14},{4,8},{6,10},{8,4},{10,6},{12,0},{14,2},{1,7},{3,13}... | collective-permute-start | bytes 294920 | tf_op jit(solution)/shard_map/ppermute | solution.py:610
  46.8 4.7 %collective-permute-start.22 = (bf16[2,2,48,256]{3,2,1,0:T(8,128)(2,1)S(1)}, bf16[2,2,48,256]{3,2,1,0:T(8,128)(2,1)S(1)}, u32[]{:S(2)}, u32[]{:S(2)}) collective-permute-start(bf16[2,2,48,256]{3,2,1,0:T(8,128)(2,1)S(1)} %get-tuple-element.149), channel_id=1, source_target_pairs={{1,11},{5,15},{11,1},{15,5},{17,27},{21,31},{27,17},{31,21}} | collective-permute-start | bytes 294920 | tf_op jit(solution)/shard_map/ppermute | solution.py:610
  51.5 11.9 %collective-permute-start.23 = (bf16[584,256]{1,0:T(8,128)(2,1)S(1)}, bf16[584,256]{1,0:T(8,128)(2,1)S(1)}, u32[]{:S(2)}, u32[]{:S(2)}) collective-permute-start(bf16[584,256]{1,0:T(8,128)(2,1)S(1)} %get-tuple-element.150), channel_id=1, source_target_pairs={{0,2},{2,0},{4,6},{6,4},{8,10},{10,8},{12,14},{14,12},{1,3},{3,1},... | collective-permute-start | bytes 897032 | tf_op jit(solution)/shard_map/ppermute | solution.py:659
  53.6 4.5 %collective-permute-start.24 = (bf16[144,256]{1,0:T(8,128)(2,1)S(1)}, bf16[144,256]{1,0:T(8,128)(2,1)S(1)}, u32[]{:S(2)}, u32[]{:S(2)}) collective-permute-start(bf16[144,256]{1,0:T(8,128)(2,1)S(1)} %get-tuple-element.153), channel_id=1, source_target_pairs={{0,4},{2,6},{4,0},{6,2},{8,12},{10,14},{12,8},{14,10},{1,5},{3,7},... | collective-permute-start | bytes 221192 | tf_op jit(solution)/shard_map/ppermute | solution.py:662
  53.7 5.3 %collective-permute-start.25 = (bf16[144,256]{1,0:T(8,128)(2,1)S(1)}, bf16[144,256]{1,0:T(8,128)(2,1)S(1)}, u32[]{:S(2)}, u32[]{:S(2)}) collective-permute-start(bf16[144,256]{1,0:T(8,128)(2,1)S(1)} %get-tuple-element.154), channel_id=1, source_target_pairs={{0,8},{2,10},{4,12},{6,14},{8,0},{10,2},{12,4},{14,6},{1,9},{3,11}... | collective-permute-start | bytes 221192 | tf_op jit(solution)/shard_map/ppermute | solution.py:662
  56.6 6.8 %collective-permute-start.26 = (bf16[144,256]{1,0:T(8,128)(2,1)S(1)}, bf16[144,256]{1,0:T(8,128)(2,1)S(1)}, u32[]{:S(2)}, u32[]{:S(2)}) collective-permute-start(bf16[144,256]{1,0:T(8,128)(2,1)S(1)} %get-tuple-element.155), channel_id=1, source_target_pairs={{0,12},{2,14},{4,8},{6,10},{8,4},{10,6},{12,0},{14,2},{1,13},{3,15... | collective-permute-start | bytes 221192 | tf_op jit(solution)/shard_map/ppermute | solution.py:662
  63.5 36.7 %copy-start.1 = (bf16[3,3,256,256]{3,2,1,0:T(8,128)(2,1)S(1)}, bf16[3,3,256,256]{3,2,1,0:T(8,128)(2,1)}, u32[]{:S(2)}) copy-start(bf16[3,3,256,256]{3,2,1,0:T(8,128)(2,1)} %param.10) | copy-start | bytes 3538948
  63.5 20.8 %collective-permute-start.33 = (bf16[2,2,192,256]{3,2,1,0:T(8,128)(2,1)S(1)}, bf16[2,2,192,256]{3,2,1,0:T(8,128)(2,1)S(1)}, u32[]{:S(2)}, u32[]{:S(2)}) collective-permute-start(bf16[2,2,192,256]{3,2,1,0:T(8,128)(2,1)S(1)} %get-tuple-element.171), channel_id=1, source_target_pairs={{0,2},{2,0},{4,6},{6,4},{8,10},{10,8},{12,14},{14,12},{1,15},{3,5}... | collective-permute-start | bytes 1179656 | tf_op jit(solution)/shard_map/ppermute | solution.py:610
  63.6 7.0 %collective-permute-start.32 = (bf16[144,256]{1,0:T(8,128)(2,1)S(1)}, bf16[144,256]{1,0:T(8,128)(2,1)S(1)}, u32[]{:S(2)}, u32[]{:S(2)}) collective-permute-start(bf16[144,256]{1,0:T(8,128)(2,1)S(1)} %shard_map.110), channel_id=1, source_target_pairs={{0,12},{2,14},{4,8},{6,10},{8,4},{10,6},{12,0},{14,2},{1,13},{3,15... | collective-permute-start | bytes 221192 | tf_op jit(solution)/shard_map/ppermute | solution.py:662
  65.9 7.2 %collective-permute-start.31 = (bf16[144,256]{1,0:T(8,128)(2,1)S(1)}, bf16[144,256]{1,0:T(8,128)(2,1)S(1)}, u32[]{:S(2)}, u32[]{:S(2)}) collective-permute-start(bf16[144,256]{1,0:T(8,128)(2,1)S(1)} %shard_map.110), channel_id=1, source_target_pairs={{0,8},{2,10},{4,12},{6,14},{8,0},{10,2},{12,4},{14,6},{1,9},{3,11}... | collective-permute-start | bytes 221192 | tf_op jit(solution)/shard_map/ppermute | solution.py:662
  66.9 17.4 %collective-permute-start.27 = (bf16[152,256]{1,0:T(8,128)(2,1)S(1)}, bf16[152,256]{1,0:T(8,128)(2,1)S(1)}, u32[]{:S(2)}, u32[]{:S(2)}) collective-permute-start(bf16[152,256]{1,0:T(8,128)(2,1)S(1)} %get-tuple-element.167), channel_id=1, source_target_pairs={{0,4},{2,6},{4,0},{6,2},{8,12},{10,14},{12,8},{14,10},{1,5},{3,7},... | collective-permute-start | bytes 233480 | tf_op jit(solution)/shard_map/ppermute | solution.py:662
  68.1 16.2 %collective-permute-start.28 = (bf16[152,256]{1,0:T(8,128)(2,1)S(1)}, bf16[152,256]{1,0:T(8,128)(2,1)S(1)}, u32[]{:S(2)}, u32[]{:S(2)}) collective-permute-start(bf16[152,256]{1,0:T(8,128)(2,1)S(1)} %get-tuple-element.168), channel_id=1, source_target_pairs={{0,8},{2,10},{4,12},{6,14},{8,0},{10,2},{12,4},{14,6},{1,9},{3,11}... | collective-permute-start | bytes 233480 | tf_op jit(solution)/shard_map/ppermute | solution.py:662
  70.6 13.7 %collective-permute-start.29 = (bf16[152,256]{1,0:T(8,128)(2,1)S(1)}, bf16[152,256]{1,0:T(8,128)(2,1)S(1)}, u32[]{:S(2)}, u32[]{:S(2)}) collective-permute-start(bf16[152,256]{1,0:T(8,128)(2,1)S(1)} %get-tuple-element.169), channel_id=1, source_target_pairs={{0,12},{2,14},{4,8},{6,10},{8,4},{10,6},{12,0},{14,2},{1,13},{3,15... | collective-permute-start | bytes 233480 | tf_op jit(solution)/shard_map/ppermute | solution.py:662
  73.1 11.2 %collective-permute-start.30 = (bf16[144,256]{1,0:T(8,128)(2,1)S(1)}, bf16[144,256]{1,0:T(8,128)(2,1)S(1)}, u32[]{:S(2)}, u32[]{:S(2)}) collective-permute-start(bf16[144,256]{1,0:T(8,128)(2,1)S(1)} %shard_map.110), channel_id=1, source_target_pairs={{0,4},{2,6},{4,0},{6,2},{8,12},{10,14},{12,8},{14,10},{1,5},{3,7},... | collective-permute-start | bytes 221192 | tf_op jit(solution)/shard_map/ppermute | solution.py:662
  84.3 14.9 %collective-permute-start.38 = (bf16[2,2,192,256]{3,2,1,0:T(8,128)(2,1)S(1)}, bf16[2,2,192,256]{3,2,1,0:T(8,128)(2,1)S(1)}, u32[]{:S(2)}, u32[]{:S(2)}) collective-permute-start(bf16[2,2,192,256]{3,2,1,0:T(8,128)(2,1)S(1)} %collective-permute-done.33.refs_0_), channel_id=1, source_target_pairs={{0,1},{1,0},{2,3},{3,2},{4,5},{5,4},{6,7},{7,6},{8,9},{9,8},{10,11... | collective-permute-start | bytes 1179656 | tf_op jit(solution)/shard_map/ppermute | solution.py:580
  85.0 14.2 %collective-permute-start.37 = (bf16[576,256]{1,0:T(8,128)(2,1)S(1)}, bf16[576,256]{1,0:T(8,128)(2,1)S(1)}, u32[]{:S(2)}, u32[]{:S(2)}) collective-permute-start(bf16[576,256]{1,0:T(8,128)(2,1)S(1)} %constant_dynamic-update-slice_fusion.refs_0_), channel_id=1, source_target_pairs={{0,2},{2,0},{4,6},{6,4},{8,10},{10,8},{12,14},{14,12},{1,3},{3,1},... | collective-permute-start | bytes 884744 | tf_op jit(solution)/shard_map/ppermute | solution.py:659
  88.3 1.3 %collective-permute-start.39 = (bf16[2,2,48,256]{3,2,1,0:T(8,128)(2,1)S(1)}, bf16[2,2,48,256]{3,2,1,0:T(8,128)(2,1)S(1)}, u32[]{:S(2)}, u32[]{:S(2)}) collective-permute-start(bf16[2,2,48,256]{3,2,1,0:T(8,128)(2,1)S(1)} %collective-permute-done.20.refs_2_), channel_id=1, source_target_pairs={{0,1},{1,0},{2,3},{3,2},{4,5},{5,4},{6,7},{7,6},{8,9},{9,8},{10,11... | collective-permute-start | bytes 294920 | tf_op jit(solution)/shard_map/ppermute | solution.py:580
  88.4 3.7 %collective-permute-start.40 = (bf16[2,2,48,256]{3,2,1,0:T(8,128)(2,1)S(1)}, bf16[2,2,48,256]{3,2,1,0:T(8,128)(2,1)S(1)}, u32[]{:S(2)}, u32[]{:S(2)}) collective-permute-start(bf16[2,2,48,256]{3,2,1,0:T(8,128)(2,1)S(1)} %collective-permute-done.21.refs_4_), channel_id=1, source_target_pairs={{0,1},{1,0},{2,3},{3,2},{4,5},{5,4},{6,7},{7,6},{8,9},{9,8},{10,11... | collective-permute-start | bytes 294920 | tf_op jit(solution)/shard_map/ppermute | solution.py:580
  88.8 3.4 %collective-permute-start.41 = (bf16[2,2,48,256]{3,2,1,0:T(8,128)(2,1)S(1)}, bf16[2,2,48,256]{3,2,1,0:T(8,128)(2,1)S(1)}, u32[]{:S(2)}, u32[]{:S(2)}) collective-permute-start(bf16[2,2,48,256]{3,2,1,0:T(8,128)(2,1)S(1)} %collective-permute-done.22.refs_6_), channel_id=1, source_target_pairs={{0,1},{1,0},{2,3},{3,2},{4,5},{5,4},{6,7},{7,6},{8,9},{9,8},{10,11... | collective-permute-start | bytes 294920 | tf_op jit(solution)/shard_map/ppermute | solution.py:580
  89.6 7.0 %collective-permute-start.36 = (bf16[144,256]{1,0:T(8,128)(2,1)S(1)}, bf16[144,256]{1,0:T(8,128)(2,1)S(1)}, u32[]{:S(2)}, u32[]{:S(2)}) collective-permute-start(bf16[144,256]{1,0:T(8,128)(2,1)S(1)} %get-tuple-element.186), channel_id=1, source_target_pairs={{0,12},{2,14},{4,8},{6,10},{8,4},{10,6},{12,0},{14,2},{1,13},{3,15... | collective-permute-start | bytes 221192 | tf_op jit(solution)/shard_map/ppermute | solution.py:662
  92.0 7.2 %collective-permute-start.35 = (bf16[144,256]{1,0:T(8,128)(2,1)S(1)}, bf16[144,256]{1,0:T(8,128)(2,1)S(1)}, u32[]{:S(2)}, u32[]{:S(2)}) collective-permute-start(bf16[144,256]{1,0:T(8,128)(2,1)S(1)} %get-tuple-element.186), channel_id=1, source_target_pairs={{0,8},{2,10},{4,12},{6,14},{8,0},{10,2},{12,4},{14,6},{1,9},{3,11}... | collective-permute-start | bytes 221192 | tf_op jit(solution)/shard_map/ppermute | solution.py:662
  92.2 7.1 %collective-permute-start.34 = (bf16[144,256]{1,0:T(8,128)(2,1)S(1)}, bf16[144,256]{1,0:T(8,128)(2,1)S(1)}, u32[]{:S(2)}, u32[]{:S(2)}) collective-permute-start(bf16[144,256]{1,0:T(8,128)(2,1)S(1)} %get-tuple-element.186), channel_id=1, source_target_pairs={{0,4},{2,6},{4,0},{6,2},{8,12},{10,14},{12,8},{14,10},{1,5},{3,7},... | collective-permute-start | bytes 221192 | tf_op jit(solution)/shard_map/ppermute | solution.py:662
  99.3 8.9 %collective-permute-start.42 = (bf16[576,256]{1,0:T(8,128)(2,1)S(1)}, bf16[576,256]{1,0:T(8,128)(2,1)S(1)}, u32[]{:S(2)}, u32[]{:S(2)}) collective-permute-start(bf16[576,256]{1,0:T(8,128)(2,1)S(1)} %constant_dynamic-update-slice_fusion.4.refs_0_), channel_id=1, source_target_pairs={{0,2},{2,0},{4,6},{6,4},{8,10},{10,8},{12,14},{14,12},{1,3},{3,1},... | collective-permute-start | bytes 884744 | tf_op jit(solution)/shard_map/ppermute | solution.py:659
  99.7 8.5 %collective-permute-start.45 = (bf16[576,256]{1,0:T(8,128)(2,1)S(1)}, bf16[576,256]{1,0:T(8,128)(2,1)S(1)}, u32[]{:S(2)}, u32[]{:S(2)}) collective-permute-start(bf16[576,256]{1,0:T(8,128)(2,1)S(1)} %constant_dynamic-update-slice_fusion.refs_0_), channel_id=1, source_target_pairs={{0,1},{1,0},{2,3},{3,2},{4,5},{5,4},{6,7},{7,6},{8,9},{9,8},{10,11... | collective-permute-start | bytes 884744 | tf_op jit(solution)/shard_map/ppermute | solution.py:580
  99.7 10.3 %collective-permute-start.43 = (bf16[576,256]{1,0:T(8,128)(2,1)S(1)}, bf16[576,256]{1,0:T(8,128)(2,1)S(1)}, u32[]{:S(2)}, u32[]{:S(2)}) collective-permute-start(bf16[576,256]{1,0:T(8,128)(2,1)S(1)} %constant_dynamic-update-slice_fusion.4.refs_0_), channel_id=1, source_target_pairs={{0,1},{1,0},{2,3},{3,2},{4,5},{5,4},{6,7},{7,6},{8,9},{9,8},{10,11... | collective-permute-start | bytes 884744 | tf_op jit(solution)/shard_map/ppermute | solution.py:580
  100.2 8.0 %collective-permute-start.46 = (bf16[576,256]{1,0:T(8,128)(2,1)S(1)}, bf16[576,256]{1,0:T(8,128)(2,1)S(1)}, u32[]{:S(2)}, u32[]{:S(2)}) collective-permute-start(bf16[576,256]{1,0:T(8,128)(2,1)S(1)} %collective-permute-done.37.refs_1_), channel_id=1, source_target_pairs={{0,1},{1,0},{2,3},{3,2},{4,5},{5,4},{6,7},{7,6},{8,9},{9,8},{10,11... | collective-permute-start | bytes 884744 | tf_op jit(solution)/shard_map/ppermute | solution.py:580
  108.2 1.8 %collective-permute-start.44 = (bf16[576,256]{1,0:T(8,128)(2,1)S(1)}, bf16[576,256]{1,0:T(8,128)(2,1)S(1)}, u32[]{:S(2)}, u32[]{:S(2)}) collective-permute-start(bf16[576,256]{1,0:T(8,128)(2,1)S(1)} %collective-permute-done.42.refs_1_), channel_id=1, source_target_pairs={{0,1},{1,0},{2,3},{3,2},{4,5},{5,4},{6,7},{7,6},{8,9},{9,8},{10,11... | collective-permute-start | bytes 884744 | tf_op jit(solution)/shard_map/ppermute | solution.py:580

commit v14 on v10

--- a/solution.py
+++ b/solution.py
@@ -710,13 +710,15 @@
 
     own1, bias_sum = sum_z(keep1, recvs1, bias_sum)
     own1 = [own1] + [along_z(own1, j) for j in range(1, zcount)]
+    back = {i: swap_dp(came[i]) for i in steps}
+    own1[-1], back = barrier((own1[-1], back))
     own2 = jnp.concatenate(own2, axis=0)
     other2 = along_y(own2)
     own1 = jnp.concatenate(own1, axis=0)
     other1 = along_y(own1)
     messages = []
     for i in steps:
-        messages += [came[i], swap_dp(came[i])]
+        messages += [came[i], back[i]]
     messages.append(packed[-1])
     own1, messages = barrier((own1, messages))
     state, grad = call(

time: 108 us -> 120 us (1.11)
  waiting for transfers between devices: 29.2 us -> 39.1 us
  starting transfers between devices: 51.7 us -> 53.5 us
    ppermute x4, waiting for transfers between devices: 0.03 us -> 8.58 us  [along_y(): return lax.ppermute(v, 'tile', [(i, i ^ 1) for i in range(tiles)])]
    ppermute x12, starting transfers between devices: 22.7 us -> 26.9 us  [along_z(): return lax.ppermute(v, 'tile', [(i, i ^ 2 * j) for i in range(tiles)])]
    ppermute x23, starting transfers between devices: 11.4 us -> 9.2 us  [swap_dp(): return lax.ppermute(v, 'dp', [(i, count - 1 - i) for i in range(count)])]
    ppermute x12, waiting for transfers between devices: 13.9 us -> 15.2 us  [along_z(): return lax.ppermute(v, 'tile', [(i, i ^ 2 * j) for i in range(tiles)])]
  transfers between devices with their start and end apart: 47 -> 47, of which waited for: 22 -> 19; matrix products, arithmetic and copies ran while one was open for 0% -> 0% of each run, Pallas kernels for 8% -> 7%
where the time goes in v14:
time: 120 us
  starting transfers between devices  53.5 us (45%)
  waiting for transfers between devices  39.1 us (33%)
  Pallas kernels  20.9 us (17%)
  local copies, waits for them, and re-layouts  5.22 us (4%)
    ppermute x12, starting transfers between devices, along_z(): return lax.ppermute(v, 'tile', [(i, i ^ 2 * j) for i in range(tiles)])  26.9 us
    pallas_call x14, Pallas kernels, run(): pl.pallas_call(kernel, out_shape=[jax.ShapeDtypeStruct(s, dt) for s, dt i...  20.9 us
    ppermute x12, waiting for transfers between devices, along_z(): return lax.ppermute(v, 'tile', [(i, i ^ 2 * j) for i in range(tiles)])  15.2 us
    ppermute x8, starting transfers between devices, across(): return lax.ppermute(v, ('tile', 'dp'), pairs[step])  14.4 us
    ppermute x23, starting transfers between devices, swap_dp(): return lax.ppermute(v, 'dp', [(i, count - 1 - i) for i in range(count)])  9.2 us
    ppermute x8, waiting for transfers between devices, across(): return lax.ppermute(v, ('tile', 'dp'), pairs[step])  9.14 us
    ppermute x4, waiting for transfers between devices, along_y(): return lax.ppermute(v, 'tile', [(i, i ^ 1) for i in range(tiles)])  8.58 us
    ppermute x23, waiting for transfers between devices, swap_dp(): return lax.ppermute(v, 'dp', [(i, count - 1 - i) for i in range(count)])  6.12 us
  transfers between devices with their start and end apart: 47, of which 19 were waited for; matrix products, arithmetic and copies ran while one was open for 0% of the time, Pallas kernels for 7%

profile of v14, /device:TPU:0, one launch (start us, length us, event | category | flops | bytes accessed | tf_op | source)
XLA Modules:
  0.0 119.5 jit_solution(4673461232903861828)
XLA Ops:
  0.6 0.8 copy.12.ep
  1.4 0.9 copy-done.2
  2.3 0.9 copy-done.4
  3.3 2.2 %shard_map.101 = (bf16[2,192,256]{2,1,0:T(8,128)(2,1)S(1)}, bf16[2,48,256]{2,1,0:T(8,128)(2,1)S(1)}, bf16[2,48,256]{2,1,0:T(8,128)(2,1)S(1)}, bf16[2,48,256]{2,1...) custom-call(s32[6,4]{1,0:T(8,128)S(1)} %copy.12.ep, ...), custom_call_target="tpu_custom_call" | custom-call | tf_op jit(solution)/shard_map/pallas_call | solution.py:566
  5.4 0.5 collective-permute-start
  6.0 0.4 collective-permute-start.2
  6.5 0.6 collective-permute-done.1.refs_5_
  7.2 0.2 collective-permute-done.2.refs_6_
  7.3 0.3 collective-permute-done.3.refs_7_
  7.7 2.7 %collective-permute-start.4 = (bf16[2,2,192,256]{3,2,1,0:T(8,128)(2,1)S(1)}, bf16[2,2,192,256]{3,2,1,0:T(8,128)(2,1)S(1)}, u32[]{:S(2)}, u32[]{:S(2)}) collective-permute-start(bf16[2,2,192,256]{3,2,1,0:T(8,128)(2,1)S(1)} %get-tuple-element.108), channel_id=1, source_target_pairs={{0,2},{2,0},{4,6},{6,4},{8,10},{10,8},{12,14},{14,12},{1,15},{3,5}... | collective-permute-start | bytes 1179656 | tf_op jit(solution)/shard_map/ppermute | solution.py:610
  10.5 3.5 %collective-permute-start.5 = (bf16[2,2,48,256]{3,2,1,0:T(8,128)(2,1)S(1)}, bf16[2,2,48,256]{3,2,1,0:T(8,128)(2,1)S(1)}, u32[]{:S(2)}, u32[]{:S(2)}) collective-permute-start(bf16[2,2,48,256]{3,2,1,0:T(8,128)(2,1)S(1)} %get-tuple-element.109), channel_id=1, source_target_pairs={{0,4},{4,0},{10,14},{14,10},{1,9},{3,11},{5,13},{7,15},{9,1},{11,3... | collective-permute-start | bytes 294920 | tf_op jit(solution)/shard_map/ppermute | solution.py:610
  14.0 0.9 collective-permute-start.6
  14.8 0.7 collective-permute-start.7
  15.5 1.3 %copy-done = bf16[3,3,256,256]{3,2,1,0:T(8,128)(2,1)S(1)} copy-done((bf16[3,3,256,256]{3,2,1,0:T(8,128)(2,1)S(1)}, bf16[3,3,256,256]{3,2,1,0:T(8,128)(2,1)}, u32[]{:S(2)}) %copy-start) | copy-done | bytes 1179672
  16.8 1.3 %copy-done.6 = bf16[3,3,256,256]{3,2,1,0:T(8,128)(2,1)S(1)} copy-done((bf16[3,3,256,256]{3,2,1,0:T(8,128)(2,1)S(1)}, bf16[3,3,256,256]{3,2,1,0:T(8,128)(2,1)}, u32[]{:S(2)}) %copy-start.6) | copy-done | bytes 1179672
  18.0 0.7 shard_map.103
  18.7 2.9 %collective-permute-done.6.refs_4_ = bf16[2,2,48,256]{3,2,1,0:T(8,128)(2,1)S(1)} collective-permute-done((bf16[2,2,48,256]{3,2,1,0:T(8,128)(2,1)S(1)}, bf16[2,2,48,256]{3,2,1,0:T(8,128)(2,1)S(1)}, u32[]{:S(2)}, u32[]{:S(2)}) %collective-permute-start.6) | collective-permute-done | bytes 98336 | tf_op jit(solution)/shard_map/ppermute | solution.py:610
  21.7 4.5 %collective-permute-start.8 = (bf16[2,2,192,256]{3,2,1,0:T(8,128)(2,1)S(1)}, bf16[2,2,192,256]{3,2,1,0:T(8,128)(2,1)S(1)}, u32[]{:S(2)}, u32[]{:S(2)}) collective-permute-start(bf16[2,2,192,256]{3,2,1,0:T(8,128)(2,1)S(1)} %collective-permute-done.4.refs_0_), channel_id=1, source_target_pairs={{0,1},{1,0},{2,3},{3,2},{4,5},{5,4},{6,7},{7,6},{8,9},{9,8},{10,11... | collective-permute-start | bytes 1179656 | tf_op jit(solution)/shard_map/ppermute | solution.py:580
  26.2 0.5 collective-permute-start.10
  26.7 1.0 collective-permute-done.9.refs_3_
  27.6 0.1 collective-permute-done.10.refs_5_
  27.8 0.2 collective-permute-done.11.refs_7_
  28.0 8.3 %shard_map.104 = (bf16[9,128,256]{2,1,0:T(8,128)(2,1)S(1)}, f32[9,128,256]{2,1,0:T(8,128)S(1)}, bf16[9,128,256]{2,1,0:T(8,128)(2,1)S(1)}, f32[9,128,256]{2,1,0:T...) custom-call(s32[6,4]{1,0:T(8,128)S(1)} %copy.12.ep, ...), custom_call_target="tpu_custom_call" | custom-call | tf_op jit(solution)/shard_map/pallas_call | solution.py:566
  36.3 0.4 collective-permute-start.12
  36.7 0.2 collective-permute-start.36
  36.8 0.3 collective-permute-start.13
  37.2 2.0 %collective-permute-done.13.refs_1_ = bf16[8,256]{1,0:T(8,128)(2,1)S(1)} collective-permute-done((bf16[8,256]{1,0:T(8,128)(2,1)S(1)}, bf16[8,256]{1,0:T(8,128)(2,1)S(1)}, u32[]{:S(2)}, u32[]{:S(2)}) %collective-permute-start.13) | collective-permute-done | bytes 4128 | tf_op jit(solution)/shard_map/ppermute | solution.py:580
  39.2 0.1 shard_map.105
  39.4 0.4 collective-permute-start.15
  39.8 0.2 collective-permute-start.16
  40.0 0.3 collective-permute-start.17
  40.3 0.2 collective-permute-start.18
  40.5 0.1 shard_map.111
  40.6 0.4 collective-permute-done.16.refs_5_
  41.0 1.9 %collective-permute-start.37 = (bf16[576,256]{1,0:T(8,128)(2,1)S(1)}, bf16[576,256]{1,0:T(8,128)(2,1)S(1)}, u32[]{:S(2)}, u32[]{:S(2)}) collective-permute-start(bf16[576,256]{1,0:T(8,128)(2,1)S(1)} %get-tuple-element.190), channel_id=1, source_target_pairs={{0,2},{2,0},{4,6},{6,4},{8,10},{10,8},{12,14},{14,12},{1,3},{3,1},... | collective-permute-start | bytes 884744 | tf_op jit(solution)/shard_map/ppermute | solution.py:659
  43.0 2.8 %collective-permute-start.19 = (bf16[2,2,48,256]{3,2,1,0:T(8,128)(2,1)S(1)}, bf16[2,2,48,256]{3,2,1,0:T(8,128)(2,1)S(1)}, u32[]{:S(2)}, u32[]{:S(2)}) collective-permute-start(bf16[2,2,48,256]{3,2,1,0:T(8,128)(2,1)S(1)} %get-tuple-element.136), channel_id=1, source_target_pairs={{0,4},{4,0},{10,14},{14,10},{1,9},{3,11},{5,13},{7,15},{9,1},{11,3... | collective-permute-start | bytes 294920 | tf_op jit(solution)/shard_map/ppermute | solution.py:610
  45.8 1.3 %collective-permute-start.20 = (bf16[2,2,48,256]{3,2,1,0:T(8,128)(2,1)S(1)}, bf16[2,2,48,256]{3,2,1,0:T(8,128)(2,1)S(1)}, u32[]{:S(2)}, u32[]{:S(2)}) collective-permute-start(bf16[2,2,48,256]{3,2,1,0:T(8,128)(2,1)S(1)} %get-tuple-element.137), channel_id=1, source_target_pairs={{0,12},{2,14},{4,8},{6,10},{8,4},{10,6},{12,0},{14,2},{1,7},{3,13}... | collective-permute-start | bytes 294920 | tf_op jit(solution)/shard_map/ppermute | solution.py:610
  47.1 3.3 %collective-permute-done.19.refs_2_ = bf16[2,2,48,256]{3,2,1,0:T(8,128)(2,1)S(1)} collective-permute-done((bf16[2,2,48,256]{3,2,1,0:T(8,128)(2,1)S(1)}, bf16[2,2,48,256]{3,2,1,0:T(8,128)(2,1)S(1)}, u32[]{:S(2)}, u32[]{:S(2)}) %collective-permute-start.19) | collective-permute-done | bytes 98336 | tf_op jit(solution)/shard_map/ppermute | solution.py:610
  50.5 2.8 %collective-permute-done.20.refs_4_ = bf16[2,2,48,256]{3,2,1,0:T(8,128)(2,1)S(1)} collective-permute-done((bf16[2,2,48,256]{3,2,1,0:T(8,128)(2,1)S(1)}, bf16[2,2,48,256]{3,2,1,0:T(8,128)(2,1)S(1)}, u32[]{:S(2)}, u32[]{:S(2)}) %collective-permute-start.20) | collective-permute-done | bytes 98336 | tf_op jit(solution)/shard_map/ppermute | solution.py:610
  53.3 0.1 shard_map.107
  53.4 1.8 %collective-permute-start.24 = (bf16[2,2,192,256]{3,2,1,0:T(8,128)(2,1)S(1)}, bf16[2,2,192,256]{3,2,1,0:T(8,128)(2,1)S(1)}, u32[]{:S(2)}, u32[]{:S(2)}) collective-permute-start(bf16[2,2,192,256]{3,2,1,0:T(8,128)(2,1)S(1)} %get-tuple-element.149), channel_id=1, source_target_pairs={{0,2},{2,0},{4,6},{6,4},{8,10},{10,8},{12,14},{14,12},{1,15},{3,5}... | collective-permute-start | bytes 1179656 | tf_op jit(solution)/shard_map/ppermute | solution.py:610
  55.2 0.9 collective-permute-done.37.recv_ref
  56.2 1.0 collective-permute-start.38
  57.2 7.1 %collective-permute-start.39 = (bf16[144,256]{1,0:T(8,128)(2,1)S(1)}, bf16[144,256]{1,0:T(8,128)(2,1)S(1)}, u32[]{:S(2)}, u32[]{:S(2)}) collective-permute-start(bf16[144,256]{1,0:T(8,128)(2,1)S(1)} %get-tuple-element.193), channel_id=1, source_target_pairs={{0,8},{2,10},{4,12},{6,14},{8,0},{10,2},{12,4},{14,6},{1,9},{3,11}... | collective-permute-start | bytes 221192 | tf_op jit(solution)/shard_map/ppermute | solution.py:662
  64.3 0.6 collective-permute-start.21
  64.9 3.8 %collective-permute-start.22 = (bf16[152,256]{1,0:T(8,128)(2,1)S(1)}, bf16[152,256]{1,0:T(8,128)(2,1)S(1)}, u32[]{:S(2)}, u32[]{:S(2)}) collective-permute-start(bf16[152,256]{1,0:T(8,128)(2,1)S(1)} %get-tuple-element.147), channel_id=1, source_target_pairs={{0,8},{2,10},{4,12},{6,14},{8,0},{10,2},{12,4},{14,6},{1,9},{3,11}... | collective-permute-start | bytes 233480 | tf_op jit(solution)/shard_map/ppermute | solution.py:662
  68.7 0.7 collective-permute-done.39.refs_1_
  69.4 4.7 %collective-permute-start.23 = (bf16[152,256]{1,0:T(8,128)(2,1)S(1)}, bf16[152,256]{1,0:T(8,128)(2,1)S(1)}, u32[]{:S(2)}, u32[]{:S(2)}) collective-permute-start(bf16[152,256]{1,0:T(8,128)(2,1)S(1)} %get-tuple-element.148), channel_id=1, source_target_pairs={{0,12},{2,14},{4,8},{6,10},{8,4},{10,6},{12,0},{14,2},{1,13},{3,15... | collective-permute-start | bytes 233480 | tf_op jit(solution)/shard_map/ppermute | solution.py:662
  74.2 0.8 collective-permute-start.25
  75.2 2.4 %collective-permute-done.22.refs_1_ = bf16[152,256]{1,0:T(8,128)(2,1)S(1)} collective-permute-done((bf16[152,256]{1,0:T(8,128)(2,1)S(1)}, bf16[152,256]{1,0:T(8,128)(2,1)S(1)}, u32[]{:S(2)}, u32[]{:S(2)}) %collective-permute-start.22) | collective-permute-done | bytes 77856 | tf_op jit(solution)/shard_map/ppermute | solution.py:662
  77.6 1.5 %collective-permute-start.42 = (bf16[144,256]{1,0:T(8,128)(2,1)S(1)}, bf16[144,256]{1,0:T(8,128)(2,1)S(1)}, u32[]{:S(2)}, u32[]{:S(2)}) collective-permute-start(bf16[144,256]{1,0:T(8,128)(2,1)S(1)} %shard_map.113), channel_id=1, source_target_pairs={{0,8},{2,10},{4,12},{6,14},{8,0},{10,2},{12,4},{14,6},{1,9},{3,11}... | collective-permute-start | bytes 221192 | tf_op jit(solution)/shard_map/ppermute | solution.py:662
  79.1 4.5 %collective-permute-start.41 = (bf16[144,256]{1,0:T(8,128)(2,1)S(1)}, bf16[144,256]{1,0:T(8,128)(2,1)S(1)}, u32[]{:S(2)}, u32[]{:S(2)}) collective-permute-start(bf16[144,256]{1,0:T(8,128)(2,1)S(1)} %shard_map.113), channel_id=1, source_target_pairs={{0,4},{2,6},{4,0},{6,2},{8,12},{10,14},{12,8},{14,10},{1,5},{3,7},... | collective-permute-start | bytes 221192 | tf_op jit(solution)/shard_map/ppermute | solution.py:662
  83.6 0.5 collective-permute-start.31
  84.2 1.7 %collective-permute-done.41 = bf16[144,256]{1,0:T(8,128)(2,1)S(1)} collective-permute-done((bf16[144,256]{1,0:T(8,128)(2,1)S(1)}, bf16[144,256]{1,0:T(8,128)(2,1)S(1)}, u32[]{:S(2)}, u32[]{:S(2)}) %collective-permute-start.41) | collective-permute-done | bytes 73760 | tf_op jit(solution)/shard_map/ppermute | solution.py:662
  86.0 3.5 %collective-permute-start.28 = (bf16[144,256]{1,0:T(8,128)(2,1)S(1)}, bf16[144,256]{1,0:T(8,128)(2,1)S(1)}, u32[]{:S(2)}, u32[]{:S(2)}) collective-permute-start(bf16[144,256]{1,0:T(8,128)(2,1)S(1)} %get-tuple-element.155), channel_id=1, source_target_pairs={{0,12},{2,14},{4,8},{6,10},{8,4},{10,6},{12,0},{14,2},{1,13},{3,15... | collective-permute-start | bytes 221192 | tf_op jit(solution)/shard_map/ppermute | solution.py:662
  89.5 4.3 %collective-permute-done.26 = bf16[144,256]{1,0:T(8,128)(2,1)S(1)} collective-permute-done((bf16[144,256]{1,0:T(8,128)(2,1)S(1)}, bf16[144,256]{1,0:T(8,128)(2,1)S(1)}, u32[]{:S(2)}, u32[]{:S(2)}) %collective-permute-start.26) | collective-permute-done | bytes 73760 | tf_op jit(solution)/shard_map/ppermute | solution.py:662
  93.9 6.0 %collective-permute-done.27 = bf16[144,256]{1,0:T(8,128)(2,1)S(1)} collective-permute-done((bf16[144,256]{1,0:T(8,128)(2,1)S(1)}, bf16[144,256]{1,0:T(8,128)(2,1)S(1)}, u32[]{:S(2)}, u32[]{:S(2)}) %collective-permute-start.27) | collective-permute-done | bytes 73760 | tf_op jit(solution)/shard_map/ppermute | solution.py:662
  100.1 1.2 collective-permute-done.32.refs_7_
  101.2 0.9 collective-permute-start.33
  102.2 7.7 %collective-permute-done.44.refs_1_ = bf16[576,256]{1,0:T(8,128)(2,1)S(1)} collective-permute-done((bf16[576,256]{1,0:T(8,128)(2,1)S(1)}, bf16[576,256]{1,0:T(8,128)(2,1)S(1)}, u32[]{:S(2)}, u32[]{:S(2)}) %collective-permute-start.44) | collective-permute-done | bytes 294944 | tf_op jit(solution)/shard_map/ppermute | solution.py:659
  109.8 0.5 collective-permute-start.34
  110.3 5.6 %shard_map.109 = (bf16[18,24,256]{2,1,0:T(8,128)(2,1)}, f32[18,24,256]{2,1,0:T(8,128)}) custom-call(s32[6,4]{1,0:T(8,128)S(1)} %copy.12.ep, bf16[18,24,256]{2,1,0:T(8,128)(2,1)S(1)} %bitcast.20, bf16[18,24,256]{2,1,0:T(8,128)(2,1)S(1)} %bitcast.23, bf16[18,24,256]{2,1,0:T(8,128)(2,1)S(1)} %get-tuple-element.161.hid_ref, ...), custom_call_target="tpu_custom_call" | custom-call | tf_op jit(solution)/shard_map/pallas_call | solution.py:566
  116.0 1.8 %shard_map.114 = f32[9,256,256]{2,1,0:T(8,128)} custom-call(bf16[576,256]{1,0:T(8,128)(2,1)S(1)} %pad_maximum_fusion.refs_0_, bf16[576,256]{1,0:T(8,128)(2,1)S(1)} %collective-permute-done.44.refs_1_, bf16[576,256]{1,0:T(8,128)(2,1)S(1)} %collective-permute-done.45.refs_2_, bf16[576,256]{1,0:T(8,128)(2,1)S(1)} %collective-permute-done.46.refs_3_), custom_call_target="tpu_custom_call" | custom-call | tf_op jit(solution)/shard_map/pallas_call | solution.py:566
  117.8 1.8 %shard_map.110 = (f32[9,256,256]{2,1,0:T(8,128)}, f32[1,256]{1,0:T(1,128)}) custom-call(bf16[576,256]{1,0:T(8,128)(2,1)S(1)} %constant_dynamic-update-slice_fusion.refs_0_, bf16[576,256]{1,0:T(8,128)(2,1)S(1)} %collective-permute-done.33.refs_1_, bf16[576,256]{1,0:T(8,128)(2,1)S(1)} %collective-permute-done.34.refs_2_, ...), custom_call_target="tpu_custom_call" | custom-call | tf_op jit(solution)/shard_map/pallas_call | solution.py:566
  (66 shorter events, 0.9 us)
Async XLA Ops:
  1.4 0.9 copy-start.2
  2.3 0.9 copy-start.4
  5.4 2.3 %collective-permute-start = (bf16[2,192,256]{2,1,0:T(8,128)(2,1)S(1)}, bf16[2,192,256]{2,1,0:T(8,128)(2,1)S(1)}, u32[]{:S(2)}, u32[]{:S(2)}) collective-permute-start(bf16[2,192,256]{2,1,0:T(8,128)(2,1)S(1)} %get-tuple-element.104), channel_id=1, source_target_pairs={{0,1},{1,0},{2,3},{3,2},{4,5},{5,4},{6,7},{7,6},{8,9},{9,8},{10,11... | collective-permute-start | bytes 589832 | tf_op jit(solution)/shard_map/ppermute | solution.py:580
  6.0 1.2 %collective-permute-start.1 = (bf16[2,48,256]{2,1,0:T(8,128)(2,1)S(1)}, bf16[2,48,256]{2,1,0:T(8,128)(2,1)S(1)}, u32[]{:S(2)}, u32[]{:S(2)}) collective-permute-start(bf16[2,48,256]{2,1,0:T(8,128)(2,1)S(1)} %get-tuple-element.105), channel_id=1, source_target_pairs={{0,1},{1,0},{2,3},{3,2},{4,5},{5,4},{6,7},{7,6},{8,9},{9,8},{10,11... | collective-permute-start | bytes 147464 | tf_op jit(solution)/shard_map/ppermute | solution.py:580
  6.0 1.3 %collective-permute-start.2 = (bf16[2,48,256]{2,1,0:T(8,128)(2,1)S(1)}, bf16[2,48,256]{2,1,0:T(8,128)(2,1)S(1)}, u32[]{:S(2)}, u32[]{:S(2)}) collective-permute-start(bf16[2,48,256]{2,1,0:T(8,128)(2,1)S(1)} %get-tuple-element.106), channel_id=1, source_target_pairs={{0,1},{1,0},{2,3},{3,2},{4,5},{5,4},{6,7},{7,6},{8,9},{9,8},{10,11... | collective-permute-start | bytes 147464 | tf_op jit(solution)/shard_map/ppermute | solution.py:580
  6.5 1.2 %collective-permute-start.3 = (bf16[2,48,256]{2,1,0:T(8,128)(2,1)S(1)}, bf16[2,48,256]{2,1,0:T(8,128)(2,1)S(1)}, u32[]{:S(2)}, u32[]{:S(2)}) collective-permute-start(bf16[2,48,256]{2,1,0:T(8,128)(2,1)S(1)} %get-tuple-element.107), channel_id=1, source_target_pairs={{0,1},{1,0},{2,3},{3,2},{4,5},{5,4},{6,7},{7,6},{8,9},{9,8},{10,11... | collective-permute-start | bytes 147464 | tf_op jit(solution)/shard_map/ppermute | solution.py:580
  7.7 13.9 %collective-permute-start.4 = (bf16[2,2,192,256]{3,2,1,0:T(8,128)(2,1)S(1)}, bf16[2,2,192,256]{3,2,1,0:T(8,128)(2,1)S(1)}, u32[]{:S(2)}, u32[]{:S(2)}) collective-permute-start(bf16[2,2,192,256]{3,2,1,0:T(8,128)(2,1)S(1)} %get-tuple-element.108), channel_id=1, source_target_pairs={{0,2},{2,0},{4,6},{6,4},{8,10},{10,8},{12,14},{14,12},{1,15},{3,5}... | collective-permute-start | bytes 1179656 | tf_op jit(solution)/shard_map/ppermute | solution.py:610
  10.5 8.2 %collective-permute-start.5 = (bf16[2,2,48,256]{3,2,1,0:T(8,128)(2,1)S(1)}, bf16[2,2,48,256]{3,2,1,0:T(8,128)(2,1)S(1)}, u32[]{:S(2)}, u32[]{:S(2)}) collective-permute-start(bf16[2,2,48,256]{3,2,1,0:T(8,128)(2,1)S(1)} %get-tuple-element.109), channel_id=1, source_target_pairs={{0,4},{4,0},{10,14},{14,10},{1,9},{3,11},{5,13},{7,15},{9,1},{11,3... | collective-permute-start | bytes 294920 | tf_op jit(solution)/shard_map/ppermute | solution.py:610
  14.0 7.7 %collective-permute-start.6 = (bf16[2,2,48,256]{3,2,1,0:T(8,128)(2,1)S(1)}, bf16[2,2,48,256]{3,2,1,0:T(8,128)(2,1)S(1)}, u32[]{:S(2)}, u32[]{:S(2)}) collective-permute-start(bf16[2,2,48,256]{3,2,1,0:T(8,128)(2,1)S(1)} %get-tuple-element.110), channel_id=1, source_target_pairs={{0,12},{2,14},{4,8},{6,10},{8,4},{10,6},{12,0},{14,2},{1,7},{3,13}... | collective-permute-start | bytes 294920 | tf_op jit(solution)/shard_map/ppermute | solution.py:610
  14.8 6.8 %collective-permute-start.7 = (bf16[2,2,48,256]{3,2,1,0:T(8,128)(2,1)S(1)}, bf16[2,2,48,256]{3,2,1,0:T(8,128)(2,1)S(1)}, u32[]{:S(2)}, u32[]{:S(2)}) collective-permute-start(bf16[2,2,48,256]{3,2,1,0:T(8,128)(2,1)S(1)} %get-tuple-element.111), channel_id=1, source_target_pairs={{1,11},{5,15},{11,1},{15,5},{17,27},{21,31},{27,17},{31,21}} | collective-permute-start | bytes 294920 | tf_op jit(solution)/shard_map/ppermute | solution.py:610
  15.5 1.3 %copy-start = (bf16[3,3,256,256]{3,2,1,0:T(8,128)(2,1)S(1)}, bf16[3,3,256,256]{3,2,1,0:T(8,128)(2,1)}, u32[]{:S(2)}) copy-start(bf16[3,3,256,256]{3,2,1,0:T(8,128)(2,1)} %param.10) | copy-start | bytes 3538948
  16.8 1.3 %copy-start.6 = (bf16[3,3,256,256]{3,2,1,0:T(8,128)(2,1)S(1)}, bf16[3,3,256,256]{3,2,1,0:T(8,128)(2,1)}, u32[]{:S(2)}) copy-start(bf16[3,3,256,256]{3,2,1,0:T(8,128)(2,1)} %param.8) | copy-start | bytes 3538948
  18.0 9.9 %copy-start.3 = (bf16[1,6,3,24,256]{4,3,2,1,0:T(8,128)(2,1)S(1)}, bf16[1,6,3,24,256]{4,3,2,1,0:T(8,128)(2,1)}, u32[]{:S(2)}) copy-start(bf16[1,6,3,24,256]{4,3,2,1,0:T(8,128)(2,1)} %param.6) | copy-start | bytes 663556
  18.0 9.9 %copy-start.5 = (bf16[1,1,6,3,24,256]{5,4,3,2,1,0:T(8,128)(2,1)S(1)}, bf16[1,1,6,3,24,256]{5,4,3,2,1,0:T(8,128)(2,1)}, u32[]{:S(2)}) copy-start(bf16[1,1,6,3,24,256]{5,4,3,2,1,0:T(8,128)(2,1)} %param.7) | copy-start | bytes 663556
  18.0 9.9 %copy-start.7 = (f32[256]{0:T(256)S(1)}, f32[256]{0:T(256)}, u32[]{:S(2)}) copy-start(f32[256]{0:T(256)} %param.9) | copy-start | bytes 3076
  21.7 6.3 %collective-permute-start.8 = (bf16[2,2,192,256]{3,2,1,0:T(8,128)(2,1)S(1)}, bf16[2,2,192,256]{3,2,1,0:T(8,128)(2,1)S(1)}, u32[]{:S(2)}, u32[]{:S(2)}) collective-permute-start(bf16[2,2,192,256]{3,2,1,0:T(8,128)(2,1)S(1)} %collective-permute-done.4.refs_0_), channel_id=1, source_target_pairs={{0,1},{1,0},{2,3},{3,2},{4,5},{5,4},{6,7},{7,6},{8,9},{9,8},{10,11... | collective-permute-start | bytes 1179656 | tf_op jit(solution)/shard_map/ppermute | solution.py:580
  26.1 1.5 %collective-permute-start.9 = (bf16[2,2,48,256]{3,2,1,0:T(8,128)(2,1)S(1)}, bf16[2,2,48,256]{3,2,1,0:T(8,128)(2,1)S(1)}, u32[]{:S(2)}, u32[]{:S(2)}) collective-permute-start(bf16[2,2,48,256]{3,2,1,0:T(8,128)(2,1)S(1)} %collective-permute-done.5.refs_2_), channel_id=1, source_target_pairs={{0,1},{1,0},{2,3},{3,2},{4,5},{5,4},{6,7},{7,6},{8,9},{9,8},{10,11... | collective-permute-start | bytes 294920 | tf_op jit(solution)/shard_map/ppermute | solution.py:580
  26.2 1.6 %collective-permute-start.10 = (bf16[2,2,48,256]{3,2,1,0:T(8,128)(2,1)S(1)}, bf16[2,2,48,256]{3,2,1,0:T(8,128)(2,1)S(1)}, u32[]{:S(2)}, u32[]{:S(2)}) collective-permute-start(bf16[2,2,48,256]{3,2,1,0:T(8,128)(2,1)S(1)} %collective-permute-done.6.refs_4_), channel_id=1, source_target_pairs={{0,1},{1,0},{2,3},{3,2},{4,5},{5,4},{6,7},{7,6},{8,9},{9,8},{10,11... | collective-permute-start | bytes 294920 | tf_op jit(solution)/shard_map/ppermute | solution.py:580
  26.7 1.3 %collective-permute-start.11 = (bf16[2,2,48,256]{3,2,1,0:T(8,128)(2,1)S(1)}, bf16[2,2,48,256]{3,2,1,0:T(8,128)(2,1)S(1)}, u32[]{:S(2)}, u32[]{:S(2)}) collective-permute-start(bf16[2,2,48,256]{3,2,1,0:T(8,128)(2,1)S(1)} %collective-permute-done.7.refs_6_), channel_id=1, source_target_pairs={{0,1},{1,0},{2,3},{3,2},{4,5},{5,4},{6,7},{7,6},{8,9},{9,8},{10,11... | collective-permute-start | bytes 294920 | tf_op jit(solution)/shard_map/ppermute | solution.py:580
  36.3 2.9 %collective-permute-start.12 = (bf16[9,128,256]{2,1,0:T(8,128)(2,1)S(1)}, bf16[9,128,256]{2,1,0:T(8,128)(2,1)S(1)}, u32[]{:S(2)}, u32[]{:S(2)}) collective-permute-start(bf16[9,128,256]{2,1,0:T(8,128)(2,1)S(1)} %get-tuple-element.123), channel_id=1, source_target_pairs={{0,1},{1,0},{2,3},{3,2},{4,5},{5,4},{6,7},{7,6},{8,9},{9,8},{10,11... | collective-permute-start | bytes 1769480 | tf_op jit(solution)/shard_map/ppermute | solution.py:580
  36.7 3.7 %collective-permute-start.36 = (bf16[9,128,256]{2,1,0:T(8,128)(2,1)S(1)}, bf16[9,128,256]{2,1,0:T(8,128)(2,1)S(1)}, u32[]{:S(2)}, u32[]{:S(2)}) collective-permute-start(bf16[9,128,256]{2,1,0:T(8,128)(2,1)S(1)} %get-tuple-element.188), channel_id=1, source_target_pairs={{0,1},{1,0},{2,3},{3,2},{4,5},{5,4},{6,7},{7,6},{8,9},{9,8},{10,11... | collective-permute-start | bytes 1769480 | tf_op jit(solution)/shard_map/ppermute | solution.py:580
  36.8 2.3 %collective-permute-start.13 = (bf16[8,256]{1,0:T(8,128)(2,1)S(1)}, bf16[8,256]{1,0:T(8,128)(2,1)S(1)}, u32[]{:S(2)}, u32[]{:S(2)}) collective-permute-start(bf16[8,256]{1,0:T(8,128)(2,1)S(1)} %get-tuple-element.125), channel_id=1, source_target_pairs={{0,1},{1,0},{2,3},{3,2},{4,5},{5,4},{6,7},{7,6},{8,9},{9,8},{10,11... | collective-permute-start | bytes 12296 | tf_op jit(solution)/shard_map/ppermute | solution.py:580
  39.3 14.0 %collective-permute-start.14 = (bf16[584,256]{1,0:T(8,128)(2,1)S(1)}, bf16[584,256]{1,0:T(8,128)(2,1)S(1)}, u32[]{:S(2)}, u32[]{:S(2)}) collective-permute-start(bf16[584,256]{1,0:T(8,128)(2,1)S(1)} %get-tuple-element.127), channel_id=1, source_target_pairs={{0,2},{2,0},{4,6},{6,4},{8,10},{10,8},{12,14},{14,12},{1,3},{3,1},... | collective-permute-start | bytes 897032 | tf_op jit(solution)/shard_map/ppermute | solution.py:659
  39.4 3.5 %collective-permute-start.15 = (bf16[2,192,256]{2,1,0:T(8,128)(2,1)S(1)}, bf16[2,192,256]{2,1,0:T(8,128)(2,1)S(1)}, u32[]{:S(2)}, u32[]{:S(2)}) collective-permute-start(bf16[2,192,256]{2,1,0:T(8,128)(2,1)S(1)} %get-tuple-element.132), channel_id=1, source_target_pairs={{0,1},{1,0},{2,3},{3,2},{4,5},{5,4},{6,7},{7,6},{8,9},{9,8},{10,11... | collective-permute-start | bytes 589832 | tf_op jit(solution)/shard_map/ppermute | solution.py:580
  39.8 1.2 %collective-permute-start.16 = (bf16[2,48,256]{2,1,0:T(8,128)(2,1)S(1)}, bf16[2,48,256]{2,1,0:T(8,128)(2,1)S(1)}, u32[]{:S(2)}, u32[]{:S(2)}) collective-permute-start(bf16[2,48,256]{2,1,0:T(8,128)(2,1)S(1)} %get-tuple-element.133), channel_id=1, source_target_pairs={{0,1},{1,0},{2,3},{3,2},{4,5},{5,4},{6,7},{7,6},{8,9},{9,8},{10,11... | collective-permute-start | bytes 147464 | tf_op jit(solution)/shard_map/ppermute | solution.py:580
  40.0 3.0 %collective-permute-start.17 = (bf16[2,48,256]{2,1,0:T(8,128)(2,1)S(1)}, bf16[2,48,256]{2,1,0:T(8,128)(2,1)S(1)}, u32[]{:S(2)}, u32[]{:S(2)}) collective-permute-start(bf16[2,48,256]{2,1,0:T(8,128)(2,1)S(1)} %get-tuple-element.134), channel_id=1, source_target_pairs={{0,1},{1,0},{2,3},{3,2},{4,5},{5,4},{6,7},{7,6},{8,9},{9,8},{10,11... | collective-permute-start | bytes 147464 | tf_op jit(solution)/shard_map/ppermute | solution.py:580
  40.3 2.6 %collective-permute-start.18 = (bf16[2,48,256]{2,1,0:T(8,128)(2,1)S(1)}, bf16[2,48,256]{2,1,0:T(8,128)(2,1)S(1)}, u32[]{:S(2)}, u32[]{:S(2)}) collective-permute-start(bf16[2,48,256]{2,1,0:T(8,128)(2,1)S(1)} %get-tuple-element.135), channel_id=1, source_target_pairs={{0,1},{1,0},{2,3},{3,2},{4,5},{5,4},{6,7},{7,6},{8,9},{9,8},{10,11... | collective-permute-start | bytes 147464 | tf_op jit(solution)/shard_map/ppermute | solution.py:580
  41.0 15.1 %collective-permute-start.37 = (bf16[576,256]{1,0:T(8,128)(2,1)S(1)}, bf16[576,256]{1,0:T(8,128)(2,1)S(1)}, u32[]{:S(2)}, u32[]{:S(2)}) collective-permute-start(bf16[576,256]{1,0:T(8,128)(2,1)S(1)} %get-tuple-element.190), channel_id=1, source_target_pairs={{0,2},{2,0},{4,6},{6,4},{8,10},{10,8},{12,14},{14,12},{1,3},{3,1},... | collective-permute-start | bytes 884744 | tf_op jit(solution)/shard_map/ppermute | solution.py:659
  43.0 7.4 %collective-permute-start.19 = (bf16[2,2,48,256]{3,2,1,0:T(8,128)(2,1)S(1)}, bf16[2,2,48,256]{3,2,1,0:T(8,128)(2,1)S(1)}, u32[]{:S(2)}, u32[]{:S(2)}) collective-permute-start(bf16[2,2,48,256]{3,2,1,0:T(8,128)(2,1)S(1)} %get-tuple-element.136), channel_id=1, source_target_pairs={{0,4},{4,0},{10,14},{14,10},{1,9},{3,11},{5,13},{7,15},{9,1},{11,3... | collective-permute-start | bytes 294920 | tf_op jit(solution)/shard_map/ppermute | solution.py:610
  45.8 7.5 %collective-permute-start.20 = (bf16[2,2,48,256]{3,2,1,0:T(8,128)(2,1)S(1)}, bf16[2,2,48,256]{3,2,1,0:T(8,128)(2,1)S(1)}, u32[]{:S(2)}, u32[]{:S(2)}) collective-permute-start(bf16[2,2,48,256]{3,2,1,0:T(8,128)(2,1)S(1)} %get-tuple-element.137), channel_id=1, source_target_pairs={{0,12},{2,14},{4,8},{6,10},{8,4},{10,6},{12,0},{14,2},{1,7},{3,13}... | collective-permute-start | bytes 294920 | tf_op jit(solution)/shard_map/ppermute | solution.py:610
  53.4 30.2 %collective-permute-start.24 = (bf16[2,2,192,256]{3,2,1,0:T(8,128)(2,1)S(1)}, bf16[2,2,192,256]{3,2,1,0:T(8,128)(2,1)S(1)}, u32[]{:S(2)}, u32[]{:S(2)}) collective-permute-start(bf16[2,2,192,256]{3,2,1,0:T(8,128)(2,1)S(1)} %get-tuple-element.149), channel_id=1, source_target_pairs={{0,2},{2,0},{4,6},{6,4},{8,10},{10,8},{12,14},{14,12},{1,15},{3,5}... | collective-permute-start | bytes 1179656 | tf_op jit(solution)/shard_map/ppermute | solution.py:610
  56.2 54.1 %copy-start.1 = (bf16[3,3,256,256]{3,2,1,0:T(8,128)(2,1)S(1)}, bf16[3,3,256,256]{3,2,1,0:T(8,128)(2,1)}, u32[]{:S(2)}) copy-start(bf16[3,3,256,256]{3,2,1,0:T(8,128)(2,1)} %param.10) | copy-start | bytes 3538948
  56.2 8.7 %collective-permute-start.38 = (bf16[144,256]{1,0:T(8,128)(2,1)S(1)}, bf16[144,256]{1,0:T(8,128)(2,1)S(1)}, u32[]{:S(2)}, u32[]{:S(2)}) collective-permute-start(bf16[144,256]{1,0:T(8,128)(2,1)S(1)} %get-tuple-element.192), channel_id=1, source_target_pairs={{0,4},{2,6},{4,0},{6,2},{8,12},{10,14},{12,8},{14,10},{1,5},{3,7},... | collective-permute-start | bytes 221192 | tf_op jit(solution)/shard_map/ppermute | solution.py:662
  57.2 12.2 %collective-permute-start.39 = (bf16[144,256]{1,0:T(8,128)(2,1)S(1)}, bf16[144,256]{1,0:T(8,128)(2,1)S(1)}, u32[]{:S(2)}, u32[]{:S(2)}) collective-permute-start(bf16[144,256]{1,0:T(8,128)(2,1)S(1)} %get-tuple-element.193), channel_id=1, source_target_pairs={{0,8},{2,10},{4,12},{6,14},{8,0},{10,2},{12,4},{14,6},{1,9},{3,11}... | collective-permute-start | bytes 221192 | tf_op jit(solution)/shard_map/ppermute | solution.py:662
  64.3 9.9 %collective-permute-start.40 = (bf16[144,256]{1,0:T(8,128)(2,1)S(1)}, bf16[144,256]{1,0:T(8,128)(2,1)S(1)}, u32[]{:S(2)}, u32[]{:S(2)}) collective-permute-start(bf16[144,256]{1,0:T(8,128)(2,1)S(1)} %get-tuple-element.194), channel_id=1, source_target_pairs={{0,12},{2,14},{4,8},{6,10},{8,4},{10,6},{12,0},{14,2},{1,13},{3,15... | collective-permute-start | bytes 221192 | tf_op jit(solution)/shard_map/ppermute | solution.py:662
  64.3 10.7 %collective-permute-start.21 = (bf16[152,256]{1,0:T(8,128)(2,1)S(1)}, bf16[152,256]{1,0:T(8,128)(2,1)S(1)}, u32[]{:S(2)}, u32[]{:S(2)}) collective-permute-start(bf16[152,256]{1,0:T(8,128)(2,1)S(1)} %get-tuple-element.146), channel_id=1, source_target_pairs={{0,4},{2,6},{4,0},{6,2},{8,12},{10,14},{12,8},{14,10},{1,5},{3,7},... | collective-permute-start | bytes 233480 | tf_op jit(solution)/shard_map/ppermute | solution.py:662
  64.9 12.7 %collective-permute-start.22 = (bf16[152,256]{1,0:T(8,128)(2,1)S(1)}, bf16[152,256]{1,0:T(8,128)(2,1)S(1)}, u32[]{:S(2)}, u32[]{:S(2)}) collective-permute-start(bf16[152,256]{1,0:T(8,128)(2,1)S(1)} %get-tuple-element.147), channel_id=1, source_target_pairs={{0,8},{2,10},{4,12},{6,14},{8,0},{10,2},{12,4},{14,6},{1,9},{3,11}... | collective-permute-start | bytes 233480 | tf_op jit(solution)/shard_map/ppermute | solution.py:662
  69.4 9.7 %collective-permute-start.23 = (bf16[152,256]{1,0:T(8,128)(2,1)S(1)}, bf16[152,256]{1,0:T(8,128)(2,1)S(1)}, u32[]{:S(2)}, u32[]{:S(2)}) collective-permute-start(bf16[152,256]{1,0:T(8,128)(2,1)S(1)} %get-tuple-element.148), channel_id=1, source_target_pairs={{0,12},{2,14},{4,8},{6,10},{8,4},{10,6},{12,0},{14,2},{1,13},{3,15... | collective-permute-start | bytes 233480 | tf_op jit(solution)/shard_map/ppermute | solution.py:662
  74.2 9.4 %collective-permute-start.25 = (bf16[2,2,48,256]{3,2,1,0:T(8,128)(2,1)S(1)}, bf16[2,2,48,256]{3,2,1,0:T(8,128)(2,1)S(1)}, u32[]{:S(2)}, u32[]{:S(2)}) collective-permute-start(bf16[2,2,48,256]{3,2,1,0:T(8,128)(2,1)S(1)} %get-tuple-element.150), channel_id=1, source_target_pairs={{1,11},{5,15},{11,1},{15,5},{17,27},{21,31},{27,17},{31,21}} | collective-permute-start | bytes 294920 | tf_op jit(solution)/shard_map/ppermute | solution.py:610
  75.1 9.1 %collective-permute-start.43 = (bf16[144,256]{1,0:T(8,128)(2,1)S(1)}, bf16[144,256]{1,0:T(8,128)(2,1)S(1)}, u32[]{:S(2)}, u32[]{:S(2)}) collective-permute-start(bf16[144,256]{1,0:T(8,128)(2,1)S(1)} %shard_map.113), channel_id=1, source_target_pairs={{0,12},{2,14},{4,8},{6,10},{8,4},{10,6},{12,0},{14,2},{1,13},{3,15... | collective-permute-start | bytes 221192 | tf_op jit(solution)/shard_map/ppermute | solution.py:662
  77.6 6.6 %collective-permute-start.42 = (bf16[144,256]{1,0:T(8,128)(2,1)S(1)}, bf16[144,256]{1,0:T(8,128)(2,1)S(1)}, u32[]{:S(2)}, u32[]{:S(2)}) collective-permute-start(bf16[144,256]{1,0:T(8,128)(2,1)S(1)} %shard_map.113), channel_id=1, source_target_pairs={{0,8},{2,10},{4,12},{6,14},{8,0},{10,2},{12,4},{14,6},{1,9},{3,11}... | collective-permute-start | bytes 221192 | tf_op jit(solution)/shard_map/ppermute | solution.py:662
  79.1 6.8 %collective-permute-start.41 = (bf16[144,256]{1,0:T(8,128)(2,1)S(1)}, bf16[144,256]{1,0:T(8,128)(2,1)S(1)}, u32[]{:S(2)}, u32[]{:S(2)}) collective-permute-start(bf16[144,256]{1,0:T(8,128)(2,1)S(1)} %shard_map.113), channel_id=1, source_target_pairs={{0,4},{2,6},{4,0},{6,2},{8,12},{10,14},{12,8},{14,10},{1,5},{3,7},... | collective-permute-start | bytes 221192 | tf_op jit(solution)/shard_map/ppermute | solution.py:662
  83.6 16.3 %collective-permute-start.30 = (bf16[2,2,48,256]{3,2,1,0:T(8,128)(2,1)S(1)}, bf16[2,2,48,256]{3,2,1,0:T(8,128)(2,1)S(1)}, u32[]{:S(2)}, u32[]{:S(2)}) collective-permute-start(bf16[2,2,48,256]{3,2,1,0:T(8,128)(2,1)S(1)} %collective-permute-done.19.refs_2_), channel_id=1, source_target_pairs={{0,1},{1,0},{2,3},{3,2},{4,5},{5,4},{6,7},{7,6},{8,9},{9,8},{10,11... | collective-permute-start | bytes 294920 | tf_op jit(solution)/shard_map/ppermute | solution.py:580
  83.6 16.4 %collective-permute-start.31 = (bf16[2,2,48,256]{3,2,1,0:T(8,128)(2,1)S(1)}, bf16[2,2,48,256]{3,2,1,0:T(8,128)(2,1)S(1)}, u32[]{:S(2)}, u32[]{:S(2)}) collective-permute-start(bf16[2,2,48,256]{3,2,1,0:T(8,128)(2,1)S(1)} %collective-permute-done.20.refs_4_), channel_id=1, source_target_pairs={{0,1},{1,0},{2,3},{3,2},{4,5},{5,4},{6,7},{7,6},{8,9},{9,8},{10,11... | collective-permute-start | bytes 294920 | tf_op jit(solution)/shard_map/ppermute | solution.py:580
  84.1 17.1 %collective-permute-start.29 = (bf16[2,2,192,256]{3,2,1,0:T(8,128)(2,1)S(1)}, bf16[2,2,192,256]{3,2,1,0:T(8,128)(2,1)S(1)}, u32[]{:S(2)}, u32[]{:S(2)}) collective-permute-start(bf16[2,2,192,256]{3,2,1,0:T(8,128)(2,1)S(1)} %collective-permute-done.24.refs_0_), channel_id=1, source_target_pairs={{0,1},{1,0},{2,3},{3,2},{4,5},{5,4},{6,7},{7,6},{8,9},{9,8},{10,11... | collective-permute-start | bytes 1179656 | tf_op jit(solution)/shard_map/ppermute | solution.py:580
  86.0 14.0 %collective-permute-start.28 = (bf16[144,256]{1,0:T(8,128)(2,1)S(1)}, bf16[144,256]{1,0:T(8,128)(2,1)S(1)}, u32[]{:S(2)}, u32[]{:S(2)}) collective-permute-start(bf16[144,256]{1,0:T(8,128)(2,1)S(1)} %get-tuple-element.155), channel_id=1, source_target_pairs={{0,12},{2,14},{4,8},{6,10},{8,4},{10,6},{12,0},{14,2},{1,13},{3,15... | collective-permute-start | bytes 221192 | tf_op jit(solution)/shard_map/ppermute | solution.py:662
  89.5 4.4 %collective-permute-start.26 = (bf16[144,256]{1,0:T(8,128)(2,1)S(1)}, bf16[144,256]{1,0:T(8,128)(2,1)S(1)}, u32[]{:S(2)}, u32[]{:S(2)}) collective-permute-start(bf16[144,256]{1,0:T(8,128)(2,1)S(1)} %get-tuple-element.155), channel_id=1, source_target_pairs={{0,4},{2,6},{4,0},{6,2},{8,12},{10,14},{12,8},{14,10},{1,5},{3,7},... | collective-permute-start | bytes 221192 | tf_op jit(solution)/shard_map/ppermute | solution.py:662
  93.9 6.0 %collective-permute-start.27 = (bf16[144,256]{1,0:T(8,128)(2,1)S(1)}, bf16[144,256]{1,0:T(8,128)(2,1)S(1)}, u32[]{:S(2)}, u32[]{:S(2)}) collective-permute-start(bf16[144,256]{1,0:T(8,128)(2,1)S(1)} %get-tuple-element.155), channel_id=1, source_target_pairs={{0,8},{2,10},{4,12},{6,14},{8,0},{10,2},{12,4},{14,6},{1,9},{3,11}... | collective-permute-start | bytes 221192 | tf_op jit(solution)/shard_map/ppermute | solution.py:662
  99.9 1.3 %collective-permute-start.32 = (bf16[2,2,48,256]{3,2,1,0:T(8,128)(2,1)S(1)}, bf16[2,2,48,256]{3,2,1,0:T(8,128)(2,1)S(1)}, u32[]{:S(2)}, u32[]{:S(2)}) collective-permute-start(bf16[2,2,48,256]{3,2,1,0:T(8,128)(2,1)S(1)} %collective-permute-done.25.refs_6_), channel_id=1, source_target_pairs={{0,1},{1,0},{2,3},{3,2},{4,5},{5,4},{6,7},{7,6},{8,9},{9,8},{10,11... | collective-permute-start | bytes 294920 | tf_op jit(solution)/shard_map/ppermute | solution.py:580
  100.0 9.9 %collective-permute-start.44 = (bf16[576,256]{1,0:T(8,128)(2,1)S(1)}, bf16[576,256]{1,0:T(8,128)(2,1)S(1)}, u32[]{:S(2)}, u32[]{:S(2)}) collective-permute-start(bf16[576,256]{1,0:T(8,128)(2,1)S(1)} %pad_maximum_fusion.refs_0_), channel_id=1, source_target_pairs={{0,2},{2,0},{4,6},{6,4},{8,10},{10,8},{12,14},{14,12},{1,3},{3,1},... | collective-permute-start | bytes 884744 | tf_op jit(solution)/shard_map/ppermute | solution.py:659
  101.2 14.7 %collective-permute-start.33 = (bf16[576,256]{1,0:T(8,128)(2,1)S(1)}, bf16[576,256]{1,0:T(8,128)(2,1)S(1)}, u32[]{:S(2)}, u32[]{:S(2)}) collective-permute-start(bf16[576,256]{1,0:T(8,128)(2,1)S(1)} %constant_dynamic-update-slice_fusion.refs_0_), channel_id=1, source_target_pairs={{0,2},{2,0},{4,6},{6,4},{8,10},{10,8},{12,14},{14,12},{1,3},{3,1},... | collective-permute-start | bytes 884744 | tf_op jit(solution)/shard_map/ppermute | solution.py:659
  102.2 13.8 %collective-permute-start.45 = (bf16[576,256]{1,0:T(8,128)(2,1)S(1)}, bf16[576,256]{1,0:T(8,128)(2,1)S(1)}, u32[]{:S(2)}, u32[]{:S(2)}) collective-permute-start(bf16[576,256]{1,0:T(8,128)(2,1)S(1)} %pad_maximum_fusion.refs_0_), channel_id=1, source_target_pairs={{0,1},{1,0},{2,3},{3,2},{4,5},{5,4},{6,7},{7,6},{8,9},{9,8},{10,11... | collective-permute-start | bytes 884744 | tf_op jit(solution)/shard_map/ppermute | solution.py:580
  109.8 6.2 %collective-permute-start.46 = (bf16[576,256]{1,0:T(8,128)(2,1)S(1)}, bf16[576,256]{1,0:T(8,128)(2,1)S(1)}, u32[]{:S(2)}, u32[]{:S(2)}) collective-permute-start(bf16[576,256]{1,0:T(8,128)(2,1)S(1)} %collective-permute-done.44.refs_1_), channel_id=1, source_target_pairs={{0,1},{1,0},{2,3},{3,2},{4,5},{5,4},{6,7},{7,6},{8,9},{9,8},{10,11... | collective-permute-start | bytes 884744 | tf_op jit(solution)/shard_map/ppermute | solution.py:580
  109.8 7.9 %collective-permute-start.34 = (bf16[576,256]{1,0:T(8,128)(2,1)S(1)}, bf16[576,256]{1,0:T(8,128)(2,1)S(1)}, u32[]{:S(2)}, u32[]{:S(2)}) collective-permute-start(bf16[576,256]{1,0:T(8,128)(2,1)S(1)} %constant_dynamic-update-slice_fusion.refs_0_), channel_id=1, source_target_pairs={{0,1},{1,0},{2,3},{3,2},{4,5},{5,4},{6,7},{7,6},{8,9},{9,8},{10,11... | collective-permute-start | bytes 884744 | tf_op jit(solution)/shard_map/ppermute | solution.py:580
  116.0 1.8 %collective-permute-start.35 = (bf16[576,256]{1,0:T(8,128)(2,1)S(1)}, bf16[576,256]{1,0:T(8,128)(2,1)S(1)}, u32[]{:S(2)}, u32[]{:S(2)}) collective-permute-start(bf16[576,256]{1,0:T(8,128)(2,1)S(1)} %collective-permute-done.33.refs_1_), channel_id=1, source_target_pairs={{0,1},{1,0},{2,3},{3,2},{4,5},{5,4},{6,7},{7,6},{8,9},{9,8},{10,11... | collective-permute-start | bytes 884744 | tf_op jit(solution)/shard_map/ppermute | solution.py:580

commit v15 on v10

--- a/solution.py
+++ b/solution.py
@@ -134,9 +134,9 @@
         ref[which] = jnp.dot(hot, sources[which], preferred_element_type=F32).astype(BF)
 
 
-def pack_kernel(dm, ep, x_ref, up_ref, *refs):
+def pack_kernel(dm, ep, fields_ref, *refs):
     t, p = lax.axis_index("tile"), lax.axis_index("dp")
-    fields = (x_ref[...], up_ref[...])
+    fields = (fields_ref[0], fields_ref[1])
     write_messages(dm, ep, t, p, fields, refs[:-1])
     write_self(dm, ep, t, fields, refs[-1])
 
@@ -611,7 +611,7 @@
 
     packed = call(
         functools.partial(pack_kernel, dm), msg_shapes, smem_first=True
-    )(edge_partner, x.reshape(flat), d.reshape(flat))
+    )(edge_partner, jnp.stack([x.reshape(flat), d.reshape(flat)]))
     came = [across(v, i) for i, v in enumerate(merged(packed))]
     came, w1s, w1t, w2t = lax.optimization_barrier((came, w1s, w1t, w2t))
     messages = []

time: 108 us -> 108 us (level)
  local copies, waits for them, and re-layouts: 5.22 us -> 2.17 us
  waiting for transfers between devices: 29.2 us -> 30.5 us
  other arithmetic: 0.02 us -> 1.11 us
    unnamed x20 -> x14, local copies, waits for them, and re-layouts: 5.21 us -> 2.16 us
    ppermute x8, waiting for transfers between devices: 8.5 us -> 9.78 us  [across(): return lax.ppermute(v, ('tile', 'dp'), pairs[step])]
    another operation x0 -> x1, other arithmetic: none -> 1.08 us  [on_device(): jnp.stack([x.reshape(flat), d.reshape(flat)])]
  transfers between devices with their start and end apart: 47 -> 47, of which waited for: 22 -> 23; matrix products, arithmetic and copies ran while one was open for 0% -> 0% of each run, Pallas kernels for 8% -> 8%
where the time goes in v15:
time: 108 us; the launch traced here: 107 us
  starting transfers between devices  51.7 us (48%)
  waiting for transfers between devices  30.5 us (28%)
  Pallas kernels  20.9 us (19%)
  local copies, waits for them, and re-layouts  2.17 us (2%)
  other arithmetic  1.11 us (1%)
    ppermute x12, starting transfers between devices, along_z(): return lax.ppermute(v, 'tile', [(i, i ^ 2 * j) for i in range(tiles)])  22.7 us
    pallas_call x14, Pallas kernels, run(): pl.pallas_call(kernel, out_shape=[jax.ShapeDtypeStruct(s, dt) for s, dt i...  20.9 us
    ppermute x8, starting transfers between devices, across(): return lax.ppermute(v, ('tile', 'dp'), pairs[step])  15.5 us
    ppermute x12, waiting for transfers between devices, along_z(): return lax.ppermute(v, 'tile', [(i, i ^ 2 * j) for i in range(tiles)])  13.9 us
    ppermute x23, starting transfers between devices, swap_dp(): return lax.ppermute(v, 'dp', [(i, count - 1 - i) for i in range(count)])  11.4 us
    ppermute x8, waiting for transfers between devices, across(): return lax.ppermute(v, ('tile', 'dp'), pairs[step])  9.78 us
    ppermute x23, waiting for transfers between devices, swap_dp(): return lax.ppermute(v, 'dp', [(i, count - 1 - i) for i in range(count)])  6.79 us
    ppermute x4, starting transfers between devices, along_y(): return lax.ppermute(v, 'tile', [(i, i ^ 1) for i in range(tiles)])  2.23 us
  transfers between devices with their start and end apart: 47, of which 23 were waited for; matrix products, arithmetic and copies ran while one was open for 0% of the time, Pallas kernels for 8%

profile of v15, /device:TPU:0, one launch (start us, length us, event | category | flops | bytes accessed | tf_op | source)
XLA Modules:
  0.0 107.3 jit_solution(6013203732845763393)
XLA Ops:
  0.6 0.9 copy.12.ep
  1.5 1.1 %pad_maximum_fusion.fields_ref = bf16[2,432,256]{2,1,0:T(8,128)(2,1)S(1)} fusion(bf16[1,432,256]{2,1,0:T(8,128)(2,1)} %bitcast.21, bf16[1,432,256]{2,1,0:T(8,128)(2,1)} %bitcast.18), kind=kLoop, calls=%fused_computation | loop fusion | flops 221184 | bytes 884736 | tf_op jit(solution)/shard_map/stack | solution.py:614
  2.6 2.2 %shard_map.101 = (bf16[2,192,256]{2,1,0:T(8,128)(2,1)S(1)}, bf16[2,48,256]{2,1,0:T(8,128)(2,1)S(1)}, bf16[2,48,256]{2,1,0:T(8,128)(2,1)S(1)}, bf16[2,48,256]{2,1...) custom-call(s32[6,4]{1,0:T(8,128)S(1)} %copy.12.ep, ...), custom_call_target="tpu_custom_call" | custom-call | tf_op jit(solution)/shard_map/pallas_call | solution.py:566
  4.8 0.5 collective-permute-start
  5.4 0.4 collective-permute-start.2
  5.9 0.6 collective-permute-done.1.refs_5_
  6.7 0.3 collective-permute-done.3.refs_7_
  7.1 2.7 %collective-permute-start.4 = (bf16[2,2,192,256]{3,2,1,0:T(8,128)(2,1)S(1)}, bf16[2,2,192,256]{3,2,1,0:T(8,128)(2,1)S(1)}, u32[]{:S(2)}, u32[]{:S(2)}) collective-permute-start(bf16[2,2,192,256]{3,2,1,0:T(8,128)(2,1)S(1)} %get-tuple-element.103), channel_id=1, source_target_pairs={{0,2},{2,0},{4,6},{6,4},{8,10},{10,8},{12,14},{14,12},{1,15},{3,5}... | collective-permute-start | bytes 1179656 | tf_op jit(solution)/shard_map/ppermute | solution.py:610
  9.8 3.5 %collective-permute-start.5 = (bf16[2,2,48,256]{3,2,1,0:T(8,128)(2,1)S(1)}, bf16[2,2,48,256]{3,2,1,0:T(8,128)(2,1)S(1)}, u32[]{:S(2)}, u32[]{:S(2)}) collective-permute-start(bf16[2,2,48,256]{3,2,1,0:T(8,128)(2,1)S(1)} %get-tuple-element.104), channel_id=1, source_target_pairs={{0,4},{4,0},{10,14},{14,10},{1,9},{3,11},{5,13},{7,15},{9,1},{11,3... | collective-permute-start | bytes 294920 | tf_op jit(solution)/shard_map/ppermute | solution.py:610
  13.3 0.8 collective-permute-start.6
  14.1 0.7 collective-permute-start.7
  14.8 1.3 %copy-done.3 = bf16[3,3,256,256]{3,2,1,0:T(8,128)(2,1)S(1)} copy-done((bf16[3,3,256,256]{3,2,1,0:T(8,128)(2,1)S(1)}, bf16[3,3,256,256]{3,2,1,0:T(8,128)(2,1)}, u32[]{:S(2)}) %copy-start.3) | copy-done | bytes 1179672
  16.1 0.7 shard_map.103
  16.8 0.6 collective-permute-done.5.refs_2_
  17.4 3.6 %collective-permute-done.6.refs_4_ = bf16[2,2,48,256]{3,2,1,0:T(8,128)(2,1)S(1)} collective-permute-done((bf16[2,2,48,256]{3,2,1,0:T(8,128)(2,1)S(1)}, bf16[2,2,48,256]{3,2,1,0:T(8,128)(2,1)S(1)}, u32[]{:S(2)}, u32[]{:S(2)}) %collective-permute-start.6) | collective-permute-done | bytes 98336 | tf_op jit(solution)/shard_map/ppermute | solution.py:610
  21.0 4.5 %collective-permute-start.8 = (bf16[2,2,192,256]{3,2,1,0:T(8,128)(2,1)S(1)}, bf16[2,2,192,256]{3,2,1,0:T(8,128)(2,1)S(1)}, u32[]{:S(2)}, u32[]{:S(2)}) collective-permute-start(bf16[2,2,192,256]{3,2,1,0:T(8,128)(2,1)S(1)} %collective-permute-done.4.refs_0_), channel_id=1, source_target_pairs={{0,1},{1,0},{2,3},{3,2},{4,5},{5,4},{6,7},{7,6},{8,9},{9,8},{10,11... | collective-permute-start | bytes 1179656 | tf_op jit(solution)/shard_map/ppermute | solution.py:580
  25.5 0.5 collective-permute-start.10
  26.0 1.0 collective-permute-done.9.refs_3_
  27.1 0.2 collective-permute-done.11.refs_7_
  27.3 8.3 %shard_map.104 = (bf16[9,128,256]{2,1,0:T(8,128)(2,1)S(1)}, f32[9,128,256]{2,1,0:T(8,128)S(1)}, bf16[9,128,256]{2,1,0:T(8,128)(2,1)S(1)}, f32[9,128,256]{2,1,0:T...) custom-call(s32[6,4]{1,0:T(8,128)S(1)} %copy.12.ep, ...), custom_call_target="tpu_custom_call" | custom-call | tf_op jit(solution)/shard_map/pallas_call | solution.py:566
  35.6 0.4 collective-permute-start.12
  36.0 0.2 collective-permute-start.36
  36.2 0.3 collective-permute-start.13
  36.5 2.0 %collective-permute-done.13.refs_1_ = bf16[8,256]{1,0:T(8,128)(2,1)S(1)} collective-permute-done((bf16[8,256]{1,0:T(8,128)(2,1)S(1)}, bf16[8,256]{1,0:T(8,128)(2,1)S(1)}, u32[]{:S(2)}, u32[]{:S(2)}) %collective-permute-start.13) | collective-permute-done | bytes 4128 | tf_op jit(solution)/shard_map/ppermute | solution.py:580
  38.7 0.4 collective-permute-start.15
  39.1 0.2 collective-permute-start.16
  39.4 2.0 %collective-permute-start.37 = (bf16[576,256]{1,0:T(8,128)(2,1)S(1)}, bf16[576,256]{1,0:T(8,128)(2,1)S(1)}, u32[]{:S(2)}, u32[]{:S(2)}) collective-permute-start(bf16[576,256]{1,0:T(8,128)(2,1)S(1)} %get-tuple-element.180), channel_id=1, source_target_pairs={{0,2},{2,0},{4,6},{6,4},{8,10},{10,8},{12,14},{14,12},{1,3},{3,1},... | collective-permute-start | bytes 884744 | tf_op jit(solution)/shard_map/ppermute | solution.py:659
  41.4 0.5 collective-permute-start.18
  41.9 0.7 collective-permute-done.17.refs_6_
  42.7 0.2 collective-permute-done.18.refs_7_
  42.9 2.8 %collective-permute-start.19 = (bf16[2,2,48,256]{3,2,1,0:T(8,128)(2,1)S(1)}, bf16[2,2,48,256]{3,2,1,0:T(8,128)(2,1)S(1)}, u32[]{:S(2)}, u32[]{:S(2)}) collective-permute-start(bf16[2,2,48,256]{3,2,1,0:T(8,128)(2,1)S(1)} %get-tuple-element.131), channel_id=1, source_target_pairs={{0,4},{4,0},{10,14},{14,10},{1,9},{3,11},{5,13},{7,15},{9,1},{11,3... | collective-permute-start | bytes 294920 | tf_op jit(solution)/shard_map/ppermute | solution.py:610
  45.7 1.6 %collective-permute-start.20 = (bf16[2,2,48,256]{3,2,1,0:T(8,128)(2,1)S(1)}, bf16[2,2,48,256]{3,2,1,0:T(8,128)(2,1)S(1)}, u32[]{:S(2)}, u32[]{:S(2)}) collective-permute-start(bf16[2,2,48,256]{3,2,1,0:T(8,128)(2,1)S(1)} %get-tuple-element.132), channel_id=1, source_target_pairs={{0,12},{2,14},{4,8},{6,10},{8,4},{10,6},{12,0},{14,2},{1,7},{3,13}... | collective-permute-start | bytes 294920 | tf_op jit(solution)/shard_map/ppermute | solution.py:610
  47.3 3.1 %collective-permute-done.19.refs_2_ = bf16[2,2,48,256]{3,2,1,0:T(8,128)(2,1)S(1)} collective-permute-done((bf16[2,2,48,256]{3,2,1,0:T(8,128)(2,1)S(1)}, bf16[2,2,48,256]{3,2,1,0:T(8,128)(2,1)S(1)}, u32[]{:S(2)}, u32[]{:S(2)}) %collective-permute-start.19) | collective-permute-done | bytes 98336 | tf_op jit(solution)/shard_map/ppermute | solution.py:610
  50.4 2.4 %collective-permute-done.20.refs_4_ = bf16[2,2,48,256]{3,2,1,0:T(8,128)(2,1)S(1)} collective-permute-done((bf16[2,2,48,256]{3,2,1,0:T(8,128)(2,1)S(1)}, bf16[2,2,48,256]{3,2,1,0:T(8,128)(2,1)S(1)}, u32[]{:S(2)}, u32[]{:S(2)}) %collective-permute-start.20) | collective-permute-done | bytes 98336 | tf_op jit(solution)/shard_map/ppermute | solution.py:610
  52.9 2.5 %collective-permute-start.24 = (bf16[2,2,192,256]{3,2,1,0:T(8,128)(2,1)S(1)}, bf16[2,2,192,256]{3,2,1,0:T(8,128)(2,1)S(1)}, u32[]{:S(2)}, u32[]{:S(2)}) collective-permute-start(bf16[2,2,192,256]{3,2,1,0:T(8,128)(2,1)S(1)} %get-tuple-element.144), channel_id=1, source_target_pairs={{0,2},{2,0},{4,6},{6,4},{8,10},{10,8},{12,14},{14,12},{1,15},{3,5}... | collective-permute-start | bytes 1179656 | tf_op jit(solution)/shard_map/ppermute | solution.py:610
  55.6 0.9 collective-permute-start.38
  56.5 2.9 %collective-permute-start.39 = (bf16[144,256]{1,0:T(8,128)(2,1)S(1)}, bf16[144,256]{1,0:T(8,128)(2,1)S(1)}, u32[]{:S(2)}, u32[]{:S(2)}) collective-permute-start(bf16[144,256]{1,0:T(8,128)(2,1)S(1)} %get-tuple-element.183), channel_id=1, source_target_pairs={{0,8},{2,10},{4,12},{6,14},{8,0},{10,2},{12,4},{14,6},{1,9},{3,11}... | collective-permute-start | bytes 221192 | tf_op jit(solution)/shard_map/ppermute | solution.py:662
  59.4 0.6 collective-permute-start.40
  60.0 0.8 collective-permute-done.38.refs_0_
  60.8 2.4 %collective-permute-done.39.refs_1_ = bf16[144,256]{1,0:T(8,128)(2,1)S(1)} collective-permute-done((bf16[144,256]{1,0:T(8,128)(2,1)S(1)}, bf16[144,256]{1,0:T(8,128)(2,1)S(1)}, u32[]{:S(2)}, u32[]{:S(2)}) %collective-permute-start.39) | collective-permute-done | bytes 73760 | tf_op jit(solution)/shard_map/ppermute | solution.py:662
  63.3 3.2 %collective-permute-done.40.refs_2_ = bf16[144,256]{1,0:T(8,128)(2,1)S(1)} collective-permute-done((bf16[144,256]{1,0:T(8,128)(2,1)S(1)}, bf16[144,256]{1,0:T(8,128)(2,1)S(1)}, u32[]{:S(2)}, u32[]{:S(2)}) %collective-permute-start.40) | collective-permute-done | bytes 73760 | tf_op jit(solution)/shard_map/ppermute | solution.py:662
  66.5 4.2 %collective-permute-start.43 = (bf16[144,256]{1,0:T(8,128)(2,1)S(1)}, bf16[144,256]{1,0:T(8,128)(2,1)S(1)}, u32[]{:S(2)}, u32[]{:S(2)}) collective-permute-start(bf16[144,256]{1,0:T(8,128)(2,1)S(1)} %shard_map.113), channel_id=1, source_target_pairs={{0,12},{2,14},{4,8},{6,10},{8,4},{10,6},{12,0},{14,2},{1,13},{3,15... | collective-permute-start | bytes 221192 | tf_op jit(solution)/shard_map/ppermute | solution.py:662
  70.7 0.2 collective-permute-start.42
  70.9 0.5 collective-permute-start.41
  71.4 1.5 %collective-permute-start.21 = (bf16[152,256]{1,0:T(8,128)(2,1)S(1)}, bf16[152,256]{1,0:T(8,128)(2,1)S(1)}, u32[]{:S(2)}, u32[]{:S(2)}) collective-permute-start(bf16[152,256]{1,0:T(8,128)(2,1)S(1)} %get-tuple-element.141), channel_id=1, source_target_pairs={{0,4},{2,6},{4,0},{6,2},{8,12},{10,14},{12,8},{14,10},{1,5},{3,7},... | collective-permute-start | bytes 233480 | tf_op jit(solution)/shard_map/ppermute | solution.py:662
  73.0 0.5 collective-permute-done.43
  73.5 4.7 %collective-permute-start.22 = (bf16[152,256]{1,0:T(8,128)(2,1)S(1)}, bf16[152,256]{1,0:T(8,128)(2,1)S(1)}, u32[]{:S(2)}, u32[]{:S(2)}) collective-permute-start(bf16[152,256]{1,0:T(8,128)(2,1)S(1)} %get-tuple-element.142), channel_id=1, source_target_pairs={{0,8},{2,10},{4,12},{6,14},{8,0},{10,2},{12,4},{14,6},{1,9},{3,11}... | collective-permute-start | bytes 233480 | tf_op jit(solution)/shard_map/ppermute | solution.py:662
  78.2 2.6 %collective-permute-start.23 = (bf16[152,256]{1,0:T(8,128)(2,1)S(1)}, bf16[152,256]{1,0:T(8,128)(2,1)S(1)}, u32[]{:S(2)}, u32[]{:S(2)}) collective-permute-start(bf16[152,256]{1,0:T(8,128)(2,1)S(1)} %get-tuple-element.143), channel_id=1, source_target_pairs={{0,12},{2,14},{4,8},{6,10},{8,4},{10,6},{12,0},{14,2},{1,13},{3,15... | collective-permute-start | bytes 233480 | tf_op jit(solution)/shard_map/ppermute | solution.py:662
  80.8 0.8 collective-permute-start.25
  81.8 0.8 collective-permute-done.22.refs_1_
  82.6 1.8 %collective-permute-done.23.refs_2_ = bf16[152,256]{1,0:T(8,128)(2,1)S(1)} collective-permute-done((bf16[152,256]{1,0:T(8,128)(2,1)S(1)}, bf16[152,256]{1,0:T(8,128)(2,1)S(1)}, u32[]{:S(2)}, u32[]{:S(2)}) %collective-permute-start.23) | collective-permute-done | bytes 77856 | tf_op jit(solution)/shard_map/ppermute | solution.py:662
  84.5 3.6 %collective-permute-start.28 = (bf16[144,256]{1,0:T(8,128)(2,1)S(1)}, bf16[144,256]{1,0:T(8,128)(2,1)S(1)}, u32[]{:S(2)}, u32[]{:S(2)}) collective-permute-start(bf16[144,256]{1,0:T(8,128)(2,1)S(1)} %get-tuple-element.150), channel_id=1, source_target_pairs={{0,12},{2,14},{4,8},{6,10},{8,4},{10,6},{12,0},{14,2},{1,13},{3,15... | collective-permute-start | bytes 221192 | tf_op jit(solution)/shard_map/ppermute | solution.py:662
  88.0 0.9 collective-permute-start.26
  88.9 1.5 %collective-permute-start.30 = (bf16[2,2,192,256]{3,2,1,0:T(8,128)(2,1)S(1)}, bf16[2,2,192,256]{3,2,1,0:T(8,128)(2,1)S(1)}, u32[]{:S(2)}, u32[]{:S(2)}) collective-permute-start(bf16[2,2,192,256]{3,2,1,0:T(8,128)(2,1)S(1)} %collective-permute-done.24.refs_0_), channel_id=1, source_target_pairs={{0,1},{1,0},{2,3},{3,2},{4,5},{5,4},{6,7},{7,6},{8,9},{9,8},{10,11... | collective-permute-start | bytes 1179656 | tf_op jit(solution)/shard_map/ppermute | solution.py:580
  90.5 3.3 %collective-permute-done.26 = bf16[144,256]{1,0:T(8,128)(2,1)S(1)} collective-permute-done((bf16[144,256]{1,0:T(8,128)(2,1)S(1)}, bf16[144,256]{1,0:T(8,128)(2,1)S(1)}, u32[]{:S(2)}, u32[]{:S(2)}) %collective-permute-start.26) | collective-permute-done | bytes 73760 | tf_op jit(solution)/shard_map/ppermute | solution.py:662
  93.8 1.0 collective-permute-done.27
  94.9 0.5 collective-permute-start.32
  95.4 0.8 collective-permute-done.31.refs_3_
  96.4 0.4 collective-permute-start.45
  96.9 0.6 collective-permute-done.33.refs_7_
  97.5 5.6 %shard_map.109 = (bf16[18,24,256]{2,1,0:T(8,128)(2,1)}, f32[18,24,256]{2,1,0:T(8,128)}) custom-call(s32[6,4]{1,0:T(8,128)S(1)} %copy.12.ep, bf16[18,24,256]{2,1,0:T(8,128)(2,1)S(1)} %bitcast.20, bf16[18,24,256]{2,1,0:T(8,128)(2,1)S(1)} %bitcast.23, bf16[18,24,256]{2,1,0:T(8,128)(2,1)S(1)} %get-tuple-element.151.hid_ref, ...), custom_call_target="tpu_custom_call" | custom-call | tf_op jit(solution)/shard_map/pallas_call | solution.py:566
  103.3 0.4 collective-permute-start.34
  103.7 1.8 %shard_map.114 = f32[9,256,256]{2,1,0:T(8,128)} custom-call(bf16[576,256]{1,0:T(8,128)(2,1)S(1)} %pad_maximum_fusion.1.refs_0_, bf16[576,256]{1,0:T(8,128)(2,1)S(1)} %collective-permute-done.44.refs_1_, bf16[576,256]{1,0:T(8,128)(2,1)S(1)} %collective-permute-done.45.refs_2_, bf16[576,256]{1,0:T(8,128)(2,1)S(1)} %collective-permute-done.46.refs_3_), custom_call_target="tpu_custom_call" | custom-call | tf_op jit(solution)/shard_map/pallas_call | solution.py:566
  105.5 1.8 %shard_map.110 = (f32[9,256,256]{2,1,0:T(8,128)}, f32[1,256]{1,0:T(1,128)}) custom-call(bf16[576,256]{1,0:T(8,128)(2,1)S(1)} %constant_dynamic-update-slice_fusion.refs_0_, bf16[576,256]{1,0:T(8,128)(2,1)S(1)} %collective-permute-done.29.refs_1_, bf16[576,256]{1,0:T(8,128)(2,1)S(1)} %collective-permute-done.34.refs_2_, ...), custom_call_target="tpu_custom_call" | custom-call | tf_op jit(solution)/shard_map/pallas_call | solution.py:566
  (61 shorter events, 1.9 us)
Async XLA Ops:
  0.6 14.2 %copy-start = (bf16[3,3,256,256]{3,2,1,0:T(8,128)(2,1)S(1)}, bf16[3,3,256,256]{3,2,1,0:T(8,128)(2,1)}, u32[]{:S(2)}) copy-start(bf16[3,3,256,256]{3,2,1,0:T(8,128)(2,1)} %param.10) | copy-start | bytes 3538948
  4.8 2.3 %collective-permute-start = (bf16[2,192,256]{2,1,0:T(8,128)(2,1)S(1)}, bf16[2,192,256]{2,1,0:T(8,128)(2,1)S(1)}, u32[]{:S(2)}, u32[]{:S(2)}) collective-permute-start(bf16[2,192,256]{2,1,0:T(8,128)(2,1)S(1)} %get-tuple-element.99), channel_id=1, source_target_pairs={{0,1},{1,0},{2,3},{3,2},{4,5},{5,4},{6,7},{7,6},{8,9},{9,8},{10,11... | collective-permute-start | bytes 589832 | tf_op jit(solution)/shard_map/ppermute | solution.py:580
  5.3 1.2 %collective-permute-start.1 = (bf16[2,48,256]{2,1,0:T(8,128)(2,1)S(1)}, bf16[2,48,256]{2,1,0:T(8,128)(2,1)S(1)}, u32[]{:S(2)}, u32[]{:S(2)}) collective-permute-start(bf16[2,48,256]{2,1,0:T(8,128)(2,1)S(1)} %get-tuple-element.100), channel_id=1, source_target_pairs={{0,1},{1,0},{2,3},{3,2},{4,5},{5,4},{6,7},{7,6},{8,9},{9,8},{10,11... | collective-permute-start | bytes 147464 | tf_op jit(solution)/shard_map/ppermute | solution.py:580
  5.4 1.3 %collective-permute-start.2 = (bf16[2,48,256]{2,1,0:T(8,128)(2,1)S(1)}, bf16[2,48,256]{2,1,0:T(8,128)(2,1)S(1)}, u32[]{:S(2)}, u32[]{:S(2)}) collective-permute-start(bf16[2,48,256]{2,1,0:T(8,128)(2,1)S(1)} %get-tuple-element.101), channel_id=1, source_target_pairs={{0,1},{1,0},{2,3},{3,2},{4,5},{5,4},{6,7},{7,6},{8,9},{9,8},{10,11... | collective-permute-start | bytes 147464 | tf_op jit(solution)/shard_map/ppermute | solution.py:580
  5.8 1.2 %collective-permute-start.3 = (bf16[2,48,256]{2,1,0:T(8,128)(2,1)S(1)}, bf16[2,48,256]{2,1,0:T(8,128)(2,1)S(1)}, u32[]{:S(2)}, u32[]{:S(2)}) collective-permute-start(bf16[2,48,256]{2,1,0:T(8,128)(2,1)S(1)} %get-tuple-element.102), channel_id=1, source_target_pairs={{0,1},{1,0},{2,3},{3,2},{4,5},{5,4},{6,7},{7,6},{8,9},{9,8},{10,11... | collective-permute-start | bytes 147464 | tf_op jit(solution)/shard_map/ppermute | solution.py:580
  7.1 13.9 %collective-permute-start.4 = (bf16[2,2,192,256]{3,2,1,0:T(8,128)(2,1)S(1)}, bf16[2,2,192,256]{3,2,1,0:T(8,128)(2,1)S(1)}, u32[]{:S(2)}, u32[]{:S(2)}) collective-permute-start(bf16[2,2,192,256]{3,2,1,0:T(8,128)(2,1)S(1)} %get-tuple-element.103), channel_id=1, source_target_pairs={{0,2},{2,0},{4,6},{6,4},{8,10},{10,8},{12,14},{14,12},{1,15},{3,5}... | collective-permute-start | bytes 1179656 | tf_op jit(solution)/shard_map/ppermute | solution.py:610
  9.8 7.6 %collective-permute-start.5 = (bf16[2,2,48,256]{3,2,1,0:T(8,128)(2,1)S(1)}, bf16[2,2,48,256]{3,2,1,0:T(8,128)(2,1)S(1)}, u32[]{:S(2)}, u32[]{:S(2)}) collective-permute-start(bf16[2,2,48,256]{3,2,1,0:T(8,128)(2,1)S(1)} %get-tuple-element.104), channel_id=1, source_target_pairs={{0,4},{4,0},{10,14},{14,10},{1,9},{3,11},{5,13},{7,15},{9,1},{11,3... | collective-permute-start | bytes 294920 | tf_op jit(solution)/shard_map/ppermute | solution.py:610
  13.3 7.7 %collective-permute-start.6 = (bf16[2,2,48,256]{3,2,1,0:T(8,128)(2,1)S(1)}, bf16[2,2,48,256]{3,2,1,0:T(8,128)(2,1)S(1)}, u32[]{:S(2)}, u32[]{:S(2)}) collective-permute-start(bf16[2,2,48,256]{3,2,1,0:T(8,128)(2,1)S(1)} %get-tuple-element.105), channel_id=1, source_target_pairs={{0,12},{2,14},{4,8},{6,10},{8,4},{10,6},{12,0},{14,2},{1,7},{3,13}... | collective-permute-start | bytes 294920 | tf_op jit(solution)/shard_map/ppermute | solution.py:610
  14.1 6.8 %collective-permute-start.7 = (bf16[2,2,48,256]{3,2,1,0:T(8,128)(2,1)S(1)}, bf16[2,2,48,256]{3,2,1,0:T(8,128)(2,1)S(1)}, u32[]{:S(2)}, u32[]{:S(2)}) collective-permute-start(bf16[2,2,48,256]{3,2,1,0:T(8,128)(2,1)S(1)} %get-tuple-element.106), channel_id=1, source_target_pairs={{1,11},{5,15},{11,1},{15,5},{17,27},{21,31},{27,17},{31,21}} | collective-permute-start | bytes 294920 | tf_op jit(solution)/shard_map/ppermute | solution.py:610
  14.8 1.3 %copy-start.3 = (bf16[3,3,256,256]{3,2,1,0:T(8,128)(2,1)S(1)}, bf16[3,3,256,256]{3,2,1,0:T(8,128)(2,1)}, u32[]{:S(2)}) copy-start(bf16[3,3,256,256]{3,2,1,0:T(8,128)(2,1)} %param.8) | copy-start | bytes 3538948
  16.1 11.2 %copy-start.1 = (bf16[1,6,3,24,256]{4,3,2,1,0:T(8,128)(2,1)S(1)}, bf16[1,6,3,24,256]{4,3,2,1,0:T(8,128)(2,1)}, u32[]{:S(2)}) copy-start(bf16[1,6,3,24,256]{4,3,2,1,0:T(8,128)(2,1)} %param.6) | copy-start | bytes 663556
  16.1 11.2 %copy-start.2 = (bf16[1,1,6,3,24,256]{5,4,3,2,1,0:T(8,128)(2,1)S(1)}, bf16[1,1,6,3,24,256]{5,4,3,2,1,0:T(8,128)(2,1)}, u32[]{:S(2)}) copy-start(bf16[1,1,6,3,24,256]{5,4,3,2,1,0:T(8,128)(2,1)} %param.7) | copy-start | bytes 663556
  16.1 11.2 %copy-start.4 = (f32[256]{0:T(256)S(1)}, f32[256]{0:T(256)}, u32[]{:S(2)}) copy-start(f32[256]{0:T(256)} %param.9) | copy-start | bytes 3076
  21.0 6.3 %collective-permute-start.8 = (bf16[2,2,192,256]{3,2,1,0:T(8,128)(2,1)S(1)}, bf16[2,2,192,256]{3,2,1,0:T(8,128)(2,1)S(1)}, u32[]{:S(2)}, u32[]{:S(2)}) collective-permute-start(bf16[2,2,192,256]{3,2,1,0:T(8,128)(2,1)S(1)} %collective-permute-done.4.refs_0_), channel_id=1, source_target_pairs={{0,1},{1,0},{2,3},{3,2},{4,5},{5,4},{6,7},{7,6},{8,9},{9,8},{10,11... | collective-permute-start | bytes 1179656 | tf_op jit(solution)/shard_map/ppermute | solution.py:580
  25.5 1.5 %collective-permute-start.9 = (bf16[2,2,48,256]{3,2,1,0:T(8,128)(2,1)S(1)}, bf16[2,2,48,256]{3,2,1,0:T(8,128)(2,1)S(1)}, u32[]{:S(2)}, u32[]{:S(2)}) collective-permute-start(bf16[2,2,48,256]{3,2,1,0:T(8,128)(2,1)S(1)} %collective-permute-done.5.refs_2_), channel_id=1, source_target_pairs={{0,1},{1,0},{2,3},{3,2},{4,5},{5,4},{6,7},{7,6},{8,9},{9,8},{10,11... | collective-permute-start | bytes 294920 | tf_op jit(solution)/shard_map/ppermute | solution.py:580
  25.5 1.6 %collective-permute-start.10 = (bf16[2,2,48,256]{3,2,1,0:T(8,128)(2,1)S(1)}, bf16[2,2,48,256]{3,2,1,0:T(8,128)(2,1)S(1)}, u32[]{:S(2)}, u32[]{:S(2)}) collective-permute-start(bf16[2,2,48,256]{3,2,1,0:T(8,128)(2,1)S(1)} %collective-permute-done.6.refs_4_), channel_id=1, source_target_pairs={{0,1},{1,0},{2,3},{3,2},{4,5},{5,4},{6,7},{7,6},{8,9},{9,8},{10,11... | collective-permute-start | bytes 294920 | tf_op jit(solution)/shard_map/ppermute | solution.py:580
  26.0 1.3 %collective-permute-start.11 = (bf16[2,2,48,256]{3,2,1,0:T(8,128)(2,1)S(1)}, bf16[2,2,48,256]{3,2,1,0:T(8,128)(2,1)S(1)}, u32[]{:S(2)}, u32[]{:S(2)}) collective-permute-start(bf16[2,2,48,256]{3,2,1,0:T(8,128)(2,1)S(1)} %collective-permute-done.7.refs_6_), channel_id=1, source_target_pairs={{0,1},{1,0},{2,3},{3,2},{4,5},{5,4},{6,7},{7,6},{8,9},{9,8},{10,11... | collective-permute-start | bytes 294920 | tf_op jit(solution)/shard_map/ppermute | solution.py:580
  35.6 2.9 %collective-permute-start.12 = (bf16[9,128,256]{2,1,0:T(8,128)(2,1)S(1)}, bf16[9,128,256]{2,1,0:T(8,128)(2,1)S(1)}, u32[]{:S(2)}, u32[]{:S(2)}) collective-permute-start(bf16[9,128,256]{2,1,0:T(8,128)(2,1)S(1)} %get-tuple-element.118), channel_id=1, source_target_pairs={{0,1},{1,0},{2,3},{3,2},{4,5},{5,4},{6,7},{7,6},{8,9},{9,8},{10,11... | collective-permute-start | bytes 1769480 | tf_op jit(solution)/shard_map/ppermute | solution.py:580
  36.0 3.3 %collective-permute-start.36 = (bf16[9,128,256]{2,1,0:T(8,128)(2,1)S(1)}, bf16[9,128,256]{2,1,0:T(8,128)(2,1)S(1)}, u32[]{:S(2)}, u32[]{:S(2)}) collective-permute-start(bf16[9,128,256]{2,1,0:T(8,128)(2,1)S(1)} %get-tuple-element.178), channel_id=1, source_target_pairs={{0,1},{1,0},{2,3},{3,2},{4,5},{5,4},{6,7},{7,6},{8,9},{9,8},{10,11... | collective-permute-start | bytes 1769480 | tf_op jit(solution)/shard_map/ppermute | solution.py:580
  36.2 2.3 %collective-permute-start.13 = (bf16[8,256]{1,0:T(8,128)(2,1)S(1)}, bf16[8,256]{1,0:T(8,128)(2,1)S(1)}, u32[]{:S(2)}, u32[]{:S(2)}) collective-permute-start(bf16[8,256]{1,0:T(8,128)(2,1)S(1)} %get-tuple-element.120), channel_id=1, source_target_pairs={{0,1},{1,0},{2,3},{3,2},{4,5},{5,4},{6,7},{7,6},{8,9},{9,8},{10,11... | collective-permute-start | bytes 12296 | tf_op jit(solution)/shard_map/ppermute | solution.py:580
  38.7 14.2 %collective-permute-start.14 = (bf16[584,256]{1,0:T(8,128)(2,1)S(1)}, bf16[584,256]{1,0:T(8,128)(2,1)S(1)}, u32[]{:S(2)}, u32[]{:S(2)}) collective-permute-start(bf16[584,256]{1,0:T(8,128)(2,1)S(1)} %get-tuple-element.122), channel_id=1, source_target_pairs={{0,2},{2,0},{4,6},{6,4},{8,10},{10,8},{12,14},{14,12},{1,3},{3,1},... | collective-permute-start | bytes 897032 | tf_op jit(solution)/shard_map/ppermute | solution.py:659
  38.7 4.1 %collective-permute-start.15 = (bf16[2,192,256]{2,1,0:T(8,128)(2,1)S(1)}, bf16[2,192,256]{2,1,0:T(8,128)(2,1)S(1)}, u32[]{:S(2)}, u32[]{:S(2)}) collective-permute-start(bf16[2,192,256]{2,1,0:T(8,128)(2,1)S(1)} %get-tuple-element.127), channel_id=1, source_target_pairs={{0,1},{1,0},{2,3},{3,2},{4,5},{5,4},{6,7},{7,6},{8,9},{9,8},{10,11... | collective-permute-start | bytes 589832 | tf_op jit(solution)/shard_map/ppermute | solution.py:580
  39.1 2.3 %collective-permute-start.16 = (bf16[2,48,256]{2,1,0:T(8,128)(2,1)S(1)}, bf16[2,48,256]{2,1,0:T(8,128)(2,1)S(1)}, u32[]{:S(2)}, u32[]{:S(2)}) collective-permute-start(bf16[2,48,256]{2,1,0:T(8,128)(2,1)S(1)} %get-tuple-element.128), channel_id=1, source_target_pairs={{0,1},{1,0},{2,3},{3,2},{4,5},{5,4},{6,7},{7,6},{8,9},{9,8},{10,11... | collective-permute-start | bytes 147464 | tf_op jit(solution)/shard_map/ppermute | solution.py:580
  39.4 16.1 %collective-permute-start.37 = (bf16[576,256]{1,0:T(8,128)(2,1)S(1)}, bf16[576,256]{1,0:T(8,128)(2,1)S(1)}, u32[]{:S(2)}, u32[]{:S(2)}) collective-permute-start(bf16[576,256]{1,0:T(8,128)(2,1)S(1)} %get-tuple-element.180), channel_id=1, source_target_pairs={{0,2},{2,0},{4,6},{6,4},{8,10},{10,8},{12,14},{14,12},{1,3},{3,1},... | collective-permute-start | bytes 884744 | tf_op jit(solution)/shard_map/ppermute | solution.py:659
  41.4 1.2 %collective-permute-start.17 = (bf16[2,48,256]{2,1,0:T(8,128)(2,1)S(1)}, bf16[2,48,256]{2,1,0:T(8,128)(2,1)S(1)}, u32[]{:S(2)}, u32[]{:S(2)}) collective-permute-start(bf16[2,48,256]{2,1,0:T(8,128)(2,1)S(1)} %get-tuple-element.129), channel_id=1, source_target_pairs={{0,1},{1,0},{2,3},{3,2},{4,5},{5,4},{6,7},{7,6},{8,9},{9,8},{10,11... | collective-permute-start | bytes 147464 | tf_op jit(solution)/shard_map/ppermute | solution.py:580
  41.4 1.4 %collective-permute-start.18 = (bf16[2,48,256]{2,1,0:T(8,128)(2,1)S(1)}, bf16[2,48,256]{2,1,0:T(8,128)(2,1)S(1)}, u32[]{:S(2)}, u32[]{:S(2)}) collective-permute-start(bf16[2,48,256]{2,1,0:T(8,128)(2,1)S(1)} %get-tuple-element.130), channel_id=1, source_target_pairs={{0,1},{1,0},{2,3},{3,2},{4,5},{5,4},{6,7},{7,6},{8,9},{9,8},{10,11... | collective-permute-start | bytes 147464 | tf_op jit(solution)/shard_map/ppermute | solution.py:580
  42.9 7.5 %collective-permute-start.19 = (bf16[2,2,48,256]{3,2,1,0:T(8,128)(2,1)S(1)}, bf16[2,2,48,256]{3,2,1,0:T(8,128)(2,1)S(1)}, u32[]{:S(2)}, u32[]{:S(2)}) collective-permute-start(bf16[2,2,48,256]{3,2,1,0:T(8,128)(2,1)S(1)} %get-tuple-element.131), channel_id=1, source_target_pairs={{0,4},{4,0},{10,14},{14,10},{1,9},{3,11},{5,13},{7,15},{9,1},{11,3... | collective-permute-start | bytes 294920 | tf_op jit(solution)/shard_map/ppermute | solution.py:610
  45.7 7.1 %collective-permute-start.20 = (bf16[2,2,48,256]{3,2,1,0:T(8,128)(2,1)S(1)}, bf16[2,2,48,256]{3,2,1,0:T(8,128)(2,1)S(1)}, u32[]{:S(2)}, u32[]{:S(2)}) collective-permute-start(bf16[2,2,48,256]{3,2,1,0:T(8,128)(2,1)S(1)} %get-tuple-element.132), channel_id=1, source_target_pairs={{0,12},{2,14},{4,8},{6,10},{8,4},{10,6},{12,0},{14,2},{1,7},{3,13}... | collective-permute-start | bytes 294920 | tf_op jit(solution)/shard_map/ppermute | solution.py:610
  52.9 31.5 %collective-permute-start.24 = (bf16[2,2,192,256]{3,2,1,0:T(8,128)(2,1)S(1)}, bf16[2,2,192,256]{3,2,1,0:T(8,128)(2,1)S(1)}, u32[]{:S(2)}, u32[]{:S(2)}) collective-permute-start(bf16[2,2,192,256]{3,2,1,0:T(8,128)(2,1)S(1)} %get-tuple-element.144), channel_id=1, source_target_pairs={{0,2},{2,0},{4,6},{6,4},{8,10},{10,8},{12,14},{14,12},{1,15},{3,5}... | collective-permute-start | bytes 1179656 | tf_op jit(solution)/shard_map/ppermute | solution.py:610
  55.6 5.3 %collective-permute-start.38 = (bf16[144,256]{1,0:T(8,128)(2,1)S(1)}, bf16[144,256]{1,0:T(8,128)(2,1)S(1)}, u32[]{:S(2)}, u32[]{:S(2)}) collective-permute-start(bf16[144,256]{1,0:T(8,128)(2,1)S(1)} %get-tuple-element.182), channel_id=1, source_target_pairs={{0,4},{2,6},{4,0},{6,2},{8,12},{10,14},{12,8},{14,10},{1,5},{3,7},... | collective-permute-start | bytes 221192 | tf_op jit(solution)/shard_map/ppermute | solution.py:662
  56.5 6.7 %collective-permute-start.39 = (bf16[144,256]{1,0:T(8,128)(2,1)S(1)}, bf16[144,256]{1,0:T(8,128)(2,1)S(1)}, u32[]{:S(2)}, u32[]{:S(2)}) collective-permute-start(bf16[144,256]{1,0:T(8,128)(2,1)S(1)} %get-tuple-element.183), channel_id=1, source_target_pairs={{0,8},{2,10},{4,12},{6,14},{8,0},{10,2},{12,4},{14,6},{1,9},{3,11}... | collective-permute-start | bytes 221192 | tf_op jit(solution)/shard_map/ppermute | solution.py:662
  59.4 7.0 %collective-permute-start.40 = (bf16[144,256]{1,0:T(8,128)(2,1)S(1)}, bf16[144,256]{1,0:T(8,128)(2,1)S(1)}, u32[]{:S(2)}, u32[]{:S(2)}) collective-permute-start(bf16[144,256]{1,0:T(8,128)(2,1)S(1)} %get-tuple-element.184), channel_id=1, source_target_pairs={{0,12},{2,14},{4,8},{6,10},{8,4},{10,6},{12,0},{14,2},{1,13},{3,15... | collective-permute-start | bytes 221192 | tf_op jit(solution)/shard_map/ppermute | solution.py:662
  66.5 7.0 %collective-permute-start.43 = (bf16[144,256]{1,0:T(8,128)(2,1)S(1)}, bf16[144,256]{1,0:T(8,128)(2,1)S(1)}, u32[]{:S(2)}, u32[]{:S(2)}) collective-permute-start(bf16[144,256]{1,0:T(8,128)(2,1)S(1)} %shard_map.113), channel_id=1, source_target_pairs={{0,12},{2,14},{4,8},{6,10},{8,4},{10,6},{12,0},{14,2},{1,13},{3,15... | collective-permute-start | bytes 221192 | tf_op jit(solution)/shard_map/ppermute | solution.py:662
  70.7 7.5 %collective-permute-start.42 = (bf16[144,256]{1,0:T(8,128)(2,1)S(1)}, bf16[144,256]{1,0:T(8,128)(2,1)S(1)}, u32[]{:S(2)}, u32[]{:S(2)}) collective-permute-start(bf16[144,256]{1,0:T(8,128)(2,1)S(1)} %shard_map.113), channel_id=1, source_target_pairs={{0,8},{2,10},{4,12},{6,14},{8,0},{10,2},{12,4},{14,6},{1,9},{3,11}... | collective-permute-start | bytes 221192 | tf_op jit(solution)/shard_map/ppermute | solution.py:662
  70.9 9.9 %collective-permute-start.41 = (bf16[144,256]{1,0:T(8,128)(2,1)S(1)}, bf16[144,256]{1,0:T(8,128)(2,1)S(1)}, u32[]{:S(2)}, u32[]{:S(2)}) collective-permute-start(bf16[144,256]{1,0:T(8,128)(2,1)S(1)} %shard_map.113), channel_id=1, source_target_pairs={{0,4},{2,6},{4,0},{6,2},{8,12},{10,14},{12,8},{14,10},{1,5},{3,7},... | collective-permute-start | bytes 221192 | tf_op jit(solution)/shard_map/ppermute | solution.py:662
  71.4 10.3 %collective-permute-start.21 = (bf16[152,256]{1,0:T(8,128)(2,1)S(1)}, bf16[152,256]{1,0:T(8,128)(2,1)S(1)}, u32[]{:S(2)}, u32[]{:S(2)}) collective-permute-start(bf16[152,256]{1,0:T(8,128)(2,1)S(1)} %get-tuple-element.141), channel_id=1, source_target_pairs={{0,4},{2,6},{4,0},{6,2},{8,12},{10,14},{12,8},{14,10},{1,5},{3,7},... | collective-permute-start | bytes 233480 | tf_op jit(solution)/shard_map/ppermute | solution.py:662
  73.5 9.1 %collective-permute-start.22 = (bf16[152,256]{1,0:T(8,128)(2,1)S(1)}, bf16[152,256]{1,0:T(8,128)(2,1)S(1)}, u32[]{:S(2)}, u32[]{:S(2)}) collective-permute-start(bf16[152,256]{1,0:T(8,128)(2,1)S(1)} %get-tuple-element.142), channel_id=1, source_target_pairs={{0,8},{2,10},{4,12},{6,14},{8,0},{10,2},{12,4},{14,6},{1,9},{3,11}... | collective-permute-start | bytes 233480 | tf_op jit(solution)/shard_map/ppermute | solution.py:662
  78.2 6.2 %collective-permute-start.23 = (bf16[152,256]{1,0:T(8,128)(2,1)S(1)}, bf16[152,256]{1,0:T(8,128)(2,1)S(1)}, u32[]{:S(2)}, u32[]{:S(2)}) collective-permute-start(bf16[152,256]{1,0:T(8,128)(2,1)S(1)} %get-tuple-element.143), channel_id=1, source_target_pairs={{0,12},{2,14},{4,8},{6,10},{8,4},{10,6},{12,0},{14,2},{1,13},{3,15... | collective-permute-start | bytes 233480 | tf_op jit(solution)/shard_map/ppermute | solution.py:662
  80.8 3.6 %collective-permute-start.25 = (bf16[2,2,48,256]{3,2,1,0:T(8,128)(2,1)S(1)}, bf16[2,2,48,256]{3,2,1,0:T(8,128)(2,1)S(1)}, u32[]{:S(2)}, u32[]{:S(2)}) collective-permute-start(bf16[2,2,48,256]{3,2,1,0:T(8,128)(2,1)S(1)} %get-tuple-element.145), channel_id=1, source_target_pairs={{1,11},{5,15},{11,1},{15,5},{17,27},{21,31},{27,17},{31,21}} | collective-permute-start | bytes 294920 | tf_op jit(solution)/shard_map/ppermute | solution.py:610
  81.7 15.1 %collective-permute-start.44 = (bf16[576,256]{1,0:T(8,128)(2,1)S(1)}, bf16[576,256]{1,0:T(8,128)(2,1)S(1)}, u32[]{:S(2)}, u32[]{:S(2)}) collective-permute-start(bf16[576,256]{1,0:T(8,128)(2,1)S(1)} %pad_maximum_fusion.1.refs_0_), channel_id=1, source_target_pairs={{0,2},{2,0},{4,6},{6,4},{8,10},{10,8},{12,14},{14,12},{1,3},{3,1},... | collective-permute-start | bytes 884744 | tf_op jit(solution)/shard_map/ppermute | solution.py:659
  84.5 10.3 %collective-permute-start.28 = (bf16[144,256]{1,0:T(8,128)(2,1)S(1)}, bf16[144,256]{1,0:T(8,128)(2,1)S(1)}, u32[]{:S(2)}, u32[]{:S(2)}) collective-permute-start(bf16[144,256]{1,0:T(8,128)(2,1)S(1)} %get-tuple-element.150), channel_id=1, source_target_pairs={{0,12},{2,14},{4,8},{6,10},{8,4},{10,6},{12,0},{14,2},{1,13},{3,15... | collective-permute-start | bytes 221192 | tf_op jit(solution)/shard_map/ppermute | solution.py:662
  88.0 6.7 %collective-permute-start.27 = (bf16[144,256]{1,0:T(8,128)(2,1)S(1)}, bf16[144,256]{1,0:T(8,128)(2,1)S(1)}, u32[]{:S(2)}, u32[]{:S(2)}) collective-permute-start(bf16[144,256]{1,0:T(8,128)(2,1)S(1)} %get-tuple-element.150), channel_id=1, source_target_pairs={{0,8},{2,10},{4,12},{6,14},{8,0},{10,2},{12,4},{14,6},{1,9},{3,11}... | collective-permute-start | bytes 221192 | tf_op jit(solution)/shard_map/ppermute | solution.py:662
  88.0 5.7 %collective-permute-start.26 = (bf16[144,256]{1,0:T(8,128)(2,1)S(1)}, bf16[144,256]{1,0:T(8,128)(2,1)S(1)}, u32[]{:S(2)}, u32[]{:S(2)}) collective-permute-start(bf16[144,256]{1,0:T(8,128)(2,1)S(1)} %get-tuple-element.150), channel_id=1, source_target_pairs={{0,4},{2,6},{4,0},{6,2},{8,12},{10,14},{12,8},{14,10},{1,5},{3,7},... | collective-permute-start | bytes 221192 | tf_op jit(solution)/shard_map/ppermute | solution.py:662
  88.9 8.6 %collective-permute-start.30 = (bf16[2,2,192,256]{3,2,1,0:T(8,128)(2,1)S(1)}, bf16[2,2,192,256]{3,2,1,0:T(8,128)(2,1)S(1)}, u32[]{:S(2)}, u32[]{:S(2)}) collective-permute-start(bf16[2,2,192,256]{3,2,1,0:T(8,128)(2,1)S(1)} %collective-permute-done.24.refs_0_), channel_id=1, source_target_pairs={{0,1},{1,0},{2,3},{3,2},{4,5},{5,4},{6,7},{7,6},{8,9},{9,8},{10,11... | collective-permute-start | bytes 1179656 | tf_op jit(solution)/shard_map/ppermute | solution.py:580
  94.8 8.4 %collective-permute-start.29 = (bf16[576,256]{1,0:T(8,128)(2,1)S(1)}, bf16[576,256]{1,0:T(8,128)(2,1)S(1)}, u32[]{:S(2)}, u32[]{:S(2)}) collective-permute-start(bf16[576,256]{1,0:T(8,128)(2,1)S(1)} %constant_dynamic-update-slice_fusion.refs_0_), channel_id=1, source_target_pairs={{0,2},{2,0},{4,6},{6,4},{8,10},{10,8},{12,14},{14,12},{1,3},{3,1},... | collective-permute-start | bytes 884744 | tf_op jit(solution)/shard_map/ppermute | solution.py:659
  94.8 1.4 %collective-permute-start.31 = (bf16[2,2,48,256]{3,2,1,0:T(8,128)(2,1)S(1)}, bf16[2,2,48,256]{3,2,1,0:T(8,128)(2,1)S(1)}, u32[]{:S(2)}, u32[]{:S(2)}) collective-permute-start(bf16[2,2,48,256]{3,2,1,0:T(8,128)(2,1)S(1)} %collective-permute-done.19.refs_2_), channel_id=1, source_target_pairs={{0,1},{1,0},{2,3},{3,2},{4,5},{5,4},{6,7},{7,6},{8,9},{9,8},{10,11... | collective-permute-start | bytes 294920 | tf_op jit(solution)/shard_map/ppermute | solution.py:580
  94.9 1.4 %collective-permute-start.32 = (bf16[2,2,48,256]{3,2,1,0:T(8,128)(2,1)S(1)}, bf16[2,2,48,256]{3,2,1,0:T(8,128)(2,1)S(1)}, u32[]{:S(2)}, u32[]{:S(2)}) collective-permute-start(bf16[2,2,48,256]{3,2,1,0:T(8,128)(2,1)S(1)} %collective-permute-done.20.refs_4_), channel_id=1, source_target_pairs={{0,1},{1,0},{2,3},{3,2},{4,5},{5,4},{6,7},{7,6},{8,9},{9,8},{10,11... | collective-permute-start | bytes 294920 | tf_op jit(solution)/shard_map/ppermute | solution.py:580
  96.2 1.3 %collective-permute-start.33 = (bf16[2,2,48,256]{3,2,1,0:T(8,128)(2,1)S(1)}, bf16[2,2,48,256]{3,2,1,0:T(8,128)(2,1)S(1)}, u32[]{:S(2)}, u32[]{:S(2)}) collective-permute-start(bf16[2,2,48,256]{3,2,1,0:T(8,128)(2,1)S(1)} %collective-permute-done.25.refs_6_), channel_id=1, source_target_pairs={{0,1},{1,0},{2,3},{3,2},{4,5},{5,4},{6,7},{7,6},{8,9},{9,8},{10,11... | collective-permute-start | bytes 294920 | tf_op jit(solution)/shard_map/ppermute | solution.py:580
  96.4 7.3 %collective-permute-start.45 = (bf16[576,256]{1,0:T(8,128)(2,1)S(1)}, bf16[576,256]{1,0:T(8,128)(2,1)S(1)}, u32[]{:S(2)}, u32[]{:S(2)}) collective-permute-start(bf16[576,256]{1,0:T(8,128)(2,1)S(1)} %pad_maximum_fusion.1.refs_0_), channel_id=1, source_target_pairs={{0,1},{1,0},{2,3},{3,2},{4,5},{5,4},{6,7},{7,6},{8,9},{9,8},{10,11... | collective-permute-start | bytes 884744 | tf_op jit(solution)/shard_map/ppermute | solution.py:580
  96.7 7.0 %collective-permute-start.46 = (bf16[576,256]{1,0:T(8,128)(2,1)S(1)}, bf16[576,256]{1,0:T(8,128)(2,1)S(1)}, u32[]{:S(2)}, u32[]{:S(2)}) collective-permute-start(bf16[576,256]{1,0:T(8,128)(2,1)S(1)} %collective-permute-done.44.refs_1_), channel_id=1, source_target_pairs={{0,1},{1,0},{2,3},{3,2},{4,5},{5,4},{6,7},{7,6},{8,9},{9,8},{10,11... | collective-permute-start | bytes 884744 | tf_op jit(solution)/shard_map/ppermute | solution.py:580
  103.2 2.3 %collective-permute-start.35 = (bf16[576,256]{1,0:T(8,128)(2,1)S(1)}, bf16[576,256]{1,0:T(8,128)(2,1)S(1)}, u32[]{:S(2)}, u32[]{:S(2)}) collective-permute-start(bf16[576,256]{1,0:T(8,128)(2,1)S(1)} %collective-permute-done.29.refs_1_), channel_id=1, source_target_pairs={{0,1},{1,0},{2,3},{3,2},{4,5},{5,4},{6,7},{7,6},{8,9},{9,8},{10,11... | collective-permute-start | bytes 884744 | tf_op jit(solution)/shard_map/ppermute | solution.py:580
  103.3 2.2 %collective-permute-start.34 = (bf16[576,256]{1,0:T(8,128)(2,1)S(1)}, bf16[576,256]{1,0:T(8,128)(2,1)S(1)}, u32[]{:S(2)}, u32[]{:S(2)}) collective-permute-start(bf16[576,256]{1,0:T(8,128)(2,1)S(1)} %constant_dynamic-update-slice_fusion.refs_0_), channel_id=1, source_target_pairs={{0,1},{1,0},{2,3},{3,2},{4,5},{5,4},{6,7},{7,6},{8,9},{9,8},{10,11... | collective-permute-start | bytes 884744 | tf_op jit(solution)/shard_map/ppermute | solution.py:580
